TPU v7x, 128 devices: a whole 4x4x4 slice. The times are simulated.
128 devices in a mesh: leaf: 8 (over x, core), panel: 16 (over z, y).
Axes of the slice: x: 4, y: 4, z: 4, core: 2. Of those that a mesh axis runs over, the one named last changes fastest.
Arguments:
- live_tiles: int32 [15], replicated, may hold values from 8 to 16
- row_tiles: int32 [14, 8], replicated, may hold values from 0 to 47, as said below
- rhs0: float32 [256, 16384], P('panel', 'leaf'), may hold values from -6 to 6
- rhs1: float32 [256, 8192], P('panel', 'leaf'), may hold values from -6 to 6
- rhs2: float32 [256, 4096], P('panel', 'leaf'), may hold values from -6 to 6
- rhs3: float32 [256, 2048], P('panel', 'leaf'), may hold values from -6 to 6
- dinv0: float32 [16384, 2048], P('leaf', 'panel'), as said below
- dinv1: float32 [8192, 2048], P('leaf', 'panel'), as said below
- dinv2: float32 [4096, 2048], P('leaf', 'panel'), as said below
- dinv3: float32 [2048, 2048], P('leaf', 'panel'), as said below
- off0: float32 [8192, 2048], P('leaf', 'panel'), may hold values from -0.125 to 0.125
- off1: float32 [4096, 2048], P('leaf', 'panel'), may hold values from -0.125 to 0.125
- off2: float32 [2048, 2048], P('leaf', 'panel'), may hold values from -0.125 to 0.125
Outputs:
- sol0: float32 [256, 16384], P('panel', 'leaf')
- sol1: float32 [256, 8192], P('panel', 'leaf')
- sol2: float32 [256, 4096], P('panel', 'leaf')
- sol3: float32 [256, 2048], P('panel', 'leaf')
Inputs may be any that keep to these rules, and one draw needn't show every extreme that they name: `row_tiles`: each row names 8 different tiles; for a supernode of level k every value is below (3 - k) * 16. `live_tiles`: counted level by level in the supernodes' order. `dinv0`: each 2048 x 2048 row block is lower triangular with diagonal entries from 0.5 to 2. `dinv1`: each 2048 x 2048 row block is lower triangular with diagonal entries from 0.5 to 2. `dinv2`: each 2048 x 2048 row block is lower triangular with diagonal entries from 0.5 to 2. `dinv3`: each 2048 x 2048 row block is lower triangular with diagonal entries from 0.5 to 2.
All inputs are finite; a program needn't handle non-finite values.
Results may differ from a plain program's by a relative error of at most 0.00028.
Values sent between devices are 32-bit elements; how exact they have to be, the bound alone decides.
No kernel may reach another device: no remote copies, remote signals or barrier semaphores. Data moves between devices by JAX's collectives and lax.ppermute only.
A program may use at most 64 MiB of HBM per device.

v0:
```python
import jax
import jax.numpy as jnp
from jax import lax
from jax.sharding import PartitionSpec as P

B = 128
LEVELS = 4


highest = lax.Precision.HIGHEST


def swapped(block, axis, bit):
    count = lax.axis_size(axis)
    route = []
    for low in range(count):
        high = low | 1 << bit
        if high != low and high < count:
            route += [(low, high), (high, low)]
    return lax.ppermute(block, axis, route)


def in_blocks(shard, dim, count):
    before, after = (shard.shape[:dim], shard.shape[dim + 1 :])
    return jnp.moveaxis(shard.reshape(*before, count, -1, *after), dim, 0)


def sent_and_summed(shard, axis, dim):
    parts = in_blocks(shard, dim, lax.axis_size(axis))
    arrived = lax.all_to_all(parts, axis, split_axis=0, concat_axis=0, tiled=True)
    return arrived.sum(axis=0)


def from_everyone(shard, axis):
    copies = jnp.broadcast_to(shard, (lax.axis_size(axis), *shard.shape))
    return lax.all_to_all(copies, axis, split_axis=0, concat_axis=0, tiled=True)


def joined_along(parts, dim):
    shape = list(parts.shape[1:])
    shape[dim] *= parts.shape[0]
    return jnp.moveaxis(parts, 0, dim).reshape(shape)


def gather_directly(shard, axis, dim):
    parts = from_everyone(shard, axis)
    return joined_along(parts, dim)


def leaf_bit(leaf_index, bit_number):
    return leaf_index // 2**bit_number % 2


def group_rows(vector, height, leaf_index):
    for bit_number in range(height):
        partner = swapped(vector, "leaf", bit_number)
        is_lower = leaf_bit(leaf_index, bit_number) == 0
        vector = jnp.where(
            is_lower, jnp.concatenate([vector, partner], 1), jnp.concatenate([partner, vector], 1)
        )
    return vector


def group_halving(buffer, height, leaf_index):
    for bit_number in reversed(range(height)):
        half_width = buffer.shape[1] // 2
        is_lower = leaf_bit(leaf_index, bit_number) == 0
        kept_half = jnp.where(is_lower, buffer[:, :half_width], buffer[:, half_width:])
        given_half = jnp.where(is_lower, buffer[:, half_width:], buffer[:, :half_width])
        buffer = kept_half + swapped(given_half, "leaf", bit_number)
    return buffer


def group_total(partial_sum, height):
    for bit_number in range(height):
        partial_sum = partial_sum + swapped(partial_sum, "leaf", bit_number)
    return partial_sum


def to_columns(vector, height, leaf_index):
    full_rows = group_rows(vector, height, leaf_index)
    return lax.all_to_all(full_rows, "panel", split_axis=1, concat_axis=0, tiled=True)


def contract_last(left, right):
    return lax.dot_general(
        left, right, (((1,), (1,)), ((), ())), precision=highest, preferred_element_type=jnp.float32
    )


def selector(chosen, offset, tile_count):
    return (chosen[:, None] == offset + jnp.arange(tile_count, dtype=jnp.int32)[None, :]).astype(
        jnp.float32
    )


def geometry(height, leaf_index, live_tiles, first_node, order_rows):
    group_width = 2**height
    node_index = leaf_index // group_width
    group_place = leaf_index % group_width
    rows_here = order_rows // group_width
    live_count = lax.dynamic_index_in_dim(live_tiles, first_node + node_index, keepdims=False)
    node_mask = (jnp.arange(order_rows, dtype=jnp.int32) < live_count * B).astype(jnp.float32)
    local_mask = lax.dynamic_slice_in_dim(node_mask, group_place * rows_here, rows_here)
    return (node_index, group_place, rows_here, node_mask, local_mask)


def chosen_tiles(row_tiles, first_node, node_index, group_place, local_tiles):
    entry = lax.dynamic_index_in_dim(row_tiles, first_node + node_index, keepdims=False)
    return lax.dynamic_slice_in_dim(entry, group_place * local_tiles, local_tiles)


def local(
    live_tiles, row_tiles, rhs0, rhs1, rhs2, rhs3, dinv0, dinv1, dinv2, dinv3, off0, off1, off2
):
    right_sides = [rhs0, rhs1, rhs2, rhs3]
    inverses = [dinv0, dinv1, dinv2, dinv3]
    off_rows = [off0, off1, off2]
    leaf_index = lax.axis_index("leaf")
    panel_index = lax.axis_index("panel")
    leaf_count = lax.axis_size("leaf")
    panel_count = lax.axis_size("panel")
    order_rows = dinv0.shape[0]
    tile_count = order_rows // B
    share_rows = rhs0.shape[0]
    all_rhs = share_rows * panel_count
    off_tiles = row_tiles.shape[1]
    first_nodes = []
    start_node = 0
    for height in range(LEVELS):
        first_nodes.append(start_node)
        start_node = start_node + leaf_count // 2**height
    buffers = [jnp.zeros((share_rows, order_rows), jnp.float32) for height in range(LEVELS)]
    columns_kept = []
    for height in range(LEVELS):
        node_index, group_place, rows_here, node_mask, local_mask = geometry(
            height, leaf_index, live_tiles, first_nodes[height], order_rows
        )
        residual = right_sides[height]
        if height > 0:
            residual = residual - group_halving(buffers[height], height, leaf_index)
        spread = to_columns(residual * local_mask[None, :], height, leaf_index)
        inverse = inverses[height]
        solved = sent_and_summed(contract_last(spread, inverse), "panel", 0)
        columns = to_columns(solved * local_mask[None, :], height, leaf_index)
        columns_kept.append(columns)
        if height < LEVELS - 1:
            block_rows = off_rows[height]
            update = sent_and_summed(contract_last(columns, block_rows), "panel", 0)
            local_tiles = off_tiles // 2**height
            chosen = chosen_tiles(
                row_tiles, first_nodes[height], node_index, group_place, local_tiles
            )
            pieces = update.reshape(share_rows, local_tiles, B)
            for ancestor in range(height + 1, LEVELS):
                picked = selector(chosen, (ancestor - height - 1) * tile_count, tile_count)
                sent = jnp.einsum("rtb,tc->rcb", pieces, picked, precision=highest)
                buffers[ancestor] = buffers[ancestor] + sent.reshape(share_rows, order_rows)
    full_solutions = [None] * LEVELS
    outputs = [None] * LEVELS
    for height in reversed(range(LEVELS)):
        node_index, group_place, rows_here, node_mask, local_mask = geometry(
            height, leaf_index, live_tiles, first_nodes[height], order_rows
        )
        target = columns_kept[height]
        if height < LEVELS - 1:
            local_tiles = off_tiles // 2**height
            chosen = chosen_tiles(
                row_tiles, first_nodes[height], node_index, group_place, local_tiles
            )
            gathered = jnp.zeros((all_rhs, local_tiles, B), jnp.float32)
            for ancestor in range(height + 1, LEVELS):
                picked = selector(chosen, (ancestor - height - 1) * tile_count, tile_count)
                above = full_solutions[ancestor].reshape(all_rhs, tile_count, B)
                gathered = gathered + jnp.einsum("rcb,tc->rtb", above, picked, precision=highest)
            correction = jnp.dot(
                gathered.reshape(all_rhs, local_tiles * B),
                off_rows[height],
                precision=highest,
                preferred_element_type=jnp.float32,
            )
            target = target - group_total(correction, height)
        whole_target = gather_directly(target, "panel", 1) * node_mask[None, :]
        mine = lax.dynamic_slice_in_dim(whole_target, group_place * rows_here, rows_here, 1)
        partial_sum = jnp.dot(
            mine, inverses[height], precision=highest, preferred_element_type=jnp.float32
        )
        partial_sum = group_total(partial_sum, height)
        whole_solution = gather_directly(partial_sum, "panel", 1) * node_mask[None, :]
        full_solutions[height] = whole_solution
        outputs[height] = lax.dynamic_slice(
            whole_solution,
            (panel_index * share_rows, group_place * rows_here),
            (share_rows, rows_here),
        )
    return tuple(outputs)


def solution(mesh):
    return jax.shard_map(
        local,
        mesh=mesh,
        in_specs=(
            P(),
            P(),
            P("panel", "leaf"),
            P("panel", "leaf"),
            P("panel", "leaf"),
            P("panel", "leaf"),
            P("leaf", "panel"),
            P("leaf", "panel"),
            P("leaf", "panel"),
            P("leaf", "panel"),
            P("leaf", "panel"),
            P("leaf", "panel"),
            P("leaf", "panel"),
        ),
        out_specs=(P("panel", "leaf"), P("panel", "leaf"), P("panel", "leaf"), P("panel", "leaf")),
        check_vma=False,
    )
```

profile of v0, /device:TPU:0, one launch (start us, length us, event | category | flops | bytes accessed | tf_op | source)
XLA Modules:
  0.0 660.0 jit_solution(12149150702845184301)
XLA Ops:
  3.7 15.9 %all_to_all.194 = f32[16,16,128]{2,0,1:T(8,128)S(1)} all-to-all(f32[16,16,128]{2,0,1:T(8,128)S(1)} %copy_bitcast_fusion.3), channel_id=1, replica_groups=mesh['leaf'=8,'panel'=16] {'panel'}, dimensions={1} | all-to-all | bytes 262144 | tf_op jit(solution)/shard_map/all_to_all | solution.py:82
  19.6 3.1 fusion.3
  22.8 3.7 all-to-all-start.1
  26.5 29.4 %all-to-all-done.1 = f32[16,16,2048]{2,1,0:T(8,128)S(1)} async-done(((f32[16,16,2048]{2,1,0:T(8,128)}), f32[16,16,2048]{2,1,0:T(8,128)S(1)}, u32[]{:S(2)}, u32[]{:S(2)}) %all-to-all-start.1) | async-done | bytes 2097184 | tf_op jit(solution)/shard_map/all_to_all | solution.py:30
  56.0 10.7 %all_to_all.195 = f32[16,16,128]{2,0,1:T(8,128)S(1)} all-to-all(f32[16,16,128]{2,0,1:T(8,128)S(1)} %bitcast_multiply_fusion.4), channel_id=1, replica_groups=mesh['leaf'=8,'panel'=16] {'panel'}, dimensions={1} | all-to-all | bytes 262144 | tf_op jit(solution)/shard_map/all_to_all | solution.py:82
  66.8 3.0 fusion.12
  69.8 3.8 all-to-all-start.3
  74.5 15.5 %all-to-all-done.3 = f32[16,16,1024]{2,1,0:T(8,128)S(1)} async-done(((f32[16,16,1024]{2,1,0:T(8,128)}), f32[16,16,1024]{2,1,0:T(8,128)S(1)}, u32[]{:S(2)}, u32[]{:S(2)}) %all-to-all-start.3) | async-done | bytes 1048608 | tf_op jit(solution)/shard_map/all_to_all | solution.py:30
  93.1 11.0 %all_to_all.196 = f32[16,16,128]{2,0,1:T(8,128)S(1)} all-to-all(f32[16,16,128]{2,0,1:T(8,128)S(1)} %maximum_select_fusion), channel_id=1, replica_groups=mesh['leaf'=8,'panel'=16] {'panel'}, dimensions={1} | all-to-all | bytes 262144 | tf_op jit(solution)/shard_map/all_to_all | solution.py:82
  106.1 3.8 all-to-all-start.5
  109.9 16.5 %all-to-all-done.5 = f32[16,16,1024]{2,1,0:T(8,128)S(1)} async-done(((f32[16,16,1024]{2,1,0:T(8,128)}), f32[16,16,1024]{2,1,0:T(8,128)S(1)}, u32[]{:S(2)}, u32[]{:S(2)}) %all-to-all-start.5) | async-done | bytes 1048608 | tf_op jit(solution)/shard_map/all_to_all | solution.py:30
  127.8 10.9 %all_to_all.197 = f32[16,16,128]{2,0,1:T(8,128)S(1)} all-to-all(f32[16,16,128]{2,0,1:T(8,128)S(1)} %maximum_select_fusion.1), channel_id=1, replica_groups=mesh['leaf'=8,'panel'=16] {'panel'}, dimensions={1} | all-to-all | bytes 262144 | tf_op jit(solution)/shard_map/all_to_all | solution.py:82
  140.1 3.7 all-to-all-start.7
  144.4 10.1 %all-to-all-done.7 = f32[16,16,512]{2,1,0:T(8,128)S(1)} async-done(((f32[16,16,512]{2,1,0:T(8,128)}), f32[16,16,512]{2,1,0:T(8,128)S(1)}, u32[]{:S(2)}, u32[]{:S(2)}) %all-to-all-start.7) | async-done | bytes 524320 | tf_op jit(solution)/shard_map/all_to_all | solution.py:30
  163.5 2.8 collective-permute-done.6
  166.3 11.0 %all_to_all.198 = f32[16,16,128]{2,0,1:T(8,128)S(1)} all-to-all(f32[16,16,128]{2,0,1:T(8,128)S(1)} %maximum_select_fusion.2), channel_id=1, replica_groups=mesh['leaf'=8,'panel'=16] {'panel'}, dimensions={1} | all-to-all | bytes 262144 | tf_op jit(solution)/shard_map/all_to_all | solution.py:82
  178.7 3.7 all-to-all-start.9
  182.5 10.0 %all-to-all-done.9 = f32[16,16,512]{2,1,0:T(8,128)S(1)} async-done(((f32[16,16,512]{2,1,0:T(8,128)}), f32[16,16,512]{2,1,0:T(8,128)S(1)}, u32[]{:S(2)}, u32[]{:S(2)}) %all-to-all-start.9) | async-done | bytes 524320 | tf_op jit(solution)/shard_map/all_to_all | solution.py:30
  195.5 2.8 collective-permute-done.8
  198.9 3.7 all-to-all-start.10
  203.6 7.0 %all-to-all-done.10 = f32[16,16,128]{2,0,1:T(8,128)S(1)} async-done(((f32[16,16,128]{2,0,1:T(8,128)}), f32[16,16,128]{2,0,1:T(8,128)S(1)}, u32[]{:S(2)}, u32[]{:S(2)}) %all-to-all-start.10) | async-done | bytes 131104 | tf_op jit(solution)/shard_map/all_to_all | solution.py:82
  211.6 3.5 all-to-all-start.11
  215.9 8.0 %all-to-all-done.11 = f32[16,16,256]{2,1,0:T(8,128)S(1)} async-done(((f32[16,16,256]{2,1,0:T(8,128)}), f32[16,16,256]{2,1,0:T(8,128)S(1)}, u32[]{:S(2)}, u32[]{:S(2)}) %all-to-all-start.11) | async-done | bytes 262176 | tf_op jit(solution)/shard_map/all_to_all | solution.py:30
  224.3 3.1 collective-permute-start.9
  227.4 2.8 collective-permute-done.9
  240.7 3.1 collective-permute-start.14
  243.8 2.7 collective-permute-done.14
  246.5 10.9 %all_to_all.199 = f32[16,16,128]{2,0,1:T(8,128)S(1)} all-to-all(f32[16,16,128]{2,0,1:T(8,128)S(1)} %maximum_select_fusion.4), channel_id=1, replica_groups=mesh['leaf'=8,'panel'=16] {'panel'}, dimensions={1} | all-to-all | bytes 262144 | tf_op jit(solution)/shard_map/all_to_all | solution.py:82
  258.5 3.5 all-to-all-start.13
  262.1 8.6 %all-to-all-done.13 = f32[16,16,256]{2,1,0:T(8,128)S(1)} async-done(((f32[16,16,256]{2,1,0:T(8,128)}), f32[16,16,256]{2,1,0:T(8,128)S(1)}, u32[]{:S(2)}, u32[]{:S(2)}) %all-to-all-start.13) | async-done | bytes 262176 | tf_op jit(solution)/shard_map/all_to_all | solution.py:30
  276.0 3.1 collective-permute-start.17
  279.1 2.7 collective-permute-done.17
  281.8 10.9 %all_to_all.200 = f32[16,16,128]{2,0,1:T(8,128)S(1)} all-to-all(f32[16,16,128]{2,0,1:T(8,128)S(1)} %maximum_select_fusion.5), channel_id=1, replica_groups=mesh['leaf'=8,'panel'=16] {'panel'}, dimensions={1} | all-to-all | bytes 262144 | tf_op jit(solution)/shard_map/all_to_all | solution.py:82
  292.9 28.2 %all_to_all.201 = f32[16,256,128]{2,1,0:T(8,128)S(1)} all-to-all(f32[16,256,128]{2,1,0:T(8,128)S(1)} %broadcast_in_dim.16), channel_id=1, replica_groups=mesh['leaf'=8,'panel'=16] {'panel'}, dimensions={0} | all-to-all | bytes 4194304 | tf_op jit(solution)/shard_map/all_to_all | solution.py:36
  328.0 3.8 collective-permute-done.19
  331.8 3.0 collective-permute-start.20
  334.8 3.6 collective-permute-done.20
  339.9 4.4 all-to-all-start.16
  345.0 28.5 %all-to-all-done.16 = f32[16,256,128]{2,1,0:T(8,128)} async-done(((f32[16,256,128]{2,1,0:T(8,128)}), f32[16,256,128]{2,1,0:T(8,128)}, u32[]{:S(2)}, u32[]{:S(2)}) %all-to-all-start.16) | async-done | bytes 2097184 | tf_op jit(solution)/shard_map/all_to_all | solution.py:36
  376.7 2.4 bitcast_multiply_fusion.3
  379.1 2.2 copy.130
  386.5 3.9 collective-permute-done.22
  390.6 31.7 %all_to_all.202 = f32[16,256,128]{2,1,0:T(8,128)} all-to-all(f32[16,256,128]{2,1,0:T(8,128)S(1)} %broadcast_in_dim.18), channel_id=1, replica_groups=mesh['leaf'=8,'panel'=16] {'panel'}, dimensions={0} | all-to-all | bytes 4194304 | tf_op jit(solution)/shard_map/all_to_all | solution.py:36
  422.3 2.9 copy.131
  430.6 3.9 collective-permute-done.24
  436.1 4.4 all-to-all-start.18
  440.5 31.0 %all-to-all-done.18 = f32[16,256,128]{2,1,0:T(8,128)} async-done(((f32[16,256,128]{2,1,0:T(8,128)}), f32[16,256,128]{2,1,0:T(8,128)}, u32[]{:S(2)}, u32[]{:S(2)}) %all-to-all-start.18) | async-done | bytes 2097184 | tf_op jit(solution)/shard_map/all_to_all | solution.py:36
  471.5 2.9 copy.132
  474.4 3.3 bitcast_multiply_fusion.2
  477.7 3.1 copy.133
  480.8 2.4 fusion.83
  486.4 32.4 %all_to_all.203 = f32[16,256,128]{2,1,0:T(8,128)} all-to-all(f32[16,256,128]{2,1,0:T(8,128)S(1)} %broadcast_in_dim.20), channel_id=1, replica_groups=mesh['leaf'=8,'panel'=16] {'panel'}, dimensions={0} | all-to-all | bytes 4194304 | tf_op jit(solution)/shard_map/all_to_all | solution.py:36
  518.9 2.9 copy.135
  521.7 3.3 fusion.2
  528.1 4.7 all-to-all-start.20
  532.8 34.0 %all-to-all-done.20 = f32[16,256,128]{2,1,0:T(8,128)} async-done(((f32[16,256,128]{2,1,0:T(8,128)}), f32[16,256,128]{2,1,0:T(8,128)}, u32[]{:S(2)}, u32[]{:S(2)}) %all-to-all-start.20) | async-done | bytes 2097184 | tf_op jit(solution)/shard_map/all_to_all | solution.py:36
  566.8 3.0 copy.136
  569.7 3.3 bitcast_multiply_fusion.1
  573.1 3.0 copy.137
  576.1 2.5 fusion.48
  581.8 31.3 %all_to_all.204 = f32[16,256,128]{2,1,0:T(8,128)S(1)} all-to-all(f32[16,256,128]{2,1,0:T(8,128)S(1)} %broadcast_in_dim.22), channel_id=1, replica_groups=mesh['leaf'=8,'panel'=16] {'panel'}, dimensions={0} | all-to-all | bytes 4194304 | tf_op jit(solution)/shard_map/all_to_all | solution.py:36
  616.9 3.5 fusion.95
  622.0 3.8 all-to-all-start.22
  633.5 21.4 %all-to-all-done.22 = f32[16,256,128]{2,1,0:T(8,128)S(1)} async-done(((f32[16,256,128]{2,1,0:T(8,128)}), f32[16,256,128]{2,1,0:T(8,128)S(1)}, u32[]{:S(2)}, u32[]{:S(2)}) %all-to-all-start.22) | async-done | bytes 2097184 | tf_op jit(solution)/shard_map/all_to_all | solution.py:36
  (233 shorter events, 95.3 us)
Async XLA Ops:
  0.6 19.0 %copy-start = (f32[2048,128]{1,0:T(8,128)S(1)}, f32[2048,128]{1,0:T(8,128)}, u32[]{:S(2)}) copy-start(f32[2048,128]{1,0:T(8,128)} %param.19) | copy-start | bytes 3145732
  22.8 33.1 %all-to-all-start.1 = ((f32[16,16,2048]{2,1,0:T(8,128)}), f32[16,16,2048]{2,1,0:T(8,128)S(1)}, u32[]{:S(2)}, u32[]{:S(2)}) async-start(f32[16,16,2048]{2,1,0:T(8,128)} %fusion.3), calls=%async_computation.1 | async-start | bytes 4194304 | tf_op jit(solution)/shard_map/all_to_all | solution.py:30
  56.0 18.2 %copy-start.21 = (s32[14,8]{0,1:T(8,128)S(1)}, s32[14,8]{0,1:T(8,128)}, u32[]{:S(2)}) copy-start(s32[14,8]{0,1:T(8,128)} %param.14) | copy-start | bytes 1348
  69.8 22.0 %copy-start.11 = (f32[16,1024]{1,0:T(8,128)S(1)}, f32[16,1024]{1,0:T(8,128)}, u32[]{:S(2)}) copy-start(f32[16,1024]{1,0:T(8,128)} %param.16) | copy-start | bytes 196612
  69.8 34.3 %copy-start.4 = (f32[1024,128]{1,0:T(8,128)S(1)}, f32[1024,128]{1,0:T(8,128)}, u32[]{:S(2)}) copy-start(f32[1024,128]{1,0:T(8,128)} %param.20) | copy-start | bytes 1572868
  69.8 20.1 %all-to-all-start.3 = ((f32[16,16,1024]{2,1,0:T(8,128)}), f32[16,16,1024]{2,1,0:T(8,128)S(1)}, u32[]{:S(2)}, u32[]{:S(2)}) async-start(f32[16,16,1024]{2,1,0:T(8,128)} %fusion.12), calls=%async_computation.3 | async-start | bytes 2097152 | tf_op jit(solution)/shard_map/all_to_all | solution.py:30
  74.5 69.6 %copy-start.15 = (s32[8]{0:T(128)}, s32[8]{0:T(128)S(1)}, u32[]{:S(2)}) copy-start(s32[8]{0:T(128)S(1)} %dynamic-slice_reduce_fusion) | copy-start | bytes 100
  90.4 1.3 collective-permute-start
  91.8 1.3 collective-permute-start.1
  106.1 32.6 %copy-start.6 = (f32[512,128]{1,0:T(8,128)S(1)}, f32[512,128]{1,0:T(8,128)}, u32[]{:S(2)}) copy-start(f32[512,128]{1,0:T(8,128)} %param.24) | copy-start | bytes 786436
  106.1 20.3 %all-to-all-start.5 = ((f32[16,16,1024]{2,1,0:T(8,128)}), f32[16,16,1024]{2,1,0:T(8,128)S(1)}, u32[]{:S(2)}, u32[]{:S(2)}) async-start(f32[16,16,1024]{2,1,0:T(8,128)} %fusion.10), calls=%async_computation.5 | async-start | bytes 2097152 | tf_op jit(solution)/shard_map/all_to_all | solution.py:30
  126.5 1.3 collective-permute-start.2
  127.8 32.8 %copy-start.12 = (f32[16,512]{1,0:T(8,128)S(1)}, f32[16,512]{1,0:T(8,128)}, u32[]{:S(2)}) copy-start(f32[16,512]{1,0:T(8,128)} %param.17) | copy-start | bytes 98308
  140.1 37.3 %copy-start.5 = (f32[512,128]{1,0:T(8,128)S(1)}, f32[512,128]{1,0:T(8,128)}, u32[]{:S(2)}) copy-start(f32[512,128]{1,0:T(8,128)} %param.21) | copy-start | bytes 786436
  140.1 14.4 %all-to-all-start.7 = ((f32[16,16,512]{2,1,0:T(8,128)}), f32[16,16,512]{2,1,0:T(8,128)S(1)}, u32[]{:S(2)}, u32[]{:S(2)}) async-start(f32[16,16,512]{2,1,0:T(8,128)} %fusion.21), calls=%async_computation.7 | async-start | bytes 1048576 | tf_op jit(solution)/shard_map/all_to_all | solution.py:30
  144.0 71.5 %copy-start.19 = (s32[4]{0:T(128)}, s32[4]{0:T(128)S(1)}, u32[]{:S(2)}) copy-start(s32[4]{0:T(128)S(1)} %dynamic-slice_reduce_fusion.1) | copy-start | bytes 52
  144.0 71.5 %copy-start.22 = (s32[16]{0:T(128)}, s32[16]{0:T(128)S(1)}, u32[]{:S(2)}) copy-start(s32[16]{0:T(128)S(1)} %iota_add_fusion.1) | copy-start | bytes 196
  155.0 4.3 collective-permute-start.3
  159.3 1.3 collective-permute-start.4
  160.6 1.3 collective-permute-start.5
  161.9 4.3 collective-permute-start.6
  166.3 44.3 %copy-start.9 = (f32[256,128]{1,0:T(8,128)S(1)}, f32[256,128]{1,0:T(8,128)}, u32[]{:S(2)}) copy-start(f32[256,128]{1,0:T(8,128)} %param.25) | copy-start | bytes 393220
  178.7 36.5 %copy-start.16 = (s32[8]{0:T(128)S(1)}, s32[8]{0:T(128)}, u32[]{:S(2)}) copy-start(s32[8]{0:T(128)} %copy-done.15) | copy-start | bytes 100
  178.7 13.8 %all-to-all-start.9 = ((f32[16,16,512]{2,1,0:T(8,128)}), f32[16,16,512]{2,1,0:T(8,128)S(1)}, u32[]{:S(2)}, u32[]{:S(2)}) async-start(f32[16,16,512]{2,1,0:T(8,128)} %fusion.19), calls=%async_computation.9 | async-start | bytes 1048576 | tf_op jit(solution)/shard_map/all_to_all | solution.py:30
  192.6 1.3 collective-permute-start.7
  192.7 42.7 %copy-start.18 = (f32[16,256]{1,0:T(8,128)S(1)}, f32[16,256]{1,0:T(8,128)}, u32[]{:S(2)}) copy-start(f32[16,256]{1,0:T(8,128)} %param.18) | copy-start | bytes 49156
  193.9 4.3 collective-permute-start.8
  198.9 11.6 %all-to-all-start.10 = ((f32[16,16,128]{2,0,1:T(8,128)}), f32[16,16,128]{2,0,1:T(8,128)S(1)}, u32[]{:S(2)}, u32[]{:S(2)}) async-start(f32[16,16,128]{2,0,1:T(8,128)} %maximum_select_fusion.3), calls=%async_computation.10 | async-start | bytes 262144 | tf_op jit(solution)/shard_map/all_to_all | solution.py:82
  203.5 53.9 %copy-start.25 = (s32[2]{0:T(128)}, s32[2]{0:T(128)S(1)}, u32[]{:S(2)}) copy-start(s32[2]{0:T(128)S(1)} %dynamic-slice_reduce_fusion.2) | copy-start | bytes 28
  203.5 53.9 %copy-start.26 = (s32[16]{0:T(128)}, s32[16]{0:T(128)S(1)}, u32[]{:S(2)}) copy-start(s32[16]{0:T(128)S(1)} %iota_add_fusion) | copy-start | bytes 196
  203.5 53.9 %copy-start.8 = (f32[256,128]{1,0:T(8,128)S(1)}, f32[256,128]{1,0:T(8,128)}, u32[]{:S(2)}) copy-start(f32[256,128]{1,0:T(8,128)} %param.22) | copy-start | bytes 393220
  211.6 12.2 %all-to-all-start.11 = ((f32[16,16,256]{2,1,0:T(8,128)}), f32[16,16,256]{2,1,0:T(8,128)S(1)}, u32[]{:S(2)}, u32[]{:S(2)}) async-start(f32[16,16,256]{2,1,0:T(8,128)} %fusion.27), calls=%async_computation.11 | async-start | bytes 524288 | tf_op jit(solution)/shard_map/all_to_all | solution.py:30
  224.3 5.8 collective-permute-start.9
  230.2 4.0 collective-permute-start.10
  234.2 1.3 collective-permute-start.11
  234.4 58.3 %copy-start.13 = (f32[256]{0:T(256)}, f32[256]{0:T(256)S(1)}, u32[]{:S(2)}) copy-start(f32[256]{0:T(256)S(1)} %dynamic_slice.78) | copy-start | bytes 3076
  235.5 1.3 collective-permute-start.12
  236.7 3.9 collective-permute-start.13
  240.7 5.8 collective-permute-start.14
  258.5 12.2 %all-to-all-start.13 = ((f32[16,16,256]{2,1,0:T(8,128)}), f32[16,16,256]{2,1,0:T(8,128)S(1)}, u32[]{:S(2)}, u32[]{:S(2)}) async-start(f32[16,16,256]{2,1,0:T(8,128)} %fusion.24), calls=%async_computation.13 | async-start | bytes 524288 | tf_op jit(solution)/shard_map/all_to_all | solution.py:30
  270.8 1.3 collective-permute-start.15
  272.0 3.9 collective-permute-start.16
  276.0 5.8 collective-permute-start.17
  324.7 1.4 collective-permute-start.18
  326.1 5.7 collective-permute-start.19
  331.8 6.6 collective-permute-start.20
  339.9 33.6 %all-to-all-start.16 = ((f32[16,256,128]{2,1,0:T(8,128)}), f32[16,256,128]{2,1,0:T(8,128)}, u32[]{:S(2)}, u32[]{:S(2)}) async-start(f32[16,256,128]{2,1,0:T(8,128)} %broadcast_in_dim.17), calls=%async_computation.16 | async-start | bytes 4194304 | tf_op jit(solution)/shard_map/all_to_all | solution.py:36
  375.4 1.3 copy-start.2
  381.4 1.6 copy-start.10
  383.3 1.4 collective-permute-start.21
  384.8 5.6 collective-permute-start.22
  427.4 1.4 collective-permute-start.23
  428.9 5.6 collective-permute-start.24
  436.1 35.5 %all-to-all-start.18 = ((f32[16,256,128]{2,1,0:T(8,128)}), f32[16,256,128]{2,1,0:T(8,128)}, u32[]{:S(2)}, u32[]{:S(2)}) async-start(f32[16,256,128]{2,1,0:T(8,128)} %broadcast_in_dim.19), calls=%async_computation.18 | async-start | bytes 4194304 | tf_op jit(solution)/shard_map/all_to_all | solution.py:36
  477.7 3.1 copy-start.20
  480.8 2.4 copy-start.23
  484.8 1.4 collective-permute-start.25
  525.1 1.4 collective-permute-start.26
  528.1 38.7 %all-to-all-start.20 = ((f32[16,256,128]{2,1,0:T(8,128)}), f32[16,256,128]{2,1,0:T(8,128)}, u32[]{:S(2)}, u32[]{:S(2)}) async-start(f32[16,256,128]{2,1,0:T(8,128)} %broadcast_in_dim.21), calls=%async_computation.20 | async-start | bytes 4194304 | tf_op jit(solution)/shard_map/all_to_all | solution.py:36
  573.1 3.0 copy-start.17
  576.1 2.6 copy-start.1
  576.1 2.6 copy-start.24
  622.0 3.9 copy-start.14
  622.0 32.9 %all-to-all-start.22 = ((f32[16,256,128]{2,1,0:T(8,128)}), f32[16,256,128]{2,1,0:T(8,128)S(1)}, u32[]{:S(2)}, u32[]{:S(2)}) async-start(f32[16,256,128]{2,1,0:T(8,128)} %broadcast_in_dim.23), calls=%async_computation.22 | async-start | bytes 4194304 | tf_op jit(solution)/shard_map/all_to_all | solution.py:36
  (3 other events, 2.8 us)
where the time goes:
time: 671 us; the launch traced here: 660 us
  waiting for transfers between devices  273 us (41%)
  blocking collectives  205 us (31%)
  starting transfers between devices  76.4 us (11%)
  local copies, waits for them, and re-layouts  43.6 us (6%)
  matrix products  36.7 us (5%)
  other arithmetic  20.2 us (3%)
    all_to_all x4, blocking collectives, from_everyone(): return lax.all_to_all(copies, axis, split_axis=0, concat_axis=0, tiled=True)  124 us
    all_to_all x4, waiting for transfers between devices, from_everyone(): return lax.all_to_all(copies, axis, split_axis=0, concat_axis=0, tiled=True)  115 us
    all_to_all x7, waiting for transfers between devices, sent_and_summed(): lax.all_to_all(parts, axis, split_axis=0, concat_axis=0, tiled=True)  98 us
    all_to_all x7, blocking collectives, to_columns(): lax.all_to_all(full_rows, 'panel', split_axis=1, concat_axis=0, tiled=True)  81.3 us
    ppermute x27, waiting for transfers between devices, swapped(): return lax.ppermute(block, axis, route)  53.4 us
    ppermute x27, starting transfers between devices, swapped(): return lax.ppermute(block, axis, route)  29.5 us
    all_to_all x7, starting transfers between devices, sent_and_summed(): lax.all_to_all(parts, axis, split_axis=0, concat_axis=0, tiled=True)  25.8 us
    all_to_all x8, local copies, waits for them, and re-layouts, from_everyone(): return lax.all_to_all(copies, axis, split_axis=0, concat_axis=0, tiled=True)  19.1 us
  transfers between devices with their start and end apart: 39, of which 39 were waited for; matrix products, arithmetic and copies ran while one was open for 2% of the time, Pallas kernels for 0%

commit v1 on v0

v1 whole, which is shorter than its diff:
```python
import functools
import jax
import jax.numpy as jnp
from jax import lax
from jax.experimental import pallas as pl
from jax.experimental.pallas import tpu as pltpu
from jax.sharding import Mesh, PartitionSpec as P

B = 128
ORDER = 2048
NT = 16
f32 = jnp.float32
bf16 = jnp.bfloat16

ZI, YI, CI, X0, X1 = 0, 1, 2, 3, 4
LIVE = 5
TILES = 16


def own_tiles(level):
    return TILES + 16 * level


def partner_tiles(level):
    return TILES + 16 * level + 8


def shift(v, axis, s):
    return lax.ppermute(v, axis, [(i, (i + s) % 4) for i in range(4)])


def flip(v, axis):
    return lax.ppermute(v, axis, [(0, 1), (1, 0)])


def gather4(v, axis):
    return [v] + [shift(v, axis, s) for s in (1, 2, 3)]


def scatter4(parts, axis):
    return [parts[0]] + [shift(parts[s], axis, -s) for s in (1, 2, 3)]


def ring(v, axis, dim):
    h = v.shape[dim] // 2
    a = shift(v, axis, 1)
    b = shift(v, axis, -1)
    c = shift(lax.slice_in_dim(a, 0, h, axis=dim), axis, 1)
    d = shift(lax.slice_in_dim(b, h, 2 * h, axis=dim), axis, -1)
    return [v, a, b, c, d]


def ordered(mine, other, bit, dim):
    return jnp.where(
        bit == 0, jnp.concatenate([mine, other], dim), jnp.concatenate([other, mine], dim)
    )


def halves(v, bit):
    h = v.shape[0] // 2
    return (
        jnp.where(bit == 0, v[:h], v[h:]),
        jnp.where(bit == 0, v[h:], v[:h]),
    )


def stacked(v):
    hi = v.astype(bf16).astype(f32)
    return jnp.concatenate([hi, v - hi], 0).astype(bf16)


def product(left, w, dims):
    hi = w.astype(bf16)
    lo = (w - hi.astype(f32)).astype(bf16)
    r = lax.dot_general(left, hi, (dims, ((), ())), preferred_element_type=f32)
    r = r + lax.dot_general(left, lo, (dims, ((), ())), preferred_element_type=f32)
    n = left.shape[0] // 2
    return r[:n] + r[n:]


NTD = ((1,), (1,))
NND = ((1,), (0,))


def copies_first(meta, e, f, ev, fv, sems):
    zi = meta[ZI]
    out_e, out_f = [], []
    spots = [zi, lax.rem(zi + 3, 4), lax.rem(zi + 1, 4)]
    far = lax.rem(zi + 2, 4)
    k = 0

    def tile(t):
        return pl.ds(pl.multiple_of(t * B, B), B)

    for ref, w in zip(e[:3], spots):
        for s in range(4):
            out_e.append(pltpu.make_async_copy(ref.at[s], ev.at[:, tile(w * 4 + s)], sems.at[k]))
            k += 1
    for ref, base in ((e[3], 0), (e[4], 2)):
        for s in range(2):
            out_e.append(
                pltpu.make_async_copy(ref.at[s], ev.at[:, tile(far * 4 + base + s)], sems.at[k])
            )
            k += 1
    for ref, w in zip(f[:3], spots):
        out_f.append(pltpu.make_async_copy(ref, fv.at[:, tile(w)], sems.at[k]))
        k += 1
    for ref, base in ((f[3], 0), (f[4], 512)):
        out_f.append(pltpu.make_async_copy(ref, fv.at[pl.ds(base, 512), tile(far)], sems.at[k]))
        k += 1
    return out_e, out_f


def copies_upper(meta, bufs, ev, fv, sems):
    ci = meta[CI]
    out_e, out_f = [], []
    k = 0
    for ref, q in ((bufs[0], ci), (bufs[1], 1 - ci)):
        rows = pl.ds(pl.multiple_of(q * 256, 256), 256)
        for w in range(4):
            for s in range(4):
                out_e.append(
                    pltpu.make_async_copy(
                        ref.at[w, pl.ds(s * 256, 256)],
                        ev.at[rows, pl.ds((4 * s + w) * B, B)],
                        sems.at[k],
                    )
                )
                k += 1
    if fv is not None:
        for ref, q in ((bufs[0], ci), (bufs[1], 1 - ci)):
            rows = pl.ds(pl.multiple_of(q * 512, 512), 512)
            for w in range(4):
                out_f.append(
                    pltpu.make_async_copy(
                        ref.at[w, pl.ds(1024, 512)], fv.at[rows, pl.ds(w * B, B)], sems.at[k]
                    )
                )
                k += 1
    return out_e, out_f


def column_mask(meta, level, n):
    col = lax.broadcasted_iota(jnp.int32, (n, ORDER), 1)
    return col < meta[LIVE + level] * B


def row_mask(meta, level, n):
    own = lax.broadcasted_iota(jnp.int32, (n, 512), 1) // B
    tile = 4 * own + meta[YI] if level == 0 else 4 * meta[ZI] + own
    return tile < meta[LIVE + level]


def solve_rows(ev, cs, put):
    def body(j, carry):
        rows = pl.ds(pl.multiple_of(j * 256, 256), 256)
        put(rows, product(cs, ev[rows, :], NTD))
        return carry

    lax.fori_loop(0, 2, body, 0)


def forward_kernel(level, n, mode, meta, *refs):
    count = 10 if level == 0 else 2
    c_refs, refs = refs[:4], refs[4:]
    w_refs, refs = refs[:count], refs[count:]
    if mode == "rs":
        y_out, u_out = refs[:2]
        refs = refs[2:]
    else:
        y_out, keep_out, give_out = refs[:3]
        refs = refs[3:]
    ev, fv, cv, yv, uv, sems = refs
    if level == 0:
        ce, cf = copies_first(meta, w_refs[:5], w_refs[5:], ev, fv, sems)
    else:
        ce, cf = copies_upper(meta, w_refs, ev, fv, sems)
    for c in ce + cf:
        c.start()
    r = n // 4
    if level < 2:
        for s in range(4):
            cv[pl.ds(s * r, r), :] = c_refs[s][...]
        c = cv[...]
    else:
        c = summed(c_refs, r)
    c = jnp.where(column_mask(meta, level, n), c, 0.0)
    cs = stacked(c)
    for c in ce:
        c.wait()
    mask = row_mask(meta, level, n)

    def put_y(rows, v):
        yv[:, rows] = v

    solve_rows(ev, cs, put_y)
    y = jnp.where(mask, yv[...], 0.0)
    y_out[...] = y
    ys = stacked(y)
    for c in cf:
        c.wait()

    def body(j, carry):
        rows = pl.ds(pl.multiple_of(j * 256, 256), 256)
        uv[:, rows] = product(ys, fv[rows, :], NTD)
        return carry

    lax.fori_loop(0, 4, body, 0)
    if mode == "rs":
        for s in range(4):
            u_out[s] = uv[pl.ds(s * r, r), :]
    else:
        split_rows(uv, r, meta[X0] if level == 1 else meta[X1], keep_out, give_out)


def split_rows(v, r, bit, keep_out, give_out):
    h = r // 2
    for s in range(4):
        low = v[pl.ds(s * r, h), :]
        high = v[pl.ds(s * r + h, h), :]
        keep_out[pl.ds(s * h, h), :] = jnp.where(bit == 0, low, high)
        give_out[pl.ds(s * h, h), :] = jnp.where(bit == 0, high, low)


def summed(refs, r):
    parts = []
    for s in range(4):
        total = refs[0][pl.ds(s * r, r), :]
        for d in (1, 2, 3):
            total = total + refs[d][pl.ds((s - d) % 4 * r, r), :]
        parts.append(total)
    return jnp.concatenate(parts, 0)


def add_tiles(meta, at, src, acc):
    for t in range(8):
        v = meta[at + t]
        cols = pl.ds(pl.multiple_of(lax.rem(v, NT) * B, B), B)
        lev = lax.div(v, NT)
        acc[lev, :, cols] = acc[lev, :, cols] + src[:, t * B : (t + 1) * B]


def take_tiles(meta, at, anc, dst):
    for t in range(8):
        v = meta[at + t]
        cols = pl.ds(pl.multiple_of(lax.rem(v, NT) * B, B), B)
        dst[:, t * B : (t + 1) * B] = anc[lax.div(v, NT), :, cols]


def s01_kernel(meta, keep, recv, b1, c1, pk, pg, acc):
    acc[...] = jnp.zeros_like(acc)
    add_tiles(meta, own_tiles(0), keep, acc)
    add_tiles(meta, partner_tiles(0), recv, acc)
    c1[...] = b1[...] - acc[0]
    for i in (0, 1):
        low, high = acc[i + 1, 0:4, :], acc[i + 1, 4:8, :]
        pk[i] = jnp.where(meta[X0] == 0, low, high)
        pg[i] = jnp.where(meta[X0] == 0, high, low)


def s12_kernel(meta, keep, recv, b2, pk, pr, part, keep3, give3, acc):
    acc[...] = jnp.zeros_like(acc)
    add_tiles(meta, own_tiles(1), keep, acc)
    add_tiles(meta, partner_tiles(1), recv, acc)
    part[...] = -acc[0]
    part[0:4, :] = part[0:4, :] + (b2[...] - (pk[0] + pr[0]))
    acc[1, 0:4, :] = acc[1, 0:4, :] + (pk[1] + pr[1])
    split_rows(acc.at[1], 4, meta[X1], keep3, give3)


def s23_kernel(meta, keep, recv, b3, keep3, recv3, part, acc):
    acc[...] = jnp.zeros_like(acc)
    add_tiles(meta, own_tiles(2), keep, acc)
    add_tiles(meta, partner_tiles(2), recv, acc)
    part[...] = -(acc[0] + (keep3[...] + recv3[...]))
    part[0:2, :] = part[0:2, :] + b3[...]


def top_kernel(meta, c0, c1, c2, c3, wa, wb, x_out, ev, yv, sems):
    ce, _ = copies_upper(meta, (wa, wb), ev, None, sems)
    for c in ce:
        c.start()
    c = summed((c0, c1, c2, c3), 2)
    keep = column_mask(meta, 3, 8)
    cs = stacked(jnp.where(keep, c, 0.0))
    for c in ce:
        c.wait()

    def put_y(rows, v):
        yv[:, rows] = v

    solve_rows(ev, cs, put_y)
    y = jnp.where(row_mask(meta, 3, 8), yv[...], 0.0)
    back(meta, 3, 8, ev, y, x_out)


def back(meta, level, n, ev, z, x_out):
    zs = stacked(z)
    live = meta[LIVE + level] * B

    def body(j, carry):
        cols = pl.ds(pl.multiple_of(j * 512, 512), 512)
        v = product(zs, ev[:, cols], NND)
        col = lax.broadcasted_iota(jnp.int32, (n, 512), 1) + j * 512
        x_out[:, cols] = jnp.where(col < live, v, 0.0)
        return carry

    lax.fori_loop(0, 4, body, 0)


def x3_kernel(meta, c0, c1, c2, c3, x_out, give, anc):
    x = summed((c0, c1, c2, c3), 2)
    x_out[...] = x
    anc[0] = x
    take_tiles(meta, partner_tiles(2), anc, give)


def merged(a, b, h, bit):
    parts = []
    for s in range(4):
        u, v = a[s * h : (s + 1) * h, :], b[s * h : (s + 1) * h, :]
        parts += [jnp.where(bit == 0, u, v), jnp.where(bit == 0, v, u)]
    return jnp.concatenate(parts, 0)


def x2_kernel(meta, c0, c1, c2, c3, x3, x3r, anc_out, give):
    anc_out[0] = summed((c0, c1, c2, c3), 4)
    anc_out[1] = merged(x3[...], x3r[...], 2, meta[X1])
    take_tiles(meta, partner_tiles(1), anc_out, give)


def x1_kernel(meta, c0, c1, c2, c3, a_mine, a_other, anc_out, give, own):
    anc_out[0] = (c0[...] + c1[...]) + (c2[...] + c3[...])
    for i in (0, 1):
        u, v = a_mine[i], a_other[i]
        bit = meta[X0]
        anc_out[i + 1, 0:4, :] = jnp.where(bit == 0, u, v)
        anc_out[i + 1, 4:8, :] = jnp.where(bit == 0, v, u)
    take_tiles(meta, partner_tiles(0), anc_out, give)
    take_tiles(meta, own_tiles(0), anc_out, own)


def backward_kernel(level, n, meta, *refs):
    count = 10 if level == 0 else 2
    if level == 0:
        g_refs, refs = refs[:4], refs[4:]
    else:
        (anc, recv), refs = refs[:2], refs[2:]
    y_ref, refs = refs[0], refs[1:]
    w_refs, refs = refs[:count], refs[count:]
    x_out, ev, fv, gv, ov, sems = refs
    if level == 0:
        ce, cf = copies_first(meta, w_refs[:5], w_refs[5:], ev, fv, sems)
    else:
        ce, cf = copies_upper(meta, w_refs, ev, fv, sems)
    for c in cf + ce:
        c.start()
    r = n // 4
    if level == 0:
        for s in range(4):
            gv[pl.ds(s * r, r), :] = g_refs[s][...]
        g = gv[...]
    else:
        take_tiles(meta, own_tiles(level), anc, ov)
        bit = meta[X0] if level == 1 else meta[X1]
        g = merged(ov[...], recv[...], r // 2, bit)
    gs = stacked(g)
    for c in cf:
        c.wait()
    z = y_ref[...] - product(gs, fv[...], NND)
    z = jnp.where(row_mask(meta, level, n), z, 0.0)
    for c in ce:
        c.wait()
    back(meta, level, n, ev, z, x_out)


SMEM = pl.BlockSpec(memory_space=pltpu.SMEM)
VMEM = pl.BlockSpec(memory_space=pltpu.VMEM)
ANY = pl.BlockSpec(memory_space=pl.ANY)


def call(kernel, name, shapes, scratch, meta, small, weights=(), flops=0):
    moved = sum(w.size * 4 for w in weights) + sum(v.size * 4 for v in small)
    return pl.pallas_call(
        kernel,
        out_shape=[jax.ShapeDtypeStruct(s, f32) for s in shapes],
        in_specs=[SMEM] + [VMEM] * len(small) + [ANY] * len(weights),
        out_specs=[VMEM] * len(shapes),
        scratch_shapes=scratch,
        compiler_params=pltpu.CompilerParams(vmem_limit_bytes=24 * 2**20),
        cost_estimate=pl.CostEstimate(flops=flops, bytes_accessed=moved, transcendentals=0),
        name=name,
    )(meta, *small, *weights)


def local(
    live_tiles, row_tiles, rhs0, rhs1, rhs2, rhs3, dinv0, dinv1, dinv2, dinv3, off0, off1, off2
):
    zi, yi = lax.axis_index("z"), lax.axis_index("y")
    ci, x0, x1 = lax.axis_index("core"), lax.axis_index("x0"), lax.axis_index("x1")
    leaf = x1 * 4 + x0 * 2 + ci
    first = [0, 8, 12, 14]
    nodes = [first[k] + leaf // 2**k for k in range(4)]
    partners = [first[k] + (leaf // 2**k ^ 1) for k in range(3)]
    lives = [live_tiles[n] for n in nodes]
    tables = []
    for k in range(3):
        tables += [row_tiles[nodes[k]], row_tiles[partners[k]]]
    head = jnp.stack([zi, yi, ci, x0, x1, *lives] + [jnp.int32(0)] * 7).astype(jnp.int32)
    meta = jnp.concatenate([head, *tables])

    e0 = jnp.swapaxes(dinv0.reshape(4, 4, B, B), 0, 1).reshape(4, 512, B)
    f0 = ring(off0, "z", 0)
    e0 = lax.all_to_all(e0, "y", 0, 0, tiled=True)
    e0 = ring(e0, "z", 0)
    w0 = e0 + f0

    def upper(dinv, off, bits):
        e, f = dinv, off
        for axis, bit in bits:
            e = ordered(e, flip(e, axis), bit, 0)
            if f is not None:
                f = ordered(f, flip(f, axis), bit, 0)
        e = lax.dynamic_index_in_dim(e.reshape(4, 2, 256, B), ci, 1, keepdims=False)
        e = lax.all_to_all(e, "z", 0, 0, tiled=True).reshape(1024, B)
        if f is not None:
            e = jnp.concatenate([e, lax.dynamic_slice_in_dim(f, ci * 512, 512)], 0)
        mine = lax.all_gather(e, "y", axis=0, tiled=False)
        return mine, flip(mine, "core")

    bits = [("core", ci), ("x0", x0), ("x1", x1)]
    w1 = upper(dinv1, off1, bits[:1])
    w2 = upper(dinv2, off2, bits[:2])
    w3 = upper(dinv3, None, bits)

    def spread(rhs, levels):
        v = rhs
        for axis, bit in bits[:levels]:
            keep, give = halves(v, bit)
            v = ordered(keep, flip(give, axis), bit, 1)
        return v

    b1, b2, b3 = spread(rhs1, 1), spread(rhs2, 2), spread(rhs3, 3)

    dma = pltpu.SemaphoreType.DMA
    ev, fv = pltpu.VMEM((512, ORDER), f32), pltpu.VMEM((1024, 512), f32)

    def work(n):
        return [pltpu.VMEM((n, ORDER), f32), pltpu.VMEM((n, 512), f32), pltpu.VMEM((n, 1024), f32)]

    def flops(n):
        return 2 * n * 512 * (2048 + 1024) * 12

    y0, u = call(
        functools.partial(forward_kernel, 0, 64, "rs"), "f0", [(64, 512), (4, 16, 1024)],
        [ev, fv, *work(64), dma((24,))], meta, gather4(rhs0, "y"), w0, flops(64),
    )
    parts = scatter4([u[s] for s in range(4)], "y")
    u = (parts[0] + parts[1]) + (parts[2] + parts[3])
    keep, give = halves(u, ci)
    c1, pk, pg = call(
        s01_kernel, "s01", [(8, ORDER), (2, 4, ORDER), (2, 4, ORDER)],
        [pltpu.VMEM((3, 8, ORDER), f32)], meta, [keep, flip(give, "core"), b1],
    )
    pr = flip(pg, "x0")
    y1, keep, give = call(
        functools.partial(forward_kernel, 1, 32, "ar"), "f1", [(32, 512), (16, 1024), (16, 1024)],
        [ev, fv, *work(32), dma((40,))], meta, gather4(c1, "z"), w1, flops(32),
    )
    part, keep3, give3 = call(
        s12_kernel, "s12", [(16, ORDER), (8, ORDER), (8, ORDER)],
        [pltpu.VMEM((2, 16, ORDER), f32)], meta, [keep, flip(give, "x0"), b2, pk, pr],
    )
    recv3 = flip(give3, "x1")
    y2, keep, give = call(
        functools.partial(forward_kernel, 2, 16, "ar"), "f2", [(16, 512), (8, 1024), (8, 1024)],
        [ev, fv, *work(16), dma((40,))], meta, gather4(part, "z"), w2, flops(16),
    )
    (part,) = call(
        s23_kernel, "s23", [(8, ORDER)],
        [pltpu.VMEM((1, 8, ORDER), f32)], meta, [keep, flip(give, "x1"), b3, keep3, recv3],
    )

    (part,) = call(
        top_kernel, "top", [(8, ORDER)], [ev, pltpu.VMEM((8, 512), f32), dma((32,))],
        meta, gather4(part, "z"), w3, flops(8),
    )
    x3, give = call(
        x3_kernel, "x3", [(8, ORDER), (8, 1024)], [pltpu.VMEM((1, 8, ORDER), f32)],
        meta, gather4(part, "z"),
    )
    recv = flip(give, "x1")
    x3r = flip(x3, "x1")

    def rest(n, small):
        return [ev, fv, pltpu.VMEM((n, 1024), f32), pltpu.VMEM((n // 2, 1024), f32), dma((40,))]

    (part,) = call(
        functools.partial(backward_kernel, 2, 16), "b2", [(16, ORDER)], rest(16, 0),
        meta, [x3[None], recv, y2], w2, flops(16),
    )
    anc, give = call(
        x2_kernel, "x2", [(2, 16, ORDER), (16, 1024)], [],
        meta, gather4(part, "z") + [x3, x3r],
    )
    recv = flip(give, "x0")
    a_mine = anc[:, :4]
    a_other = flip(a_mine, "x0")
    (part,) = call(
        functools.partial(backward_kernel, 1, 32), "b1", [(32, ORDER)], rest(32, 0),
        meta, [anc, recv, y1], w1, flops(32),
    )
    anc, give, own = call(
        x1_kernel, "x1", [(3, 8, ORDER), (8, 1024), (8, 1024)], [],
        meta, scatter4([part[8 * s : 8 * s + 8] for s in range(4)], "z") + [a_mine, a_other],
    )
    g = ordered(own, flip(give, "core"), ci, 0)
    (part,) = call(
        functools.partial(backward_kernel, 0, 64), "b0", [(64, ORDER)], rest(64, 0),
        meta, gather4(g, "y") + [y0], w0, flops(64),
    )
    parts = scatter4([part[16 * s : 16 * s + 16] for s in range(4)], "y")
    sol0 = (parts[0] + parts[1]) + (parts[2] + parts[3])

    outs = [sol0]
    for k in (1, 2, 3):
        width = ORDER // 2**k
        place = leaf % 2**k
        mine = lax.dynamic_slice_in_dim(anc[k - 1], place * width, width, 1)
        give = lax.dynamic_slice_in_dim(anc[k - 1], (place ^ 1) * width, width, 1)
        outs.append(ordered(mine, flip(give, "core"), ci, 0))
    return tuple(outs)


def solution(mesh):
    fine = Mesh(mesh.devices.reshape(2, 2, 2, 4, 4), ("x1", "x0", "core", "z", "y"))
    leaf, panel = ("x1", "x0", "core"), ("z", "y")
    return jax.shard_map(
        local,
        mesh=fine,
        in_specs=(P(), P()) + (P(panel, leaf),) * 4 + (P(leaf, panel),) * 7,
        out_specs=(P(panel, leaf),) * 4,
        check_vma=False,
    )
```

time: 671 us -> 362 us (0.54); the launches traced: 660 us -> 361 us
  blocking collectives: 205 us -> 36.2 us
  waiting for transfers between devices: 273 us -> 145 us
  Pallas kernels: 0 us -> 36.9 us
  matrix products: 36.7 us -> 0 us
  local copies, waits for them, and re-layouts: 43.6 us -> 30.4 us
  between operations: 4.85 us -> 14.5 us
  starting transfers between devices: 76.4 us -> 85 us
  other arithmetic: 20.2 us -> 13.1 us
    all_to_all x12 -> x2, waiting for transfers between devices: 220 us -> 9.34 us  [upper(): e = lax.all_to_all(e, 'z', 0, 0, tiled=True).reshape(1024, B)]
    all_to_all x11 -> x2, blocking collectives: 205 us -> 36.2 us  [the longest x1 24.7 us: local(): e0 = lax.all_to_all(e0, 'y', 0, 0, tiled=True)]
    ppermute x27 -> x69, waiting for transfers between devices: 53.4 us -> 135 us  [the longest x38 74.4 us: shift(): return lax.ppermute(v, axis, [(i, (i + s) % 4) for i in range(4)])]
    ppermute x27 -> x69, starting transfers between devices: 29.5 us -> 76.1 us  [the longest x38 46.4 us: shift(): return lax.ppermute(v, axis, [(i, (i + s) % 4) for i in range(4)])]
    all_to_all x12 -> x2, starting transfers between devices: 46.9 us -> 8.86 us  [upper(): e = lax.all_to_all(e, 'z', 0, 0, tiled=True).reshape(1024, B)]
    pallas_call x0 -> x13, Pallas kernels: none -> 36.9 us  [call(): pl.pallas_call(kernel, out_shape=[jax.ShapeDtypeStruct(s, f32) for s in s...]
    dot_general x26 -> x0, matrix products: 36.7 us -> none  [the longest x7 13.1 us: contract_last(): lax.dot_general(left, right, (((1,), (1,)), ((), ())), precision=highest,...]
    all_to_all x8 -> x0, local copies, waits for them, and re-layouts: 19.1 us -> none  [from_everyone(): return lax.all_to_all(copies, axis, split_axis=0, concat_axis=0, tiled=True)]
  transfers between devices with their start and end apart: 39 -> 74, of which waited for: 39 -> 42; matrix products, arithmetic and copies ran while one was open for 2% -> 6% of each run, Pallas kernels for 0% -> 7%
where the time goes in v1:
time: 362 us; the launch traced here: 361 us
  waiting for transfers between devices  145 us (40%)
  starting transfers between devices  85 us (23%)
  Pallas kernels  36.9 us (10%)
  blocking collectives  36.2 us (10%)
  local copies, waits for them, and re-layouts  30.4 us (8%)
  between operations  14.5 us (4%)
  other arithmetic  13.1 us (4%)
    ppermute x38, waiting for transfers between devices, shift(): return lax.ppermute(v, axis, [(i, (i + s) % 4) for i in range(4)])  74.4 us
    ppermute x31, waiting for transfers between devices, flip(): return lax.ppermute(v, axis, [(0, 1), (1, 0)])  60.8 us
    ppermute x38, starting transfers between devices, shift(): return lax.ppermute(v, axis, [(i, (i + s) % 4) for i in range(4)])  46.4 us
    pallas_call x13, Pallas kernels, call(): pl.pallas_call(kernel, out_shape=[jax.ShapeDtypeStruct(s, f32) for s in s...  36.9 us
    ppermute x31, starting transfers between devices, flip(): return lax.ppermute(v, axis, [(0, 1), (1, 0)])  29.7 us
    all_to_all x1, blocking collectives, local(): e0 = lax.all_to_all(e0, 'y', 0, 0, tiled=True)  24.7 us
    unnamed x78, local copies, waits for them, and re-layouts  19.3 us
    all_to_all x1, blocking collectives, upper(): e = lax.all_to_all(e, 'z', 0, 0, tiled=True).reshape(1024, B)  11.5 us
  transfers between devices with their start and end apart: 74, of which 42 were waited for; matrix products, arithmetic and copies ran while one was open for 6% of the time, Pallas kernels for 7%

profile of v1, /device:TPU:0, one launch (start us, length us, event | category | flops | bytes accessed | tf_op | source)
XLA Modules:
  0.0 360.9 jit_solution(8111504770225975396)
XLA Ops:
  7.3 2.1 collective-permute-done.19
  11.6 5.4 %all-to-all-start.1 = ((f32[4,256,128]{2,1,0:T(8,128)}), f32[4,256,128]{2,1,0:T(8,128)S(1)}, u32[]{:S(2)}, u32[]{:S(2)}) async-start(f32[4,256,128]{2,1,0:T(8,128)} %dynamic-slice_bitcast_fusion.2), calls=%async_computation.1 | async-start | bytes 1048576 | tf_op jit(solution)/shard_map/all_to_all | solution.py:425
  18.7 8.0 %all-to-all-done.1 = f32[4,256,128]{2,1,0:T(8,128)S(1)} async-done(((f32[4,256,128]{2,1,0:T(8,128)}), f32[4,256,128]{2,1,0:T(8,128)S(1)}, u32[]{:S(2)}, u32[]{:S(2)}) %all-to-all-start.1) | async-done | bytes 524320 | tf_op jit(solution)/shard_map/all_to_all | solution.py:425
  29.4 1.6 collective-permute-start.30
  31.0 12.5 %collective-permute-done.30 = f32[1024,128]{1,0:T(8,128)S(1)} collective-permute-done((f32[1024,128]{1,0:T(8,128)S(1)}, f32[1024,128]{1,0:T(8,128)S(1)}, u32[]{:S(2)}, u32[]{:S(2)}) %collective-permute-start.30) | collective-permute-done | bytes 524320 | tf_op jit(solution)/shard_map/ppermute | solution.py:33
  44.5 3.5 all-to-all-start.2
  48.0 1.6 collective-permute-start.32
  49.6 6.1 %collective-permute-done.32 = f32[512,128]{1,0:T(8,128)S(1)} collective-permute-done((f32[512,128]{1,0:T(8,128)S(1)}, f32[512,128]{1,0:T(8,128)S(1)}, u32[]{:S(2)}, u32[]{:S(2)}) %collective-permute-start.32) | collective-permute-done | bytes 262176 | tf_op jit(solution)/shard_map/ppermute | solution.py:33
  59.7 1.6 collective-permute-start.43
  61.3 6.9 %collective-permute-done.43 = f32[512,128]{1,0:T(8,128)S(1)} collective-permute-done((f32[512,128]{1,0:T(8,128)S(1)}, f32[512,128]{1,0:T(8,128)S(1)}, u32[]{:S(2)}, u32[]{:S(2)}) %collective-permute-start.43) | collective-permute-done | bytes 262176 | tf_op jit(solution)/shard_map/ppermute | solution.py:33
  68.2 3.1 collective-permute-start.44
  71.3 11.6 %collective-permute-done.44 = f32[1024,128]{1,0:T(8,128)S(1)} collective-permute-done((f32[1024,128]{1,0:T(8,128)S(1)}, f32[1024,128]{1,0:T(8,128)S(1)}, u32[]{:S(2)}, u32[]{:S(2)}) %collective-permute-start.44) | collective-permute-done | bytes 524320 | tf_op jit(solution)/shard_map/ppermute | solution.py:33
  83.1 11.5 %all_to_all.20 = f32[4,256,128]{2,1,0:T(8,128)} all-to-all(f32[4,256,128]{2,1,0:T(8,128)S(1)} %dynamic-slice_bitcast_fusion), channel_id=1, replica_groups=mesh['x1'=2,'x0'=2,'core'=2,'z'=4,'y'=4] {'z'}, dimensions={0} | all-to-all | bytes 1048576 | tf_op jit(solution)/shard_map/all_to_all | solution.py:425
  94.8 24.7 %all_to_all.21.refs_4_.refs_5_ = f32[4,512,128]{2,1,0:T(8,128)S(1)} all-to-all(f32[4,512,128]{2,1,0:T(8,128)S(1)} %bitcast.53), channel_id=1, replica_groups=mesh['x1'=2,'x0'=2,'core'=2,'z'=4,'y'=4] {'y'}, dimensions={0} | all-to-all | bytes 2097152 | tf_op jit(solution)/shard_map/all_to_all | solution.py:414
  119.5 1.6 collective-permute-start.3
  121.1 1.7 collective-permute-start.4
  124.3 4.8 %collective-permute-done.35 = f32[8,256]{1,0:T(8,128)S(1)} collective-permute-done((f32[8,256]{1,0:T(8,128)S(1)}, f32[8,256]{1,0:T(8,128)S(1)}, u32[]{:S(2)}, u32[]{:S(2)}) %collective-permute-start.35) | collective-permute-done | bytes 8224 | tf_op jit(solution)/shard_map/ppermute | solution.py:33
  129.1 1.8 collective-permute-start.8
  131.5 2.0 collective-permute-start.1
  133.6 8.3 %collective-permute-done.1.refs_2_ = f32[16,2048]{1,0:T(8,128)S(1)} collective-permute-done((f32[16,2048]{1,0:T(8,128)S(1)}, f32[16,2048]{1,0:T(8,128)S(1)}, u32[]{:S(2)}, u32[]{:S(2)}) %collective-permute-start.1) | collective-permute-done | bytes 131104 | tf_op jit(solution)/shard_map/ppermute | solution.py:29
  142.5 13.3 %collective-permute-done.8.refs_11_.refs_12_ = f32[1024,128]{1,0:T(8,128)} collective-permute-done((f32[1024,128]{1,0:T(8,128)}, f32[1024,128]{1,0:T(8,128)}, u32[]{:S(2)}, u32[]{:S(2)}) %collective-permute-start.8) | collective-permute-done | bytes 524320 | tf_op jit(solution)/shard_map/ppermute | solution.py:29
  155.8 1.7 collective-permute-start.2
  157.5 1.7 slice.156
  159.2 3.0 collective-permute-start.10
  164.9 3.2 concatenate.123.meta
  168.2 3.2 collective-permute-start.6
  177.3 11.5 %collective-permute-done.9.refs_12_.refs_13_ = f32[512,128]{1,0:T(8,128)S(1)} collective-permute-done((f32[512,128]{1,0:T(8,128)S(1)}, f32[512,128]{1,0:T(8,128)S(1)}, u32[]{:S(2)}, u32[]{:S(2)}) %collective-permute-start.9) | collective-permute-done | bytes 262176 | tf_op jit(solution)/shard_map/ppermute | solution.py:29
  189.1 1.7 copy-done.4
  197.0 5.1 %f0.1 = (f32[64,512]{1,0:T(8,128)S(1)}, f32[4,16,1024]{2,1,0:T(8,128)S(1)}) custom-call(s32[64]{0:T(128)S(1)} %concatenate.123.meta, f32[16,2048]{1,0:T(8,128)S(1)} %copy-done.23, f32[16,2048]{1,0:T(8,128)S(1)} %copy-done.25, f32[16,2048]{1,0:T(8,128)S(1)} %copy-done.27, f32[16,2048]{1,0:T(8,128)} %collective-permute-done.2.refs_3_, ...), custom_call_target="tpu_custom_call" | custom-call | flops 2415919104 | bytes 6815744 | tf_op jit(solution)/shard_map/f0/pallas_call | solution.py:384
  204.7 2.1 collective-permute-start.12
  209.2 1.9 collective-permute-done.12
  211.1 2.4 collective-permute-done.13
  218.1 5.7 %collective-permute-done.16.refs_1_ = f32[8,2048]{1,0:T(8,128)S(1)} collective-permute-done((f32[8,2048]{1,0:T(8,128)S(1)}, f32[8,2048]{1,0:T(8,128)S(1)}, u32[]{:S(2)}, u32[]{:S(2)}) %collective-permute-start.16) | collective-permute-done | bytes 65568 | tf_op jit(solution)/shard_map/ppermute | solution.py:29
  224.3 3.7 %collective-permute-done.18.refs_3_ = f32[8,2048]{1,0:T(8,128)S(1)} collective-permute-done((f32[8,2048]{1,0:T(8,128)S(1)}, f32[8,2048]{1,0:T(8,128)S(1)}, u32[]{:S(2)}, u32[]{:S(2)}) %collective-permute-start.18) | collective-permute-done | bytes 65568 | tf_op jit(solution)/shard_map/ppermute | solution.py:29
  228.0 5.6 %f1.1 = (f32[32,512]{1,0:T(8,128)S(1)}, f32[16,1024]{1,0:T(8,128)S(1)}, f32[16,1024]{1,0:T(8,128)S(1)}) custom-call(s32[64]{0:T(128)S(1)} %concatenate.123.meta, f32[8,2048]{1,0:T(8,128)S(1)} %get-tuple-element.26.refs_0_, f32[8,2048]{1,0:T(8,128)S(1)} %collective-permute-done.16.refs_1_, f32[8,2048]{1,0:T(8,128)S(1)} %collective-permute-done.17.refs_2_, ...), custom_call_target="tpu_custom_call" | custom-call | flops 1207959552 | bytes 6553600 | tf_op jit(solution)/shard_map/f1/pallas_call | solution.py:384
  233.7 2.0 collective-permute-start.22
  235.7 2.3 collective-permute-done.22.recv
  238.9 2.7 collective-permute-start.27
  242.1 4.3 %collective-permute-done.26.refs_1_ = f32[16,2048]{1,0:T(8,128)S(1)} collective-permute-done((f32[16,2048]{1,0:T(8,128)S(1)}, f32[16,2048]{1,0:T(8,128)S(1)}, u32[]{:S(2)}, u32[]{:S(2)}) %collective-permute-start.26) | collective-permute-done | bytes 131104 | tf_op jit(solution)/shard_map/ppermute | solution.py:29
  246.4 3.4 collective-permute-start.37
  250.0 5.4 %f2.1 = (f32[16,512]{1,0:T(8,128)S(1)}, f32[8,1024]{1,0:T(8,128)S(1)}, f32[8,1024]{1,0:T(8,128)S(1)}) custom-call(s32[64]{0:T(128)S(1)} %concatenate.123.meta, f32[16,2048]{1,0:T(8,128)S(1)} %get-tuple-element.31.refs_0_, f32[16,2048]{1,0:T(8,128)S(1)} %collective-permute-done.26.refs_1_, f32[16,2048]{1,0:T(8,128)S(1)} %collective-permute-done.27.refs_2_, ...), custom_call_target="tpu_custom_call" | custom-call | flops 603979776 | bytes 6815744 | tf_op jit(solution)/shard_map/f2/pallas_call | solution.py:384
  255.3 3.5 collective-permute-start.34
  258.9 2.0 collective-permute-done.34.recv
  261.6 3.6 collective-permute-start.40
  269.4 4.1 %top.1.c0 = f32[8,2048]{1,0:T(8,128)S(1)} custom-call(s32[64]{0:T(128)S(1)} %concatenate.123.meta, f32[8,2048]{1,0:T(8,128)S(1)} %s23.1.c0, f32[8,2048]{1,0:T(8,128)S(1)} %collective-permute-done.39.c1, f32[8,2048]{1,0:T(8,128)S(1)} %collective-permute-done.40.c2, f32[8,2048]{1,0:T(8,128)S(1)} %collective-permute-done.41.c3, f32[4,1024,128]{2,1,0:T(8,128)S(1)} %copy-done.2, ...), custom_call_target="tpu_custom_call" | custom-call | flops 301989888 | bytes 4456448 | tf_op jit(solution)/shard_map/top/pallas_call | solution.py:384
  274.1 2.8 collective-permute-start.47
  281.8 3.2 collective-permute-start.49
  285.0 2.3 collective-permute-done.49.refs_1_
  287.3 4.2 %b2.1.c0 = f32[16,2048]{1,0:T(8,128)S(1)} custom-call(s32[64]{0:T(128)S(1)} %concatenate.123.meta, f32[1,8,2048]{2,1,0:T(8,128)S(1)} %bitcast.52, f32[8,1024]{1,0:T(8,128)S(1)} %collective-permute-done.49.refs_1_, f32[16,512]{1,0:T(8,128)S(1)} %get-tuple-element.38.refs_2_, f32[4,1536,128]{2,1,0:T(8,128)S(1)} %bitcast.51, ...), custom_call_target="tpu_custom_call" | custom-call | flops 603979776 | bytes 6422528 | tf_op jit(solution)/shard_map/b2/pallas_call | solution.py:384
  292.4 2.8 collective-permute-start.51
  295.7 3.1 collective-permute-start.53
  298.9 2.6 collective-permute-done.53.x3r
  302.2 1.7 collective-permute-start.54
  304.4 2.1 collective-permute-done.54.refs_1_
  306.5 4.3 %b1.1 = f32[32,2048]{1,0:T(8,128)S(1)} custom-call(s32[64]{0:T(128)S(1)} %concatenate.123.meta, f32[2,16,2048]{2,1,0:T(8,128)S(1)} %get-tuple-element.39.refs_0_, f32[16,1024]{1,0:T(8,128)S(1)} %collective-permute-done.54.refs_1_, f32[32,512]{1,0:T(8,128)S(1)} %get-tuple-element.41.refs_2_, f32[4,1536,128]{2,1,0:T(8,128)S(1)} %bitcast.48, ...), custom_call_target="tpu_custom_call" | custom-call | flops 1207959552 | bytes 6684672 | tf_op jit(solution)/shard_map/b1/pallas_call | solution.py:384
  312.1 2.4 collective-permute-start.56
  315.2 2.7 collective-permute-done.56.c2
  317.9 2.1 collective-permute-done.57.c3
  322.5 1.9 collective-permute-start.61
  326.4 2.9 collective-permute-done.60.refs_1_
  338.5 4.3 %b0.1 = f32[64,2048]{1,0:T(8,128)S(1)} custom-call(s32[64]{0:T(128)S(1)} %concatenate.123.meta, f32[16,1024]{1,0:T(8,128)S(1)} %maximum_select_fusion.8.refs_0_, f32[16,1024]{1,0:T(8,128)S(1)} %collective-permute-done.60.refs_1_, f32[16,1024]{1,0:T(8,128)S(1)} %collective-permute-done.61.refs_2_, f32[16,1024]{1,0:T(8,128)S(1)} %collective-permute-done.62.refs_3_, ...), custom_call_target="tpu_custom_call" | custom-call | flops 2415919104 | bytes 6684672 | tf_op jit(solution)/shard_map/b0/pallas_call | solution.py:384
  342.8 2.5 collective-permute-start.63
  347.5 2.8 collective-permute-done.63
  350.3 2.4 collective-permute-done.64
  (231 shorter events, 74.2 us)
Async XLA Ops:
  11.6 15.2 %all-to-all-start.1 = ((f32[4,256,128]{2,1,0:T(8,128)}), f32[4,256,128]{2,1,0:T(8,128)S(1)}, u32[]{:S(2)}, u32[]{:S(2)}) async-start(f32[4,256,128]{2,1,0:T(8,128)} %dynamic-slice_bitcast_fusion.2), calls=%async_computation.1 | async-start | bytes 1048576 | tf_op jit(solution)/shard_map/all_to_all | solution.py:425
  17.0 106.9 %all-gather.8.cloned.1.call-start = ((), (), s32[]{:S(2)}) async-start(), calls=%async_computation.5 | async-start | bytes 3932160 | tf_op jit(solution)/shard_map/all_gather | solution.py:428
  29.4 14.0 %collective-permute-start.30 = (f32[1024,128]{1,0:T(8,128)S(1)}, f32[1024,128]{1,0:T(8,128)S(1)}, u32[]{:S(2)}, u32[]{:S(2)}) collective-permute-start(f32[1024,128]{1,0:T(8,128)S(1)} %maximum_select_fusion.3), channel_id=1, source_target_pairs={{0,32},{32,0},{1,33},{33,1},{2,34},{34,2},{3,35},{35,3},{4,36},{36... | collective-permute-start | bytes 1572872 | tf_op jit(solution)/shard_map/ppermute | solution.py:33
  31.0 17.0 %collective-permute-start.31 = (f32[256,128]{1,0:T(8,128)S(1)}, f32[256,128]{1,0:T(8,128)S(1)}, u32[]{:S(2)}, u32[]{:S(2)}) collective-permute-start(f32[256,128]{1,0:T(8,128)S(1)} %copy-done.34), channel_id=1, source_target_pairs={{0,16},{16,0},{1,17},{17,1},{2,18},{18,2},{3,19},{19,3},{4,20},{20... | collective-permute-start | bytes 393224 | tf_op jit(solution)/shard_map/ppermute | solution.py:33
  44.5 12.8 %all-to-all-start.2 = ((f32[4,256,128]{2,1,0:T(8,128)}), f32[4,256,128]{2,1,0:T(8,128)S(1)}, u32[]{:S(2)}, u32[]{:S(2)}) async-start(f32[4,256,128]{2,1,0:T(8,128)} %dynamic-slice_bitcast_fusion.1), calls=%async_computation.2 | async-start | bytes 1048576 | tf_op jit(solution)/shard_map/all_to_all | solution.py:425
  47.9 107.9 %all-gather.10.cloned.1.call-start = ((), (), s32[]{:S(2)}) async-start(), calls=%async_computation.6 | async-start | bytes 3932160 | tf_op jit(solution)/shard_map/all_gather | solution.py:428
  48.0 7.7 %collective-permute-start.32 = (f32[512,128]{1,0:T(8,128)S(1)}, f32[512,128]{1,0:T(8,128)S(1)}, u32[]{:S(2)}, u32[]{:S(2)}) collective-permute-start(f32[512,128]{1,0:T(8,128)S(1)} %maximum_select_fusion.5), channel_id=1, source_target_pairs={{0,32},{32,0},{1,33},{33,1},{2,34},{34,2},{3,35},{35,3},{4,36},{36... | collective-permute-start | bytes 786440 | tf_op jit(solution)/shard_map/ppermute | solution.py:33
  58.2 145.7 %all-gather.6.cloned.1.call-start = ((), (), s32[]{:S(2)}) async-start(), calls=%async_computation.4 | async-start | bytes 2621440 | tf_op jit(solution)/shard_map/all_gather | solution.py:428
  59.7 8.4 %collective-permute-start.43 = (f32[512,128]{1,0:T(8,128)S(1)}, f32[512,128]{1,0:T(8,128)S(1)}, u32[]{:S(2)}, u32[]{:S(2)}) collective-permute-start(f32[512,128]{1,0:T(8,128)S(1)} %maximum_select_fusion.6), channel_id=1, source_target_pairs={{0,32},{32,0},{1,33},{33,1},{2,34},{34,2},{3,35},{35,3},{4,36},{36... | collective-permute-start | bytes 786440 | tf_op jit(solution)/shard_map/ppermute | solution.py:33
  68.2 14.7 %collective-permute-start.44 = (f32[1024,128]{1,0:T(8,128)S(1)}, f32[1024,128]{1,0:T(8,128)S(1)}, u32[]{:S(2)}, u32[]{:S(2)}) collective-permute-start(f32[1024,128]{1,0:T(8,128)S(1)} %maximum_select_fusion.4), channel_id=1, source_target_pairs={{0,64},{64,0},{1,65},{65,1},{2,66},{66,2},{3,67},{67,3},{4,68},{68... | collective-permute-start | bytes 1572872 | tf_op jit(solution)/shard_map/ppermute | solution.py:33
  119.5 36.3 %collective-permute-start.3 = (f32[4,512,128]{2,1,0:T(8,128)S(1)}, f32[4,512,128]{2,1,0:T(8,128)S(1)}, u32[]{:S(2)}, u32[]{:S(2)}) collective-permute-start(f32[4,512,128]{2,1,0:T(8,128)S(1)} %all_to_all.21.refs_4_.refs_5_), channel_id=1, source_target_pairs={{0,4},{4,8},{8,12},{12,0},{1,5},{5,9},{9,13},{13,1},{2,6},{6,10},{... | collective-permute-start | bytes 3145736 | tf_op jit(solution)/shard_map/ppermute | solution.py:29
  121.1 38.1 %collective-permute-start.4 = (f32[4,512,128]{2,1,0:T(8,128)S(1)}, f32[4,512,128]{2,1,0:T(8,128)S(1)}, u32[]{:S(2)}, u32[]{:S(2)}) collective-permute-start(f32[4,512,128]{2,1,0:T(8,128)S(1)} %all_to_all.21.refs_4_.refs_5_), channel_id=1, source_target_pairs={{0,12},{4,0},{8,4},{12,8},{1,13},{5,1},{9,5},{13,9},{2,14},{6,2},{... | collective-permute-start | bytes 3145736 | tf_op jit(solution)/shard_map/ppermute | solution.py:29
  122.8 8.1 %collective-permute-start = (f32[16,2048]{1,0:T(8,128)S(1)}, f32[16,2048]{1,0:T(8,128)S(1)}, u32[]{:S(2)}, u32[]{:S(2)}) collective-permute-start(f32[16,2048]{1,0:T(8,128)S(1)} %copy-done.23), channel_id=1, source_target_pairs={{0,1},{1,2},{2,3},{3,0},{4,5},{5,6},{6,7},{7,4},{8,9},{9,10},{10,1... | collective-permute-start | bytes 393224 | tf_op jit(solution)/shard_map/ppermute | solution.py:29
  123.8 104.2 %collective-permute-start.21 = (f32[4,1536,128]{2,1,0:T(8,128)}, f32[4,1536,128]{2,1,0:T(8,128)}, u32[]{:S(2)}, u32[]{:S(2)}) collective-permute-start(f32[4,1536,128]{2,1,0:T(8,128)} %bitcast.46), channel_id=1, source_target_pairs={{0,16},{16,0},{1,17},{17,1},{2,18},{18,2},{3,19},{19,3},{4,20},{20... | collective-permute-start | bytes 9437192 | tf_op jit(solution)/shard_map/ppermute | solution.py:33
  123.8 5.3 %collective-permute-start.35 = (f32[8,256]{1,0:T(8,128)S(1)}, f32[8,256]{1,0:T(8,128)S(1)}, u32[]{:S(2)}, u32[]{:S(2)}) collective-permute-start(f32[8,256]{1,0:T(8,128)S(1)} %get-tuple-element.84), channel_id=1, source_target_pairs={{0,16},{16,0},{1,17},{17,1},{2,18},{18,2},{3,19},{19,3},{4,20},{20... | collective-permute-start | bytes 24584 | tf_op jit(solution)/shard_map/ppermute | solution.py:33
  129.1 26.7 %collective-permute-start.8 = (f32[1024,128]{1,0:T(8,128)}, f32[1024,128]{1,0:T(8,128)}, u32[]{:S(2)}, u32[]{:S(2)}) collective-permute-start(f32[1024,128]{1,0:T(8,128)} %refs_10_.1), channel_id=1, source_target_pairs={{0,12},{4,0},{8,4},{12,8},{1,13},{5,1},{9,5},{13,9},{2,14},{6,2},{... | collective-permute-start | bytes 1572872 | tf_op jit(solution)/shard_map/ppermute | solution.py:29
  131.5 10.3 %collective-permute-start.1 = (f32[16,2048]{1,0:T(8,128)S(1)}, f32[16,2048]{1,0:T(8,128)S(1)}, u32[]{:S(2)}, u32[]{:S(2)}) collective-permute-start(f32[16,2048]{1,0:T(8,128)S(1)} %copy-done.23), channel_id=1, source_target_pairs={{0,2},{1,3},{2,0},{3,1},{4,6},{5,7},{6,4},{7,5},{8,10},{9,11},{10,... | collective-permute-start | bytes 393224 | tf_op jit(solution)/shard_map/ppermute | solution.py:29
  142.5 25.8 %collective-permute-start.7 = (f32[1024,128]{1,0:T(8,128)}, f32[1024,128]{1,0:T(8,128)}, u32[]{:S(2)}, u32[]{:S(2)}) collective-permute-start(f32[1024,128]{1,0:T(8,128)} %refs_10_.1), channel_id=1, source_target_pairs={{0,4},{4,8},{8,12},{12,0},{1,5},{5,9},{9,13},{13,1},{2,6},{6,10},{... | collective-permute-start | bytes 1572872 | tf_op jit(solution)/shard_map/ppermute | solution.py:29
  155.8 94.1 %collective-permute-start.33 = (f32[4,1536,128]{2,1,0:T(8,128)}, f32[4,1536,128]{2,1,0:T(8,128)}, u32[]{:S(2)}, u32[]{:S(2)}) collective-permute-start(f32[4,1536,128]{2,1,0:T(8,128)} %bitcast.49), channel_id=1, source_target_pairs={{0,16},{16,0},{1,17},{17,1},{2,18},{18,2},{3,19},{19,3},{4,20},{20... | collective-permute-start | bytes 9437192 | tf_op jit(solution)/shard_map/ppermute | solution.py:33
  155.8 12.3 %collective-permute-start.2 = (f32[16,2048]{1,0:T(8,128)S(1)}, f32[16,2048]{1,0:T(8,128)}, u32[]{:S(2)}, u32[]{:S(2)}) collective-permute-start(f32[16,2048]{1,0:T(8,128)S(1)} %copy-done.23), channel_id=1, source_target_pairs={{0,3},{1,0},{2,1},{3,2},{4,7},{5,4},{6,5},{7,6},{8,11},{9,8},{10,9... | collective-permute-start | bytes 393224 | tf_op jit(solution)/shard_map/ppermute | solution.py:29
  159.2 14.6 %collective-permute-start.10 = (f32[512,128]{1,0:T(8,128)}, f32[512,128]{1,0:T(8,128)S(1)}, u32[]{:S(2)}, u32[]{:S(2)}) collective-permute-start(f32[512,128]{1,0:T(8,128)} %slice.156), channel_id=1, source_target_pairs={{0,12},{4,0},{8,4},{12,8},{1,13},{5,1},{9,5},{13,9},{2,14},{6,2},{... | collective-permute-start | bytes 786440 | tf_op jit(solution)/shard_map/ppermute | solution.py:29
  168.2 20.9 %collective-permute-start.5 = (f32[2,512,128]{2,1,0:T(8,128)S(1)}, f32[2,512,128]{2,1,0:T(8,128)S(1)}, u32[]{:S(2)}, u32[]{:S(2)}) collective-permute-start(f32[2,512,128]{2,1,0:T(8,128)S(1)} %slice.153), channel_id=1, source_target_pairs={{0,4},{4,8},{8,12},{12,0},{1,5},{5,9},{9,13},{13,1},{2,6},{6,10},{... | collective-permute-start | bytes 1572872 | tf_op jit(solution)/shard_map/ppermute | solution.py:29
  168.2 20.8 %collective-permute-start.6 = (f32[2,512,128]{2,1,0:T(8,128)S(1)}, f32[2,512,128]{2,1,0:T(8,128)S(1)}, u32[]{:S(2)}, u32[]{:S(2)}) collective-permute-start(f32[2,512,128]{2,1,0:T(8,128)S(1)} %slice.154), channel_id=1, source_target_pairs={{0,12},{4,0},{8,4},{12,8},{1,13},{5,1},{9,5},{13,9},{2,14},{6,2},{... | collective-permute-start | bytes 1572872 | tf_op jit(solution)/shard_map/ppermute | solution.py:29
  174.6 14.2 %collective-permute-start.9 = (f32[512,128]{1,0:T(8,128)S(1)}, f32[512,128]{1,0:T(8,128)S(1)}, u32[]{:S(2)}, u32[]{:S(2)}) collective-permute-start(f32[512,128]{1,0:T(8,128)S(1)} %slice.155), channel_id=1, source_target_pairs={{0,4},{4,8},{8,12},{12,0},{1,5},{5,9},{9,13},{13,1},{2,6},{6,10},{... | collective-permute-start | bytes 786440 | tf_op jit(solution)/shard_map/ppermute | solution.py:29
  188.8 16.0 %collective-permute-start.23 = (f32[8,512]{1,0:T(8,128)}, f32[8,512]{1,0:T(8,128)}, u32[]{:S(2)}, u32[]{:S(2)}) collective-permute-start(f32[8,512]{1,0:T(8,128)} %get-tuple-element.78), channel_id=1, source_target_pairs={{0,16},{16,0},{1,17},{17,1},{2,18},{18,2},{3,19},{19,3},{4,20},{20... | collective-permute-start | bytes 49160 | tf_op jit(solution)/shard_map/ppermute | solution.py:33
  203.5 4.5 %collective-permute-start.11 = (f32[16,1024]{1,0:T(8,128)}, f32[16,1024]{1,0:T(8,128)S(1)}, u32[]{:S(2)}, u32[]{:S(2)}) collective-permute-start(f32[16,1024]{1,0:T(8,128)} %get-tuple-element.61), channel_id=1, source_target_pairs={{0,3},{1,0},{2,1},{3,2},{4,7},{5,4},{6,5},{7,6},{8,11},{9,8},{10,9... | collective-permute-start | bytes 196616 | tf_op jit(solution)/shard_map/ppermute | solution.py:29
  203.9 61.7 %collective-permute-start.45 = (f32[4,1024,128]{2,1,0:T(8,128)}, f32[4,1024,128]{2,1,0:T(8,128)S(1)}, u32[]{:S(2)}, u32[]{:S(2)}) collective-permute-start(f32[4,1024,128]{2,1,0:T(8,128)} %all-gather.6.cloned.1.call-done.wa), channel_id=1, source_target_pairs={{0,16},{16,0},{1,17},{17,1},{2,18},{18,2},{3,19},{19,3},{4,20},{20... | collective-permute-start | bytes 6291464 | tf_op jit(solution)/shard_map/ppermute | solution.py:33
  204.7 6.3 %collective-permute-start.12 = (f32[16,1024]{1,0:T(8,128)}, f32[16,1024]{1,0:T(8,128)S(1)}, u32[]{:S(2)}, u32[]{:S(2)}) collective-permute-start(f32[16,1024]{1,0:T(8,128)} %get-tuple-element.60), channel_id=1, source_target_pairs={{0,2},{1,3},{2,0},{3,1},{4,6},{5,7},{6,4},{7,5},{8,10},{9,11},{10,... | collective-permute-start | bytes 196616 | tf_op jit(solution)/shard_map/ppermute | solution.py:29
  208.0 5.5 %collective-permute-start.13 = (f32[16,1024]{1,0:T(8,128)S(1)}, f32[16,1024]{1,0:T(8,128)S(1)}, u32[]{:S(2)}, u32[]{:S(2)}) collective-permute-start(f32[16,1024]{1,0:T(8,128)S(1)} %get-tuple-element.59), channel_id=1, source_target_pairs={{0,1},{1,2},{2,3},{3,0},{4,5},{5,6},{6,7},{7,4},{8,9},{9,10},{10,1... | collective-permute-start | bytes 196616 | tf_op jit(solution)/shard_map/ppermute | solution.py:29
  216.9 6.8 %collective-permute-start.16 = (f32[8,2048]{1,0:T(8,128)S(1)}, f32[8,2048]{1,0:T(8,128)S(1)}, u32[]{:S(2)}, u32[]{:S(2)}) collective-permute-start(f32[8,2048]{1,0:T(8,128)S(1)} %get-tuple-element.26.refs_0_), channel_id=1, source_target_pairs={{0,4},{4,8},{8,12},{12,0},{1,5},{5,9},{9,13},{13,1},{2,6},{6,10},{... | collective-permute-start | bytes 196616 | tf_op jit(solution)/shard_map/ppermute | solution.py:29
  217.1 6.7 %collective-permute-start.17 = (f32[8,2048]{1,0:T(8,128)S(1)}, f32[8,2048]{1,0:T(8,128)S(1)}, u32[]{:S(2)}, u32[]{:S(2)}) collective-permute-start(f32[8,2048]{1,0:T(8,128)S(1)} %get-tuple-element.26.refs_0_), channel_id=1, source_target_pairs={{0,8},{4,12},{8,0},{12,4},{1,9},{5,13},{9,1},{13,5},{2,10},{6,14},... | collective-permute-start | bytes 196616 | tf_op jit(solution)/shard_map/ppermute | solution.py:29
  223.8 11.9 %collective-permute-start.24 = (f32[4,1024]{1,0:T(4,128)S(1)}, f32[4,1024]{1,0:T(4,128)S(1)}, u32[]{:S(2)}, u32[]{:S(2)}) collective-permute-start(f32[4,1024]{1,0:T(4,128)S(1)} %get-tuple-element.76), channel_id=1, source_target_pairs={{0,32},{32,0},{1,33},{33,1},{2,34},{34,2},{3,35},{35,3},{4,36},{36... | collective-permute-start | bytes 49160 | tf_op jit(solution)/shard_map/ppermute | solution.py:33
  228.0 7.7 %collective-permute-start.25 = (f32[2,4,2048]{2,1,0:T(4,128)S(1)}, f32[2,4,2048]{2,1,0:T(4,128)S(1)}, u32[]{:S(2)}, u32[]{:S(2)}) collective-permute-start(f32[2,4,2048]{2,1,0:T(4,128)S(1)} %get-tuple-element.30), channel_id=1, source_target_pairs={{0,32},{32,0},{1,33},{33,1},{2,34},{34,2},{3,35},{35,3},{4,36},{36... | collective-permute-start | bytes 196616 | tf_op jit(solution)/shard_map/ppermute | solution.py:33
  233.7 4.3 %collective-permute-start.22 = (f32[16,1024]{1,0:T(8,128)S(1)}, f32[16,1024]{1,0:T(8,128)S(1)}, u32[]{:S(2)}, u32[]{:S(2)}) collective-permute-start(f32[16,1024]{1,0:T(8,128)S(1)} %get-tuple-element.28), channel_id=1, source_target_pairs={{0,32},{32,0},{1,33},{33,1},{2,34},{34,2},{3,35},{35,3},{4,36},{36... | collective-permute-start | bytes 196616 | tf_op jit(solution)/shard_map/ppermute | solution.py:33
  238.8 7.7 %collective-permute-start.26 = (f32[16,2048]{1,0:T(8,128)S(1)}, f32[16,2048]{1,0:T(8,128)S(1)}, u32[]{:S(2)}, u32[]{:S(2)}) collective-permute-start(f32[16,2048]{1,0:T(8,128)S(1)} %get-tuple-element.31.refs_0_), channel_id=1, source_target_pairs={{0,4},{4,8},{8,12},{12,0},{1,5},{5,9},{9,13},{13,1},{2,6},{6,10},{... | collective-permute-start | bytes 393224 | tf_op jit(solution)/shard_map/ppermute | solution.py:29
  238.9 11.0 %collective-permute-start.27 = (f32[16,2048]{1,0:T(8,128)S(1)}, f32[16,2048]{1,0:T(8,128)S(1)}, u32[]{:S(2)}, u32[]{:S(2)}) collective-permute-start(f32[16,2048]{1,0:T(8,128)S(1)} %get-tuple-element.31.refs_0_), channel_id=1, source_target_pairs={{0,8},{4,12},{8,0},{12,4},{1,9},{5,13},{9,1},{13,5},{2,10},{6,14},... | collective-permute-start | bytes 393224 | tf_op jit(solution)/shard_map/ppermute | solution.py:29
  241.5 8.4 %collective-permute-start.28 = (f32[16,2048]{1,0:T(8,128)S(1)}, f32[16,2048]{1,0:T(8,128)S(1)}, u32[]{:S(2)}, u32[]{:S(2)}) collective-permute-start(f32[16,2048]{1,0:T(8,128)S(1)} %get-tuple-element.31.refs_0_), channel_id=1, source_target_pairs={{0,12},{4,0},{8,4},{12,8},{1,13},{5,1},{9,5},{13,9},{2,14},{6,2},{... | collective-permute-start | bytes 393224 | tf_op jit(solution)/shard_map/ppermute | solution.py:29
  246.4 12.4 %collective-permute-start.37 = (f32[2,1024]{1,0:T(2,128)S(1)}, f32[2,1024]{1,0:T(2,128)S(1)}, u32[]{:S(2)}, u32[]{:S(2)}) collective-permute-start(f32[2,1024]{1,0:T(2,128)S(1)} %get-tuple-element.80), channel_id=1, source_target_pairs={{0,64},{64,0},{1,65},{65,1},{2,66},{66,2},{3,67},{67,3},{4,68},{68... | collective-permute-start | bytes 24584 | tf_op jit(solution)/shard_map/ppermute | solution.py:33
  249.9 9.0 %collective-permute-start.38 = (f32[8,2048]{1,0:T(8,128)S(1)}, f32[8,2048]{1,0:T(8,128)S(1)}, u32[]{:S(2)}, u32[]{:S(2)}) collective-permute-start(f32[8,2048]{1,0:T(8,128)S(1)} %get-tuple-element.35), channel_id=1, source_target_pairs={{0,64},{64,0},{1,65},{65,1},{2,66},{66,2},{3,67},{67,3},{4,68},{68... | collective-permute-start | bytes 196616 | tf_op jit(solution)/shard_map/ppermute | solution.py:33
  255.3 5.5 %collective-permute-start.34 = (f32[8,1024]{1,0:T(8,128)S(1)}, f32[8,1024]{1,0:T(8,128)S(1)}, u32[]{:S(2)}, u32[]{:S(2)}) collective-permute-start(f32[8,1024]{1,0:T(8,128)S(1)} %get-tuple-element.33), channel_id=1, source_target_pairs={{0,64},{64,0},{1,65},{65,1},{2,66},{66,2},{3,67},{67,3},{4,68},{68... | collective-permute-start | bytes 98312 | tf_op jit(solution)/shard_map/ppermute | solution.py:33
  261.5 5.5 %collective-permute-start.39 = (f32[8,2048]{1,0:T(8,128)S(1)}, f32[8,2048]{1,0:T(8,128)S(1)}, u32[]{:S(2)}, u32[]{:S(2)}) collective-permute-start(f32[8,2048]{1,0:T(8,128)S(1)} %s23.1.c0), channel_id=1, source_target_pairs={{0,4},{4,8},{8,12},{12,0},{1,5},{5,9},{9,13},{13,1},{2,6},{6,10},{... | collective-permute-start | bytes 196616 | tf_op jit(solution)/shard_map/ppermute | solution.py:29
  261.6 6.5 %collective-permute-start.40 = (f32[8,2048]{1,0:T(8,128)S(1)}, f32[8,2048]{1,0:T(8,128)S(1)}, u32[]{:S(2)}, u32[]{:S(2)}) collective-permute-start(f32[8,2048]{1,0:T(8,128)S(1)} %s23.1.c0), channel_id=1, source_target_pairs={{0,8},{4,12},{8,0},{12,4},{1,9},{5,13},{9,1},{13,5},{2,10},{6,14},... | collective-permute-start | bytes 196616 | tf_op jit(solution)/shard_map/ppermute | solution.py:29
  265.1 4.3 %collective-permute-start.41 = (f32[8,2048]{1,0:T(8,128)S(1)}, f32[8,2048]{1,0:T(8,128)S(1)}, u32[]{:S(2)}, u32[]{:S(2)}) collective-permute-start(f32[8,2048]{1,0:T(8,128)S(1)} %s23.1.c0), channel_id=1, source_target_pairs={{0,12},{4,0},{8,4},{12,8},{1,13},{5,1},{9,5},{13,9},{2,14},{6,2},{... | collective-permute-start | bytes 196616 | tf_op jit(solution)/shard_map/ppermute | solution.py:29
  273.5 5.5 %collective-permute-start.46 = (f32[8,2048]{1,0:T(8,128)S(1)}, f32[8,2048]{1,0:T(8,128)S(1)}, u32[]{:S(2)}, u32[]{:S(2)}) collective-permute-start(f32[8,2048]{1,0:T(8,128)S(1)} %top.1.c0), channel_id=1, source_target_pairs={{0,4},{4,8},{8,12},{12,0},{1,5},{5,9},{9,13},{13,1},{2,6},{6,10},{... | collective-permute-start | bytes 196616 | tf_op jit(solution)/shard_map/ppermute | solution.py:29
  274.1 5.8 %collective-permute-start.47 = (f32[8,2048]{1,0:T(8,128)S(1)}, f32[8,2048]{1,0:T(8,128)S(1)}, u32[]{:S(2)}, u32[]{:S(2)}) collective-permute-start(f32[8,2048]{1,0:T(8,128)S(1)} %top.1.c0), channel_id=1, source_target_pairs={{0,8},{4,12},{8,0},{12,4},{1,9},{5,13},{9,1},{13,5},{2,10},{6,14},... | collective-permute-start | bytes 196616 | tf_op jit(solution)/shard_map/ppermute | solution.py:29
  276.9 4.3 %collective-permute-start.48 = (f32[8,2048]{1,0:T(8,128)S(1)}, f32[8,2048]{1,0:T(8,128)S(1)}, u32[]{:S(2)}, u32[]{:S(2)}) collective-permute-start(f32[8,2048]{1,0:T(8,128)S(1)} %top.1.c0), channel_id=1, source_target_pairs={{0,12},{4,0},{8,4},{12,8},{1,13},{5,1},{9,5},{13,9},{2,14},{6,2},{... | collective-permute-start | bytes 196616 | tf_op jit(solution)/shard_map/ppermute | solution.py:29
  281.8 5.5 %collective-permute-start.49 = (f32[8,1024]{1,0:T(8,128)S(1)}, f32[8,1024]{1,0:T(8,128)S(1)}, u32[]{:S(2)}, u32[]{:S(2)}) collective-permute-start(f32[8,1024]{1,0:T(8,128)S(1)} %get-tuple-element.37), channel_id=1, source_target_pairs={{0,64},{64,0},{1,65},{65,1},{2,66},{66,2},{3,67},{67,3},{4,68},{68... | collective-permute-start | bytes 98312 | tf_op jit(solution)/shard_map/ppermute | solution.py:33
  291.5 10.0 %collective-permute-start.50 = (f32[16,2048]{1,0:T(8,128)S(1)}, f32[16,2048]{1,0:T(8,128)S(1)}, u32[]{:S(2)}, u32[]{:S(2)}) collective-permute-start(f32[16,2048]{1,0:T(8,128)S(1)} %b2.1.c0), channel_id=1, source_target_pairs={{0,4},{4,8},{8,12},{12,0},{1,5},{5,9},{9,13},{13,1},{2,6},{6,10},{... | collective-permute-start | bytes 393224 | tf_op jit(solution)/shard_map/ppermute | solution.py:29
  292.4 9.1 %collective-permute-start.51 = (f32[16,2048]{1,0:T(8,128)S(1)}, f32[16,2048]{1,0:T(8,128)S(1)}, u32[]{:S(2)}, u32[]{:S(2)}) collective-permute-start(f32[16,2048]{1,0:T(8,128)S(1)} %b2.1.c0), channel_id=1, source_target_pairs={{0,8},{4,12},{8,0},{12,4},{1,9},{5,13},{9,1},{13,5},{2,10},{6,14},... | collective-permute-start | bytes 393224 | tf_op jit(solution)/shard_map/ppermute | solution.py:29
  295.2 6.3 %collective-permute-start.52 = (f32[16,2048]{1,0:T(8,128)S(1)}, f32[16,2048]{1,0:T(8,128)S(1)}, u32[]{:S(2)}, u32[]{:S(2)}) collective-permute-start(f32[16,2048]{1,0:T(8,128)S(1)} %b2.1.c0), channel_id=1, source_target_pairs={{0,12},{4,0},{8,4},{12,8},{1,13},{5,1},{9,5},{13,9},{2,14},{6,2},{... | collective-permute-start | bytes 393224 | tf_op jit(solution)/shard_map/ppermute | solution.py:29
  295.7 5.8 %collective-permute-start.53 = (f32[8,2048]{1,0:T(8,128)S(1)}, f32[8,2048]{1,0:T(8,128)S(1)}, u32[]{:S(2)}, u32[]{:S(2)}) collective-permute-start(f32[8,2048]{1,0:T(8,128)S(1)} %get-tuple-element.36.x3), channel_id=1, source_target_pairs={{0,64},{64,0},{1,65},{65,1},{2,66},{66,2},{3,67},{67,3},{4,68},{68... | collective-permute-start | bytes 196616 | tf_op jit(solution)/shard_map/ppermute | solution.py:33
  302.2 4.3 %collective-permute-start.54 = (f32[16,1024]{1,0:T(8,128)S(1)}, f32[16,1024]{1,0:T(8,128)S(1)}, u32[]{:S(2)}, u32[]{:S(2)}) collective-permute-start(f32[16,1024]{1,0:T(8,128)S(1)} %get-tuple-element.40), channel_id=1, source_target_pairs={{0,32},{32,0},{1,33},{33,1},{2,34},{34,2},{3,35},{35,3},{4,36},{36... | collective-permute-start | bytes 196616 | tf_op jit(solution)/shard_map/ppermute | solution.py:33
  303.9 10.6 %collective-permute-start.58 = (f32[2,4,2048]{2,1,0:T(4,128)S(1)}, f32[2,4,2048]{2,1,0:T(4,128)S(1)}, u32[]{:S(2)}, u32[]{:S(2)}) collective-permute-start(f32[2,4,2048]{2,1,0:T(4,128)S(1)} %slice.145.a_mine), channel_id=1, source_target_pairs={{0,32},{32,0},{1,33},{33,1},{2,34},{34,2},{3,35},{35,3},{4,36},{36... | collective-permute-start | bytes 196616 | tf_op jit(solution)/shard_map/ppermute | solution.py:33
  310.9 4.3 %collective-permute-start.55 = (f32[8,2048]{1,0:T(8,128)S(1)}, f32[8,2048]{1,0:T(8,128)S(1)}, u32[]{:S(2)}, u32[]{:S(2)}) collective-permute-start(f32[8,2048]{1,0:T(8,128)S(1)} %get-tuple-element.57), channel_id=1, source_target_pairs={{0,12},{4,0},{8,4},{12,8},{1,13},{5,1},{9,5},{13,9},{2,14},{6,2},{... | collective-permute-start | bytes 196616 | tf_op jit(solution)/shard_map/ppermute | solution.py:29
  312.1 5.8 %collective-permute-start.56 = (f32[8,2048]{1,0:T(8,128)S(1)}, f32[8,2048]{1,0:T(8,128)S(1)}, u32[]{:S(2)}, u32[]{:S(2)}) collective-permute-start(f32[8,2048]{1,0:T(8,128)S(1)} %get-tuple-element.56), channel_id=1, source_target_pairs={{0,8},{4,12},{8,0},{12,4},{1,9},{5,13},{9,1},{13,5},{2,10},{6,14},... | collective-permute-start | bytes 196616 | tf_op jit(solution)/shard_map/ppermute | solution.py:29
  314.5 5.5 %collective-permute-start.57 = (f32[8,2048]{1,0:T(8,128)S(1)}, f32[8,2048]{1,0:T(8,128)S(1)}, u32[]{:S(2)}, u32[]{:S(2)}) collective-permute-start(f32[8,2048]{1,0:T(8,128)S(1)} %get-tuple-element.55), channel_id=1, source_target_pairs={{0,4},{4,8},{8,12},{12,0},{1,5},{5,9},{9,13},{13,1},{2,6},{6,10},{... | collective-permute-start | bytes 196616 | tf_op jit(solution)/shard_map/ppermute | solution.py:29
  320.7 25.5 %collective-permute-start.67 = (f32[8,512]{1,0:T(8,128)S(1)}, f32[8,512]{1,0:T(8,128)S(1)}, u32[]{:S(2)}, u32[]{:S(2)}) collective-permute-start(f32[8,512]{1,0:T(8,128)S(1)} %get-tuple-element.68), channel_id=1, source_target_pairs={{0,16},{16,0},{1,17},{17,1},{2,18},{18,2},{3,19},{19,3},{4,20},{20... | collective-permute-start | bytes 49160 | tf_op jit(solution)/shard_map/ppermute | solution.py:33
  321.3 25.5 %collective-permute-start.66 = (f32[8,1024]{1,0:T(8,128)S(1)}, f32[8,1024]{1,0:T(8,128)S(1)}, u32[]{:S(2)}, u32[]{:S(2)}) collective-permute-start(f32[8,1024]{1,0:T(8,128)S(1)} %get-tuple-element.70), channel_id=1, source_target_pairs={{0,16},{16,0},{1,17},{17,1},{2,18},{18,2},{3,19},{19,3},{4,20},{20... | collective-permute-start | bytes 98312 | tf_op jit(solution)/shard_map/ppermute | solution.py:33
  322.4 6.8 %collective-permute-start.60 = (f32[16,1024]{1,0:T(8,128)S(1)}, f32[16,1024]{1,0:T(8,128)S(1)}, u32[]{:S(2)}, u32[]{:S(2)}) collective-permute-start(f32[16,1024]{1,0:T(8,128)S(1)} %maximum_select_fusion.8.refs_0_), channel_id=1, source_target_pairs={{0,1},{1,2},{2,3},{3,0},{4,5},{5,6},{6,7},{7,4},{8,9},{9,10},{10,1... | collective-permute-start | bytes 196616 | tf_op jit(solution)/shard_map/ppermute | solution.py:29
  322.5 6.7 %collective-permute-start.61 = (f32[16,1024]{1,0:T(8,128)S(1)}, f32[16,1024]{1,0:T(8,128)S(1)}, u32[]{:S(2)}, u32[]{:S(2)}) collective-permute-start(f32[16,1024]{1,0:T(8,128)S(1)} %maximum_select_fusion.8.refs_0_), channel_id=1, source_target_pairs={{0,2},{1,3},{2,0},{3,1},{4,6},{5,7},{6,4},{7,5},{8,10},{9,11},{10,... | collective-permute-start | bytes 196616 | tf_op jit(solution)/shard_map/ppermute | solution.py:29
  324.4 5.4 %collective-permute-start.62 = (f32[16,1024]{1,0:T(8,128)S(1)}, f32[16,1024]{1,0:T(8,128)S(1)}, u32[]{:S(2)}, u32[]{:S(2)}) collective-permute-start(f32[16,1024]{1,0:T(8,128)S(1)} %maximum_select_fusion.8.refs_0_), channel_id=1, source_target_pairs={{0,3},{1,0},{2,1},{3,2},{4,7},{5,4},{6,5},{7,6},{8,11},{9,8},{10,9... | collective-permute-start | bytes 196616 | tf_op jit(solution)/shard_map/ppermute | solution.py:29
  342.8 7.5 %collective-permute-start.63 = (f32[16,2048]{1,0:T(8,128)S(1)}, f32[16,2048]{1,0:T(8,128)S(1)}, u32[]{:S(2)}, u32[]{:S(2)}) collective-permute-start(f32[16,2048]{1,0:T(8,128)S(1)} %get-tuple-element.54), channel_id=1, source_target_pairs={{0,3},{1,0},{2,1},{3,2},{4,7},{5,4},{6,5},{7,6},{8,11},{9,8},{10,9... | collective-permute-start | bytes 393224 | tf_op jit(solution)/shard_map/ppermute | solution.py:29
  345.3 7.4 %collective-permute-start.64 = (f32[16,2048]{1,0:T(8,128)S(1)}, f32[16,2048]{1,0:T(8,128)S(1)}, u32[]{:S(2)}, u32[]{:S(2)}) collective-permute-start(f32[16,2048]{1,0:T(8,128)S(1)} %get-tuple-element.53), channel_id=1, source_target_pairs={{0,2},{1,3},{2,0},{3,1},{4,6},{5,7},{6,4},{7,5},{8,10},{9,11},{10,... | collective-permute-start | bytes 393224 | tf_op jit(solution)/shard_map/ppermute | solution.py:29
  346.0 7.7 %collective-permute-start.65 = (f32[16,2048]{1,0:T(8,128)S(1)}, f32[16,2048]{1,0:T(8,128)S(1)}, u32[]{:S(2)}, u32[]{:S(2)}) collective-permute-start(f32[16,2048]{1,0:T(8,128)S(1)} %get-tuple-element.52), channel_id=1, source_target_pairs={{0,1},{1,2},{2,3},{3,0},{4,5},{5,6},{6,7},{7,4},{8,9},{9,10},{10,1... | collective-permute-start | bytes 393224 | tf_op jit(solution)/shard_map/ppermute | solution.py:29
  (49 other events, 679.3 us)
Sparse Core Ops, SparseCore 0:
  27.9 39.0 all-gather.7
  68.7 50.6 all-gather.9
  121.0 32.9 all-gather.5

commit v2 on v1

--- a/solution.py
+++ b/solution.py
@@ -112,31 +112,31 @@
 
 
 def copies_upper(meta, bufs, ev, fv, sems):
-    ci = meta[CI]
+    ci, yi = meta[CI], meta[YI]
+    sources = []
+    for i, q in ((0, ci), (1, 1 - ci)):
+        if len(bufs) == 2:
+            sources += [(bufs[i].at[w], q, w) for w in range(4)]
+        else:
+            sources += [(bufs[4 * i + d], q, lax.rem(yi + 4 - d, 4)) for d in range(4)]
     out_e, out_f = [], []
     k = 0
-    for ref, q in ((bufs[0], ci), (bufs[1], 1 - ci)):
+    for ref, q, w in sources:
         rows = pl.ds(pl.multiple_of(q * 256, 256), 256)
-        for w in range(4):
-            for s in range(4):
-                out_e.append(
-                    pltpu.make_async_copy(
-                        ref.at[w, pl.ds(s * 256, 256)],
-                        ev.at[rows, pl.ds((4 * s + w) * B, B)],
-                        sems.at[k],
-                    )
-                )
-                k += 1
+        for s in range(4):
+            cols = pl.ds(pl.multiple_of((4 * s + w) * B, B), B)
+            out_e.append(
+                pltpu.make_async_copy(ref.at[pl.ds(s * 256, 256)], ev.at[rows, cols], sems.at[k])
+            )
+            k += 1
     if fv is not None:
-        for ref, q in ((bufs[0], ci), (bufs[1], 1 - ci)):
+        for ref, q, w in sources:
             rows = pl.ds(pl.multiple_of(q * 512, 512), 512)
-            for w in range(4):
-                out_f.append(
-                    pltpu.make_async_copy(
-                        ref.at[w, pl.ds(1024, 512)], fv.at[rows, pl.ds(w * B, B)], sems.at[k]
-                    )
-                )
-                k += 1
+            cols = pl.ds(pl.multiple_of(w * B, B), B)
+            out_f.append(
+                pltpu.make_async_copy(ref.at[pl.ds(1024, 512)], fv.at[rows, cols], sems.at[k])
+            )
+            k += 1
     return out_e, out_f
 
 
@@ -160,13 +160,16 @@
     lax.fori_loop(0, 2, body, 0)
 
 
+WEIGHTS = (10, 2, 8, 2)
+
+
 def forward_kernel(level, n, mode, meta, *refs):
-    count = 10 if level == 0 else 2
+    count = WEIGHTS[level]
     c_refs, refs = refs[:4], refs[4:]
     w_refs, refs = refs[:count], refs[count:]
     if mode == "rs":
-        y_out, u_out = refs[:2]
-        refs = refs[2:]
+        y_out, u_out = refs[0], refs[1:5]
+        refs = refs[5:]
     else:
         y_out, keep_out, give_out = refs[:3]
         refs = refs[3:]
@@ -208,7 +211,7 @@
     lax.fori_loop(0, 4, body, 0)
     if mode == "rs":
         for s in range(4):
-            u_out[s] = uv[pl.ds(s * r, r), :]
+            u_out[s][...] = uv[pl.ds(s * r, r), :]
     else:
         split_rows(uv, r, meta[X0] if level == 1 else meta[X1], keep_out, give_out)
 
@@ -291,7 +294,7 @@
 
     solve_rows(ev, cs, put_y)
     y = jnp.where(row_mask(meta, 3, 8), yv[...], 0.0)
-    back(meta, 3, 8, ev, y, x_out)
+    back(meta, 3, 8, ev, y, [x_out])
 
 
 def back(meta, level, n, ev, z, x_out):
@@ -302,7 +305,10 @@
         cols = pl.ds(pl.multiple_of(j * 512, 512), 512)
         v = product(zs, ev[:, cols], NND)
         col = lax.broadcasted_iota(jnp.int32, (n, 512), 1) + j * 512
-        x_out[:, cols] = jnp.where(col < live, v, 0.0)
+        v = jnp.where(col < live, v, 0.0)
+        r = n // len(x_out)
+        for s, out in enumerate(x_out):
+            out[:, cols] = v[s * r : (s + 1) * r]
         return carry
 
     lax.fori_loop(0, 4, body, 0)
@@ -341,14 +347,14 @@
 
 
 def backward_kernel(level, n, meta, *refs):
-    count = 10 if level == 0 else 2
+    count = WEIGHTS[level]
     if level == 0:
         g_refs, refs = refs[:4], refs[4:]
     else:
         (anc, recv), refs = refs[:2], refs[2:]
     y_ref, refs = refs[0], refs[1:]
     w_refs, refs = refs[:count], refs[count:]
-    x_out, ev, fv, gv, ov, sems = refs
+    x_out, (ev, fv, gv, ov, sems) = refs[:-5], refs[-5:]
     if level == 0:
         ce, cf = copies_first(meta, w_refs[:5], w_refs[5:], ev, fv, sems)
     else:
@@ -380,6 +386,8 @@
 
 
 def call(kernel, name, shapes, scratch, meta, small, weights=(), flops=0):
+    if name != "f0":
+        weights = [pltpu.with_memory_space_constraint(w, pltpu.HBM) for w in weights]
     moved = sum(w.size * 4 for w in weights) + sum(v.size * 4 for v in small)
     return pl.pallas_call(
         kernel,
@@ -387,7 +395,7 @@
         in_specs=[SMEM] + [VMEM] * len(small) + [ANY] * len(weights),
         out_specs=[VMEM] * len(shapes),
         scratch_shapes=scratch,
-        compiler_params=pltpu.CompilerParams(vmem_limit_bytes=24 * 2**20),
+        compiler_params=pltpu.CompilerParams(vmem_limit_bytes=(14 if flops else 3) * 2**20),
         cost_estimate=pl.CostEstimate(flops=flops, bytes_accessed=moved, transcendentals=0),
         name=name,
     )(meta, *small, *weights)
@@ -412,26 +420,43 @@
     e0 = jnp.swapaxes(dinv0.reshape(4, 4, B, B), 0, 1).reshape(4, 512, B)
     f0 = ring(off0, "z", 0)
     e0 = lax.all_to_all(e0, "y", 0, 0, tiled=True)
-    e0 = ring(e0, "z", 0)
-    w0 = e0 + f0
-
-    def upper(dinv, off, bits):
-        e, f = dinv, off
-        for axis, bit in bits:
-            e = ordered(e, flip(e, axis), bit, 0)
-            if f is not None:
-                f = ordered(f, flip(f, axis), bit, 0)
-        e = lax.dynamic_index_in_dim(e.reshape(4, 2, 256, B), ci, 1, keepdims=False)
-        e = lax.all_to_all(e, "z", 0, 0, tiled=True).reshape(1024, B)
-        if f is not None:
-            e = jnp.concatenate([e, lax.dynamic_slice_in_dim(f, ci * 512, 512)], 0)
+
+    bits = [("core", ci), ("x0", x0), ("x1", x1)]
+
+    def grouped(v, levels):
+        for axis, bit in bits[:levels]:
+            v = ordered(v, flip(v, axis), bit, 0)
+        return v
+
+    def half_block(e, levels):
+        e = grouped(e, levels)
+        return lax.dynamic_index_in_dim(e.reshape(4, 2, 256, B), ci, 1, keepdims=False)
+
+    def packed(e, f, levels):
+        e = e.reshape(1024, B)
+        if f is None:
+            return e
+        return jnp.concatenate([e, lax.dynamic_slice_in_dim(grouped(f, levels), ci * 512, 512)], 0)
+
+    def gathered(e):
         mine = lax.all_gather(e, "y", axis=0, tiled=False)
         return mine, flip(mine, "core")
 
-    bits = [("core", ci), ("x0", x0), ("x1", x1)]
-    w1 = upper(dinv1, off1, bits[:1])
-    w2 = upper(dinv2, off2, bits[:2])
-    w3 = upper(dinv3, None, bits)
+    e1 = half_block(dinv1, 1)
+    e0, e1 = lax.optimization_barrier((e0, e1))
+    e0 = ring(e0, "z", 0)
+    e1 = lax.all_to_all(e1, "z", 0, 0, tiled=True)
+    w0 = e0 + f0
+    w1 = gathered(packed(e1, off1, 1))
+    near, e1, dinv2, off2, dinv3, rhs1, rhs2, rhs3 = lax.optimization_barrier(
+        (e0[1], e1, dinv2, off2, dinv3, rhs1, rhs2, rhs3)
+    )
+    e2 = lax.all_to_all(half_block(dinv2, 2), "z", 0, 0, tiled=True)
+    pieces = gather4(packed(e2, off2, 2), "y")
+    w2 = pieces + [flip(v, "core") for v in pieces]
+    e3 = half_block(dinv3, 3)
+    e2, e3 = lax.optimization_barrier((e2, e3))
+    w3 = gathered(packed(lax.all_to_all(e3, "z", 0, 0, tiled=True), None, 3))
 
     def spread(rhs, levels):
         v = rhs
@@ -451,11 +476,11 @@
     def flops(n):
         return 2 * n * 512 * (2048 + 1024) * 12
 
-    y0, u = call(
-        functools.partial(forward_kernel, 0, 64, "rs"), "f0", [(64, 512), (4, 16, 1024)],
+    y0, *u = call(
+        functools.partial(forward_kernel, 0, 64, "rs"), "f0", [(64, 512)] + [(16, 1024)] * 4,
         [ev, fv, *work(64), dma((24,))], meta, gather4(rhs0, "y"), w0, flops(64),
     )
-    parts = scatter4([u[s] for s in range(4)], "y")
+    parts = scatter4(u, "y")
     u = (parts[0] + parts[1]) + (parts[2] + parts[3])
     keep, give = halves(u, ci)
     c1, pk, pg = call(
@@ -506,20 +531,20 @@
     recv = flip(give, "x0")
     a_mine = anc[:, :4]
     a_other = flip(a_mine, "x0")
-    (part,) = call(
-        functools.partial(backward_kernel, 1, 32), "b1", [(32, ORDER)], rest(32, 0),
+    parts = call(
+        functools.partial(backward_kernel, 1, 32), "b1", [(8, ORDER)] * 4, rest(32, 0),
         meta, [anc, recv, y1], w1, flops(32),
     )
     anc, give, own = call(
         x1_kernel, "x1", [(3, 8, ORDER), (8, 1024), (8, 1024)], [],
-        meta, scatter4([part[8 * s : 8 * s + 8] for s in range(4)], "z") + [a_mine, a_other],
+        meta, scatter4(parts, "z") + [a_mine, a_other],
     )
     g = ordered(own, flip(give, "core"), ci, 0)
-    (part,) = call(
-        functools.partial(backward_kernel, 0, 64), "b0", [(64, ORDER)], rest(64, 0),
+    parts = call(
+        functools.partial(backward_kernel, 0, 64), "b0", [(16, ORDER)] * 4, rest(64, 0),
         meta, gather4(g, "y") + [y0], w0, flops(64),
     )
-    parts = scatter4([part[16 * s : 16 * s + 16] for s in range(4)], "y")
+    parts = scatter4(parts, "y")
     sol0 = (parts[0] + parts[1]) + (parts[2] + parts[3])
 
     outs = [sol0]

time: 362 us -> 367 us (1.014)
  waiting for transfers between devices: 145 us -> 184 us
  blocking collectives: 36.2 us -> 0 us
  local copies, waits for them, and re-layouts: 30.4 us -> 17.5 us
  starting transfers between devices: 85 us -> 97.2 us
  Pallas kernels: 36.9 us -> 40.8 us
    all_to_all x2 -> x0, blocking collectives: 36.2 us -> none  [the longest x1 24.7 us: local(): e0 = lax.all_to_all(e0, 'y', 0, 0, tiled=True)]
    ppermute x38 -> x41, waiting for transfers between devices: 74.4 us -> 100 us  [shift(): return lax.ppermute(v, axis, [(i, (i + s) % 4) for i in range(4)])]
    all_to_all x2 -> x4, waiting for transfers between devices: 9.34 us -> 28.5 us  [the longest x1 14.7 us: local(): e0 = lax.all_to_all(e0, 'y', 0, 0, tiled=True)]
    unnamed x78 -> x64, local copies, waits for them, and re-layouts: 19.3 us -> 3.38 us
    ppermute x38 -> x41, starting transfers between devices: 46.4 us -> 55.3 us  [shift(): return lax.ppermute(v, axis, [(i, (i + s) % 4) for i in range(4)])]
    all_to_all x2 -> x4, starting transfers between devices: 8.86 us -> 17.7 us  [the longest x1 5.31 us: local(): e1 = lax.all_to_all(e1, 'z', 0, 0, tiled=True)]
    ppermute x31 -> x34, starting transfers between devices: 29.7 us -> 24.1 us  [flip(): return lax.ppermute(v, axis, [(0, 1), (1, 0)])]
    ppermute x31 -> x34, waiting for transfers between devices: 60.8 us -> 55.4 us  [flip(): return lax.ppermute(v, axis, [(0, 1), (1, 0)])]
  transfers between devices with their start and end apart: 74 -> 81, of which waited for: 42 -> 37; matrix products, arithmetic and copies ran while one was open for 6% -> 7% of each run, Pallas kernels for 7% -> 8%
where the time goes in v2:
time: 367 us; the launch traced here: 366 us
  waiting for transfers between devices  184 us (50%)
  starting transfers between devices  97.2 us (26%)
  Pallas kernels  40.8 us (11%)
  local copies, waits for them, and re-layouts  17.5 us (5%)
  between operations  14.7 us (4%)
  other arithmetic  11.6 us (3%)
    ppermute x41, waiting for transfers between devices, shift(): return lax.ppermute(v, axis, [(i, (i + s) % 4) for i in range(4)])  100 us
    ppermute x34, waiting for transfers between devices, flip(): return lax.ppermute(v, axis, [(0, 1), (1, 0)])  55.4 us
    ppermute x41, starting transfers between devices, shift(): return lax.ppermute(v, axis, [(i, (i + s) % 4) for i in range(4)])  55.3 us
    pallas_call x13, Pallas kernels, call(): pl.pallas_call(kernel, out_shape=[jax.ShapeDtypeStruct(s, f32) for s in s...  40.8 us
    ppermute x34, starting transfers between devices, flip(): return lax.ppermute(v, axis, [(0, 1), (1, 0)])  24.1 us
    all_to_all x1, waiting for transfers between devices, local(): e0 = lax.all_to_all(e0, 'y', 0, 0, tiled=True)  14.7 us
  transfers between devices with their start and end apart: 81, of which 37 were waited for; matrix products, arithmetic and copies ran while one was open for 7% of the time, Pallas kernels for 8%

profile of v2, /device:TPU:0, one launch (start us, length us, event | category | flops | bytes accessed | tf_op | source)
XLA Modules:
  0.0 366.0 jit_solution(6357912074330616810)
XLA Ops:
  7.3 2.4 copy.18
  9.6 4.7 %all-to-all-start = ((f32[4,512,128]{2,1,0:T(8,128)}), f32[4,512,128]{2,1,0:T(8,128)S(1)}, u32[]{:S(2)}, u32[]{:S(2)}) async-start(f32[4,512,128]{2,1,0:T(8,128)} %bitcast.7), calls=%async_computation | async-start | bytes 2097152 | tf_op jit(solution)/shard_map/all_to_all | solution.py:422
  15.3 14.7 %all-to-all-done.refs_4_.refs_5_ = f32[4,512,128]{2,1,0:T(8,128)S(1)} async-done(((f32[4,512,128]{2,1,0:T(8,128)}), f32[4,512,128]{2,1,0:T(8,128)S(1)}, u32[]{:S(2)}, u32[]{:S(2)}) %all-to-all-start) | async-done | bytes 1048608 | tf_op jit(solution)/shard_map/all_to_all | solution.py:422
  30.0 5.3 %all-to-all-start.1 = ((f32[4,256,128]{2,1,0:T(8,128)}), f32[4,256,128]{2,1,0:T(8,128)S(1)}, u32[]{:S(2)}, u32[]{:S(2)}) async-start(f32[4,256,128]{2,1,0:T(8,128)} %dynamic-slice_bitcast_fusion.2), calls=%async_computation.1 | async-start | bytes 1048576 | tf_op jit(solution)/shard_map/all_to_all | solution.py:448
  35.4 1.5 collective-permute-done.20
  37.1 7.2 %all-to-all-done.1 = f32[4,256,128]{2,1,0:T(8,128)S(1)} async-done(((f32[4,256,128]{2,1,0:T(8,128)}), f32[4,256,128]{2,1,0:T(8,128)S(1)}, u32[]{:S(2)}, u32[]{:S(2)}) %all-to-all-start.1) | async-done | bytes 524320 | tf_op jit(solution)/shard_map/all_to_all | solution.py:448
  45.9 23.5 %collective-permute-done.4.refs_5_.refs_6_ = f32[4,512,128]{2,1,0:T(8,128)S(1)} collective-permute-done((f32[4,512,128]{2,1,0:T(8,128)S(1)}, f32[4,512,128]{2,1,0:T(8,128)S(1)}, u32[]{:S(2)}, u32[]{:S(2)}) %collective-permute-start.4) | collective-permute-done | bytes 1048608 | tf_op jit(solution)/shard_map/ppermute | solution.py:29
  71.0 1.6 collective-permute-start.30
  73.2 17.6 %collective-permute-done.49 = f32[512,128]{1,0:T(8,128)} collective-permute-done((f32[512,128]{1,0:T(8,128)S(1)}, f32[512,128]{1,0:T(8,128)}, u32[]{:S(2)}, u32[]{:S(2)}) %collective-permute-start.49) | collective-permute-done | bytes 262176 | tf_op jit(solution)/shard_map/ppermute | solution.py:33
  91.9 3.1 collective-permute-start.50
  97.2 3.6 all-to-all-start.2
  100.8 5.9 %collective-permute-done.50 = f32[1024,128]{1,0:T(8,128)} collective-permute-done((f32[1024,128]{1,0:T(8,128)S(1)}, f32[1024,128]{1,0:T(8,128)}, u32[]{:S(2)}, u32[]{:S(2)}) %collective-permute-start.50) | collective-permute-done | bytes 524320 | tf_op jit(solution)/shard_map/ppermute | solution.py:33
  109.7 4.1 %all-to-all-start.3 = ((f32[4,256,128]{2,1,0:T(8,128)}), f32[4,256,128]{2,1,0:T(8,128)}, u32[]{:S(2)}, u32[]{:S(2)}) async-start(f32[4,256,128]{2,1,0:T(8,128)} %dynamic-slice_bitcast_fusion), calls=%async_computation.3 | async-start | bytes 1048576 | tf_op jit(solution)/shard_map/all_to_all | solution.py:459
  113.9 1.9 collective-permute-start.8
  117.2 1.9 collective-permute-start.5
  119.1 5.8 %all-to-all-done.3 = f32[4,256,128]{2,1,0:T(8,128)} async-done(((f32[4,256,128]{2,1,0:T(8,128)}), f32[4,256,128]{2,1,0:T(8,128)}, u32[]{:S(2)}, u32[]{:S(2)}) %all-to-all-start.3) | async-done | bytes 524320 | tf_op jit(solution)/shard_map/all_to_all | solution.py:459
  125.5 2.1 collective-permute-start.1
  130.1 3.2 concatenate.123.meta
  133.4 1.7 slice.107
  135.0 1.7 slice.108
  140.2 13.6 %collective-permute-done.5.refs_6_.refs_7_ = f32[4,512,128]{2,1,0:T(8,128)S(1)} collective-permute-done((f32[4,512,128]{2,1,0:T(8,128)S(1)}, f32[4,512,128]{2,1,0:T(8,128)S(1)}, u32[]{:S(2)}, u32[]{:S(2)}) %collective-permute-start.5) | collective-permute-done | bytes 1048608 | tf_op jit(solution)/shard_map/ppermute | solution.py:29
  155.8 1.5 collective-permute-start.6
  157.9 1.7 collective-permute-start.7
  161.1 1.9 collective-permute-start.11
  163.8 13.1 %collective-permute-done.10.refs_12_.refs_13_ = f32[512,128]{1,0:T(8,128)S(1)} collective-permute-done((f32[512,128]{1,0:T(8,128)}, f32[512,128]{1,0:T(8,128)S(1)}, u32[]{:S(2)}, u32[]{:S(2)}) %collective-permute-start.10) | collective-permute-done | bytes 262176 | tf_op jit(solution)/shard_map/ppermute | solution.py:29
  180.9 4.6 %f0.1 = (f32[64,512]{1,0:T(8,128)S(1)}, f32[16,1024]{1,0:T(8,128)S(1)}, f32[16,1024]{1,0:T(8,128)S(1)}, f32[16,1024]{1,0:T(8,128)S(1)}, f32[16,1024]{1,0:T(8,128)S(1)}) custom-call(s32[64]{0:T(128)S(1)} %concatenate.123.meta, f32[16,2048]{1,0:T(8,128)S(1)} %copy-done.7, f32[16,2048]{1,0:T(8,128)S(1)} %copy-done.9, f32[16,2048]{1,0:T(8,128)S(1)} %copy-done.11, ...), custom_call_target="tpu_custom_call" | custom-call | flops 2415919104 | bytes 6815744 | tf_op jit(solution)/shard_map/f0/pallas_call | solution.py:392
  185.5 1.5 collective-permute-start.13
  187.1 3.2 collective-permute-start.12
  190.3 1.5 collective-permute-done.13
  194.0 5.5 %collective-permute-done.32 = f32[512,128]{1,0:T(8,128)S(1)} collective-permute-done((f32[512,128]{1,0:T(8,128)S(1)}, f32[512,128]{1,0:T(8,128)S(1)}, u32[]{:S(2)}, u32[]{:S(2)}) %collective-permute-start.32) | collective-permute-done | bytes 262176 | tf_op jit(solution)/shard_map/ppermute | solution.py:33
  201.0 3.3 collective-permute-start.18
  205.1 1.6 collective-permute-start.34
  207.3 3.7 %collective-permute-done.19.refs_3_ = f32[8,2048]{1,0:T(8,128)S(1)} collective-permute-done((f32[8,2048]{1,0:T(8,128)S(1)}, f32[8,2048]{1,0:T(8,128)S(1)}, u32[]{:S(2)}, u32[]{:S(2)}) %collective-permute-start.19) | collective-permute-done | bytes 65568 | tf_op jit(solution)/shard_map/ppermute | solution.py:29
  211.7 3.6 collective-permute-done.25.pr
  216.6 21.4 %collective-permute-done.33.refs_5_.refs_4_ = f32[1536,128]{1,0:T(8,128)S(1)} collective-permute-done((f32[1536,128]{1,0:T(8,128)S(1)}, f32[1536,128]{1,0:T(8,128)S(1)}, u32[]{:S(2)}, u32[]{:S(2)}) %collective-permute-start.33) | collective-permute-done | bytes 786464 | tf_op jit(solution)/shard_map/ppermute | solution.py:29
  238.6 5.9 %f1.1 = (f32[32,512]{1,0:T(8,128)S(1)}, f32[16,1024]{1,0:T(8,128)S(1)}, f32[16,1024]{1,0:T(8,128)S(1)}) custom-call(s32[64]{0:T(128)S(1)} %concatenate.123.meta, f32[8,2048]{1,0:T(8,128)S(1)} %get-tuple-element.52.refs_0_, f32[8,2048]{1,0:T(8,128)S(1)} %collective-permute-done.17.refs_1_, f32[8,2048]{1,0:T(8,128)S(1)} %collective-permute-done.18.refs_2_, ...), custom_call_target="tpu_custom_call" | custom-call | flops 1207959552 | bytes 6553600 | tf_op jit(solution)/shard_map/f1/pallas_call | solution.py:392
  245.5 3.6 collective-permute-done.22.recv
  249.9 1.6 collective-permute-start.26
  252.4 1.9 collective-permute-start.28
  254.3 2.7 collective-permute-start.43
  257.0 2.9 collective-permute-done.26.refs_1_
  259.9 2.7 collective-permute-start.44
  262.7 5.7 %f2.1 = (f32[16,512]{1,0:T(8,128)S(1)}, f32[8,1024]{1,0:T(8,128)S(1)}, f32[8,1024]{1,0:T(8,128)S(1)}) custom-call(s32[64]{0:T(128)S(1)} %concatenate.123.meta, f32[16,2048]{1,0:T(8,128)S(1)} %get-tuple-element.58.refs_0_, f32[16,2048]{1,0:T(8,128)S(1)} %collective-permute-done.26.refs_1_, f32[16,2048]{1,0:T(8,128)S(1)} %collective-permute-done.27.refs_2_, ...), custom_call_target="tpu_custom_call" | custom-call | flops 603979776 | bytes 6815744 | tf_op jit(solution)/shard_map/f2/pallas_call | solution.py:392
  269.3 4.6 %collective-permute-done.40.recv = f32[8,1024]{1,0:T(8,128)S(1)} collective-permute-done((f32[8,1024]{1,0:T(8,128)S(1)}, f32[8,1024]{1,0:T(8,128)S(1)}, u32[]{:S(2)}, u32[]{:S(2)}) %collective-permute-start.40) | collective-permute-done | bytes 32800 | tf_op jit(solution)/shard_map/ppermute | solution.py:33
  274.6 2.0 collective-permute-start.46
  277.9 2.9 collective-permute-done.45.c1
  281.6 5.6 %top.1.c0 = f32[8,2048]{1,0:T(8,128)S(1)} custom-call(s32[64]{0:T(128)S(1)} %concatenate.123.meta, f32[8,2048]{1,0:T(8,128)S(1)} %s23.1.c0, f32[8,2048]{1,0:T(8,128)S(1)} %collective-permute-done.45.c1, f32[8,2048]{1,0:T(8,128)S(1)} %collective-permute-done.46.c2, f32[8,2048]{1,0:T(8,128)S(1)} %collective-permute-done.47.c3, ...), custom_call_target="tpu_custom_call" | custom-call | flops 301989888 | bytes 4456448 | tf_op jit(solution)/shard_map/top/pallas_call | solution.py:392
  288.6 2.5 collective-permute-start.53
  292.8 1.6 collective-permute-done.53.c2
  297.2 4.3 %collective-permute-done.55.refs_1_ = f32[8,1024]{1,0:T(8,128)S(1)} collective-permute-done((f32[8,1024]{1,0:T(8,128)S(1)}, f32[8,1024]{1,0:T(8,128)S(1)}, u32[]{:S(2)}, u32[]{:S(2)}) %collective-permute-start.55) | collective-permute-done | bytes 32800 | tf_op jit(solution)/shard_map/ppermute | solution.py:33
  301.5 5.0 %b2.1.c0 = f32[16,2048]{1,0:T(8,128)S(1)} custom-call(s32[64]{0:T(128)S(1)} %concatenate.123.meta, f32[1,8,2048]{2,1,0:T(8,128)S(1)} %bitcast.35, f32[8,1024]{1,0:T(8,128)S(1)} %collective-permute-done.55.refs_1_, f32[16,512]{1,0:T(8,128)S(1)} %get-tuple-element.70.refs_2_, f32[1536,128]{1,0:T(8,128)} %copy-done.14, f32[1536,128]{1,0:T(8,128)} %copy-done.15, ...), custom_call_target="tpu_custom_call" | custom-call | flops 603979776 | bytes 6422528 | tf_op jit(solution)/shard_map/b2/pallas_call | solution.py:392
  306.8 2.8 collective-permute-start.57
  311.8 4.7 %collective-permute-done.59.x3r = f32[8,2048]{1,0:T(8,128)S(1)} collective-permute-done((f32[8,2048]{1,0:T(8,128)S(1)}, f32[8,2048]{1,0:T(8,128)S(1)}, u32[]{:S(2)}, u32[]{:S(2)}) %collective-permute-start.59) | collective-permute-done | bytes 65568 | tf_op jit(solution)/shard_map/ppermute | solution.py:33
  317.5 1.9 collective-permute-start.64
  319.4 2.1 collective-permute-done.60.refs_1_
  321.5 5.0 %b1.1 = (f32[8,2048]{1,0:T(8,128)S(1)}, f32[8,2048]{1,0:T(8,128)S(1)}, f32[8,2048]{1,0:T(8,128)S(1)}, f32[8,2048]{1,0:T(8,128)S(1)}) custom-call(s32[64]{0:T(128)S(1)} %concatenate.123.meta, f32[2,16,2048]{2,1,0:T(8,128)S(1)} %get-tuple-element.71.refs_0_, f32[16,1024]{1,0:T(8,128)S(1)} %collective-permute-done.60.refs_1_, ...), custom_call_target="tpu_custom_call" | custom-call | flops 1207959552 | bytes 6684672 | tf_op jit(solution)/shard_map/b1/pallas_call | solution.py:392
  327.8 1.8 collective-permute-start.62
  330.9 2.7 collective-permute-done.62.c2
  333.6 1.5 collective-permute-done.63.c3
  338.1 2.2 collective-permute-start.68
  340.9 2.9 collective-permute-done.66.refs_1_
  344.4 5.2 %b0.1 = (f32[16,2048]{1,0:T(8,128)S(1)}, f32[16,2048]{1,0:T(8,128)S(1)}, f32[16,2048]{1,0:T(8,128)S(1)}, f32[16,2048]{1,0:T(8,128)S(1)}) custom-call(s32[64]{0:T(128)S(1)} %concatenate.123.meta, f32[16,1024]{1,0:T(8,128)S(1)} %maximum_select_fusion.8.refs_0_, f32[16,1024]{1,0:T(8,128)S(1)} %collective-permute-done.66.refs_1_, ...), custom_call_target="tpu_custom_call" | custom-call | flops 2415919104 | bytes 6684672 | tf_op jit(solution)/shard_map/b0/pallas_call | solution.py:392
  350.6 2.4 collective-permute-start.71
  355.1 2.1 collective-permute-done.70
  (225 shorter events, 63.3 us)
Async XLA Ops:
  7.2 7.1 %collective-permute-start.3 = (f32[1024,128]{1,0:T(8,128)}, f32[1024,128]{1,0:T(8,128)S(1)}, u32[]{:S(2)}, u32[]{:S(2)}) collective-permute-start(f32[1024,128]{1,0:T(8,128)} %param.20), channel_id=1, source_target_pairs={{0,16},{16,0},{1,17},{17,1},{2,18},{18,2},{3,19},{19,3},{4,20},{20... | collective-permute-start | bytes 1572872 | tf_op jit(solution)/shard_map/ppermute | solution.py:33
  9.6 20.4 %all-to-all-start = ((f32[4,512,128]{2,1,0:T(8,128)}), f32[4,512,128]{2,1,0:T(8,128)S(1)}, u32[]{:S(2)}, u32[]{:S(2)}) async-start(f32[4,512,128]{2,1,0:T(8,128)} %bitcast.7), calls=%async_computation | async-start | bytes 2097152 | tf_op jit(solution)/shard_map/all_to_all | solution.py:422
  30.0 14.3 %all-to-all-start.1 = ((f32[4,256,128]{2,1,0:T(8,128)}), f32[4,256,128]{2,1,0:T(8,128)S(1)}, u32[]{:S(2)}, u32[]{:S(2)}) async-start(f32[4,256,128]{2,1,0:T(8,128)} %dynamic-slice_bitcast_fusion.2), calls=%async_computation.1 | async-start | bytes 1048576 | tf_op jit(solution)/shard_map/all_to_all | solution.py:448
  35.3 102.8 %all-gather.6.cloned.1.call-start = ((), (), s32[]{:S(2)}) async-start(), calls=%async_computation.5 | async-start | bytes 3932160 | tf_op jit(solution)/shard_map/all_gather | solution.py:442
  45.3 24.2 %collective-permute-start.4 = (f32[4,512,128]{2,1,0:T(8,128)S(1)}, f32[4,512,128]{2,1,0:T(8,128)S(1)}, u32[]{:S(2)}, u32[]{:S(2)}) collective-permute-start(f32[4,512,128]{2,1,0:T(8,128)S(1)} %all-to-all-done.refs_4_.refs_5_), channel_id=1, source_target_pairs={{0,4},{4,8},{8,12},{12,0},{1,5},{5,9},{9,13},{13,1},{2,6},{6,10},{... | collective-permute-start | bytes 3145736 | tf_op jit(solution)/shard_map/ppermute | solution.py:29
  71.0 24.0 %collective-permute-start.30 = (f32[1024,128]{1,0:T(8,128)S(1)}, f32[1024,128]{1,0:T(8,128)}, u32[]{:S(2)}, u32[]{:S(2)}) collective-permute-start(f32[1024,128]{1,0:T(8,128)S(1)} %maximum_select_fusion.3), channel_id=1, source_target_pairs={{0,32},{32,0},{1,33},{33,1},{2,34},{34,2},{3,35},{35,3},{4,36},{36... | collective-permute-start | bytes 1572872 | tf_op jit(solution)/shard_map/ppermute | solution.py:33
  72.6 18.2 %collective-permute-start.49 = (f32[512,128]{1,0:T(8,128)S(1)}, f32[512,128]{1,0:T(8,128)}, u32[]{:S(2)}, u32[]{:S(2)}) collective-permute-start(f32[512,128]{1,0:T(8,128)S(1)} %maximum_select_fusion.6), channel_id=1, source_target_pairs={{0,32},{32,0},{1,33},{33,1},{2,34},{34,2},{3,35},{35,3},{4,36},{36... | collective-permute-start | bytes 786440 | tf_op jit(solution)/shard_map/ppermute | solution.py:33
  91.9 14.8 %collective-permute-start.50 = (f32[1024,128]{1,0:T(8,128)S(1)}, f32[1024,128]{1,0:T(8,128)}, u32[]{:S(2)}, u32[]{:S(2)}) collective-permute-start(f32[1024,128]{1,0:T(8,128)S(1)} %maximum_select_fusion.4), channel_id=1, source_target_pairs={{0,64},{64,0},{1,65},{65,1},{2,66},{66,2},{3,67},{67,3},{4,68},{68... | collective-permute-start | bytes 1572872 | tf_op jit(solution)/shard_map/ppermute | solution.py:33
  97.2 12.5 %all-to-all-start.2 = ((f32[4,256,128]{2,1,0:T(8,128)}), f32[4,256,128]{2,1,0:T(8,128)S(1)}, u32[]{:S(2)}, u32[]{:S(2)}) async-start(f32[4,256,128]{2,1,0:T(8,128)} %dynamic-slice_bitcast_fusion.1), calls=%async_computation.2 | async-start | bytes 1048576 | tf_op jit(solution)/shard_map/all_to_all | solution.py:454
  109.7 15.2 %all-to-all-start.3 = ((f32[4,256,128]{2,1,0:T(8,128)}), f32[4,256,128]{2,1,0:T(8,128)}, u32[]{:S(2)}, u32[]{:S(2)}) async-start(f32[4,256,128]{2,1,0:T(8,128)} %dynamic-slice_bitcast_fusion), calls=%async_computation.3 | async-start | bytes 1048576 | tf_op jit(solution)/shard_map/all_to_all | solution.py:459
  113.9 93.5 %all-gather.4.cloned.1.call-start = ((), (), s32[]{:S(2)}) async-start(), calls=%async_computation.4 | async-start | bytes 2621440 | tf_op jit(solution)/shard_map/all_gather | solution.py:442
  113.9 19.4 %collective-permute-start.8 = (f32[1024,128]{1,0:T(8,128)}, f32[1024,128]{1,0:T(8,128)}, u32[]{:S(2)}, u32[]{:S(2)}) collective-permute-start(f32[1024,128]{1,0:T(8,128)} %refs_10_.1), channel_id=1, source_target_pairs={{0,4},{4,8},{8,12},{12,0},{1,5},{5,9},{9,13},{13,1},{2,6},{6,10},{... | collective-permute-start | bytes 1572872 | tf_op jit(solution)/shard_map/ppermute | solution.py:29
  115.8 19.2 %collective-permute-start.9 = (f32[1024,128]{1,0:T(8,128)}, f32[1024,128]{1,0:T(8,128)}, u32[]{:S(2)}, u32[]{:S(2)}) collective-permute-start(f32[1024,128]{1,0:T(8,128)} %refs_10_.1), channel_id=1, source_target_pairs={{0,12},{4,0},{8,4},{12,8},{1,13},{5,1},{9,5},{13,9},{2,14},{6,2},{... | collective-permute-start | bytes 1572872 | tf_op jit(solution)/shard_map/ppermute | solution.py:29
  117.2 36.5 %collective-permute-start.5 = (f32[4,512,128]{2,1,0:T(8,128)S(1)}, f32[4,512,128]{2,1,0:T(8,128)S(1)}, u32[]{:S(2)}, u32[]{:S(2)}) collective-permute-start(f32[4,512,128]{2,1,0:T(8,128)S(1)} %all-to-all-done.refs_4_.refs_5_), channel_id=1, source_target_pairs={{0,12},{4,0},{8,4},{12,8},{1,13},{5,1},{9,5},{13,9},{2,14},{6,2},{... | collective-permute-start | bytes 3145736 | tf_op jit(solution)/shard_map/ppermute | solution.py:29
  124.9 30.2 %collective-permute-start = (f32[16,2048]{1,0:T(8,128)S(1)}, f32[16,2048]{1,0:T(8,128)S(1)}, u32[]{:S(2)}, u32[]{:S(2)}) collective-permute-start(f32[16,2048]{1,0:T(8,128)S(1)} %copy-done.7), channel_id=1, source_target_pairs={{0,1},{1,2},{2,3},{3,0},{4,5},{5,6},{6,7},{7,4},{8,9},{9,10},{10,1... | collective-permute-start | bytes 393224 | tf_op jit(solution)/shard_map/ppermute | solution.py:29
  125.5 31.8 %collective-permute-start.1 = (f32[16,2048]{1,0:T(8,128)S(1)}, f32[16,2048]{1,0:T(8,128)S(1)}, u32[]{:S(2)}, u32[]{:S(2)}) collective-permute-start(f32[16,2048]{1,0:T(8,128)S(1)} %copy-done.7), channel_id=1, source_target_pairs={{0,2},{1,3},{2,0},{3,1},{4,6},{5,7},{6,4},{7,5},{8,10},{9,11},{10,... | collective-permute-start | bytes 393224 | tf_op jit(solution)/shard_map/ppermute | solution.py:29
  138.1 100.4 %collective-permute-start.21 = (f32[4,1536,128]{2,1,0:T(8,128)}, f32[4,1536,128]{2,1,0:T(8,128)}, u32[]{:S(2)}, u32[]{:S(2)}) collective-permute-start(f32[4,1536,128]{2,1,0:T(8,128)} %bitcast.36), channel_id=1, source_target_pairs={{0,16},{16,0},{1,17},{17,1},{2,18},{18,2},{3,19},{19,3},{4,20},{20... | collective-permute-start | bytes 9437192 | tf_op jit(solution)/shard_map/ppermute | solution.py:33
  138.9 16.1 %collective-permute-start.41 = (f32[8,256]{1,0:T(8,128)S(1)}, f32[8,256]{1,0:T(8,128)S(1)}, u32[]{:S(2)}, u32[]{:S(2)}) collective-permute-start(f32[8,256]{1,0:T(8,128)S(1)} %get-tuple-element.114), channel_id=1, source_target_pairs={{0,16},{16,0},{1,17},{17,1},{2,18},{18,2},{3,19},{19,3},{4,20},{20... | collective-permute-start | bytes 24584 | tf_op jit(solution)/shard_map/ppermute | solution.py:33
  153.7 5.9 %collective-permute-start.2 = (f32[16,2048]{1,0:T(8,128)S(1)}, f32[16,2048]{1,0:T(8,128)S(1)}, u32[]{:S(2)}, u32[]{:S(2)}) collective-permute-start(f32[16,2048]{1,0:T(8,128)S(1)} %copy-done.7), channel_id=1, source_target_pairs={{0,3},{1,0},{2,1},{3,2},{4,7},{5,4},{6,5},{7,6},{8,11},{9,8},{10,9... | collective-permute-start | bytes 393224 | tf_op jit(solution)/shard_map/ppermute | solution.py:29
  155.8 23.1 %collective-permute-start.6 = (f32[2,512,128]{2,1,0:T(8,128)S(1)}, f32[2,512,128]{2,1,0:T(8,128)S(1)}, u32[]{:S(2)}, u32[]{:S(2)}) collective-permute-start(f32[2,512,128]{2,1,0:T(8,128)S(1)} %slice.105), channel_id=1, source_target_pairs={{0,4},{4,8},{8,12},{12,0},{1,5},{5,9},{9,13},{13,1},{2,6},{6,10},{... | collective-permute-start | bytes 1572872 | tf_op jit(solution)/shard_map/ppermute | solution.py:29
  157.9 20.9 %collective-permute-start.7 = (f32[2,512,128]{2,1,0:T(8,128)S(1)}, f32[2,512,128]{2,1,0:T(8,128)S(1)}, u32[]{:S(2)}, u32[]{:S(2)}) collective-permute-start(f32[2,512,128]{2,1,0:T(8,128)S(1)} %slice.106), channel_id=1, source_target_pairs={{0,12},{4,0},{8,4},{12,8},{1,13},{5,1},{9,5},{13,9},{2,14},{6,2},{... | collective-permute-start | bytes 1572872 | tf_op jit(solution)/shard_map/ppermute | solution.py:29
  159.7 17.2 %collective-permute-start.10 = (f32[512,128]{1,0:T(8,128)}, f32[512,128]{1,0:T(8,128)S(1)}, u32[]{:S(2)}, u32[]{:S(2)}) collective-permute-start(f32[512,128]{1,0:T(8,128)} %slice.107), channel_id=1, source_target_pairs={{0,4},{4,8},{8,12},{12,0},{1,5},{5,9},{9,13},{13,1},{2,6},{6,10},{... | collective-permute-start | bytes 786440 | tf_op jit(solution)/shard_map/ppermute | solution.py:29
  161.1 16.5 %collective-permute-start.11 = (f32[512,128]{1,0:T(8,128)}, f32[512,128]{1,0:T(8,128)S(1)}, u32[]{:S(2)}, u32[]{:S(2)}) collective-permute-start(f32[512,128]{1,0:T(8,128)} %slice.108), channel_id=1, source_target_pairs={{0,12},{4,0},{8,4},{12,8},{1,13},{5,1},{9,5},{13,9},{2,14},{6,2},{... | collective-permute-start | bytes 786440 | tf_op jit(solution)/shard_map/ppermute | solution.py:29
  176.9 10.2 %collective-permute-start.31 = (f32[256,128]{1,0:T(8,128)}, f32[256,128]{1,0:T(8,128)S(1)}, u32[]{:S(2)}, u32[]{:S(2)}) collective-permute-start(f32[256,128]{1,0:T(8,128)} %param.25), channel_id=1, source_target_pairs={{0,16},{16,0},{1,17},{17,1},{2,18},{18,2},{3,19},{19,3},{4,20},{20... | collective-permute-start | bytes 393224 | tf_op jit(solution)/shard_map/ppermute | solution.py:33
  177.6 26.7 %collective-permute-start.42 = (f32[4,512]{1,0:T(4,128)S(1)}, f32[4,512]{1,0:T(4,128)S(1)}, u32[]{:S(2)}, u32[]{:S(2)}) collective-permute-start(f32[4,512]{1,0:T(4,128)S(1)} %get-tuple-element.112), channel_id=1, source_target_pairs={{0,32},{32,0},{1,33},{33,1},{2,34},{34,2},{3,35},{35,3},{4,36},{36... | collective-permute-start | bytes 24584 | tf_op jit(solution)/shard_map/ppermute | solution.py:33
  185.5 6.3 %collective-permute-start.13 = (f32[16,1024]{1,0:T(8,128)S(1)}, f32[16,1024]{1,0:T(8,128)S(1)}, u32[]{:S(2)}, u32[]{:S(2)}) collective-permute-start(f32[16,1024]{1,0:T(8,128)S(1)} %get-tuple-element.48), channel_id=1, source_target_pairs={{0,2},{1,3},{2,0},{3,1},{4,6},{5,7},{6,4},{7,5},{8,10},{9,11},{10,... | collective-permute-start | bytes 196616 | tf_op jit(solution)/shard_map/ppermute | solution.py:29
  187.1 5.5 %collective-permute-start.14 = (f32[16,1024]{1,0:T(8,128)S(1)}, f32[16,1024]{1,0:T(8,128)S(1)}, u32[]{:S(2)}, u32[]{:S(2)}) collective-permute-start(f32[16,1024]{1,0:T(8,128)S(1)} %get-tuple-element.49), channel_id=1, source_target_pairs={{0,1},{1,2},{2,3},{3,0},{4,5},{5,6},{6,7},{7,4},{8,9},{9,10},{10,1... | collective-permute-start | bytes 196616 | tf_op jit(solution)/shard_map/ppermute | solution.py:29
  187.1 6.8 %collective-permute-start.12 = (f32[16,1024]{1,0:T(8,128)S(1)}, f32[16,1024]{1,0:T(8,128)S(1)}, u32[]{:S(2)}, u32[]{:S(2)}) collective-permute-start(f32[16,1024]{1,0:T(8,128)S(1)} %get-tuple-element.47), channel_id=1, source_target_pairs={{0,3},{1,0},{2,1},{3,2},{4,7},{5,4},{6,5},{7,6},{8,11},{9,8},{10,9... | collective-permute-start | bytes 196616 | tf_op jit(solution)/shard_map/ppermute | solution.py:29
  191.9 13.2 %collective-permute-start.24 = (f32[4,1024]{1,0:T(4,128)S(1)}, f32[4,1024]{1,0:T(4,128)S(1)}, u32[]{:S(2)}, u32[]{:S(2)}) collective-permute-start(f32[4,1024]{1,0:T(4,128)S(1)} %get-tuple-element.106), channel_id=1, source_target_pairs={{0,32},{32,0},{1,33},{33,1},{2,34},{34,2},{3,35},{35,3},{4,36},{36... | collective-permute-start | bytes 49160 | tf_op jit(solution)/shard_map/ppermute | solution.py:33
  192.6 7.0 %collective-permute-start.32 = (f32[512,128]{1,0:T(8,128)S(1)}, f32[512,128]{1,0:T(8,128)S(1)}, u32[]{:S(2)}, u32[]{:S(2)}) collective-permute-start(f32[512,128]{1,0:T(8,128)S(1)} %maximum_select_fusion.5), channel_id=1, source_target_pairs={{0,32},{32,0},{1,33},{33,1},{2,34},{34,2},{3,35},{35,3},{4,36},{36... | collective-permute-start | bytes 786440 | tf_op jit(solution)/shard_map/ppermute | solution.py:33
  193.9 5.8 %collective-permute-start.15 = (f32[8,1024]{1,0:T(8,128)S(1)}, f32[8,1024]{1,0:T(8,128)S(1)}, u32[]{:S(2)}, u32[]{:S(2)}) collective-permute-start(f32[8,1024]{1,0:T(8,128)S(1)} %get-tuple-element.103), channel_id=1, source_target_pairs={{0,16},{16,0},{1,17},{17,1},{2,18},{18,2},{3,19},{19,3},{4,20},{20... | collective-permute-start | bytes 98312 | tf_op jit(solution)/shard_map/ppermute | solution.py:33
  200.4 6.3 %collective-permute-start.17 = (f32[8,2048]{1,0:T(8,128)S(1)}, f32[8,2048]{1,0:T(8,128)S(1)}, u32[]{:S(2)}, u32[]{:S(2)}) collective-permute-start(f32[8,2048]{1,0:T(8,128)S(1)} %get-tuple-element.52.refs_0_), channel_id=1, source_target_pairs={{0,4},{4,8},{8,12},{12,0},{1,5},{5,9},{9,13},{13,1},{2,6},{6,10},{... | collective-permute-start | bytes 196616 | tf_op jit(solution)/shard_map/ppermute | solution.py:29
  201.0 6.3 %collective-permute-start.18 = (f32[8,2048]{1,0:T(8,128)S(1)}, f32[8,2048]{1,0:T(8,128)S(1)}, u32[]{:S(2)}, u32[]{:S(2)}) collective-permute-start(f32[8,2048]{1,0:T(8,128)S(1)} %get-tuple-element.52.refs_0_), channel_id=1, source_target_pairs={{0,8},{4,12},{8,0},{12,4},{1,9},{5,13},{9,1},{13,5},{2,10},{6,14},... | collective-permute-start | bytes 196616 | tf_op jit(solution)/shard_map/ppermute | solution.py:29
  204.3 33.7 %collective-permute-start.33 = (f32[1536,128]{1,0:T(8,128)S(1)}, f32[1536,128]{1,0:T(8,128)S(1)}, u32[]{:S(2)}, u32[]{:S(2)}) collective-permute-start(f32[1536,128]{1,0:T(8,128)S(1)} %pad_maximum_fusion.1.refs_4_.refs_3_), channel_id=1, source_target_pairs={{0,1},{1,2},{2,3},{3,0},{4,5},{5,6},{6,7},{7,4},{8,9},{9,10},{10,1... | collective-permute-start | bytes 2359304 | tf_op jit(solution)/shard_map/ppermute | solution.py:29
  205.1 32.9 %collective-permute-start.34 = (f32[1536,128]{1,0:T(8,128)S(1)}, f32[1536,128]{1,0:T(8,128)S(1)}, u32[]{:S(2)}, u32[]{:S(2)}) collective-permute-start(f32[1536,128]{1,0:T(8,128)S(1)} %pad_maximum_fusion.1.refs_4_.refs_3_), channel_id=1, source_target_pairs={{0,2},{1,3},{2,0},{3,1},{4,6},{5,7},{6,4},{7,5},{8,10},{9,11},{10,... | collective-permute-start | bytes 2359304 | tf_op jit(solution)/shard_map/ppermute | solution.py:29
  207.3 70.5 %collective-permute-start.51 = (f32[4,1024,128]{2,1,0:T(8,128)}, f32[4,1024,128]{2,1,0:T(8,128)S(1)}, u32[]{:S(2)}, u32[]{:S(2)}) collective-permute-start(f32[4,1024,128]{2,1,0:T(8,128)} %all-gather.4.cloned.1.call-done.wa), channel_id=1, source_target_pairs={{0,16},{16,0},{1,17},{17,1},{2,18},{18,2},{3,19},{19,3},{4,20},{20... | collective-permute-start | bytes 6291464 | tf_op jit(solution)/shard_map/ppermute | solution.py:33
  215.3 29.3 %collective-permute-start.35 = (f32[1536,128]{1,0:T(8,128)S(1)}, f32[1536,128]{1,0:T(8,128)S(1)}, u32[]{:S(2)}, u32[]{:S(2)}) collective-permute-start(f32[1536,128]{1,0:T(8,128)S(1)} %pad_maximum_fusion.1.refs_4_.refs_3_), channel_id=1, source_target_pairs={{0,3},{1,0},{2,1},{3,2},{4,7},{5,4},{6,5},{7,6},{8,11},{9,8},{10,9... | collective-permute-start | bytes 2359304 | tf_op jit(solution)/shard_map/ppermute | solution.py:29
  238.0 11.9 %collective-permute-start.36 = (f32[1536,128]{1,0:T(8,128)S(1)}, f32[1536,128]{1,0:T(8,128)S(1)}, u32[]{:S(2)}, u32[]{:S(2)}) collective-permute-start(f32[1536,128]{1,0:T(8,128)S(1)} %pad_maximum_fusion.1.refs_4_.refs_3_), channel_id=1, source_target_pairs={{0,16},{16,0},{1,17},{17,1},{2,18},{18,2},{3,19},{19,3},{4,20},{20... | collective-permute-start | bytes 2359304 | tf_op jit(solution)/shard_map/ppermute | solution.py:33
  238.1 13.4 %collective-permute-start.37 = (f32[1536,128]{1,0:T(8,128)S(1)}, f32[1536,128]{1,0:T(8,128)S(1)}, u32[]{:S(2)}, u32[]{:S(2)}) collective-permute-start(f32[1536,128]{1,0:T(8,128)S(1)} %collective-permute-done.33.refs_5_.refs_4_), channel_id=1, source_target_pairs={{0,16},{16,0},{1,17},{17,1},{2,18},{18,2},{3,19},{19,3},{4,20},{20... | collective-permute-start | bytes 2359304 | tf_op jit(solution)/shard_map/ppermute | solution.py:33
  238.6 13.8 %collective-permute-start.38 = (f32[1536,128]{1,0:T(8,128)S(1)}, f32[1536,128]{1,0:T(8,128)S(1)}, u32[]{:S(2)}, u32[]{:S(2)}) collective-permute-start(f32[1536,128]{1,0:T(8,128)S(1)} %collective-permute-done.34.refs_6_.refs_5_), channel_id=1, source_target_pairs={{0,16},{16,0},{1,17},{17,1},{2,18},{18,2},{3,19},{19,3},{4,20},{20... | collective-permute-start | bytes 2359304 | tf_op jit(solution)/shard_map/ppermute | solution.py:33
  249.9 10.0 %collective-permute-start.26 = (f32[16,2048]{1,0:T(8,128)S(1)}, f32[16,2048]{1,0:T(8,128)S(1)}, u32[]{:S(2)}, u32[]{:S(2)}) collective-permute-start(f32[16,2048]{1,0:T(8,128)S(1)} %get-tuple-element.58.refs_0_), channel_id=1, source_target_pairs={{0,4},{4,8},{8,12},{12,0},{1,5},{5,9},{9,13},{13,1},{2,6},{6,10},{... | collective-permute-start | bytes 393224 | tf_op jit(solution)/shard_map/ppermute | solution.py:29
  251.5 11.2 %collective-permute-start.27 = (f32[16,2048]{1,0:T(8,128)S(1)}, f32[16,2048]{1,0:T(8,128)S(1)}, u32[]{:S(2)}, u32[]{:S(2)}) collective-permute-start(f32[16,2048]{1,0:T(8,128)S(1)} %get-tuple-element.58.refs_0_), channel_id=1, source_target_pairs={{0,8},{4,12},{8,0},{12,4},{1,9},{5,13},{9,1},{13,5},{2,10},{6,14},... | collective-permute-start | bytes 393224 | tf_op jit(solution)/shard_map/ppermute | solution.py:29
  252.4 10.3 %collective-permute-start.28 = (f32[16,2048]{1,0:T(8,128)S(1)}, f32[16,2048]{1,0:T(8,128)S(1)}, u32[]{:S(2)}, u32[]{:S(2)}) collective-permute-start(f32[16,2048]{1,0:T(8,128)S(1)} %get-tuple-element.58.refs_0_), channel_id=1, source_target_pairs={{0,12},{4,0},{8,4},{12,8},{1,13},{5,1},{9,5},{13,9},{2,14},{6,2},{... | collective-permute-start | bytes 393224 | tf_op jit(solution)/shard_map/ppermute | solution.py:29
  254.3 15.0 %collective-permute-start.43 = (f32[2,1024]{1,0:T(2,128)S(1)}, f32[2,1024]{1,0:T(2,128)S(1)}, u32[]{:S(2)}, u32[]{:S(2)}) collective-permute-start(f32[2,1024]{1,0:T(2,128)S(1)} %get-tuple-element.110), channel_id=1, source_target_pairs={{0,64},{64,0},{1,65},{65,1},{2,66},{66,2},{3,67},{67,3},{4,68},{68... | collective-permute-start | bytes 24584 | tf_op jit(solution)/shard_map/ppermute | solution.py:33
  259.9 9.4 %collective-permute-start.44 = (f32[8,2048]{1,0:T(8,128)S(1)}, f32[8,2048]{1,0:T(8,128)S(1)}, u32[]{:S(2)}, u32[]{:S(2)}) collective-permute-start(f32[8,2048]{1,0:T(8,128)S(1)} %get-tuple-element.65), channel_id=1, source_target_pairs={{0,64},{64,0},{1,65},{65,1},{2,66},{66,2},{3,67},{67,3},{4,68},{68... | collective-permute-start | bytes 196616 | tf_op jit(solution)/shard_map/ppermute | solution.py:33
  268.4 5.5 %collective-permute-start.40 = (f32[8,1024]{1,0:T(8,128)S(1)}, f32[8,1024]{1,0:T(8,128)S(1)}, u32[]{:S(2)}, u32[]{:S(2)}) collective-permute-start(f32[8,1024]{1,0:T(8,128)S(1)} %get-tuple-element.62), channel_id=1, source_target_pairs={{0,64},{64,0},{1,65},{65,1},{2,66},{66,2},{3,67},{67,3},{4,68},{68... | collective-permute-start | bytes 98312 | tf_op jit(solution)/shard_map/ppermute | solution.py:33
  274.5 6.2 %collective-permute-start.45 = (f32[8,2048]{1,0:T(8,128)S(1)}, f32[8,2048]{1,0:T(8,128)S(1)}, u32[]{:S(2)}, u32[]{:S(2)}) collective-permute-start(f32[8,2048]{1,0:T(8,128)S(1)} %s23.1.c0), channel_id=1, source_target_pairs={{0,4},{4,8},{8,12},{12,0},{1,5},{5,9},{9,13},{13,1},{2,6},{6,10},{... | collective-permute-start | bytes 196616 | tf_op jit(solution)/shard_map/ppermute | solution.py:29
  274.6 6.2 %collective-permute-start.46 = (f32[8,2048]{1,0:T(8,128)S(1)}, f32[8,2048]{1,0:T(8,128)S(1)}, u32[]{:S(2)}, u32[]{:S(2)}) collective-permute-start(f32[8,2048]{1,0:T(8,128)S(1)} %s23.1.c0), channel_id=1, source_target_pairs={{0,8},{4,12},{8,0},{12,4},{1,9},{5,13},{9,1},{13,5},{2,10},{6,14},... | collective-permute-start | bytes 196616 | tf_op jit(solution)/shard_map/ppermute | solution.py:29
  287.2 5.5 %collective-permute-start.52 = (f32[8,2048]{1,0:T(8,128)S(1)}, f32[8,2048]{1,0:T(8,128)S(1)}, u32[]{:S(2)}, u32[]{:S(2)}) collective-permute-start(f32[8,2048]{1,0:T(8,128)S(1)} %top.1.c0), channel_id=1, source_target_pairs={{0,4},{4,8},{8,12},{12,0},{1,5},{5,9},{9,13},{13,1},{2,6},{6,10},{... | collective-permute-start | bytes 196616 | tf_op jit(solution)/shard_map/ppermute | solution.py:29
  288.6 5.8 %collective-permute-start.53 = (f32[8,2048]{1,0:T(8,128)S(1)}, f32[8,2048]{1,0:T(8,128)S(1)}, u32[]{:S(2)}, u32[]{:S(2)}) collective-permute-start(f32[8,2048]{1,0:T(8,128)S(1)} %top.1.c0), channel_id=1, source_target_pairs={{0,8},{4,12},{8,0},{12,4},{1,9},{5,13},{9,1},{13,5},{2,10},{6,14},... | collective-permute-start | bytes 196616 | tf_op jit(solution)/shard_map/ppermute | solution.py:29
  306.5 10.0 %collective-permute-start.56 = (f32[16,2048]{1,0:T(8,128)S(1)}, f32[16,2048]{1,0:T(8,128)S(1)}, u32[]{:S(2)}, u32[]{:S(2)}) collective-permute-start(f32[16,2048]{1,0:T(8,128)S(1)} %b2.1.c0), channel_id=1, source_target_pairs={{0,4},{4,8},{8,12},{12,0},{1,5},{5,9},{9,13},{13,1},{2,6},{6,10},{... | collective-permute-start | bytes 393224 | tf_op jit(solution)/shard_map/ppermute | solution.py:29
  306.8 9.7 %collective-permute-start.57 = (f32[16,2048]{1,0:T(8,128)S(1)}, f32[16,2048]{1,0:T(8,128)S(1)}, u32[]{:S(2)}, u32[]{:S(2)}) collective-permute-start(f32[16,2048]{1,0:T(8,128)S(1)} %b2.1.c0), channel_id=1, source_target_pairs={{0,8},{4,12},{8,0},{12,4},{1,9},{5,13},{9,1},{13,5},{2,10},{6,14},... | collective-permute-start | bytes 393224 | tf_op jit(solution)/shard_map/ppermute | solution.py:29
  309.6 6.9 %collective-permute-start.58 = (f32[16,2048]{1,0:T(8,128)S(1)}, f32[16,2048]{1,0:T(8,128)S(1)}, u32[]{:S(2)}, u32[]{:S(2)}) collective-permute-start(f32[16,2048]{1,0:T(8,128)S(1)} %b2.1.c0), channel_id=1, source_target_pairs={{0,12},{4,0},{8,4},{12,8},{1,13},{5,1},{9,5},{13,9},{2,14},{6,2},{... | collective-permute-start | bytes 393224 | tf_op jit(solution)/shard_map/ppermute | solution.py:29
  310.7 5.8 %collective-permute-start.59 = (f32[8,2048]{1,0:T(8,128)S(1)}, f32[8,2048]{1,0:T(8,128)S(1)}, u32[]{:S(2)}, u32[]{:S(2)}) collective-permute-start(f32[8,2048]{1,0:T(8,128)S(1)} %get-tuple-element.68.x3), channel_id=1, source_target_pairs={{0,64},{64,0},{1,65},{65,1},{2,66},{66,2},{3,67},{67,3},{4,68},{68... | collective-permute-start | bytes 196616 | tf_op jit(solution)/shard_map/ppermute | solution.py:33
  317.5 12.6 %collective-permute-start.64 = (f32[2,4,2048]{2,1,0:T(4,128)S(1)}, f32[2,4,2048]{2,1,0:T(4,128)S(1)}, u32[]{:S(2)}, u32[]{:S(2)}) collective-permute-start(f32[2,4,2048]{2,1,0:T(4,128)S(1)} %slice.101.a_mine), channel_id=1, source_target_pairs={{0,32},{32,0},{1,33},{33,1},{2,34},{34,2},{3,35},{35,3},{4,36},{36... | collective-permute-start | bytes 196616 | tf_op jit(solution)/shard_map/ppermute | solution.py:33
  327.8 5.8 %collective-permute-start.62 = (f32[8,2048]{1,0:T(8,128)S(1)}, f32[8,2048]{1,0:T(8,128)S(1)}, u32[]{:S(2)}, u32[]{:S(2)}) collective-permute-start(f32[8,2048]{1,0:T(8,128)S(1)} %get-tuple-element.76), channel_id=1, source_target_pairs={{0,8},{4,12},{8,0},{12,4},{1,9},{5,13},{9,1},{13,5},{2,10},{6,14},... | collective-permute-start | bytes 196616 | tf_op jit(solution)/shard_map/ppermute | solution.py:29
  335.9 18.6 %collective-permute-start.72 = (f32[8,1024]{1,0:T(8,128)S(1)}, f32[8,1024]{1,0:T(8,128)S(1)}, u32[]{:S(2)}, u32[]{:S(2)}) collective-permute-start(f32[8,1024]{1,0:T(8,128)S(1)} %get-tuple-element.100), channel_id=1, source_target_pairs={{0,16},{16,0},{1,17},{17,1},{2,18},{18,2},{3,19},{19,3},{4,20},{20... | collective-permute-start | bytes 98312 | tf_op jit(solution)/shard_map/ppermute | solution.py:33
  336.4 17.4 %collective-permute-start.73 = (f32[8,512]{1,0:T(8,128)S(1)}, f32[8,512]{1,0:T(8,128)S(1)}, u32[]{:S(2)}, u32[]{:S(2)}) collective-permute-start(f32[8,512]{1,0:T(8,128)S(1)} %get-tuple-element.98), channel_id=1, source_target_pairs={{0,16},{16,0},{1,17},{17,1},{2,18},{18,2},{3,19},{19,3},{4,20},{20... | collective-permute-start | bytes 49160 | tf_op jit(solution)/shard_map/ppermute | solution.py:33
  337.0 6.8 %collective-permute-start.66 = (f32[16,1024]{1,0:T(8,128)S(1)}, f32[16,1024]{1,0:T(8,128)S(1)}, u32[]{:S(2)}, u32[]{:S(2)}) collective-permute-start(f32[16,1024]{1,0:T(8,128)S(1)} %maximum_select_fusion.8.refs_0_), channel_id=1, source_target_pairs={{0,1},{1,2},{2,3},{3,0},{4,5},{5,6},{6,7},{7,4},{8,9},{9,10},{10,1... | collective-permute-start | bytes 196616 | tf_op jit(solution)/shard_map/ppermute | solution.py:29
  337.1 6.7 %collective-permute-start.67 = (f32[16,1024]{1,0:T(8,128)S(1)}, f32[16,1024]{1,0:T(8,128)S(1)}, u32[]{:S(2)}, u32[]{:S(2)}) collective-permute-start(f32[16,1024]{1,0:T(8,128)S(1)} %maximum_select_fusion.8.refs_0_), channel_id=1, source_target_pairs={{0,2},{1,3},{2,0},{3,1},{4,6},{5,7},{6,4},{7,5},{8,10},{9,11},{10,... | collective-permute-start | bytes 196616 | tf_op jit(solution)/shard_map/ppermute | solution.py:29
  338.1 6.3 %collective-permute-start.68 = (f32[16,1024]{1,0:T(8,128)S(1)}, f32[16,1024]{1,0:T(8,128)S(1)}, u32[]{:S(2)}, u32[]{:S(2)}) collective-permute-start(f32[16,1024]{1,0:T(8,128)S(1)} %maximum_select_fusion.8.refs_0_), channel_id=1, source_target_pairs={{0,3},{1,0},{2,1},{3,2},{4,7},{5,4},{6,5},{7,6},{8,11},{9,8},{10,9... | collective-permute-start | bytes 196616 | tf_op jit(solution)/shard_map/ppermute | solution.py:29
  349.6 7.5 %collective-permute-start.70 = (f32[16,2048]{1,0:T(8,128)S(1)}, f32[16,2048]{1,0:T(8,128)S(1)}, u32[]{:S(2)}, u32[]{:S(2)}) collective-permute-start(f32[16,2048]{1,0:T(8,128)S(1)} %get-tuple-element.83), channel_id=1, source_target_pairs={{0,2},{1,3},{2,0},{3,1},{4,6},{5,7},{6,4},{7,5},{8,10},{9,11},{10,... | collective-permute-start | bytes 393224 | tf_op jit(solution)/shard_map/ppermute | solution.py:29
  350.6 7.9 %collective-permute-start.71 = (f32[16,2048]{1,0:T(8,128)S(1)}, f32[16,2048]{1,0:T(8,128)S(1)}, u32[]{:S(2)}, u32[]{:S(2)}) collective-permute-start(f32[16,2048]{1,0:T(8,128)S(1)} %get-tuple-element.84), channel_id=1, source_target_pairs={{0,1},{1,2},{2,3},{3,0},{4,5},{5,6},{6,7},{7,4},{8,9},{9,10},{10,1... | collective-permute-start | bytes 393224 | tf_op jit(solution)/shard_map/ppermute | solution.py:29
  352.9 5.6 %collective-permute-start.69 = (f32[16,2048]{1,0:T(8,128)S(1)}, f32[16,2048]{1,0:T(8,128)S(1)}, u32[]{:S(2)}, u32[]{:S(2)}) collective-permute-start(f32[16,2048]{1,0:T(8,128)S(1)} %get-tuple-element.82), channel_id=1, source_target_pairs={{0,3},{1,0},{2,1},{3,2},{4,7},{5,4},{6,5},{7,6},{8,11},{9,8},{10,9... | collective-permute-start | bytes 393224 | tf_op jit(solution)/shard_map/ppermute | solution.py:29
  (49 other events, 816.4 us)
Sparse Core Ops, SparseCore 0:
  45.4 37.0 all-gather.5
  125.0 27.5 all-gather.3

commit v3 on v2

--- a/solution.py
+++ b/solution.py
@@ -160,7 +160,7 @@
     lax.fori_loop(0, 2, body, 0)
 
 
-WEIGHTS = (10, 2, 8, 2)
+WEIGHTS = (10, 2, 2, 8)
 
 
 def forward_kernel(level, n, mode, meta, *refs):
@@ -279,8 +279,9 @@
     part[0:2, :] = part[0:2, :] + b3[...]
 
 
-def top_kernel(meta, c0, c1, c2, c3, wa, wb, x_out, ev, yv, sems):
-    ce, _ = copies_upper(meta, (wa, wb), ev, None, sems)
+def top_kernel(meta, c0, c1, c2, c3, *refs):
+    w_refs, (x_out, ev, yv, sems) = refs[:8], refs[8:]
+    ce, _ = copies_upper(meta, w_refs, ev, None, sems)
     for c in ce:
         c.start()
     c = summed((c0, c1, c2, c3), 2)
@@ -417,55 +418,58 @@
     head = jnp.stack([zi, yi, ci, x0, x1, *lives] + [jnp.int32(0)] * 7).astype(jnp.int32)
     meta = jnp.concatenate([head, *tables])
 
+    bits = [("core", ci), ("x0", x0), ("x1", x1)]
+
+    def joined(v, i):
+        axis, bit = bits[i]
+        return None if v is None else ordered(v, flip(v, axis), bit, 0)
+
+    def half_block(e):
+        return lax.dynamic_index_in_dim(e.reshape(4, 2, 256, B), ci, 1, keepdims=False)
+
+    def half_rows(f):
+        return lax.dynamic_slice_in_dim(f, ci * 512, 512)
+
+    def rows_to_z(e):
+        return lax.all_to_all(e, "z", 0, 0, tiled=True).reshape(1024, B)
+
+    def gathered(e, f):
+        return lax.all_gather(jnp.concatenate([e, f], 0), "y", axis=0, tiled=False)
+
+    def spread(v, i):
+        axis, bit = bits[i]
+        keep, give = halves(v, bit)
+        return ordered(keep, flip(give, axis), bit, 1)
+
+    gate = lax.optimization_barrier
     e0 = jnp.swapaxes(dinv0.reshape(4, 4, B, B), 0, 1).reshape(4, 512, B)
-    f0 = ring(off0, "z", 0)
     e0 = lax.all_to_all(e0, "y", 0, 0, tiled=True)
-
-    bits = [("core", ci), ("x0", x0), ("x1", x1)]
-
-    def grouped(v, levels):
-        for axis, bit in bits[:levels]:
-            v = ordered(v, flip(v, axis), bit, 0)
-        return v
-
-    def half_block(e, levels):
-        e = grouped(e, levels)
-        return lax.dynamic_index_in_dim(e.reshape(4, 2, 256, B), ci, 1, keepdims=False)
-
-    def packed(e, f, levels):
-        e = e.reshape(1024, B)
-        if f is None:
-            return e
-        return jnp.concatenate([e, lax.dynamic_slice_in_dim(grouped(f, levels), ci * 512, 512)], 0)
-
-    def gathered(e):
-        mine = lax.all_gather(e, "y", axis=0, tiled=False)
-        return mine, flip(mine, "core")
-
-    e1 = half_block(dinv1, 1)
-    e0, e1 = lax.optimization_barrier((e0, e1))
-    e0 = ring(e0, "z", 0)
-    e1 = lax.all_to_all(e1, "z", 0, 0, tiled=True)
-    w0 = e0 + f0
-    w1 = gathered(packed(e1, off1, 1))
-    near, e1, dinv2, off2, dinv3, rhs1, rhs2, rhs3 = lax.optimization_barrier(
-        (e0[1], e1, dinv2, off2, dinv3, rhs1, rhs2, rhs3)
-    )
-    e2 = lax.all_to_all(half_block(dinv2, 2), "z", 0, 0, tiled=True)
-    pieces = gather4(packed(e2, off2, 2), "y")
-    w2 = pieces + [flip(v, "core") for v in pieces]
-    e3 = half_block(dinv3, 3)
-    e2, e3 = lax.optimization_barrier((e2, e3))
-    w3 = gathered(packed(lax.all_to_all(e3, "z", 0, 0, tiled=True), None, 3))
-
-    def spread(rhs, levels):
-        v = rhs
-        for axis, bit in bits[:levels]:
-            keep, give = halves(v, bit)
-            v = ordered(keep, flip(give, axis), bit, 1)
-        return v
-
-    b1, b2, b3 = spread(rhs1, 1), spread(rhs2, 2), spread(rhs3, 3)
+    fa, fb = shift(off0, "z", 1), shift(off0, "z", -1)
+    e1 = rows_to_z(half_block(joined(dinv1, 0)))
+    f1 = half_rows(joined(off1, 0))
+    e2, f2 = joined(dinv2, 0), joined(off2, 0)
+    e3 = joined(joined(joined(dinv3, 2), 1), 0).reshape(2, 2, 2, 256, B)
+    e3 = half_block(e3.transpose(2, 1, 0, 3, 4))
+    e0, fa, fb, e1, f1, e2, f2, e3 = gate((e0, fa, fb, e1, f1, e2, f2, e3))
+    m1 = gathered(e1, f1)
+
+    ea, eb = shift(e0, "z", 1), shift(e0, "z", -1)
+    fc, fd = shift(fa[:512], "z", 1), shift(fb[512:], "z", -1)
+    e2, f2 = half_block(joined(e2, 1)), half_rows(joined(f2, 1))
+    e3 = rows_to_z(e3)
+    b1, b2, b3 = spread(rhs1, 0), spread(rhs2, 0), spread(rhs3, 0)
+    ea, eb, fc, fd, e2, f2, e3, b1, b2, b3 = gate((ea, eb, fc, fd, e2, f2, e3, b1, b2, b3))
+
+    ec, ed = shift(ea[:2], "z", 1), shift(eb[2:], "z", -1)
+    e2 = rows_to_z(e2)
+    w3 = gather4(e3, "y")
+    b2, b3 = spread(b2, 1), spread(b3, 1)
+    c0 = gather4(rhs0, "y")
+    ec, ed, e2, b2, b3, c0, w3 = gate((ec, ed, e2, b2, b3, c0, w3))
+    w0 = [e0, ea, eb, ec, ed, off0, fa, fb, fc, fd]
+    m2 = gathered(e2, f2)
+    b3 = spread(b3, 2)
+    w3 = w3 + [flip(v, "core") for v in w3]
 
     dma = pltpu.SemaphoreType.DMA
     ev, fv = pltpu.VMEM((512, ORDER), f32), pltpu.VMEM((1024, 512), f32)
@@ -478,8 +482,10 @@
 
     y0, *u = call(
         functools.partial(forward_kernel, 0, 64, "rs"), "f0", [(64, 512)] + [(16, 1024)] * 4,
-        [ev, fv, *work(64), dma((24,))], meta, gather4(rhs0, "y"), w0, flops(64),
-    )
+        [ev, fv, *work(64), dma((24,))], meta, c0, w0, flops(64),
+    )
+    m1, _ = gate((m1, y0))
+    w1 = m1, flip(m1, "core")
     parts = scatter4(u, "y")
     u = (parts[0] + parts[1]) + (parts[2] + parts[3])
     keep, give = halves(u, ci)
@@ -496,6 +502,8 @@
         s12_kernel, "s12", [(16, ORDER), (8, ORDER), (8, ORDER)],
         [pltpu.VMEM((2, 16, ORDER), f32)], meta, [keep, flip(give, "x0"), b2, pk, pr],
     )
+    m2, _ = gate((m2, part))
+    w2 = m2, flip(m2, "core")
     recv3 = flip(give3, "x1")
     y2, keep, give = call(
         functools.partial(forward_kernel, 2, 16, "ar"), "f2", [(16, 512), (8, 1024), (8, 1024)],

time: 367 us -> 306 us (0.83)
  waiting for transfers between devices: 184 us -> 103 us
  other arithmetic: 11.6 us -> 21.5 us
  local copies, waits for them, and re-layouts: 17.5 us -> 23.9 us
    ppermute x41, waiting for transfers between devices: 100 us -> 51 us  [shift(): return lax.ppermute(v, axis, [(i, (i + s) % 4) for i in range(4)])]
    ppermute x34, waiting for transfers between devices: 55.4 us -> 35.7 us  [flip(): return lax.ppermute(v, axis, [(0, 1), (1, 0)])]
    all_to_all x1, waiting for transfers between devices: 14.7 us -> 3.11 us  [local(): e0 = lax.all_to_all(e0, 'y', 0, 0, tiled=True)]
    select_n x19, other arithmetic: 7.02 us -> 16.2 us  [ordered(): jnp.where(bit == 0, jnp.concatenate([mine, other], dim), jnp.concatenate(...]
    unnamed x64 -> x58, local copies, waits for them, and re-layouts: 3.38 us -> 10.2 us
  transfers between devices with their start and end apart: 81 -> 81, of which waited for: 37 -> 38; matrix products, arithmetic and copies ran while one was open for 7% -> 11% of each run, Pallas kernels for 8% -> 10%
where the time goes in v3:
time: 306 us; the launch traced here: 304 us
  waiting for transfers between devices  103 us (34%)
  starting transfers between devices  99 us (32%)
  Pallas kernels  42.3 us (14%)
  local copies, waits for them, and re-layouts  23.9 us (8%)
  other arithmetic  21.5 us (7%)
  between operations  14.7 us (5%)
    ppermute x41, starting transfers between devices, shift(): return lax.ppermute(v, axis, [(i, (i + s) % 4) for i in range(4)])  53.9 us
    ppermute x41, waiting for transfers between devices, shift(): return lax.ppermute(v, axis, [(i, (i + s) % 4) for i in range(4)])  51 us
    pallas_call x13, Pallas kernels, call(): pl.pallas_call(kernel, out_shape=[jax.ShapeDtypeStruct(s, f32) for s in s...  42.3 us
    ppermute x34, waiting for transfers between devices, flip(): return lax.ppermute(v, axis, [(0, 1), (1, 0)])  35.7 us
    ppermute x34, starting transfers between devices, flip(): return lax.ppermute(v, axis, [(0, 1), (1, 0)])  26.8 us
    select_n x19, other arithmetic, ordered(): jnp.where(bit == 0, jnp.concatenate([mine, other], dim), jnp.concatenate(...  16.2 us
    all_to_all x3, starting transfers between devices, rows_to_z(): return lax.all_to_all(e, 'z', 0, 0, tiled=True).reshape(1024, B)  13.6 us
    all_to_all x3, waiting for transfers between devices, rows_to_z(): return lax.all_to_all(e, 'z', 0, 0, tiled=True).reshape(1024, B)  13.2 us
  transfers between devices with their start and end apart: 81, of which 38 were waited for; matrix products, arithmetic and copies ran while one was open for 11% of the time, Pallas kernels for 10%

profile of v3, /device:TPU:0, one launch (start us, length us, event | category | flops | bytes accessed | tf_op | source)
XLA Modules:
  0.0 304.3 jit_solution(12551210097189003283)
XLA Ops:
  7.2 3.2 %collective-permute-start.6 = (f32[256,128]{1,0:T(8,128)}, f32[256,128]{1,0:T(8,128)S(1)}, u32[]{:S(2)}, u32[]{:S(2)}) collective-permute-start(f32[256,128]{1,0:T(8,128)} %param.22), channel_id=1, source_target_pairs={{0,64},{64,0},{1,65},{65,1},{2,66},{66,2},{3,67},{67,3},{4,68},{68... | collective-permute-start | bytes 393224 | tf_op jit(solution)/shard_map/ppermute | solution.py:33
  10.4 3.7 %collective-permute-done.6 = f32[256,128]{1,0:T(8,128)S(1)} collective-permute-done((f32[256,128]{1,0:T(8,128)}, f32[256,128]{1,0:T(8,128)S(1)}, u32[]{:S(2)}, u32[]{:S(2)}) %collective-permute-start.6) | collective-permute-done | bytes 131104 | tf_op jit(solution)/shard_map/ppermute | solution.py:33
  15.1 1.8 collective-permute-start.7
  16.9 2.4 copy.19
  19.3 4.5 %all-to-all-start = ((f32[4,512,128]{2,1,0:T(8,128)}), f32[4,512,128]{2,1,0:T(8,128)S(1)}, u32[]{:S(2)}, u32[]{:S(2)}) async-start(f32[4,512,128]{2,1,0:T(8,128)} %bitcast.7), calls=%async_computation | async-start | bytes 2097152 | tf_op jit(solution)/shard_map/all_to_all | solution.py:446
  23.9 1.9 collective-permute-start
  25.9 2.2 collective-permute-start.1
  28.1 1.7 maximum_select_fusion.5
  29.8 1.9 maximum_select_fusion.4
  32.2 2.0 maximum_select_fusion.3
  36.4 3.1 %all-to-all-done.refs_4_.refs_5_ = f32[4,512,128]{2,1,0:T(8,128)S(1)} async-done(((f32[4,512,128]{2,1,0:T(8,128)}), f32[4,512,128]{2,1,0:T(8,128)S(1)}, u32[]{:S(2)}, u32[]{:S(2)}) %all-to-all-start) | async-done | bytes 1048608 | tf_op jit(solution)/shard_map/all_to_all | solution.py:446
  39.5 5.3 %all-to-all-start.1 = ((f32[4,256,128]{2,1,0:T(8,128)}), f32[4,256,128]{2,1,0:T(8,128)S(1)}, u32[]{:S(2)}, u32[]{:S(2)}) async-start(f32[4,256,128]{2,1,0:T(8,128)} %dynamic-slice_bitcast_fusion.2), calls=%async_computation.1 | async-start | bytes 1048576 | tf_op jit(solution)/shard_map/all_to_all | solution.py:434
  48.6 5.3 %all-to-all-done.1 = f32[4,256,128]{2,1,0:T(8,128)S(1)} async-done(((f32[4,256,128]{2,1,0:T(8,128)}), f32[4,256,128]{2,1,0:T(8,128)S(1)}, u32[]{:S(2)}, u32[]{:S(2)}) %all-to-all-start.1) | async-done | bytes 524320 | tf_op jit(solution)/shard_map/all_to_all | solution.py:434
  65.2 4.1 %all-to-all-start.2 = ((f32[4,256,128]{2,1,0:T(8,128)}), f32[4,256,128]{2,1,0:T(8,128)}, u32[]{:S(2)}, u32[]{:S(2)}) async-start(f32[4,256,128]{2,1,0:T(8,128)} %dynamic-slice_bitcast_fusion.1), calls=%async_computation.2 | async-start | bytes 1048576 | tf_op jit(solution)/shard_map/all_to_all | solution.py:434
  69.3 10.0 %collective-permute-done.14 = f32[512,128]{1,0:T(8,128)} collective-permute-done((f32[512,128]{1,0:T(8,128)}, f32[512,128]{1,0:T(8,128)}, u32[]{:S(2)}, u32[]{:S(2)}) %collective-permute-start.14) | collective-permute-done | bytes 262176 | tf_op jit(solution)/shard_map/ppermute | solution.py:33
  79.9 1.8 fusion.1
  81.7 2.7 collective-permute-start.12
  84.4 1.7 maximum_select_fusion.2
  87.0 7.8 %collective-permute-done.11.refs_12_.refs_13_ = f32[512,128]{1,0:T(8,128)S(1)} collective-permute-done((f32[512,128]{1,0:T(8,128)}, f32[512,128]{1,0:T(8,128)S(1)}, u32[]{:S(2)}, u32[]{:S(2)}) %collective-permute-start.11) | collective-permute-done | bytes 262176 | tf_op jit(solution)/shard_map/ppermute | solution.py:29
  96.8 2.6 collective-permute-start.24
  103.2 3.2 %collective-permute-start.19 = (f32[2,512,128]{2,1,0:T(8,128)}, f32[2,512,128]{2,1,0:T(8,128)}, u32[]{:S(2)}, u32[]{:S(2)}) collective-permute-start(f32[2,512,128]{2,1,0:T(8,128)} %slice.92), channel_id=1, source_target_pairs={{0,12},{4,0},{8,4},{12,8},{1,13},{5,1},{9,5},{13,9},{2,14},{6,2},{... | collective-permute-start | bytes 1572872 | tf_op jit(solution)/shard_map/ppermute | solution.py:29
  106.5 2.3 collective-permute-start.26
  110.0 4.1 %all-to-all-start.3 = ((f32[4,256,128]{2,1,0:T(8,128)}), f32[4,256,128]{2,1,0:T(8,128)}, u32[]{:S(2)}, u32[]{:S(2)}) async-start(f32[4,256,128]{2,1,0:T(8,128)} %dynamic-slice_bitcast_fusion), calls=%async_computation.3 | async-start | bytes 1048576 | tf_op jit(solution)/shard_map/all_to_all | solution.py:434
  114.4 7.9 %all-to-all-done.3 = f32[4,256,128]{2,1,0:T(8,128)} async-done(((f32[4,256,128]{2,1,0:T(8,128)}), f32[4,256,128]{2,1,0:T(8,128)}, u32[]{:S(2)}, u32[]{:S(2)}) %all-to-all-start.3) | async-done | bytes 524320 | tf_op jit(solution)/shard_map/all_to_all | solution.py:434
  122.3 8.1 %collective-permute-done.25.refs_1_ = f32[1024,128]{1,0:T(8,128)} collective-permute-done((f32[1024,128]{1,0:T(8,128)}, f32[1024,128]{1,0:T(8,128)}, u32[]{:S(2)}, u32[]{:S(2)}) %collective-permute-start.25) | collective-permute-done | bytes 524320 | tf_op jit(solution)/shard_map/ppermute | solution.py:29
  130.9 2.1 pad_maximum_fusion.1
  134.1 2.6 concatenate.123.meta
  141.8 5.9 %f0.1 = (f32[64,512]{1,0:T(8,128)S(1)}, f32[16,1024]{1,0:T(8,128)S(1)}, f32[16,1024]{1,0:T(8,128)S(1)}, f32[16,1024]{1,0:T(8,128)S(1)}, f32[16,1024]{1,0:T(8,128)S(1)}) custom-call(s32[64]{0:T(128)S(1)} %concatenate.123.meta, f32[16,2048]{1,0:T(8,128)S(1)} %copy-done.13, f32[16,2048]{1,0:T(8,128)} %collective-permute-done.22.refs_1_, ...), custom_call_target="tpu_custom_call" | custom-call | flops 2415919104 | bytes 6815744 | tf_op jit(solution)/shard_map/f0/pallas_call | solution.py:393
  149.7 2.3 collective-permute-start.28
  152.9 3.3 %collective-permute-done.28 = f32[16,1024]{1,0:T(8,128)S(1)} collective-permute-done((f32[16,1024]{1,0:T(8,128)}, f32[16,1024]{1,0:T(8,128)S(1)}, u32[]{:S(2)}, u32[]{:S(2)}) %collective-permute-start.28) | collective-permute-done | bytes 65568 | tf_op jit(solution)/shard_map/ppermute | solution.py:29
  156.3 3.8 %collective-permute-done.29 = f32[16,1024]{1,0:T(8,128)S(1)} collective-permute-done((f32[16,1024]{1,0:T(8,128)}, f32[16,1024]{1,0:T(8,128)S(1)}, u32[]{:S(2)}, u32[]{:S(2)}) %collective-permute-start.29) | collective-permute-done | bytes 65568 | tf_op jit(solution)/shard_map/ppermute | solution.py:29
  162.7 1.9 collective-permute-start.33
  166.6 2.9 collective-permute-done.32.refs_1_
  170.1 1.8 copy-done.18
  171.8 5.9 %f1.1 = (f32[32,512]{1,0:T(8,128)S(1)}, f32[16,1024]{1,0:T(8,128)S(1)}, f32[16,1024]{1,0:T(8,128)S(1)}) custom-call(s32[64]{0:T(128)S(1)} %concatenate.123.meta, f32[8,2048]{1,0:T(8,128)S(1)} %get-tuple-element.94.refs_0_, f32[8,2048]{1,0:T(8,128)S(1)} %collective-permute-done.32.refs_1_, f32[8,2048]{1,0:T(8,128)S(1)} %collective-permute-done.33.refs_2_, ...), custom_call_target="tpu_custom_call" | custom-call | flops 1207959552 | bytes 6553600 | tf_op jit(solution)/shard_map/f1/pallas_call | solution.py:393
  178.5 3.6 %collective-permute-done.36.recv = f32[16,1024]{1,0:T(8,128)S(1)} collective-permute-done((f32[16,1024]{1,0:T(8,128)S(1)}, f32[16,1024]{1,0:T(8,128)S(1)}, u32[]{:S(2)}, u32[]{:S(2)}) %collective-permute-start.36) | collective-permute-done | bytes 65568 | tf_op jit(solution)/shard_map/ppermute | solution.py:33
  184.0 2.8 collective-permute-start.39
  186.9 2.8 collective-permute-start.43
  189.7 2.4 collective-permute-done.43
  194.0 2.7 collective-permute-start.44
  196.7 5.7 %f2.1 = (f32[16,512]{1,0:T(8,128)S(1)}, f32[8,1024]{1,0:T(8,128)S(1)}, f32[8,1024]{1,0:T(8,128)S(1)}) custom-call(s32[64]{0:T(128)S(1)} %concatenate.123.meta, f32[16,2048]{1,0:T(8,128)S(1)} %get-tuple-element.104.refs_0_, f32[16,2048]{1,0:T(8,128)S(1)} %collective-permute-done.38.refs_1_, f32[16,2048]{1,0:T(8,128)S(1)} %collective-permute-done.39.refs_2_, ...), custom_call_target="tpu_custom_call" | custom-call | flops 603979776 | bytes 6815744 | tf_op jit(solution)/shard_map/f2/pallas_call | solution.py:393
  202.5 1.8 collective-permute-start.42
  204.3 3.7 %collective-permute-done.42.recv = f32[8,1024]{1,0:T(8,128)S(1)} collective-permute-done((f32[8,1024]{1,0:T(8,128)S(1)}, f32[8,1024]{1,0:T(8,128)S(1)}, u32[]{:S(2)}, u32[]{:S(2)}) %collective-permute-start.42) | collective-permute-done | bytes 32800 | tf_op jit(solution)/shard_map/ppermute | solution.py:33
  209.8 2.5 collective-permute-start.46
  216.6 5.6 %top.1.c0 = f32[8,2048]{1,0:T(8,128)S(1)} custom-call(s32[64]{0:T(128)S(1)} %concatenate.123.meta, f32[8,2048]{1,0:T(8,128)S(1)} %s23.1.c0, f32[8,2048]{1,0:T(8,128)S(1)} %collective-permute-done.45.c1, f32[8,2048]{1,0:T(8,128)S(1)} %collective-permute-done.46.c2, f32[8,2048]{1,0:T(8,128)S(1)} %collective-permute-done.47.c3, f32[1024,128]{1,0:T(8,128)} %bitcast.17.refs_0_, ...), custom_call_target="tpu_custom_call" | custom-call | flops 301989888 | bytes 4456448 | tf_op jit(solution)/shard_map/top/pallas_call | solution.py:393
  222.7 2.8 collective-permute-start.53
  230.4 1.9 collective-permute-start.55
  232.3 3.6 %collective-permute-done.55.refs_1_ = f32[8,1024]{1,0:T(8,128)S(1)} collective-permute-done((f32[8,1024]{1,0:T(8,128)S(1)}, f32[8,1024]{1,0:T(8,128)S(1)}, u32[]{:S(2)}, u32[]{:S(2)}) %collective-permute-start.55) | collective-permute-done | bytes 32800 | tf_op jit(solution)/shard_map/ppermute | solution.py:33
  235.9 4.9 %b2.1.c0 = f32[16,2048]{1,0:T(8,128)S(1)} custom-call(s32[64]{0:T(128)S(1)} %concatenate.123.meta, f32[1,8,2048]{2,1,0:T(8,128)S(1)} %bitcast.39, f32[8,1024]{1,0:T(8,128)S(1)} %collective-permute-done.55.refs_1_, f32[16,512]{1,0:T(8,128)S(1)} %get-tuple-element.119.refs_2_, f32[4,1536,128]{2,1,0:T(8,128)} %bitcast.45, f32[4,1536,128]{2,1,0:T(8,128)} %copy-done.19), custom_call_target="tpu_custom_call" | custom-call | flops 603979776 | bytes 6422528 | tf_op jit(solution)/shard_map/b2/pallas_call | solution.py:393
  241.8 2.8 collective-permute-start.57
  245.1 1.8 collective-permute-start.59
  246.9 4.0 %collective-permute-done.59.x3r = f32[8,2048]{1,0:T(8,128)S(1)} collective-permute-done((f32[8,2048]{1,0:T(8,128)S(1)}, f32[8,2048]{1,0:T(8,128)S(1)}, u32[]{:S(2)}, u32[]{:S(2)}) %collective-permute-start.59) | collective-permute-done | bytes 65568 | tf_op jit(solution)/shard_map/ppermute | solution.py:33
  251.9 1.8 collective-permute-start.64
  253.7 2.1 collective-permute-done.60.refs_1_
  255.9 5.1 %b1.1 = (f32[8,2048]{1,0:T(8,128)S(1)}, f32[8,2048]{1,0:T(8,128)S(1)}, f32[8,2048]{1,0:T(8,128)S(1)}, f32[8,2048]{1,0:T(8,128)S(1)}) custom-call(s32[64]{0:T(128)S(1)} %concatenate.123.meta, f32[2,16,2048]{2,1,0:T(8,128)S(1)} %get-tuple-element.120.refs_0_, f32[16,1024]{1,0:T(8,128)S(1)} %collective-permute-done.60.refs_1_, ...), custom_call_target="tpu_custom_call" | custom-call | flops 1207959552 | bytes 6684672 | tf_op jit(solution)/shard_map/b1/pallas_call | solution.py:393
  262.3 2.4 collective-permute-start.62
  265.4 2.7 collective-permute-done.62.c2
  268.1 2.2 collective-permute-done.63.c3
  273.3 3.4 %collective-permute-start.67 = (f32[16,1024]{1,0:T(8,128)S(1)}, f32[16,1024]{1,0:T(8,128)S(1)}, u32[]{:S(2)}, u32[]{:S(2)}) collective-permute-start(f32[16,1024]{1,0:T(8,128)S(1)} %maximum_select_fusion.8.refs_0_), channel_id=1, source_target_pairs={{0,2},{1,3},{2,0},{3,1},{4,6},{5,7},{6,4},{7,5},{8,10},{9,11},{10,... | collective-permute-start | bytes 196616 | tf_op jit(solution)/shard_map/ppermute | solution.py:29
  278.2 2.0 collective-permute-done.67.refs_2_
  281.0 5.2 %b0.1 = (f32[16,2048]{1,0:T(8,128)S(1)}, f32[16,2048]{1,0:T(8,128)S(1)}, f32[16,2048]{1,0:T(8,128)S(1)}, f32[16,2048]{1,0:T(8,128)S(1)}) custom-call(s32[64]{0:T(128)S(1)} %concatenate.123.meta, f32[16,1024]{1,0:T(8,128)S(1)} %maximum_select_fusion.8.refs_0_, f32[16,1024]{1,0:T(8,128)S(1)} %collective-permute-done.66.refs_1_, ...), custom_call_target="tpu_custom_call" | custom-call | flops 2415919104 | bytes 6684672 | tf_op jit(solution)/shard_map/b0/pallas_call | solution.py:393
  286.2 1.8 collective-permute-start.69
  290.4 2.9 collective-permute-done.69
  293.4 2.3 collective-permute-done.70
  (220 shorter events, 72.3 us)
Async XLA Ops:
  7.2 6.9 %collective-permute-start.6 = (f32[256,128]{1,0:T(8,128)}, f32[256,128]{1,0:T(8,128)S(1)}, u32[]{:S(2)}, u32[]{:S(2)}) collective-permute-start(f32[256,128]{1,0:T(8,128)} %param.22), channel_id=1, source_target_pairs={{0,64},{64,0},{1,65},{65,1},{2,66},{66,2},{3,67},{67,3},{4,68},{68... | collective-permute-start | bytes 393224 | tf_op jit(solution)/shard_map/ppermute | solution.py:33
  10.4 23.8 %collective-permute-start.2 = (f32[1024,128]{1,0:T(8,128)}, f32[1024,128]{1,0:T(8,128)}, u32[]{:S(2)}, u32[]{:S(2)}) collective-permute-start(f32[1024,128]{1,0:T(8,128)} %param.20), channel_id=1, source_target_pairs={{0,16},{16,0},{1,17},{17,1},{2,18},{18,2},{3,19},{19,3},{4,20},{20... | collective-permute-start | bytes 1572872 | tf_op jit(solution)/shard_map/ppermute | solution.py:33
  15.1 14.7 %collective-permute-start.7 = (f32[512,128]{1,0:T(8,128)S(1)}, f32[512,128]{1,0:T(8,128)}, u32[]{:S(2)}, u32[]{:S(2)}) collective-permute-start(f32[512,128]{1,0:T(8,128)S(1)} %maximum_select_fusion.6), channel_id=1, source_target_pairs={{0,32},{32,0},{1,33},{33,1},{2,34},{34,2},{3,35},{35,3},{4,36},{36... | collective-permute-start | bytes 786440 | tf_op jit(solution)/shard_map/ppermute | solution.py:33
  16.9 9.0 %collective-permute-start.5 = (f32[256,128]{1,0:T(8,128)}, f32[256,128]{1,0:T(8,128)}, u32[]{:S(2)}, u32[]{:S(2)}) collective-permute-start(f32[256,128]{1,0:T(8,128)} %param.25), channel_id=1, source_target_pairs={{0,16},{16,0},{1,17},{17,1},{2,18},{18,2},{3,19},{19,3},{4,20},{20... | collective-permute-start | bytes 393224 | tf_op jit(solution)/shard_map/ppermute | solution.py:33
  19.3 20.2 %all-to-all-start = ((f32[4,512,128]{2,1,0:T(8,128)}), f32[4,512,128]{2,1,0:T(8,128)S(1)}, u32[]{:S(2)}, u32[]{:S(2)}) async-start(f32[4,512,128]{2,1,0:T(8,128)} %bitcast.7), calls=%async_computation | async-start | bytes 2097152 | tf_op jit(solution)/shard_map/all_to_all | solution.py:446
  23.7 7.9 %collective-permute-start.4 = (f32[512,128]{1,0:T(8,128)}, f32[512,128]{1,0:T(8,128)}, u32[]{:S(2)}, u32[]{:S(2)}) collective-permute-start(f32[512,128]{1,0:T(8,128)} %param.21), channel_id=1, source_target_pairs={{0,16},{16,0},{1,17},{17,1},{2,18},{18,2},{3,19},{19,3},{4,20},{20... | collective-permute-start | bytes 786440 | tf_op jit(solution)/shard_map/ppermute | solution.py:33
  23.9 24.6 %collective-permute-start = (f32[1024,128]{1,0:T(8,128)S(1)}, f32[1024,128]{1,0:T(8,128)S(1)}, u32[]{:S(2)}, u32[]{:S(2)}) collective-permute-start(f32[1024,128]{1,0:T(8,128)S(1)} %copy-done.7), channel_id=1, source_target_pairs={{0,4},{4,8},{8,12},{12,0},{1,5},{5,9},{9,13},{13,1},{2,6},{6,10},{... | collective-permute-start | bytes 1572872 | tf_op jit(solution)/shard_map/ppermute | solution.py:29
  25.9 22.7 %collective-permute-start.1 = (f32[1024,128]{1,0:T(8,128)S(1)}, f32[1024,128]{1,0:T(8,128)S(1)}, u32[]{:S(2)}, u32[]{:S(2)}) collective-permute-start(f32[1024,128]{1,0:T(8,128)S(1)} %copy-done.7), channel_id=1, source_target_pairs={{0,12},{4,0},{8,4},{12,8},{1,13},{5,1},{9,5},{13,9},{2,14},{6,2},{... | collective-permute-start | bytes 1572872 | tf_op jit(solution)/shard_map/ppermute | solution.py:29
  29.8 15.0 %collective-permute-start.3 = (f32[512,128]{1,0:T(8,128)}, f32[512,128]{1,0:T(8,128)}, u32[]{:S(2)}, u32[]{:S(2)}) collective-permute-start(f32[512,128]{1,0:T(8,128)} %param.24), channel_id=1, source_target_pairs={{0,16},{16,0},{1,17},{17,1},{2,18},{18,2},{3,19},{19,3},{4,20},{20... | collective-permute-start | bytes 786440 | tf_op jit(solution)/shard_map/ppermute | solution.py:33
  31.7 14.3 %collective-permute-start.8 = (f32[1024,128]{1,0:T(8,128)}, f32[1024,128]{1,0:T(8,128)}, u32[]{:S(2)}, u32[]{:S(2)}) collective-permute-start(f32[1024,128]{1,0:T(8,128)} %maximum_select_fusion.4), channel_id=1, source_target_pairs={{0,16},{16,0},{1,17},{17,1},{2,18},{18,2},{3,19},{19,3},{4,20},{20... | collective-permute-start | bytes 1572872 | tf_op jit(solution)/shard_map/ppermute | solution.py:33
  39.5 14.4 %all-to-all-start.1 = ((f32[4,256,128]{2,1,0:T(8,128)}), f32[4,256,128]{2,1,0:T(8,128)S(1)}, u32[]{:S(2)}, u32[]{:S(2)}) async-start(f32[4,256,128]{2,1,0:T(8,128)} %dynamic-slice_bitcast_fusion.2), calls=%async_computation.1 | async-start | bytes 1048576 | tf_op jit(solution)/shard_map/all_to_all | solution.py:434
  44.8 104.9 %all-gather.5.cloned.1.call-start = ((), (), s32[]{:S(2)}) async-start(), calls=%async_computation.4 | async-start | bytes 3932160 | tf_op jit(solution)/shard_map/all_gather | solution.py:437
  56.3 43.1 %collective-permute-start.10 = (f32[4,512,128]{2,1,0:T(8,128)S(1)}, f32[4,512,128]{2,1,0:T(8,128)S(1)}, u32[]{:S(2)}, u32[]{:S(2)}) collective-permute-start(f32[4,512,128]{2,1,0:T(8,128)S(1)} %all-to-all-done.refs_4_.refs_5_), channel_id=1, source_target_pairs={{0,12},{4,0},{8,4},{12,8},{1,13},{5,1},{9,5},{13,9},{2,14},{6,2},{... | collective-permute-start | bytes 3145736 | tf_op jit(solution)/shard_map/ppermute | solution.py:29
  57.4 42.0 %collective-permute-start.9 = (f32[4,512,128]{2,1,0:T(8,128)S(1)}, f32[4,512,128]{2,1,0:T(8,128)S(1)}, u32[]{:S(2)}, u32[]{:S(2)}) collective-permute-start(f32[4,512,128]{2,1,0:T(8,128)S(1)} %all-to-all-done.refs_4_.refs_5_), channel_id=1, source_target_pairs={{0,4},{4,8},{8,12},{12,0},{1,5},{5,9},{9,13},{13,1},{2,6},{6,10},{... | collective-permute-start | bytes 3145736 | tf_op jit(solution)/shard_map/ppermute | solution.py:29
  59.0 22.7 %collective-permute-start.13 = (f32[1024,128]{1,0:T(8,128)}, f32[1024,128]{1,0:T(8,128)}, u32[]{:S(2)}, u32[]{:S(2)}) collective-permute-start(f32[1024,128]{1,0:T(8,128)} %maximum_select_fusion.3), channel_id=1, source_target_pairs={{0,32},{32,0},{1,33},{33,1},{2,34},{34,2},{3,35},{35,3},{4,36},{36... | collective-permute-start | bytes 1572872 | tf_op jit(solution)/shard_map/ppermute | solution.py:33
  60.2 19.1 %collective-permute-start.14 = (f32[512,128]{1,0:T(8,128)}, f32[512,128]{1,0:T(8,128)}, u32[]{:S(2)}, u32[]{:S(2)}) collective-permute-start(f32[512,128]{1,0:T(8,128)} %maximum_select_fusion.5), channel_id=1, source_target_pairs={{0,32},{32,0},{1,33},{33,1},{2,34},{34,2},{3,35},{35,3},{4,36},{36... | collective-permute-start | bytes 786440 | tf_op jit(solution)/shard_map/ppermute | solution.py:33
  61.2 42.0 %collective-permute-start.22 = (f32[16,2048]{1,0:T(8,128)S(1)}, f32[16,2048]{1,0:T(8,128)}, u32[]{:S(2)}, u32[]{:S(2)}) collective-permute-start(f32[16,2048]{1,0:T(8,128)S(1)} %copy-done.13), channel_id=1, source_target_pairs={{0,1},{1,2},{2,3},{3,0},{4,5},{5,6},{6,7},{7,4},{8,9},{9,10},{10,1... | collective-permute-start | bytes 393224 | tf_op jit(solution)/shard_map/ppermute | solution.py:29
  65.2 34.2 %all-to-all-start.2 = ((f32[4,256,128]{2,1,0:T(8,128)}), f32[4,256,128]{2,1,0:T(8,128)}, u32[]{:S(2)}, u32[]{:S(2)}) async-start(f32[4,256,128]{2,1,0:T(8,128)} %dynamic-slice_bitcast_fusion.1), calls=%async_computation.2 | async-start | bytes 1048576 | tf_op jit(solution)/shard_map/all_to_all | solution.py:434
  79.3 15.4 %collective-permute-start.11 = (f32[512,128]{1,0:T(8,128)}, f32[512,128]{1,0:T(8,128)S(1)}, u32[]{:S(2)}, u32[]{:S(2)}) collective-permute-start(f32[512,128]{1,0:T(8,128)} %slice.83), channel_id=1, source_target_pairs={{0,4},{4,8},{8,12},{12,0},{1,5},{5,9},{9,13},{13,1},{2,6},{6,10},{... | collective-permute-start | bytes 786440 | tf_op jit(solution)/shard_map/ppermute | solution.py:29
  81.7 14.4 %collective-permute-start.12 = (f32[512,128]{1,0:T(8,128)}, f32[512,128]{1,0:T(8,128)S(1)}, u32[]{:S(2)}, u32[]{:S(2)}) collective-permute-start(f32[512,128]{1,0:T(8,128)} %slice.84), channel_id=1, source_target_pairs={{0,12},{4,0},{8,4},{12,8},{1,13},{5,1},{9,5},{13,9},{2,14},{6,2},{... | collective-permute-start | bytes 786440 | tf_op jit(solution)/shard_map/ppermute | solution.py:29
  95.5 7.8 %collective-permute-start.23 = (f32[16,2048]{1,0:T(8,128)S(1)}, f32[16,2048]{1,0:T(8,128)}, u32[]{:S(2)}, u32[]{:S(2)}) collective-permute-start(f32[16,2048]{1,0:T(8,128)S(1)} %copy-done.13), channel_id=1, source_target_pairs={{0,2},{1,3},{2,0},{3,1},{4,6},{5,7},{6,4},{7,5},{8,10},{9,11},{10,... | collective-permute-start | bytes 393224 | tf_op jit(solution)/shard_map/ppermute | solution.py:29
  96.8 9.7 %collective-permute-start.24 = (f32[16,2048]{1,0:T(8,128)S(1)}, f32[16,2048]{1,0:T(8,128)}, u32[]{:S(2)}, u32[]{:S(2)}) collective-permute-start(f32[16,2048]{1,0:T(8,128)S(1)} %copy-done.13), channel_id=1, source_target_pairs={{0,3},{1,0},{2,1},{3,2},{4,7},{5,4},{6,5},{7,6},{8,11},{9,8},{10,9... | collective-permute-start | bytes 393224 | tf_op jit(solution)/shard_map/ppermute | solution.py:29
  99.4 9.4 %collective-permute-start.20 = (f32[4,1024]{1,0:T(4,128)S(1)}, f32[4,1024]{1,0:T(4,128)S(1)}, u32[]{:S(2)}, u32[]{:S(2)}) collective-permute-start(f32[4,1024]{1,0:T(4,128)S(1)} %get-tuple-element.154), channel_id=1, source_target_pairs={{0,32},{32,0},{1,33},{33,1},{2,34},{34,2},{3,35},{35,3},{4,36},{36... | collective-permute-start | bytes 49160 | tf_op jit(solution)/shard_map/ppermute | solution.py:33
  100.1 6.4 %collective-permute-start.21 = (f32[4,512]{1,0:T(4,128)S(1)}, f32[4,512]{1,0:T(4,128)S(1)}, u32[]{:S(2)}, u32[]{:S(2)}) collective-permute-start(f32[4,512]{1,0:T(4,128)S(1)} %get-tuple-element.160), channel_id=1, source_target_pairs={{0,32},{32,0},{1,33},{33,1},{2,34},{34,2},{3,35},{35,3},{4,36},{36... | collective-permute-start | bytes 24584 | tf_op jit(solution)/shard_map/ppermute | solution.py:33
  103.2 19.0 %collective-permute-start.18 = (f32[2,512,128]{2,1,0:T(8,128)}, f32[2,512,128]{2,1,0:T(8,128)}, u32[]{:S(2)}, u32[]{:S(2)}) collective-permute-start(f32[2,512,128]{2,1,0:T(8,128)} %slice.91), channel_id=1, source_target_pairs={{0,4},{4,8},{8,12},{12,0},{1,5},{5,9},{9,13},{13,1},{2,6},{6,10},{... | collective-permute-start | bytes 1572872 | tf_op jit(solution)/shard_map/ppermute | solution.py:29
  103.2 19.0 %collective-permute-start.19 = (f32[2,512,128]{2,1,0:T(8,128)}, f32[2,512,128]{2,1,0:T(8,128)}, u32[]{:S(2)}, u32[]{:S(2)}) collective-permute-start(f32[2,512,128]{2,1,0:T(8,128)} %slice.92), channel_id=1, source_target_pairs={{0,12},{4,0},{8,4},{12,8},{1,13},{5,1},{9,5},{13,9},{2,14},{6,2},{... | collective-permute-start | bytes 1572872 | tf_op jit(solution)/shard_map/ppermute | solution.py:29
  106.5 23.8 %collective-permute-start.25 = (f32[1024,128]{1,0:T(8,128)}, f32[1024,128]{1,0:T(8,128)}, u32[]{:S(2)}, u32[]{:S(2)}) collective-permute-start(f32[1024,128]{1,0:T(8,128)} %bitcast.17.refs_0_), channel_id=1, source_target_pairs={{0,1},{1,2},{2,3},{3,0},{4,5},{5,6},{6,7},{7,4},{8,9},{9,10},{10,1... | collective-permute-start | bytes 1572872 | tf_op jit(solution)/shard_map/ppermute | solution.py:29
  106.5 23.8 %collective-permute-start.26 = (f32[1024,128]{1,0:T(8,128)}, f32[1024,128]{1,0:T(8,128)}, u32[]{:S(2)}, u32[]{:S(2)}) collective-permute-start(f32[1024,128]{1,0:T(8,128)} %bitcast.17.refs_0_), channel_id=1, source_target_pairs={{0,2},{1,3},{2,0},{3,1},{4,6},{5,7},{6,4},{7,5},{8,10},{9,11},{10,... | collective-permute-start | bytes 1572872 | tf_op jit(solution)/shard_map/ppermute | solution.py:29
  108.8 22.1 %collective-permute-start.27 = (f32[1024,128]{1,0:T(8,128)}, f32[1024,128]{1,0:T(8,128)}, u32[]{:S(2)}, u32[]{:S(2)}) collective-permute-start(f32[1024,128]{1,0:T(8,128)} %bitcast.17.refs_0_), channel_id=1, source_target_pairs={{0,3},{1,0},{2,1},{3,2},{4,7},{5,4},{6,5},{7,6},{8,11},{9,8},{10,9... | collective-permute-start | bytes 1572872 | tf_op jit(solution)/shard_map/ppermute | solution.py:29
  110.0 12.3 %all-to-all-start.3 = ((f32[4,256,128]{2,1,0:T(8,128)}), f32[4,256,128]{2,1,0:T(8,128)}, u32[]{:S(2)}, u32[]{:S(2)}) async-start(f32[4,256,128]{2,1,0:T(8,128)} %dynamic-slice_bitcast_fusion), calls=%async_computation.3 | async-start | bytes 1048576 | tf_op jit(solution)/shard_map/all_to_all | solution.py:434
  114.1 68.7 %all-gather.7.cloned.1.call-start = ((), (), s32[]{:S(2)}) async-start(), calls=%async_computation.5 | async-start | bytes 3932160 | tf_op jit(solution)/shard_map/all_gather | solution.py:437
  149.7 20.4 %collective-permute-start.35 = (f32[4,1536,128]{2,1,0:T(8,128)}, f32[4,1536,128]{2,1,0:T(8,128)S(1)}, u32[]{:S(2)}, u32[]{:S(2)}) collective-permute-start(f32[4,1536,128]{2,1,0:T(8,128)} %bitcast.40), channel_id=1, source_target_pairs={{0,16},{16,0},{1,17},{17,1},{2,18},{18,2},{3,19},{19,3},{4,20},{20... | collective-permute-start | bytes 9437192 | tf_op jit(solution)/shard_map/ppermute | solution.py:33
  149.7 6.6 %collective-permute-start.28 = (f32[16,1024]{1,0:T(8,128)}, f32[16,1024]{1,0:T(8,128)S(1)}, u32[]{:S(2)}, u32[]{:S(2)}) collective-permute-start(f32[16,1024]{1,0:T(8,128)} %copy-done.15), channel_id=1, source_target_pairs={{0,3},{1,0},{2,1},{3,2},{4,7},{5,4},{6,5},{7,6},{8,11},{9,8},{10,9... | collective-permute-start | bytes 196616 | tf_op jit(solution)/shard_map/ppermute | solution.py:29
  152.0 8.0 %collective-permute-start.29 = (f32[16,1024]{1,0:T(8,128)}, f32[16,1024]{1,0:T(8,128)S(1)}, u32[]{:S(2)}, u32[]{:S(2)}) collective-permute-start(f32[16,1024]{1,0:T(8,128)} %copy-done.14), channel_id=1, source_target_pairs={{0,2},{1,3},{2,0},{3,1},{4,6},{5,7},{6,4},{7,5},{8,10},{9,11},{10,... | collective-permute-start | bytes 196616 | tf_op jit(solution)/shard_map/ppermute | solution.py:29
  152.1 8.6 %collective-permute-start.30 = (f32[16,1024]{1,0:T(8,128)S(1)}, f32[16,1024]{1,0:T(8,128)S(1)}, u32[]{:S(2)}, u32[]{:S(2)}) collective-permute-start(f32[16,1024]{1,0:T(8,128)S(1)} %get-tuple-element.92), channel_id=1, source_target_pairs={{0,1},{1,2},{2,3},{3,0},{4,5},{5,6},{6,7},{7,4},{8,9},{9,10},{10,1... | collective-permute-start | bytes 196616 | tf_op jit(solution)/shard_map/ppermute | solution.py:29
  162.6 6.8 %collective-permute-start.32 = (f32[8,2048]{1,0:T(8,128)S(1)}, f32[8,2048]{1,0:T(8,128)S(1)}, u32[]{:S(2)}, u32[]{:S(2)}) collective-permute-start(f32[8,2048]{1,0:T(8,128)S(1)} %get-tuple-element.94.refs_0_), channel_id=1, source_target_pairs={{0,4},{4,8},{8,12},{12,0},{1,5},{5,9},{9,13},{13,1},{2,6},{6,10},{... | collective-permute-start | bytes 196616 | tf_op jit(solution)/shard_map/ppermute | solution.py:29
  162.7 6.8 %collective-permute-start.33 = (f32[8,2048]{1,0:T(8,128)S(1)}, f32[8,2048]{1,0:T(8,128)S(1)}, u32[]{:S(2)}, u32[]{:S(2)}) collective-permute-start(f32[8,2048]{1,0:T(8,128)S(1)} %get-tuple-element.94.refs_0_), channel_id=1, source_target_pairs={{0,8},{4,12},{8,0},{12,4},{1,9},{5,13},{9,1},{13,5},{2,10},{6,14},... | collective-permute-start | bytes 196616 | tf_op jit(solution)/shard_map/ppermute | solution.py:29
  165.9 12.5 %collective-permute-start.37 = (f32[2,4,2048]{2,1,0:T(4,128)S(1)}, f32[2,4,2048]{2,1,0:T(4,128)S(1)}, u32[]{:S(2)}, u32[]{:S(2)}) collective-permute-start(f32[2,4,2048]{2,1,0:T(4,128)S(1)} %get-tuple-element.103), channel_id=1, source_target_pairs={{0,32},{32,0},{1,33},{33,1},{2,34},{34,2},{3,35},{35,3},{4,36},{36... | collective-permute-start | bytes 196616 | tf_op jit(solution)/shard_map/ppermute | solution.py:33
  182.8 11.1 %collective-permute-start.41 = (f32[4,1536,128]{2,1,0:T(8,128)}, f32[4,1536,128]{2,1,0:T(8,128)S(1)}, u32[]{:S(2)}, u32[]{:S(2)}) collective-permute-start(f32[4,1536,128]{2,1,0:T(8,128)} %bitcast.43), channel_id=1, source_target_pairs={{0,16},{16,0},{1,17},{17,1},{2,18},{18,2},{3,19},{19,3},{4,20},{20... | collective-permute-start | bytes 9437192 | tf_op jit(solution)/shard_map/ppermute | solution.py:33
  182.9 9.2 %collective-permute-start.38 = (f32[16,2048]{1,0:T(8,128)S(1)}, f32[16,2048]{1,0:T(8,128)S(1)}, u32[]{:S(2)}, u32[]{:S(2)}) collective-permute-start(f32[16,2048]{1,0:T(8,128)S(1)} %get-tuple-element.104.refs_0_), channel_id=1, source_target_pairs={{0,4},{4,8},{8,12},{12,0},{1,5},{5,9},{9,13},{13,1},{2,6},{6,10},{... | collective-permute-start | bytes 393224 | tf_op jit(solution)/shard_map/ppermute | solution.py:29
  184.0 9.5 %collective-permute-start.39 = (f32[16,2048]{1,0:T(8,128)S(1)}, f32[16,2048]{1,0:T(8,128)S(1)}, u32[]{:S(2)}, u32[]{:S(2)}) collective-permute-start(f32[16,2048]{1,0:T(8,128)S(1)} %get-tuple-element.104.refs_0_), channel_id=1, source_target_pairs={{0,8},{4,12},{8,0},{12,4},{1,9},{5,13},{9,1},{13,5},{2,10},{6,14},... | collective-permute-start | bytes 393224 | tf_op jit(solution)/shard_map/ppermute | solution.py:29
  186.9 6.6 %collective-permute-start.40 = (f32[16,2048]{1,0:T(8,128)S(1)}, f32[16,2048]{1,0:T(8,128)S(1)}, u32[]{:S(2)}, u32[]{:S(2)}) collective-permute-start(f32[16,2048]{1,0:T(8,128)S(1)} %get-tuple-element.104.refs_0_), channel_id=1, source_target_pairs={{0,12},{4,0},{8,4},{12,8},{1,13},{5,1},{9,5},{13,9},{2,14},{6,2},{... | collective-permute-start | bytes 393224 | tf_op jit(solution)/shard_map/ppermute | solution.py:29
  192.1 17.7 %collective-permute-start.48 = (f32[1024,128]{1,0:T(8,128)}, f32[1024,128]{1,0:T(8,128)S(1)}, u32[]{:S(2)}, u32[]{:S(2)}) collective-permute-start(f32[1024,128]{1,0:T(8,128)} %bitcast.17.refs_0_), channel_id=1, source_target_pairs={{0,16},{16,0},{1,17},{17,1},{2,18},{18,2},{3,19},{19,3},{4,20},{20... | collective-permute-start | bytes 1572872 | tf_op jit(solution)/shard_map/ppermute | solution.py:33
  192.1 20.2 %collective-permute-start.49 = (f32[1024,128]{1,0:T(8,128)}, f32[1024,128]{1,0:T(8,128)S(1)}, u32[]{:S(2)}, u32[]{:S(2)}) collective-permute-start(f32[1024,128]{1,0:T(8,128)} %collective-permute-done.25.refs_1_), channel_id=1, source_target_pairs={{0,16},{16,0},{1,17},{17,1},{2,18},{18,2},{3,19},{19,3},{4,20},{20... | collective-permute-start | bytes 1572872 | tf_op jit(solution)/shard_map/ppermute | solution.py:33
  193.5 19.3 %collective-permute-start.50 = (f32[1024,128]{1,0:T(8,128)}, f32[1024,128]{1,0:T(8,128)S(1)}, u32[]{:S(2)}, u32[]{:S(2)}) collective-permute-start(f32[1024,128]{1,0:T(8,128)} %collective-permute-done.26.refs_2_), channel_id=1, source_target_pairs={{0,16},{16,0},{1,17},{17,1},{2,18},{18,2},{3,19},{19,3},{4,20},{20... | collective-permute-start | bytes 1572872 | tf_op jit(solution)/shard_map/ppermute | solution.py:33
  193.5 19.3 %collective-permute-start.51 = (f32[1024,128]{1,0:T(8,128)}, f32[1024,128]{1,0:T(8,128)S(1)}, u32[]{:S(2)}, u32[]{:S(2)}) collective-permute-start(f32[1024,128]{1,0:T(8,128)} %collective-permute-done.27.refs_3_), channel_id=1, source_target_pairs={{0,16},{16,0},{1,17},{17,1},{2,18},{18,2},{3,19},{19,3},{4,20},{20... | collective-permute-start | bytes 1572872 | tf_op jit(solution)/shard_map/ppermute | solution.py:33
  194.0 8.4 %collective-permute-start.44 = (f32[8,2048]{1,0:T(8,128)S(1)}, f32[8,2048]{1,0:T(8,128)S(1)}, u32[]{:S(2)}, u32[]{:S(2)}) collective-permute-start(f32[8,2048]{1,0:T(8,128)S(1)} %get-tuple-element.112), channel_id=1, source_target_pairs={{0,64},{64,0},{1,65},{65,1},{2,66},{66,2},{3,67},{67,3},{4,68},{68... | collective-permute-start | bytes 196616 | tf_op jit(solution)/shard_map/ppermute | solution.py:33
  208.6 5.5 %collective-permute-start.45 = (f32[8,2048]{1,0:T(8,128)S(1)}, f32[8,2048]{1,0:T(8,128)S(1)}, u32[]{:S(2)}, u32[]{:S(2)}) collective-permute-start(f32[8,2048]{1,0:T(8,128)S(1)} %s23.1.c0), channel_id=1, source_target_pairs={{0,4},{4,8},{8,12},{12,0},{1,5},{5,9},{9,13},{13,1},{2,6},{6,10},{... | collective-permute-start | bytes 196616 | tf_op jit(solution)/shard_map/ppermute | solution.py:29
  209.8 5.8 %collective-permute-start.46 = (f32[8,2048]{1,0:T(8,128)S(1)}, f32[8,2048]{1,0:T(8,128)S(1)}, u32[]{:S(2)}, u32[]{:S(2)}) collective-permute-start(f32[8,2048]{1,0:T(8,128)S(1)} %s23.1.c0), channel_id=1, source_target_pairs={{0,8},{4,12},{8,0},{12,4},{1,9},{5,13},{9,1},{13,5},{2,10},{6,14},... | collective-permute-start | bytes 196616 | tf_op jit(solution)/shard_map/ppermute | solution.py:29
  222.7 5.8 %collective-permute-start.53 = (f32[8,2048]{1,0:T(8,128)S(1)}, f32[8,2048]{1,0:T(8,128)S(1)}, u32[]{:S(2)}, u32[]{:S(2)}) collective-permute-start(f32[8,2048]{1,0:T(8,128)S(1)} %top.1.c0), channel_id=1, source_target_pairs={{0,8},{4,12},{8,0},{12,4},{1,9},{5,13},{9,1},{13,5},{2,10},{6,14},... | collective-permute-start | bytes 196616 | tf_op jit(solution)/shard_map/ppermute | solution.py:29
  240.9 10.0 %collective-permute-start.56 = (f32[16,2048]{1,0:T(8,128)S(1)}, f32[16,2048]{1,0:T(8,128)S(1)}, u32[]{:S(2)}, u32[]{:S(2)}) collective-permute-start(f32[16,2048]{1,0:T(8,128)S(1)} %b2.1.c0), channel_id=1, source_target_pairs={{0,4},{4,8},{8,12},{12,0},{1,5},{5,9},{9,13},{13,1},{2,6},{6,10},{... | collective-permute-start | bytes 393224 | tf_op jit(solution)/shard_map/ppermute | solution.py:29
  241.8 9.0 %collective-permute-start.57 = (f32[16,2048]{1,0:T(8,128)S(1)}, f32[16,2048]{1,0:T(8,128)S(1)}, u32[]{:S(2)}, u32[]{:S(2)}) collective-permute-start(f32[16,2048]{1,0:T(8,128)S(1)} %b2.1.c0), channel_id=1, source_target_pairs={{0,8},{4,12},{8,0},{12,4},{1,9},{5,13},{9,1},{13,5},{2,10},{6,14},... | collective-permute-start | bytes 393224 | tf_op jit(solution)/shard_map/ppermute | solution.py:29
  244.6 6.2 %collective-permute-start.58 = (f32[16,2048]{1,0:T(8,128)S(1)}, f32[16,2048]{1,0:T(8,128)S(1)}, u32[]{:S(2)}, u32[]{:S(2)}) collective-permute-start(f32[16,2048]{1,0:T(8,128)S(1)} %b2.1.c0), channel_id=1, source_target_pairs={{0,12},{4,0},{8,4},{12,8},{1,13},{5,1},{9,5},{13,9},{2,14},{6,2},{... | collective-permute-start | bytes 393224 | tf_op jit(solution)/shard_map/ppermute | solution.py:29
  245.1 5.8 %collective-permute-start.59 = (f32[8,2048]{1,0:T(8,128)S(1)}, f32[8,2048]{1,0:T(8,128)S(1)}, u32[]{:S(2)}, u32[]{:S(2)}) collective-permute-start(f32[8,2048]{1,0:T(8,128)S(1)} %get-tuple-element.117.x3), channel_id=1, source_target_pairs={{0,64},{64,0},{1,65},{65,1},{2,66},{66,2},{3,67},{67,3},{4,68},{68... | collective-permute-start | bytes 196616 | tf_op jit(solution)/shard_map/ppermute | solution.py:33
  251.9 12.8 %collective-permute-start.64 = (f32[2,4,2048]{2,1,0:T(4,128)S(1)}, f32[2,4,2048]{2,1,0:T(4,128)S(1)}, u32[]{:S(2)}, u32[]{:S(2)}) collective-permute-start(f32[2,4,2048]{2,1,0:T(4,128)S(1)} %slice.101.a_mine), channel_id=1, source_target_pairs={{0,32},{32,0},{1,33},{33,1},{2,34},{34,2},{3,35},{35,3},{4,36},{36... | collective-permute-start | bytes 196616 | tf_op jit(solution)/shard_map/ppermute | solution.py:33
  262.3 5.8 %collective-permute-start.62 = (f32[8,2048]{1,0:T(8,128)S(1)}, f32[8,2048]{1,0:T(8,128)S(1)}, u32[]{:S(2)}, u32[]{:S(2)}) collective-permute-start(f32[8,2048]{1,0:T(8,128)S(1)} %get-tuple-element.125), channel_id=1, source_target_pairs={{0,8},{4,12},{8,0},{12,4},{1,9},{5,13},{9,1},{13,5},{2,10},{6,14},... | collective-permute-start | bytes 196616 | tf_op jit(solution)/shard_map/ppermute | solution.py:29
  270.9 5.9 %collective-permute-start.74 = (f32[8,256]{1,0:T(8,128)S(1)}, f32[8,256]{1,0:T(8,128)S(1)}, u32[]{:S(2)}, u32[]{:S(2)}) collective-permute-start(f32[8,256]{1,0:T(8,128)S(1)} %get-tuple-element.144), channel_id=1, source_target_pairs={{0,16},{16,0},{1,17},{17,1},{2,18},{18,2},{3,19},{19,3},{4,20},{20... | collective-permute-start | bytes 24584 | tf_op jit(solution)/shard_map/ppermute | solution.py:33
  271.0 18.2 %collective-permute-start.73 = (f32[8,512]{1,0:T(8,128)S(1)}, f32[8,512]{1,0:T(8,128)S(1)}, u32[]{:S(2)}, u32[]{:S(2)}) collective-permute-start(f32[8,512]{1,0:T(8,128)S(1)} %get-tuple-element.146), channel_id=1, source_target_pairs={{0,16},{16,0},{1,17},{17,1},{2,18},{18,2},{3,19},{19,3},{4,20},{20... | collective-permute-start | bytes 49160 | tf_op jit(solution)/shard_map/ppermute | solution.py:33
  271.6 18.2 %collective-permute-start.72 = (f32[8,1024]{1,0:T(8,128)S(1)}, f32[8,1024]{1,0:T(8,128)S(1)}, u32[]{:S(2)}, u32[]{:S(2)}) collective-permute-start(f32[8,1024]{1,0:T(8,128)S(1)} %get-tuple-element.148), channel_id=1, source_target_pairs={{0,16},{16,0},{1,17},{17,1},{2,18},{18,2},{3,19},{19,3},{4,20},{20... | collective-permute-start | bytes 98312 | tf_op jit(solution)/shard_map/ppermute | solution.py:33
  272.7 5.6 %collective-permute-start.66 = (f32[16,1024]{1,0:T(8,128)S(1)}, f32[16,1024]{1,0:T(8,128)S(1)}, u32[]{:S(2)}, u32[]{:S(2)}) collective-permute-start(f32[16,1024]{1,0:T(8,128)S(1)} %maximum_select_fusion.8.refs_0_), channel_id=1, source_target_pairs={{0,1},{1,2},{2,3},{3,0},{4,5},{5,6},{6,7},{7,4},{8,9},{9,10},{10,1... | collective-permute-start | bytes 196616 | tf_op jit(solution)/shard_map/ppermute | solution.py:29
  273.3 6.9 %collective-permute-start.67 = (f32[16,1024]{1,0:T(8,128)S(1)}, f32[16,1024]{1,0:T(8,128)S(1)}, u32[]{:S(2)}, u32[]{:S(2)}) collective-permute-start(f32[16,1024]{1,0:T(8,128)S(1)} %maximum_select_fusion.8.refs_0_), channel_id=1, source_target_pairs={{0,2},{1,3},{2,0},{3,1},{4,6},{5,7},{6,4},{7,5},{8,10},{9,11},{10,... | collective-permute-start | bytes 196616 | tf_op jit(solution)/shard_map/ppermute | solution.py:29
  286.2 7.2 %collective-permute-start.69 = (f32[16,2048]{1,0:T(8,128)S(1)}, f32[16,2048]{1,0:T(8,128)S(1)}, u32[]{:S(2)}, u32[]{:S(2)}) collective-permute-start(f32[16,2048]{1,0:T(8,128)S(1)} %get-tuple-element.130), channel_id=1, source_target_pairs={{0,3},{1,0},{2,1},{3,2},{4,7},{5,4},{6,5},{7,6},{8,11},{9,8},{10,9... | collective-permute-start | bytes 393224 | tf_op jit(solution)/shard_map/ppermute | solution.py:29
  288.0 7.7 %collective-permute-start.70 = (f32[16,2048]{1,0:T(8,128)S(1)}, f32[16,2048]{1,0:T(8,128)S(1)}, u32[]{:S(2)}, u32[]{:S(2)}) collective-permute-start(f32[16,2048]{1,0:T(8,128)S(1)} %get-tuple-element.131), channel_id=1, source_target_pairs={{0,2},{1,3},{2,0},{3,1},{4,6},{5,7},{6,4},{7,5},{8,10},{9,11},{10,... | collective-permute-start | bytes 393224 | tf_op jit(solution)/shard_map/ppermute | solution.py:29
  288.4 8.3 %collective-permute-start.71 = (f32[16,2048]{1,0:T(8,128)S(1)}, f32[16,2048]{1,0:T(8,128)S(1)}, u32[]{:S(2)}, u32[]{:S(2)}) collective-permute-start(f32[16,2048]{1,0:T(8,128)S(1)} %get-tuple-element.132), channel_id=1, source_target_pairs={{0,1},{1,2},{2,3},{3,0},{4,5},{5,6},{6,7},{7,4},{8,9},{9,10},{10,1... | collective-permute-start | bytes 393224 | tf_op jit(solution)/shard_map/ppermute | solution.py:29
  (46 other events, 505.6 us)
Sparse Core Ops, SparseCore 0:
  55.0 38.3 all-gather.4
  133.1 40.2 all-gather.6

commit v4 on v3

--- a/solution.py
+++ b/solution.py
@@ -12,17 +12,27 @@
 f32 = jnp.float32
 bf16 = jnp.bfloat16
 
-ZI, YI, CI, X0, X1 = 0, 1, 2, 3, 4
-LIVE = 5
-TILES = 16
-
-
-def own_tiles(level):
-    return TILES + 16 * level
-
-
-def partner_tiles(level):
-    return TILES + 16 * level + 8
+FIRST = (0, 8, 12, 14)
+
+
+class Place:
+    def __init__(self, meta):
+        self.meta = meta
+        self.leaf = meta[0] >> 4
+        self.zi, self.yi = (meta[0] >> 2) & 3, meta[0] & 3
+        self.ci, self.x0, self.x1 = self.leaf & 1, (self.leaf >> 1) & 1, self.leaf >> 2
+
+    def live(self, level):
+        return self.meta[1 + FIRST[level] + (self.leaf >> level)]
+
+    def own(self, level):
+        return 16 + 8 * (FIRST[level] + (self.leaf >> level))
+
+    def partner(self, level):
+        return 16 + 8 * (FIRST[level] + ((self.leaf >> level) ^ 1))
+
+    def bit(self, level):
+        return (self.ci, self.x0, self.x1)[level]
 
 
 def shift(v, axis, s):
@@ -83,7 +93,7 @@
 
 
 def copies_first(meta, e, f, ev, fv, sems):
-    zi = meta[ZI]
+    zi = Place(meta).zi
     out_e, out_f = [], []
     spots = [zi, lax.rem(zi + 3, 4), lax.rem(zi + 1, 4)]
     far = lax.rem(zi + 2, 4)
@@ -111,14 +121,9 @@
     return out_e, out_f
 
 
-def copies_upper(meta, bufs, ev, fv, sems):
-    ci, yi = meta[CI], meta[YI]
-    sources = []
-    for i, q in ((0, ci), (1, 1 - ci)):
-        if len(bufs) == 2:
-            sources += [(bufs[i].at[w], q, w) for w in range(4)]
-        else:
-            sources += [(bufs[4 * i + d], q, lax.rem(yi + 4 - d, 4)) for d in range(4)]
+def copies_upper(level, meta, bufs, ev, fv, sems):
+    ci = Place(meta).ci
+    sources = [(bufs[i].at[w], q, w) for i, q in ((0, ci), (1, 1 - ci)) for w in range(4)]
     out_e, out_f = [], []
     k = 0
     for ref, q, w in sources:
@@ -131,24 +136,29 @@
             k += 1
     if fv is not None:
         for ref, q, w in sources:
-            rows = pl.ds(pl.multiple_of(q * 512, 512), 512)
-            cols = pl.ds(pl.multiple_of(w * B, B), B)
-            out_f.append(
-                pltpu.make_async_copy(ref.at[pl.ds(1024, 512)], fv.at[rows, cols], sems.at[k])
-            )
-            k += 1
+            for h in range(level):
+                n = 512 // level
+                rows = pl.ds(pl.multiple_of(h * 512 + q * n, n), n)
+                cols = pl.ds(pl.multiple_of(w * B, B), B)
+                out_f.append(
+                    pltpu.make_async_copy(
+                        ref.at[pl.ds(1024 + h * n, n)], fv.at[rows, cols], sems.at[k]
+                    )
+                )
+                k += 1
     return out_e, out_f
 
 
 def column_mask(meta, level, n):
     col = lax.broadcasted_iota(jnp.int32, (n, ORDER), 1)
-    return col < meta[LIVE + level] * B
+    return col < Place(meta).live(level) * B
 
 
 def row_mask(meta, level, n):
     own = lax.broadcasted_iota(jnp.int32, (n, 512), 1) // B
-    tile = 4 * own + meta[YI] if level == 0 else 4 * meta[ZI] + own
-    return tile < meta[LIVE + level]
+    place = Place(meta)
+    tile = 4 * own + place.yi if level == 0 else 4 * place.zi + own
+    return tile < Place(meta).live(level)
 
 
 def solve_rows(ev, cs, put):
@@ -160,7 +170,7 @@
     lax.fori_loop(0, 2, body, 0)
 
 
-WEIGHTS = (10, 2, 2, 8)
+WEIGHTS = (10, 2, 2, 2)
 
 
 def forward_kernel(level, n, mode, meta, *refs):
@@ -177,7 +187,7 @@
     if level == 0:
         ce, cf = copies_first(meta, w_refs[:5], w_refs[5:], ev, fv, sems)
     else:
-        ce, cf = copies_upper(meta, w_refs, ev, fv, sems)
+        ce, cf = copies_upper(level, meta, w_refs, ev, fv, sems)
     for c in ce + cf:
         c.start()
     r = n // 4
@@ -213,7 +223,7 @@
         for s in range(4):
             u_out[s][...] = uv[pl.ds(s * r, r), :]
     else:
-        split_rows(uv, r, meta[X0] if level == 1 else meta[X1], keep_out, give_out)
+        split_rows(uv, r, Place(meta).bit(level), keep_out, give_out)
 
 
 def split_rows(v, r, bit, keep_out, give_out):
@@ -252,36 +262,36 @@
 
 def s01_kernel(meta, keep, recv, b1, c1, pk, pg, acc):
     acc[...] = jnp.zeros_like(acc)
-    add_tiles(meta, own_tiles(0), keep, acc)
-    add_tiles(meta, partner_tiles(0), recv, acc)
+    add_tiles(meta, Place(meta).own(0), keep, acc)
+    add_tiles(meta, Place(meta).partner(0), recv, acc)
     c1[...] = b1[...] - acc[0]
     for i in (0, 1):
         low, high = acc[i + 1, 0:4, :], acc[i + 1, 4:8, :]
-        pk[i] = jnp.where(meta[X0] == 0, low, high)
-        pg[i] = jnp.where(meta[X0] == 0, high, low)
+        pk[i] = jnp.where(Place(meta).x0 == 0, low, high)
+        pg[i] = jnp.where(Place(meta).x0 == 0, high, low)
 
 
 def s12_kernel(meta, keep, recv, b2, pk, pr, part, keep3, give3, acc):
     acc[...] = jnp.zeros_like(acc)
-    add_tiles(meta, own_tiles(1), keep, acc)
-    add_tiles(meta, partner_tiles(1), recv, acc)
+    add_tiles(meta, Place(meta).own(1), keep, acc)
+    add_tiles(meta, Place(meta).partner(1), recv, acc)
     part[...] = -acc[0]
     part[0:4, :] = part[0:4, :] + (b2[...] - (pk[0] + pr[0]))
     acc[1, 0:4, :] = acc[1, 0:4, :] + (pk[1] + pr[1])
-    split_rows(acc.at[1], 4, meta[X1], keep3, give3)
+    split_rows(acc.at[1], 4, Place(meta).x1, keep3, give3)
 
 
 def s23_kernel(meta, keep, recv, b3, keep3, recv3, part, acc):
     acc[...] = jnp.zeros_like(acc)
-    add_tiles(meta, own_tiles(2), keep, acc)
-    add_tiles(meta, partner_tiles(2), recv, acc)
+    add_tiles(meta, Place(meta).own(2), keep, acc)
+    add_tiles(meta, Place(meta).partner(2), recv, acc)
     part[...] = -(acc[0] + (keep3[...] + recv3[...]))
     part[0:2, :] = part[0:2, :] + b3[...]
 
 
 def top_kernel(meta, c0, c1, c2, c3, *refs):
-    w_refs, (x_out, ev, yv, sems) = refs[:8], refs[8:]
-    ce, _ = copies_upper(meta, w_refs, ev, None, sems)
+    w_refs, (x_out, ev, yv, sems) = refs[:2], refs[2:]
+    ce, _ = copies_upper(3, meta, w_refs, ev, None, sems)
     for c in ce:
         c.start()
     c = summed((c0, c1, c2, c3), 2)
@@ -300,7 +310,7 @@
 
 def back(meta, level, n, ev, z, x_out):
     zs = stacked(z)
-    live = meta[LIVE + level] * B
+    live = Place(meta).live(level) * B
 
     def body(j, carry):
         cols = pl.ds(pl.multiple_of(j * 512, 512), 512)
@@ -319,7 +329,7 @@
     x = summed((c0, c1, c2, c3), 2)
     x_out[...] = x
     anc[0] = x
-    take_tiles(meta, partner_tiles(2), anc, give)
+    take_tiles(meta, Place(meta).partner(2), anc, give)
 
 
 def merged(a, b, h, bit):
@@ -332,19 +342,19 @@
 
 def x2_kernel(meta, c0, c1, c2, c3, x3, x3r, anc_out, give):
     anc_out[0] = summed((c0, c1, c2, c3), 4)
-    anc_out[1] = merged(x3[...], x3r[...], 2, meta[X1])
-    take_tiles(meta, partner_tiles(1), anc_out, give)
+    anc_out[1] = merged(x3[...], x3r[...], 2, Place(meta).x1)
+    take_tiles(meta, Place(meta).partner(1), anc_out, give)
 
 
 def x1_kernel(meta, c0, c1, c2, c3, a_mine, a_other, anc_out, give, own):
     anc_out[0] = (c0[...] + c1[...]) + (c2[...] + c3[...])
     for i in (0, 1):
         u, v = a_mine[i], a_other[i]
-        bit = meta[X0]
+        bit = Place(meta).x0
         anc_out[i + 1, 0:4, :] = jnp.where(bit == 0, u, v)
         anc_out[i + 1, 4:8, :] = jnp.where(bit == 0, v, u)
-    take_tiles(meta, partner_tiles(0), anc_out, give)
-    take_tiles(meta, own_tiles(0), anc_out, own)
+    take_tiles(meta, Place(meta).partner(0), anc_out, give)
+    take_tiles(meta, Place(meta).own(0), anc_out, own)
 
 
 def backward_kernel(level, n, meta, *refs):
@@ -359,7 +369,7 @@
     if level == 0:
         ce, cf = copies_first(meta, w_refs[:5], w_refs[5:], ev, fv, sems)
     else:
-        ce, cf = copies_upper(meta, w_refs, ev, fv, sems)
+        ce, cf = copies_upper(level, meta, w_refs, ev, fv, sems)
     for c in cf + ce:
         c.start()
     r = n // 4
@@ -368,8 +378,8 @@
             gv[pl.ds(s * r, r), :] = g_refs[s][...]
         g = gv[...]
     else:
-        take_tiles(meta, own_tiles(level), anc, ov)
-        bit = meta[X0] if level == 1 else meta[X1]
+        take_tiles(meta, Place(meta).own(level), anc, ov)
+        bit = Place(meta).bit(level)
         g = merged(ov[...], recv[...], r // 2, bit)
     gs = stacked(g)
     for c in cf:
@@ -387,8 +397,7 @@
 
 
 def call(kernel, name, shapes, scratch, meta, small, weights=(), flops=0):
-    if name != "f0":
-        weights = [pltpu.with_memory_space_constraint(w, pltpu.HBM) for w in weights]
+    weights = [pltpu.with_memory_space_constraint(w, pltpu.HBM) for w in weights]
     moved = sum(w.size * 4 for w in weights) + sum(v.size * 4 for v in small)
     return pl.pallas_call(
         kernel,
@@ -405,71 +414,56 @@
 def local(
     live_tiles, row_tiles, rhs0, rhs1, rhs2, rhs3, dinv0, dinv1, dinv2, dinv3, off0, off1, off2
 ):
-    zi, yi = lax.axis_index("z"), lax.axis_index("y")
     ci, x0, x1 = lax.axis_index("core"), lax.axis_index("x0"), lax.axis_index("x1")
     leaf = x1 * 4 + x0 * 2 + ci
-    first = [0, 8, 12, 14]
-    nodes = [first[k] + leaf // 2**k for k in range(4)]
-    partners = [first[k] + (leaf // 2**k ^ 1) for k in range(3)]
-    lives = [live_tiles[n] for n in nodes]
-    tables = []
-    for k in range(3):
-        tables += [row_tiles[nodes[k]], row_tiles[partners[k]]]
-    head = jnp.stack([zi, yi, ci, x0, x1, *lives] + [jnp.int32(0)] * 7).astype(jnp.int32)
-    meta = jnp.concatenate([head, *tables])
-
+    here = leaf * 16 + lax.axis_index("z") * 4 + lax.axis_index("y")
+    meta = jnp.concatenate([here.reshape(1), live_tiles, row_tiles.reshape(-1)])
     bits = [("core", ci), ("x0", x0), ("x1", x1)]
 
-    def joined(v, i):
+    def joined(v, i, dim=0):
         axis, bit = bits[i]
-        return None if v is None else ordered(v, flip(v, axis), bit, 0)
-
-    def half_block(e):
-        return lax.dynamic_index_in_dim(e.reshape(4, 2, 256, B), ci, 1, keepdims=False)
-
-    def half_rows(f):
-        return lax.dynamic_slice_in_dim(f, ci * 512, 512)
+        return ordered(v, flip(v, axis), bit, dim)
+
+    def swapped(pair, dim):
+        mine = lax.dynamic_index_in_dim(pair, ci, dim, keepdims=False)
+        give = lax.dynamic_index_in_dim(pair, 1 - ci, dim, keepdims=False)
+        return mine, flip(give, "core")
 
     def rows_to_z(e):
         return lax.all_to_all(e, "z", 0, 0, tiled=True).reshape(1024, B)
 
-    def gathered(e, f):
-        return lax.all_gather(jnp.concatenate([e, f], 0), "y", axis=0, tiled=False)
-
-    def spread(v, i):
-        axis, bit = bits[i]
-        keep, give = halves(v, bit)
-        return ordered(keep, flip(give, axis), bit, 1)
+    def gathered(e):
+        return lax.all_gather(e, "y", axis=0, tiled=False)
+
+    def spread(v, levels):
+        for axis, bit in bits[:levels]:
+            keep, give = halves(v, bit)
+            v = ordered(keep, flip(give, axis), bit, 1)
+        return v
 
     gate = lax.optimization_barrier
     e0 = jnp.swapaxes(dinv0.reshape(4, 4, B, B), 0, 1).reshape(4, 512, B)
+    e0, dinv1, off0 = gate((e0, dinv1, off0))
     e0 = lax.all_to_all(e0, "y", 0, 0, tiled=True)
     fa, fb = shift(off0, "z", 1), shift(off0, "z", -1)
-    e1 = rows_to_z(half_block(joined(dinv1, 0)))
-    f1 = half_rows(joined(off1, 0))
-    e2, f2 = joined(dinv2, 0), joined(off2, 0)
-    e3 = joined(joined(joined(dinv3, 2), 1), 0).reshape(2, 2, 2, 256, B)
-    e3 = half_block(e3.transpose(2, 1, 0, 3, 4))
-    e0, fa, fb, e1, f1, e2, f2, e3 = gate((e0, fa, fb, e1, f1, e2, f2, e3))
-    m1 = gathered(e1, f1)
+    e1 = ordered(*swapped(dinv1.reshape(2, 2, 256, B), 1), ci, 0)
+    e1, fa, fb = gate((e1, fa, fb))
+    e1 = rows_to_z(e1)
+    e0, fa, fb, e1, dinv2, off2, dinv3 = gate((e0, fa, fb, e1, dinv2, off2, dinv3))
+    m1 = gathered(jnp.concatenate([e1, off1], 0))
 
     ea, eb = shift(e0, "z", 1), shift(e0, "z", -1)
     fc, fd = shift(fa[:512], "z", 1), shift(fb[512:], "z", -1)
-    e2, f2 = half_block(joined(e2, 1)), half_rows(joined(f2, 1))
-    e3 = rows_to_z(e3)
-    b1, b2, b3 = spread(rhs1, 0), spread(rhs2, 0), spread(rhs3, 0)
-    ea, eb, fc, fd, e2, f2, e3, b1, b2, b3 = gate((ea, eb, fc, fd, e2, f2, e3, b1, b2, b3))
-
+    e2 = joined(ordered(*(v[None] for v in swapped(dinv2.reshape(2, 256, B), 0)), ci, 0), 1)
+    f2 = joined(off2, 1)
+    e3 = joined(joined(dinv3[None], 1), 2)
+    e2, e3 = rows_to_z(e2), rows_to_z(e3)
+    c0 = gather4(rhs0, "y")
+    ea, eb, fc, fd, e2, f2, e3, c0 = gate((ea, eb, fc, fd, e2, f2, e3, c0))
     ec, ed = shift(ea[:2], "z", 1), shift(eb[2:], "z", -1)
-    e2 = rows_to_z(e2)
-    w3 = gather4(e3, "y")
-    b2, b3 = spread(b2, 1), spread(b3, 1)
-    c0 = gather4(rhs0, "y")
-    ec, ed, e2, b2, b3, c0, w3 = gate((ec, ed, e2, b2, b3, c0, w3))
     w0 = [e0, ea, eb, ec, ed, off0, fa, fb, fc, fd]
-    m2 = gathered(e2, f2)
-    b3 = spread(b3, 2)
-    w3 = w3 + [flip(v, "core") for v in w3]
+    m2 = gathered(jnp.concatenate([e2, f2], 0))
+    m3 = gathered(e3)
 
     dma = pltpu.SemaphoreType.DMA
     ev, fv = pltpu.VMEM((512, ORDER), f32), pltpu.VMEM((1024, 512), f32)
@@ -484,7 +478,8 @@
         functools.partial(forward_kernel, 0, 64, "rs"), "f0", [(64, 512)] + [(16, 1024)] * 4,
         [ev, fv, *work(64), dma((24,))], meta, c0, w0, flops(64),
     )
-    m1, _ = gate((m1, y0))
+    m1, rhs1, rhs2, rhs3, _ = gate((m1, rhs1, rhs2, rhs3, y0))
+    b1, b2, b3 = spread(rhs1, 1), spread(rhs2, 2), spread(rhs3, 3)
     w1 = m1, flip(m1, "core")
     parts = scatter4(u, "y")
     u = (parts[0] + parts[1]) + (parts[2] + parts[3])
@@ -496,7 +491,7 @@
     pr = flip(pg, "x0")
     y1, keep, give = call(
         functools.partial(forward_kernel, 1, 32, "ar"), "f1", [(32, 512), (16, 1024), (16, 1024)],
-        [ev, fv, *work(32), dma((40,))], meta, gather4(c1, "z"), w1, flops(32),
+        [ev, fv, *work(32), dma((48,))], meta, gather4(c1, "z"), w1, flops(32),
     )
     part, keep3, give3 = call(
         s12_kernel, "s12", [(16, ORDER), (8, ORDER), (8, ORDER)],
@@ -507,13 +502,15 @@
     recv3 = flip(give3, "x1")
     y2, keep, give = call(
         functools.partial(forward_kernel, 2, 16, "ar"), "f2", [(16, 512), (8, 1024), (8, 1024)],
-        [ev, fv, *work(16), dma((40,))], meta, gather4(part, "z"), w2, flops(16),
+        [ev, fv, *work(16), dma((48,))], meta, gather4(part, "z"), w2, flops(16),
     )
     (part,) = call(
         s23_kernel, "s23", [(8, ORDER)],
         [pltpu.VMEM((1, 8, ORDER), f32)], meta, [keep, flip(give, "x1"), b3, keep3, recv3],
     )
 
+    m3, _ = gate((m3, part))
+    w3 = m3, flip(m3, "core")
     (part,) = call(
         top_kernel, "top", [(8, ORDER)], [ev, pltpu.VMEM((8, 512), f32), dma((32,))],
         meta, gather4(part, "z"), w3, flops(8),
@@ -526,7 +523,7 @@
     x3r = flip(x3, "x1")
 
     def rest(n, small):
-        return [ev, fv, pltpu.VMEM((n, 1024), f32), pltpu.VMEM((n // 2, 1024), f32), dma((40,))]
+        return [ev, fv, pltpu.VMEM((n, 1024), f32), pltpu.VMEM((n // 2, 1024), f32), dma((48,))]
 
     (part,) = call(
         functools.partial(backward_kernel, 2, 16), "b2", [(16, ORDER)], rest(16, 0),

time: 306 us -> 287 us (0.938)
  other arithmetic: 21.5 us -> 6.46 us
  local copies, waits for them, and re-layouts: 23.9 us -> 11.4 us
  blocking collectives: 0 us -> 12.4 us
  waiting for transfers between devices: 103 us -> 99.8 us
    select_n x19 -> x16, other arithmetic: 16.2 us -> 3.68 us  [ordered(): jnp.where(bit == 0, jnp.concatenate([mine, other], dim), jnp.concatenate(...]
    all_to_all x0 -> x1, blocking collectives: none -> 12.4 us  [rows_to_z(): return lax.all_to_all(e, 'z', 0, 0, tiled=True).reshape(1024, B)]
    ppermute x41 -> x38, waiting for transfers between devices: 51 us -> 58.5 us  [shift(): return lax.ppermute(v, axis, [(i, (i + s) % 4) for i in range(4)])]
    unnamed x58 -> x37, local copies, waits for them, and re-layouts: 10.2 us -> 4.74 us
    ppermute x41 -> x38, starting transfers between devices: 53.9 us -> 58.8 us  [shift(): return lax.ppermute(v, axis, [(i, (i + s) % 4) for i in range(4)])]
    ppermute x34 -> x28, waiting for transfers between devices: 35.7 us -> 31.4 us  [flip(): return lax.ppermute(v, axis, [(0, 1), (1, 0)])]
    all_to_all x3 -> x2, starting transfers between devices: 13.6 us -> 9.86 us  [rows_to_z(): return lax.all_to_all(e, 'z', 0, 0, tiled=True).reshape(1024, B)]
    all_to_all x3 -> x2, waiting for transfers between devices: 13.2 us -> 9.79 us  [rows_to_z(): return lax.all_to_all(e, 'z', 0, 0, tiled=True).reshape(1024, B)]
  transfers between devices with their start and end apart: 81 -> 72, of which waited for: 38 -> 42; matrix products, arithmetic and copies ran while one was open for 11% -> 3% of each run, Pallas kernels for 10% -> 11%
where the time goes in v4:
time: 287 us; the launch traced here: 286 us
  waiting for transfers between devices  99.8 us (35%)
  starting transfers between devices  99 us (34%)
  Pallas kernels  42.8 us (15%)
  between operations  14.3 us (5%)
  blocking collectives  12.4 us (4%)
  local copies, waits for them, and re-layouts  11.4 us (4%)
  other arithmetic  6.46 us (2%)
    ppermute x38, starting transfers between devices, shift(): return lax.ppermute(v, axis, [(i, (i + s) % 4) for i in range(4)])  58.8 us
    ppermute x38, waiting for transfers between devices, shift(): return lax.ppermute(v, axis, [(i, (i + s) % 4) for i in range(4)])  58.5 us
    pallas_call x13, Pallas kernels, call(): pl.pallas_call(kernel, out_shape=[jax.ShapeDtypeStruct(s, f32) for s in s...  42.8 us
    ppermute x28, waiting for transfers between devices, flip(): return lax.ppermute(v, axis, [(0, 1), (1, 0)])  31.4 us
    ppermute x28, starting transfers between devices, flip(): return lax.ppermute(v, axis, [(0, 1), (1, 0)])  25.5 us
    all_to_all x1, blocking collectives, rows_to_z(): return lax.all_to_all(e, 'z', 0, 0, tiled=True).reshape(1024, B)  12.4 us
    all_to_all x2, starting transfers between devices, rows_to_z(): return lax.all_to_all(e, 'z', 0, 0, tiled=True).reshape(1024, B)  9.86 us
    all_to_all x2, waiting for transfers between devices, rows_to_z(): return lax.all_to_all(e, 'z', 0, 0, tiled=True).reshape(1024, B)  9.79 us
  transfers between devices with their start and end apart: 72, of which 42 were waited for; matrix products, arithmetic and copies ran while one was open for 3% of the time, Pallas kernels for 11%

profile of v4, /device:TPU:0, one launch (start us, length us, event | category | flops | bytes accessed | tf_op | source)
XLA Modules:
  0.0 286.0 jit_solution(16297556829450722278)
XLA Ops:
  7.2 2.4 copy.20
  9.5 4.7 %all-to-all-start = ((f32[4,512,128]{2,1,0:T(8,128)}), f32[4,512,128]{2,1,0:T(8,128)S(1)}, u32[]{:S(2)}, u32[]{:S(2)}) async-start(f32[4,512,128]{2,1,0:T(8,128)} %bitcast.3), calls=%async_computation | async-start | bytes 2097152 | tf_op jit(solution)/shard_map/all_to_all | solution.py:447
  14.3 2.0 collective-permute-start.1
  16.2 2.2 collective-permute-start.2
  18.6 1.5 collective-permute-done
  20.2 10.2 %collective-permute-done.1.refs_10_.refs_11_ = f32[1024,128]{1,0:T(8,128)} collective-permute-done((f32[1024,128]{1,0:T(8,128)}, f32[1024,128]{1,0:T(8,128)}, u32[]{:S(2)}, u32[]{:S(2)}) %collective-permute-start.1) | collective-permute-done | bytes 524320 | tf_op jit(solution)/shard_map/ppermute | solution.py:39
  30.3 12.4 %all_to_all.20 = f32[4,256,128]{2,1,0:T(8,128)S(1)} all-to-all(f32[4,256,128]{2,1,0:T(8,128)S(1)} %maximum_select_fusion), channel_id=1, replica_groups=mesh['x1'=2,'x0'=2,'core'=2,'z'=4,'y'=4] {'z'}, dimensions={0} | all-to-all | bytes 1048576 | tf_op jit(solution)/shard_map/all_to_all | solution.py:433
  43.8 1.6 collective-permute-start.10
  45.3 3.5 %collective-permute-done.10 = f32[1,256,128]{2,1,0:T(8,128)S(1)} collective-permute-done((f32[1,256,128]{2,1,0:T(8,128)S(1)}, f32[1,256,128]{2,1,0:T(8,128)S(1)}, u32[]{:S(2)}, u32[]{:S(2)}) %collective-permute-start.10) | collective-permute-done | bytes 131104 | tf_op jit(solution)/shard_map/ppermute | solution.py:43
  48.8 3.9 %collective-permute-start.11 = (f32[2,256,128]{2,1,0:T(8,128)S(1)}, f32[2,256,128]{2,1,0:T(8,128)S(1)}, u32[]{:S(2)}, u32[]{:S(2)}) collective-permute-start(f32[2,256,128]{2,1,0:T(8,128)S(1)} %maximum_select_fusion.5), channel_id=1, source_target_pairs={{0,64},{64,0},{1,65},{65,1},{2,66},{66,2},{3,67},{67,3},{4,68},{68... | collective-permute-start | bytes 786440 | tf_op jit(solution)/shard_map/ppermute | solution.py:43
  53.3 2.7 collective-permute-start.4
  57.9 3.5 %all-to-all-start.3 = ((f32[4,256,128]{2,1,0:T(8,128)}), f32[4,256,128]{2,1,0:T(8,128)S(1)}, u32[]{:S(2)}, u32[]{:S(2)}) async-start(f32[4,256,128]{2,1,0:T(8,128)} %maximum_select_fusion.2), calls=%async_computation.3 | async-start | bytes 1048576 | tf_op jit(solution)/shard_map/all_to_all | solution.py:433
  62.7 1.5 collective-permute-start.12
  64.2 2.7 collective-permute-start.13
  66.9 2.3 collective-permute-done.8
  70.1 9.8 %all-to-all-done.3 = f32[4,256,128]{2,1,0:T(8,128)S(1)} async-done(((f32[4,256,128]{2,1,0:T(8,128)}), f32[4,256,128]{2,1,0:T(8,128)S(1)}, u32[]{:S(2)}, u32[]{:S(2)}) %all-to-all-start.3) | async-done | bytes 524320 | tf_op jit(solution)/shard_map/all_to_all | solution.py:433
  79.8 6.4 %all-to-all-start.2 = ((f32[4,256,128]{2,1,0:T(8,128)}), f32[4,256,128]{2,1,0:T(8,128)S(1)}, u32[]{:S(2)}, u32[]{:S(2)}) async-start(f32[4,256,128]{2,1,0:T(8,128)} %maximum_select_fusion.1), calls=%async_computation.2 | async-start | bytes 1048576 | tf_op jit(solution)/shard_map/all_to_all | solution.py:433
  89.0 2.0 collective-permute-start.5
  92.4 2.4 collective-permute-start.14
  94.8 2.5 collective-permute-done.14.refs_3_
  97.3 2.7 collective-permute-done.5.refs_12_.refs_13_
  105.0 2.3 collective-permute-start.16
  107.6 5.7 %collective-permute-done.15.refs_7_.refs_8_ = f32[2,512,128]{2,1,0:T(8,128)S(1)} collective-permute-done((f32[2,512,128]{2,1,0:T(8,128)S(1)}, f32[2,512,128]{2,1,0:T(8,128)S(1)}, u32[]{:S(2)}, u32[]{:S(2)}) %collective-permute-start.15) | collective-permute-done | bytes 524320 | tf_op jit(solution)/shard_map/ppermute | solution.py:39
  115.0 5.9 %f0.1 = (f32[64,512]{1,0:T(8,128)S(1)}, f32[16,1024]{1,0:T(8,128)S(1)}, f32[16,1024]{1,0:T(8,128)S(1)}, f32[16,1024]{1,0:T(8,128)S(1)}, f32[16,1024]{1,0:T(8,128)S(1)}) custom-call(s32[128]{0:T(128)S(1)} %pad_add_fusion.meta, f32[16,2048]{1,0:T(8,128)S(1)} %copy-done, f32[16,2048]{1,0:T(8,128)S(1)} %collective-permute-done.12.refs_1_, ...), custom_call_target="tpu_custom_call" | custom-call | flops 2415919104 | bytes 6815744 | tf_op jit(solution)/shard_map/f0/pallas_call | solution.py:402
  121.1 2.6 collective-permute-start.17
  125.6 2.1 collective-permute-done.17
  127.8 3.7 %collective-permute-done.18 = f32[16,1024]{1,0:T(8,128)S(1)} collective-permute-done((f32[16,1024]{1,0:T(8,128)S(1)}, f32[16,1024]{1,0:T(8,128)S(1)}, u32[]{:S(2)}, u32[]{:S(2)}) %collective-permute-start.18) | collective-permute-done | bytes 65568 | tf_op jit(solution)/shard_map/ppermute | solution.py:39
  136.8 3.7 %collective-permute-start.23 = (f32[8,2048]{1,0:T(8,128)S(1)}, f32[8,2048]{1,0:T(8,128)S(1)}, u32[]{:S(2)}, u32[]{:S(2)}) collective-permute-start(f32[8,2048]{1,0:T(8,128)S(1)} %get-tuple-element.93.refs_0_), channel_id=1, source_target_pairs={{0,8},{4,12},{8,0},{12,4},{1,9},{5,13},{9,1},{13,5},{2,10},{6,14},... | collective-permute-start | bytes 196616 | tf_op jit(solution)/shard_map/ppermute | solution.py:39
  140.8 1.4 collective-permute-start.28
  144.7 1.8 copy-done.1
  146.5 6.0 %f1.1 = (f32[32,512]{1,0:T(8,128)S(1)}, f32[16,1024]{1,0:T(8,128)S(1)}, f32[16,1024]{1,0:T(8,128)S(1)}) custom-call(s32[128]{0:T(128)S(1)} %pad_add_fusion.meta, f32[8,2048]{1,0:T(8,128)S(1)} %get-tuple-element.93.refs_0_, f32[8,2048]{1,0:T(8,128)S(1)} %collective-permute-done.22.refs_1_, f32[8,2048]{1,0:T(8,128)S(1)} %collective-permute-done.23.refs_2_, ...), custom_call_target="tpu_custom_call" | custom-call | flops 1207959552 | bytes 6553600 | tf_op jit(solution)/shard_map/f1/pallas_call | solution.py:402
  153.5 3.3 %collective-permute-done.26.recv = f32[16,1024]{1,0:T(8,128)S(1)} collective-permute-done((f32[16,1024]{1,0:T(8,128)S(1)}, f32[16,1024]{1,0:T(8,128)S(1)}, u32[]{:S(2)}, u32[]{:S(2)}) %collective-permute-start.26) | collective-permute-done | bytes 65568 | tf_op jit(solution)/shard_map/ppermute | solution.py:43
  158.3 4.7 %collective-permute-done.35 = f32[8,256]{1,0:T(8,128)S(1)} collective-permute-done((f32[8,256]{1,0:T(8,128)S(1)}, f32[8,256]{1,0:T(8,128)S(1)}, u32[]{:S(2)}, u32[]{:S(2)}) %collective-permute-start.35) | collective-permute-done | bytes 8224 | tf_op jit(solution)/shard_map/ppermute | solution.py:43
  164.0 2.8 collective-permute-done.36
  166.9 2.8 collective-permute-start.31
  171.0 4.4 %collective-permute-done.30.refs_1_ = f32[16,2048]{1,0:T(8,128)S(1)} collective-permute-done((f32[16,2048]{1,0:T(8,128)S(1)}, f32[16,2048]{1,0:T(8,128)S(1)}, u32[]{:S(2)}, u32[]{:S(2)}) %collective-permute-start.30) | collective-permute-done | bytes 131104 | tf_op jit(solution)/shard_map/ppermute | solution.py:39
  175.9 5.8 %f2.1 = (f32[16,512]{1,0:T(8,128)S(1)}, f32[8,1024]{1,0:T(8,128)S(1)}, f32[8,1024]{1,0:T(8,128)S(1)}) custom-call(s32[128]{0:T(128)S(1)} %pad_add_fusion.meta, f32[16,2048]{1,0:T(8,128)S(1)} %get-tuple-element.100.refs_0_, f32[16,2048]{1,0:T(8,128)S(1)} %collective-permute-done.30.refs_1_, f32[16,2048]{1,0:T(8,128)S(1)} %collective-permute-done.31.refs_2_, ...), custom_call_target="tpu_custom_call" | custom-call | flops 603979776 | bytes 6815744 | tf_op jit(solution)/shard_map/f2/pallas_call | solution.py:402
  181.8 3.0 %collective-permute-start.34 = (f32[8,1024]{1,0:T(8,128)S(1)}, f32[8,1024]{1,0:T(8,128)S(1)}, u32[]{:S(2)}, u32[]{:S(2)}) collective-permute-start(f32[8,1024]{1,0:T(8,128)S(1)} %get-tuple-element.105), channel_id=1, source_target_pairs={{0,64},{64,0},{1,65},{65,1},{2,66},{66,2},{3,67},{67,3},{4,68},{68... | collective-permute-start | bytes 98312 | tf_op jit(solution)/shard_map/ppermute | solution.py:43
  184.8 2.4 collective-permute-done.34.recv
  189.0 3.2 %collective-permute-start.40 = (f32[8,2048]{1,0:T(8,128)S(1)}, f32[8,2048]{1,0:T(8,128)S(1)}, u32[]{:S(2)}, u32[]{:S(2)}) collective-permute-start(f32[8,2048]{1,0:T(8,128)S(1)} %s23.1.c0), channel_id=1, source_target_pairs={{0,8},{4,12},{8,0},{12,4},{1,9},{5,13},{9,1},{13,5},{2,10},{6,14},... | collective-permute-start | bytes 196616 | tf_op jit(solution)/shard_map/ppermute | solution.py:39
  192.2 1.5 collective-permute-done.39.c1
  193.8 2.3 collective-permute-done.40.c2
  196.5 1.3 copy-done.2
  197.8 5.6 %top.1.c0 = f32[8,2048]{1,0:T(8,128)S(1)} custom-call(s32[128]{0:T(128)S(1)} %pad_add_fusion.meta, f32[8,2048]{1,0:T(8,128)S(1)} %s23.1.c0, f32[8,2048]{1,0:T(8,128)S(1)} %collective-permute-done.39.c1, f32[8,2048]{1,0:T(8,128)S(1)} %collective-permute-done.40.c2, f32[8,2048]{1,0:T(8,128)S(1)} %collective-permute-done.41.c3, f32[4,1024,128]{2,1,0:T(8,128)} %bitcast.42, ...), custom_call_target="tpu_custom_call" | custom-call | flops 301989888 | bytes 4456448 | tf_op jit(solution)/shard_map/top/pallas_call | solution.py:402
  203.7 3.1 %collective-permute-start.44 = (f32[8,2048]{1,0:T(8,128)S(1)}, f32[8,2048]{1,0:T(8,128)S(1)}, u32[]{:S(2)}, u32[]{:S(2)}) collective-permute-start(f32[8,2048]{1,0:T(8,128)S(1)} %top.1.c0), channel_id=1, source_target_pairs={{0,8},{4,12},{8,0},{12,4},{1,9},{5,13},{9,1},{13,5},{2,10},{6,14},... | collective-permute-start | bytes 196616 | tf_op jit(solution)/shard_map/ppermute | solution.py:39
  207.6 1.9 collective-permute-done.43.c1
  211.8 2.8 collective-permute-start.46
  214.5 2.7 collective-permute-done.46.refs_1_
  217.3 5.1 %b2.1.c0 = f32[16,2048]{1,0:T(8,128)S(1)} custom-call(s32[128]{0:T(128)S(1)} %pad_add_fusion.meta, f32[1,8,2048]{2,1,0:T(8,128)S(1)} %bitcast.34, f32[8,1024]{1,0:T(8,128)S(1)} %collective-permute-done.46.refs_1_, f32[16,512]{1,0:T(8,128)S(1)} %get-tuple-element.113.refs_2_, f32[4,1536,128]{2,1,0:T(8,128)} %bitcast.40, ...), custom_call_target="tpu_custom_call" | custom-call | flops 603979776 | bytes 6422528 | tf_op jit(solution)/shard_map/b2/pallas_call | solution.py:402
  223.2 3.1 %collective-permute-start.48 = (f32[16,2048]{1,0:T(8,128)S(1)}, f32[16,2048]{1,0:T(8,128)S(1)}, u32[]{:S(2)}, u32[]{:S(2)}) collective-permute-start(f32[16,2048]{1,0:T(8,128)S(1)} %b2.1.c0), channel_id=1, source_target_pairs={{0,8},{4,12},{8,0},{12,4},{1,9},{5,13},{9,1},{13,5},{2,10},{6,14},... | collective-permute-start | bytes 393224 | tf_op jit(solution)/shard_map/ppermute | solution.py:39
  226.6 2.7 collective-permute-start.50
  229.3 3.1 %collective-permute-done.50.x3r = f32[8,2048]{1,0:T(8,128)S(1)} collective-permute-done((f32[8,2048]{1,0:T(8,128)S(1)}, f32[8,2048]{1,0:T(8,128)S(1)}, u32[]{:S(2)}, u32[]{:S(2)}) %collective-permute-start.50) | collective-permute-done | bytes 65568 | tf_op jit(solution)/shard_map/ppermute | solution.py:43
  235.5 2.1 collective-permute-done.51.refs_1_
  237.6 5.2 %b1.1 = (f32[8,2048]{1,0:T(8,128)S(1)}, f32[8,2048]{1,0:T(8,128)S(1)}, f32[8,2048]{1,0:T(8,128)S(1)}, f32[8,2048]{1,0:T(8,128)S(1)}) custom-call(s32[128]{0:T(128)S(1)} %pad_add_fusion.meta, f32[2,16,2048]{2,1,0:T(8,128)S(1)} %get-tuple-element.114.refs_0_, f32[16,1024]{1,0:T(8,128)S(1)} %collective-permute-done.51.refs_1_, ...), custom_call_target="tpu_custom_call" | custom-call | flops 1207959552 | bytes 6684672 | tf_op jit(solution)/shard_map/b1/pallas_call | solution.py:402
  244.1 2.9 %collective-permute-start.53 = (f32[8,2048]{1,0:T(8,128)S(1)}, f32[8,2048]{1,0:T(8,128)S(1)}, u32[]{:S(2)}, u32[]{:S(2)}) collective-permute-start(f32[8,2048]{1,0:T(8,128)S(1)} %get-tuple-element.119), channel_id=1, source_target_pairs={{0,8},{4,12},{8,0},{12,4},{1,9},{5,13},{9,1},{13,5},{2,10},{6,14},... | collective-permute-start | bytes 196616 | tf_op jit(solution)/shard_map/ppermute | solution.py:39
  247.2 2.7 collective-permute-done.53.c2
  249.9 2.6 collective-permute-done.54.c3
  256.0 2.4 collective-permute-start.58
  259.6 1.4 collective-permute-done.57.refs_1_
  262.7 5.2 %b0.1 = (f32[16,2048]{1,0:T(8,128)S(1)}, f32[16,2048]{1,0:T(8,128)S(1)}, f32[16,2048]{1,0:T(8,128)S(1)}, f32[16,2048]{1,0:T(8,128)S(1)}) custom-call(s32[128]{0:T(128)S(1)} %pad_add_fusion.meta, f32[16,1024]{1,0:T(8,128)S(1)} %maximum_select_fusion.7.refs_0_, f32[16,1024]{1,0:T(8,128)S(1)} %collective-permute-done.57.refs_1_, ...), custom_call_target="tpu_custom_call" | custom-call | flops 2415919104 | bytes 6684672 | tf_op jit(solution)/shard_map/b0/pallas_call | solution.py:402
  268.0 2.3 collective-permute-start.60
  272.5 2.6 collective-permute-done.60
  275.1 2.3 collective-permute-done.61
  277.5 1.3 collective-permute-done.62
  (175 shorter events, 53.0 us)
Async XLA Ops:
  9.5 20.8 %all-to-all-start = ((f32[4,512,128]{2,1,0:T(8,128)}), f32[4,512,128]{2,1,0:T(8,128)S(1)}, u32[]{:S(2)}, u32[]{:S(2)}) async-start(f32[4,512,128]{2,1,0:T(8,128)} %bitcast.3), calls=%async_computation | async-start | bytes 2097152 | tf_op jit(solution)/shard_map/all_to_all | solution.py:447
  14.2 106.7 %all-gather.7.cloned.1.call-start = ((), (), s32[]{:S(2)}) async-start(), calls=%async_computation.4 | async-start | bytes 3932160 | tf_op jit(solution)/shard_map/all_gather | solution.py:436
  14.3 16.1 %collective-permute-start.1 = (f32[1024,128]{1,0:T(8,128)}, f32[1024,128]{1,0:T(8,128)}, u32[]{:S(2)}, u32[]{:S(2)}) collective-permute-start(f32[1024,128]{1,0:T(8,128)} %refs_10_), channel_id=1, source_target_pairs={{0,4},{4,8},{8,12},{12,0},{1,5},{5,9},{9,13},{13,1},{2,6},{6,10},{... | collective-permute-start | bytes 1572872 | tf_op jit(solution)/shard_map/ppermute | solution.py:39
  16.2 14.1 %collective-permute-start.2 = (f32[1024,128]{1,0:T(8,128)}, f32[1024,128]{1,0:T(8,128)}, u32[]{:S(2)}, u32[]{:S(2)}) collective-permute-start(f32[1024,128]{1,0:T(8,128)} %refs_10_), channel_id=1, source_target_pairs={{0,12},{4,0},{8,4},{12,8},{1,13},{5,1},{9,5},{13,9},{2,14},{6,2},{... | collective-permute-start | bytes 1572872 | tf_op jit(solution)/shard_map/ppermute | solution.py:39
  43.8 5.0 %collective-permute-start.10 = (f32[1,256,128]{2,1,0:T(8,128)S(1)}, f32[1,256,128]{2,1,0:T(8,128)S(1)}, u32[]{:S(2)}, u32[]{:S(2)}) collective-permute-start(f32[1,256,128]{2,1,0:T(8,128)S(1)} %bitcast.49), channel_id=1, source_target_pairs={{0,32},{32,0},{1,33},{33,1},{2,34},{34,2},{3,35},{35,3},{4,36},{36... | collective-permute-start | bytes 393224 | tf_op jit(solution)/shard_map/ppermute | solution.py:43
  48.8 8.2 %collective-permute-start.11 = (f32[2,256,128]{2,1,0:T(8,128)S(1)}, f32[2,256,128]{2,1,0:T(8,128)S(1)}, u32[]{:S(2)}, u32[]{:S(2)}) collective-permute-start(f32[2,256,128]{2,1,0:T(8,128)S(1)} %maximum_select_fusion.5), channel_id=1, source_target_pairs={{0,64},{64,0},{1,65},{65,1},{2,66},{66,2},{3,67},{67,3},{4,68},{68... | collective-permute-start | bytes 786440 | tf_op jit(solution)/shard_map/ppermute | solution.py:43
  52.7 48.0 %collective-permute-start.3 = (f32[4,512,128]{2,1,0:T(8,128)S(1)}, f32[4,512,128]{2,1,0:T(8,128)}, u32[]{:S(2)}, u32[]{:S(2)}) collective-permute-start(f32[4,512,128]{2,1,0:T(8,128)S(1)} %all-to-all-done.refs_4_.refs_5_), channel_id=1, source_target_pairs={{0,4},{4,8},{8,12},{12,0},{1,5},{5,9},{9,13},{13,1},{2,6},{6,10},{... | collective-permute-start | bytes 3145736 | tf_op jit(solution)/shard_map/ppermute | solution.py:39
  53.3 47.5 %collective-permute-start.4 = (f32[4,512,128]{2,1,0:T(8,128)S(1)}, f32[4,512,128]{2,1,0:T(8,128)}, u32[]{:S(2)}, u32[]{:S(2)}) collective-permute-start(f32[4,512,128]{2,1,0:T(8,128)S(1)} %all-to-all-done.refs_4_.refs_5_), channel_id=1, source_target_pairs={{0,12},{4,0},{8,4},{12,8},{1,13},{5,1},{9,5},{13,9},{2,14},{6,2},{... | collective-permute-start | bytes 3145736 | tf_op jit(solution)/shard_map/ppermute | solution.py:39
  56.0 5.4 %collective-permute-start.7 = (f32[256,128]{1,0:T(8,128)S(1)}, f32[256,128]{1,0:T(8,128)S(1)}, u32[]{:S(2)}, u32[]{:S(2)}) collective-permute-start(f32[256,128]{1,0:T(8,128)S(1)} %get-tuple-element.131), channel_id=1, source_target_pairs={{0,16},{16,0},{1,17},{17,1},{2,18},{18,2},{3,19},{19,3},{4,20},{20... | collective-permute-start | bytes 393224 | tf_op jit(solution)/shard_map/ppermute | solution.py:43
  57.9 21.9 %all-to-all-start.3 = ((f32[4,256,128]{2,1,0:T(8,128)}), f32[4,256,128]{2,1,0:T(8,128)S(1)}, u32[]{:S(2)}, u32[]{:S(2)}) async-start(f32[4,256,128]{2,1,0:T(8,128)} %maximum_select_fusion.2), calls=%async_computation.3 | async-start | bytes 1048576 | tf_op jit(solution)/shard_map/all_to_all | solution.py:433
  61.4 7.8 %collective-permute-start.8 = (f32[2,256,128]{2,1,0:T(8,128)S(1)}, f32[2,256,128]{2,1,0:T(8,128)S(1)}, u32[]{:S(2)}, u32[]{:S(2)}) collective-permute-start(f32[2,256,128]{2,1,0:T(8,128)S(1)} %maximum_select_fusion.3), channel_id=1, source_target_pairs={{0,32},{32,0},{1,33},{33,1},{2,34},{34,2},{3,35},{35,3},{4,36},{36... | collective-permute-start | bytes 786440 | tf_op jit(solution)/shard_map/ppermute | solution.py:43
  62.7 26.3 %collective-permute-start.12 = (f32[16,2048]{1,0:T(8,128)S(1)}, f32[16,2048]{1,0:T(8,128)S(1)}, u32[]{:S(2)}, u32[]{:S(2)}) collective-permute-start(f32[16,2048]{1,0:T(8,128)S(1)} %copy-done), channel_id=1, source_target_pairs={{0,1},{1,2},{2,3},{3,0},{4,5},{5,6},{6,7},{7,4},{8,9},{9,10},{10,1... | collective-permute-start | bytes 393224 | tf_op jit(solution)/shard_map/ppermute | solution.py:39
  64.2 26.8 %collective-permute-start.13 = (f32[16,2048]{1,0:T(8,128)S(1)}, f32[16,2048]{1,0:T(8,128)S(1)}, u32[]{:S(2)}, u32[]{:S(2)}) collective-permute-start(f32[16,2048]{1,0:T(8,128)S(1)} %copy-done), channel_id=1, source_target_pairs={{0,2},{1,3},{2,0},{3,1},{4,6},{5,7},{6,4},{7,5},{8,10},{9,11},{10,... | collective-permute-start | bytes 393224 | tf_op jit(solution)/shard_map/ppermute | solution.py:39
  79.8 20.9 %all-to-all-start.2 = ((f32[4,256,128]{2,1,0:T(8,128)}), f32[4,256,128]{2,1,0:T(8,128)S(1)}, u32[]{:S(2)}, u32[]{:S(2)}) async-start(f32[4,256,128]{2,1,0:T(8,128)} %maximum_select_fusion.1), calls=%async_computation.2 | async-start | bytes 1048576 | tf_op jit(solution)/shard_map/all_to_all | solution.py:433
  86.2 71.3 %all-gather.9.cloned.1.call-start = ((), (), s32[]{:S(2)}) async-start(), calls=%async_computation.5 | async-start | bytes 3932160 | tf_op jit(solution)/shard_map/all_gather | solution.py:436
  86.3 6.1 %collective-permute-start.9 = (f32[256,128]{1,0:T(8,128)S(1)}, f32[256,128]{1,0:T(8,128)S(1)}, u32[]{:S(2)}, u32[]{:S(2)}) collective-permute-start(f32[256,128]{1,0:T(8,128)S(1)} %copy-done.9), channel_id=1, source_target_pairs={{0,32},{32,0},{1,33},{33,1},{2,34},{34,2},{3,35},{35,3},{4,36},{36... | collective-permute-start | bytes 393224 | tf_op jit(solution)/shard_map/ppermute | solution.py:43
  89.0 11.0 %collective-permute-start.5 = (f32[512,128]{1,0:T(8,128)S(1)}, f32[512,128]{1,0:T(8,128)S(1)}, u32[]{:S(2)}, u32[]{:S(2)}) collective-permute-start(f32[512,128]{1,0:T(8,128)S(1)} %slice.83), channel_id=1, source_target_pairs={{0,4},{4,8},{8,12},{12,0},{1,5},{5,9},{9,13},{13,1},{2,6},{6,10},{... | collective-permute-start | bytes 786440 | tf_op jit(solution)/shard_map/ppermute | solution.py:39
  91.1 9.7 %collective-permute-start.6 = (f32[512,128]{1,0:T(8,128)S(1)}, f32[512,128]{1,0:T(8,128)}, u32[]{:S(2)}, u32[]{:S(2)}) collective-permute-start(f32[512,128]{1,0:T(8,128)S(1)} %slice.84), channel_id=1, source_target_pairs={{0,12},{4,0},{8,4},{12,8},{1,13},{5,1},{9,5},{13,9},{2,14},{6,2},{... | collective-permute-start | bytes 786440 | tf_op jit(solution)/shard_map/ppermute | solution.py:39
  92.4 5.0 %collective-permute-start.14 = (f32[16,2048]{1,0:T(8,128)S(1)}, f32[16,2048]{1,0:T(8,128)S(1)}, u32[]{:S(2)}, u32[]{:S(2)}) collective-permute-start(f32[16,2048]{1,0:T(8,128)S(1)} %copy-done), channel_id=1, source_target_pairs={{0,3},{1,0},{2,1},{3,2},{4,7},{5,4},{6,5},{7,6},{8,11},{9,8},{10,9... | collective-permute-start | bytes 393224 | tf_op jit(solution)/shard_map/ppermute | solution.py:39
  101.7 86.2 %all-gather.11.cloned.1.call-start = ((), (), s32[]{:S(2)}) async-start(), calls=%async_computation.6 | async-start | bytes 2621440 | tf_op jit(solution)/shard_map/all_gather | solution.py:436
  102.8 10.5 %collective-permute-start.15 = (f32[2,512,128]{2,1,0:T(8,128)S(1)}, f32[2,512,128]{2,1,0:T(8,128)S(1)}, u32[]{:S(2)}, u32[]{:S(2)}) collective-permute-start(f32[2,512,128]{2,1,0:T(8,128)S(1)} %slice.85), channel_id=1, source_target_pairs={{0,4},{4,8},{8,12},{12,0},{1,5},{5,9},{9,13},{13,1},{2,6},{6,10},{... | collective-permute-start | bytes 1572872 | tf_op jit(solution)/shard_map/ppermute | solution.py:39
  105.0 9.3 %collective-permute-start.16 = (f32[2,512,128]{2,1,0:T(8,128)S(1)}, f32[2,512,128]{2,1,0:T(8,128)S(1)}, u32[]{:S(2)}, u32[]{:S(2)}) collective-permute-start(f32[2,512,128]{2,1,0:T(8,128)S(1)} %slice.86), channel_id=1, source_target_pairs={{0,12},{4,0},{8,4},{12,8},{1,13},{5,1},{9,5},{13,9},{2,14},{6,2},{... | collective-permute-start | bytes 1572872 | tf_op jit(solution)/shard_map/ppermute | solution.py:39
  121.0 23.7 %collective-permute-start.25 = (f32[4,1536,128]{2,1,0:T(8,128)}, f32[4,1536,128]{2,1,0:T(8,128)S(1)}, u32[]{:S(2)}, u32[]{:S(2)}) collective-permute-start(f32[4,1536,128]{2,1,0:T(8,128)} %bitcast.35), channel_id=1, source_target_pairs={{0,16},{16,0},{1,17},{17,1},{2,18},{18,2},{3,19},{19,3},{4,20},{20... | collective-permute-start | bytes 9437192 | tf_op jit(solution)/shard_map/ppermute | solution.py:43
  121.1 6.7 %collective-permute-start.17 = (f32[16,1024]{1,0:T(8,128)S(1)}, f32[16,1024]{1,0:T(8,128)S(1)}, u32[]{:S(2)}, u32[]{:S(2)}) collective-permute-start(f32[16,1024]{1,0:T(8,128)S(1)} %get-tuple-element.87), channel_id=1, source_target_pairs={{0,3},{1,0},{2,1},{3,2},{4,7},{5,4},{6,5},{7,6},{8,11},{9,8},{10,9... | collective-permute-start | bytes 196616 | tf_op jit(solution)/shard_map/ppermute | solution.py:39
  123.7 7.8 %collective-permute-start.18 = (f32[16,1024]{1,0:T(8,128)S(1)}, f32[16,1024]{1,0:T(8,128)S(1)}, u32[]{:S(2)}, u32[]{:S(2)}) collective-permute-start(f32[16,1024]{1,0:T(8,128)S(1)} %get-tuple-element.88), channel_id=1, source_target_pairs={{0,2},{1,3},{2,0},{3,1},{4,6},{5,7},{6,4},{7,5},{8,10},{9,11},{10,... | collective-permute-start | bytes 196616 | tf_op jit(solution)/shard_map/ppermute | solution.py:39
  124.8 8.1 %collective-permute-start.19 = (f32[16,1024]{1,0:T(8,128)S(1)}, f32[16,1024]{1,0:T(8,128)S(1)}, u32[]{:S(2)}, u32[]{:S(2)}) collective-permute-start(f32[16,1024]{1,0:T(8,128)S(1)} %get-tuple-element.89), channel_id=1, source_target_pairs={{0,1},{1,2},{2,3},{3,0},{4,5},{5,6},{6,7},{7,4},{8,9},{9,10},{10,1... | collective-permute-start | bytes 196616 | tf_op jit(solution)/shard_map/ppermute | solution.py:39
  135.6 6.6 %collective-permute-start.22 = (f32[8,2048]{1,0:T(8,128)S(1)}, f32[8,2048]{1,0:T(8,128)S(1)}, u32[]{:S(2)}, u32[]{:S(2)}) collective-permute-start(f32[8,2048]{1,0:T(8,128)S(1)} %get-tuple-element.93.refs_0_), channel_id=1, source_target_pairs={{0,4},{4,8},{8,12},{12,0},{1,5},{5,9},{9,13},{13,1},{2,6},{6,10},{... | collective-permute-start | bytes 196616 | tf_op jit(solution)/shard_map/ppermute | solution.py:39
  136.8 7.2 %collective-permute-start.23 = (f32[8,2048]{1,0:T(8,128)S(1)}, f32[8,2048]{1,0:T(8,128)S(1)}, u32[]{:S(2)}, u32[]{:S(2)}) collective-permute-start(f32[8,2048]{1,0:T(8,128)S(1)} %get-tuple-element.93.refs_0_), channel_id=1, source_target_pairs={{0,8},{4,12},{8,0},{12,4},{1,9},{5,13},{9,1},{13,5},{2,10},{6,14},... | collective-permute-start | bytes 196616 | tf_op jit(solution)/shard_map/ppermute | solution.py:39
  140.4 4.3 %collective-permute-start.24 = (f32[8,2048]{1,0:T(8,128)S(1)}, f32[8,2048]{1,0:T(8,128)S(1)}, u32[]{:S(2)}, u32[]{:S(2)}) collective-permute-start(f32[8,2048]{1,0:T(8,128)S(1)} %get-tuple-element.93.refs_0_), channel_id=1, source_target_pairs={{0,12},{4,0},{8,4},{12,8},{1,13},{5,1},{9,5},{13,9},{2,14},{6,2},{... | collective-permute-start | bytes 196616 | tf_op jit(solution)/shard_map/ppermute | solution.py:39
  140.8 12.6 %collective-permute-start.28 = (f32[4,1024]{1,0:T(4,128)S(1)}, f32[4,1024]{1,0:T(4,128)S(1)}, u32[]{:S(2)}, u32[]{:S(2)}) collective-permute-start(f32[4,1024]{1,0:T(4,128)S(1)} %get-tuple-element.146), channel_id=1, source_target_pairs={{0,32},{32,0},{1,33},{33,1},{2,34},{34,2},{3,35},{35,3},{4,36},{36... | collective-permute-start | bytes 49160 | tf_op jit(solution)/shard_map/ppermute | solution.py:43
  142.2 11.2 %collective-permute-start.29 = (f32[2,4,2048]{2,1,0:T(4,128)S(1)}, f32[2,4,2048]{2,1,0:T(4,128)S(1)}, u32[]{:S(2)}, u32[]{:S(2)}) collective-permute-start(f32[2,4,2048]{2,1,0:T(4,128)S(1)} %get-tuple-element.99), channel_id=1, source_target_pairs={{0,32},{32,0},{1,33},{33,1},{2,34},{34,2},{3,35},{35,3},{4,36},{36... | collective-permute-start | bytes 196616 | tf_op jit(solution)/shard_map/ppermute | solution.py:43
  152.5 4.3 %collective-permute-start.26 = (f32[16,1024]{1,0:T(8,128)S(1)}, f32[16,1024]{1,0:T(8,128)S(1)}, u32[]{:S(2)}, u32[]{:S(2)}) collective-permute-start(f32[16,1024]{1,0:T(8,128)S(1)} %get-tuple-element.96), channel_id=1, source_target_pairs={{0,32},{32,0},{1,33},{33,1},{2,34},{34,2},{3,35},{35,3},{4,36},{36... | collective-permute-start | bytes 196616 | tf_op jit(solution)/shard_map/ppermute | solution.py:43
  157.6 18.4 %collective-permute-start.33 = (f32[4,1536,128]{2,1,0:T(8,128)}, f32[4,1536,128]{2,1,0:T(8,128)}, u32[]{:S(2)}, u32[]{:S(2)}) collective-permute-start(f32[4,1536,128]{2,1,0:T(8,128)} %bitcast.38), channel_id=1, source_target_pairs={{0,16},{16,0},{1,17},{17,1},{2,18},{18,2},{3,19},{19,3},{4,20},{20... | collective-permute-start | bytes 9437192 | tf_op jit(solution)/shard_map/ppermute | solution.py:43
  157.7 5.2 %collective-permute-start.35 = (f32[8,256]{1,0:T(8,128)S(1)}, f32[8,256]{1,0:T(8,128)S(1)}, u32[]{:S(2)}, u32[]{:S(2)}) collective-permute-start(f32[8,256]{1,0:T(8,128)S(1)} %get-tuple-element.154), channel_id=1, source_target_pairs={{0,16},{16,0},{1,17},{17,1},{2,18},{18,2},{3,19},{19,3},{4,20},{20... | collective-permute-start | bytes 24584 | tf_op jit(solution)/shard_map/ppermute | solution.py:43
  166.7 8.6 %collective-permute-start.30 = (f32[16,2048]{1,0:T(8,128)S(1)}, f32[16,2048]{1,0:T(8,128)S(1)}, u32[]{:S(2)}, u32[]{:S(2)}) collective-permute-start(f32[16,2048]{1,0:T(8,128)S(1)} %get-tuple-element.100.refs_0_), channel_id=1, source_target_pairs={{0,4},{4,8},{8,12},{12,0},{1,5},{5,9},{9,13},{13,1},{2,6},{6,10},{... | collective-permute-start | bytes 393224 | tf_op jit(solution)/shard_map/ppermute | solution.py:39
  166.9 8.5 %collective-permute-start.31 = (f32[16,2048]{1,0:T(8,128)S(1)}, f32[16,2048]{1,0:T(8,128)S(1)}, u32[]{:S(2)}, u32[]{:S(2)}) collective-permute-start(f32[16,2048]{1,0:T(8,128)S(1)} %get-tuple-element.100.refs_0_), channel_id=1, source_target_pairs={{0,8},{4,12},{8,0},{12,4},{1,9},{5,13},{9,1},{13,5},{2,10},{6,14},... | collective-permute-start | bytes 393224 | tf_op jit(solution)/shard_map/ppermute | solution.py:39
  169.7 6.2 %collective-permute-start.32 = (f32[16,2048]{1,0:T(8,128)S(1)}, f32[16,2048]{1,0:T(8,128)S(1)}, u32[]{:S(2)}, u32[]{:S(2)}) collective-permute-start(f32[16,2048]{1,0:T(8,128)S(1)} %get-tuple-element.100.refs_0_), channel_id=1, source_target_pairs={{0,12},{4,0},{8,4},{12,8},{1,13},{5,1},{9,5},{13,9},{2,14},{6,2},{... | collective-permute-start | bytes 393224 | tf_op jit(solution)/shard_map/ppermute | solution.py:39
  170.9 13.9 %collective-permute-start.37 = (f32[2,1024]{1,0:T(2,128)S(1)}, f32[2,1024]{1,0:T(2,128)S(1)}, u32[]{:S(2)}, u32[]{:S(2)}) collective-permute-start(f32[2,1024]{1,0:T(2,128)S(1)} %get-tuple-element.150), channel_id=1, source_target_pairs={{0,64},{64,0},{1,65},{65,1},{2,66},{66,2},{3,67},{67,3},{4,68},{68... | collective-permute-start | bytes 24584 | tf_op jit(solution)/shard_map/ppermute | solution.py:43
  175.4 9.5 %collective-permute-start.38 = (f32[8,2048]{1,0:T(8,128)S(1)}, f32[8,2048]{1,0:T(8,128)S(1)}, u32[]{:S(2)}, u32[]{:S(2)}) collective-permute-start(f32[8,2048]{1,0:T(8,128)S(1)} %get-tuple-element.108), channel_id=1, source_target_pairs={{0,64},{64,0},{1,65},{65,1},{2,66},{66,2},{3,67},{67,3},{4,68},{68... | collective-permute-start | bytes 196616 | tf_op jit(solution)/shard_map/ppermute | solution.py:43
  181.8 5.5 %collective-permute-start.34 = (f32[8,1024]{1,0:T(8,128)S(1)}, f32[8,1024]{1,0:T(8,128)S(1)}, u32[]{:S(2)}, u32[]{:S(2)}) collective-permute-start(f32[8,1024]{1,0:T(8,128)S(1)} %get-tuple-element.105), channel_id=1, source_target_pairs={{0,64},{64,0},{1,65},{65,1},{2,66},{66,2},{3,67},{67,3},{4,68},{68... | collective-permute-start | bytes 98312 | tf_op jit(solution)/shard_map/ppermute | solution.py:43
  187.9 8.6 %collective-permute-start.42 = (f32[4,1024,128]{2,1,0:T(8,128)}, f32[4,1024,128]{2,1,0:T(8,128)S(1)}, u32[]{:S(2)}, u32[]{:S(2)}) collective-permute-start(f32[4,1024,128]{2,1,0:T(8,128)} %bitcast.41), channel_id=1, source_target_pairs={{0,16},{16,0},{1,17},{17,1},{2,18},{18,2},{3,19},{19,3},{4,20},{20... | collective-permute-start | bytes 6291464 | tf_op jit(solution)/shard_map/ppermute | solution.py:43
  188.0 5.7 %collective-permute-start.39 = (f32[8,2048]{1,0:T(8,128)S(1)}, f32[8,2048]{1,0:T(8,128)S(1)}, u32[]{:S(2)}, u32[]{:S(2)}) collective-permute-start(f32[8,2048]{1,0:T(8,128)S(1)} %s23.1.c0), channel_id=1, source_target_pairs={{0,4},{4,8},{8,12},{12,0},{1,5},{5,9},{9,13},{13,1},{2,6},{6,10},{... | collective-permute-start | bytes 196616 | tf_op jit(solution)/shard_map/ppermute | solution.py:39
  189.0 7.0 %collective-permute-start.40 = (f32[8,2048]{1,0:T(8,128)S(1)}, f32[8,2048]{1,0:T(8,128)S(1)}, u32[]{:S(2)}, u32[]{:S(2)}) collective-permute-start(f32[8,2048]{1,0:T(8,128)S(1)} %s23.1.c0), channel_id=1, source_target_pairs={{0,8},{4,12},{8,0},{12,4},{1,9},{5,13},{9,1},{13,5},{2,10},{6,14},... | collective-permute-start | bytes 196616 | tf_op jit(solution)/shard_map/ppermute | solution.py:39
  203.4 6.1 %collective-permute-start.43 = (f32[8,2048]{1,0:T(8,128)S(1)}, f32[8,2048]{1,0:T(8,128)S(1)}, u32[]{:S(2)}, u32[]{:S(2)}) collective-permute-start(f32[8,2048]{1,0:T(8,128)S(1)} %top.1.c0), channel_id=1, source_target_pairs={{0,4},{4,8},{8,12},{12,0},{1,5},{5,9},{9,13},{13,1},{2,6},{6,10},{... | collective-permute-start | bytes 196616 | tf_op jit(solution)/shard_map/ppermute | solution.py:39
  203.7 6.5 %collective-permute-start.44 = (f32[8,2048]{1,0:T(8,128)S(1)}, f32[8,2048]{1,0:T(8,128)S(1)}, u32[]{:S(2)}, u32[]{:S(2)}) collective-permute-start(f32[8,2048]{1,0:T(8,128)S(1)} %top.1.c0), channel_id=1, source_target_pairs={{0,8},{4,12},{8,0},{12,4},{1,9},{5,13},{9,1},{13,5},{2,10},{6,14},... | collective-permute-start | bytes 196616 | tf_op jit(solution)/shard_map/ppermute | solution.py:39
  211.8 5.5 %collective-permute-start.46 = (f32[8,1024]{1,0:T(8,128)S(1)}, f32[8,1024]{1,0:T(8,128)S(1)}, u32[]{:S(2)}, u32[]{:S(2)}) collective-permute-start(f32[8,1024]{1,0:T(8,128)S(1)} %get-tuple-element.112), channel_id=1, source_target_pairs={{0,64},{64,0},{1,65},{65,1},{2,66},{66,2},{3,67},{67,3},{4,68},{68... | collective-permute-start | bytes 98312 | tf_op jit(solution)/shard_map/ppermute | solution.py:43
  222.4 10.0 %collective-permute-start.47 = (f32[16,2048]{1,0:T(8,128)S(1)}, f32[16,2048]{1,0:T(8,128)S(1)}, u32[]{:S(2)}, u32[]{:S(2)}) collective-permute-start(f32[16,2048]{1,0:T(8,128)S(1)} %b2.1.c0), channel_id=1, source_target_pairs={{0,4},{4,8},{8,12},{12,0},{1,5},{5,9},{9,13},{13,1},{2,6},{6,10},{... | collective-permute-start | bytes 393224 | tf_op jit(solution)/shard_map/ppermute | solution.py:39
  223.2 9.2 %collective-permute-start.48 = (f32[16,2048]{1,0:T(8,128)S(1)}, f32[16,2048]{1,0:T(8,128)S(1)}, u32[]{:S(2)}, u32[]{:S(2)}) collective-permute-start(f32[16,2048]{1,0:T(8,128)S(1)} %b2.1.c0), channel_id=1, source_target_pairs={{0,8},{4,12},{8,0},{12,4},{1,9},{5,13},{9,1},{13,5},{2,10},{6,14},... | collective-permute-start | bytes 393224 | tf_op jit(solution)/shard_map/ppermute | solution.py:39
  226.3 6.1 %collective-permute-start.49 = (f32[16,2048]{1,0:T(8,128)S(1)}, f32[16,2048]{1,0:T(8,128)S(1)}, u32[]{:S(2)}, u32[]{:S(2)}) collective-permute-start(f32[16,2048]{1,0:T(8,128)S(1)} %b2.1.c0), channel_id=1, source_target_pairs={{0,12},{4,0},{8,4},{12,8},{1,13},{5,1},{9,5},{13,9},{2,14},{6,2},{... | collective-permute-start | bytes 393224 | tf_op jit(solution)/shard_map/ppermute | solution.py:39
  226.6 5.8 %collective-permute-start.50 = (f32[8,2048]{1,0:T(8,128)S(1)}, f32[8,2048]{1,0:T(8,128)S(1)}, u32[]{:S(2)}, u32[]{:S(2)}) collective-permute-start(f32[8,2048]{1,0:T(8,128)S(1)} %get-tuple-element.111.x3), channel_id=1, source_target_pairs={{0,64},{64,0},{1,65},{65,1},{2,66},{66,2},{3,67},{67,3},{4,68},{68... | collective-permute-start | bytes 196616 | tf_op jit(solution)/shard_map/ppermute | solution.py:43
  233.0 4.6 %collective-permute-start.51 = (f32[16,1024]{1,0:T(8,128)S(1)}, f32[16,1024]{1,0:T(8,128)S(1)}, u32[]{:S(2)}, u32[]{:S(2)}) collective-permute-start(f32[16,1024]{1,0:T(8,128)S(1)} %get-tuple-element.115), channel_id=1, source_target_pairs={{0,32},{32,0},{1,33},{33,1},{2,34},{34,2},{3,35},{35,3},{4,36},{36... | collective-permute-start | bytes 196616 | tf_op jit(solution)/shard_map/ppermute | solution.py:43
  234.2 12.7 %collective-permute-start.55 = (f32[2,4,2048]{2,1,0:T(4,128)S(1)}, f32[2,4,2048]{2,1,0:T(4,128)S(1)}, u32[]{:S(2)}, u32[]{:S(2)}) collective-permute-start(f32[2,4,2048]{2,1,0:T(4,128)S(1)} %slice.101.a_mine), channel_id=1, source_target_pairs={{0,32},{32,0},{1,33},{33,1},{2,34},{34,2},{3,35},{35,3},{4,36},{36... | collective-permute-start | bytes 196616 | tf_op jit(solution)/shard_map/ppermute | solution.py:43
  242.8 4.3 %collective-permute-start.52 = (f32[8,2048]{1,0:T(8,128)S(1)}, f32[8,2048]{1,0:T(8,128)S(1)}, u32[]{:S(2)}, u32[]{:S(2)}) collective-permute-start(f32[8,2048]{1,0:T(8,128)S(1)} %get-tuple-element.118), channel_id=1, source_target_pairs={{0,12},{4,0},{8,4},{12,8},{1,13},{5,1},{9,5},{13,9},{2,14},{6,2},{... | collective-permute-start | bytes 196616 | tf_op jit(solution)/shard_map/ppermute | solution.py:39
  244.1 5.8 %collective-permute-start.53 = (f32[8,2048]{1,0:T(8,128)S(1)}, f32[8,2048]{1,0:T(8,128)S(1)}, u32[]{:S(2)}, u32[]{:S(2)}) collective-permute-start(f32[8,2048]{1,0:T(8,128)S(1)} %get-tuple-element.119), channel_id=1, source_target_pairs={{0,8},{4,12},{8,0},{12,4},{1,9},{5,13},{9,1},{13,5},{2,10},{6,14},... | collective-permute-start | bytes 196616 | tf_op jit(solution)/shard_map/ppermute | solution.py:39
  247.0 5.5 %collective-permute-start.54 = (f32[8,2048]{1,0:T(8,128)S(1)}, f32[8,2048]{1,0:T(8,128)S(1)}, u32[]{:S(2)}, u32[]{:S(2)}) collective-permute-start(f32[8,2048]{1,0:T(8,128)S(1)} %get-tuple-element.120), channel_id=1, source_target_pairs={{0,4},{4,8},{8,12},{12,0},{1,5},{5,9},{9,13},{13,1},{2,6},{6,10},{... | collective-permute-start | bytes 196616 | tf_op jit(solution)/shard_map/ppermute | solution.py:39
  253.1 5.3 %collective-permute-start.65 = (f32[8,256]{1,0:T(8,128)S(1)}, f32[8,256]{1,0:T(8,128)S(1)}, u32[]{:S(2)}, u32[]{:S(2)}) collective-permute-start(f32[8,256]{1,0:T(8,128)S(1)} %get-tuple-element.136), channel_id=1, source_target_pairs={{0,16},{16,0},{1,17},{17,1},{2,18},{18,2},{3,19},{19,3},{4,20},{20... | collective-permute-start | bytes 24584 | tf_op jit(solution)/shard_map/ppermute | solution.py:43
  253.2 18.0 %collective-permute-start.64 = (f32[8,512]{1,0:T(8,128)S(1)}, f32[8,512]{1,0:T(8,128)S(1)}, u32[]{:S(2)}, u32[]{:S(2)}) collective-permute-start(f32[8,512]{1,0:T(8,128)S(1)} %get-tuple-element.138), channel_id=1, source_target_pairs={{0,16},{16,0},{1,17},{17,1},{2,18},{18,2},{3,19},{19,3},{4,20},{20... | collective-permute-start | bytes 49160 | tf_op jit(solution)/shard_map/ppermute | solution.py:43
  253.8 18.1 %collective-permute-start.63 = (f32[8,1024]{1,0:T(8,128)S(1)}, f32[8,1024]{1,0:T(8,128)S(1)}, u32[]{:S(2)}, u32[]{:S(2)}) collective-permute-start(f32[8,1024]{1,0:T(8,128)S(1)} %get-tuple-element.140), channel_id=1, source_target_pairs={{0,16},{16,0},{1,17},{17,1},{2,18},{18,2},{3,19},{19,3},{4,20},{20... | collective-permute-start | bytes 98312 | tf_op jit(solution)/shard_map/ppermute | solution.py:43
  254.9 6.0 %collective-permute-start.57 = (f32[16,1024]{1,0:T(8,128)S(1)}, f32[16,1024]{1,0:T(8,128)S(1)}, u32[]{:S(2)}, u32[]{:S(2)}) collective-permute-start(f32[16,1024]{1,0:T(8,128)S(1)} %maximum_select_fusion.7.refs_0_), channel_id=1, source_target_pairs={{0,1},{1,2},{2,3},{3,0},{4,5},{5,6},{6,7},{7,4},{8,9},{9,10},{10,1... | collective-permute-start | bytes 196616 | tf_op jit(solution)/shard_map/ppermute | solution.py:39
  256.0 6.1 %collective-permute-start.58 = (f32[16,1024]{1,0:T(8,128)S(1)}, f32[16,1024]{1,0:T(8,128)S(1)}, u32[]{:S(2)}, u32[]{:S(2)}) collective-permute-start(f32[16,1024]{1,0:T(8,128)S(1)} %maximum_select_fusion.7.refs_0_), channel_id=1, source_target_pairs={{0,2},{1,3},{2,0},{3,1},{4,6},{5,7},{6,4},{7,5},{8,10},{9,11},{10,... | collective-permute-start | bytes 196616 | tf_op jit(solution)/shard_map/ppermute | solution.py:39
  258.4 4.3 %collective-permute-start.59 = (f32[16,1024]{1,0:T(8,128)S(1)}, f32[16,1024]{1,0:T(8,128)S(1)}, u32[]{:S(2)}, u32[]{:S(2)}) collective-permute-start(f32[16,1024]{1,0:T(8,128)S(1)} %maximum_select_fusion.7.refs_0_), channel_id=1, source_target_pairs={{0,3},{1,0},{2,1},{3,2},{4,7},{5,4},{6,5},{7,6},{8,11},{9,8},{10,9... | collective-permute-start | bytes 196616 | tf_op jit(solution)/shard_map/ppermute | solution.py:39
  268.0 7.2 %collective-permute-start.60 = (f32[16,2048]{1,0:T(8,128)S(1)}, f32[16,2048]{1,0:T(8,128)S(1)}, u32[]{:S(2)}, u32[]{:S(2)}) collective-permute-start(f32[16,2048]{1,0:T(8,128)S(1)} %get-tuple-element.124), channel_id=1, source_target_pairs={{0,3},{1,0},{2,1},{3,2},{4,7},{5,4},{6,5},{7,6},{8,11},{9,8},{10,9... | collective-permute-start | bytes 393224 | tf_op jit(solution)/shard_map/ppermute | solution.py:39
  270.3 7.2 %collective-permute-start.61 = (f32[16,2048]{1,0:T(8,128)S(1)}, f32[16,2048]{1,0:T(8,128)S(1)}, u32[]{:S(2)}, u32[]{:S(2)}) collective-permute-start(f32[16,2048]{1,0:T(8,128)S(1)} %get-tuple-element.125), channel_id=1, source_target_pairs={{0,2},{1,3},{2,0},{3,1},{4,6},{5,7},{6,4},{7,5},{8,10},{9,11},{10,... | collective-permute-start | bytes 393224 | tf_op jit(solution)/shard_map/ppermute | solution.py:39
  270.7 8.1 %collective-permute-start.62 = (f32[16,2048]{1,0:T(8,128)S(1)}, f32[16,2048]{1,0:T(8,128)S(1)}, u32[]{:S(2)}, u32[]{:S(2)}) collective-permute-start(f32[16,2048]{1,0:T(8,128)S(1)} %get-tuple-element.126), channel_id=1, source_target_pairs={{0,1},{1,2},{2,3},{3,0},{4,5},{5,6},{6,7},{7,4},{8,9},{9,10},{10,1... | collective-permute-start | bytes 393224 | tf_op jit(solution)/shard_map/ppermute | solution.py:39
  (26 other events, 365.6 us)
Sparse Core Ops, SparseCore 0:
  43.9 44.4 all-gather.6
  101.8 40.7 all-gather.8
  157.8 27.7 all-gather.10

commit v5 on v4

--- a/solution.py
+++ b/solution.py
@@ -92,61 +92,55 @@
 NND = ((1,), (0,))
 
 
-def copies_first(meta, e, f, ev, fv, sems):
+def copies_first(meta, refs, ev, fv, sems):
+    e, f = refs[:5], refs[5:]
     zi = Place(meta).zi
-    out_e, out_f = [], []
     spots = [zi, lax.rem(zi + 3, 4), lax.rem(zi + 1, 4)]
     far = lax.rem(zi + 2, 4)
+    pairs_e = [(ref, ev.at[w]) for ref, w in zip(e[:3], spots)]
+    pairs_e += [(e[3], ev.at[far, 0:2]), (e[4], ev.at[far, 2:4])]
+    pairs_f = [(ref, fv.at[w]) for ref, w in zip(f[:3], spots)]
+    pairs_f += [(f[3], fv.at[far, 0:2]), (f[4], fv.at[far, 2:4])]
+    made = [
+        pltpu.make_async_copy(src, dst, sems.at[k]) for k, (src, dst) in enumerate(pairs_e + pairs_f)
+    ]
+    return made[:5], [], made[5:]
+
+
+def copies_upper(level, meta, bufs, ev, fv, sems):
+    place = Place(meta)
+    groups = ([], [], [])
     k = 0
-
-    def tile(t):
-        return pl.ds(pl.multiple_of(t * B, B), B)
-
-    for ref, w in zip(e[:3], spots):
-        for s in range(4):
-            out_e.append(pltpu.make_async_copy(ref.at[s], ev.at[:, tile(w * 4 + s)], sems.at[k]))
-            k += 1
-    for ref, base in ((e[3], 0), (e[4], 2)):
-        for s in range(2):
-            out_e.append(
-                pltpu.make_async_copy(ref.at[s], ev.at[:, tile(far * 4 + base + s)], sems.at[k])
-            )
-            k += 1
-    for ref, w in zip(f[:3], spots):
-        out_f.append(pltpu.make_async_copy(ref, fv.at[:, tile(w)], sems.at[k]))
-        k += 1
-    for ref, base in ((f[3], 0), (f[4], 512)):
-        out_f.append(pltpu.make_async_copy(ref, fv.at[pl.ds(base, 512), tile(far)], sems.at[k]))
-        k += 1
-    return out_e, out_f
-
-
-def copies_upper(level, meta, bufs, ev, fv, sems):
-    ci = Place(meta).ci
-    sources = [(bufs[i].at[w], q, w) for i, q in ((0, ci), (1, 1 - ci)) for w in range(4)]
-    out_e, out_f = [], []
-    k = 0
-    for ref, q, w in sources:
+    for i, q in ((0, place.ci), (1, 1 - place.ci)):
         rows = pl.ds(pl.multiple_of(q * 256, 256), 256)
-        for s in range(4):
-            cols = pl.ds(pl.multiple_of((4 * s + w) * B, B), B)
-            out_e.append(
-                pltpu.make_async_copy(ref.at[pl.ds(s * 256, 256)], ev.at[rows, cols], sems.at[k])
-            )
-            k += 1
-    if fv is not None:
-        for ref, q, w in sources:
-            for h in range(level):
-                n = 512 // level
-                rows = pl.ds(pl.multiple_of(h * 512 + q * n, n), n)
-                cols = pl.ds(pl.multiple_of(w * B, B), B)
-                out_f.append(
-                    pltpu.make_async_copy(
-                        ref.at[pl.ds(1024 + h * n, n)], fv.at[rows, cols], sems.at[k]
-                    )
-                )
+        pairs = [(bufs[i].at[:, s], ev.at[:, lax.rem(place.zi + 4 - s, 4), rows]) for s in range(4)]
+        late = []
+        if level == 1:
+            late = [(bufs[i].at[:, 4:6], fv.at[:, pl.ds(2 * q, 2)])]
+        elif level == 2:
+            late = [(bufs[i].at[:, 4 + h], fv.at[:, 2 * h + q]) for h in (0, 1)]
+        for group, some in ((groups[i], pairs), (groups[2], late)):
+            for src, dst in some:
+                group.append(pltpu.make_async_copy(src, dst, sems.at[k]))
                 k += 1
-    return out_e, out_f
+    return groups
+
+
+def copies(level, meta, refs, ev, fv, sems):
+    if level == 0:
+        return copies_first(meta, refs, ev, fv, sems)
+    return copies_upper(level, meta, refs, ev, fv, sems)
+
+
+def finish(group):
+    for c in group:
+        c.wait()
+
+
+def tiles_in_order(level):
+    if level == 0:
+        return [(t // 4, t % 4) for t in range(NT)]
+    return [(t % 4, t // 4) for t in range(NT)]
 
 
 def column_mask(meta, level, n):
@@ -161,10 +155,18 @@
     return tile < Place(meta).live(level)
 
 
-def solve_rows(ev, cs, put):
+def solve_rows(level, meta, ev, yv, cs, late):
+    first = Place(meta).ci if level else 0
+
     def body(j, carry):
-        rows = pl.ds(pl.multiple_of(j * 256, 256), 256)
-        put(rows, product(cs, ev[rows, :], NTD))
+        @pl.when(j == 1)
+        def _():
+            finish(late)
+
+        at = pl.multiple_of(jnp.where(j == 0, first, 1 - first) * 256, 256)
+        rows = pl.ds(at, 256)
+        w = jnp.concatenate([ev[w, s, rows, :] for w, s in tiles_in_order(level)], 1)
+        yv[:, rows] = product(cs, w, NTD)
         return carry
 
     lax.fori_loop(0, 2, body, 0)
@@ -184,11 +186,8 @@
         y_out, keep_out, give_out = refs[:3]
         refs = refs[3:]
     ev, fv, cv, yv, uv, sems = refs
-    if level == 0:
-        ce, cf = copies_first(meta, w_refs[:5], w_refs[5:], ev, fv, sems)
-    else:
-        ce, cf = copies_upper(level, meta, w_refs, ev, fv, sems)
-    for c in ce + cf:
+    early, late, last = copies(level, meta, w_refs, ev, fv, sems)
+    for c in [*early, *late, *last]:
         c.start()
     r = n // 4
     if level < 2:
@@ -197,25 +196,17 @@
         c = cv[...]
     else:
         c = summed(c_refs, r)
-    c = jnp.where(column_mask(meta, level, n), c, 0.0)
-    cs = stacked(c)
-    for c in ce:
-        c.wait()
-    mask = row_mask(meta, level, n)
-
-    def put_y(rows, v):
-        yv[:, rows] = v
-
-    solve_rows(ev, cs, put_y)
-    y = jnp.where(mask, yv[...], 0.0)
+    cs = stacked(jnp.where(column_mask(meta, level, n), c, 0.0))
+    finish(early)
+    solve_rows(level, meta, ev, yv, cs, late)
+    y = jnp.where(row_mask(meta, level, n), yv[...], 0.0)
     y_out[...] = y
     ys = stacked(y)
-    for c in cf:
-        c.wait()
+    finish(last)
 
     def body(j, carry):
-        rows = pl.ds(pl.multiple_of(j * 256, 256), 256)
-        uv[:, rows] = product(ys, fv[rows, :], NTD)
+        w = jnp.concatenate([fv[w, j] for w in range(4)], 1)
+        uv[:, pl.ds(pl.multiple_of(j * 256, 256), 256)] = product(ys, w, NTD)
         return carry
 
     lax.fori_loop(0, 4, body, 0)
@@ -260,52 +251,55 @@
         dst[:, t * B : (t + 1) * B] = anc[lax.div(v, NT), :, cols]
 
 
-def s01_kernel(meta, keep, recv, b1, c1, pk, pg, acc):
+def s01_kernel(meta, keep, recv, b_mine, b_other, c1, pk, pg, acc):
+    place = Place(meta)
     acc[...] = jnp.zeros_like(acc)
-    add_tiles(meta, Place(meta).own(0), keep, acc)
-    add_tiles(meta, Place(meta).partner(0), recv, acc)
-    c1[...] = b1[...] - acc[0]
+    add_tiles(meta, place.own(0), keep, acc)
+    add_tiles(meta, place.partner(0), recv, acc)
+    group = (0, place.x0, place.leaf >> 1)
+    for ref, c in ((b_mine, place.ci), (b_other, 1 - place.ci)):
+        at = 0
+        for i in range(3):
+            width = 1024 >> i
+            cols = pl.ds(pl.multiple_of((2 * group[i] + c) * width, width), width)
+            acc[i, :, cols] = acc[i, :, cols] - ref[:, at : at + width]
+            at += width
+    c1[...] = -acc[0]
     for i in (0, 1):
         low, high = acc[i + 1, 0:4, :], acc[i + 1, 4:8, :]
-        pk[i] = jnp.where(Place(meta).x0 == 0, low, high)
-        pg[i] = jnp.where(Place(meta).x0 == 0, high, low)
-
-
-def s12_kernel(meta, keep, recv, b2, pk, pr, part, keep3, give3, acc):
+        pk[i] = jnp.where(place.x0 == 0, low, high)
+        pg[i] = jnp.where(place.x0 == 0, high, low)
+
+
+def s12_kernel(meta, keep, recv, pk, pr, part, keep3, give3, acc):
+    place = Place(meta)
     acc[...] = jnp.zeros_like(acc)
-    add_tiles(meta, Place(meta).own(1), keep, acc)
-    add_tiles(meta, Place(meta).partner(1), recv, acc)
+    add_tiles(meta, place.own(1), keep, acc)
+    add_tiles(meta, place.partner(1), recv, acc)
+    for i in (0, 1):
+        acc[i, 0:4, :] = acc[i, 0:4, :] + (pk[i] + pr[i])
     part[...] = -acc[0]
-    part[0:4, :] = part[0:4, :] + (b2[...] - (pk[0] + pr[0]))
-    acc[1, 0:4, :] = acc[1, 0:4, :] + (pk[1] + pr[1])
-    split_rows(acc.at[1], 4, Place(meta).x1, keep3, give3)
-
-
-def s23_kernel(meta, keep, recv, b3, keep3, recv3, part, acc):
+    split_rows(acc.at[1], 4, place.x1, keep3, give3)
+
+
+def s23_kernel(meta, keep, recv, keep3, recv3, part, acc):
+    place = Place(meta)
     acc[...] = jnp.zeros_like(acc)
-    add_tiles(meta, Place(meta).own(2), keep, acc)
-    add_tiles(meta, Place(meta).partner(2), recv, acc)
+    add_tiles(meta, place.own(2), keep, acc)
+    add_tiles(meta, place.partner(2), recv, acc)
     part[...] = -(acc[0] + (keep3[...] + recv3[...]))
-    part[0:2, :] = part[0:2, :] + b3[...]
 
 
 def top_kernel(meta, c0, c1, c2, c3, *refs):
     w_refs, (x_out, ev, yv, sems) = refs[:2], refs[2:]
-    ce, _ = copies_upper(3, meta, w_refs, ev, None, sems)
-    for c in ce:
+    early, late, _ = copies(3, meta, w_refs, ev, None, sems)
+    for c in [*early, *late]:
         c.start()
     c = summed((c0, c1, c2, c3), 2)
-    keep = column_mask(meta, 3, 8)
-    cs = stacked(jnp.where(keep, c, 0.0))
-    for c in ce:
-        c.wait()
-
-    def put_y(rows, v):
-        yv[:, rows] = v
-
-    solve_rows(ev, cs, put_y)
-    y = jnp.where(row_mask(meta, 3, 8), yv[...], 0.0)
-    back(meta, 3, 8, ev, y, [x_out])
+    cs = stacked(jnp.where(column_mask(meta, 3, 8), c, 0.0))
+    finish(early)
+    solve_rows(3, meta, ev, yv, cs, late)
+    back(meta, 3, 8, ev, jnp.where(row_mask(meta, 3, 8), yv[...], 0.0), [x_out])
 
 
 def back(meta, level, n, ev, z, x_out):
@@ -314,7 +308,8 @@
 
     def body(j, carry):
         cols = pl.ds(pl.multiple_of(j * 512, 512), 512)
-        v = product(zs, ev[:, cols], NND)
+        w = jnp.concatenate([ev[j, i] if level == 0 else ev[i, j] for i in range(4)], 1)
+        v = product(zs, w, NND)
         col = lax.broadcasted_iota(jnp.int32, (n, 512), 1) + j * 512
         v = jnp.where(col < live, v, 0.0)
         r = n // len(x_out)
@@ -366,11 +361,8 @@
     y_ref, refs = refs[0], refs[1:]
     w_refs, refs = refs[:count], refs[count:]
     x_out, (ev, fv, gv, ov, sems) = refs[:-5], refs[-5:]
-    if level == 0:
-        ce, cf = copies_first(meta, w_refs[:5], w_refs[5:], ev, fv, sems)
-    else:
-        ce, cf = copies_upper(level, meta, w_refs, ev, fv, sems)
-    for c in cf + ce:
+    early, late, first = copies(level, meta, w_refs, ev, fv, sems)
+    for c in [*first, *early, *late]:
         c.start()
     r = n // 4
     if level == 0:
@@ -379,15 +371,14 @@
         g = gv[...]
     else:
         take_tiles(meta, Place(meta).own(level), anc, ov)
-        bit = Place(meta).bit(level)
-        g = merged(ov[...], recv[...], r // 2, bit)
+        g = merged(ov[...], recv[...], r // 2, Place(meta).bit(level))
     gs = stacked(g)
-    for c in cf:
-        c.wait()
-    z = y_ref[...] - product(gs, fv[...], NND)
+    finish(first)
+    w = jnp.concatenate([fv[w].reshape(1024, B) for w in range(4)], 1)
+    z = y_ref[...] - product(gs, w, NND)
     z = jnp.where(row_mask(meta, level, n), z, 0.0)
-    for c in ce:
-        c.wait()
+    finish(early)
+    finish(late)
     back(meta, level, n, ev, z, x_out)
 
 
@@ -415,8 +406,9 @@
     live_tiles, row_tiles, rhs0, rhs1, rhs2, rhs3, dinv0, dinv1, dinv2, dinv3, off0, off1, off2
 ):
     ci, x0, x1 = lax.axis_index("core"), lax.axis_index("x0"), lax.axis_index("x1")
+    zi = lax.axis_index("z")
     leaf = x1 * 4 + x0 * 2 + ci
-    here = leaf * 16 + lax.axis_index("z") * 4 + lax.axis_index("y")
+    here = leaf * 16 + zi * 4 + lax.axis_index("y")
     meta = jnp.concatenate([here.reshape(1), live_tiles, row_tiles.reshape(-1)])
     bits = [("core", ci), ("x0", x0), ("x1", x1)]
 
@@ -424,49 +416,50 @@
         axis, bit = bits[i]
         return ordered(v, flip(v, axis), bit, dim)
 
-    def swapped(pair, dim):
-        mine = lax.dynamic_index_in_dim(pair, ci, dim, keepdims=False)
-        give = lax.dynamic_index_in_dim(pair, 1 - ci, dim, keepdims=False)
-        return mine, flip(give, "core")
-
-    def rows_to_z(e):
-        return lax.all_to_all(e, "z", 0, 0, tiled=True).reshape(1024, B)
-
-    def gathered(e):
-        return lax.all_gather(e, "y", axis=0, tiled=False)
-
-    def spread(v, levels):
-        for axis, bit in bits[:levels]:
-            keep, give = halves(v, bit)
-            v = ordered(keep, flip(give, axis), bit, 1)
-        return v
+    def pick(v, i, dim=0):
+        return lax.dynamic_index_in_dim(v, i, dim, keepdims=False)
+
+    def for_z(pair, other, bit):
+        blocks = []
+        for s in range(4):
+            z = (zi + s) % 4
+            blocks.append(jnp.where(z // 2 == bit, pick(pair, z % 2), pick(other, z % 2)))
+        return [blocks[0]] + [shift(blocks[s], "z", s) for s in (1, 2, 3)]
+
+    def gathered(blocks, f):
+        parts = [v[None] for v in blocks] + ([] if f is None else [f.reshape(2, 256, B)])
+        return lax.all_gather(jnp.concatenate(parts, 0), "y", axis=0, tiled=False)
 
     gate = lax.optimization_barrier
     e0 = jnp.swapaxes(dinv0.reshape(4, 4, B, B), 0, 1).reshape(4, 512, B)
-    e0, dinv1, off0 = gate((e0, dinv1, off0))
+    e0, dinv1, off0 = gate((e0, dinv1, off0.reshape(4, 256, B)))
     e0 = lax.all_to_all(e0, "y", 0, 0, tiled=True)
     fa, fb = shift(off0, "z", 1), shift(off0, "z", -1)
-    e1 = ordered(*swapped(dinv1.reshape(2, 2, 256, B), 1), ci, 0)
-    e1, fa, fb = gate((e1, fa, fb))
-    e1 = rows_to_z(e1)
+    e1 = dinv1.reshape(2, 2, 256, B)
+    e1 = for_z(pick(e1, ci, 1), flip(pick(e1, 1 - ci, 1), "core"), ci)
     e0, fa, fb, e1, dinv2, off2, dinv3 = gate((e0, fa, fb, e1, dinv2, off2, dinv3))
-    m1 = gathered(jnp.concatenate([e1, off1], 0))
+    m1 = gathered(e1, off1)
 
     ea, eb = shift(e0, "z", 1), shift(e0, "z", -1)
-    fc, fd = shift(fa[:512], "z", 1), shift(fb[512:], "z", -1)
-    e2 = joined(ordered(*(v[None] for v in swapped(dinv2.reshape(2, 256, B), 0)), ci, 0), 1)
+    fc, fd = shift(fa[:2], "z", 1), shift(fb[2:], "z", -1)
+    e2 = dinv2.reshape(2, 256, B)
+    e2 = ordered(pick(e2, ci)[None], flip(pick(e2, 1 - ci)[None], "core"), ci, 0)
+    e2 = for_z(e2, flip(e2, "x0"), x0)
     f2 = joined(off2, 1)
-    e3 = joined(joined(dinv3[None], 1), 2)
-    e2, e3 = rows_to_z(e2), rows_to_z(e3)
+    e3 = joined(dinv3[None], 1)
+    e3 = for_z(e3, flip(e3, "x1"), x1)
     c0 = gather4(rhs0, "y")
     ea, eb, fc, fd, e2, f2, e3, c0 = gate((ea, eb, fc, fd, e2, f2, e3, c0))
     ec, ed = shift(ea[:2], "z", 1), shift(eb[2:], "z", -1)
+    b_mine, b_other = halves(jnp.concatenate([rhs1, rhs2, rhs3], 1), ci)
+    b_other = flip(b_other, "core")
+    ec, ed, b_mine, b_other = gate((ec, ed, b_mine, b_other))
     w0 = [e0, ea, eb, ec, ed, off0, fa, fb, fc, fd]
-    m2 = gathered(jnp.concatenate([e2, f2], 0))
-    m3 = gathered(e3)
+    m2 = gathered(e2, f2)
+    m3 = gathered(e3, None)
 
     dma = pltpu.SemaphoreType.DMA
-    ev, fv = pltpu.VMEM((512, ORDER), f32), pltpu.VMEM((1024, 512), f32)
+    ev, fv = pltpu.VMEM((4, 4, 512, B), f32), pltpu.VMEM((4, 4, 256, B), f32)
 
     def work(n):
         return [pltpu.VMEM((n, ORDER), f32), pltpu.VMEM((n, 512), f32), pltpu.VMEM((n, 1024), f32)]
@@ -476,43 +469,42 @@
 
     y0, *u = call(
         functools.partial(forward_kernel, 0, 64, "rs"), "f0", [(64, 512)] + [(16, 1024)] * 4,
-        [ev, fv, *work(64), dma((24,))], meta, c0, w0, flops(64),
-    )
-    m1, rhs1, rhs2, rhs3, _ = gate((m1, rhs1, rhs2, rhs3, y0))
-    b1, b2, b3 = spread(rhs1, 1), spread(rhs2, 2), spread(rhs3, 3)
+        [ev, fv, *work(64), dma((10,))], meta, c0, w0, flops(64),
+    )
+    m1, _ = gate((m1, y0))
     w1 = m1, flip(m1, "core")
     parts = scatter4(u, "y")
     u = (parts[0] + parts[1]) + (parts[2] + parts[3])
     keep, give = halves(u, ci)
     c1, pk, pg = call(
         s01_kernel, "s01", [(8, ORDER), (2, 4, ORDER), (2, 4, ORDER)],
-        [pltpu.VMEM((3, 8, ORDER), f32)], meta, [keep, flip(give, "core"), b1],
+        [pltpu.VMEM((3, 8, ORDER), f32)], meta, [keep, flip(give, "core"), b_mine, b_other],
     )
     pr = flip(pg, "x0")
     y1, keep, give = call(
         functools.partial(forward_kernel, 1, 32, "ar"), "f1", [(32, 512), (16, 1024), (16, 1024)],
-        [ev, fv, *work(32), dma((48,))], meta, gather4(c1, "z"), w1, flops(32),
+        [ev, fv, *work(32), dma((12,))], meta, gather4(c1, "z"), w1, flops(32),
     )
     part, keep3, give3 = call(
         s12_kernel, "s12", [(16, ORDER), (8, ORDER), (8, ORDER)],
-        [pltpu.VMEM((2, 16, ORDER), f32)], meta, [keep, flip(give, "x0"), b2, pk, pr],
+        [pltpu.VMEM((2, 16, ORDER), f32)], meta, [keep, flip(give, "x0"), pk, pr],
     )
     m2, _ = gate((m2, part))
     w2 = m2, flip(m2, "core")
     recv3 = flip(give3, "x1")
     y2, keep, give = call(
         functools.partial(forward_kernel, 2, 16, "ar"), "f2", [(16, 512), (8, 1024), (8, 1024)],
-        [ev, fv, *work(16), dma((48,))], meta, gather4(part, "z"), w2, flops(16),
+        [ev, fv, *work(16), dma((12,))], meta, gather4(part, "z"), w2, flops(16),
     )
     (part,) = call(
         s23_kernel, "s23", [(8, ORDER)],
-        [pltpu.VMEM((1, 8, ORDER), f32)], meta, [keep, flip(give, "x1"), b3, keep3, recv3],
+        [pltpu.VMEM((1, 8, ORDER), f32)], meta, [keep, flip(give, "x1"), keep3, recv3],
     )
 
     m3, _ = gate((m3, part))
     w3 = m3, flip(m3, "core")
     (part,) = call(
-        top_kernel, "top", [(8, ORDER)], [ev, pltpu.VMEM((8, 512), f32), dma((32,))],
+        top_kernel, "top", [(8, ORDER)], [ev, pltpu.VMEM((8, 512), f32), dma((8,))],
         meta, gather4(part, "z"), w3, flops(8),
     )
     x3, give = call(
@@ -523,7 +515,7 @@
     x3r = flip(x3, "x1")
 
     def rest(n, small):
-        return [ev, fv, pltpu.VMEM((n, 1024), f32), pltpu.VMEM((n // 2, 1024), f32), dma((48,))]
+        return [ev, fv, pltpu.VMEM((n, 1024), f32), pltpu.VMEM((n // 2, 1024), f32), dma((12,))]
 
     (part,) = call(
         functools.partial(backward_kernel, 2, 16), "b2", [(16, ORDER)], rest(16, 0),

time: 287 us -> 272 us (0.948)
  blocking collectives: 12.4 us -> 0 us
  local copies, waits for them, and re-layouts: 11.4 us -> 16.7 us
  Pallas kernels: 42.8 us -> 38.5 us
    all_to_all x1 -> x0, blocking collectives: 12.4 us -> none  [rows_to_z(): return lax.all_to_all(e, 'z', 0, 0, tiled=True).reshape(1024, B)]
    ppermute x38 -> x47, starting transfers between devices: 58.8 us -> 70.6 us  [shift(): return lax.ppermute(v, axis, [(i, (i + s) % 4) for i in range(4)])]
    ppermute x38 -> x47, waiting for transfers between devices: 58.5 us -> 69 us  [shift(): return lax.ppermute(v, axis, [(i, (i + s) % 4) for i in range(4)])]
    ppermute x28 -> x23, waiting for transfers between devices: 31.4 us -> 20.9 us  [flip(): return lax.ppermute(v, axis, [(0, 1), (1, 0)])]
    all_to_all x2 -> x0, starting transfers between devices: 9.86 us -> none  [rows_to_z(): return lax.all_to_all(e, 'z', 0, 0, tiled=True).reshape(1024, B)]
    all_to_all x2 -> x0, waiting for transfers between devices: 9.79 us -> none  [rows_to_z(): return lax.all_to_all(e, 'z', 0, 0, tiled=True).reshape(1024, B)]
    all_gather x3, waiting for transfers between devices: 0.06 us -> 8.24 us  [gathered(): return lax.all_gather(jnp.concatenate(parts, 0), 'y', axis=0, tiled=False)]
    unnamed x37 -> x43, local copies, waits for them, and re-layouts: 4.74 us -> 10 us
  transfers between devices with their start and end apart: 72 -> 74, of which waited for: 42 -> 41; matrix products, arithmetic and copies ran while one was open for 3% -> 4% of each run, Pallas kernels for 11% -> 10%
where the time goes in v5:
time: 272 us; the launch traced here: 271 us
  starting transfers between devices  98.2 us (36%)
  waiting for transfers between devices  98.2 us (36%)
  Pallas kernels  38.5 us (14%)
  local copies, waits for them, and re-layouts  16.7 us (6%)
  between operations  14.5 us (5%)
  other arithmetic  5.1 us (2%)
    ppermute x47, starting transfers between devices, shift(): return lax.ppermute(v, axis, [(i, (i + s) % 4) for i in range(4)])  70.6 us
    ppermute x47, waiting for transfers between devices, shift(): return lax.ppermute(v, axis, [(i, (i + s) % 4) for i in range(4)])  69 us
    pallas_call x13, Pallas kernels, call(): pl.pallas_call(kernel, out_shape=[jax.ShapeDtypeStruct(s, f32) for s in s...  38.5 us
    ppermute x23, starting transfers between devices, flip(): return lax.ppermute(v, axis, [(0, 1), (1, 0)])  22.8 us
    ppermute x23, waiting for transfers between devices, flip(): return lax.ppermute(v, axis, [(0, 1), (1, 0)])  20.9 us
    unnamed x43, local copies, waits for them, and re-layouts  10 us
    all_gather x3, waiting for transfers between devices, gathered(): return lax.all_gather(jnp.concatenate(parts, 0), 'y', axis=0, tiled=False)  8.24 us
  transfers between devices with their start and end apart: 74, of which 41 were waited for; matrix products, arithmetic and copies ran while one was open for 4% of the time, Pallas kernels for 10%

profile of v5, /device:TPU:0, one launch (start us, length us, event | category | flops | bytes accessed | tf_op | source)
XLA Modules:
  0.0 271.1 jit_solution(2290130321854783785)
XLA Ops:
  7.2 2.4 copy.22
  9.5 4.7 %all-to-all-start = ((f32[4,512,128]{2,1,0:T(8,128)}), f32[4,512,128]{2,1,0:T(8,128)S(1)}, u32[]{:S(2)}, u32[]{:S(2)}) async-start(f32[4,512,128]{2,1,0:T(8,128)} %bitcast.3), calls=%async_computation | async-start | bytes 2097152 | tf_op jit(solution)/shard_map/all_to_all | solution.py:436
  14.3 2.0 collective-permute-start
  16.3 2.2 collective-permute-start.1
  20.2 3.4 %collective-permute-start.4 = (f32[256,128]{1,0:T(8,128)S(1)}, f32[256,128]{1,0:T(8,128)S(1)}, u32[]{:S(2)}, u32[]{:S(2)}) collective-permute-start(f32[256,128]{1,0:T(8,128)S(1)} %get-tuple-element.143), channel_id=1, source_target_pairs={{0,8},{4,12},{8,0},{12,4},{1,9},{5,13},{9,1},{13,5},{2,10},{6,14},... | collective-permute-start | bytes 393224 | tf_op jit(solution)/shard_map/ppermute | solution.py:39
  24.7 8.7 %collective-permute-done.3 = f32[256,128]{1,0:T(8,128)S(1)} collective-permute-done((f32[256,128]{1,0:T(8,128)S(1)}, f32[256,128]{1,0:T(8,128)S(1)}, u32[]{:S(2)}, u32[]{:S(2)}) %collective-permute-start.3) | collective-permute-done | bytes 131104 | tf_op jit(solution)/shard_map/ppermute | solution.py:39
  33.3 3.7 %collective-permute-done.4 = f32[256,128]{1,0:T(8,128)S(1)} collective-permute-done((f32[256,128]{1,0:T(8,128)S(1)}, f32[256,128]{1,0:T(8,128)S(1)}, u32[]{:S(2)}, u32[]{:S(2)}) %collective-permute-start.4) | collective-permute-done | bytes 131104 | tf_op jit(solution)/shard_map/ppermute | solution.py:39
  40.8 1.6 collective-permute-start.16
  42.4 3.2 %collective-permute-start.7 = (f32[4,512,128]{2,1,0:T(8,128)S(1)}, f32[4,512,128]{2,1,0:T(8,128)}, u32[]{:S(2)}, u32[]{:S(2)}) collective-permute-start(f32[4,512,128]{2,1,0:T(8,128)S(1)} %all-to-all-done.refs_4_.refs_5_), channel_id=1, source_target_pairs={{0,12},{4,0},{8,4},{12,8},{1,13},{5,1},{9,5},{13,9},{2,14},{6,2},{... | collective-permute-start | bytes 3145736 | tf_op jit(solution)/shard_map/ppermute | solution.py:39
  45.6 1.7 collective-permute-start.21
  47.3 2.7 collective-permute-start.22
  52.0 2.7 %collective-permute-start.17 = (f32[2,256,128]{2,1,0:T(8,128)S(1)}, f32[2,256,128]{2,1,0:T(8,128)S(1)}, u32[]{:S(2)}, u32[]{:S(2)}) collective-permute-start(f32[2,256,128]{2,1,0:T(8,128)S(1)} %maximum_select_fusion.2), channel_id=1, source_target_pairs={{0,64},{64,0},{1,65},{65,1},{2,66},{66,2},{3,67},{67,3},{4,68},{68... | collective-permute-start | bytes 786440 | tf_op jit(solution)/shard_map/ppermute | solution.py:43
  54.9 1.8 collective-permute-done.23.refs_3_
  58.7 3.4 %collective-permute-done.15 = f32[256,128]{1,0:T(8,128)S(1)} collective-permute-done((f32[256,128]{1,0:T(8,128)S(1)}, f32[256,128]{1,0:T(8,128)S(1)}, u32[]{:S(2)}, u32[]{:S(2)}) %collective-permute-start.15) | collective-permute-done | bytes 131104 | tf_op jit(solution)/shard_map/ppermute | solution.py:43
  63.2 1.9 collective-permute-start.11
  65.8 6.7 %collective-permute-done.8.refs_12_.refs_13_ = f32[2,256,128]{2,1,0:T(8,128)} collective-permute-done((f32[2,256,128]{2,1,0:T(8,128)S(1)}, f32[2,256,128]{2,1,0:T(8,128)}, u32[]{:S(2)}, u32[]{:S(2)}) %collective-permute-start.8) | collective-permute-done | bytes 262176 | tf_op jit(solution)/shard_map/ppermute | solution.py:39
  72.5 2.5 collective-permute-start.19
  75.8 4.0 %collective-permute-done.18 = f32[256,128]{1,0:T(8,128)S(1)} collective-permute-done((f32[256,128]{1,0:T(8,128)}, f32[256,128]{1,0:T(8,128)S(1)}, u32[]{:S(2)}, u32[]{:S(2)}) %collective-permute-start.18) | collective-permute-done | bytes 131104 | tf_op jit(solution)/shard_map/ppermute | solution.py:39
  80.6 1.6 collective-permute-start.13
  82.2 2.2 collective-permute-start.14
  84.5 2.9 %collective-permute-done.12 = f32[256,128]{1,0:T(8,128)S(1)} collective-permute-done((f32[256,128]{1,0:T(8,128)S(1)}, f32[256,128]{1,0:T(8,128)S(1)}, u32[]{:S(2)}, u32[]{:S(2)}) %collective-permute-start.12) | collective-permute-done | bytes 131104 | tf_op jit(solution)/shard_map/ppermute | solution.py:39
  94.6 1.9 collective-permute-start.25
  98.2 4.5 %collective-permute-done.24.refs_7_.refs_8_ = f32[2,512,128]{2,1,0:T(8,128)S(1)} collective-permute-done((f32[2,512,128]{2,1,0:T(8,128)S(1)}, f32[2,512,128]{2,1,0:T(8,128)S(1)}, u32[]{:S(2)}, u32[]{:S(2)}) %collective-permute-start.24) | collective-permute-done | bytes 524320 | tf_op jit(solution)/shard_map/ppermute | solution.py:39
  103.9 5.7 %f0.1 = (f32[64,512]{1,0:T(8,128)S(1)}, f32[16,1024]{1,0:T(8,128)S(1)}, f32[16,1024]{1,0:T(8,128)S(1)}, f32[16,1024]{1,0:T(8,128)S(1)}, f32[16,1024]{1,0:T(8,128)S(1)}) custom-call(s32[128]{0:T(128)S(1)} %pad_add_fusion.meta, f32[16,2048]{1,0:T(8,128)S(1)} %copy-done, f32[16,2048]{1,0:T(8,128)S(1)} %collective-permute-done.21.refs_1_, ...), custom_call_target="tpu_custom_call" | custom-call | flops 2415919104 | bytes 6815744 | tf_op jit(solution)/shard_map/f0/pallas_call | solution.py:393
  110.0 2.2 collective-permute-start.27
  114.1 2.3 collective-permute-done.27
  116.4 3.7 %collective-permute-done.28 = f32[16,1024]{1,0:T(8,128)S(1)} collective-permute-done((f32[16,1024]{1,0:T(8,128)S(1)}, f32[16,1024]{1,0:T(8,128)S(1)}, u32[]{:S(2)}, u32[]{:S(2)}) %collective-permute-start.28) | collective-permute-done | bytes 65568 | tf_op jit(solution)/shard_map/ppermute | solution.py:39
  123.3 1.6 collective-permute-start.31
  124.9 3.6 %collective-permute-start.32 = (f32[8,2048]{1,0:T(8,128)S(1)}, f32[8,2048]{1,0:T(8,128)S(1)}, u32[]{:S(2)}, u32[]{:S(2)}) collective-permute-start(f32[8,2048]{1,0:T(8,128)S(1)} %get-tuple-element.98.refs_0_), channel_id=1, source_target_pairs={{0,8},{4,12},{8,0},{12,4},{1,9},{5,13},{9,1},{13,5},{2,10},{6,14},... | collective-permute-start | bytes 196616 | tf_op jit(solution)/shard_map/ppermute | solution.py:39
  130.1 1.9 collective-permute-done.32.refs_2_
  132.7 1.8 copy-done.1
  134.5 4.9 %f1.1 = (f32[32,512]{1,0:T(8,128)S(1)}, f32[16,1024]{1,0:T(8,128)S(1)}, f32[16,1024]{1,0:T(8,128)S(1)}) custom-call(s32[128]{0:T(128)S(1)} %pad_add_fusion.meta, f32[8,2048]{1,0:T(8,128)S(1)} %get-tuple-element.98.refs_0_, f32[8,2048]{1,0:T(8,128)S(1)} %collective-permute-done.31.refs_1_, f32[8,2048]{1,0:T(8,128)S(1)} %collective-permute-done.32.refs_2_, ...), custom_call_target="tpu_custom_call" | custom-call | flops 1207959552 | bytes 6553600 | tf_op jit(solution)/shard_map/f1/pallas_call | solution.py:393
  140.0 3.8 %collective-permute-done.35.recv = f32[16,1024]{1,0:T(8,128)S(1)} collective-permute-done((f32[16,1024]{1,0:T(8,128)S(1)}, f32[16,1024]{1,0:T(8,128)S(1)}, u32[]{:S(2)}, u32[]{:S(2)}) %collective-permute-start.35) | collective-permute-done | bytes 65568 | tf_op jit(solution)/shard_map/ppermute | solution.py:43
  146.1 3.3 %collective-permute-start.38 = (f32[16,2048]{1,0:T(8,128)S(1)}, f32[16,2048]{1,0:T(8,128)S(1)}, u32[]{:S(2)}, u32[]{:S(2)}) collective-permute-start(f32[16,2048]{1,0:T(8,128)S(1)} %get-tuple-element.109.refs_0_), channel_id=1, source_target_pairs={{0,8},{4,12},{8,0},{12,4},{1,9},{5,13},{9,1},{13,5},{2,10},{6,14},... | collective-permute-start | bytes 393224 | tf_op jit(solution)/shard_map/ppermute | solution.py:39
  149.8 2.7 %collective-permute-start.42 = (f32[8,2048]{1,0:T(8,128)S(1)}, f32[8,2048]{1,0:T(8,128)S(1)}, u32[]{:S(2)}, u32[]{:S(2)}) collective-permute-start(f32[8,2048]{1,0:T(8,128)S(1)} %get-tuple-element.119), channel_id=1, source_target_pairs={{0,64},{64,0},{1,65},{65,1},{2,66},{66,2},{3,67},{67,3},{4,68},{68... | collective-permute-start | bytes 196616 | tf_op jit(solution)/shard_map/ppermute | solution.py:43
  152.7 3.4 %collective-permute-done.38.refs_2_ = f32[16,2048]{1,0:T(8,128)S(1)} collective-permute-done((f32[16,2048]{1,0:T(8,128)S(1)}, f32[16,2048]{1,0:T(8,128)S(1)}, u32[]{:S(2)}, u32[]{:S(2)}) %collective-permute-start.38) | collective-permute-done | bytes 131104 | tf_op jit(solution)/shard_map/ppermute | solution.py:39
  156.1 4.7 %f2.1 = (f32[16,512]{1,0:T(8,128)S(1)}, f32[8,1024]{1,0:T(8,128)S(1)}, f32[8,1024]{1,0:T(8,128)S(1)}) custom-call(s32[128]{0:T(128)S(1)} %pad_add_fusion.meta, f32[16,2048]{1,0:T(8,128)S(1)} %get-tuple-element.109.refs_0_, f32[16,2048]{1,0:T(8,128)S(1)} %collective-permute-done.37.refs_1_, f32[16,2048]{1,0:T(8,128)S(1)} %collective-permute-done.38.refs_2_, ...), custom_call_target="tpu_custom_call" | custom-call | flops 603979776 | bytes 6815744 | tf_op jit(solution)/shard_map/f2/pallas_call | solution.py:393
  160.8 2.8 %collective-permute-start.41 = (f32[8,1024]{1,0:T(8,128)S(1)}, f32[8,1024]{1,0:T(8,128)S(1)}, u32[]{:S(2)}, u32[]{:S(2)}) collective-permute-start(f32[8,1024]{1,0:T(8,128)S(1)} %get-tuple-element.117), channel_id=1, source_target_pairs={{0,64},{64,0},{1,65},{65,1},{2,66},{66,2},{3,67},{67,3},{4,68},{68... | collective-permute-start | bytes 98312 | tf_op jit(solution)/shard_map/ppermute | solution.py:43
  163.6 2.7 collective-permute-done.41.recv
  167.0 8.2 %all-gather.11.cloned.1.call-done = f32[16,256,128]{2,1,0:T(8,128)} async-done(((f32[4,256,128]{2,1,0:T(8,128)}), f32[16,256,128]{2,1,0:T(8,128)}) %all-gather.11.cloned.1.call-update) | async-done | bytes 2097168 | tf_op jit(solution)/shard_map/all_gather | solution.py:431
  175.2 1.6 collective-permute-start.43
  176.7 2.9 %collective-permute-start.44 = (f32[8,2048]{1,0:T(8,128)S(1)}, f32[8,2048]{1,0:T(8,128)S(1)}, u32[]{:S(2)}, u32[]{:S(2)}) collective-permute-start(f32[8,2048]{1,0:T(8,128)S(1)} %s23.1.c0), channel_id=1, source_target_pairs={{0,8},{4,12},{8,0},{12,4},{1,9},{5,13},{9,1},{13,5},{2,10},{6,14},... | collective-permute-start | bytes 196616 | tf_op jit(solution)/shard_map/ppermute | solution.py:39
  180.9 2.5 collective-permute-done.44.c2
  185.2 4.6 %top.1.c0 = f32[8,2048]{1,0:T(8,128)S(1)} custom-call(s32[128]{0:T(128)S(1)} %pad_add_fusion.meta, f32[8,2048]{1,0:T(8,128)S(1)} %s23.1.c0, f32[8,2048]{1,0:T(8,128)S(1)} %collective-permute-done.43.c1, f32[8,2048]{1,0:T(8,128)S(1)} %collective-permute-done.44.c2, f32[8,2048]{1,0:T(8,128)S(1)} %collective-permute-done.45.c3, f32[4,4,256,128]{3,2,1,0:T(8,128)} %bitcast.89, ...), custom_call_target="tpu_custom_call" | custom-call | flops 301989888 | bytes 4456448 | tf_op jit(solution)/shard_map/top/pallas_call | solution.py:393
  190.8 3.2 %collective-permute-start.48 = (f32[8,2048]{1,0:T(8,128)S(1)}, f32[8,2048]{1,0:T(8,128)S(1)}, u32[]{:S(2)}, u32[]{:S(2)}) collective-permute-start(f32[8,2048]{1,0:T(8,128)S(1)} %top.1.c0), channel_id=1, source_target_pairs={{0,8},{4,12},{8,0},{12,4},{1,9},{5,13},{9,1},{13,5},{2,10},{6,14},... | collective-permute-start | bytes 196616 | tf_op jit(solution)/shard_map/ppermute | solution.py:39
  198.9 3.1 %collective-permute-start.50 = (f32[8,1024]{1,0:T(8,128)S(1)}, f32[8,1024]{1,0:T(8,128)S(1)}, u32[]{:S(2)}, u32[]{:S(2)}) collective-permute-start(f32[8,1024]{1,0:T(8,128)S(1)} %get-tuple-element.126), channel_id=1, source_target_pairs={{0,64},{64,0},{1,65},{65,1},{2,66},{66,2},{3,67},{67,3},{4,68},{68... | collective-permute-start | bytes 98312 | tf_op jit(solution)/shard_map/ppermute | solution.py:43
  201.9 2.4 collective-permute-done.50.refs_1_
  204.4 4.7 %b2.1.c0 = f32[16,2048]{1,0:T(8,128)S(1)} custom-call(s32[128]{0:T(128)S(1)} %pad_add_fusion.meta, f32[1,8,2048]{2,1,0:T(8,128)S(1)} %bitcast.81, f32[8,1024]{1,0:T(8,128)S(1)} %collective-permute-done.50.refs_1_, f32[16,512]{1,0:T(8,128)S(1)} %get-tuple-element.127.refs_2_, f32[4,6,256,128]{3,2,1,0:T(8,128)} %bitcast.87, ...), custom_call_target="tpu_custom_call" | custom-call | flops 603979776 | bytes 6422528 | tf_op jit(solution)/shard_map/b2/pallas_call | solution.py:393
  209.5 3.1 %collective-permute-start.52 = (f32[16,2048]{1,0:T(8,128)S(1)}, f32[16,2048]{1,0:T(8,128)S(1)}, u32[]{:S(2)}, u32[]{:S(2)}) collective-permute-start(f32[16,2048]{1,0:T(8,128)S(1)} %b2.1.c0), channel_id=1, source_target_pairs={{0,8},{4,12},{8,0},{12,4},{1,9},{5,13},{9,1},{13,5},{2,10},{6,14},... | collective-permute-start | bytes 393224 | tf_op jit(solution)/shard_map/ppermute | solution.py:39
  213.3 3.0 %collective-permute-start.54 = (f32[8,2048]{1,0:T(8,128)S(1)}, f32[8,2048]{1,0:T(8,128)S(1)}, u32[]{:S(2)}, u32[]{:S(2)}) collective-permute-start(f32[8,2048]{1,0:T(8,128)S(1)} %get-tuple-element.125.x3), channel_id=1, source_target_pairs={{0,64},{64,0},{1,65},{65,1},{2,66},{66,2},{3,67},{67,3},{4,68},{68... | collective-permute-start | bytes 196616 | tf_op jit(solution)/shard_map/ppermute | solution.py:43
  216.3 3.1 %collective-permute-done.54.x3r = f32[8,2048]{1,0:T(8,128)S(1)} collective-permute-done((f32[8,2048]{1,0:T(8,128)S(1)}, f32[8,2048]{1,0:T(8,128)S(1)}, u32[]{:S(2)}, u32[]{:S(2)}) %collective-permute-start.54) | collective-permute-done | bytes 65568 | tf_op jit(solution)/shard_map/ppermute | solution.py:43
  220.1 1.7 collective-permute-start.55
  222.3 2.1 collective-permute-done.55.refs_1_
  224.4 4.8 %b1.1 = (f32[8,2048]{1,0:T(8,128)S(1)}, f32[8,2048]{1,0:T(8,128)S(1)}, f32[8,2048]{1,0:T(8,128)S(1)}, f32[8,2048]{1,0:T(8,128)S(1)}) custom-call(s32[128]{0:T(128)S(1)} %pad_add_fusion.meta, f32[2,16,2048]{2,1,0:T(8,128)S(1)} %get-tuple-element.128.refs_0_, f32[16,1024]{1,0:T(8,128)S(1)} %collective-permute-done.55.refs_1_, ...), custom_call_target="tpu_custom_call" | custom-call | flops 1207959552 | bytes 6684672 | tf_op jit(solution)/shard_map/b1/pallas_call | solution.py:393
  230.2 2.3 collective-permute-start.57
  233.6 2.3 collective-permute-done.57.c2
  235.9 2.0 collective-permute-done.58.c3
  241.0 1.8 collective-permute-start.62
  242.8 2.1 collective-permute-start.63
  245.5 1.8 collective-permute-done.61.refs_1_
  247.8 4.9 %b0.1 = (f32[16,2048]{1,0:T(8,128)S(1)}, f32[16,2048]{1,0:T(8,128)S(1)}, f32[16,2048]{1,0:T(8,128)S(1)}, f32[16,2048]{1,0:T(8,128)S(1)}) custom-call(s32[128]{0:T(128)S(1)} %pad_add_fusion.meta, f32[16,1024]{1,0:T(8,128)S(1)} %maximum_select_fusion.3.refs_0_, f32[16,1024]{1,0:T(8,128)S(1)} %collective-permute-done.61.refs_1_, ...), custom_call_target="tpu_custom_call" | custom-call | flops 2415919104 | bytes 6684672 | tf_op jit(solution)/shard_map/b0/pallas_call | solution.py:393
  252.7 2.7 %collective-permute-start.64 = (f32[16,2048]{1,0:T(8,128)S(1)}, f32[16,2048]{1,0:T(8,128)S(1)}, u32[]{:S(2)}, u32[]{:S(2)}) collective-permute-start(f32[16,2048]{1,0:T(8,128)S(1)} %get-tuple-element.138), channel_id=1, source_target_pairs={{0,3},{1,0},{2,1},{3,2},{4,7},{5,4},{6,5},{7,6},{8,11},{9,8},{10,9... | collective-permute-start | bytes 393224 | tf_op jit(solution)/shard_map/ppermute | solution.py:39
  257.7 2.5 collective-permute-done.64
  260.2 2.4 collective-permute-done.65
  (175 shorter events, 57.6 us)
Async XLA Ops:
  9.5 27.5 %all-to-all-start = ((f32[4,512,128]{2,1,0:T(8,128)}), f32[4,512,128]{2,1,0:T(8,128)S(1)}, u32[]{:S(2)}, u32[]{:S(2)}) async-start(f32[4,512,128]{2,1,0:T(8,128)} %bitcast.3), calls=%async_computation | async-start | bytes 2097152 | tf_op jit(solution)/shard_map/all_to_all | solution.py:436
  14.2 95.5 %all-gather.7.cloned.1.call-start = ((), (), s32[]{:S(2)}) async-start(), calls=%async_computation.1 | async-start | bytes 3932160 | tf_op jit(solution)/shard_map/all_gather | solution.py:431
  14.3 22.8 %collective-permute-start = (f32[4,256,128]{2,1,0:T(8,128)}, f32[4,256,128]{2,1,0:T(8,128)S(1)}, u32[]{:S(2)}, u32[]{:S(2)}) collective-permute-start(f32[4,256,128]{2,1,0:T(8,128)} %bitcast.4.refs_9_.refs_10_), channel_id=1, source_target_pairs={{0,4},{4,8},{8,12},{12,0},{1,5},{5,9},{9,13},{13,1},{2,6},{6,10},{... | collective-permute-start | bytes 1572872 | tf_op jit(solution)/shard_map/ppermute | solution.py:39
  16.3 20.8 %collective-permute-start.1 = (f32[4,256,128]{2,1,0:T(8,128)}, f32[4,256,128]{2,1,0:T(8,128)}, u32[]{:S(2)}, u32[]{:S(2)}) collective-permute-start(f32[4,256,128]{2,1,0:T(8,128)} %bitcast.4.refs_9_.refs_10_), channel_id=1, source_target_pairs={{0,12},{4,0},{8,4},{12,8},{1,13},{5,1},{9,5},{13,9},{2,14},{6,2},{... | collective-permute-start | bytes 1572872 | tf_op jit(solution)/shard_map/ppermute | solution.py:39
  20.2 13.2 %collective-permute-start.3 = (f32[256,128]{1,0:T(8,128)S(1)}, f32[256,128]{1,0:T(8,128)S(1)}, u32[]{:S(2)}, u32[]{:S(2)}) collective-permute-start(f32[256,128]{1,0:T(8,128)S(1)} %get-tuple-element.144), channel_id=1, source_target_pairs={{0,4},{4,8},{8,12},{12,0},{1,5},{5,9},{9,13},{13,1},{2,6},{6,10},{... | collective-permute-start | bytes 393224 | tf_op jit(solution)/shard_map/ppermute | solution.py:39
  20.2 16.8 %collective-permute-start.4 = (f32[256,128]{1,0:T(8,128)S(1)}, f32[256,128]{1,0:T(8,128)S(1)}, u32[]{:S(2)}, u32[]{:S(2)}) collective-permute-start(f32[256,128]{1,0:T(8,128)S(1)} %get-tuple-element.143), channel_id=1, source_target_pairs={{0,8},{4,12},{8,0},{12,4},{1,9},{5,13},{9,1},{13,5},{2,10},{6,14},... | collective-permute-start | bytes 393224 | tf_op jit(solution)/shard_map/ppermute | solution.py:39
  23.6 13.4 %collective-permute-start.5 = (f32[256,128]{1,0:T(8,128)S(1)}, f32[256,128]{1,0:T(8,128)S(1)}, u32[]{:S(2)}, u32[]{:S(2)}) collective-permute-start(f32[256,128]{1,0:T(8,128)S(1)} %get-tuple-element.142), channel_id=1, source_target_pairs={{0,12},{4,0},{8,4},{12,8},{1,13},{5,1},{9,5},{13,9},{2,14},{6,2},{... | collective-permute-start | bytes 393224 | tf_op jit(solution)/shard_map/ppermute | solution.py:39
  40.8 103.8 %all-gather.9.cloned.1.call-start = ((), (), s32[]{:S(2)}) async-start(), calls=%async_computation.2 | async-start | bytes 3932160 | tf_op jit(solution)/shard_map/all_gather | solution.py:431
  40.8 9.2 %collective-permute-start.16 = (f32[1,256,128]{2,1,0:T(8,128)S(1)}, f32[1,256,128]{2,1,0:T(8,128)S(1)}, u32[]{:S(2)}, u32[]{:S(2)}) collective-permute-start(f32[1,256,128]{2,1,0:T(8,128)S(1)} %bitcast.97), channel_id=1, source_target_pairs={{0,32},{32,0},{1,33},{33,1},{2,34},{34,2},{3,35},{35,3},{4,36},{36... | collective-permute-start | bytes 393224 | tf_op jit(solution)/shard_map/ppermute | solution.py:43
  42.4 45.9 %collective-permute-start.6 = (f32[4,512,128]{2,1,0:T(8,128)S(1)}, f32[4,512,128]{2,1,0:T(8,128)}, u32[]{:S(2)}, u32[]{:S(2)}) collective-permute-start(f32[4,512,128]{2,1,0:T(8,128)S(1)} %all-to-all-done.refs_4_.refs_5_), channel_id=1, source_target_pairs={{0,4},{4,8},{8,12},{12,0},{1,5},{5,9},{9,13},{13,1},{2,6},{6,10},{... | collective-permute-start | bytes 3145736 | tf_op jit(solution)/shard_map/ppermute | solution.py:39
  42.4 45.9 %collective-permute-start.7 = (f32[4,512,128]{2,1,0:T(8,128)S(1)}, f32[4,512,128]{2,1,0:T(8,128)}, u32[]{:S(2)}, u32[]{:S(2)}) collective-permute-start(f32[4,512,128]{2,1,0:T(8,128)S(1)} %all-to-all-done.refs_4_.refs_5_), channel_id=1, source_target_pairs={{0,12},{4,0},{8,4},{12,8},{1,13},{5,1},{9,5},{13,9},{2,14},{6,2},{... | collective-permute-start | bytes 3145736 | tf_op jit(solution)/shard_map/ppermute | solution.py:39
  45.6 6.4 %collective-permute-start.21 = (f32[16,2048]{1,0:T(8,128)S(1)}, f32[16,2048]{1,0:T(8,128)S(1)}, u32[]{:S(2)}, u32[]{:S(2)}) collective-permute-start(f32[16,2048]{1,0:T(8,128)S(1)} %copy-done), channel_id=1, source_target_pairs={{0,1},{1,2},{2,3},{3,0},{4,5},{5,6},{6,7},{7,4},{8,9},{9,10},{10,1... | collective-permute-start | bytes 393224 | tf_op jit(solution)/shard_map/ppermute | solution.py:39
  47.3 7.4 %collective-permute-start.22 = (f32[16,2048]{1,0:T(8,128)S(1)}, f32[16,2048]{1,0:T(8,128)S(1)}, u32[]{:S(2)}, u32[]{:S(2)}) collective-permute-start(f32[16,2048]{1,0:T(8,128)S(1)} %copy-done), channel_id=1, source_target_pairs={{0,2},{1,3},{2,0},{3,1},{4,6},{5,7},{6,4},{7,5},{8,10},{9,11},{10,... | collective-permute-start | bytes 393224 | tf_op jit(solution)/shard_map/ppermute | solution.py:39
  50.0 6.6 %collective-permute-start.23 = (f32[16,2048]{1,0:T(8,128)S(1)}, f32[16,2048]{1,0:T(8,128)S(1)}, u32[]{:S(2)}, u32[]{:S(2)}) collective-permute-start(f32[16,2048]{1,0:T(8,128)S(1)} %copy-done), channel_id=1, source_target_pairs={{0,3},{1,0},{2,1},{3,2},{4,7},{5,4},{6,5},{7,6},{8,11},{9,8},{10,9... | collective-permute-start | bytes 393224 | tf_op jit(solution)/shard_map/ppermute | solution.py:39
  52.0 11.2 %collective-permute-start.17 = (f32[2,256,128]{2,1,0:T(8,128)S(1)}, f32[2,256,128]{2,1,0:T(8,128)S(1)}, u32[]{:S(2)}, u32[]{:S(2)}) collective-permute-start(f32[2,256,128]{2,1,0:T(8,128)S(1)} %maximum_select_fusion.2), channel_id=1, source_target_pairs={{0,64},{64,0},{1,65},{65,1},{2,66},{66,2},{3,67},{67,3},{4,68},{68... | collective-permute-start | bytes 786440 | tf_op jit(solution)/shard_map/ppermute | solution.py:43
  56.6 5.5 %collective-permute-start.15 = (f32[256,128]{1,0:T(8,128)S(1)}, f32[256,128]{1,0:T(8,128)S(1)}, u32[]{:S(2)}, u32[]{:S(2)}) collective-permute-start(f32[256,128]{1,0:T(8,128)S(1)} %copy-done.10), channel_id=1, source_target_pairs={{0,32},{32,0},{1,33},{33,1},{2,34},{34,2},{3,35},{35,3},{4,36},{36... | collective-permute-start | bytes 393224 | tf_op jit(solution)/shard_map/ppermute | solution.py:43
  58.6 13.9 %collective-permute-start.8 = (f32[2,256,128]{2,1,0:T(8,128)S(1)}, f32[2,256,128]{2,1,0:T(8,128)}, u32[]{:S(2)}, u32[]{:S(2)}) collective-permute-start(f32[2,256,128]{2,1,0:T(8,128)S(1)} %slice.43), channel_id=1, source_target_pairs={{0,4},{4,8},{8,12},{12,0},{1,5},{5,9},{9,13},{13,1},{2,6},{6,10},{... | collective-permute-start | bytes 786440 | tf_op jit(solution)/shard_map/ppermute | solution.py:39
  62.1 10.4 %collective-permute-start.9 = (f32[2,256,128]{2,1,0:T(8,128)S(1)}, f32[2,256,128]{2,1,0:T(8,128)}, u32[]{:S(2)}, u32[]{:S(2)}) collective-permute-start(f32[2,256,128]{2,1,0:T(8,128)S(1)} %slice.44), channel_id=1, source_target_pairs={{0,12},{4,0},{8,4},{12,8},{1,13},{5,1},{9,5},{13,9},{2,14},{6,2},{... | collective-permute-start | bytes 786440 | tf_op jit(solution)/shard_map/ppermute | solution.py:39
  63.2 11.8 %collective-permute-start.11 = (f32[2,256,128]{2,1,0:T(8,128)S(1)}, f32[2,256,128]{2,1,0:T(8,128)S(1)}, u32[]{:S(2)}, u32[]{:S(2)}) collective-permute-start(f32[2,256,128]{2,1,0:T(8,128)S(1)} %maximum_select_fusion), channel_id=1, source_target_pairs={{0,32},{32,0},{1,33},{33,1},{2,34},{34,2},{3,35},{35,3},{4,36},{36... | collective-permute-start | bytes 786440 | tf_op jit(solution)/shard_map/ppermute | solution.py:43
  72.5 7.4 %collective-permute-start.18 = (f32[256,128]{1,0:T(8,128)}, f32[256,128]{1,0:T(8,128)S(1)}, u32[]{:S(2)}, u32[]{:S(2)}) collective-permute-start(f32[256,128]{1,0:T(8,128)} %get-tuple-element.148), channel_id=1, source_target_pairs={{0,4},{4,8},{8,12},{12,0},{1,5},{5,9},{9,13},{13,1},{2,6},{6,10},{... | collective-permute-start | bytes 393224 | tf_op jit(solution)/shard_map/ppermute | solution.py:39
  72.5 8.2 %collective-permute-start.19 = (f32[256,128]{1,0:T(8,128)}, f32[256,128]{1,0:T(8,128)S(1)}, u32[]{:S(2)}, u32[]{:S(2)}) collective-permute-start(f32[256,128]{1,0:T(8,128)} %get-tuple-element.147), channel_id=1, source_target_pairs={{0,8},{4,12},{8,0},{12,4},{1,9},{5,13},{9,1},{13,5},{2,10},{6,14},... | collective-permute-start | bytes 393224 | tf_op jit(solution)/shard_map/ppermute | solution.py:39
  74.9 7.3 %collective-permute-start.20 = (f32[256,128]{1,0:T(8,128)}, f32[256,128]{1,0:T(8,128)S(1)}, u32[]{:S(2)}, u32[]{:S(2)}) collective-permute-start(f32[256,128]{1,0:T(8,128)} %get-tuple-element.146), channel_id=1, source_target_pairs={{0,12},{4,0},{8,4},{12,8},{1,13},{5,1},{9,5},{13,9},{2,14},{6,2},{... | collective-permute-start | bytes 393224 | tf_op jit(solution)/shard_map/ppermute | solution.py:39
  79.9 7.6 %collective-permute-start.12 = (f32[256,128]{1,0:T(8,128)S(1)}, f32[256,128]{1,0:T(8,128)S(1)}, u32[]{:S(2)}, u32[]{:S(2)}) collective-permute-start(f32[256,128]{1,0:T(8,128)S(1)} %get-tuple-element.152), channel_id=1, source_target_pairs={{0,4},{4,8},{8,12},{12,0},{1,5},{5,9},{9,13},{13,1},{2,6},{6,10},{... | collective-permute-start | bytes 393224 | tf_op jit(solution)/shard_map/ppermute | solution.py:39
  80.6 6.8 %collective-permute-start.13 = (f32[256,128]{1,0:T(8,128)S(1)}, f32[256,128]{1,0:T(8,128)S(1)}, u32[]{:S(2)}, u32[]{:S(2)}) collective-permute-start(f32[256,128]{1,0:T(8,128)S(1)} %get-tuple-element.151), channel_id=1, source_target_pairs={{0,8},{4,12},{8,0},{12,4},{1,9},{5,13},{9,1},{13,5},{2,10},{6,14},... | collective-permute-start | bytes 393224 | tf_op jit(solution)/shard_map/ppermute | solution.py:39
  82.2 6.1 %collective-permute-start.14 = (f32[256,128]{1,0:T(8,128)S(1)}, f32[256,128]{1,0:T(8,128)S(1)}, u32[]{:S(2)}, u32[]{:S(2)}) collective-permute-start(f32[256,128]{1,0:T(8,128)S(1)} %get-tuple-element.150), channel_id=1, source_target_pairs={{0,12},{4,0},{8,4},{12,8},{1,13},{5,1},{9,5},{13,9},{2,14},{6,2},{... | collective-permute-start | bytes 393224 | tf_op jit(solution)/shard_map/ppermute | solution.py:39
  89.3 85.9 %all-gather.11.cloned.1.call-start = ((), (), s32[]{:S(2)}) async-start(), calls=%async_computation.3 | async-start | bytes 2621440 | tf_op jit(solution)/shard_map/all_gather | solution.py:431
  92.0 10.6 %collective-permute-start.24 = (f32[2,512,128]{2,1,0:T(8,128)S(1)}, f32[2,512,128]{2,1,0:T(8,128)S(1)}, u32[]{:S(2)}, u32[]{:S(2)}) collective-permute-start(f32[2,512,128]{2,1,0:T(8,128)S(1)} %slice.45), channel_id=1, source_target_pairs={{0,4},{4,8},{8,12},{12,0},{1,5},{5,9},{9,13},{13,1},{2,6},{6,10},{... | collective-permute-start | bytes 1572872 | tf_op jit(solution)/shard_map/ppermute | solution.py:39
  94.6 9.4 %collective-permute-start.25 = (f32[2,512,128]{2,1,0:T(8,128)S(1)}, f32[2,512,128]{2,1,0:T(8,128)}, u32[]{:S(2)}, u32[]{:S(2)}) collective-permute-start(f32[2,512,128]{2,1,0:T(8,128)S(1)} %slice.46), channel_id=1, source_target_pairs={{0,12},{4,0},{8,4},{12,8},{1,13},{5,1},{9,5},{13,9},{2,14},{6,2},{... | collective-permute-start | bytes 1572872 | tf_op jit(solution)/shard_map/ppermute | solution.py:39
  109.7 23.0 %collective-permute-start.34 = (f32[4,6,256,128]{3,2,1,0:T(8,128)}, f32[4,6,256,128]{3,2,1,0:T(8,128)S(1)}, u32[]{:S(2)}, u32[]{:S(2)}) collective-permute-start(f32[4,6,256,128]{3,2,1,0:T(8,128)} %bitcast.82), channel_id=1, source_target_pairs={{0,16},{16,0},{1,17},{17,1},{2,18},{18,2},{3,19},{19,3},{4,20},{20... | collective-permute-start | bytes 9437192 | tf_op jit(solution)/shard_map/ppermute | solution.py:43
  110.0 6.4 %collective-permute-start.27 = (f32[16,1024]{1,0:T(8,128)S(1)}, f32[16,1024]{1,0:T(8,128)S(1)}, u32[]{:S(2)}, u32[]{:S(2)}) collective-permute-start(f32[16,1024]{1,0:T(8,128)S(1)} %get-tuple-element.93), channel_id=1, source_target_pairs={{0,3},{1,0},{2,1},{3,2},{4,7},{5,4},{6,5},{7,6},{8,11},{9,8},{10,9... | collective-permute-start | bytes 196616 | tf_op jit(solution)/shard_map/ppermute | solution.py:39
  112.2 7.8 %collective-permute-start.28 = (f32[16,1024]{1,0:T(8,128)S(1)}, f32[16,1024]{1,0:T(8,128)S(1)}, u32[]{:S(2)}, u32[]{:S(2)}) collective-permute-start(f32[16,1024]{1,0:T(8,128)S(1)} %get-tuple-element.94), channel_id=1, source_target_pairs={{0,2},{1,3},{2,0},{3,1},{4,6},{5,7},{6,4},{7,5},{8,10},{9,11},{10,... | collective-permute-start | bytes 196616 | tf_op jit(solution)/shard_map/ppermute | solution.py:39
  113.2 8.1 %collective-permute-start.29 = (f32[16,1024]{1,0:T(8,128)S(1)}, f32[16,1024]{1,0:T(8,128)S(1)}, u32[]{:S(2)}, u32[]{:S(2)}) collective-permute-start(f32[16,1024]{1,0:T(8,128)S(1)} %get-tuple-element.95), channel_id=1, source_target_pairs={{0,1},{1,2},{2,3},{3,0},{4,5},{5,6},{6,7},{7,4},{8,9},{9,10},{10,1... | collective-permute-start | bytes 196616 | tf_op jit(solution)/shard_map/ppermute | solution.py:39
  123.3 6.8 %collective-permute-start.31 = (f32[8,2048]{1,0:T(8,128)S(1)}, f32[8,2048]{1,0:T(8,128)S(1)}, u32[]{:S(2)}, u32[]{:S(2)}) collective-permute-start(f32[8,2048]{1,0:T(8,128)S(1)} %get-tuple-element.98.refs_0_), channel_id=1, source_target_pairs={{0,4},{4,8},{8,12},{12,0},{1,5},{5,9},{9,13},{13,1},{2,6},{6,10},{... | collective-permute-start | bytes 196616 | tf_op jit(solution)/shard_map/ppermute | solution.py:39
  124.9 7.1 %collective-permute-start.32 = (f32[8,2048]{1,0:T(8,128)S(1)}, f32[8,2048]{1,0:T(8,128)S(1)}, u32[]{:S(2)}, u32[]{:S(2)}) collective-permute-start(f32[8,2048]{1,0:T(8,128)S(1)} %get-tuple-element.98.refs_0_), channel_id=1, source_target_pairs={{0,8},{4,12},{8,0},{12,4},{1,9},{5,13},{9,1},{13,5},{2,10},{6,14},... | collective-permute-start | bytes 196616 | tf_op jit(solution)/shard_map/ppermute | solution.py:39
  129.6 10.4 %collective-permute-start.36 = (f32[2,4,2048]{2,1,0:T(4,128)S(1)}, f32[2,4,2048]{2,1,0:T(4,128)S(1)}, u32[]{:S(2)}, u32[]{:S(2)}) collective-permute-start(f32[2,4,2048]{2,1,0:T(4,128)S(1)} %get-tuple-element.108), channel_id=1, source_target_pairs={{0,32},{32,0},{1,33},{33,1},{2,34},{34,2},{3,35},{35,3},{4,36},{36... | collective-permute-start | bytes 196616 | tf_op jit(solution)/shard_map/ppermute | solution.py:43
  139.4 4.3 %collective-permute-start.35 = (f32[16,1024]{1,0:T(8,128)S(1)}, f32[16,1024]{1,0:T(8,128)S(1)}, u32[]{:S(2)}, u32[]{:S(2)}) collective-permute-start(f32[16,1024]{1,0:T(8,128)S(1)} %get-tuple-element.106), channel_id=1, source_target_pairs={{0,32},{32,0},{1,33},{33,1},{2,34},{34,2},{3,35},{35,3},{4,36},{36... | collective-permute-start | bytes 196616 | tf_op jit(solution)/shard_map/ppermute | solution.py:43
  144.5 11.6 %collective-permute-start.40 = (f32[4,6,256,128]{3,2,1,0:T(8,128)}, f32[4,6,256,128]{3,2,1,0:T(8,128)}, u32[]{:S(2)}, u32[]{:S(2)}) collective-permute-start(f32[4,6,256,128]{3,2,1,0:T(8,128)} %bitcast.85), channel_id=1, source_target_pairs={{0,16},{16,0},{1,17},{17,1},{2,18},{18,2},{3,19},{19,3},{4,20},{20... | collective-permute-start | bytes 9437192 | tf_op jit(solution)/shard_map/ppermute | solution.py:43
  145.5 7.2 %collective-permute-start.37 = (f32[16,2048]{1,0:T(8,128)S(1)}, f32[16,2048]{1,0:T(8,128)S(1)}, u32[]{:S(2)}, u32[]{:S(2)}) collective-permute-start(f32[16,2048]{1,0:T(8,128)S(1)} %get-tuple-element.109.refs_0_), channel_id=1, source_target_pairs={{0,4},{4,8},{8,12},{12,0},{1,5},{5,9},{9,13},{13,1},{2,6},{6,10},{... | collective-permute-start | bytes 393224 | tf_op jit(solution)/shard_map/ppermute | solution.py:39
  146.1 10.0 %collective-permute-start.38 = (f32[16,2048]{1,0:T(8,128)S(1)}, f32[16,2048]{1,0:T(8,128)S(1)}, u32[]{:S(2)}, u32[]{:S(2)}) collective-permute-start(f32[16,2048]{1,0:T(8,128)S(1)} %get-tuple-element.109.refs_0_), channel_id=1, source_target_pairs={{0,8},{4,12},{8,0},{12,4},{1,9},{5,13},{9,1},{13,5},{2,10},{6,14},... | collective-permute-start | bytes 393224 | tf_op jit(solution)/shard_map/ppermute | solution.py:39
  149.3 6.7 %collective-permute-start.39 = (f32[16,2048]{1,0:T(8,128)S(1)}, f32[16,2048]{1,0:T(8,128)S(1)}, u32[]{:S(2)}, u32[]{:S(2)}) collective-permute-start(f32[16,2048]{1,0:T(8,128)S(1)} %get-tuple-element.109.refs_0_), channel_id=1, source_target_pairs={{0,12},{4,0},{8,4},{12,8},{1,13},{5,1},{9,5},{13,9},{2,14},{6,2},{... | collective-permute-start | bytes 393224 | tf_op jit(solution)/shard_map/ppermute | solution.py:39
  149.8 13.9 %collective-permute-start.42 = (f32[8,2048]{1,0:T(8,128)S(1)}, f32[8,2048]{1,0:T(8,128)S(1)}, u32[]{:S(2)}, u32[]{:S(2)}) collective-permute-start(f32[8,2048]{1,0:T(8,128)S(1)} %get-tuple-element.119), channel_id=1, source_target_pairs={{0,64},{64,0},{1,65},{65,1},{2,66},{66,2},{3,67},{67,3},{4,68},{68... | collective-permute-start | bytes 196616 | tf_op jit(solution)/shard_map/ppermute | solution.py:43
  160.8 5.5 %collective-permute-start.41 = (f32[8,1024]{1,0:T(8,128)S(1)}, f32[8,1024]{1,0:T(8,128)S(1)}, u32[]{:S(2)}, u32[]{:S(2)}) collective-permute-start(f32[8,1024]{1,0:T(8,128)S(1)} %get-tuple-element.117), channel_id=1, source_target_pairs={{0,64},{64,0},{1,65},{65,1},{2,66},{66,2},{3,67},{67,3},{4,68},{68... | collective-permute-start | bytes 98312 | tf_op jit(solution)/shard_map/ppermute | solution.py:43
  175.2 8.7 %collective-permute-start.46 = (f32[4,4,256,128]{3,2,1,0:T(8,128)}, f32[4,4,256,128]{3,2,1,0:T(8,128)S(1)}, u32[]{:S(2)}, u32[]{:S(2)}) collective-permute-start(f32[4,4,256,128]{3,2,1,0:T(8,128)} %bitcast.88), channel_id=1, source_target_pairs={{0,16},{16,0},{1,17},{17,1},{2,18},{18,2},{3,19},{19,3},{4,20},{20... | collective-permute-start | bytes 6291464 | tf_op jit(solution)/shard_map/ppermute | solution.py:43
  175.2 5.8 %collective-permute-start.43 = (f32[8,2048]{1,0:T(8,128)S(1)}, f32[8,2048]{1,0:T(8,128)S(1)}, u32[]{:S(2)}, u32[]{:S(2)}) collective-permute-start(f32[8,2048]{1,0:T(8,128)S(1)} %s23.1.c0), channel_id=1, source_target_pairs={{0,4},{4,8},{8,12},{12,0},{1,5},{5,9},{9,13},{13,1},{2,6},{6,10},{... | collective-permute-start | bytes 196616 | tf_op jit(solution)/shard_map/ppermute | solution.py:39
  176.7 6.7 %collective-permute-start.44 = (f32[8,2048]{1,0:T(8,128)S(1)}, f32[8,2048]{1,0:T(8,128)S(1)}, u32[]{:S(2)}, u32[]{:S(2)}) collective-permute-start(f32[8,2048]{1,0:T(8,128)S(1)} %s23.1.c0), channel_id=1, source_target_pairs={{0,8},{4,12},{8,0},{12,4},{1,9},{5,13},{9,1},{13,5},{2,10},{6,14},... | collective-permute-start | bytes 196616 | tf_op jit(solution)/shard_map/ppermute | solution.py:39
  189.8 5.6 %collective-permute-start.47 = (f32[8,2048]{1,0:T(8,128)S(1)}, f32[8,2048]{1,0:T(8,128)S(1)}, u32[]{:S(2)}, u32[]{:S(2)}) collective-permute-start(f32[8,2048]{1,0:T(8,128)S(1)} %top.1.c0), channel_id=1, source_target_pairs={{0,4},{4,8},{8,12},{12,0},{1,5},{5,9},{9,13},{13,1},{2,6},{6,10},{... | collective-permute-start | bytes 196616 | tf_op jit(solution)/shard_map/ppermute | solution.py:39
  190.8 6.1 %collective-permute-start.48 = (f32[8,2048]{1,0:T(8,128)S(1)}, f32[8,2048]{1,0:T(8,128)S(1)}, u32[]{:S(2)}, u32[]{:S(2)}) collective-permute-start(f32[8,2048]{1,0:T(8,128)S(1)} %top.1.c0), channel_id=1, source_target_pairs={{0,8},{4,12},{8,0},{12,4},{1,9},{5,13},{9,1},{13,5},{2,10},{6,14},... | collective-permute-start | bytes 196616 | tf_op jit(solution)/shard_map/ppermute | solution.py:39
  198.9 5.5 %collective-permute-start.50 = (f32[8,1024]{1,0:T(8,128)S(1)}, f32[8,1024]{1,0:T(8,128)S(1)}, u32[]{:S(2)}, u32[]{:S(2)}) collective-permute-start(f32[8,1024]{1,0:T(8,128)S(1)} %get-tuple-element.126), channel_id=1, source_target_pairs={{0,64},{64,0},{1,65},{65,1},{2,66},{66,2},{3,67},{67,3},{4,68},{68... | collective-permute-start | bytes 98312 | tf_op jit(solution)/shard_map/ppermute | solution.py:43
  209.1 10.3 %collective-permute-start.51 = (f32[16,2048]{1,0:T(8,128)S(1)}, f32[16,2048]{1,0:T(8,128)S(1)}, u32[]{:S(2)}, u32[]{:S(2)}) collective-permute-start(f32[16,2048]{1,0:T(8,128)S(1)} %b2.1.c0), channel_id=1, source_target_pairs={{0,4},{4,8},{8,12},{12,0},{1,5},{5,9},{9,13},{13,1},{2,6},{6,10},{... | collective-permute-start | bytes 393224 | tf_op jit(solution)/shard_map/ppermute | solution.py:39
  209.5 10.0 %collective-permute-start.52 = (f32[16,2048]{1,0:T(8,128)S(1)}, f32[16,2048]{1,0:T(8,128)S(1)}, u32[]{:S(2)}, u32[]{:S(2)}) collective-permute-start(f32[16,2048]{1,0:T(8,128)S(1)} %b2.1.c0), channel_id=1, source_target_pairs={{0,8},{4,12},{8,0},{12,4},{1,9},{5,13},{9,1},{13,5},{2,10},{6,14},... | collective-permute-start | bytes 393224 | tf_op jit(solution)/shard_map/ppermute | solution.py:39
  212.6 6.8 %collective-permute-start.53 = (f32[16,2048]{1,0:T(8,128)S(1)}, f32[16,2048]{1,0:T(8,128)S(1)}, u32[]{:S(2)}, u32[]{:S(2)}) collective-permute-start(f32[16,2048]{1,0:T(8,128)S(1)} %b2.1.c0), channel_id=1, source_target_pairs={{0,12},{4,0},{8,4},{12,8},{1,13},{5,1},{9,5},{13,9},{2,14},{6,2},{... | collective-permute-start | bytes 393224 | tf_op jit(solution)/shard_map/ppermute | solution.py:39
  213.3 6.1 %collective-permute-start.54 = (f32[8,2048]{1,0:T(8,128)S(1)}, f32[8,2048]{1,0:T(8,128)S(1)}, u32[]{:S(2)}, u32[]{:S(2)}) collective-permute-start(f32[8,2048]{1,0:T(8,128)S(1)} %get-tuple-element.125.x3), channel_id=1, source_target_pairs={{0,64},{64,0},{1,65},{65,1},{2,66},{66,2},{3,67},{67,3},{4,68},{68... | collective-permute-start | bytes 196616 | tf_op jit(solution)/shard_map/ppermute | solution.py:43
  220.1 4.3 %collective-permute-start.55 = (f32[16,1024]{1,0:T(8,128)S(1)}, f32[16,1024]{1,0:T(8,128)S(1)}, u32[]{:S(2)}, u32[]{:S(2)}) collective-permute-start(f32[16,1024]{1,0:T(8,128)S(1)} %get-tuple-element.129), channel_id=1, source_target_pairs={{0,32},{32,0},{1,33},{33,1},{2,34},{34,2},{3,35},{35,3},{4,36},{36... | collective-permute-start | bytes 196616 | tf_op jit(solution)/shard_map/ppermute | solution.py:43
  221.8 11.1 %collective-permute-start.59 = (f32[2,4,2048]{2,1,0:T(4,128)S(1)}, f32[2,4,2048]{2,1,0:T(4,128)S(1)}, u32[]{:S(2)}, u32[]{:S(2)}) collective-permute-start(f32[2,4,2048]{2,1,0:T(4,128)S(1)} %slice.51.a_mine), channel_id=1, source_target_pairs={{0,32},{32,0},{1,33},{33,1},{2,34},{34,2},{3,35},{35,3},{4,36},{36... | collective-permute-start | bytes 196616 | tf_op jit(solution)/shard_map/ppermute | solution.py:43
  230.2 5.8 %collective-permute-start.57 = (f32[8,2048]{1,0:T(8,128)S(1)}, f32[8,2048]{1,0:T(8,128)S(1)}, u32[]{:S(2)}, u32[]{:S(2)}) collective-permute-start(f32[8,2048]{1,0:T(8,128)S(1)} %get-tuple-element.133), channel_id=1, source_target_pairs={{0,8},{4,12},{8,0},{12,4},{1,9},{5,13},{9,1},{13,5},{2,10},{6,14},... | collective-permute-start | bytes 196616 | tf_op jit(solution)/shard_map/ppermute | solution.py:39
  232.4 5.5 %collective-permute-start.58 = (f32[8,2048]{1,0:T(8,128)S(1)}, f32[8,2048]{1,0:T(8,128)S(1)}, u32[]{:S(2)}, u32[]{:S(2)}) collective-permute-start(f32[8,2048]{1,0:T(8,128)S(1)} %get-tuple-element.134), channel_id=1, source_target_pairs={{0,4},{4,8},{8,12},{12,0},{1,5},{5,9},{9,13},{13,1},{2,6},{6,10},{... | collective-permute-start | bytes 196616 | tf_op jit(solution)/shard_map/ppermute | solution.py:39
  238.7 17.7 %collective-permute-start.68 = (f32[8,512]{1,0:T(8,128)S(1)}, f32[8,512]{1,0:T(8,128)S(1)}, u32[]{:S(2)}, u32[]{:S(2)}) collective-permute-start(f32[8,512]{1,0:T(8,128)S(1)} %get-tuple-element.164), channel_id=1, source_target_pairs={{0,16},{16,0},{1,17},{17,1},{2,18},{18,2},{3,19},{19,3},{4,20},{20... | collective-permute-start | bytes 49160 | tf_op jit(solution)/shard_map/ppermute | solution.py:43
  239.3 17.7 %collective-permute-start.67 = (f32[8,1024]{1,0:T(8,128)S(1)}, f32[8,1024]{1,0:T(8,128)S(1)}, u32[]{:S(2)}, u32[]{:S(2)}) collective-permute-start(f32[8,1024]{1,0:T(8,128)S(1)} %get-tuple-element.166), channel_id=1, source_target_pairs={{0,16},{16,0},{1,17},{17,1},{2,18},{18,2},{3,19},{19,3},{4,20},{20... | collective-permute-start | bytes 98312 | tf_op jit(solution)/shard_map/ppermute | solution.py:43
  240.4 6.8 %collective-permute-start.61 = (f32[16,1024]{1,0:T(8,128)S(1)}, f32[16,1024]{1,0:T(8,128)S(1)}, u32[]{:S(2)}, u32[]{:S(2)}) collective-permute-start(f32[16,1024]{1,0:T(8,128)S(1)} %maximum_select_fusion.3.refs_0_), channel_id=1, source_target_pairs={{0,1},{1,2},{2,3},{3,0},{4,5},{5,6},{6,7},{7,4},{8,9},{9,10},{10,1... | collective-permute-start | bytes 196616 | tf_op jit(solution)/shard_map/ppermute | solution.py:39
  241.0 6.2 %collective-permute-start.62 = (f32[16,1024]{1,0:T(8,128)S(1)}, f32[16,1024]{1,0:T(8,128)S(1)}, u32[]{:S(2)}, u32[]{:S(2)}) collective-permute-start(f32[16,1024]{1,0:T(8,128)S(1)} %maximum_select_fusion.3.refs_0_), channel_id=1, source_target_pairs={{0,2},{1,3},{2,0},{3,1},{4,6},{5,7},{6,4},{7,5},{8,10},{9,11},{10,... | collective-permute-start | bytes 196616 | tf_op jit(solution)/shard_map/ppermute | solution.py:39
  242.8 5.0 %collective-permute-start.63 = (f32[16,1024]{1,0:T(8,128)S(1)}, f32[16,1024]{1,0:T(8,128)S(1)}, u32[]{:S(2)}, u32[]{:S(2)}) collective-permute-start(f32[16,1024]{1,0:T(8,128)S(1)} %maximum_select_fusion.3.refs_0_), channel_id=1, source_target_pairs={{0,3},{1,0},{2,1},{3,2},{4,7},{5,4},{6,5},{7,6},{8,11},{9,8},{10,9... | collective-permute-start | bytes 196616 | tf_op jit(solution)/shard_map/ppermute | solution.py:39
  252.7 7.5 %collective-permute-start.64 = (f32[16,2048]{1,0:T(8,128)S(1)}, f32[16,2048]{1,0:T(8,128)S(1)}, u32[]{:S(2)}, u32[]{:S(2)}) collective-permute-start(f32[16,2048]{1,0:T(8,128)S(1)} %get-tuple-element.138), channel_id=1, source_target_pairs={{0,3},{1,0},{2,1},{3,2},{4,7},{5,4},{6,5},{7,6},{8,11},{9,8},{10,9... | collective-permute-start | bytes 393224 | tf_op jit(solution)/shard_map/ppermute | solution.py:39
  255.5 7.1 %collective-permute-start.65 = (f32[16,2048]{1,0:T(8,128)S(1)}, f32[16,2048]{1,0:T(8,128)S(1)}, u32[]{:S(2)}, u32[]{:S(2)}) collective-permute-start(f32[16,2048]{1,0:T(8,128)S(1)} %get-tuple-element.139), channel_id=1, source_target_pairs={{0,2},{1,3},{2,0},{3,1},{4,6},{5,7},{6,4},{7,5},{8,10},{9,11},{10,... | collective-permute-start | bytes 393224 | tf_op jit(solution)/shard_map/ppermute | solution.py:39
  256.0 7.9 %collective-permute-start.66 = (f32[16,2048]{1,0:T(8,128)S(1)}, f32[16,2048]{1,0:T(8,128)S(1)}, u32[]{:S(2)}, u32[]{:S(2)}) collective-permute-start(f32[16,2048]{1,0:T(8,128)S(1)} %get-tuple-element.140), channel_id=1, source_target_pairs={{0,1},{1,2},{2,3},{3,0},{4,5},{5,6},{6,7},{7,4},{8,9},{9,10},{10,1... | collective-permute-start | bytes 393224 | tf_op jit(solution)/shard_map/ppermute | solution.py:39
  (26 other events, 303.9 us)
Sparse Core Ops, SparseCore 0:
  40.9 39.7 all-gather.6
  89.4 43.7 all-gather.8
  145.6 29.5 all-gather.10

commit v6 on v5

--- a/solution.py
+++ b/solution.py
@@ -44,11 +44,13 @@
 
 
 def gather4(v, axis):
-    return [v] + [shift(v, axis, s) for s in (1, 2, 3)]
+    far = shift(v, axis, 2)
+    return [v, shift(v, axis, 1), far, shift(v, axis, 3)]
 
 
 def scatter4(parts, axis):
-    return [parts[0]] + [shift(parts[s], axis, -s) for s in (1, 2, 3)]
+    far = shift(parts[2], axis, 2)
+    return [parts[0], shift(parts[1], axis, -1), far, shift(parts[3], axis, 1)]
 
 
 def ring(v, axis, dim):
@@ -424,6 +426,9 @@
         for s in range(4):
             z = (zi + s) % 4
             blocks.append(jnp.where(z // 2 == bit, pick(pair, z % 2), pick(other, z % 2)))
+        return blocks
+
+    def over_z(blocks):
         return [blocks[0]] + [shift(blocks[s], "z", s) for s in (1, 2, 3)]
 
     def gathered(blocks, f):
@@ -432,30 +437,37 @@
 
     gate = lax.optimization_barrier
     e0 = jnp.swapaxes(dinv0.reshape(4, 4, B, B), 0, 1).reshape(4, 512, B)
-    e0, dinv1, off0 = gate((e0, dinv1, off0.reshape(4, 256, B)))
+    e1 = dinv1.reshape(2, 2, 256, B)
+    e1_mine, e1_other = pick(e1, ci, 1), flip(pick(e1, 1 - ci, 1), "core")
+    e0, e1_mine, e1_other = gate((e0, e1_mine, e1_other))
     e0 = lax.all_to_all(e0, "y", 0, 0, tiled=True)
+    e1 = for_z(e1_mine, e1_other, ci)
+    e1, off0 = gate((e1, off0.reshape(4, 256, B)))
+    e1 = over_z(e1)
     fa, fb = shift(off0, "z", 1), shift(off0, "z", -1)
-    e1 = dinv1.reshape(2, 2, 256, B)
-    e1 = for_z(pick(e1, ci, 1), flip(pick(e1, 1 - ci, 1), "core"), ci)
-    e0, fa, fb, e1, dinv2, off2, dinv3 = gate((e0, fa, fb, e1, dinv2, off2, dinv3))
+    e0, fa, fb, e1, dinv2, off2, dinv3, rhs0 = gate((e0, fa, fb, e1, dinv2, off2, dinv3, rhs0))
     m1 = gathered(e1, off1)
 
     ea, eb = shift(e0, "z", 1), shift(e0, "z", -1)
-    fc, fd = shift(fa[:2], "z", 1), shift(fb[2:], "z", -1)
     e2 = dinv2.reshape(2, 256, B)
     e2 = ordered(pick(e2, ci)[None], flip(pick(e2, 1 - ci)[None], "core"), ci, 0)
-    e2 = for_z(e2, flip(e2, "x0"), x0)
+    e2 = over_z(for_z(e2, flip(e2, "x0"), x0))
     f2 = joined(off2, 1)
+    fc, fd = shift(fa[:2], "z", 1), shift(fb[2:], "z", -1)
+    c0 = gather4(rhs0, "y")
+    e2[0], ea, eb, fc, fd, c0 = gate((e2[0], ea, eb, fc, fd, c0))
+    ec, ed = shift(ea[:2], "z", 1), shift(eb[2:], "z", -1)
     e3 = joined(dinv3[None], 1)
-    e3 = for_z(e3, flip(e3, "x1"), x1)
-    c0 = gather4(rhs0, "y")
-    ea, eb, fc, fd, e2, f2, e3, c0 = gate((ea, eb, fc, fd, e2, f2, e3, c0))
-    ec, ed = shift(ea[:2], "z", 1), shift(eb[2:], "z", -1)
+    e3_other = flip(e3, "x1")
     b_mine, b_other = halves(jnp.concatenate([rhs1, rhs2, rhs3], 1), ci)
     b_other = flip(b_other, "core")
-    ec, ed, b_mine, b_other = gate((ec, ed, b_mine, b_other))
+    ec, ed, e2, f2, e3, e3_other, b_mine, b_other = gate(
+        (ec, ed, e2, f2, e3, e3_other, b_mine, b_other)
+    )
+    m2 = gathered(e2, f2)
     w0 = [e0, ea, eb, ec, ed, off0, fa, fb, fc, fd]
-    m2 = gathered(e2, f2)
+    e3 = over_z(for_z(e3, e3_other, x1))
+    e3, b_mine = gate((e3, b_mine))
     m3 = gathered(e3, None)
 
     dma = pltpu.SemaphoreType.DMA

time: 272 us -> 267 us (0.982)
  waiting for transfers between devices: 98.2 us -> 93.3 us
  starting transfers between devices: 98.2 us -> 101 us
    ppermute x47, starting transfers between devices: 70.6 us -> 75.6 us  [shift(): return lax.ppermute(v, axis, [(i, (i + s) % 4) for i in range(4)])]
    unnamed x43 -> x45, local copies, waits for them, and re-layouts: 10 us -> 6.95 us
  transfers between devices with their start and end apart: 74 -> 74, of which waited for: 41 -> 37; matrix products, arithmetic and copies ran while one was open for 4% -> 4% of each run, Pallas kernels for 10% -> 10%
where the time goes in v6:
time: 267 us; the launch traced here: 266 us
  starting transfers between devices  101 us (38%)
  waiting for transfers between devices  93.3 us (35%)
  Pallas kernels  38.5 us (14%)
  local copies, waits for them, and re-layouts  14.7 us (6%)
  between operations  14.4 us (5%)
  other arithmetic  3.77 us (1%)
    ppermute x47, starting transfers between devices, shift(): return lax.ppermute(v, axis, [(i, (i + s) % 4) for i in range(4)])  75.6 us
    ppermute x47, waiting for transfers between devices, shift(): return lax.ppermute(v, axis, [(i, (i + s) % 4) for i in range(4)])  68 us
    pallas_call x13, Pallas kernels, call(): pl.pallas_call(kernel, out_shape=[jax.ShapeDtypeStruct(s, f32) for s in s...  38.5 us
    ppermute x23, starting transfers between devices, flip(): return lax.ppermute(v, axis, [(0, 1), (1, 0)])  20.6 us
    ppermute x23, waiting for transfers between devices, flip(): return lax.ppermute(v, axis, [(0, 1), (1, 0)])  18.2 us
    all_gather x3, waiting for transfers between devices, gathered(): return lax.all_gather(jnp.concatenate(parts, 0), 'y', axis=0, tiled=False)  7.04 us
    unnamed x45, local copies, waits for them, and re-layouts  6.95 us
  transfers between devices with their start and end apart: 74, of which 37 were waited for; matrix products, arithmetic and copies ran while one was open for 4% of the time, Pallas kernels for 10%

profile of v6, /device:TPU:0, one launch (start us, length us, event | category | flops | bytes accessed | tf_op | source)
XLA Modules:
  0.0 265.6 jit_solution(7283412520386170619)
XLA Ops:
  8.4 2.4 copy.22
  10.7 4.7 %all-to-all-start = ((f32[4,512,128]{2,1,0:T(8,128)}), f32[4,512,128]{2,1,0:T(8,128)S(1)}, u32[]{:S(2)}, u32[]{:S(2)}) async-start(f32[4,512,128]{2,1,0:T(8,128)} %bitcast.3), calls=%async_computation | async-start | bytes 2097152 | tf_op jit(solution)/shard_map/all_to_all | solution.py:443
  15.5 2.0 collective-permute-start.1
  17.5 2.2 collective-permute-start.2
  19.7 3.4 %collective-permute-start.4 = (f32[256,128]{1,0:T(8,128)S(1)}, f32[256,128]{1,0:T(8,128)S(1)}, u32[]{:S(2)}, u32[]{:S(2)}) collective-permute-start(f32[256,128]{1,0:T(8,128)S(1)} %get-tuple-element.89), channel_id=1, source_target_pairs={{0,8},{4,12},{8,0},{12,4},{1,9},{5,13},{9,1},{13,5},{2,10},{6,14},... | collective-permute-start | bytes 393224 | tf_op jit(solution)/shard_map/ppermute | solution.py:39
  24.1 10.6 %collective-permute-done.3 = f32[256,128]{1,0:T(8,128)S(1)} collective-permute-done((f32[256,128]{1,0:T(8,128)S(1)}, f32[256,128]{1,0:T(8,128)S(1)}, u32[]{:S(2)}, u32[]{:S(2)}) %collective-permute-start.3) | collective-permute-done | bytes 131104 | tf_op jit(solution)/shard_map/ppermute | solution.py:39
  34.7 4.0 %collective-permute-done.4 = f32[256,128]{1,0:T(8,128)S(1)} collective-permute-done((f32[256,128]{1,0:T(8,128)S(1)}, f32[256,128]{1,0:T(8,128)S(1)}, u32[]{:S(2)}, u32[]{:S(2)}) %collective-permute-start.4) | collective-permute-done | bytes 131104 | tf_op jit(solution)/shard_map/ppermute | solution.py:39
  41.9 3.2 %collective-permute-start.9 = (f32[4,512,128]{2,1,0:T(8,128)S(1)}, f32[4,512,128]{2,1,0:T(8,128)}, u32[]{:S(2)}, u32[]{:S(2)}) collective-permute-start(f32[4,512,128]{2,1,0:T(8,128)S(1)} %all-to-all-done.refs_4_.refs_5_), channel_id=1, source_target_pairs={{0,12},{4,0},{8,4},{12,8},{1,13},{5,1},{9,5},{13,9},{2,14},{6,2},{... | collective-permute-start | bytes 3145736 | tf_op jit(solution)/shard_map/ppermute | solution.py:39
  45.2 1.8 collective-permute-start.12
  47.0 2.7 %collective-permute-start.13 = (f32[16,2048]{1,0:T(8,128)S(1)}, f32[16,2048]{1,0:T(8,128)S(1)}, u32[]{:S(2)}, u32[]{:S(2)}) collective-permute-start(f32[16,2048]{1,0:T(8,128)S(1)} %copy-done), channel_id=1, source_target_pairs={{0,2},{1,3},{2,0},{3,1},{4,6},{5,7},{6,4},{7,5},{8,10},{9,11},{10,... | collective-permute-start | bytes 393224 | tf_op jit(solution)/shard_map/ppermute | solution.py:39
  49.6 1.5 collective-permute-start.21
  52.3 1.5 collective-permute-start.7
  57.4 3.2 %collective-permute-start.11 = (f32[2,256,128]{2,1,0:T(8,128)S(1)}, f32[2,256,128]{2,1,0:T(8,128)}, u32[]{:S(2)}, u32[]{:S(2)}) collective-permute-start(f32[2,256,128]{2,1,0:T(8,128)S(1)} %slice.44), channel_id=1, source_target_pairs={{0,12},{4,0},{8,4},{12,8},{1,13},{5,1},{9,5},{13,9},{2,14},{6,2},{... | collective-permute-start | bytes 786440 | tf_op jit(solution)/shard_map/ppermute | solution.py:39
  60.6 2.3 collective-permute-start.14
  63.1 6.2 %collective-permute-done.14.refs_3_ = f32[16,2048]{1,0:T(8,128)S(1)} collective-permute-done((f32[16,2048]{1,0:T(8,128)S(1)}, f32[16,2048]{1,0:T(8,128)S(1)}, u32[]{:S(2)}, u32[]{:S(2)}) %collective-permute-start.14) | collective-permute-done | bytes 131104 | tf_op jit(solution)/shard_map/ppermute | solution.py:39
  69.2 1.4 collective-permute-start.20
  70.6 2.5 collective-permute-done.10.refs_12_.refs_13_
  73.2 3.0 %collective-permute-start.22 = (f32[2,256,128]{2,1,0:T(8,128)S(1)}, f32[2,256,128]{2,1,0:T(8,128)S(1)}, u32[]{:S(2)}, u32[]{:S(2)}) collective-permute-start(f32[2,256,128]{2,1,0:T(8,128)S(1)} %maximum_select_fusion.2), channel_id=1, source_target_pairs={{0,64},{64,0},{1,65},{65,1},{2,66},{66,2},{3,67},{67,3},{4,68},{68... | collective-permute-start | bytes 786440 | tf_op jit(solution)/shard_map/ppermute | solution.py:43
  78.4 3.3 %collective-permute-start.16 = (f32[2,512,128]{2,1,0:T(8,128)S(1)}, f32[2,512,128]{2,1,0:T(8,128)S(1)}, u32[]{:S(2)}, u32[]{:S(2)}) collective-permute-start(f32[2,512,128]{2,1,0:T(8,128)S(1)} %slice.46), channel_id=1, source_target_pairs={{0,12},{4,0},{8,4},{12,8},{1,13},{5,1},{9,5},{13,9},{2,14},{6,2},{... | collective-permute-start | bytes 1572872 | tf_op jit(solution)/shard_map/ppermute | solution.py:39
  83.1 1.5 collective-permute-start.18
  84.6 1.8 collective-permute-start.19
  86.4 9.7 %collective-permute-done.17 = f32[256,128]{1,0:T(8,128)S(1)} collective-permute-done((f32[256,128]{1,0:T(8,128)S(1)}, f32[256,128]{1,0:T(8,128)S(1)}, u32[]{:S(2)}, u32[]{:S(2)}) %collective-permute-start.17) | collective-permute-done | bytes 131104 | tf_op jit(solution)/shard_map/ppermute | solution.py:39
  98.1 5.7 %f0.1 = (f32[64,512]{1,0:T(8,128)S(1)}, f32[16,1024]{1,0:T(8,128)S(1)}, f32[16,1024]{1,0:T(8,128)S(1)}, f32[16,1024]{1,0:T(8,128)S(1)}, f32[16,1024]{1,0:T(8,128)S(1)}) custom-call(s32[128]{0:T(128)S(1)} %pad_add_fusion.meta, f32[16,2048]{1,0:T(8,128)S(1)} %copy-done, f32[16,2048]{1,0:T(8,128)S(1)} %collective-permute-done.12.refs_1_, ...), custom_call_target="tpu_custom_call" | custom-call | flops 2415919104 | bytes 6815744 | tf_op jit(solution)/shard_map/f0/pallas_call | solution.py:395
  104.0 2.4 collective-permute-start.24
  108.4 1.8 collective-permute-done.24
  110.2 3.1 %collective-permute-start.29 = (f32[256,128]{1,0:T(8,128)S(1)}, f32[256,128]{1,0:T(8,128)S(1)}, u32[]{:S(2)}, u32[]{:S(2)}) collective-permute-start(f32[256,128]{1,0:T(8,128)S(1)} %get-tuple-element.163), channel_id=1, source_target_pairs={{0,8},{4,12},{8,0},{12,4},{1,9},{5,13},{9,1},{13,5},{2,10},{6,14},... | collective-permute-start | bytes 393224 | tf_op jit(solution)/shard_map/ppermute | solution.py:39
  113.9 3.5 %collective-permute-start.30 = (f32[256,128]{1,0:T(8,128)S(1)}, f32[256,128]{1,0:T(8,128)S(1)}, u32[]{:S(2)}, u32[]{:S(2)}) collective-permute-start(f32[256,128]{1,0:T(8,128)S(1)} %get-tuple-element.162), channel_id=1, source_target_pairs={{0,12},{4,0},{8,4},{12,8},{1,13},{5,1},{9,5},{13,9},{2,14},{6,2},{... | collective-permute-start | bytes 393224 | tf_op jit(solution)/shard_map/ppermute | solution.py:39
  117.5 1.6 collective-permute-done.29
  120.7 5.1 %collective-permute-start.32 = (f32[8,2048]{1,0:T(8,128)S(1)}, f32[8,2048]{1,0:T(8,128)S(1)}, u32[]{:S(2)}, u32[]{:S(2)}) collective-permute-start(f32[8,2048]{1,0:T(8,128)S(1)} %get-tuple-element.118.refs_0_), channel_id=1, source_target_pairs={{0,8},{4,12},{8,0},{12,4},{1,9},{5,13},{9,1},{13,5},{2,10},{6,14},... | collective-permute-start | bytes 196616 | tf_op jit(solution)/shard_map/ppermute | solution.py:39
  127.0 1.8 collective-permute-done.32.refs_2_
  130.1 5.0 %f1.1 = (f32[32,512]{1,0:T(8,128)S(1)}, f32[16,1024]{1,0:T(8,128)S(1)}, f32[16,1024]{1,0:T(8,128)S(1)}) custom-call(s32[128]{0:T(128)S(1)} %pad_add_fusion.meta, f32[8,2048]{1,0:T(8,128)S(1)} %get-tuple-element.118.refs_0_, f32[8,2048]{1,0:T(8,128)S(1)} %collective-permute-done.31.refs_1_, f32[8,2048]{1,0:T(8,128)S(1)} %collective-permute-done.32.refs_2_, ...), custom_call_target="tpu_custom_call" | custom-call | flops 1207959552 | bytes 6553600 | tf_op jit(solution)/shard_map/f1/pallas_call | solution.py:395
  135.7 3.6 %collective-permute-done.35.recv = f32[16,1024]{1,0:T(8,128)S(1)} collective-permute-done((f32[16,1024]{1,0:T(8,128)S(1)}, f32[16,1024]{1,0:T(8,128)S(1)}, u32[]{:S(2)}, u32[]{:S(2)}) %collective-permute-start.35) | collective-permute-done | bytes 65568 | tf_op jit(solution)/shard_map/ppermute | solution.py:43
  141.2 4.0 %collective-permute-start.38 = (f32[16,2048]{1,0:T(8,128)S(1)}, f32[16,2048]{1,0:T(8,128)S(1)}, u32[]{:S(2)}, u32[]{:S(2)}) collective-permute-start(f32[16,2048]{1,0:T(8,128)S(1)} %get-tuple-element.129.refs_0_), channel_id=1, source_target_pairs={{0,8},{4,12},{8,0},{12,4},{1,9},{5,13},{9,1},{13,5},{2,10},{6,14},... | collective-permute-start | bytes 393224 | tf_op jit(solution)/shard_map/ppermute | solution.py:39
  145.3 1.4 collective-permute-start.42
  146.7 1.6 collective-permute-done.37.refs_1_
  148.3 3.6 %collective-permute-done.38.refs_2_ = f32[16,2048]{1,0:T(8,128)S(1)} collective-permute-done((f32[16,2048]{1,0:T(8,128)S(1)}, f32[16,2048]{1,0:T(8,128)S(1)}, u32[]{:S(2)}, u32[]{:S(2)}) %collective-permute-start.38) | collective-permute-done | bytes 131104 | tf_op jit(solution)/shard_map/ppermute | solution.py:39
  151.8 4.7 %f2.1 = (f32[16,512]{1,0:T(8,128)S(1)}, f32[8,1024]{1,0:T(8,128)S(1)}, f32[8,1024]{1,0:T(8,128)S(1)}) custom-call(s32[128]{0:T(128)S(1)} %pad_add_fusion.meta, f32[16,2048]{1,0:T(8,128)S(1)} %get-tuple-element.129.refs_0_, f32[16,2048]{1,0:T(8,128)S(1)} %collective-permute-done.37.refs_1_, f32[16,2048]{1,0:T(8,128)S(1)} %collective-permute-done.38.refs_2_, ...), custom_call_target="tpu_custom_call" | custom-call | flops 603979776 | bytes 6815744 | tf_op jit(solution)/shard_map/f2/pallas_call | solution.py:395
  157.2 4.9 %collective-permute-done.41.recv = f32[8,1024]{1,0:T(8,128)S(1)} collective-permute-done((f32[8,1024]{1,0:T(8,128)S(1)}, f32[8,1024]{1,0:T(8,128)S(1)}, u32[]{:S(2)}, u32[]{:S(2)}) %collective-permute-start.41) | collective-permute-done | bytes 32800 | tf_op jit(solution)/shard_map/ppermute | solution.py:43
  162.7 7.0 %all-gather.11.cloned.1.call-done = f32[16,256,128]{2,1,0:T(8,128)} async-done(((f32[4,256,128]{2,1,0:T(8,128)}), f32[16,256,128]{2,1,0:T(8,128)}) %all-gather.11.cloned.1.call-update) | async-done | bytes 2097168 | tf_op jit(solution)/shard_map/all_gather | solution.py:436
  169.7 1.6 collective-permute-start.43
  171.3 2.9 %collective-permute-start.44 = (f32[8,2048]{1,0:T(8,128)S(1)}, f32[8,2048]{1,0:T(8,128)S(1)}, u32[]{:S(2)}, u32[]{:S(2)}) collective-permute-start(f32[8,2048]{1,0:T(8,128)S(1)} %s23.1.c0), channel_id=1, source_target_pairs={{0,8},{4,12},{8,0},{12,4},{1,9},{5,13},{9,1},{13,5},{2,10},{6,14},... | collective-permute-start | bytes 196616 | tf_op jit(solution)/shard_map/ppermute | solution.py:39
  175.5 2.5 collective-permute-done.44.c2
  179.7 4.6 %top.1.c0 = f32[8,2048]{1,0:T(8,128)S(1)} custom-call(s32[128]{0:T(128)S(1)} %pad_add_fusion.meta, f32[8,2048]{1,0:T(8,128)S(1)} %s23.1.c0, f32[8,2048]{1,0:T(8,128)S(1)} %collective-permute-done.43.c1, f32[8,2048]{1,0:T(8,128)S(1)} %collective-permute-done.44.c2, f32[8,2048]{1,0:T(8,128)S(1)} %collective-permute-done.45.c3, f32[4,4,256,128]{3,2,1,0:T(8,128)} %bitcast.87, ...), custom_call_target="tpu_custom_call" | custom-call | flops 301989888 | bytes 4456448 | tf_op jit(solution)/shard_map/top/pallas_call | solution.py:395
  185.3 3.2 %collective-permute-start.48 = (f32[8,2048]{1,0:T(8,128)S(1)}, f32[8,2048]{1,0:T(8,128)S(1)}, u32[]{:S(2)}, u32[]{:S(2)}) collective-permute-start(f32[8,2048]{1,0:T(8,128)S(1)} %top.1.c0), channel_id=1, source_target_pairs={{0,8},{4,12},{8,0},{12,4},{1,9},{5,13},{9,1},{13,5},{2,10},{6,14},... | collective-permute-start | bytes 196616 | tf_op jit(solution)/shard_map/ppermute | solution.py:39
  190.0 1.5 collective-permute-done.48.c2
  193.4 3.1 %collective-permute-start.50 = (f32[8,1024]{1,0:T(8,128)S(1)}, f32[8,1024]{1,0:T(8,128)S(1)}, u32[]{:S(2)}, u32[]{:S(2)}) collective-permute-start(f32[8,1024]{1,0:T(8,128)S(1)} %get-tuple-element.146), channel_id=1, source_target_pairs={{0,64},{64,0},{1,65},{65,1},{2,66},{66,2},{3,67},{67,3},{4,68},{68... | collective-permute-start | bytes 98312 | tf_op jit(solution)/shard_map/ppermute | solution.py:43
  196.5 2.4 collective-permute-done.50.refs_1_
  198.9 4.7 %b2.1.c0 = f32[16,2048]{1,0:T(8,128)S(1)} custom-call(s32[128]{0:T(128)S(1)} %pad_add_fusion.meta, f32[1,8,2048]{2,1,0:T(8,128)S(1)} %bitcast.79, f32[8,1024]{1,0:T(8,128)S(1)} %collective-permute-done.50.refs_1_, f32[16,512]{1,0:T(8,128)S(1)} %get-tuple-element.147.refs_2_, f32[4,6,256,128]{3,2,1,0:T(8,128)} %bitcast.85, ...), custom_call_target="tpu_custom_call" | custom-call | flops 603979776 | bytes 6422528 | tf_op jit(solution)/shard_map/b2/pallas_call | solution.py:395
  204.0 3.1 %collective-permute-start.52 = (f32[16,2048]{1,0:T(8,128)S(1)}, f32[16,2048]{1,0:T(8,128)S(1)}, u32[]{:S(2)}, u32[]{:S(2)}) collective-permute-start(f32[16,2048]{1,0:T(8,128)S(1)} %b2.1.c0), channel_id=1, source_target_pairs={{0,8},{4,12},{8,0},{12,4},{1,9},{5,13},{9,1},{13,5},{2,10},{6,14},... | collective-permute-start | bytes 393224 | tf_op jit(solution)/shard_map/ppermute | solution.py:39
  207.9 3.0 %collective-permute-start.54 = (f32[8,2048]{1,0:T(8,128)S(1)}, f32[8,2048]{1,0:T(8,128)S(1)}, u32[]{:S(2)}, u32[]{:S(2)}) collective-permute-start(f32[8,2048]{1,0:T(8,128)S(1)} %get-tuple-element.145.x3), channel_id=1, source_target_pairs={{0,64},{64,0},{1,65},{65,1},{2,66},{66,2},{3,67},{67,3},{4,68},{68... | collective-permute-start | bytes 196616 | tf_op jit(solution)/shard_map/ppermute | solution.py:43
  210.8 3.1 %collective-permute-done.54.x3r = f32[8,2048]{1,0:T(8,128)S(1)} collective-permute-done((f32[8,2048]{1,0:T(8,128)S(1)}, f32[8,2048]{1,0:T(8,128)S(1)}, u32[]{:S(2)}, u32[]{:S(2)}) %collective-permute-start.54) | collective-permute-done | bytes 65568 | tf_op jit(solution)/shard_map/ppermute | solution.py:43
  214.6 1.7 collective-permute-start.55
  216.8 2.1 collective-permute-done.55.refs_1_
  219.0 4.8 %b1.1 = (f32[8,2048]{1,0:T(8,128)S(1)}, f32[8,2048]{1,0:T(8,128)S(1)}, f32[8,2048]{1,0:T(8,128)S(1)}, f32[8,2048]{1,0:T(8,128)S(1)}) custom-call(s32[128]{0:T(128)S(1)} %pad_add_fusion.meta, f32[2,16,2048]{2,1,0:T(8,128)S(1)} %get-tuple-element.148.refs_0_, f32[16,1024]{1,0:T(8,128)S(1)} %collective-permute-done.55.refs_1_, ...), custom_call_target="tpu_custom_call" | custom-call | flops 1207959552 | bytes 6684672 | tf_op jit(solution)/shard_map/b1/pallas_call | solution.py:395
  224.7 2.3 collective-permute-start.57
  228.1 2.3 collective-permute-done.57.c2
  230.5 2.0 collective-permute-done.58.c3
  235.5 1.8 collective-permute-start.62
  237.3 2.1 collective-permute-start.63
  240.0 1.8 collective-permute-done.61.refs_1_
  242.3 4.9 %b0.1 = (f32[16,2048]{1,0:T(8,128)S(1)}, f32[16,2048]{1,0:T(8,128)S(1)}, f32[16,2048]{1,0:T(8,128)S(1)}, f32[16,2048]{1,0:T(8,128)S(1)}) custom-call(s32[128]{0:T(128)S(1)} %pad_add_fusion.meta, f32[16,1024]{1,0:T(8,128)S(1)} %maximum_select_fusion.3.refs_0_, f32[16,1024]{1,0:T(8,128)S(1)} %collective-permute-done.61.refs_1_, ...), custom_call_target="tpu_custom_call" | custom-call | flops 2415919104 | bytes 6684672 | tf_op jit(solution)/shard_map/b0/pallas_call | solution.py:395
  247.3 2.7 %collective-permute-start.64 = (f32[16,2048]{1,0:T(8,128)S(1)}, f32[16,2048]{1,0:T(8,128)S(1)}, u32[]{:S(2)}, u32[]{:S(2)}) collective-permute-start(f32[16,2048]{1,0:T(8,128)S(1)} %get-tuple-element.158), channel_id=1, source_target_pairs={{0,3},{1,0},{2,1},{3,2},{4,7},{5,4},{6,5},{7,6},{8,11},{9,8},{10,9... | collective-permute-start | bytes 393224 | tf_op jit(solution)/shard_map/ppermute | solution.py:39
  252.2 2.5 collective-permute-done.64
  254.8 2.4 collective-permute-done.65
  (177 shorter events, 46.5 us)
Async XLA Ops:
  10.7 28.6 %all-to-all-start = ((f32[4,512,128]{2,1,0:T(8,128)}), f32[4,512,128]{2,1,0:T(8,128)S(1)}, u32[]{:S(2)}, u32[]{:S(2)}) async-start(f32[4,512,128]{2,1,0:T(8,128)} %bitcast.3), calls=%async_computation | async-start | bytes 2097152 | tf_op jit(solution)/shard_map/all_to_all | solution.py:443
  15.4 88.4 %all-gather.7.cloned.1.call-start = ((), (), s32[]{:S(2)}) async-start(), calls=%async_computation.1 | async-start | bytes 3932160 | tf_op jit(solution)/shard_map/all_gather | solution.py:436
  15.5 23.2 %collective-permute-start.1 = (f32[4,256,128]{2,1,0:T(8,128)S(1)}, f32[4,256,128]{2,1,0:T(8,128)S(1)}, u32[]{:S(2)}, u32[]{:S(2)}) collective-permute-start(f32[4,256,128]{2,1,0:T(8,128)S(1)} %bitcast.101), channel_id=1, source_target_pairs={{0,4},{4,8},{8,12},{12,0},{1,5},{5,9},{9,13},{13,1},{2,6},{6,10},{... | collective-permute-start | bytes 1572872 | tf_op jit(solution)/shard_map/ppermute | solution.py:39
  17.5 21.2 %collective-permute-start.2 = (f32[4,256,128]{2,1,0:T(8,128)S(1)}, f32[4,256,128]{2,1,0:T(8,128)}, u32[]{:S(2)}, u32[]{:S(2)}) collective-permute-start(f32[4,256,128]{2,1,0:T(8,128)S(1)} %bitcast.102), channel_id=1, source_target_pairs={{0,12},{4,0},{8,4},{12,8},{1,13},{5,1},{9,5},{13,9},{2,14},{6,2},{... | collective-permute-start | bytes 1572872 | tf_op jit(solution)/shard_map/ppermute | solution.py:39
  19.7 15.0 %collective-permute-start.3 = (f32[256,128]{1,0:T(8,128)S(1)}, f32[256,128]{1,0:T(8,128)S(1)}, u32[]{:S(2)}, u32[]{:S(2)}) collective-permute-start(f32[256,128]{1,0:T(8,128)S(1)} %get-tuple-element.88), channel_id=1, source_target_pairs={{0,4},{4,8},{8,12},{12,0},{1,5},{5,9},{9,13},{13,1},{2,6},{6,10},{... | collective-permute-start | bytes 393224 | tf_op jit(solution)/shard_map/ppermute | solution.py:39
  19.7 19.0 %collective-permute-start.4 = (f32[256,128]{1,0:T(8,128)S(1)}, f32[256,128]{1,0:T(8,128)S(1)}, u32[]{:S(2)}, u32[]{:S(2)}) collective-permute-start(f32[256,128]{1,0:T(8,128)S(1)} %get-tuple-element.89), channel_id=1, source_target_pairs={{0,8},{4,12},{8,0},{12,4},{1,9},{5,13},{9,1},{13,5},{2,10},{6,14},... | collective-permute-start | bytes 393224 | tf_op jit(solution)/shard_map/ppermute | solution.py:39
  23.1 15.6 %collective-permute-start.5 = (f32[256,128]{1,0:T(8,128)S(1)}, f32[256,128]{1,0:T(8,128)S(1)}, u32[]{:S(2)}, u32[]{:S(2)}) collective-permute-start(f32[256,128]{1,0:T(8,128)S(1)} %get-tuple-element.90), channel_id=1, source_target_pairs={{0,12},{4,0},{8,4},{12,8},{1,13},{5,1},{9,5},{13,9},{2,14},{6,2},{... | collective-permute-start | bytes 393224 | tf_op jit(solution)/shard_map/ppermute | solution.py:39
  41.7 98.5 %all-gather.9.cloned.1.call-start = ((), (), s32[]{:S(2)}) async-start(), calls=%async_computation.2 | async-start | bytes 3932160 | tf_op jit(solution)/shard_map/all_gather | solution.py:436
  41.7 34.5 %collective-permute-start.8 = (f32[4,512,128]{2,1,0:T(8,128)S(1)}, f32[4,512,128]{2,1,0:T(8,128)}, u32[]{:S(2)}, u32[]{:S(2)}) collective-permute-start(f32[4,512,128]{2,1,0:T(8,128)S(1)} %all-to-all-done.refs_4_.refs_5_), channel_id=1, source_target_pairs={{0,4},{4,8},{8,12},{12,0},{1,5},{5,9},{9,13},{13,1},{2,6},{6,10},{... | collective-permute-start | bytes 3145736 | tf_op jit(solution)/shard_map/ppermute | solution.py:39
  41.9 34.3 %collective-permute-start.9 = (f32[4,512,128]{2,1,0:T(8,128)S(1)}, f32[4,512,128]{2,1,0:T(8,128)}, u32[]{:S(2)}, u32[]{:S(2)}) collective-permute-start(f32[4,512,128]{2,1,0:T(8,128)S(1)} %all-to-all-done.refs_4_.refs_5_), channel_id=1, source_target_pairs={{0,12},{4,0},{8,4},{12,8},{1,13},{5,1},{9,5},{13,9},{2,14},{6,2},{... | collective-permute-start | bytes 3145736 | tf_op jit(solution)/shard_map/ppermute | solution.py:39
  45.1 4.6 %collective-permute-start.6 = (f32[1,256,128]{2,1,0:T(8,128)S(1)}, f32[1,256,128]{2,1,0:T(8,128)S(1)}, u32[]{:S(2)}, u32[]{:S(2)}) collective-permute-start(f32[1,256,128]{2,1,0:T(8,128)S(1)} %get-tuple-element.177), channel_id=1, source_target_pairs={{0,16},{16,0},{1,17},{17,1},{2,18},{18,2},{3,19},{19,3},{4,20},{20... | collective-permute-start | bytes 393224 | tf_op jit(solution)/shard_map/ppermute | solution.py:43
  45.2 7.1 %collective-permute-start.12 = (f32[16,2048]{1,0:T(8,128)S(1)}, f32[16,2048]{1,0:T(8,128)S(1)}, u32[]{:S(2)}, u32[]{:S(2)}) collective-permute-start(f32[16,2048]{1,0:T(8,128)S(1)} %copy-done), channel_id=1, source_target_pairs={{0,1},{1,2},{2,3},{3,0},{4,5},{5,6},{6,7},{7,4},{8,9},{9,10},{10,1... | collective-permute-start | bytes 393224 | tf_op jit(solution)/shard_map/ppermute | solution.py:39
  47.0 10.4 %collective-permute-start.13 = (f32[16,2048]{1,0:T(8,128)S(1)}, f32[16,2048]{1,0:T(8,128)S(1)}, u32[]{:S(2)}, u32[]{:S(2)}) collective-permute-start(f32[16,2048]{1,0:T(8,128)S(1)} %copy-done), channel_id=1, source_target_pairs={{0,2},{1,3},{2,0},{3,1},{4,6},{5,7},{6,4},{7,5},{8,10},{9,11},{10,... | collective-permute-start | bytes 393224 | tf_op jit(solution)/shard_map/ppermute | solution.py:39
  49.6 7.8 %collective-permute-start.21 = (f32[1,256,128]{2,1,0:T(8,128)S(1)}, f32[1,256,128]{2,1,0:T(8,128)S(1)}, u32[]{:S(2)}, u32[]{:S(2)}) collective-permute-start(f32[1,256,128]{2,1,0:T(8,128)S(1)} %bitcast.94), channel_id=1, source_target_pairs={{0,32},{32,0},{1,33},{33,1},{2,34},{34,2},{3,35},{35,3},{4,36},{36... | collective-permute-start | bytes 393224 | tf_op jit(solution)/shard_map/ppermute | solution.py:43
  52.3 8.4 %collective-permute-start.7 = (f32[2,256,128]{2,1,0:T(8,128)S(1)}, f32[2,256,128]{2,1,0:T(8,128)S(1)}, u32[]{:S(2)}, u32[]{:S(2)}) collective-permute-start(f32[2,256,128]{2,1,0:T(8,128)S(1)} %maximum_select_fusion), channel_id=1, source_target_pairs={{0,32},{32,0},{1,33},{33,1},{2,34},{34,2},{3,35},{35,3},{4,36},{36... | collective-permute-start | bytes 786440 | tf_op jit(solution)/shard_map/ppermute | solution.py:43
  57.3 15.8 %collective-permute-start.10 = (f32[2,256,128]{2,1,0:T(8,128)S(1)}, f32[2,256,128]{2,1,0:T(8,128)}, u32[]{:S(2)}, u32[]{:S(2)}) collective-permute-start(f32[2,256,128]{2,1,0:T(8,128)S(1)} %slice.43), channel_id=1, source_target_pairs={{0,4},{4,8},{8,12},{12,0},{1,5},{5,9},{9,13},{13,1},{2,6},{6,10},{... | collective-permute-start | bytes 786440 | tf_op jit(solution)/shard_map/ppermute | solution.py:39
  57.4 18.8 %collective-permute-start.11 = (f32[2,256,128]{2,1,0:T(8,128)S(1)}, f32[2,256,128]{2,1,0:T(8,128)}, u32[]{:S(2)}, u32[]{:S(2)}) collective-permute-start(f32[2,256,128]{2,1,0:T(8,128)S(1)} %slice.44), channel_id=1, source_target_pairs={{0,12},{4,0},{8,4},{12,8},{1,13},{5,1},{9,5},{13,9},{2,14},{6,2},{... | collective-permute-start | bytes 786440 | tf_op jit(solution)/shard_map/ppermute | solution.py:39
  60.6 8.6 %collective-permute-start.14 = (f32[16,2048]{1,0:T(8,128)S(1)}, f32[16,2048]{1,0:T(8,128)S(1)}, u32[]{:S(2)}, u32[]{:S(2)}) collective-permute-start(f32[16,2048]{1,0:T(8,128)S(1)} %copy-done), channel_id=1, source_target_pairs={{0,3},{1,0},{2,1},{3,2},{4,7},{5,4},{6,5},{7,6},{8,11},{9,8},{10,9... | collective-permute-start | bytes 393224 | tf_op jit(solution)/shard_map/ppermute | solution.py:39
  69.2 13.8 %collective-permute-start.20 = (f32[256,128]{1,0:T(8,128)S(1)}, f32[256,128]{1,0:T(8,128)S(1)}, u32[]{:S(2)}, u32[]{:S(2)}) collective-permute-start(f32[256,128]{1,0:T(8,128)S(1)} %copy-done.8), channel_id=1, source_target_pairs={{0,32},{32,0},{1,33},{33,1},{2,34},{34,2},{3,35},{35,3},{4,36},{36... | collective-permute-start | bytes 393224 | tf_op jit(solution)/shard_map/ppermute | solution.py:43
  73.2 11.4 %collective-permute-start.22 = (f32[2,256,128]{2,1,0:T(8,128)S(1)}, f32[2,256,128]{2,1,0:T(8,128)S(1)}, u32[]{:S(2)}, u32[]{:S(2)}) collective-permute-start(f32[2,256,128]{2,1,0:T(8,128)S(1)} %maximum_select_fusion.2), channel_id=1, source_target_pairs={{0,64},{64,0},{1,65},{65,1},{2,66},{66,2},{3,67},{67,3},{4,68},{68... | collective-permute-start | bytes 786440 | tf_op jit(solution)/shard_map/ppermute | solution.py:43
  77.3 19.3 %collective-permute-start.15 = (f32[2,512,128]{2,1,0:T(8,128)S(1)}, f32[2,512,128]{2,1,0:T(8,128)S(1)}, u32[]{:S(2)}, u32[]{:S(2)}) collective-permute-start(f32[2,512,128]{2,1,0:T(8,128)S(1)} %slice.45), channel_id=1, source_target_pairs={{0,4},{4,8},{8,12},{12,0},{1,5},{5,9},{9,13},{13,1},{2,6},{6,10},{... | collective-permute-start | bytes 1572872 | tf_op jit(solution)/shard_map/ppermute | solution.py:39
  78.4 18.1 %collective-permute-start.16 = (f32[2,512,128]{2,1,0:T(8,128)S(1)}, f32[2,512,128]{2,1,0:T(8,128)S(1)}, u32[]{:S(2)}, u32[]{:S(2)}) collective-permute-start(f32[2,512,128]{2,1,0:T(8,128)S(1)} %slice.46), channel_id=1, source_target_pairs={{0,12},{4,0},{8,4},{12,8},{1,13},{5,1},{9,5},{13,9},{2,14},{6,2},{... | collective-permute-start | bytes 1572872 | tf_op jit(solution)/shard_map/ppermute | solution.py:39
  83.1 13.1 %collective-permute-start.17 = (f32[256,128]{1,0:T(8,128)S(1)}, f32[256,128]{1,0:T(8,128)S(1)}, u32[]{:S(2)}, u32[]{:S(2)}) collective-permute-start(f32[256,128]{1,0:T(8,128)S(1)} %get-tuple-element.168), channel_id=1, source_target_pairs={{0,4},{4,8},{8,12},{12,0},{1,5},{5,9},{9,13},{13,1},{2,6},{6,10},{... | collective-permute-start | bytes 393224 | tf_op jit(solution)/shard_map/ppermute | solution.py:39
  83.1 13.1 %collective-permute-start.18 = (f32[256,128]{1,0:T(8,128)S(1)}, f32[256,128]{1,0:T(8,128)S(1)}, u32[]{:S(2)}, u32[]{:S(2)}) collective-permute-start(f32[256,128]{1,0:T(8,128)S(1)} %get-tuple-element.167), channel_id=1, source_target_pairs={{0,8},{4,12},{8,0},{12,4},{1,9},{5,13},{9,1},{13,5},{2,10},{6,14},... | collective-permute-start | bytes 393224 | tf_op jit(solution)/shard_map/ppermute | solution.py:39
  84.6 12.0 %collective-permute-start.19 = (f32[256,128]{1,0:T(8,128)S(1)}, f32[256,128]{1,0:T(8,128)S(1)}, u32[]{:S(2)}, u32[]{:S(2)}) collective-permute-start(f32[256,128]{1,0:T(8,128)S(1)} %get-tuple-element.166), channel_id=1, source_target_pairs={{0,12},{4,0},{8,4},{12,8},{1,13},{5,1},{9,5},{13,9},{2,14},{6,2},{... | collective-permute-start | bytes 393224 | tf_op jit(solution)/shard_map/ppermute | solution.py:39
  97.7 72.0 %all-gather.11.cloned.1.call-start = ((), (), s32[]{:S(2)}) async-start(), calls=%async_computation.3 | async-start | bytes 2621440 | tf_op jit(solution)/shard_map/all_gather | solution.py:436
  103.8 26.2 %collective-permute-start.34 = (f32[4,6,256,128]{3,2,1,0:T(8,128)}, f32[4,6,256,128]{3,2,1,0:T(8,128)}, u32[]{:S(2)}, u32[]{:S(2)}) collective-permute-start(f32[4,6,256,128]{3,2,1,0:T(8,128)} %bitcast.80), channel_id=1, source_target_pairs={{0,16},{16,0},{1,17},{17,1},{2,18},{18,2},{3,19},{19,3},{4,20},{20... | collective-permute-start | bytes 9437192 | tf_op jit(solution)/shard_map/ppermute | solution.py:43
  104.0 6.3 %collective-permute-start.24 = (f32[16,1024]{1,0:T(8,128)S(1)}, f32[16,1024]{1,0:T(8,128)S(1)}, u32[]{:S(2)}, u32[]{:S(2)}) collective-permute-start(f32[16,1024]{1,0:T(8,128)S(1)} %get-tuple-element.110), channel_id=1, source_target_pairs={{0,3},{1,0},{2,1},{3,2},{4,7},{5,4},{6,5},{7,6},{8,11},{9,8},{10,9... | collective-permute-start | bytes 196616 | tf_op jit(solution)/shard_map/ppermute | solution.py:39
  106.3 7.5 %collective-permute-start.25 = (f32[16,1024]{1,0:T(8,128)S(1)}, f32[16,1024]{1,0:T(8,128)S(1)}, u32[]{:S(2)}, u32[]{:S(2)}) collective-permute-start(f32[16,1024]{1,0:T(8,128)S(1)} %get-tuple-element.111), channel_id=1, source_target_pairs={{0,2},{1,3},{2,0},{3,1},{4,6},{5,7},{6,4},{7,5},{8,10},{9,11},{10,... | collective-permute-start | bytes 196616 | tf_op jit(solution)/shard_map/ppermute | solution.py:39
  107.2 10.2 %collective-permute-start.26 = (f32[16,1024]{1,0:T(8,128)S(1)}, f32[16,1024]{1,0:T(8,128)S(1)}, u32[]{:S(2)}, u32[]{:S(2)}) collective-permute-start(f32[16,1024]{1,0:T(8,128)S(1)} %get-tuple-element.112), channel_id=1, source_target_pairs={{0,1},{1,2},{2,3},{3,0},{4,5},{5,6},{6,7},{7,4},{8,9},{9,10},{10,1... | collective-permute-start | bytes 196616 | tf_op jit(solution)/shard_map/ppermute | solution.py:39
  108.1 9.4 %collective-permute-start.28 = (f32[256,128]{1,0:T(8,128)S(1)}, f32[256,128]{1,0:T(8,128)S(1)}, u32[]{:S(2)}, u32[]{:S(2)}) collective-permute-start(f32[256,128]{1,0:T(8,128)S(1)} %get-tuple-element.164), channel_id=1, source_target_pairs={{0,4},{4,8},{8,12},{12,0},{1,5},{5,9},{9,13},{13,1},{2,6},{6,10},{... | collective-permute-start | bytes 393224 | tf_op jit(solution)/shard_map/ppermute | solution.py:39
  110.2 8.9 %collective-permute-start.29 = (f32[256,128]{1,0:T(8,128)S(1)}, f32[256,128]{1,0:T(8,128)S(1)}, u32[]{:S(2)}, u32[]{:S(2)}) collective-permute-start(f32[256,128]{1,0:T(8,128)S(1)} %get-tuple-element.163), channel_id=1, source_target_pairs={{0,8},{4,12},{8,0},{12,4},{1,9},{5,13},{9,1},{13,5},{2,10},{6,14},... | collective-permute-start | bytes 393224 | tf_op jit(solution)/shard_map/ppermute | solution.py:39
  113.9 6.1 %collective-permute-start.30 = (f32[256,128]{1,0:T(8,128)S(1)}, f32[256,128]{1,0:T(8,128)S(1)}, u32[]{:S(2)}, u32[]{:S(2)}) collective-permute-start(f32[256,128]{1,0:T(8,128)S(1)} %get-tuple-element.162), channel_id=1, source_target_pairs={{0,12},{4,0},{8,4},{12,8},{1,13},{5,1},{9,5},{13,9},{2,14},{6,2},{... | collective-permute-start | bytes 393224 | tf_op jit(solution)/shard_map/ppermute | solution.py:39
  120.6 6.4 %collective-permute-start.31 = (f32[8,2048]{1,0:T(8,128)S(1)}, f32[8,2048]{1,0:T(8,128)S(1)}, u32[]{:S(2)}, u32[]{:S(2)}) collective-permute-start(f32[8,2048]{1,0:T(8,128)S(1)} %get-tuple-element.118.refs_0_), channel_id=1, source_target_pairs={{0,4},{4,8},{8,12},{12,0},{1,5},{5,9},{9,13},{13,1},{2,6},{6,10},{... | collective-permute-start | bytes 196616 | tf_op jit(solution)/shard_map/ppermute | solution.py:39
  120.7 8.0 %collective-permute-start.32 = (f32[8,2048]{1,0:T(8,128)S(1)}, f32[8,2048]{1,0:T(8,128)S(1)}, u32[]{:S(2)}, u32[]{:S(2)}) collective-permute-start(f32[8,2048]{1,0:T(8,128)S(1)} %get-tuple-element.118.refs_0_), channel_id=1, source_target_pairs={{0,8},{4,12},{8,0},{12,4},{1,9},{5,13},{9,1},{13,5},{2,10},{6,14},... | collective-permute-start | bytes 196616 | tf_op jit(solution)/shard_map/ppermute | solution.py:39
  125.8 10.0 %collective-permute-start.36 = (f32[2,4,2048]{2,1,0:T(4,128)S(1)}, f32[2,4,2048]{2,1,0:T(4,128)S(1)}, u32[]{:S(2)}, u32[]{:S(2)}) collective-permute-start(f32[2,4,2048]{2,1,0:T(4,128)S(1)} %get-tuple-element.128), channel_id=1, source_target_pairs={{0,32},{32,0},{1,33},{33,1},{2,34},{34,2},{3,35},{35,3},{4,36},{36... | collective-permute-start | bytes 196616 | tf_op jit(solution)/shard_map/ppermute | solution.py:43
  135.0 4.3 %collective-permute-start.35 = (f32[16,1024]{1,0:T(8,128)S(1)}, f32[16,1024]{1,0:T(8,128)S(1)}, u32[]{:S(2)}, u32[]{:S(2)}) collective-permute-start(f32[16,1024]{1,0:T(8,128)S(1)} %get-tuple-element.126), channel_id=1, source_target_pairs={{0,32},{32,0},{1,33},{33,1},{2,34},{34,2},{3,35},{35,3},{4,36},{36... | collective-permute-start | bytes 196616 | tf_op jit(solution)/shard_map/ppermute | solution.py:43
  140.1 11.7 %collective-permute-start.40 = (f32[4,6,256,128]{3,2,1,0:T(8,128)}, f32[4,6,256,128]{3,2,1,0:T(8,128)}, u32[]{:S(2)}, u32[]{:S(2)}) collective-permute-start(f32[4,6,256,128]{3,2,1,0:T(8,128)} %bitcast.83), channel_id=1, source_target_pairs={{0,16},{16,0},{1,17},{17,1},{2,18},{18,2},{3,19},{19,3},{4,20},{20... | collective-permute-start | bytes 9437192 | tf_op jit(solution)/shard_map/ppermute | solution.py:43
  141.1 7.2 %collective-permute-start.37 = (f32[16,2048]{1,0:T(8,128)S(1)}, f32[16,2048]{1,0:T(8,128)S(1)}, u32[]{:S(2)}, u32[]{:S(2)}) collective-permute-start(f32[16,2048]{1,0:T(8,128)S(1)} %get-tuple-element.129.refs_0_), channel_id=1, source_target_pairs={{0,4},{4,8},{8,12},{12,0},{1,5},{5,9},{9,13},{13,1},{2,6},{6,10},{... | collective-permute-start | bytes 393224 | tf_op jit(solution)/shard_map/ppermute | solution.py:39
  141.2 10.7 %collective-permute-start.38 = (f32[16,2048]{1,0:T(8,128)S(1)}, f32[16,2048]{1,0:T(8,128)S(1)}, u32[]{:S(2)}, u32[]{:S(2)}) collective-permute-start(f32[16,2048]{1,0:T(8,128)S(1)} %get-tuple-element.129.refs_0_), channel_id=1, source_target_pairs={{0,8},{4,12},{8,0},{12,4},{1,9},{5,13},{9,1},{13,5},{2,10},{6,14},... | collective-permute-start | bytes 393224 | tf_op jit(solution)/shard_map/ppermute | solution.py:39
  145.2 6.6 %collective-permute-start.39 = (f32[16,2048]{1,0:T(8,128)S(1)}, f32[16,2048]{1,0:T(8,128)S(1)}, u32[]{:S(2)}, u32[]{:S(2)}) collective-permute-start(f32[16,2048]{1,0:T(8,128)S(1)} %get-tuple-element.129.refs_0_), channel_id=1, source_target_pairs={{0,12},{4,0},{8,4},{12,8},{1,13},{5,1},{9,5},{13,9},{2,14},{6,2},{... | collective-permute-start | bytes 393224 | tf_op jit(solution)/shard_map/ppermute | solution.py:39
  145.3 11.9 %collective-permute-start.42 = (f32[8,2048]{1,0:T(8,128)S(1)}, f32[8,2048]{1,0:T(8,128)S(1)}, u32[]{:S(2)}, u32[]{:S(2)}) collective-permute-start(f32[8,2048]{1,0:T(8,128)S(1)} %get-tuple-element.139), channel_id=1, source_target_pairs={{0,64},{64,0},{1,65},{65,1},{2,66},{66,2},{3,67},{67,3},{4,68},{68... | collective-permute-start | bytes 196616 | tf_op jit(solution)/shard_map/ppermute | solution.py:43
  156.6 5.5 %collective-permute-start.41 = (f32[8,1024]{1,0:T(8,128)S(1)}, f32[8,1024]{1,0:T(8,128)S(1)}, u32[]{:S(2)}, u32[]{:S(2)}) collective-permute-start(f32[8,1024]{1,0:T(8,128)S(1)} %get-tuple-element.137), channel_id=1, source_target_pairs={{0,64},{64,0},{1,65},{65,1},{2,66},{66,2},{3,67},{67,3},{4,68},{68... | collective-permute-start | bytes 98312 | tf_op jit(solution)/shard_map/ppermute | solution.py:43
  169.7 8.7 %collective-permute-start.46 = (f32[4,4,256,128]{3,2,1,0:T(8,128)}, f32[4,4,256,128]{3,2,1,0:T(8,128)S(1)}, u32[]{:S(2)}, u32[]{:S(2)}) collective-permute-start(f32[4,4,256,128]{3,2,1,0:T(8,128)} %bitcast.86), channel_id=1, source_target_pairs={{0,16},{16,0},{1,17},{17,1},{2,18},{18,2},{3,19},{19,3},{4,20},{20... | collective-permute-start | bytes 6291464 | tf_op jit(solution)/shard_map/ppermute | solution.py:43
  169.7 5.8 %collective-permute-start.43 = (f32[8,2048]{1,0:T(8,128)S(1)}, f32[8,2048]{1,0:T(8,128)S(1)}, u32[]{:S(2)}, u32[]{:S(2)}) collective-permute-start(f32[8,2048]{1,0:T(8,128)S(1)} %s23.1.c0), channel_id=1, source_target_pairs={{0,4},{4,8},{8,12},{12,0},{1,5},{5,9},{9,13},{13,1},{2,6},{6,10},{... | collective-permute-start | bytes 196616 | tf_op jit(solution)/shard_map/ppermute | solution.py:39
  171.3 6.7 %collective-permute-start.44 = (f32[8,2048]{1,0:T(8,128)S(1)}, f32[8,2048]{1,0:T(8,128)S(1)}, u32[]{:S(2)}, u32[]{:S(2)}) collective-permute-start(f32[8,2048]{1,0:T(8,128)S(1)} %s23.1.c0), channel_id=1, source_target_pairs={{0,8},{4,12},{8,0},{12,4},{1,9},{5,13},{9,1},{13,5},{2,10},{6,14},... | collective-permute-start | bytes 196616 | tf_op jit(solution)/shard_map/ppermute | solution.py:39
  184.4 5.6 %collective-permute-start.47 = (f32[8,2048]{1,0:T(8,128)S(1)}, f32[8,2048]{1,0:T(8,128)S(1)}, u32[]{:S(2)}, u32[]{:S(2)}) collective-permute-start(f32[8,2048]{1,0:T(8,128)S(1)} %top.1.c0), channel_id=1, source_target_pairs={{0,4},{4,8},{8,12},{12,0},{1,5},{5,9},{9,13},{13,1},{2,6},{6,10},{... | collective-permute-start | bytes 196616 | tf_op jit(solution)/shard_map/ppermute | solution.py:39
  185.3 6.1 %collective-permute-start.48 = (f32[8,2048]{1,0:T(8,128)S(1)}, f32[8,2048]{1,0:T(8,128)S(1)}, u32[]{:S(2)}, u32[]{:S(2)}) collective-permute-start(f32[8,2048]{1,0:T(8,128)S(1)} %top.1.c0), channel_id=1, source_target_pairs={{0,8},{4,12},{8,0},{12,4},{1,9},{5,13},{9,1},{13,5},{2,10},{6,14},... | collective-permute-start | bytes 196616 | tf_op jit(solution)/shard_map/ppermute | solution.py:39
  193.4 5.5 %collective-permute-start.50 = (f32[8,1024]{1,0:T(8,128)S(1)}, f32[8,1024]{1,0:T(8,128)S(1)}, u32[]{:S(2)}, u32[]{:S(2)}) collective-permute-start(f32[8,1024]{1,0:T(8,128)S(1)} %get-tuple-element.146), channel_id=1, source_target_pairs={{0,64},{64,0},{1,65},{65,1},{2,66},{66,2},{3,67},{67,3},{4,68},{68... | collective-permute-start | bytes 98312 | tf_op jit(solution)/shard_map/ppermute | solution.py:43
  203.6 10.3 %collective-permute-start.51 = (f32[16,2048]{1,0:T(8,128)S(1)}, f32[16,2048]{1,0:T(8,128)S(1)}, u32[]{:S(2)}, u32[]{:S(2)}) collective-permute-start(f32[16,2048]{1,0:T(8,128)S(1)} %b2.1.c0), channel_id=1, source_target_pairs={{0,4},{4,8},{8,12},{12,0},{1,5},{5,9},{9,13},{13,1},{2,6},{6,10},{... | collective-permute-start | bytes 393224 | tf_op jit(solution)/shard_map/ppermute | solution.py:39
  204.0 10.0 %collective-permute-start.52 = (f32[16,2048]{1,0:T(8,128)S(1)}, f32[16,2048]{1,0:T(8,128)S(1)}, u32[]{:S(2)}, u32[]{:S(2)}) collective-permute-start(f32[16,2048]{1,0:T(8,128)S(1)} %b2.1.c0), channel_id=1, source_target_pairs={{0,8},{4,12},{8,0},{12,4},{1,9},{5,13},{9,1},{13,5},{2,10},{6,14},... | collective-permute-start | bytes 393224 | tf_op jit(solution)/shard_map/ppermute | solution.py:39
  207.1 6.8 %collective-permute-start.53 = (f32[16,2048]{1,0:T(8,128)S(1)}, f32[16,2048]{1,0:T(8,128)S(1)}, u32[]{:S(2)}, u32[]{:S(2)}) collective-permute-start(f32[16,2048]{1,0:T(8,128)S(1)} %b2.1.c0), channel_id=1, source_target_pairs={{0,12},{4,0},{8,4},{12,8},{1,13},{5,1},{9,5},{13,9},{2,14},{6,2},{... | collective-permute-start | bytes 393224 | tf_op jit(solution)/shard_map/ppermute | solution.py:39
  207.9 6.1 %collective-permute-start.54 = (f32[8,2048]{1,0:T(8,128)S(1)}, f32[8,2048]{1,0:T(8,128)S(1)}, u32[]{:S(2)}, u32[]{:S(2)}) collective-permute-start(f32[8,2048]{1,0:T(8,128)S(1)} %get-tuple-element.145.x3), channel_id=1, source_target_pairs={{0,64},{64,0},{1,65},{65,1},{2,66},{66,2},{3,67},{67,3},{4,68},{68... | collective-permute-start | bytes 196616 | tf_op jit(solution)/shard_map/ppermute | solution.py:43
  216.4 11.0 %collective-permute-start.59 = (f32[2,4,2048]{2,1,0:T(4,128)S(1)}, f32[2,4,2048]{2,1,0:T(4,128)S(1)}, u32[]{:S(2)}, u32[]{:S(2)}) collective-permute-start(f32[2,4,2048]{2,1,0:T(4,128)S(1)} %slice.51.a_mine), channel_id=1, source_target_pairs={{0,32},{32,0},{1,33},{33,1},{2,34},{34,2},{3,35},{35,3},{4,36},{36... | collective-permute-start | bytes 196616 | tf_op jit(solution)/shard_map/ppermute | solution.py:43
  224.7 5.8 %collective-permute-start.57 = (f32[8,2048]{1,0:T(8,128)S(1)}, f32[8,2048]{1,0:T(8,128)S(1)}, u32[]{:S(2)}, u32[]{:S(2)}) collective-permute-start(f32[8,2048]{1,0:T(8,128)S(1)} %get-tuple-element.153), channel_id=1, source_target_pairs={{0,8},{4,12},{8,0},{12,4},{1,9},{5,13},{9,1},{13,5},{2,10},{6,14},... | collective-permute-start | bytes 196616 | tf_op jit(solution)/shard_map/ppermute | solution.py:39
  227.0 5.5 %collective-permute-start.58 = (f32[8,2048]{1,0:T(8,128)S(1)}, f32[8,2048]{1,0:T(8,128)S(1)}, u32[]{:S(2)}, u32[]{:S(2)}) collective-permute-start(f32[8,2048]{1,0:T(8,128)S(1)} %get-tuple-element.154), channel_id=1, source_target_pairs={{0,4},{4,8},{8,12},{12,0},{1,5},{5,9},{9,13},{13,1},{2,6},{6,10},{... | collective-permute-start | bytes 196616 | tf_op jit(solution)/shard_map/ppermute | solution.py:39
  233.2 17.7 %collective-permute-start.68 = (f32[8,512]{1,0:T(8,128)S(1)}, f32[8,512]{1,0:T(8,128)S(1)}, u32[]{:S(2)}, u32[]{:S(2)}) collective-permute-start(f32[8,512]{1,0:T(8,128)S(1)} %get-tuple-element.186), channel_id=1, source_target_pairs={{0,16},{16,0},{1,17},{17,1},{2,18},{18,2},{3,19},{19,3},{4,20},{20... | collective-permute-start | bytes 49160 | tf_op jit(solution)/shard_map/ppermute | solution.py:43
  233.8 17.7 %collective-permute-start.67 = (f32[8,1024]{1,0:T(8,128)S(1)}, f32[8,1024]{1,0:T(8,128)S(1)}, u32[]{:S(2)}, u32[]{:S(2)}) collective-permute-start(f32[8,1024]{1,0:T(8,128)S(1)} %get-tuple-element.188), channel_id=1, source_target_pairs={{0,16},{16,0},{1,17},{17,1},{2,18},{18,2},{3,19},{19,3},{4,20},{20... | collective-permute-start | bytes 98312 | tf_op jit(solution)/shard_map/ppermute | solution.py:43
  234.9 6.8 %collective-permute-start.61 = (f32[16,1024]{1,0:T(8,128)S(1)}, f32[16,1024]{1,0:T(8,128)S(1)}, u32[]{:S(2)}, u32[]{:S(2)}) collective-permute-start(f32[16,1024]{1,0:T(8,128)S(1)} %maximum_select_fusion.3.refs_0_), channel_id=1, source_target_pairs={{0,1},{1,2},{2,3},{3,0},{4,5},{5,6},{6,7},{7,4},{8,9},{9,10},{10,1... | collective-permute-start | bytes 196616 | tf_op jit(solution)/shard_map/ppermute | solution.py:39
  235.5 6.2 %collective-permute-start.62 = (f32[16,1024]{1,0:T(8,128)S(1)}, f32[16,1024]{1,0:T(8,128)S(1)}, u32[]{:S(2)}, u32[]{:S(2)}) collective-permute-start(f32[16,1024]{1,0:T(8,128)S(1)} %maximum_select_fusion.3.refs_0_), channel_id=1, source_target_pairs={{0,2},{1,3},{2,0},{3,1},{4,6},{5,7},{6,4},{7,5},{8,10},{9,11},{10,... | collective-permute-start | bytes 196616 | tf_op jit(solution)/shard_map/ppermute | solution.py:39
  237.3 5.0 %collective-permute-start.63 = (f32[16,1024]{1,0:T(8,128)S(1)}, f32[16,1024]{1,0:T(8,128)S(1)}, u32[]{:S(2)}, u32[]{:S(2)}) collective-permute-start(f32[16,1024]{1,0:T(8,128)S(1)} %maximum_select_fusion.3.refs_0_), channel_id=1, source_target_pairs={{0,3},{1,0},{2,1},{3,2},{4,7},{5,4},{6,5},{7,6},{8,11},{9,8},{10,9... | collective-permute-start | bytes 196616 | tf_op jit(solution)/shard_map/ppermute | solution.py:39
  247.3 7.5 %collective-permute-start.64 = (f32[16,2048]{1,0:T(8,128)S(1)}, f32[16,2048]{1,0:T(8,128)S(1)}, u32[]{:S(2)}, u32[]{:S(2)}) collective-permute-start(f32[16,2048]{1,0:T(8,128)S(1)} %get-tuple-element.158), channel_id=1, source_target_pairs={{0,3},{1,0},{2,1},{3,2},{4,7},{5,4},{6,5},{7,6},{8,11},{9,8},{10,9... | collective-permute-start | bytes 393224 | tf_op jit(solution)/shard_map/ppermute | solution.py:39
  250.0 7.1 %collective-permute-start.65 = (f32[16,2048]{1,0:T(8,128)S(1)}, f32[16,2048]{1,0:T(8,128)S(1)}, u32[]{:S(2)}, u32[]{:S(2)}) collective-permute-start(f32[16,2048]{1,0:T(8,128)S(1)} %get-tuple-element.159), channel_id=1, source_target_pairs={{0,2},{1,3},{2,0},{3,1},{4,6},{5,7},{6,4},{7,5},{8,10},{9,11},{10,... | collective-permute-start | bytes 393224 | tf_op jit(solution)/shard_map/ppermute | solution.py:39
  250.5 7.9 %collective-permute-start.66 = (f32[16,2048]{1,0:T(8,128)S(1)}, f32[16,2048]{1,0:T(8,128)S(1)}, u32[]{:S(2)}, u32[]{:S(2)}) collective-permute-start(f32[16,2048]{1,0:T(8,128)S(1)} %get-tuple-element.160), channel_id=1, source_target_pairs={{0,1},{1,2},{2,3},{3,0},{4,5},{5,6},{6,7},{7,4},{8,9},{9,10},{10,1... | collective-permute-start | bytes 393224 | tf_op jit(solution)/shard_map/ppermute | solution.py:39
  (27 other events, 356.5 us)
Sparse Core Ops, SparseCore 0:
  41.8 41.8 all-gather.6
  97.8 41.1 all-gather.8
  141.2 28.4 all-gather.10

commit v7 on v6

--- a/solution.py
+++ b/solution.py
@@ -322,11 +322,8 @@
     lax.fori_loop(0, 4, body, 0)
 
 
-def x3_kernel(meta, c0, c1, c2, c3, x_out, give, anc):
-    x = summed((c0, c1, c2, c3), 2)
-    x_out[...] = x
-    anc[0] = x
-    take_tiles(meta, Place(meta).partner(2), anc, give)
+def x3_kernel(meta, c0, c1, c2, c3, x_out):
+    x_out[...] = summed((c0, c1, c2, c3), 2)
 
 
 def merged(a, b, h, bit):
@@ -373,6 +370,9 @@
         g = gv[...]
     else:
         take_tiles(meta, Place(meta).own(level), anc, ov)
+        if level == 2:
+            take_tiles(meta, Place(meta).own(level), recv, gv)
+            recv = gv
         g = merged(ov[...], recv[...], r // 2, Place(meta).bit(level))
     gs = stacked(g)
     finish(first)
@@ -439,32 +439,32 @@
     e0 = jnp.swapaxes(dinv0.reshape(4, 4, B, B), 0, 1).reshape(4, 512, B)
     e1 = dinv1.reshape(2, 2, 256, B)
     e1_mine, e1_other = pick(e1, ci, 1), flip(pick(e1, 1 - ci, 1), "core")
-    e0, e1_mine, e1_other = gate((e0, e1_mine, e1_other))
+    e0, e1_mine, e1_other, dinv2, rhs0 = gate((e0, e1_mine, e1_other, dinv2, rhs0))
     e0 = lax.all_to_all(e0, "y", 0, 0, tiled=True)
-    e1 = for_z(e1_mine, e1_other, ci)
-    e1, off0 = gate((e1, off0.reshape(4, 256, B)))
-    e1 = over_z(e1)
-    fa, fb = shift(off0, "z", 1), shift(off0, "z", -1)
-    e0, fa, fb, e1, dinv2, off2, dinv3, rhs0 = gate((e0, fa, fb, e1, dinv2, off2, dinv3, rhs0))
-    m1 = gathered(e1, off1)
-
-    ea, eb = shift(e0, "z", 1), shift(e0, "z", -1)
+    e1 = over_z(for_z(e1_mine, e1_other, ci))
     e2 = dinv2.reshape(2, 256, B)
     e2 = ordered(pick(e2, ci)[None], flip(pick(e2, 1 - ci)[None], "core"), ci, 0)
-    e2 = over_z(for_z(e2, flip(e2, "x0"), x0))
+    e2_other = flip(e2, "x0")
+    e0, e1, e2, e2_other, off0, off2, dinv3, rhs0 = gate(
+        (e0, e1, e2, e2_other, off0.reshape(4, 256, B), off2, dinv3, rhs0)
+    )
+    m1 = gathered(e1, off1)
+
+    fa, fb = shift(off0, "z", 1), shift(off0, "z", -1)
+    ea, eb = shift(e0, "z", 1), shift(e0, "z", -1)
+    e2 = over_z(for_z(e2, e2_other, x0))
     f2 = joined(off2, 1)
     fc, fd = shift(fa[:2], "z", 1), shift(fb[2:], "z", -1)
     c0 = gather4(rhs0, "y")
-    e2[0], ea, eb, fc, fd, c0 = gate((e2[0], ea, eb, fc, fd, c0))
+    e2, f2, ea, eb, fc, fd, c0 = gate((e2, f2, ea, eb, fc, fd, c0))
+
     ec, ed = shift(ea[:2], "z", 1), shift(eb[2:], "z", -1)
+    m2 = gathered(e2, f2)
     e3 = joined(dinv3[None], 1)
     e3_other = flip(e3, "x1")
     b_mine, b_other = halves(jnp.concatenate([rhs1, rhs2, rhs3], 1), ci)
     b_other = flip(b_other, "core")
-    ec, ed, e2, f2, e3, e3_other, b_mine, b_other = gate(
-        (ec, ed, e2, f2, e3, e3_other, b_mine, b_other)
-    )
-    m2 = gathered(e2, f2)
+    ec, ed, e3, e3_other, b_mine, b_other = gate((ec, ed, e3, e3_other, b_mine, b_other))
     w0 = [e0, ea, eb, ec, ed, off0, fa, fb, fc, fd]
     e3 = over_z(for_z(e3, e3_other, x1))
     e3, b_mine = gate((e3, b_mine))
@@ -519,19 +519,16 @@
         top_kernel, "top", [(8, ORDER)], [ev, pltpu.VMEM((8, 512), f32), dma((8,))],
         meta, gather4(part, "z"), w3, flops(8),
     )
-    x3, give = call(
-        x3_kernel, "x3", [(8, ORDER), (8, 1024)], [pltpu.VMEM((1, 8, ORDER), f32)],
-        meta, gather4(part, "z"),
-    )
-    recv = flip(give, "x1")
+    (x3,) = call(x3_kernel, "x3", [(8, ORDER)], [], meta, gather4(part, "z"))
     x3r = flip(x3, "x1")
 
-    def rest(n, small):
-        return [ev, fv, pltpu.VMEM((n, 1024), f32), pltpu.VMEM((n // 2, 1024), f32), dma((12,))]
+    def rest(n):
+        rows = n if n != 16 else 8
+        return [ev, fv, pltpu.VMEM((rows, 1024), f32), pltpu.VMEM((n // 2, 1024), f32), dma((12,))]
 
     (part,) = call(
-        functools.partial(backward_kernel, 2, 16), "b2", [(16, ORDER)], rest(16, 0),
-        meta, [x3[None], recv, y2], w2, flops(16),
+        functools.partial(backward_kernel, 2, 16), "b2", [(16, ORDER)], rest(16),
+        meta, [x3[None], x3r[None], y2], w2, flops(16),
     )
     anc, give = call(
         x2_kernel, "x2", [(2, 16, ORDER), (16, 1024)], [],
@@ -541,7 +538,7 @@
     a_mine = anc[:, :4]
     a_other = flip(a_mine, "x0")
     parts = call(
-        functools.partial(backward_kernel, 1, 32), "b1", [(8, ORDER)] * 4, rest(32, 0),
+        functools.partial(backward_kernel, 1, 32), "b1", [(8, ORDER)] * 4, rest(32),
         meta, [anc, recv, y1], w1, flops(32),
     )
     anc, give, own = call(
@@ -550,7 +547,7 @@
     )
     g = ordered(own, flip(give, "core"), ci, 0)
     parts = call(
-        functools.partial(backward_kernel, 0, 64), "b0", [(16, ORDER)] * 4, rest(64, 0),
+        functools.partial(backward_kernel, 0, 64), "b0", [(16, ORDER)] * 4, rest(64),
         meta, gather4(g, "y") + [y0], w0, flops(64),
     )
     parts = scatter4(parts, "y")

time: 267 us -> 285 us (1.067)
  waiting for transfers between devices: 93.3 us -> 119 us
  starting transfers between devices: 101 us -> 94.9 us
    ppermute x47, waiting for transfers between devices: 68 us -> 86.7 us  [shift(): return lax.ppermute(v, axis, [(i, (i + s) % 4) for i in range(4)])]
    ppermute x23 -> x22, waiting for transfers between devices: 18.2 us -> 24.2 us  [flip(): return lax.ppermute(v, axis, [(0, 1), (1, 0)])]
    ppermute x23 -> x22, starting transfers between devices: 20.6 us -> 15.6 us  [flip(): return lax.ppermute(v, axis, [(0, 1), (1, 0)])]
    unnamed x45 -> x41, local copies, waits for them, and re-layouts: 6.95 us -> 6.86 us
  transfers between devices with their start and end apart: 74 -> 73, of which waited for: 37 -> 44; matrix products, arithmetic and copies ran while one was open for 4% -> 4% of each run, Pallas kernels for 10% -> 10%
where the time goes in v7:
time: 285 us; the launch traced here: 284 us
  waiting for transfers between devices  119 us (42%)
  starting transfers between devices  94.9 us (33%)
  Pallas kernels  38.5 us (14%)
  between operations  14.3 us (5%)
  local copies, waits for them, and re-layouts  13.7 us (5%)
  other arithmetic  3.76 us (1%)
    ppermute x47, waiting for transfers between devices, shift(): return lax.ppermute(v, axis, [(i, (i + s) % 4) for i in range(4)])  86.7 us
    ppermute x47, starting transfers between devices, shift(): return lax.ppermute(v, axis, [(i, (i + s) % 4) for i in range(4)])  74.5 us
    pallas_call x13, Pallas kernels, call(): pl.pallas_call(kernel, out_shape=[jax.ShapeDtypeStruct(s, f32) for s in s...  38.5 us
    ppermute x22, waiting for transfers between devices, flip(): return lax.ppermute(v, axis, [(0, 1), (1, 0)])  24.2 us
    ppermute x22, starting transfers between devices, flip(): return lax.ppermute(v, axis, [(0, 1), (1, 0)])  15.6 us
    all_gather x3, waiting for transfers between devices, gathered(): return lax.all_gather(jnp.concatenate(parts, 0), 'y', axis=0, tiled=False)  7.41 us
    unnamed x41, local copies, waits for them, and re-layouts  6.86 us
  transfers between devices with their start and end apart: 73, of which 44 were waited for; matrix products, arithmetic and copies ran while one was open for 4% of the time, Pallas kernels for 10%

profile of v7, /device:TPU:0, one launch (start us, length us, event | category | flops | bytes accessed | tf_op | source)
XLA Modules:
  0.0 284.5 jit_solution(7587839803748620903)
XLA Ops:
  8.4 2.3 copy.22
  10.7 4.7 %all-to-all-start = ((f32[4,512,128]{2,1,0:T(8,128)}), f32[4,512,128]{2,1,0:T(8,128)S(1)}, u32[]{:S(2)}, u32[]{:S(2)}) async-start(f32[4,512,128]{2,1,0:T(8,128)} %bitcast.3), calls=%async_computation | async-start | bytes 2097152 | tf_op jit(solution)/shard_map/all_to_all | solution.py:443
  16.9 1.6 collective-permute-start.5
  18.5 2.0 collective-permute-start.1
  20.5 3.6 %collective-permute-start.2 = (f32[256,128]{1,0:T(8,128)S(1)}, f32[256,128]{1,0:T(8,128)S(1)}, u32[]{:S(2)}, u32[]{:S(2)}) collective-permute-start(f32[256,128]{1,0:T(8,128)S(1)} %get-tuple-element.159), channel_id=1, source_target_pairs={{0,8},{4,12},{8,0},{12,4},{1,9},{5,13},{9,1},{13,5},{2,10},{6,14},... | collective-permute-start | bytes 393224 | tf_op jit(solution)/shard_map/ppermute | solution.py:39
  26.2 4.0 %collective-permute-done.2 = f32[256,128]{1,0:T(8,128)S(1)} collective-permute-done((f32[256,128]{1,0:T(8,128)S(1)}, f32[256,128]{1,0:T(8,128)S(1)}, u32[]{:S(2)}, u32[]{:S(2)}) %collective-permute-start.2) | collective-permute-done | bytes 131104 | tf_op jit(solution)/shard_map/ppermute | solution.py:39
  32.4 2.0 collective-permute-start.10
  34.4 2.2 collective-permute-start.11
  36.6 3.2 %collective-permute-start.14 = (f32[4,256,128]{2,1,0:T(8,128)}, f32[4,256,128]{2,1,0:T(8,128)}, u32[]{:S(2)}, u32[]{:S(2)}) collective-permute-start(f32[4,256,128]{2,1,0:T(8,128)} %bitcast.102), channel_id=1, source_target_pairs={{0,12},{4,0},{8,4},{12,8},{1,13},{5,1},{9,5},{13,9},{2,14},{6,2},{... | collective-permute-start | bytes 1572872 | tf_op jit(solution)/shard_map/ppermute | solution.py:39
  39.8 1.5 collective-permute-start.9
  41.4 3.4 %collective-permute-done.9 = f32[256,128]{1,0:T(8,128)S(1)} collective-permute-done((f32[256,128]{1,0:T(8,128)S(1)}, f32[256,128]{1,0:T(8,128)S(1)}, u32[]{:S(2)}, u32[]{:S(2)}) %collective-permute-start.9) | collective-permute-done | bytes 131104 | tf_op jit(solution)/shard_map/ppermute | solution.py:43
  44.8 28.5 %collective-permute-done.6 = f32[256,128]{1,0:T(8,128)S(1)} collective-permute-done((f32[256,128]{1,0:T(8,128)S(1)}, f32[256,128]{1,0:T(8,128)S(1)}, u32[]{:S(2)}, u32[]{:S(2)}) %collective-permute-start.6) | collective-permute-done | bytes 131104 | tf_op jit(solution)/shard_map/ppermute | solution.py:39
  73.2 1.6 collective-permute-start.7
  77.1 2.6 collective-permute-done.7
  80.8 1.4 collective-permute-start.13
  82.2 2.7 collective-permute-start.15
  87.4 3.8 %collective-permute-done.18.refs_3_ = f32[16,2048]{1,0:T(8,128)S(1)} collective-permute-done((f32[16,2048]{1,0:T(8,128)S(1)}, f32[16,2048]{1,0:T(8,128)S(1)}, u32[]{:S(2)}, u32[]{:S(2)}) %collective-permute-start.18) | collective-permute-done | bytes 131104 | tf_op jit(solution)/shard_map/ppermute | solution.py:39
  94.9 1.5 collective-permute-start.21
  97.2 3.7 %collective-permute-done.21 = f32[1,256,128]{2,1,0:T(8,128)S(1)} collective-permute-done((f32[1,256,128]{2,1,0:T(8,128)S(1)}, f32[1,256,128]{2,1,0:T(8,128)S(1)}, u32[]{:S(2)}, u32[]{:S(2)}) %collective-permute-start.21) | collective-permute-done | bytes 131104 | tf_op jit(solution)/shard_map/ppermute | solution.py:43
  100.9 3.4 %collective-permute-start.22 = (f32[2,256,128]{2,1,0:T(8,128)S(1)}, f32[2,256,128]{2,1,0:T(8,128)S(1)}, u32[]{:S(2)}, u32[]{:S(2)}) collective-permute-start(f32[2,256,128]{2,1,0:T(8,128)S(1)} %maximum_select_fusion.2), channel_id=1, source_target_pairs={{0,64},{64,0},{1,65},{65,1},{2,66},{66,2},{3,67},{67,3},{4,68},{68... | collective-permute-start | bytes 786440 | tf_op jit(solution)/shard_map/ppermute | solution.py:43
  107.2 2.7 collective-permute-start.20
  111.2 4.8 %collective-permute-done.19.refs_7_.refs_8_ = f32[2,512,128]{2,1,0:T(8,128)} collective-permute-done((f32[2,512,128]{2,1,0:T(8,128)S(1)}, f32[2,512,128]{2,1,0:T(8,128)}, u32[]{:S(2)}, u32[]{:S(2)}) %collective-permute-start.19) | collective-permute-done | bytes 524320 | tf_op jit(solution)/shard_map/ppermute | solution.py:39
  116.6 5.8 %f0.1 = (f32[64,512]{1,0:T(8,128)S(1)}, f32[16,1024]{1,0:T(8,128)S(1)}, f32[16,1024]{1,0:T(8,128)S(1)}, f32[16,1024]{1,0:T(8,128)S(1)}, f32[16,1024]{1,0:T(8,128)S(1)}) custom-call(s32[128]{0:T(128)S(1)} %pad_add_fusion.meta, f32[16,2048]{1,0:T(8,128)S(1)} %copy-done, f32[16,2048]{1,0:T(8,128)S(1)} %collective-permute-done.16.refs_1_, ...), custom_call_target="tpu_custom_call" | custom-call | flops 2415919104 | bytes 6815744 | tf_op jit(solution)/shard_map/f0/pallas_call | solution.py:395
  122.5 2.6 collective-permute-start.24
  126.4 1.4 collective-permute-start.28
  127.8 1.4 collective-permute-done.24
  129.2 2.9 %collective-permute-start.29 = (f32[256,128]{1,0:T(8,128)S(1)}, f32[256,128]{1,0:T(8,128)S(1)}, u32[]{:S(2)}, u32[]{:S(2)}) collective-permute-start(f32[256,128]{1,0:T(8,128)S(1)} %get-tuple-element.151), channel_id=1, source_target_pairs={{0,8},{4,12},{8,0},{12,4},{1,9},{5,13},{9,1},{13,5},{2,10},{6,14},... | collective-permute-start | bytes 393224 | tf_op jit(solution)/shard_map/ppermute | solution.py:39
  133.0 3.7 %collective-permute-start.30 = (f32[256,128]{1,0:T(8,128)S(1)}, f32[256,128]{1,0:T(8,128)S(1)}, u32[]{:S(2)}, u32[]{:S(2)}) collective-permute-start(f32[256,128]{1,0:T(8,128)S(1)} %get-tuple-element.150), channel_id=1, source_target_pairs={{0,12},{4,0},{8,4},{12,8},{1,13},{5,1},{9,5},{13,9},{2,14},{6,2},{... | collective-permute-start | bytes 393224 | tf_op jit(solution)/shard_map/ppermute | solution.py:39
  137.8 1.6 collective-permute-done.30
  140.6 4.8 %collective-permute-start.32 = (f32[8,2048]{1,0:T(8,128)S(1)}, f32[8,2048]{1,0:T(8,128)S(1)}, u32[]{:S(2)}, u32[]{:S(2)}) collective-permute-start(f32[8,2048]{1,0:T(8,128)S(1)} %get-tuple-element.108.refs_0_), channel_id=1, source_target_pairs={{0,8},{4,12},{8,0},{12,4},{1,9},{5,13},{9,1},{13,5},{2,10},{6,14},... | collective-permute-start | bytes 196616 | tf_op jit(solution)/shard_map/ppermute | solution.py:39
  145.4 1.5 collective-permute-done.31.refs_1_
  146.8 1.5 collective-permute-done.32.refs_2_
  149.6 4.9 %f1.1 = (f32[32,512]{1,0:T(8,128)S(1)}, f32[16,1024]{1,0:T(8,128)S(1)}, f32[16,1024]{1,0:T(8,128)S(1)}) custom-call(s32[128]{0:T(128)S(1)} %pad_add_fusion.meta, f32[8,2048]{1,0:T(8,128)S(1)} %get-tuple-element.108.refs_0_, f32[8,2048]{1,0:T(8,128)S(1)} %collective-permute-done.31.refs_1_, f32[8,2048]{1,0:T(8,128)S(1)} %collective-permute-done.32.refs_2_, ...), custom_call_target="tpu_custom_call" | custom-call | flops 1207959552 | bytes 6553600 | tf_op jit(solution)/shard_map/f1/pallas_call | solution.py:395
  154.7 4.2 %collective-permute-done.35.recv = f32[16,1024]{1,0:T(8,128)S(1)} collective-permute-done((f32[16,1024]{1,0:T(8,128)S(1)}, f32[16,1024]{1,0:T(8,128)S(1)}, u32[]{:S(2)}, u32[]{:S(2)}) %collective-permute-start.35) | collective-permute-done | bytes 65568 | tf_op jit(solution)/shard_map/ppermute | solution.py:43
  160.7 2.8 collective-permute-start.38
  165.0 5.6 %collective-permute-done.37.refs_1_ = f32[16,2048]{1,0:T(8,128)S(1)} collective-permute-done((f32[16,2048]{1,0:T(8,128)S(1)}, f32[16,2048]{1,0:T(8,128)S(1)}, u32[]{:S(2)}, u32[]{:S(2)}) %collective-permute-start.37) | collective-permute-done | bytes 131104 | tf_op jit(solution)/shard_map/ppermute | solution.py:39
  171.3 4.7 %f2.1 = (f32[16,512]{1,0:T(8,128)S(1)}, f32[8,1024]{1,0:T(8,128)S(1)}, f32[8,1024]{1,0:T(8,128)S(1)}) custom-call(s32[128]{0:T(128)S(1)} %pad_add_fusion.meta, f32[16,2048]{1,0:T(8,128)S(1)} %get-tuple-element.119.refs_0_, f32[16,2048]{1,0:T(8,128)S(1)} %collective-permute-done.37.refs_1_, f32[16,2048]{1,0:T(8,128)S(1)} %collective-permute-done.38.refs_2_, ...), custom_call_target="tpu_custom_call" | custom-call | flops 603979776 | bytes 6815744 | tf_op jit(solution)/shard_map/f2/pallas_call | solution.py:395
  176.3 5.1 %collective-permute-done.41.recv = f32[8,1024]{1,0:T(8,128)S(1)} collective-permute-done((f32[8,1024]{1,0:T(8,128)S(1)}, f32[8,1024]{1,0:T(8,128)S(1)}, u32[]{:S(2)}, u32[]{:S(2)}) %collective-permute-start.41) | collective-permute-done | bytes 32800 | tf_op jit(solution)/shard_map/ppermute | solution.py:43
  182.1 7.4 %all-gather.11.cloned.1.call-done = f32[16,256,128]{2,1,0:T(8,128)} async-done(((f32[4,256,128]{2,1,0:T(8,128)}), f32[16,256,128]{2,1,0:T(8,128)}) %all-gather.11.cloned.1.call-update) | async-done | bytes 2097168 | tf_op jit(solution)/shard_map/all_gather | solution.py:436
  189.5 1.6 collective-permute-start.43
  191.1 2.9 %collective-permute-start.44 = (f32[8,2048]{1,0:T(8,128)S(1)}, f32[8,2048]{1,0:T(8,128)S(1)}, u32[]{:S(2)}, u32[]{:S(2)}) collective-permute-start(f32[8,2048]{1,0:T(8,128)S(1)} %s23.1.c0), channel_id=1, source_target_pairs={{0,8},{4,12},{8,0},{12,4},{1,9},{5,13},{9,1},{13,5},{2,10},{6,14},... | collective-permute-start | bytes 196616 | tf_op jit(solution)/shard_map/ppermute | solution.py:39
  195.3 2.5 collective-permute-done.44.c2
  199.5 4.6 %top.1.c0 = f32[8,2048]{1,0:T(8,128)S(1)} custom-call(s32[128]{0:T(128)S(1)} %pad_add_fusion.meta, f32[8,2048]{1,0:T(8,128)S(1)} %s23.1.c0, f32[8,2048]{1,0:T(8,128)S(1)} %collective-permute-done.43.c1, f32[8,2048]{1,0:T(8,128)S(1)} %collective-permute-done.44.c2, f32[8,2048]{1,0:T(8,128)S(1)} %collective-permute-done.45.c3, f32[4,4,256,128]{3,2,1,0:T(8,128)} %bitcast.89, ...), custom_call_target="tpu_custom_call" | custom-call | flops 301989888 | bytes 4456448 | tf_op jit(solution)/shard_map/top/pallas_call | solution.py:395
  205.1 3.2 %collective-permute-start.48 = (f32[8,2048]{1,0:T(8,128)S(1)}, f32[8,2048]{1,0:T(8,128)S(1)}, u32[]{:S(2)}, u32[]{:S(2)}) collective-permute-start(f32[8,2048]{1,0:T(8,128)S(1)} %top.1.c0), channel_id=1, source_target_pairs={{0,8},{4,12},{8,0},{12,4},{1,9},{5,13},{9,1},{13,5},{2,10},{6,14},... | collective-permute-start | bytes 196616 | tf_op jit(solution)/shard_map/ppermute | solution.py:39
  209.8 1.5 collective-permute-done.48.c2
  213.2 3.1 %collective-permute-start.50 = (f32[8,2048]{1,0:T(8,128)S(1)}, f32[8,2048]{1,0:T(8,128)S(1)}, u32[]{:S(2)}, u32[]{:S(2)}) collective-permute-start(f32[8,2048]{1,0:T(8,128)S(1)} %x3.1), channel_id=1, source_target_pairs={{0,64},{64,0},{1,65},{65,1},{2,66},{66,2},{3,67},{67,3},{4,68},{68... | collective-permute-start | bytes 196616 | tf_op jit(solution)/shard_map/ppermute | solution.py:43
  216.2 2.8 collective-permute-done.50.x3r
  219.0 4.7 %b2.1.c0 = f32[16,2048]{1,0:T(8,128)S(1)} custom-call(s32[128]{0:T(128)S(1)} %pad_add_fusion.meta, f32[1,8,2048]{2,1,0:T(8,128)S(1)} %bitcast.80, f32[1,8,2048]{2,1,0:T(8,128)S(1)} %bitcast.81, f32[16,512]{1,0:T(8,128)S(1)} %get-tuple-element.135.refs_2_, f32[4,6,256,128]{3,2,1,0:T(8,128)} %bitcast.87, f32[4,6,256,128]{3,2,1,0:T(8,128)} %collective-permute-done.40.refs_5_.refs_4_), custom_call_target="tpu_custom_call" | custom-call | flops 603979776 | bytes 6455296 | tf_op jit(solution)/shard_map/b2/pallas_call | solution.py:395
  224.1 3.1 %collective-permute-start.52 = (f32[16,2048]{1,0:T(8,128)S(1)}, f32[16,2048]{1,0:T(8,128)S(1)}, u32[]{:S(2)}, u32[]{:S(2)}) collective-permute-start(f32[16,2048]{1,0:T(8,128)S(1)} %b2.1.c0), channel_id=1, source_target_pairs={{0,8},{4,12},{8,0},{12,4},{1,9},{5,13},{9,1},{13,5},{2,10},{6,14},... | collective-permute-start | bytes 393224 | tf_op jit(solution)/shard_map/ppermute | solution.py:39
  228.0 2.0 collective-permute-done.51.c1
  230.0 1.6 collective-permute-done.52.c2
  232.9 1.5 collective-permute-start.54
  235.1 2.1 collective-permute-done.54.refs_1_
  237.3 4.8 %b1.1 = (f32[8,2048]{1,0:T(8,128)S(1)}, f32[8,2048]{1,0:T(8,128)S(1)}, f32[8,2048]{1,0:T(8,128)S(1)}, f32[8,2048]{1,0:T(8,128)S(1)}) custom-call(s32[128]{0:T(128)S(1)} %pad_add_fusion.meta, f32[2,16,2048]{2,1,0:T(8,128)S(1)} %get-tuple-element.136.refs_0_, f32[16,1024]{1,0:T(8,128)S(1)} %collective-permute-done.54.refs_1_, ...), custom_call_target="tpu_custom_call" | custom-call | flops 1207959552 | bytes 6684672 | tf_op jit(solution)/shard_map/b1/pallas_call | solution.py:395
  242.1 2.7 collective-permute-start.55
  245.8 1.6 collective-permute-done.55.c1
  247.4 3.3 %collective-permute-done.56.c2 = f32[8,2048]{1,0:T(8,128)S(1)} collective-permute-done((f32[8,2048]{1,0:T(8,128)S(1)}, f32[8,2048]{1,0:T(8,128)S(1)}, u32[]{:S(2)}, u32[]{:S(2)}) %collective-permute-start.56) | collective-permute-done | bytes 65568 | tf_op jit(solution)/shard_map/ppermute | solution.py:39
  254.4 1.8 collective-permute-start.61
  256.2 2.1 collective-permute-start.62
  258.9 1.8 collective-permute-done.60.refs_1_
  261.2 4.9 %b0.1 = (f32[16,2048]{1,0:T(8,128)S(1)}, f32[16,2048]{1,0:T(8,128)S(1)}, f32[16,2048]{1,0:T(8,128)S(1)}, f32[16,2048]{1,0:T(8,128)S(1)}) custom-call(s32[128]{0:T(128)S(1)} %pad_add_fusion.meta, f32[16,1024]{1,0:T(8,128)S(1)} %maximum_select_fusion.3.refs_0_, f32[16,1024]{1,0:T(8,128)S(1)} %collective-permute-done.60.refs_1_, ...), custom_call_target="tpu_custom_call" | custom-call | flops 2415919104 | bytes 6684672 | tf_op jit(solution)/shard_map/b0/pallas_call | solution.py:395
  266.1 2.7 collective-permute-start.63
  271.1 2.5 collective-permute-done.63
  273.6 2.4 collective-permute-done.64
  (171 shorter events, 53.1 us)
Async XLA Ops:
  10.7 20.4 %all-to-all-start = ((f32[4,512,128]{2,1,0:T(8,128)}), f32[4,512,128]{2,1,0:T(8,128)S(1)}, u32[]{:S(2)}, u32[]{:S(2)}) async-start(f32[4,512,128]{2,1,0:T(8,128)} %bitcast.3), calls=%async_computation | async-start | bytes 2097152 | tf_op jit(solution)/shard_map/all_to_all | solution.py:443
  15.4 107.0 %all-gather.7.cloned.1.call-start = ((), (), s32[]{:S(2)}) async-start(), calls=%async_computation.1 | async-start | bytes 3932160 | tf_op jit(solution)/shard_map/all_gather | solution.py:436
  16.9 13.3 %collective-permute-start.5 = (f32[2,256,128]{2,1,0:T(8,128)S(1)}, f32[2,256,128]{2,1,0:T(8,128)S(1)}, u32[]{:S(2)}, u32[]{:S(2)}) collective-permute-start(f32[2,256,128]{2,1,0:T(8,128)S(1)} %maximum_select_fusion), channel_id=1, source_target_pairs={{0,32},{32,0},{1,33},{33,1},{2,34},{34,2},{3,35},{35,3},{4,36},{36... | collective-permute-start | bytes 786440 | tf_op jit(solution)/shard_map/ppermute | solution.py:43
  18.5 7.7 %collective-permute-start.1 = (f32[256,128]{1,0:T(8,128)S(1)}, f32[256,128]{1,0:T(8,128)S(1)}, u32[]{:S(2)}, u32[]{:S(2)}) collective-permute-start(f32[256,128]{1,0:T(8,128)S(1)} %get-tuple-element.160), channel_id=1, source_target_pairs={{0,4},{4,8},{8,12},{12,0},{1,5},{5,9},{9,13},{13,1},{2,6},{6,10},{... | collective-permute-start | bytes 393224 | tf_op jit(solution)/shard_map/ppermute | solution.py:39
  20.5 9.7 %collective-permute-start.2 = (f32[256,128]{1,0:T(8,128)S(1)}, f32[256,128]{1,0:T(8,128)S(1)}, u32[]{:S(2)}, u32[]{:S(2)}) collective-permute-start(f32[256,128]{1,0:T(8,128)S(1)} %get-tuple-element.159), channel_id=1, source_target_pairs={{0,8},{4,12},{8,0},{12,4},{1,9},{5,13},{9,1},{13,5},{2,10},{6,14},... | collective-permute-start | bytes 393224 | tf_op jit(solution)/shard_map/ppermute | solution.py:39
  24.1 6.1 %collective-permute-start.3 = (f32[256,128]{1,0:T(8,128)S(1)}, f32[256,128]{1,0:T(8,128)S(1)}, u32[]{:S(2)}, u32[]{:S(2)}) collective-permute-start(f32[256,128]{1,0:T(8,128)S(1)} %get-tuple-element.158), channel_id=1, source_target_pairs={{0,12},{4,0},{8,4},{12,8},{1,13},{5,1},{9,5},{13,9},{2,14},{6,2},{... | collective-permute-start | bytes 393224 | tf_op jit(solution)/shard_map/ppermute | solution.py:39
  32.3 127.4 %all-gather.9.cloned.1.call-start = ((), (), s32[]{:S(2)}) async-start(), calls=%async_computation.2 | async-start | bytes 3932160 | tf_op jit(solution)/shard_map/all_gather | solution.py:436
  32.4 58.8 %collective-permute-start.10 = (f32[4,512,128]{2,1,0:T(8,128)S(1)}, f32[4,512,128]{2,1,0:T(8,128)}, u32[]{:S(2)}, u32[]{:S(2)}) collective-permute-start(f32[4,512,128]{2,1,0:T(8,128)S(1)} %all-to-all-done.refs_4_.refs_5_), channel_id=1, source_target_pairs={{0,4},{4,8},{8,12},{12,0},{1,5},{5,9},{9,13},{13,1},{2,6},{6,10},{... | collective-permute-start | bytes 3145736 | tf_op jit(solution)/shard_map/ppermute | solution.py:39
  34.4 56.8 %collective-permute-start.11 = (f32[4,512,128]{2,1,0:T(8,128)S(1)}, f32[4,512,128]{2,1,0:T(8,128)}, u32[]{:S(2)}, u32[]{:S(2)}) collective-permute-start(f32[4,512,128]{2,1,0:T(8,128)S(1)} %all-to-all-done.refs_4_.refs_5_), channel_id=1, source_target_pairs={{0,12},{4,0},{8,4},{12,8},{1,13},{5,1},{9,5},{13,9},{2,14},{6,2},{... | collective-permute-start | bytes 3145736 | tf_op jit(solution)/shard_map/ppermute | solution.py:39
  36.6 38.3 %collective-permute-start.12 = (f32[4,256,128]{2,1,0:T(8,128)}, f32[4,256,128]{2,1,0:T(8,128)S(1)}, u32[]{:S(2)}, u32[]{:S(2)}) collective-permute-start(f32[4,256,128]{2,1,0:T(8,128)} %bitcast.101), channel_id=1, source_target_pairs={{0,4},{4,8},{8,12},{12,0},{1,5},{5,9},{9,13},{13,1},{2,6},{6,10},{... | collective-permute-start | bytes 1572872 | tf_op jit(solution)/shard_map/ppermute | solution.py:39
  36.6 39.0 %collective-permute-start.14 = (f32[4,256,128]{2,1,0:T(8,128)}, f32[4,256,128]{2,1,0:T(8,128)}, u32[]{:S(2)}, u32[]{:S(2)}) collective-permute-start(f32[4,256,128]{2,1,0:T(8,128)} %bitcast.102), channel_id=1, source_target_pairs={{0,12},{4,0},{8,4},{12,8},{1,13},{5,1},{9,5},{13,9},{2,14},{6,2},{... | collective-permute-start | bytes 1572872 | tf_op jit(solution)/shard_map/ppermute | solution.py:39
  39.8 5.0 %collective-permute-start.9 = (f32[256,128]{1,0:T(8,128)S(1)}, f32[256,128]{1,0:T(8,128)S(1)}, u32[]{:S(2)}, u32[]{:S(2)}) collective-permute-start(f32[256,128]{1,0:T(8,128)S(1)} %copy-done.7), channel_id=1, source_target_pairs={{0,32},{32,0},{1,33},{33,1},{2,34},{34,2},{3,35},{35,3},{4,36},{36... | collective-permute-start | bytes 393224 | tf_op jit(solution)/shard_map/ppermute | solution.py:43
  44.8 28.5 %collective-permute-start.6 = (f32[256,128]{1,0:T(8,128)S(1)}, f32[256,128]{1,0:T(8,128)S(1)}, u32[]{:S(2)}, u32[]{:S(2)}) collective-permute-start(f32[256,128]{1,0:T(8,128)S(1)} %get-tuple-element.156), channel_id=1, source_target_pairs={{0,4},{4,8},{8,12},{12,0},{1,5},{5,9},{9,13},{13,1},{2,6},{6,10},{... | collective-permute-start | bytes 393224 | tf_op jit(solution)/shard_map/ppermute | solution.py:39
  73.2 6.5 %collective-permute-start.7 = (f32[256,128]{1,0:T(8,128)S(1)}, f32[256,128]{1,0:T(8,128)S(1)}, u32[]{:S(2)}, u32[]{:S(2)}) collective-permute-start(f32[256,128]{1,0:T(8,128)S(1)} %get-tuple-element.155), channel_id=1, source_target_pairs={{0,8},{4,12},{8,0},{12,4},{1,9},{5,13},{9,1},{13,5},{2,10},{6,14},... | collective-permute-start | bytes 393224 | tf_op jit(solution)/shard_map/ppermute | solution.py:39
  74.8 6.0 %collective-permute-start.8 = (f32[256,128]{1,0:T(8,128)S(1)}, f32[256,128]{1,0:T(8,128)S(1)}, u32[]{:S(2)}, u32[]{:S(2)}) collective-permute-start(f32[256,128]{1,0:T(8,128)S(1)} %get-tuple-element.154), channel_id=1, source_target_pairs={{0,12},{4,0},{8,4},{12,8},{1,13},{5,1},{9,5},{13,9},{2,14},{6,2},{... | collective-permute-start | bytes 393224 | tf_op jit(solution)/shard_map/ppermute | solution.py:39
  75.6 6.7 %collective-permute-start.16 = (f32[16,2048]{1,0:T(8,128)S(1)}, f32[16,2048]{1,0:T(8,128)S(1)}, u32[]{:S(2)}, u32[]{:S(2)}) collective-permute-start(f32[16,2048]{1,0:T(8,128)S(1)} %copy-done), channel_id=1, source_target_pairs={{0,1},{1,2},{2,3},{3,0},{4,5},{5,6},{6,7},{7,4},{8,9},{9,10},{10,1... | collective-permute-start | bytes 393224 | tf_op jit(solution)/shard_map/ppermute | solution.py:39
  79.7 6.5 %collective-permute-start.17 = (f32[16,2048]{1,0:T(8,128)S(1)}, f32[16,2048]{1,0:T(8,128)S(1)}, u32[]{:S(2)}, u32[]{:S(2)}) collective-permute-start(f32[16,2048]{1,0:T(8,128)S(1)} %copy-done), channel_id=1, source_target_pairs={{0,2},{1,3},{2,0},{3,1},{4,6},{5,7},{6,4},{7,5},{8,10},{9,11},{10,... | collective-permute-start | bytes 393224 | tf_op jit(solution)/shard_map/ppermute | solution.py:39
  80.8 10.4 %collective-permute-start.13 = (f32[2,256,128]{2,1,0:T(8,128)S(1)}, f32[2,256,128]{2,1,0:T(8,128)}, u32[]{:S(2)}, u32[]{:S(2)}) collective-permute-start(f32[2,256,128]{2,1,0:T(8,128)S(1)} %slice.55), channel_id=1, source_target_pairs={{0,4},{4,8},{8,12},{12,0},{1,5},{5,9},{9,13},{13,1},{2,6},{6,10},{... | collective-permute-start | bytes 786440 | tf_op jit(solution)/shard_map/ppermute | solution.py:39
  82.2 8.9 %collective-permute-start.15 = (f32[2,256,128]{2,1,0:T(8,128)S(1)}, f32[2,256,128]{2,1,0:T(8,128)}, u32[]{:S(2)}, u32[]{:S(2)}) collective-permute-start(f32[2,256,128]{2,1,0:T(8,128)S(1)} %slice.56), channel_id=1, source_target_pairs={{0,12},{4,0},{8,4},{12,8},{1,13},{5,1},{9,5},{13,9},{2,14},{6,2},{... | collective-permute-start | bytes 786440 | tf_op jit(solution)/shard_map/ppermute | solution.py:39
  86.2 5.0 %collective-permute-start.18 = (f32[16,2048]{1,0:T(8,128)S(1)}, f32[16,2048]{1,0:T(8,128)S(1)}, u32[]{:S(2)}, u32[]{:S(2)}) collective-permute-start(f32[16,2048]{1,0:T(8,128)S(1)} %copy-done), channel_id=1, source_target_pairs={{0,3},{1,0},{2,1},{3,2},{4,7},{5,4},{6,5},{7,6},{8,11},{9,8},{10,9... | collective-permute-start | bytes 393224 | tf_op jit(solution)/shard_map/ppermute | solution.py:39
  94.0 95.5 %all-gather.11.cloned.1.call-start = ((), (), s32[]{:S(2)}) async-start(), calls=%async_computation.3 | async-start | bytes 2621440 | tf_op jit(solution)/shard_map/all_gather | solution.py:436
  94.9 6.0 %collective-permute-start.21 = (f32[1,256,128]{2,1,0:T(8,128)S(1)}, f32[1,256,128]{2,1,0:T(8,128)S(1)}, u32[]{:S(2)}, u32[]{:S(2)}) collective-permute-start(f32[1,256,128]{2,1,0:T(8,128)S(1)} %bitcast.96), channel_id=1, source_target_pairs={{0,32},{32,0},{1,33},{33,1},{2,34},{34,2},{3,35},{35,3},{4,36},{36... | collective-permute-start | bytes 393224 | tf_op jit(solution)/shard_map/ppermute | solution.py:43
  100.9 10.3 %collective-permute-start.22 = (f32[2,256,128]{2,1,0:T(8,128)S(1)}, f32[2,256,128]{2,1,0:T(8,128)S(1)}, u32[]{:S(2)}, u32[]{:S(2)}) collective-permute-start(f32[2,256,128]{2,1,0:T(8,128)S(1)} %maximum_select_fusion.2), channel_id=1, source_target_pairs={{0,64},{64,0},{1,65},{65,1},{2,66},{66,2},{3,67},{67,3},{4,68},{68... | collective-permute-start | bytes 786440 | tf_op jit(solution)/shard_map/ppermute | solution.py:43
  105.4 10.6 %collective-permute-start.19 = (f32[2,512,128]{2,1,0:T(8,128)S(1)}, f32[2,512,128]{2,1,0:T(8,128)}, u32[]{:S(2)}, u32[]{:S(2)}) collective-permute-start(f32[2,512,128]{2,1,0:T(8,128)S(1)} %slice.45), channel_id=1, source_target_pairs={{0,4},{4,8},{8,12},{12,0},{1,5},{5,9},{9,13},{13,1},{2,6},{6,10},{... | collective-permute-start | bytes 1572872 | tf_op jit(solution)/shard_map/ppermute | solution.py:39
  107.2 9.4 %collective-permute-start.20 = (f32[2,512,128]{2,1,0:T(8,128)S(1)}, f32[2,512,128]{2,1,0:T(8,128)}, u32[]{:S(2)}, u32[]{:S(2)}) collective-permute-start(f32[2,512,128]{2,1,0:T(8,128)S(1)} %slice.46), channel_id=1, source_target_pairs={{0,12},{4,0},{8,4},{12,8},{1,13},{5,1},{9,5},{13,9},{2,14},{6,2},{... | collective-permute-start | bytes 1572872 | tf_op jit(solution)/shard_map/ppermute | solution.py:39
  122.4 27.2 %collective-permute-start.34 = (f32[4,6,256,128]{3,2,1,0:T(8,128)}, f32[4,6,256,128]{3,2,1,0:T(8,128)}, u32[]{:S(2)}, u32[]{:S(2)}) collective-permute-start(f32[4,6,256,128]{3,2,1,0:T(8,128)} %bitcast.82), channel_id=1, source_target_pairs={{0,16},{16,0},{1,17},{17,1},{2,18},{18,2},{3,19},{19,3},{4,20},{20... | collective-permute-start | bytes 9437192 | tf_op jit(solution)/shard_map/ppermute | solution.py:43
  122.5 6.7 %collective-permute-start.24 = (f32[16,1024]{1,0:T(8,128)S(1)}, f32[16,1024]{1,0:T(8,128)S(1)}, u32[]{:S(2)}, u32[]{:S(2)}) collective-permute-start(f32[16,1024]{1,0:T(8,128)S(1)} %get-tuple-element.100), channel_id=1, source_target_pairs={{0,3},{1,0},{2,1},{3,2},{4,7},{5,4},{6,5},{7,6},{8,11},{9,8},{10,9... | collective-permute-start | bytes 196616 | tf_op jit(solution)/shard_map/ppermute | solution.py:39
  125.1 7.8 %collective-permute-start.25 = (f32[16,1024]{1,0:T(8,128)S(1)}, f32[16,1024]{1,0:T(8,128)S(1)}, u32[]{:S(2)}, u32[]{:S(2)}) collective-permute-start(f32[16,1024]{1,0:T(8,128)S(1)} %get-tuple-element.101), channel_id=1, source_target_pairs={{0,2},{1,3},{2,0},{3,1},{4,6},{5,7},{6,4},{7,5},{8,10},{9,11},{10,... | collective-permute-start | bytes 196616 | tf_op jit(solution)/shard_map/ppermute | solution.py:39
  126.3 10.4 %collective-permute-start.26 = (f32[16,1024]{1,0:T(8,128)S(1)}, f32[16,1024]{1,0:T(8,128)S(1)}, u32[]{:S(2)}, u32[]{:S(2)}) collective-permute-start(f32[16,1024]{1,0:T(8,128)S(1)} %get-tuple-element.102), channel_id=1, source_target_pairs={{0,1},{1,2},{2,3},{3,0},{4,5},{5,6},{6,7},{7,4},{8,9},{9,10},{10,1... | collective-permute-start | bytes 196616 | tf_op jit(solution)/shard_map/ppermute | solution.py:39
  126.4 10.4 %collective-permute-start.28 = (f32[256,128]{1,0:T(8,128)S(1)}, f32[256,128]{1,0:T(8,128)S(1)}, u32[]{:S(2)}, u32[]{:S(2)}) collective-permute-start(f32[256,128]{1,0:T(8,128)S(1)} %get-tuple-element.152), channel_id=1, source_target_pairs={{0,4},{4,8},{8,12},{12,0},{1,5},{5,9},{9,13},{13,1},{2,6},{6,10},{... | collective-permute-start | bytes 393224 | tf_op jit(solution)/shard_map/ppermute | solution.py:39
  129.2 8.6 %collective-permute-start.29 = (f32[256,128]{1,0:T(8,128)S(1)}, f32[256,128]{1,0:T(8,128)S(1)}, u32[]{:S(2)}, u32[]{:S(2)}) collective-permute-start(f32[256,128]{1,0:T(8,128)S(1)} %get-tuple-element.151), channel_id=1, source_target_pairs={{0,8},{4,12},{8,0},{12,4},{1,9},{5,13},{9,1},{13,5},{2,10},{6,14},... | collective-permute-start | bytes 393224 | tf_op jit(solution)/shard_map/ppermute | solution.py:39
  133.0 6.5 %collective-permute-start.30 = (f32[256,128]{1,0:T(8,128)S(1)}, f32[256,128]{1,0:T(8,128)S(1)}, u32[]{:S(2)}, u32[]{:S(2)}) collective-permute-start(f32[256,128]{1,0:T(8,128)S(1)} %get-tuple-element.150), channel_id=1, source_target_pairs={{0,12},{4,0},{8,4},{12,8},{1,13},{5,1},{9,5},{13,9},{2,14},{6,2},{... | collective-permute-start | bytes 393224 | tf_op jit(solution)/shard_map/ppermute | solution.py:39
  140.1 6.7 %collective-permute-start.31 = (f32[8,2048]{1,0:T(8,128)S(1)}, f32[8,2048]{1,0:T(8,128)S(1)}, u32[]{:S(2)}, u32[]{:S(2)}) collective-permute-start(f32[8,2048]{1,0:T(8,128)S(1)} %get-tuple-element.108.refs_0_), channel_id=1, source_target_pairs={{0,4},{4,8},{8,12},{12,0},{1,5},{5,9},{9,13},{13,1},{2,6},{6,10},{... | collective-permute-start | bytes 196616 | tf_op jit(solution)/shard_map/ppermute | solution.py:39
  140.6 7.7 %collective-permute-start.32 = (f32[8,2048]{1,0:T(8,128)S(1)}, f32[8,2048]{1,0:T(8,128)S(1)}, u32[]{:S(2)}, u32[]{:S(2)}) collective-permute-start(f32[8,2048]{1,0:T(8,128)S(1)} %get-tuple-element.108.refs_0_), channel_id=1, source_target_pairs={{0,8},{4,12},{8,0},{12,4},{1,9},{5,13},{9,1},{13,5},{2,10},{6,14},... | collective-permute-start | bytes 196616 | tf_op jit(solution)/shard_map/ppermute | solution.py:39
  145.4 9.3 %collective-permute-start.36 = (f32[2,4,2048]{2,1,0:T(4,128)S(1)}, f32[2,4,2048]{2,1,0:T(4,128)S(1)}, u32[]{:S(2)}, u32[]{:S(2)}) collective-permute-start(f32[2,4,2048]{2,1,0:T(4,128)S(1)} %get-tuple-element.118), channel_id=1, source_target_pairs={{0,32},{32,0},{1,33},{33,1},{2,34},{34,2},{3,35},{35,3},{4,36},{36... | collective-permute-start | bytes 196616 | tf_op jit(solution)/shard_map/ppermute | solution.py:43
  154.6 4.3 %collective-permute-start.35 = (f32[16,1024]{1,0:T(8,128)S(1)}, f32[16,1024]{1,0:T(8,128)S(1)}, u32[]{:S(2)}, u32[]{:S(2)}) collective-permute-start(f32[16,1024]{1,0:T(8,128)S(1)} %get-tuple-element.116), channel_id=1, source_target_pairs={{0,32},{32,0},{1,33},{33,1},{2,34},{34,2},{3,35},{35,3},{4,36},{36... | collective-permute-start | bytes 196616 | tf_op jit(solution)/shard_map/ppermute | solution.py:43
  159.7 11.6 %collective-permute-start.40 = (f32[4,6,256,128]{3,2,1,0:T(8,128)}, f32[4,6,256,128]{3,2,1,0:T(8,128)}, u32[]{:S(2)}, u32[]{:S(2)}) collective-permute-start(f32[4,6,256,128]{3,2,1,0:T(8,128)} %bitcast.85), channel_id=1, source_target_pairs={{0,16},{16,0},{1,17},{17,1},{2,18},{18,2},{3,19},{19,3},{4,20},{20... | collective-permute-start | bytes 9437192 | tf_op jit(solution)/shard_map/ppermute | solution.py:43
  160.7 10.0 %collective-permute-start.37 = (f32[16,2048]{1,0:T(8,128)S(1)}, f32[16,2048]{1,0:T(8,128)S(1)}, u32[]{:S(2)}, u32[]{:S(2)}) collective-permute-start(f32[16,2048]{1,0:T(8,128)S(1)} %get-tuple-element.119.refs_0_), channel_id=1, source_target_pairs={{0,4},{4,8},{8,12},{12,0},{1,5},{5,9},{9,13},{13,1},{2,6},{6,10},{... | collective-permute-start | bytes 393224 | tf_op jit(solution)/shard_map/ppermute | solution.py:39
  160.7 9.9 %collective-permute-start.38 = (f32[16,2048]{1,0:T(8,128)S(1)}, f32[16,2048]{1,0:T(8,128)S(1)}, u32[]{:S(2)}, u32[]{:S(2)}) collective-permute-start(f32[16,2048]{1,0:T(8,128)S(1)} %get-tuple-element.119.refs_0_), channel_id=1, source_target_pairs={{0,8},{4,12},{8,0},{12,4},{1,9},{5,13},{9,1},{13,5},{2,10},{6,14},... | collective-permute-start | bytes 393224 | tf_op jit(solution)/shard_map/ppermute | solution.py:39
  163.6 7.7 %collective-permute-start.39 = (f32[16,2048]{1,0:T(8,128)S(1)}, f32[16,2048]{1,0:T(8,128)S(1)}, u32[]{:S(2)}, u32[]{:S(2)}) collective-permute-start(f32[16,2048]{1,0:T(8,128)S(1)} %get-tuple-element.119.refs_0_), channel_id=1, source_target_pairs={{0,12},{4,0},{8,4},{12,8},{1,13},{5,1},{9,5},{13,9},{2,14},{6,2},{... | collective-permute-start | bytes 393224 | tf_op jit(solution)/shard_map/ppermute | solution.py:39
  164.9 11.5 %collective-permute-start.42 = (f32[8,2048]{1,0:T(8,128)S(1)}, f32[8,2048]{1,0:T(8,128)S(1)}, u32[]{:S(2)}, u32[]{:S(2)}) collective-permute-start(f32[8,2048]{1,0:T(8,128)S(1)} %get-tuple-element.129), channel_id=1, source_target_pairs={{0,64},{64,0},{1,65},{65,1},{2,66},{66,2},{3,67},{67,3},{4,68},{68... | collective-permute-start | bytes 196616 | tf_op jit(solution)/shard_map/ppermute | solution.py:43
  176.0 5.5 %collective-permute-start.41 = (f32[8,1024]{1,0:T(8,128)S(1)}, f32[8,1024]{1,0:T(8,128)S(1)}, u32[]{:S(2)}, u32[]{:S(2)}) collective-permute-start(f32[8,1024]{1,0:T(8,128)S(1)} %get-tuple-element.127), channel_id=1, source_target_pairs={{0,64},{64,0},{1,65},{65,1},{2,66},{66,2},{3,67},{67,3},{4,68},{68... | collective-permute-start | bytes 98312 | tf_op jit(solution)/shard_map/ppermute | solution.py:43
  189.5 8.7 %collective-permute-start.46 = (f32[4,4,256,128]{3,2,1,0:T(8,128)}, f32[4,4,256,128]{3,2,1,0:T(8,128)S(1)}, u32[]{:S(2)}, u32[]{:S(2)}) collective-permute-start(f32[4,4,256,128]{3,2,1,0:T(8,128)} %bitcast.88), channel_id=1, source_target_pairs={{0,16},{16,0},{1,17},{17,1},{2,18},{18,2},{3,19},{19,3},{4,20},{20... | collective-permute-start | bytes 6291464 | tf_op jit(solution)/shard_map/ppermute | solution.py:43
  189.5 5.8 %collective-permute-start.43 = (f32[8,2048]{1,0:T(8,128)S(1)}, f32[8,2048]{1,0:T(8,128)S(1)}, u32[]{:S(2)}, u32[]{:S(2)}) collective-permute-start(f32[8,2048]{1,0:T(8,128)S(1)} %s23.1.c0), channel_id=1, source_target_pairs={{0,4},{4,8},{8,12},{12,0},{1,5},{5,9},{9,13},{13,1},{2,6},{6,10},{... | collective-permute-start | bytes 196616 | tf_op jit(solution)/shard_map/ppermute | solution.py:39
  191.1 6.7 %collective-permute-start.44 = (f32[8,2048]{1,0:T(8,128)S(1)}, f32[8,2048]{1,0:T(8,128)S(1)}, u32[]{:S(2)}, u32[]{:S(2)}) collective-permute-start(f32[8,2048]{1,0:T(8,128)S(1)} %s23.1.c0), channel_id=1, source_target_pairs={{0,8},{4,12},{8,0},{12,4},{1,9},{5,13},{9,1},{13,5},{2,10},{6,14},... | collective-permute-start | bytes 196616 | tf_op jit(solution)/shard_map/ppermute | solution.py:39
  204.2 5.6 %collective-permute-start.47 = (f32[8,2048]{1,0:T(8,128)S(1)}, f32[8,2048]{1,0:T(8,128)S(1)}, u32[]{:S(2)}, u32[]{:S(2)}) collective-permute-start(f32[8,2048]{1,0:T(8,128)S(1)} %top.1.c0), channel_id=1, source_target_pairs={{0,4},{4,8},{8,12},{12,0},{1,5},{5,9},{9,13},{13,1},{2,6},{6,10},{... | collective-permute-start | bytes 196616 | tf_op jit(solution)/shard_map/ppermute | solution.py:39
  205.1 6.1 %collective-permute-start.48 = (f32[8,2048]{1,0:T(8,128)S(1)}, f32[8,2048]{1,0:T(8,128)S(1)}, u32[]{:S(2)}, u32[]{:S(2)}) collective-permute-start(f32[8,2048]{1,0:T(8,128)S(1)} %top.1.c0), channel_id=1, source_target_pairs={{0,8},{4,12},{8,0},{12,4},{1,9},{5,13},{9,1},{13,5},{2,10},{6,14},... | collective-permute-start | bytes 196616 | tf_op jit(solution)/shard_map/ppermute | solution.py:39
  213.2 5.8 %collective-permute-start.50 = (f32[8,2048]{1,0:T(8,128)S(1)}, f32[8,2048]{1,0:T(8,128)S(1)}, u32[]{:S(2)}, u32[]{:S(2)}) collective-permute-start(f32[8,2048]{1,0:T(8,128)S(1)} %x3.1), channel_id=1, source_target_pairs={{0,64},{64,0},{1,65},{65,1},{2,66},{66,2},{3,67},{67,3},{4,68},{68... | collective-permute-start | bytes 196616 | tf_op jit(solution)/shard_map/ppermute | solution.py:43
  223.8 6.2 %collective-permute-start.51 = (f32[16,2048]{1,0:T(8,128)S(1)}, f32[16,2048]{1,0:T(8,128)S(1)}, u32[]{:S(2)}, u32[]{:S(2)}) collective-permute-start(f32[16,2048]{1,0:T(8,128)S(1)} %b2.1.c0), channel_id=1, source_target_pairs={{0,4},{4,8},{8,12},{12,0},{1,5},{5,9},{9,13},{13,1},{2,6},{6,10},{... | collective-permute-start | bytes 393224 | tf_op jit(solution)/shard_map/ppermute | solution.py:39
  224.1 7.5 %collective-permute-start.52 = (f32[16,2048]{1,0:T(8,128)S(1)}, f32[16,2048]{1,0:T(8,128)S(1)}, u32[]{:S(2)}, u32[]{:S(2)}) collective-permute-start(f32[16,2048]{1,0:T(8,128)S(1)} %b2.1.c0), channel_id=1, source_target_pairs={{0,8},{4,12},{8,0},{12,4},{1,9},{5,13},{9,1},{13,5},{2,10},{6,14},... | collective-permute-start | bytes 393224 | tf_op jit(solution)/shard_map/ppermute | solution.py:39
  227.3 5.0 %collective-permute-start.53 = (f32[16,2048]{1,0:T(8,128)S(1)}, f32[16,2048]{1,0:T(8,128)S(1)}, u32[]{:S(2)}, u32[]{:S(2)}) collective-permute-start(f32[16,2048]{1,0:T(8,128)S(1)} %b2.1.c0), channel_id=1, source_target_pairs={{0,12},{4,0},{8,4},{12,8},{1,13},{5,1},{9,5},{13,9},{2,14},{6,2},{... | collective-permute-start | bytes 393224 | tf_op jit(solution)/shard_map/ppermute | solution.py:39
  232.9 4.3 %collective-permute-start.54 = (f32[16,1024]{1,0:T(8,128)S(1)}, f32[16,1024]{1,0:T(8,128)S(1)}, u32[]{:S(2)}, u32[]{:S(2)}) collective-permute-start(f32[16,1024]{1,0:T(8,128)S(1)} %get-tuple-element.137), channel_id=1, source_target_pairs={{0,32},{32,0},{1,33},{33,1},{2,34},{34,2},{3,35},{35,3},{4,36},{36... | collective-permute-start | bytes 196616 | tf_op jit(solution)/shard_map/ppermute | solution.py:43
  234.5 11.3 %collective-permute-start.58 = (f32[2,4,2048]{2,1,0:T(4,128)S(1)}, f32[2,4,2048]{2,1,0:T(4,128)S(1)}, u32[]{:S(2)}, u32[]{:S(2)}) collective-permute-start(f32[2,4,2048]{2,1,0:T(4,128)S(1)} %slice.51.a_mine), channel_id=1, source_target_pairs={{0,32},{32,0},{1,33},{33,1},{2,34},{34,2},{3,35},{35,3},{4,36},{36... | collective-permute-start | bytes 196616 | tf_op jit(solution)/shard_map/ppermute | solution.py:43
  242.1 5.3 %collective-permute-start.55 = (f32[8,2048]{1,0:T(8,128)S(1)}, f32[8,2048]{1,0:T(8,128)S(1)}, u32[]{:S(2)}, u32[]{:S(2)}) collective-permute-start(f32[8,2048]{1,0:T(8,128)S(1)} %get-tuple-element.140), channel_id=1, source_target_pairs={{0,12},{4,0},{8,4},{12,8},{1,13},{5,1},{9,5},{13,9},{2,14},{6,2},{... | collective-permute-start | bytes 196616 | tf_op jit(solution)/shard_map/ppermute | solution.py:39
  244.8 5.8 %collective-permute-start.56 = (f32[8,2048]{1,0:T(8,128)S(1)}, f32[8,2048]{1,0:T(8,128)S(1)}, u32[]{:S(2)}, u32[]{:S(2)}) collective-permute-start(f32[8,2048]{1,0:T(8,128)S(1)} %get-tuple-element.141), channel_id=1, source_target_pairs={{0,8},{4,12},{8,0},{12,4},{1,9},{5,13},{9,1},{13,5},{2,10},{6,14},... | collective-permute-start | bytes 196616 | tf_op jit(solution)/shard_map/ppermute | solution.py:39
  245.1 6.2 %collective-permute-start.57 = (f32[8,2048]{1,0:T(8,128)S(1)}, f32[8,2048]{1,0:T(8,128)S(1)}, u32[]{:S(2)}, u32[]{:S(2)}) collective-permute-start(f32[8,2048]{1,0:T(8,128)S(1)} %get-tuple-element.142), channel_id=1, source_target_pairs={{0,4},{4,8},{8,12},{12,0},{1,5},{5,9},{9,13},{13,1},{2,6},{6,10},{... | collective-permute-start | bytes 196616 | tf_op jit(solution)/shard_map/ppermute | solution.py:39
  252.1 17.7 %collective-permute-start.67 = (f32[8,512]{1,0:T(8,128)S(1)}, f32[8,512]{1,0:T(8,128)S(1)}, u32[]{:S(2)}, u32[]{:S(2)}) collective-permute-start(f32[8,512]{1,0:T(8,128)S(1)} %get-tuple-element.174), channel_id=1, source_target_pairs={{0,16},{16,0},{1,17},{17,1},{2,18},{18,2},{3,19},{19,3},{4,20},{20... | collective-permute-start | bytes 49160 | tf_op jit(solution)/shard_map/ppermute | solution.py:43
  252.7 17.7 %collective-permute-start.66 = (f32[8,1024]{1,0:T(8,128)S(1)}, f32[8,1024]{1,0:T(8,128)S(1)}, u32[]{:S(2)}, u32[]{:S(2)}) collective-permute-start(f32[8,1024]{1,0:T(8,128)S(1)} %get-tuple-element.176), channel_id=1, source_target_pairs={{0,16},{16,0},{1,17},{17,1},{2,18},{18,2},{3,19},{19,3},{4,20},{20... | collective-permute-start | bytes 98312 | tf_op jit(solution)/shard_map/ppermute | solution.py:43
  253.8 6.8 %collective-permute-start.60 = (f32[16,1024]{1,0:T(8,128)S(1)}, f32[16,1024]{1,0:T(8,128)S(1)}, u32[]{:S(2)}, u32[]{:S(2)}) collective-permute-start(f32[16,1024]{1,0:T(8,128)S(1)} %maximum_select_fusion.3.refs_0_), channel_id=1, source_target_pairs={{0,1},{1,2},{2,3},{3,0},{4,5},{5,6},{6,7},{7,4},{8,9},{9,10},{10,1... | collective-permute-start | bytes 196616 | tf_op jit(solution)/shard_map/ppermute | solution.py:39
  254.4 6.2 %collective-permute-start.61 = (f32[16,1024]{1,0:T(8,128)S(1)}, f32[16,1024]{1,0:T(8,128)S(1)}, u32[]{:S(2)}, u32[]{:S(2)}) collective-permute-start(f32[16,1024]{1,0:T(8,128)S(1)} %maximum_select_fusion.3.refs_0_), channel_id=1, source_target_pairs={{0,2},{1,3},{2,0},{3,1},{4,6},{5,7},{6,4},{7,5},{8,10},{9,11},{10,... | collective-permute-start | bytes 196616 | tf_op jit(solution)/shard_map/ppermute | solution.py:39
  256.2 5.0 %collective-permute-start.62 = (f32[16,1024]{1,0:T(8,128)S(1)}, f32[16,1024]{1,0:T(8,128)S(1)}, u32[]{:S(2)}, u32[]{:S(2)}) collective-permute-start(f32[16,1024]{1,0:T(8,128)S(1)} %maximum_select_fusion.3.refs_0_), channel_id=1, source_target_pairs={{0,3},{1,0},{2,1},{3,2},{4,7},{5,4},{6,5},{7,6},{8,11},{9,8},{10,9... | collective-permute-start | bytes 196616 | tf_op jit(solution)/shard_map/ppermute | solution.py:39
  266.1 7.5 %collective-permute-start.63 = (f32[16,2048]{1,0:T(8,128)S(1)}, f32[16,2048]{1,0:T(8,128)S(1)}, u32[]{:S(2)}, u32[]{:S(2)}) collective-permute-start(f32[16,2048]{1,0:T(8,128)S(1)} %get-tuple-element.146), channel_id=1, source_target_pairs={{0,3},{1,0},{2,1},{3,2},{4,7},{5,4},{6,5},{7,6},{8,11},{9,8},{10,9... | collective-permute-start | bytes 393224 | tf_op jit(solution)/shard_map/ppermute | solution.py:39
  268.9 7.1 %collective-permute-start.64 = (f32[16,2048]{1,0:T(8,128)S(1)}, f32[16,2048]{1,0:T(8,128)S(1)}, u32[]{:S(2)}, u32[]{:S(2)}) collective-permute-start(f32[16,2048]{1,0:T(8,128)S(1)} %get-tuple-element.147), channel_id=1, source_target_pairs={{0,2},{1,3},{2,0},{3,1},{4,6},{5,7},{6,4},{7,5},{8,10},{9,11},{10,... | collective-permute-start | bytes 393224 | tf_op jit(solution)/shard_map/ppermute | solution.py:39
  269.4 7.9 %collective-permute-start.65 = (f32[16,2048]{1,0:T(8,128)S(1)}, f32[16,2048]{1,0:T(8,128)S(1)}, u32[]{:S(2)}, u32[]{:S(2)}) collective-permute-start(f32[16,2048]{1,0:T(8,128)S(1)} %get-tuple-element.148), channel_id=1, source_target_pairs={{0,1},{1,2},{2,3},{3,0},{4,5},{5,6},{6,7},{7,4},{8,9},{9,10},{10,1... | collective-permute-start | bytes 393224 | tf_op jit(solution)/shard_map/ppermute | solution.py:39
  (24 other events, 432.5 us)
Sparse Core Ops, SparseCore 0:
  32.4 39.9 all-gather.6
  94.1 42.1 all-gather.8
  160.8 28.6 all-gather.10

commit v8 on v7

--- a/solution.py
+++ b/solution.py
@@ -436,35 +436,35 @@
         return lax.all_gather(jnp.concatenate(parts, 0), "y", axis=0, tiled=False)
 
     gate = lax.optimization_barrier
+    off0 = off0.reshape(4, 256, B)
+    fa, fb = shift(off0, "z", 1), shift(off0, "z", -1)
+    fc, fd = shift(fa[:2], "z", 1), shift(fb[2:], "z", -1)
     e0 = jnp.swapaxes(dinv0.reshape(4, 4, B, B), 0, 1).reshape(4, 512, B)
+    e0 = lax.all_to_all(e0, "y", 0, 0, tiled=True)
     e1 = dinv1.reshape(2, 2, 256, B)
-    e1_mine, e1_other = pick(e1, ci, 1), flip(pick(e1, 1 - ci, 1), "core")
-    e0, e1_mine, e1_other, dinv2, rhs0 = gate((e0, e1_mine, e1_other, dinv2, rhs0))
-    e0 = lax.all_to_all(e0, "y", 0, 0, tiled=True)
-    e1 = over_z(for_z(e1_mine, e1_other, ci))
+    e1 = over_z(for_z(pick(e1, ci, 1), flip(pick(e1, 1 - ci, 1), "core"), ci))
+    e0, e1, fa, fb, fc, fd, dinv2, off2, dinv3, rhs0, rhs1 = gate(
+        (e0, e1, fa, fb, fc, fd, dinv2, off2, dinv3, rhs0, rhs1)
+    )
+    m1 = gathered(e1, off1)
+
+    ea, eb = shift(e0, "z", 1), shift(e0, "z", -1)
     e2 = dinv2.reshape(2, 256, B)
     e2 = ordered(pick(e2, ci)[None], flip(pick(e2, 1 - ci)[None], "core"), ci, 0)
     e2_other = flip(e2, "x0")
-    e0, e1, e2, e2_other, off0, off2, dinv3, rhs0 = gate(
-        (e0, e1, e2, e2_other, off0.reshape(4, 256, B), off2, dinv3, rhs0)
-    )
-    m1 = gathered(e1, off1)
-
-    fa, fb = shift(off0, "z", 1), shift(off0, "z", -1)
-    ea, eb = shift(e0, "z", 1), shift(e0, "z", -1)
-    e2 = over_z(for_z(e2, e2_other, x0))
     f2 = joined(off2, 1)
-    fc, fd = shift(fa[:2], "z", 1), shift(fb[2:], "z", -1)
-    c0 = gather4(rhs0, "y")
-    e2, f2, ea, eb, fc, fd, c0 = gate((e2, f2, ea, eb, fc, fd, c0))
-
-    ec, ed = shift(ea[:2], "z", 1), shift(eb[2:], "z", -1)
-    m2 = gathered(e2, f2)
     e3 = joined(dinv3[None], 1)
     e3_other = flip(e3, "x1")
+    c0 = gather4(rhs0, "y")
     b_mine, b_other = halves(jnp.concatenate([rhs1, rhs2, rhs3], 1), ci)
     b_other = flip(b_other, "core")
-    ec, ed, e3, e3_other, b_mine, b_other = gate((ec, ed, e3, e3_other, b_mine, b_other))
+    ea, eb, e2, e2_other, f2, e3, e3_other, c0, b_mine, b_other = gate(
+        (ea, eb, e2, e2_other, f2, e3, e3_other, c0, b_mine, b_other)
+    )
+
+    ec, ed = shift(ea[:2], "z", 1), shift(eb[2:], "z", -1)
+    e2 = over_z(for_z(e2, e2_other, x0))
+    e2[0], ec, ed = gate((e2[0], ec, ed))
     w0 = [e0, ea, eb, ec, ed, off0, fa, fb, fc, fd]
     e3 = over_z(for_z(e3, e3_other, x1))
     e3, b_mine = gate((e3, b_mine))
@@ -483,9 +483,11 @@
         functools.partial(forward_kernel, 0, 64, "rs"), "f0", [(64, 512)] + [(16, 1024)] * 4,
         [ev, fv, *work(64), dma((10,))], meta, c0, w0, flops(64),
     )
-    m1, _ = gate((m1, y0))
+    e2, _ = gate((e2, y0))
+    m2 = gathered(e2, f2)
+    parts = scatter4(u, "y")
+    m1, _ = gate((m1, parts[1]))
     w1 = m1, flip(m1, "core")
-    parts = scatter4(u, "y")
     u = (parts[0] + parts[1]) + (parts[2] + parts[3])
     keep, give = halves(u, ci)
     c1, pk, pg = call(

time: 285 us -> 264 us (0.926)
  waiting for transfers between devices: 119 us -> 98.8 us
  local copies, waits for them, and re-layouts: 13.7 us -> 8.28 us
  starting transfers between devices: 94.9 us -> 99.8 us
    ppermute x47, waiting for transfers between devices: 86.7 us -> 72.2 us  [shift(): return lax.ppermute(v, axis, [(i, (i + s) % 4) for i in range(4)])]
    ppermute x22, waiting for transfers between devices: 24.2 us -> 14.7 us  [flip(): return lax.ppermute(v, axis, [(0, 1), (1, 0)])]
    ppermute x22, starting transfers between devices: 15.6 us -> 21.6 us  [flip(): return lax.ppermute(v, axis, [(0, 1), (1, 0)])]
    all_gather x3, waiting for transfers between devices: 7.41 us -> 11.9 us  [gathered(): return lax.all_gather(jnp.concatenate(parts, 0), 'y', axis=0, tiled=False)]
    unnamed x41 -> x47, local copies, waits for them, and re-layouts: 6.86 us -> 4.85 us
  transfers between devices with their start and end apart: 73 -> 73, of which waited for: 44 -> 38; matrix products, arithmetic and copies ran while one was open for 4% -> 3% of each run, Pallas kernels for 10% -> 10%
where the time goes in v8:
time: 264 us
  starting transfers between devices  99.8 us (38%)
  waiting for transfers between devices  98.8 us (37%)
  Pallas kernels  38.4 us (15%)
  between operations  14.5 us (5%)
  local copies, waits for them, and re-layouts  8.28 us (3%)
  other arithmetic  3.77 us (1%)
    ppermute x47, starting transfers between devices, shift(): return lax.ppermute(v, axis, [(i, (i + s) % 4) for i in range(4)])  73.6 us
    ppermute x47, waiting for transfers between devices, shift(): return lax.ppermute(v, axis, [(i, (i + s) % 4) for i in range(4)])  72.2 us
    pallas_call x13, Pallas kernels, call(): pl.pallas_call(kernel, out_shape=[jax.ShapeDtypeStruct(s, f32) for s in s...  38.4 us
    ppermute x22, starting transfers between devices, flip(): return lax.ppermute(v, axis, [(0, 1), (1, 0)])  21.6 us
    ppermute x22, waiting for transfers between devices, flip(): return lax.ppermute(v, axis, [(0, 1), (1, 0)])  14.7 us
    all_gather x3, waiting for transfers between devices, gathered(): return lax.all_gather(jnp.concatenate(parts, 0), 'y', axis=0, tiled=False)  11.9 us
  transfers between devices with their start and end apart: 73, of which 38 were waited for; matrix products, arithmetic and copies ran while one was open for 3% of the time, Pallas kernels for 10%

profile of v8, /device:TPU:0, one launch (start us, length us, event | category | flops | bytes accessed | tf_op | source)
XLA Modules:
  0.0 263.7 jit_solution(13634205195877309693)
XLA Ops:
  7.2 2.1 collective-permute-start.4
  9.2 2.2 collective-permute-start.5
  11.4 2.3 copy.22
  13.8 4.6 %all-to-all-start = ((f32[4,512,128]{2,1,0:T(8,128)}), f32[4,512,128]{2,1,0:T(8,128)}, u32[]{:S(2)}, u32[]{:S(2)}) async-start(f32[4,512,128]{2,1,0:T(8,128)} %bitcast.3), calls=%async_computation | async-start | bytes 2097152 | tf_op jit(solution)/shard_map/all_to_all | solution.py:443
  18.6 4.9 %collective-permute-done.4.refs_10_.refs_11_ = f32[4,256,128]{2,1,0:T(8,128)S(1)} collective-permute-done((f32[4,256,128]{2,1,0:T(8,128)}, f32[4,256,128]{2,1,0:T(8,128)S(1)}, u32[]{:S(2)}, u32[]{:S(2)}) %collective-permute-start.4) | collective-permute-done | bytes 524320 | tf_op jit(solution)/shard_map/ppermute | solution.py:39
  24.3 2.6 collective-permute-start.7
  27.1 2.0 collective-permute-start.2
  30.3 7.6 %collective-permute-done.1 = f32[256,128]{1,0:T(8,128)S(1)} collective-permute-done((f32[256,128]{1,0:T(8,128)S(1)}, f32[256,128]{1,0:T(8,128)S(1)}, u32[]{:S(2)}, u32[]{:S(2)}) %collective-permute-start.1) | collective-permute-done | bytes 131104 | tf_op jit(solution)/shard_map/ppermute | solution.py:39
  39.2 3.2 %collective-permute-start.9 = (f32[4,512,128]{2,1,0:T(8,128)}, f32[4,512,128]{2,1,0:T(8,128)S(1)}, u32[]{:S(2)}, u32[]{:S(2)}) collective-permute-start(f32[4,512,128]{2,1,0:T(8,128)} %all-to-all-done.refs_4_.refs_5_), channel_id=1, source_target_pairs={{0,12},{4,0},{8,4},{12,8},{1,13},{5,1},{9,5},{13,9},{2,14},{6,2},{... | collective-permute-start | bytes 3145736 | tf_op jit(solution)/shard_map/ppermute | solution.py:39
  44.6 2.7 %collective-permute-done.13 = f32[1,256,128]{2,1,0:T(8,128)S(1)} collective-permute-done((f32[1,256,128]{2,1,0:T(8,128)S(1)}, f32[1,256,128]{2,1,0:T(8,128)S(1)}, u32[]{:S(2)}, u32[]{:S(2)}) %collective-permute-start.13) | collective-permute-done | bytes 131104 | tf_op jit(solution)/shard_map/ppermute | solution.py:43
  47.4 1.6 collective-permute-start.15
  50.3 3.0 %collective-permute-start.16 = (f32[16,2048]{1,0:T(8,128)S(1)}, f32[16,2048]{1,0:T(8,128)S(1)}, u32[]{:S(2)}, u32[]{:S(2)}) collective-permute-start(f32[16,2048]{1,0:T(8,128)S(1)} %copy-done), channel_id=1, source_target_pairs={{0,2},{1,3},{2,0},{3,1},{4,6},{5,7},{6,4},{7,5},{8,10},{9,11},{10,... | collective-permute-start | bytes 393224 | tf_op jit(solution)/shard_map/ppermute | solution.py:39
  53.3 3.0 %collective-permute-start.14 = (f32[2,256,128]{2,1,0:T(8,128)S(1)}, f32[2,256,128]{2,1,0:T(8,128)S(1)}, u32[]{:S(2)}, u32[]{:S(2)}) collective-permute-start(f32[2,256,128]{2,1,0:T(8,128)S(1)} %maximum_select_fusion.2), channel_id=1, source_target_pairs={{0,64},{64,0},{1,65},{65,1},{2,66},{66,2},{3,67},{67,3},{4,68},{68... | collective-permute-start | bytes 786440 | tf_op jit(solution)/shard_map/ppermute | solution.py:43
  56.9 4.1 %collective-permute-done.16.refs_2_ = f32[16,2048]{1,0:T(8,128)S(1)} collective-permute-done((f32[16,2048]{1,0:T(8,128)S(1)}, f32[16,2048]{1,0:T(8,128)S(1)}, u32[]{:S(2)}, u32[]{:S(2)}) %collective-permute-start.16) | collective-permute-done | bytes 131104 | tf_op jit(solution)/shard_map/ppermute | solution.py:39
  61.9 7.6 %collective-permute-done.17.refs_3_ = f32[16,2048]{1,0:T(8,128)S(1)} collective-permute-done((f32[16,2048]{1,0:T(8,128)S(1)}, f32[16,2048]{1,0:T(8,128)S(1)}, u32[]{:S(2)}, u32[]{:S(2)}) %collective-permute-start.17) | collective-permute-done | bytes 131104 | tf_op jit(solution)/shard_map/ppermute | solution.py:39
  71.3 2.4 collective-permute-start.20
  75.6 1.8 collective-permute-start.39
  77.4 7.9 %collective-permute-done.19.refs_7_.refs_8_ = f32[2,512,128]{2,1,0:T(8,128)} collective-permute-done((f32[2,512,128]{2,1,0:T(8,128)S(1)}, f32[2,512,128]{2,1,0:T(8,128)}, u32[]{:S(2)}, u32[]{:S(2)}) %collective-permute-start.19) | collective-permute-done | bytes 524320 | tf_op jit(solution)/shard_map/ppermute | solution.py:39
  85.3 2.5 collective-permute-done.20.refs_8_.refs_9_
  87.8 5.7 %f0.1 = (f32[64,512]{1,0:T(8,128)S(1)}, f32[16,1024]{1,0:T(8,128)S(1)}, f32[16,1024]{1,0:T(8,128)S(1)}, f32[16,1024]{1,0:T(8,128)S(1)}, f32[16,1024]{1,0:T(8,128)S(1)}) custom-call(s32[128]{0:T(128)S(1)} %pad_add_fusion.meta, f32[16,2048]{1,0:T(8,128)S(1)} %copy-done, f32[16,2048]{1,0:T(8,128)S(1)} %collective-permute-done.15.refs_1_, ...), custom_call_target="tpu_custom_call" | custom-call | flops 2415919104 | bytes 6815744 | tf_op jit(solution)/shard_map/f0/pallas_call | solution.py:395
  94.6 2.9 %collective-permute-start.21 = (f32[16,1024]{1,0:T(8,128)S(1)}, f32[16,1024]{1,0:T(8,128)S(1)}, u32[]{:S(2)}, u32[]{:S(2)}) collective-permute-start(f32[16,1024]{1,0:T(8,128)S(1)} %get-tuple-element.97), channel_id=1, source_target_pairs={{0,3},{1,0},{2,1},{3,2},{4,7},{5,4},{6,5},{7,6},{8,11},{9,8},{10,9... | collective-permute-start | bytes 196616 | tf_op jit(solution)/shard_map/ppermute | solution.py:39
  97.5 1.9 collective-permute-done.21
  99.4 2.5 collective-permute-start.22
  101.9 1.9 collective-permute-start.23
  103.9 5.1 %collective-permute-start.26 = (f32[256,128]{1,0:T(8,128)S(1)}, f32[256,128]{1,0:T(8,128)S(1)}, u32[]{:S(2)}, u32[]{:S(2)}) collective-permute-start(f32[256,128]{1,0:T(8,128)S(1)} %get-tuple-element.157), channel_id=1, source_target_pairs={{0,8},{4,12},{8,0},{12,4},{1,9},{5,13},{9,1},{13,5},{2,10},{6,14},... | collective-permute-start | bytes 393224 | tf_op jit(solution)/shard_map/ppermute | solution.py:39
  109.2 2.0 collective-permute-done.25
  111.2 4.0 %collective-permute-done.26 = f32[256,128]{1,0:T(8,128)S(1)} collective-permute-done((f32[256,128]{1,0:T(8,128)S(1)}, f32[256,128]{1,0:T(8,128)S(1)}, u32[]{:S(2)}, u32[]{:S(2)}) %collective-permute-start.26) | collective-permute-done | bytes 131104 | tf_op jit(solution)/shard_map/ppermute | solution.py:39
  116.0 3.6 %collective-permute-start.29 = (f32[8,2048]{1,0:T(8,128)S(1)}, f32[8,2048]{1,0:T(8,128)S(1)}, u32[]{:S(2)}, u32[]{:S(2)}) collective-permute-start(f32[8,2048]{1,0:T(8,128)S(1)} %get-tuple-element.105.refs_0_), channel_id=1, source_target_pairs={{0,8},{4,12},{8,0},{12,4},{1,9},{5,13},{9,1},{13,5},{2,10},{6,14},... | collective-permute-start | bytes 196616 | tf_op jit(solution)/shard_map/ppermute | solution.py:39
  119.6 1.6 collective-permute-start.33
  123.8 4.9 %f1.1 = (f32[32,512]{1,0:T(8,128)S(1)}, f32[16,1024]{1,0:T(8,128)S(1)}, f32[16,1024]{1,0:T(8,128)S(1)}) custom-call(s32[128]{0:T(128)S(1)} %pad_add_fusion.meta, f32[8,2048]{1,0:T(8,128)S(1)} %get-tuple-element.105.refs_0_, f32[8,2048]{1,0:T(8,128)S(1)} %collective-permute-done.28.refs_1_, f32[8,2048]{1,0:T(8,128)S(1)} %collective-permute-done.29.refs_2_, ...), custom_call_target="tpu_custom_call" | custom-call | flops 1207959552 | bytes 6553600 | tf_op jit(solution)/shard_map/f1/pallas_call | solution.py:395
  128.8 1.6 collective-permute-start.32
  130.4 2.7 %collective-permute-done.32.recv = f32[16,1024]{1,0:T(8,128)S(1)} collective-permute-done((f32[16,1024]{1,0:T(8,128)S(1)}, f32[16,1024]{1,0:T(8,128)S(1)}, u32[]{:S(2)}, u32[]{:S(2)}) %collective-permute-start.32) | collective-permute-done | bytes 65568 | tf_op jit(solution)/shard_map/ppermute | solution.py:43
  133.9 2.1 all-gather.9.cloned.1.call-done
  136.9 1.6 collective-permute-start.34
  138.5 2.9 %collective-permute-start.35 = (f32[16,2048]{1,0:T(8,128)S(1)}, f32[16,2048]{1,0:T(8,128)S(1)}, u32[]{:S(2)}, u32[]{:S(2)}) collective-permute-start(f32[16,2048]{1,0:T(8,128)S(1)} %get-tuple-element.115.refs_0_), channel_id=1, source_target_pairs={{0,8},{4,12},{8,0},{12,4},{1,9},{5,13},{9,1},{13,5},{2,10},{6,14},... | collective-permute-start | bytes 393224 | tf_op jit(solution)/shard_map/ppermute | solution.py:39
  142.7 3.0 %collective-permute-start.42 = (f32[8,2048]{1,0:T(8,128)S(1)}, f32[8,2048]{1,0:T(8,128)S(1)}, u32[]{:S(2)}, u32[]{:S(2)}) collective-permute-start(f32[8,2048]{1,0:T(8,128)S(1)} %get-tuple-element.127), channel_id=1, source_target_pairs={{0,64},{64,0},{1,65},{65,1},{2,66},{66,2},{3,67},{67,3},{4,68},{68... | collective-permute-start | bytes 196616 | tf_op jit(solution)/shard_map/ppermute | solution.py:43
  145.7 2.3 collective-permute-done.35.refs_2_
  148.1 4.7 %f2.1 = (f32[16,512]{1,0:T(8,128)S(1)}, f32[8,1024]{1,0:T(8,128)S(1)}, f32[8,1024]{1,0:T(8,128)S(1)}) custom-call(s32[128]{0:T(128)S(1)} %pad_add_fusion.meta, f32[16,2048]{1,0:T(8,128)S(1)} %get-tuple-element.115.refs_0_, f32[16,2048]{1,0:T(8,128)S(1)} %collective-permute-done.34.refs_1_, f32[16,2048]{1,0:T(8,128)S(1)} %collective-permute-done.35.refs_2_, ...), custom_call_target="tpu_custom_call" | custom-call | flops 603979776 | bytes 6815744 | tf_op jit(solution)/shard_map/f2/pallas_call | solution.py:395
  152.8 3.1 %collective-permute-start.41 = (f32[8,1024]{1,0:T(8,128)S(1)}, f32[8,1024]{1,0:T(8,128)S(1)}, u32[]{:S(2)}, u32[]{:S(2)}) collective-permute-start(f32[8,1024]{1,0:T(8,128)S(1)} %get-tuple-element.125), channel_id=1, source_target_pairs={{0,64},{64,0},{1,65},{65,1},{2,66},{66,2},{3,67},{67,3},{4,68},{68... | collective-permute-start | bytes 98312 | tf_op jit(solution)/shard_map/ppermute | solution.py:43
  155.9 2.4 collective-permute-done.41.recv
  158.9 9.8 %all-gather.11.cloned.1.call-done = f32[16,256,128]{2,1,0:T(8,128)} async-done(((f32[4,256,128]{2,1,0:T(8,128)}), f32[16,256,128]{2,1,0:T(8,128)}) %all-gather.11.cloned.1.call-update) | async-done | bytes 2097168 | tf_op jit(solution)/shard_map/all_gather | solution.py:436
  168.7 1.6 collective-permute-start.43
  170.3 2.9 %collective-permute-start.44 = (f32[8,2048]{1,0:T(8,128)S(1)}, f32[8,2048]{1,0:T(8,128)S(1)}, u32[]{:S(2)}, u32[]{:S(2)}) collective-permute-start(f32[8,2048]{1,0:T(8,128)S(1)} %s23.1.c0), channel_id=1, source_target_pairs={{0,8},{4,12},{8,0},{12,4},{1,9},{5,13},{9,1},{13,5},{2,10},{6,14},... | collective-permute-start | bytes 196616 | tf_op jit(solution)/shard_map/ppermute | solution.py:39
  174.6 2.4 collective-permute-done.44.c2
  178.8 4.6 %top.1.c0 = f32[8,2048]{1,0:T(8,128)S(1)} custom-call(s32[128]{0:T(128)S(1)} %pad_add_fusion.meta, f32[8,2048]{1,0:T(8,128)S(1)} %s23.1.c0, f32[8,2048]{1,0:T(8,128)S(1)} %collective-permute-done.43.c1, f32[8,2048]{1,0:T(8,128)S(1)} %collective-permute-done.44.c2, f32[8,2048]{1,0:T(8,128)S(1)} %collective-permute-done.45.c3, f32[4,4,256,128]{3,2,1,0:T(8,128)} %bitcast.91, ...), custom_call_target="tpu_custom_call" | custom-call | flops 301989888 | bytes 4456448 | tf_op jit(solution)/shard_map/top/pallas_call | solution.py:395
  184.4 3.2 %collective-permute-start.48 = (f32[8,2048]{1,0:T(8,128)S(1)}, f32[8,2048]{1,0:T(8,128)S(1)}, u32[]{:S(2)}, u32[]{:S(2)}) collective-permute-start(f32[8,2048]{1,0:T(8,128)S(1)} %top.1.c0), channel_id=1, source_target_pairs={{0,8},{4,12},{8,0},{12,4},{1,9},{5,13},{9,1},{13,5},{2,10},{6,14},... | collective-permute-start | bytes 196616 | tf_op jit(solution)/shard_map/ppermute | solution.py:39
  192.5 3.1 %collective-permute-start.50 = (f32[8,2048]{1,0:T(8,128)S(1)}, f32[8,2048]{1,0:T(8,128)S(1)}, u32[]{:S(2)}, u32[]{:S(2)}) collective-permute-start(f32[8,2048]{1,0:T(8,128)S(1)} %x3.1), channel_id=1, source_target_pairs={{0,64},{64,0},{1,65},{65,1},{2,66},{66,2},{3,67},{67,3},{4,68},{68... | collective-permute-start | bytes 196616 | tf_op jit(solution)/shard_map/ppermute | solution.py:43
  195.5 2.8 %collective-permute-done.50.x3r = f32[8,2048]{1,0:T(8,128)S(1)} collective-permute-done((f32[8,2048]{1,0:T(8,128)S(1)}, f32[8,2048]{1,0:T(8,128)S(1)}, u32[]{:S(2)}, u32[]{:S(2)}) %collective-permute-start.50) | collective-permute-done | bytes 65568 | tf_op jit(solution)/shard_map/ppermute | solution.py:43
  198.3 4.7 %b2.1.c0 = f32[16,2048]{1,0:T(8,128)S(1)} custom-call(s32[128]{0:T(128)S(1)} %pad_add_fusion.meta, f32[1,8,2048]{2,1,0:T(8,128)S(1)} %bitcast.82, f32[1,8,2048]{2,1,0:T(8,128)S(1)} %bitcast.83, f32[16,512]{1,0:T(8,128)S(1)} %get-tuple-element.133.refs_2_, f32[4,6,256,128]{3,2,1,0:T(8,128)} %bitcast.89, f32[4,6,256,128]{3,2,1,0:T(8,128)} %collective-permute-done.40.refs_5_.refs_4_), custom_call_target="tpu_custom_call" | custom-call | flops 603979776 | bytes 6455296 | tf_op jit(solution)/shard_map/b2/pallas_call | solution.py:395
  203.4 3.1 %collective-permute-start.52 = (f32[16,2048]{1,0:T(8,128)S(1)}, f32[16,2048]{1,0:T(8,128)S(1)}, u32[]{:S(2)}, u32[]{:S(2)}) collective-permute-start(f32[16,2048]{1,0:T(8,128)S(1)} %b2.1.c0), channel_id=1, source_target_pairs={{0,8},{4,12},{8,0},{12,4},{1,9},{5,13},{9,1},{13,5},{2,10},{6,14},... | collective-permute-start | bytes 393224 | tf_op jit(solution)/shard_map/ppermute | solution.py:39
  207.3 2.0 collective-permute-done.51.c1
  209.3 1.6 collective-permute-done.52.c2
  214.4 2.1 collective-permute-done.54.refs_1_
  216.6 4.8 %b1.1 = (f32[8,2048]{1,0:T(8,128)S(1)}, f32[8,2048]{1,0:T(8,128)S(1)}, f32[8,2048]{1,0:T(8,128)S(1)}, f32[8,2048]{1,0:T(8,128)S(1)}) custom-call(s32[128]{0:T(128)S(1)} %pad_add_fusion.meta, f32[2,16,2048]{2,1,0:T(8,128)S(1)} %get-tuple-element.134.refs_0_, f32[16,1024]{1,0:T(8,128)S(1)} %collective-permute-done.54.refs_1_, ...), custom_call_target="tpu_custom_call" | custom-call | flops 1207959552 | bytes 6684672 | tf_op jit(solution)/shard_map/b1/pallas_call | solution.py:395
  221.4 2.7 %collective-permute-start.55 = (f32[8,2048]{1,0:T(8,128)S(1)}, f32[8,2048]{1,0:T(8,128)S(1)}, u32[]{:S(2)}, u32[]{:S(2)}) collective-permute-start(f32[8,2048]{1,0:T(8,128)S(1)} %get-tuple-element.138), channel_id=1, source_target_pairs={{0,12},{4,0},{8,4},{12,8},{1,13},{5,1},{9,5},{13,9},{2,14},{6,2},{... | collective-permute-start | bytes 196616 | tf_op jit(solution)/shard_map/ppermute | solution.py:39
  225.1 1.6 collective-permute-done.55.c1
  226.6 3.3 %collective-permute-done.56.c2 = f32[8,2048]{1,0:T(8,128)S(1)} collective-permute-done((f32[8,2048]{1,0:T(8,128)S(1)}, f32[8,2048]{1,0:T(8,128)S(1)}, u32[]{:S(2)}, u32[]{:S(2)}) %collective-permute-start.56) | collective-permute-done | bytes 65568 | tf_op jit(solution)/shard_map/ppermute | solution.py:39
  233.6 1.8 collective-permute-start.61
  235.4 2.1 collective-permute-start.62
  238.1 1.8 collective-permute-done.60.refs_1_
  240.5 4.9 %b0.1 = (f32[16,2048]{1,0:T(8,128)S(1)}, f32[16,2048]{1,0:T(8,128)S(1)}, f32[16,2048]{1,0:T(8,128)S(1)}, f32[16,2048]{1,0:T(8,128)S(1)}) custom-call(s32[128]{0:T(128)S(1)} %pad_add_fusion.meta, f32[16,1024]{1,0:T(8,128)S(1)} %maximum_select_fusion.3.refs_0_, f32[16,1024]{1,0:T(8,128)S(1)} %collective-permute-done.60.refs_1_, ...), custom_call_target="tpu_custom_call" | custom-call | flops 2415919104 | bytes 6684672 | tf_op jit(solution)/shard_map/b0/pallas_call | solution.py:395
  245.4 2.7 %collective-permute-start.63 = (f32[16,2048]{1,0:T(8,128)S(1)}, f32[16,2048]{1,0:T(8,128)S(1)}, u32[]{:S(2)}, u32[]{:S(2)}) collective-permute-start(f32[16,2048]{1,0:T(8,128)S(1)} %get-tuple-element.144), channel_id=1, source_target_pairs={{0,3},{1,0},{2,1},{3,2},{4,7},{5,4},{6,5},{7,6},{8,11},{9,8},{10,9... | collective-permute-start | bytes 393224 | tf_op jit(solution)/shard_map/ppermute | solution.py:39
  250.4 2.5 collective-permute-done.63
  252.9 2.4 collective-permute-done.64
  (177 shorter events, 43.9 us)
Async XLA Ops:
  7.2 16.3 %collective-permute-start.4 = (f32[4,256,128]{2,1,0:T(8,128)}, f32[4,256,128]{2,1,0:T(8,128)S(1)}, u32[]{:S(2)}, u32[]{:S(2)}) collective-permute-start(f32[4,256,128]{2,1,0:T(8,128)} %bitcast.104), channel_id=1, source_target_pairs={{0,4},{4,8},{8,12},{12,0},{1,5},{5,9},{9,13},{13,1},{2,6},{6,10},{... | collective-permute-start | bytes 1572872 | tf_op jit(solution)/shard_map/ppermute | solution.py:39
  9.2 15.1 %collective-permute-start.5 = (f32[4,256,128]{2,1,0:T(8,128)}, f32[4,256,128]{2,1,0:T(8,128)S(1)}, u32[]{:S(2)}, u32[]{:S(2)}) collective-permute-start(f32[4,256,128]{2,1,0:T(8,128)} %bitcast.105), channel_id=1, source_target_pairs={{0,12},{4,0},{8,4},{12,8},{1,13},{5,1},{9,5},{13,9},{2,14},{6,2},{... | collective-permute-start | bytes 1572872 | tf_op jit(solution)/shard_map/ppermute | solution.py:39
  13.8 24.2 %all-to-all-start = ((f32[4,512,128]{2,1,0:T(8,128)}), f32[4,512,128]{2,1,0:T(8,128)}, u32[]{:S(2)}, u32[]{:S(2)}) async-start(f32[4,512,128]{2,1,0:T(8,128)} %bitcast.3), calls=%async_computation | async-start | bytes 2097152 | tf_op jit(solution)/shard_map/all_to_all | solution.py:443
  18.4 81.0 %all-gather.7.cloned.1.call-start = ((), (), s32[]{:S(2)}) async-start(), calls=%async_computation.1 | async-start | bytes 3932160 | tf_op jit(solution)/shard_map/all_gather | solution.py:436
  18.5 8.4 %collective-permute-start = (f32[2,256,128]{2,1,0:T(8,128)S(1)}, f32[2,256,128]{2,1,0:T(8,128)S(1)}, u32[]{:S(2)}, u32[]{:S(2)}) collective-permute-start(f32[2,256,128]{2,1,0:T(8,128)S(1)} %dynamic-slice_bitcast_fusion), channel_id=1, source_target_pairs={{0,16},{16,0},{1,17},{17,1},{2,18},{18,2},{3,19},{19,3},{4,20},{20... | collective-permute-start | bytes 786440 | tf_op jit(solution)/shard_map/ppermute | solution.py:43
  23.5 14.4 %collective-permute-start.6 = (f32[2,256,128]{2,1,0:T(8,128)S(1)}, f32[2,256,128]{2,1,0:T(8,128)}, u32[]{:S(2)}, u32[]{:S(2)}) collective-permute-start(f32[2,256,128]{2,1,0:T(8,128)S(1)} %slice.55), channel_id=1, source_target_pairs={{0,4},{4,8},{8,12},{12,0},{1,5},{5,9},{9,13},{13,1},{2,6},{6,10},{... | collective-permute-start | bytes 786440 | tf_op jit(solution)/shard_map/ppermute | solution.py:39
  24.3 13.6 %collective-permute-start.7 = (f32[2,256,128]{2,1,0:T(8,128)S(1)}, f32[2,256,128]{2,1,0:T(8,128)}, u32[]{:S(2)}, u32[]{:S(2)}) collective-permute-start(f32[2,256,128]{2,1,0:T(8,128)S(1)} %slice.56), channel_id=1, source_target_pairs={{0,12},{4,0},{8,4},{12,8},{1,13},{5,1},{9,5},{13,9},{2,14},{6,2},{... | collective-permute-start | bytes 786440 | tf_op jit(solution)/shard_map/ppermute | solution.py:39
  27.0 10.9 %collective-permute-start.1 = (f32[256,128]{1,0:T(8,128)S(1)}, f32[256,128]{1,0:T(8,128)S(1)}, u32[]{:S(2)}, u32[]{:S(2)}) collective-permute-start(f32[256,128]{1,0:T(8,128)S(1)} %get-tuple-element.150), channel_id=1, source_target_pairs={{0,4},{4,8},{8,12},{12,0},{1,5},{5,9},{9,13},{13,1},{2,6},{6,10},{... | collective-permute-start | bytes 393224 | tf_op jit(solution)/shard_map/ppermute | solution.py:39
  27.1 10.8 %collective-permute-start.2 = (f32[256,128]{1,0:T(8,128)S(1)}, f32[256,128]{1,0:T(8,128)S(1)}, u32[]{:S(2)}, u32[]{:S(2)}) collective-permute-start(f32[256,128]{1,0:T(8,128)S(1)} %get-tuple-element.149), channel_id=1, source_target_pairs={{0,8},{4,12},{8,0},{12,4},{1,9},{5,13},{9,1},{13,5},{2,10},{6,14},... | collective-permute-start | bytes 393224 | tf_op jit(solution)/shard_map/ppermute | solution.py:39
  29.1 8.9 %collective-permute-start.3 = (f32[256,128]{1,0:T(8,128)S(1)}, f32[256,128]{1,0:T(8,128)S(1)}, u32[]{:S(2)}, u32[]{:S(2)}) collective-permute-start(f32[256,128]{1,0:T(8,128)S(1)} %get-tuple-element.148), channel_id=1, source_target_pairs={{0,12},{4,0},{8,4},{12,8},{1,13},{5,1},{9,5},{13,9},{2,14},{6,2},{... | collective-permute-start | bytes 393224 | tf_op jit(solution)/shard_map/ppermute | solution.py:39
  39.0 97.0 %all-gather.9.cloned.1.call-start = ((), (), s32[]{:S(2)}) async-start(), calls=%async_computation.2 | async-start | bytes 3932160 | tf_op jit(solution)/shard_map/all_gather | solution.py:436
  39.1 30.5 %collective-permute-start.8 = (f32[4,512,128]{2,1,0:T(8,128)}, f32[4,512,128]{2,1,0:T(8,128)S(1)}, u32[]{:S(2)}, u32[]{:S(2)}) collective-permute-start(f32[4,512,128]{2,1,0:T(8,128)} %all-to-all-done.refs_4_.refs_5_), channel_id=1, source_target_pairs={{0,4},{4,8},{8,12},{12,0},{1,5},{5,9},{9,13},{13,1},{2,6},{6,10},{... | collective-permute-start | bytes 3145736 | tf_op jit(solution)/shard_map/ppermute | solution.py:39
  39.2 30.4 %collective-permute-start.9 = (f32[4,512,128]{2,1,0:T(8,128)}, f32[4,512,128]{2,1,0:T(8,128)S(1)}, u32[]{:S(2)}, u32[]{:S(2)}) collective-permute-start(f32[4,512,128]{2,1,0:T(8,128)} %all-to-all-done.refs_4_.refs_5_), channel_id=1, source_target_pairs={{0,12},{4,0},{8,4},{12,8},{1,13},{5,1},{9,5},{13,9},{2,14},{6,2},{... | collective-permute-start | bytes 3145736 | tf_op jit(solution)/shard_map/ppermute | solution.py:39
  42.4 5.0 %collective-permute-start.13 = (f32[1,256,128]{2,1,0:T(8,128)S(1)}, f32[1,256,128]{2,1,0:T(8,128)S(1)}, u32[]{:S(2)}, u32[]{:S(2)}) collective-permute-start(f32[1,256,128]{2,1,0:T(8,128)S(1)} %bitcast.99), channel_id=1, source_target_pairs={{0,32},{32,0},{1,33},{33,1},{2,34},{34,2},{3,35},{35,3},{4,36},{36... | collective-permute-start | bytes 393224 | tf_op jit(solution)/shard_map/ppermute | solution.py:43
  43.9 9.4 %collective-permute-start.12 = (f32[256,128]{1,0:T(8,128)S(1)}, f32[256,128]{1,0:T(8,128)S(1)}, u32[]{:S(2)}, u32[]{:S(2)}) collective-permute-start(f32[256,128]{1,0:T(8,128)S(1)} %copy-done.10), channel_id=1, source_target_pairs={{0,32},{32,0},{1,33},{33,1},{2,34},{34,2},{3,35},{35,3},{4,36},{36... | collective-permute-start | bytes 393224 | tf_op jit(solution)/shard_map/ppermute | solution.py:43
  47.4 9.0 %collective-permute-start.15 = (f32[16,2048]{1,0:T(8,128)S(1)}, f32[16,2048]{1,0:T(8,128)S(1)}, u32[]{:S(2)}, u32[]{:S(2)}) collective-permute-start(f32[16,2048]{1,0:T(8,128)S(1)} %copy-done), channel_id=1, source_target_pairs={{0,1},{1,2},{2,3},{3,0},{4,5},{5,6},{6,7},{7,4},{8,9},{9,10},{10,1... | collective-permute-start | bytes 393224 | tf_op jit(solution)/shard_map/ppermute | solution.py:39
  50.3 10.7 %collective-permute-start.16 = (f32[16,2048]{1,0:T(8,128)S(1)}, f32[16,2048]{1,0:T(8,128)S(1)}, u32[]{:S(2)}, u32[]{:S(2)}) collective-permute-start(f32[16,2048]{1,0:T(8,128)S(1)} %copy-done), channel_id=1, source_target_pairs={{0,2},{1,3},{2,0},{3,1},{4,6},{5,7},{6,4},{7,5},{8,10},{9,11},{10,... | collective-permute-start | bytes 393224 | tf_op jit(solution)/shard_map/ppermute | solution.py:39
  53.3 16.2 %collective-permute-start.14 = (f32[2,256,128]{2,1,0:T(8,128)S(1)}, f32[2,256,128]{2,1,0:T(8,128)S(1)}, u32[]{:S(2)}, u32[]{:S(2)}) collective-permute-start(f32[2,256,128]{2,1,0:T(8,128)S(1)} %maximum_select_fusion.2), channel_id=1, source_target_pairs={{0,64},{64,0},{1,65},{65,1},{2,66},{66,2},{3,67},{67,3},{4,68},{68... | collective-permute-start | bytes 786440 | tf_op jit(solution)/shard_map/ppermute | solution.py:43
  56.3 13.2 %collective-permute-start.11 = (f32[2,256,128]{2,1,0:T(8,128)S(1)}, f32[2,256,128]{2,1,0:T(8,128)S(1)}, u32[]{:S(2)}, u32[]{:S(2)}) collective-permute-start(f32[2,256,128]{2,1,0:T(8,128)S(1)} %maximum_select_fusion), channel_id=1, source_target_pairs={{0,32},{32,0},{1,33},{33,1},{2,34},{34,2},{3,35},{35,3},{4,36},{36... | collective-permute-start | bytes 786440 | tf_op jit(solution)/shard_map/ppermute | solution.py:43
  61.0 8.5 %collective-permute-start.17 = (f32[16,2048]{1,0:T(8,128)S(1)}, f32[16,2048]{1,0:T(8,128)S(1)}, u32[]{:S(2)}, u32[]{:S(2)}) collective-permute-start(f32[16,2048]{1,0:T(8,128)S(1)} %copy-done), channel_id=1, source_target_pairs={{0,3},{1,0},{2,1},{3,2},{4,7},{5,4},{6,5},{7,6},{8,11},{9,8},{10,9... | collective-permute-start | bytes 393224 | tf_op jit(solution)/shard_map/ppermute | solution.py:39
  69.6 15.7 %collective-permute-start.19 = (f32[2,512,128]{2,1,0:T(8,128)S(1)}, f32[2,512,128]{2,1,0:T(8,128)}, u32[]{:S(2)}, u32[]{:S(2)}) collective-permute-start(f32[2,512,128]{2,1,0:T(8,128)S(1)} %slice.47), channel_id=1, source_target_pairs={{0,4},{4,8},{8,12},{12,0},{1,5},{5,9},{9,13},{13,1},{2,6},{6,10},{... | collective-permute-start | bytes 1572872 | tf_op jit(solution)/shard_map/ppermute | solution.py:39
  71.3 16.4 %collective-permute-start.20 = (f32[2,512,128]{2,1,0:T(8,128)}, f32[2,512,128]{2,1,0:T(8,128)}, u32[]{:S(2)}, u32[]{:S(2)}) collective-permute-start(f32[2,512,128]{2,1,0:T(8,128)} %slice.48), channel_id=1, source_target_pairs={{0,12},{4,0},{8,4},{12,8},{1,13},{5,1},{9,5},{13,9},{2,14},{6,2},{... | collective-permute-start | bytes 1572872 | tf_op jit(solution)/shard_map/ppermute | solution.py:39
  74.1 19.4 %collective-permute-start.37 = (f32[256,128]{1,0:T(8,128)S(1)}, f32[256,128]{1,0:T(8,128)S(1)}, u32[]{:S(2)}, u32[]{:S(2)}) collective-permute-start(f32[256,128]{1,0:T(8,128)S(1)} %get-tuple-element.154), channel_id=1, source_target_pairs={{0,4},{4,8},{8,12},{12,0},{1,5},{5,9},{9,13},{13,1},{2,6},{6,10},{... | collective-permute-start | bytes 393224 | tf_op jit(solution)/shard_map/ppermute | solution.py:39
  74.2 19.4 %collective-permute-start.38 = (f32[256,128]{1,0:T(8,128)S(1)}, f32[256,128]{1,0:T(8,128)S(1)}, u32[]{:S(2)}, u32[]{:S(2)}) collective-permute-start(f32[256,128]{1,0:T(8,128)S(1)} %get-tuple-element.153), channel_id=1, source_target_pairs={{0,8},{4,12},{8,0},{12,4},{1,9},{5,13},{9,1},{13,5},{2,10},{6,14},... | collective-permute-start | bytes 393224 | tf_op jit(solution)/shard_map/ppermute | solution.py:39
  75.6 17.9 %collective-permute-start.39 = (f32[256,128]{1,0:T(8,128)S(1)}, f32[256,128]{1,0:T(8,128)S(1)}, u32[]{:S(2)}, u32[]{:S(2)}) collective-permute-start(f32[256,128]{1,0:T(8,128)S(1)} %get-tuple-element.152), channel_id=1, source_target_pairs={{0,12},{4,0},{8,4},{12,8},{1,13},{5,1},{9,5},{13,9},{2,14},{6,2},{... | collective-permute-start | bytes 393224 | tf_op jit(solution)/shard_map/ppermute | solution.py:39
  94.5 74.2 %all-gather.11.cloned.1.call-start = ((), (), s32[]{:S(2)}) async-start(), calls=%async_computation.3 | async-start | bytes 2621440 | tf_op jit(solution)/shard_map/all_gather | solution.py:436
  94.6 4.8 %collective-permute-start.21 = (f32[16,1024]{1,0:T(8,128)S(1)}, f32[16,1024]{1,0:T(8,128)S(1)}, u32[]{:S(2)}, u32[]{:S(2)}) collective-permute-start(f32[16,1024]{1,0:T(8,128)S(1)} %get-tuple-element.97), channel_id=1, source_target_pairs={{0,3},{1,0},{2,1},{3,2},{4,7},{5,4},{6,5},{7,6},{8,11},{9,8},{10,9... | collective-permute-start | bytes 196616 | tf_op jit(solution)/shard_map/ppermute | solution.py:39
  99.4 24.5 %collective-permute-start.31 = (f32[4,6,256,128]{3,2,1,0:T(8,128)}, f32[4,6,256,128]{3,2,1,0:T(8,128)}, u32[]{:S(2)}, u32[]{:S(2)}) collective-permute-start(f32[4,6,256,128]{3,2,1,0:T(8,128)} %bitcast.84), channel_id=1, source_target_pairs={{0,16},{16,0},{1,17},{17,1},{2,18},{18,2},{3,19},{19,3},{4,20},{20... | collective-permute-start | bytes 9437192 | tf_op jit(solution)/shard_map/ppermute | solution.py:43
  99.4 9.7 %collective-permute-start.22 = (f32[16,1024]{1,0:T(8,128)S(1)}, f32[16,1024]{1,0:T(8,128)S(1)}, u32[]{:S(2)}, u32[]{:S(2)}) collective-permute-start(f32[16,1024]{1,0:T(8,128)S(1)} %get-tuple-element.98), channel_id=1, source_target_pairs={{0,2},{1,3},{2,0},{3,1},{4,6},{5,7},{6,4},{7,5},{8,10},{9,11},{10,... | collective-permute-start | bytes 196616 | tf_op jit(solution)/shard_map/ppermute | solution.py:39
  101.9 7.2 %collective-permute-start.23 = (f32[16,1024]{1,0:T(8,128)S(1)}, f32[16,1024]{1,0:T(8,128)S(1)}, u32[]{:S(2)}, u32[]{:S(2)}) collective-permute-start(f32[16,1024]{1,0:T(8,128)S(1)} %get-tuple-element.99), channel_id=1, source_target_pairs={{0,1},{1,2},{2,3},{3,0},{4,5},{5,6},{6,7},{7,4},{8,9},{9,10},{10,1... | collective-permute-start | bytes 196616 | tf_op jit(solution)/shard_map/ppermute | solution.py:39
  103.9 7.3 %collective-permute-start.25 = (f32[256,128]{1,0:T(8,128)S(1)}, f32[256,128]{1,0:T(8,128)S(1)}, u32[]{:S(2)}, u32[]{:S(2)}) collective-permute-start(f32[256,128]{1,0:T(8,128)S(1)} %get-tuple-element.158), channel_id=1, source_target_pairs={{0,4},{4,8},{8,12},{12,0},{1,5},{5,9},{9,13},{13,1},{2,6},{6,10},{... | collective-permute-start | bytes 393224 | tf_op jit(solution)/shard_map/ppermute | solution.py:39
  103.9 11.2 %collective-permute-start.26 = (f32[256,128]{1,0:T(8,128)S(1)}, f32[256,128]{1,0:T(8,128)S(1)}, u32[]{:S(2)}, u32[]{:S(2)}) collective-permute-start(f32[256,128]{1,0:T(8,128)S(1)} %get-tuple-element.157), channel_id=1, source_target_pairs={{0,8},{4,12},{8,0},{12,4},{1,9},{5,13},{9,1},{13,5},{2,10},{6,14},... | collective-permute-start | bytes 393224 | tf_op jit(solution)/shard_map/ppermute | solution.py:39
  109.1 6.1 %collective-permute-start.27 = (f32[256,128]{1,0:T(8,128)S(1)}, f32[256,128]{1,0:T(8,128)S(1)}, u32[]{:S(2)}, u32[]{:S(2)}) collective-permute-start(f32[256,128]{1,0:T(8,128)S(1)} %get-tuple-element.156), channel_id=1, source_target_pairs={{0,12},{4,0},{8,4},{12,8},{1,13},{5,1},{9,5},{13,9},{2,14},{6,2},{... | collective-permute-start | bytes 393224 | tf_op jit(solution)/shard_map/ppermute | solution.py:39
  109.1 6.1 %collective-permute-start.24 = (f32[8,1024]{1,0:T(8,128)S(1)}, f32[8,1024]{1,0:T(8,128)S(1)}, u32[]{:S(2)}, u32[]{:S(2)}) collective-permute-start(f32[8,1024]{1,0:T(8,128)S(1)} %get-tuple-element.173), channel_id=1, source_target_pairs={{0,16},{16,0},{1,17},{17,1},{2,18},{18,2},{3,19},{19,3},{4,20},{20... | collective-permute-start | bytes 98312 | tf_op jit(solution)/shard_map/ppermute | solution.py:43
  115.9 6.1 %collective-permute-start.28 = (f32[8,2048]{1,0:T(8,128)S(1)}, f32[8,2048]{1,0:T(8,128)S(1)}, u32[]{:S(2)}, u32[]{:S(2)}) collective-permute-start(f32[8,2048]{1,0:T(8,128)S(1)} %get-tuple-element.105.refs_0_), channel_id=1, source_target_pairs={{0,4},{4,8},{8,12},{12,0},{1,5},{5,9},{9,13},{13,1},{2,6},{6,10},{... | collective-permute-start | bytes 196616 | tf_op jit(solution)/shard_map/ppermute | solution.py:39
  116.0 7.1 %collective-permute-start.29 = (f32[8,2048]{1,0:T(8,128)S(1)}, f32[8,2048]{1,0:T(8,128)S(1)}, u32[]{:S(2)}, u32[]{:S(2)}) collective-permute-start(f32[8,2048]{1,0:T(8,128)S(1)} %get-tuple-element.105.refs_0_), channel_id=1, source_target_pairs={{0,8},{4,12},{8,0},{12,4},{1,9},{5,13},{9,1},{13,5},{2,10},{6,14},... | collective-permute-start | bytes 196616 | tf_op jit(solution)/shard_map/ppermute | solution.py:39
  119.6 10.9 %collective-permute-start.33 = (f32[2,4,2048]{2,1,0:T(4,128)S(1)}, f32[2,4,2048]{2,1,0:T(4,128)S(1)}, u32[]{:S(2)}, u32[]{:S(2)}) collective-permute-start(f32[2,4,2048]{2,1,0:T(4,128)S(1)} %get-tuple-element.114), channel_id=1, source_target_pairs={{0,32},{32,0},{1,33},{33,1},{2,34},{34,2},{3,35},{35,3},{4,36},{36... | collective-permute-start | bytes 196616 | tf_op jit(solution)/shard_map/ppermute | solution.py:43
  136.0 12.0 %collective-permute-start.40 = (f32[4,6,256,128]{3,2,1,0:T(8,128)}, f32[4,6,256,128]{3,2,1,0:T(8,128)}, u32[]{:S(2)}, u32[]{:S(2)}) collective-permute-start(f32[4,6,256,128]{3,2,1,0:T(8,128)} %bitcast.87), channel_id=1, source_target_pairs={{0,16},{16,0},{1,17},{17,1},{2,18},{18,2},{3,19},{19,3},{4,20},{20... | collective-permute-start | bytes 9437192 | tf_op jit(solution)/shard_map/ppermute | solution.py:43
  136.9 8.8 %collective-permute-start.34 = (f32[16,2048]{1,0:T(8,128)S(1)}, f32[16,2048]{1,0:T(8,128)S(1)}, u32[]{:S(2)}, u32[]{:S(2)}) collective-permute-start(f32[16,2048]{1,0:T(8,128)S(1)} %get-tuple-element.115.refs_0_), channel_id=1, source_target_pairs={{0,4},{4,8},{8,12},{12,0},{1,5},{5,9},{9,13},{13,1},{2,6},{6,10},{... | collective-permute-start | bytes 393224 | tf_op jit(solution)/shard_map/ppermute | solution.py:39
  138.5 9.5 %collective-permute-start.35 = (f32[16,2048]{1,0:T(8,128)S(1)}, f32[16,2048]{1,0:T(8,128)S(1)}, u32[]{:S(2)}, u32[]{:S(2)}) collective-permute-start(f32[16,2048]{1,0:T(8,128)S(1)} %get-tuple-element.115.refs_0_), channel_id=1, source_target_pairs={{0,8},{4,12},{8,0},{12,4},{1,9},{5,13},{9,1},{13,5},{2,10},{6,14},... | collective-permute-start | bytes 393224 | tf_op jit(solution)/shard_map/ppermute | solution.py:39
  141.4 6.7 %collective-permute-start.36 = (f32[16,2048]{1,0:T(8,128)S(1)}, f32[16,2048]{1,0:T(8,128)S(1)}, u32[]{:S(2)}, u32[]{:S(2)}) collective-permute-start(f32[16,2048]{1,0:T(8,128)S(1)} %get-tuple-element.115.refs_0_), channel_id=1, source_target_pairs={{0,12},{4,0},{8,4},{12,8},{1,13},{5,1},{9,5},{13,9},{2,14},{6,2},{... | collective-permute-start | bytes 393224 | tf_op jit(solution)/shard_map/ppermute | solution.py:39
  142.7 13.2 %collective-permute-start.42 = (f32[8,2048]{1,0:T(8,128)S(1)}, f32[8,2048]{1,0:T(8,128)S(1)}, u32[]{:S(2)}, u32[]{:S(2)}) collective-permute-start(f32[8,2048]{1,0:T(8,128)S(1)} %get-tuple-element.127), channel_id=1, source_target_pairs={{0,64},{64,0},{1,65},{65,1},{2,66},{66,2},{3,67},{67,3},{4,68},{68... | collective-permute-start | bytes 196616 | tf_op jit(solution)/shard_map/ppermute | solution.py:43
  152.8 5.5 %collective-permute-start.41 = (f32[8,1024]{1,0:T(8,128)S(1)}, f32[8,1024]{1,0:T(8,128)S(1)}, u32[]{:S(2)}, u32[]{:S(2)}) collective-permute-start(f32[8,1024]{1,0:T(8,128)S(1)} %get-tuple-element.125), channel_id=1, source_target_pairs={{0,64},{64,0},{1,65},{65,1},{2,66},{66,2},{3,67},{67,3},{4,68},{68... | collective-permute-start | bytes 98312 | tf_op jit(solution)/shard_map/ppermute | solution.py:43
  168.7 8.7 %collective-permute-start.46 = (f32[4,4,256,128]{3,2,1,0:T(8,128)}, f32[4,4,256,128]{3,2,1,0:T(8,128)S(1)}, u32[]{:S(2)}, u32[]{:S(2)}) collective-permute-start(f32[4,4,256,128]{3,2,1,0:T(8,128)} %bitcast.90), channel_id=1, source_target_pairs={{0,16},{16,0},{1,17},{17,1},{2,18},{18,2},{3,19},{19,3},{4,20},{20... | collective-permute-start | bytes 6291464 | tf_op jit(solution)/shard_map/ppermute | solution.py:43
  168.7 5.9 %collective-permute-start.43 = (f32[8,2048]{1,0:T(8,128)S(1)}, f32[8,2048]{1,0:T(8,128)S(1)}, u32[]{:S(2)}, u32[]{:S(2)}) collective-permute-start(f32[8,2048]{1,0:T(8,128)S(1)} %s23.1.c0), channel_id=1, source_target_pairs={{0,4},{4,8},{8,12},{12,0},{1,5},{5,9},{9,13},{13,1},{2,6},{6,10},{... | collective-permute-start | bytes 196616 | tf_op jit(solution)/shard_map/ppermute | solution.py:39
  170.3 6.7 %collective-permute-start.44 = (f32[8,2048]{1,0:T(8,128)S(1)}, f32[8,2048]{1,0:T(8,128)S(1)}, u32[]{:S(2)}, u32[]{:S(2)}) collective-permute-start(f32[8,2048]{1,0:T(8,128)S(1)} %s23.1.c0), channel_id=1, source_target_pairs={{0,8},{4,12},{8,0},{12,4},{1,9},{5,13},{9,1},{13,5},{2,10},{6,14},... | collective-permute-start | bytes 196616 | tf_op jit(solution)/shard_map/ppermute | solution.py:39
  183.4 5.7 %collective-permute-start.47 = (f32[8,2048]{1,0:T(8,128)S(1)}, f32[8,2048]{1,0:T(8,128)S(1)}, u32[]{:S(2)}, u32[]{:S(2)}) collective-permute-start(f32[8,2048]{1,0:T(8,128)S(1)} %top.1.c0), channel_id=1, source_target_pairs={{0,4},{4,8},{8,12},{12,0},{1,5},{5,9},{9,13},{13,1},{2,6},{6,10},{... | collective-permute-start | bytes 196616 | tf_op jit(solution)/shard_map/ppermute | solution.py:39
  184.4 6.1 %collective-permute-start.48 = (f32[8,2048]{1,0:T(8,128)S(1)}, f32[8,2048]{1,0:T(8,128)S(1)}, u32[]{:S(2)}, u32[]{:S(2)}) collective-permute-start(f32[8,2048]{1,0:T(8,128)S(1)} %top.1.c0), channel_id=1, source_target_pairs={{0,8},{4,12},{8,0},{12,4},{1,9},{5,13},{9,1},{13,5},{2,10},{6,14},... | collective-permute-start | bytes 196616 | tf_op jit(solution)/shard_map/ppermute | solution.py:39
  192.5 5.8 %collective-permute-start.50 = (f32[8,2048]{1,0:T(8,128)S(1)}, f32[8,2048]{1,0:T(8,128)S(1)}, u32[]{:S(2)}, u32[]{:S(2)}) collective-permute-start(f32[8,2048]{1,0:T(8,128)S(1)} %x3.1), channel_id=1, source_target_pairs={{0,64},{64,0},{1,65},{65,1},{2,66},{66,2},{3,67},{67,3},{4,68},{68... | collective-permute-start | bytes 196616 | tf_op jit(solution)/shard_map/ppermute | solution.py:43
  203.1 6.2 %collective-permute-start.51 = (f32[16,2048]{1,0:T(8,128)S(1)}, f32[16,2048]{1,0:T(8,128)S(1)}, u32[]{:S(2)}, u32[]{:S(2)}) collective-permute-start(f32[16,2048]{1,0:T(8,128)S(1)} %b2.1.c0), channel_id=1, source_target_pairs={{0,4},{4,8},{8,12},{12,0},{1,5},{5,9},{9,13},{13,1},{2,6},{6,10},{... | collective-permute-start | bytes 393224 | tf_op jit(solution)/shard_map/ppermute | solution.py:39
  203.4 7.5 %collective-permute-start.52 = (f32[16,2048]{1,0:T(8,128)S(1)}, f32[16,2048]{1,0:T(8,128)S(1)}, u32[]{:S(2)}, u32[]{:S(2)}) collective-permute-start(f32[16,2048]{1,0:T(8,128)S(1)} %b2.1.c0), channel_id=1, source_target_pairs={{0,8},{4,12},{8,0},{12,4},{1,9},{5,13},{9,1},{13,5},{2,10},{6,14},... | collective-permute-start | bytes 393224 | tf_op jit(solution)/shard_map/ppermute | solution.py:39
  206.6 5.0 %collective-permute-start.53 = (f32[16,2048]{1,0:T(8,128)S(1)}, f32[16,2048]{1,0:T(8,128)S(1)}, u32[]{:S(2)}, u32[]{:S(2)}) collective-permute-start(f32[16,2048]{1,0:T(8,128)S(1)} %b2.1.c0), channel_id=1, source_target_pairs={{0,12},{4,0},{8,4},{12,8},{1,13},{5,1},{9,5},{13,9},{2,14},{6,2},{... | collective-permute-start | bytes 393224 | tf_op jit(solution)/shard_map/ppermute | solution.py:39
  213.8 11.3 %collective-permute-start.58 = (f32[2,4,2048]{2,1,0:T(4,128)S(1)}, f32[2,4,2048]{2,1,0:T(4,128)S(1)}, u32[]{:S(2)}, u32[]{:S(2)}) collective-permute-start(f32[2,4,2048]{2,1,0:T(4,128)S(1)} %slice.51.a_mine), channel_id=1, source_target_pairs={{0,32},{32,0},{1,33},{33,1},{2,34},{34,2},{3,35},{35,3},{4,36},{36... | collective-permute-start | bytes 196616 | tf_op jit(solution)/shard_map/ppermute | solution.py:43
  221.4 5.3 %collective-permute-start.55 = (f32[8,2048]{1,0:T(8,128)S(1)}, f32[8,2048]{1,0:T(8,128)S(1)}, u32[]{:S(2)}, u32[]{:S(2)}) collective-permute-start(f32[8,2048]{1,0:T(8,128)S(1)} %get-tuple-element.138), channel_id=1, source_target_pairs={{0,12},{4,0},{8,4},{12,8},{1,13},{5,1},{9,5},{13,9},{2,14},{6,2},{... | collective-permute-start | bytes 196616 | tf_op jit(solution)/shard_map/ppermute | solution.py:39
  224.1 5.8 %collective-permute-start.56 = (f32[8,2048]{1,0:T(8,128)S(1)}, f32[8,2048]{1,0:T(8,128)S(1)}, u32[]{:S(2)}, u32[]{:S(2)}) collective-permute-start(f32[8,2048]{1,0:T(8,128)S(1)} %get-tuple-element.139), channel_id=1, source_target_pairs={{0,8},{4,12},{8,0},{12,4},{1,9},{5,13},{9,1},{13,5},{2,10},{6,14},... | collective-permute-start | bytes 196616 | tf_op jit(solution)/shard_map/ppermute | solution.py:39
  224.4 6.2 %collective-permute-start.57 = (f32[8,2048]{1,0:T(8,128)S(1)}, f32[8,2048]{1,0:T(8,128)S(1)}, u32[]{:S(2)}, u32[]{:S(2)}) collective-permute-start(f32[8,2048]{1,0:T(8,128)S(1)} %get-tuple-element.140), channel_id=1, source_target_pairs={{0,4},{4,8},{8,12},{12,0},{1,5},{5,9},{9,13},{13,1},{2,6},{6,10},{... | collective-permute-start | bytes 196616 | tf_op jit(solution)/shard_map/ppermute | solution.py:39
  231.4 17.7 %collective-permute-start.67 = (f32[8,512]{1,0:T(8,128)S(1)}, f32[8,512]{1,0:T(8,128)S(1)}, u32[]{:S(2)}, u32[]{:S(2)}) collective-permute-start(f32[8,512]{1,0:T(8,128)S(1)} %get-tuple-element.170), channel_id=1, source_target_pairs={{0,16},{16,0},{1,17},{17,1},{2,18},{18,2},{3,19},{19,3},{4,20},{20... | collective-permute-start | bytes 49160 | tf_op jit(solution)/shard_map/ppermute | solution.py:43
  232.0 17.7 %collective-permute-start.66 = (f32[8,1024]{1,0:T(8,128)S(1)}, f32[8,1024]{1,0:T(8,128)S(1)}, u32[]{:S(2)}, u32[]{:S(2)}) collective-permute-start(f32[8,1024]{1,0:T(8,128)S(1)} %get-tuple-element.172), channel_id=1, source_target_pairs={{0,16},{16,0},{1,17},{17,1},{2,18},{18,2},{3,19},{19,3},{4,20},{20... | collective-permute-start | bytes 98312 | tf_op jit(solution)/shard_map/ppermute | solution.py:43
  233.1 6.8 %collective-permute-start.60 = (f32[16,1024]{1,0:T(8,128)S(1)}, f32[16,1024]{1,0:T(8,128)S(1)}, u32[]{:S(2)}, u32[]{:S(2)}) collective-permute-start(f32[16,1024]{1,0:T(8,128)S(1)} %maximum_select_fusion.3.refs_0_), channel_id=1, source_target_pairs={{0,1},{1,2},{2,3},{3,0},{4,5},{5,6},{6,7},{7,4},{8,9},{9,10},{10,1... | collective-permute-start | bytes 196616 | tf_op jit(solution)/shard_map/ppermute | solution.py:39
  233.6 6.3 %collective-permute-start.61 = (f32[16,1024]{1,0:T(8,128)S(1)}, f32[16,1024]{1,0:T(8,128)S(1)}, u32[]{:S(2)}, u32[]{:S(2)}) collective-permute-start(f32[16,1024]{1,0:T(8,128)S(1)} %maximum_select_fusion.3.refs_0_), channel_id=1, source_target_pairs={{0,2},{1,3},{2,0},{3,1},{4,6},{5,7},{6,4},{7,5},{8,10},{9,11},{10,... | collective-permute-start | bytes 196616 | tf_op jit(solution)/shard_map/ppermute | solution.py:39
  235.4 5.1 %collective-permute-start.62 = (f32[16,1024]{1,0:T(8,128)S(1)}, f32[16,1024]{1,0:T(8,128)S(1)}, u32[]{:S(2)}, u32[]{:S(2)}) collective-permute-start(f32[16,1024]{1,0:T(8,128)S(1)} %maximum_select_fusion.3.refs_0_), channel_id=1, source_target_pairs={{0,3},{1,0},{2,1},{3,2},{4,7},{5,4},{6,5},{7,6},{8,11},{9,8},{10,9... | collective-permute-start | bytes 196616 | tf_op jit(solution)/shard_map/ppermute | solution.py:39
  245.4 7.5 %collective-permute-start.63 = (f32[16,2048]{1,0:T(8,128)S(1)}, f32[16,2048]{1,0:T(8,128)S(1)}, u32[]{:S(2)}, u32[]{:S(2)}) collective-permute-start(f32[16,2048]{1,0:T(8,128)S(1)} %get-tuple-element.144), channel_id=1, source_target_pairs={{0,3},{1,0},{2,1},{3,2},{4,7},{5,4},{6,5},{7,6},{8,11},{9,8},{10,9... | collective-permute-start | bytes 393224 | tf_op jit(solution)/shard_map/ppermute | solution.py:39
  248.1 7.1 %collective-permute-start.64 = (f32[16,2048]{1,0:T(8,128)S(1)}, f32[16,2048]{1,0:T(8,128)S(1)}, u32[]{:S(2)}, u32[]{:S(2)}) collective-permute-start(f32[16,2048]{1,0:T(8,128)S(1)} %get-tuple-element.145), channel_id=1, source_target_pairs={{0,2},{1,3},{2,0},{3,1},{4,6},{5,7},{6,4},{7,5},{8,10},{9,11},{10,... | collective-permute-start | bytes 393224 | tf_op jit(solution)/shard_map/ppermute | solution.py:39
  248.6 7.9 %collective-permute-start.65 = (f32[16,2048]{1,0:T(8,128)S(1)}, f32[16,2048]{1,0:T(8,128)S(1)}, u32[]{:S(2)}, u32[]{:S(2)}) collective-permute-start(f32[16,2048]{1,0:T(8,128)S(1)} %get-tuple-element.146), channel_id=1, source_target_pairs={{0,1},{1,2},{2,3},{3,0},{4,5},{5,6},{6,7},{7,4},{8,9},{9,10},{10,1... | collective-permute-start | bytes 393224 | tf_op jit(solution)/shard_map/ppermute | solution.py:39
  (27 other events, 354.0 us)
Sparse Core Ops, SparseCore 0:
  39.1 45.6 all-gather.6
  94.7 41.2 all-gather.8
  137.7 31.0 all-gather.10

commit v9 on v8

--- a/solution.py
+++ b/solution.py
@@ -455,20 +455,19 @@
     f2 = joined(off2, 1)
     e3 = joined(dinv3[None], 1)
     e3_other = flip(e3, "x1")
-    c0 = gather4(rhs0, "y")
+    e2 = over_z(for_z(e2, e2_other, x0))
     b_mine, b_other = halves(jnp.concatenate([rhs1, rhs2, rhs3], 1), ci)
     b_other = flip(b_other, "core")
-    ea, eb, e2, e2_other, f2, e3, e3_other, c0, b_mine, b_other = gate(
-        (ea, eb, e2, e2_other, f2, e3, e3_other, c0, b_mine, b_other)
+    ea, eb, e2, f2, e3, e3_other, b_mine, b_other = gate(
+        (ea, eb, e2, f2, e3, e3_other, b_mine, b_other)
     )
 
     ec, ed = shift(ea[:2], "z", 1), shift(eb[2:], "z", -1)
-    e2 = over_z(for_z(e2, e2_other, x0))
-    e2[0], ec, ed = gate((e2[0], ec, ed))
+    m2 = gathered(e2, f2)
+    e3 = over_z(for_z(e3, e3_other, x1))
+    c0 = gather4(rhs0, "y")
+    e3[0], ec, ed, c0 = gate((e3[0], ec, ed, c0))
     w0 = [e0, ea, eb, ec, ed, off0, fa, fb, fc, fd]
-    e3 = over_z(for_z(e3, e3_other, x1))
-    e3, b_mine = gate((e3, b_mine))
-    m3 = gathered(e3, None)
 
     dma = pltpu.SemaphoreType.DMA
     ev, fv = pltpu.VMEM((4, 4, 512, B), f32), pltpu.VMEM((4, 4, 256, B), f32)
@@ -483,12 +482,12 @@
         functools.partial(forward_kernel, 0, 64, "rs"), "f0", [(64, 512)] + [(16, 1024)] * 4,
         [ev, fv, *work(64), dma((10,))], meta, c0, w0, flops(64),
     )
-    e2, _ = gate((e2, y0))
-    m2 = gathered(e2, f2)
     parts = scatter4(u, "y")
-    m1, _ = gate((m1, parts[1]))
+    e3, _ = gate((e3, y0))
+    m3 = gathered(e3, None)
+    u = (parts[0] + parts[1]) + (parts[2] + parts[3])
+    m1, _ = gate((m1, u))
     w1 = m1, flip(m1, "core")
-    u = (parts[0] + parts[1]) + (parts[2] + parts[3])
     keep, give = halves(u, ci)
     c1, pk, pg = call(
         s01_kernel, "s01", [(8, ORDER), (2, 4, ORDER), (2, 4, ORDER)],

time: 264 us -> 269 us (1.019)
  local copies, waits for them, and re-layouts: 8.28 us -> 16.7 us
  starting transfers between devices: 99.8 us -> 94.8 us
    ppermute x22, waiting for transfers between devices: 14.7 us -> 31.9 us  [flip(): return lax.ppermute(v, axis, [(0, 1), (1, 0)])]
    ppermute x47, waiting for transfers between devices: 72.2 us -> 59.2 us  [shift(): return lax.ppermute(v, axis, [(i, (i + s) % 4) for i in range(4)])]
    unnamed x47, local copies, waits for them, and re-layouts: 4.85 us -> 10.4 us
    ppermute x22, starting transfers between devices: 21.6 us -> 16.9 us  [flip(): return lax.ppermute(v, axis, [(0, 1), (1, 0)])]
    all_gather x3, waiting for transfers between devices: 11.9 us -> 8.08 us  [gathered(): return lax.all_gather(jnp.concatenate(parts, 0), 'y', axis=0, tiled=False)]
  transfers between devices with their start and end apart: 73 -> 73, of which waited for: 38 -> 43; matrix products, arithmetic and copies ran while one was open for 3% -> 4% of each run, Pallas kernels for 10% -> 10%
where the time goes in v9:
time: 269 us
  waiting for transfers between devices  99.2 us (37%)
  starting transfers between devices  94.8 us (35%)
  Pallas kernels  38.7 us (14%)
  local copies, waits for them, and re-layouts  16.7 us (6%)
  between operations  14.4 us (5%)
  other arithmetic  4.76 us (2%)
    ppermute x47, starting transfers between devices, shift(): return lax.ppermute(v, axis, [(i, (i + s) % 4) for i in range(4)])  73.2 us
    ppermute x47, waiting for transfers between devices, shift(): return lax.ppermute(v, axis, [(i, (i + s) % 4) for i in range(4)])  59.2 us
    pallas_call x13, Pallas kernels, call(): pl.pallas_call(kernel, out_shape=[jax.ShapeDtypeStruct(s, f32) for s in s...  38.7 us
    ppermute x22, waiting for transfers between devices, flip(): return lax.ppermute(v, axis, [(0, 1), (1, 0)])  31.9 us
    ppermute x22, starting transfers between devices, flip(): return lax.ppermute(v, axis, [(0, 1), (1, 0)])  16.9 us
    unnamed x47, local copies, waits for them, and re-layouts  10.4 us
    all_gather x3, waiting for transfers between devices, gathered(): return lax.all_gather(jnp.concatenate(parts, 0), 'y', axis=0, tiled=False)  8.08 us
  transfers between devices with their start and end apart: 73, of which 43 were waited for; matrix products, arithmetic and copies ran while one was open for 4% of the time, Pallas kernels for 10%

profile of v9, /device:TPU:0, one launch (start us, length us, event | category | flops | bytes accessed | tf_op | source)
XLA Modules:
  0.0 268.5 jit_solution(12494411595184690176)
XLA Ops:
  7.2 2.1 collective-permute-start.4
  9.2 2.2 collective-permute-start.5
  11.4 2.3 copy.22
  13.8 4.6 %all-to-all-start = ((f32[4,512,128]{2,1,0:T(8,128)}), f32[4,512,128]{2,1,0:T(8,128)S(1)}, u32[]{:S(2)}, u32[]{:S(2)}) async-start(f32[4,512,128]{2,1,0:T(8,128)} %bitcast.3), calls=%async_computation | async-start | bytes 2097152 | tf_op jit(solution)/shard_map/all_to_all | solution.py:443
  18.6 5.0 %collective-permute-done.4.refs_10_.refs_11_ = f32[4,256,128]{2,1,0:T(8,128)} collective-permute-done((f32[4,256,128]{2,1,0:T(8,128)}, f32[4,256,128]{2,1,0:T(8,128)}, u32[]{:S(2)}, u32[]{:S(2)}) %collective-permute-start.4) | collective-permute-done | bytes 524320 | tf_op jit(solution)/shard_map/ppermute | solution.py:39
  25.6 3.3 %collective-permute-start.7 = (f32[2,256,128]{2,1,0:T(8,128)S(1)}, f32[2,256,128]{2,1,0:T(8,128)}, u32[]{:S(2)}, u32[]{:S(2)}) collective-permute-start(f32[2,256,128]{2,1,0:T(8,128)S(1)} %slice.56), channel_id=1, source_target_pairs={{0,12},{4,0},{8,4},{12,8},{1,13},{5,1},{9,5},{13,9},{2,14},{6,2},{... | collective-permute-start | bytes 786440 | tf_op jit(solution)/shard_map/ppermute | solution.py:39
  29.1 2.0 collective-permute-start.2
  32.3 6.7 %collective-permute-done.1 = f32[256,128]{1,0:T(8,128)S(1)} collective-permute-done((f32[256,128]{1,0:T(8,128)S(1)}, f32[256,128]{1,0:T(8,128)S(1)}, u32[]{:S(2)}, u32[]{:S(2)}) %collective-permute-start.1) | collective-permute-done | bytes 131104 | tf_op jit(solution)/shard_map/ppermute | solution.py:39
  44.5 3.3 %collective-permute-start.9 = (f32[4,512,128]{2,1,0:T(8,128)S(1)}, f32[4,512,128]{2,1,0:T(8,128)S(1)}, u32[]{:S(2)}, u32[]{:S(2)}) collective-permute-start(f32[4,512,128]{2,1,0:T(8,128)S(1)} %all-to-all-done.refs_4_.refs_5_), channel_id=1, source_target_pairs={{0,12},{4,0},{8,4},{12,8},{1,13},{5,1},{9,5},{13,9},{2,14},{6,2},{... | collective-permute-start | bytes 3145736 | tf_op jit(solution)/shard_map/ppermute | solution.py:39
  47.8 1.5 collective-permute-start.16
  52.8 3.1 %collective-permute-start.17 = (f32[2,256,128]{2,1,0:T(8,128)S(1)}, f32[2,256,128]{2,1,0:T(8,128)S(1)}, u32[]{:S(2)}, u32[]{:S(2)}) collective-permute-start(f32[2,256,128]{2,1,0:T(8,128)S(1)} %maximum_select_fusion.2), channel_id=1, source_target_pairs={{0,64},{64,0},{1,65},{65,1},{2,66},{66,2},{3,67},{67,3},{4,68},{68... | collective-permute-start | bytes 786440 | tf_op jit(solution)/shard_map/ppermute | solution.py:43
  56.6 10.9 %collective-permute-done.11 = f32[2,256,128]{2,1,0:T(8,128)S(1)} collective-permute-done((f32[2,256,128]{2,1,0:T(8,128)S(1)}, f32[2,256,128]{2,1,0:T(8,128)S(1)}, u32[]{:S(2)}, u32[]{:S(2)}) %collective-permute-start.11) | collective-permute-done | bytes 262176 | tf_op jit(solution)/shard_map/ppermute | solution.py:43
  68.8 3.4 %collective-permute-start.13 = (f32[256,128]{1,0:T(8,128)S(1)}, f32[256,128]{1,0:T(8,128)S(1)}, u32[]{:S(2)}, u32[]{:S(2)}) collective-permute-start(f32[256,128]{1,0:T(8,128)S(1)} %get-tuple-element.151), channel_id=1, source_target_pairs={{0,8},{4,12},{8,0},{12,4},{1,9},{5,13},{9,1},{13,5},{2,10},{6,14},... | collective-permute-start | bytes 393224 | tf_op jit(solution)/shard_map/ppermute | solution.py:39
  73.8 2.3 collective-permute-done.12
  76.2 2.4 collective-permute-done.13
  82.9 2.5 collective-permute-start.20
  85.6 1.6 collective-permute-start.21
  87.3 2.9 %collective-permute-start.22 = (f32[16,2048]{1,0:T(8,128)S(1)}, f32[16,2048]{1,0:T(8,128)S(1)}, u32[]{:S(2)}, u32[]{:S(2)}) collective-permute-start(f32[16,2048]{1,0:T(8,128)S(1)} %copy-done), channel_id=1, source_target_pairs={{0,2},{1,3},{2,0},{3,1},{4,6},{5,7},{6,4},{7,5},{8,10},{9,11},{10,... | collective-permute-start | bytes 393224 | tf_op jit(solution)/shard_map/ppermute | solution.py:39
  92.6 3.0 %collective-permute-done.22.refs_2_ = f32[16,2048]{1,0:T(8,128)S(1)} collective-permute-done((f32[16,2048]{1,0:T(8,128)S(1)}, f32[16,2048]{1,0:T(8,128)S(1)}, u32[]{:S(2)}, u32[]{:S(2)}) %collective-permute-start.22) | collective-permute-done | bytes 131104 | tf_op jit(solution)/shard_map/ppermute | solution.py:39
  96.5 6.0 %f0.1 = (f32[64,512]{1,0:T(8,128)S(1)}, f32[16,1024]{1,0:T(8,128)S(1)}, f32[16,1024]{1,0:T(8,128)S(1)}, f32[16,1024]{1,0:T(8,128)S(1)}, f32[16,1024]{1,0:T(8,128)S(1)}) custom-call(s32[128]{0:T(128)S(1)} %pad_add_fusion.meta, f32[16,2048]{1,0:T(8,128)S(1)} %copy-done, f32[16,2048]{1,0:T(8,128)S(1)} %collective-permute-done.21.refs_1_, ...), custom_call_target="tpu_custom_call" | custom-call | flops 2415919104 | bytes 6815744 | tf_op jit(solution)/shard_map/f0/pallas_call | solution.py:395
  102.5 3.1 %collective-permute-start.24 = (f32[16,1024]{1,0:T(8,128)S(1)}, f32[16,1024]{1,0:T(8,128)S(1)}, u32[]{:S(2)}, u32[]{:S(2)}) collective-permute-start(f32[16,1024]{1,0:T(8,128)S(1)} %get-tuple-element.94), channel_id=1, source_target_pairs={{0,3},{1,0},{2,1},{3,2},{4,7},{5,4},{6,5},{7,6},{8,11},{9,8},{10,9... | collective-permute-start | bytes 196616 | tf_op jit(solution)/shard_map/ppermute | solution.py:39
  107.2 2.0 collective-permute-done.24
  109.3 4.1 %collective-permute-done.25 = f32[16,1024]{1,0:T(8,128)S(1)} collective-permute-done((f32[16,1024]{1,0:T(8,128)S(1)}, f32[16,1024]{1,0:T(8,128)S(1)}, u32[]{:S(2)}, u32[]{:S(2)}) %collective-permute-start.25) | collective-permute-done | bytes 65568 | tf_op jit(solution)/shard_map/ppermute | solution.py:39
  114.7 4.7 %collective-permute-done.27.recv = f32[8,1024]{1,0:T(8,128)S(1)} collective-permute-done((f32[8,1024]{1,0:T(8,128)S(1)}, f32[8,1024]{1,0:T(8,128)S(1)}, u32[]{:S(2)}, u32[]{:S(2)}) %collective-permute-start.27) | collective-permute-done | bytes 32800 | tf_op jit(solution)/shard_map/ppermute | solution.py:43
  120.1 1.9 collective-permute-start.28
  122.0 3.1 %collective-permute-start.29 = (f32[8,2048]{1,0:T(8,128)S(1)}, f32[8,2048]{1,0:T(8,128)S(1)}, u32[]{:S(2)}, u32[]{:S(2)}) collective-permute-start(f32[8,2048]{1,0:T(8,128)S(1)} %get-tuple-element.99.refs_0_), channel_id=1, source_target_pairs={{0,8},{4,12},{8,0},{12,4},{1,9},{5,13},{9,1},{13,5},{2,10},{6,14},... | collective-permute-start | bytes 196616 | tf_op jit(solution)/shard_map/ppermute | solution.py:39
  129.9 1.4 collective-permute-start.33
  131.3 1.8 copy-done.1
  133.0 4.9 %f1.1 = (f32[32,512]{1,0:T(8,128)S(1)}, f32[16,1024]{1,0:T(8,128)S(1)}, f32[16,1024]{1,0:T(8,128)S(1)}) custom-call(s32[128]{0:T(128)S(1)} %pad_add_fusion.meta, f32[8,2048]{1,0:T(8,128)S(1)} %get-tuple-element.99.refs_0_, f32[8,2048]{1,0:T(8,128)S(1)} %collective-permute-done.28.refs_1_, f32[8,2048]{1,0:T(8,128)S(1)} %collective-permute-done.29.refs_2_, ...), custom_call_target="tpu_custom_call" | custom-call | flops 1207959552 | bytes 6553600 | tf_op jit(solution)/shard_map/f1/pallas_call | solution.py:395
  138.7 3.7 %collective-permute-done.32.recv = f32[16,1024]{1,0:T(8,128)S(1)} collective-permute-done((f32[16,1024]{1,0:T(8,128)S(1)}, f32[16,1024]{1,0:T(8,128)S(1)}, u32[]{:S(2)}, u32[]{:S(2)}) %collective-permute-start.32) | collective-permute-done | bytes 65568 | tf_op jit(solution)/shard_map/ppermute | solution.py:43
  144.1 1.7 collective-permute-start.34
  145.7 1.8 collective-permute-start.35
  147.6 1.9 collective-permute-start.36
  150.1 1.4 collective-permute-done.34.refs_1_
  151.4 2.8 %collective-permute-done.35.refs_2_ = f32[16,2048]{1,0:T(8,128)S(1)} collective-permute-done((f32[16,2048]{1,0:T(8,128)S(1)}, f32[16,2048]{1,0:T(8,128)S(1)}, u32[]{:S(2)}, u32[]{:S(2)}) %collective-permute-start.35) | collective-permute-done | bytes 131104 | tf_op jit(solution)/shard_map/ppermute | solution.py:39
  154.6 4.7 %f2.1 = (f32[16,512]{1,0:T(8,128)S(1)}, f32[8,1024]{1,0:T(8,128)S(1)}, f32[8,1024]{1,0:T(8,128)S(1)}) custom-call(s32[128]{0:T(128)S(1)} %pad_add_fusion.meta, f32[16,2048]{1,0:T(8,128)S(1)} %get-tuple-element.109.refs_0_, f32[16,2048]{1,0:T(8,128)S(1)} %collective-permute-done.34.refs_1_, f32[16,2048]{1,0:T(8,128)S(1)} %collective-permute-done.35.refs_2_, ...), custom_call_target="tpu_custom_call" | custom-call | flops 603979776 | bytes 6815744 | tf_op jit(solution)/shard_map/f2/pallas_call | solution.py:395
  160.3 4.5 %collective-permute-done.38.recv = f32[8,1024]{1,0:T(8,128)S(1)} collective-permute-done((f32[8,1024]{1,0:T(8,128)S(1)}, f32[8,1024]{1,0:T(8,128)S(1)}, u32[]{:S(2)}, u32[]{:S(2)}) %collective-permute-start.38) | collective-permute-done | bytes 32800 | tf_op jit(solution)/shard_map/ppermute | solution.py:43
  165.5 8.0 %all-gather.11.cloned.1.call-done = f32[16,256,128]{2,1,0:T(8,128)} async-done(((f32[4,256,128]{2,1,0:T(8,128)}), f32[16,256,128]{2,1,0:T(8,128)}) %all-gather.11.cloned.1.call-update) | async-done | bytes 2097168 | tf_op jit(solution)/shard_map/all_gather | solution.py:436
  173.5 1.6 collective-permute-start.40
  175.1 2.9 %collective-permute-start.41 = (f32[8,2048]{1,0:T(8,128)S(1)}, f32[8,2048]{1,0:T(8,128)S(1)}, u32[]{:S(2)}, u32[]{:S(2)}) collective-permute-start(f32[8,2048]{1,0:T(8,128)S(1)} %s23.1.c0), channel_id=1, source_target_pairs={{0,8},{4,12},{8,0},{12,4},{1,9},{5,13},{9,1},{13,5},{2,10},{6,14},... | collective-permute-start | bytes 196616 | tf_op jit(solution)/shard_map/ppermute | solution.py:39
  178.0 1.4 collective-permute-start.42
  179.3 2.5 collective-permute-done.41.c2
  183.6 4.6 %top.1.c0 = f32[8,2048]{1,0:T(8,128)S(1)} custom-call(s32[128]{0:T(128)S(1)} %pad_add_fusion.meta, f32[8,2048]{1,0:T(8,128)S(1)} %s23.1.c0, f32[8,2048]{1,0:T(8,128)S(1)} %collective-permute-done.40.c1, f32[8,2048]{1,0:T(8,128)S(1)} %collective-permute-done.41.c2, f32[8,2048]{1,0:T(8,128)S(1)} %collective-permute-done.42.c3, f32[4,4,256,128]{3,2,1,0:T(8,128)} %bitcast.91, ...), custom_call_target="tpu_custom_call" | custom-call | flops 301989888 | bytes 4456448 | tf_op jit(solution)/shard_map/top/pallas_call | solution.py:395
  189.1 3.2 %collective-permute-start.48 = (f32[8,2048]{1,0:T(8,128)S(1)}, f32[8,2048]{1,0:T(8,128)S(1)}, u32[]{:S(2)}, u32[]{:S(2)}) collective-permute-start(f32[8,2048]{1,0:T(8,128)S(1)} %top.1.c0), channel_id=1, source_target_pairs={{0,8},{4,12},{8,0},{12,4},{1,9},{5,13},{9,1},{13,5},{2,10},{6,14},... | collective-permute-start | bytes 196616 | tf_op jit(solution)/shard_map/ppermute | solution.py:39
  193.8 1.5 collective-permute-done.48.c2
  197.2 3.1 %collective-permute-start.50 = (f32[8,2048]{1,0:T(8,128)S(1)}, f32[8,2048]{1,0:T(8,128)S(1)}, u32[]{:S(2)}, u32[]{:S(2)}) collective-permute-start(f32[8,2048]{1,0:T(8,128)S(1)} %x3.1), channel_id=1, source_target_pairs={{0,64},{64,0},{1,65},{65,1},{2,66},{66,2},{3,67},{67,3},{4,68},{68... | collective-permute-start | bytes 196616 | tf_op jit(solution)/shard_map/ppermute | solution.py:43
  200.3 2.8 %collective-permute-done.50.x3r = f32[8,2048]{1,0:T(8,128)S(1)} collective-permute-done((f32[8,2048]{1,0:T(8,128)S(1)}, f32[8,2048]{1,0:T(8,128)S(1)}, u32[]{:S(2)}, u32[]{:S(2)}) %collective-permute-start.50) | collective-permute-done | bytes 65568 | tf_op jit(solution)/shard_map/ppermute | solution.py:43
  203.1 4.7 %b2.1.c0 = f32[16,2048]{1,0:T(8,128)S(1)} custom-call(s32[128]{0:T(128)S(1)} %pad_add_fusion.meta, f32[1,8,2048]{2,1,0:T(8,128)S(1)} %bitcast.82, f32[1,8,2048]{2,1,0:T(8,128)S(1)} %bitcast.83, f32[16,512]{1,0:T(8,128)S(1)} %get-tuple-element.127.refs_2_, f32[4,6,256,128]{3,2,1,0:T(8,128)} %bitcast.89, f32[4,6,256,128]{3,2,1,0:T(8,128)} %collective-permute-done.37.refs_5_.refs_4_), custom_call_target="tpu_custom_call" | custom-call | flops 603979776 | bytes 6455296 | tf_op jit(solution)/shard_map/b2/pallas_call | solution.py:395
  208.1 3.1 %collective-permute-start.52 = (f32[16,2048]{1,0:T(8,128)S(1)}, f32[16,2048]{1,0:T(8,128)S(1)}, u32[]{:S(2)}, u32[]{:S(2)}) collective-permute-start(f32[16,2048]{1,0:T(8,128)S(1)} %b2.1.c0), channel_id=1, source_target_pairs={{0,8},{4,12},{8,0},{12,4},{1,9},{5,13},{9,1},{13,5},{2,10},{6,14},... | collective-permute-start | bytes 393224 | tf_op jit(solution)/shard_map/ppermute | solution.py:39
  212.0 2.0 collective-permute-done.51.c1
  214.0 1.6 collective-permute-done.52.c2
  217.0 1.5 collective-permute-start.54
  219.2 2.1 collective-permute-done.54.refs_1_
  221.3 4.8 %b1.1 = (f32[8,2048]{1,0:T(8,128)S(1)}, f32[8,2048]{1,0:T(8,128)S(1)}, f32[8,2048]{1,0:T(8,128)S(1)}, f32[8,2048]{1,0:T(8,128)S(1)}) custom-call(s32[128]{0:T(128)S(1)} %pad_add_fusion.meta, f32[2,16,2048]{2,1,0:T(8,128)S(1)} %get-tuple-element.128.refs_0_, f32[16,1024]{1,0:T(8,128)S(1)} %collective-permute-done.54.refs_1_, ...), custom_call_target="tpu_custom_call" | custom-call | flops 1207959552 | bytes 6684672 | tf_op jit(solution)/shard_map/b1/pallas_call | solution.py:395
  226.1 2.7 %collective-permute-start.55 = (f32[8,2048]{1,0:T(8,128)S(1)}, f32[8,2048]{1,0:T(8,128)S(1)}, u32[]{:S(2)}, u32[]{:S(2)}) collective-permute-start(f32[8,2048]{1,0:T(8,128)S(1)} %get-tuple-element.132), channel_id=1, source_target_pairs={{0,12},{4,0},{8,4},{12,8},{1,13},{5,1},{9,5},{13,9},{2,14},{6,2},{... | collective-permute-start | bytes 196616 | tf_op jit(solution)/shard_map/ppermute | solution.py:39
  229.8 1.6 collective-permute-done.55.c1
  231.4 3.3 %collective-permute-done.56.c2 = f32[8,2048]{1,0:T(8,128)S(1)} collective-permute-done((f32[8,2048]{1,0:T(8,128)S(1)}, f32[8,2048]{1,0:T(8,128)S(1)}, u32[]{:S(2)}, u32[]{:S(2)}) %collective-permute-start.56) | collective-permute-done | bytes 65568 | tf_op jit(solution)/shard_map/ppermute | solution.py:39
  238.4 1.8 collective-permute-start.61
  240.2 2.1 collective-permute-start.62
  242.9 1.8 collective-permute-done.60.refs_1_
  245.2 4.9 %b0.1 = (f32[16,2048]{1,0:T(8,128)S(1)}, f32[16,2048]{1,0:T(8,128)S(1)}, f32[16,2048]{1,0:T(8,128)S(1)}, f32[16,2048]{1,0:T(8,128)S(1)}) custom-call(s32[128]{0:T(128)S(1)} %pad_add_fusion.meta, f32[16,1024]{1,0:T(8,128)S(1)} %maximum_select_fusion.3.refs_0_, f32[16,1024]{1,0:T(8,128)S(1)} %collective-permute-done.60.refs_1_, ...), custom_call_target="tpu_custom_call" | custom-call | flops 2415919104 | bytes 6684672 | tf_op jit(solution)/shard_map/b0/pallas_call | solution.py:395
  250.1 2.7 %collective-permute-start.63 = (f32[16,2048]{1,0:T(8,128)S(1)}, f32[16,2048]{1,0:T(8,128)S(1)}, u32[]{:S(2)}, u32[]{:S(2)}) collective-permute-start(f32[16,2048]{1,0:T(8,128)S(1)} %get-tuple-element.138), channel_id=1, source_target_pairs={{0,3},{1,0},{2,1},{3,2},{4,7},{5,4},{6,5},{7,6},{8,11},{9,8},{10,9... | collective-permute-start | bytes 393224 | tf_op jit(solution)/shard_map/ppermute | solution.py:39
  255.1 2.5 collective-permute-done.63
  257.6 2.4 collective-permute-done.64
  (177 shorter events, 56.2 us)
Async XLA Ops:
  7.2 16.4 %collective-permute-start.4 = (f32[4,256,128]{2,1,0:T(8,128)}, f32[4,256,128]{2,1,0:T(8,128)}, u32[]{:S(2)}, u32[]{:S(2)}) collective-permute-start(f32[4,256,128]{2,1,0:T(8,128)} %bitcast.104), channel_id=1, source_target_pairs={{0,4},{4,8},{8,12},{12,0},{1,5},{5,9},{9,13},{13,1},{2,6},{6,10},{... | collective-permute-start | bytes 1572872 | tf_op jit(solution)/shard_map/ppermute | solution.py:39
  9.2 15.4 %collective-permute-start.5 = (f32[4,256,128]{2,1,0:T(8,128)}, f32[4,256,128]{2,1,0:T(8,128)}, u32[]{:S(2)}, u32[]{:S(2)}) collective-permute-start(f32[4,256,128]{2,1,0:T(8,128)} %bitcast.105), channel_id=1, source_target_pairs={{0,12},{4,0},{8,4},{12,8},{1,13},{5,1},{9,5},{13,9},{2,14},{6,2},{... | collective-permute-start | bytes 1572872 | tf_op jit(solution)/shard_map/ppermute | solution.py:39
  13.8 25.5 %all-to-all-start = ((f32[4,512,128]{2,1,0:T(8,128)}), f32[4,512,128]{2,1,0:T(8,128)S(1)}, u32[]{:S(2)}, u32[]{:S(2)}) async-start(f32[4,512,128]{2,1,0:T(8,128)} %bitcast.3), calls=%async_computation | async-start | bytes 2097152 | tf_op jit(solution)/shard_map/all_to_all | solution.py:443
  18.4 95.5 %all-gather.7.cloned.1.call-start = ((), (), s32[]{:S(2)}) async-start(), calls=%async_computation.1 | async-start | bytes 3932160 | tf_op jit(solution)/shard_map/all_gather | solution.py:436
  18.5 10.5 %collective-permute-start = (f32[2,256,128]{2,1,0:T(8,128)S(1)}, f32[2,256,128]{2,1,0:T(8,128)S(1)}, u32[]{:S(2)}, u32[]{:S(2)}) collective-permute-start(f32[2,256,128]{2,1,0:T(8,128)S(1)} %dynamic-slice_bitcast_fusion), channel_id=1, source_target_pairs={{0,16},{16,0},{1,17},{17,1},{2,18},{18,2},{3,19},{19,3},{4,20},{20... | collective-permute-start | bytes 786440 | tf_op jit(solution)/shard_map/ppermute | solution.py:43
  24.6 14.7 %collective-permute-start.6 = (f32[2,256,128]{2,1,0:T(8,128)S(1)}, f32[2,256,128]{2,1,0:T(8,128)}, u32[]{:S(2)}, u32[]{:S(2)}) collective-permute-start(f32[2,256,128]{2,1,0:T(8,128)S(1)} %slice.55), channel_id=1, source_target_pairs={{0,4},{4,8},{8,12},{12,0},{1,5},{5,9},{9,13},{13,1},{2,6},{6,10},{... | collective-permute-start | bytes 786440 | tf_op jit(solution)/shard_map/ppermute | solution.py:39
  25.6 13.6 %collective-permute-start.7 = (f32[2,256,128]{2,1,0:T(8,128)S(1)}, f32[2,256,128]{2,1,0:T(8,128)}, u32[]{:S(2)}, u32[]{:S(2)}) collective-permute-start(f32[2,256,128]{2,1,0:T(8,128)S(1)} %slice.56), channel_id=1, source_target_pairs={{0,12},{4,0},{8,4},{12,8},{1,13},{5,1},{9,5},{13,9},{2,14},{6,2},{... | collective-permute-start | bytes 786440 | tf_op jit(solution)/shard_map/ppermute | solution.py:39
  29.0 10.0 %collective-permute-start.1 = (f32[256,128]{1,0:T(8,128)S(1)}, f32[256,128]{1,0:T(8,128)S(1)}, u32[]{:S(2)}, u32[]{:S(2)}) collective-permute-start(f32[256,128]{1,0:T(8,128)S(1)} %get-tuple-element.144), channel_id=1, source_target_pairs={{0,4},{4,8},{8,12},{12,0},{1,5},{5,9},{9,13},{13,1},{2,6},{6,10},{... | collective-permute-start | bytes 393224 | tf_op jit(solution)/shard_map/ppermute | solution.py:39
  29.1 9.9 %collective-permute-start.2 = (f32[256,128]{1,0:T(8,128)S(1)}, f32[256,128]{1,0:T(8,128)S(1)}, u32[]{:S(2)}, u32[]{:S(2)}) collective-permute-start(f32[256,128]{1,0:T(8,128)S(1)} %get-tuple-element.143), channel_id=1, source_target_pairs={{0,8},{4,12},{8,0},{12,4},{1,9},{5,13},{9,1},{13,5},{2,10},{6,14},... | collective-permute-start | bytes 393224 | tf_op jit(solution)/shard_map/ppermute | solution.py:39
  31.1 8.2 %collective-permute-start.3 = (f32[256,128]{1,0:T(8,128)S(1)}, f32[256,128]{1,0:T(8,128)S(1)}, u32[]{:S(2)}, u32[]{:S(2)}) collective-permute-start(f32[256,128]{1,0:T(8,128)S(1)} %get-tuple-element.142), channel_id=1, source_target_pairs={{0,12},{4,0},{8,4},{12,8},{1,13},{5,1},{9,5},{13,9},{2,14},{6,2},{... | collective-permute-start | bytes 393224 | tf_op jit(solution)/shard_map/ppermute | solution.py:39
  43.9 99.2 %all-gather.9.cloned.1.call-start = ((), (), s32[]{:S(2)}) async-start(), calls=%async_computation.2 | async-start | bytes 3932160 | tf_op jit(solution)/shard_map/all_gather | solution.py:436
  44.0 35.0 %collective-permute-start.8 = (f32[4,512,128]{2,1,0:T(8,128)S(1)}, f32[4,512,128]{2,1,0:T(8,128)S(1)}, u32[]{:S(2)}, u32[]{:S(2)}) collective-permute-start(f32[4,512,128]{2,1,0:T(8,128)S(1)} %all-to-all-done.refs_4_.refs_5_), channel_id=1, source_target_pairs={{0,4},{4,8},{8,12},{12,0},{1,5},{5,9},{9,13},{13,1},{2,6},{6,10},{... | collective-permute-start | bytes 3145736 | tf_op jit(solution)/shard_map/ppermute | solution.py:39
  44.5 34.5 %collective-permute-start.9 = (f32[4,512,128]{2,1,0:T(8,128)S(1)}, f32[4,512,128]{2,1,0:T(8,128)S(1)}, u32[]{:S(2)}, u32[]{:S(2)}) collective-permute-start(f32[4,512,128]{2,1,0:T(8,128)S(1)} %all-to-all-done.refs_4_.refs_5_), channel_id=1, source_target_pairs={{0,12},{4,0},{8,4},{12,8},{1,13},{5,1},{9,5},{13,9},{2,14},{6,2},{... | collective-permute-start | bytes 3145736 | tf_op jit(solution)/shard_map/ppermute | solution.py:39
  49.3 19.5 %collective-permute-start.15 = (f32[256,128]{1,0:T(8,128)}, f32[256,128]{1,0:T(8,128)S(1)}, u32[]{:S(2)}, u32[]{:S(2)}) collective-permute-start(f32[256,128]{1,0:T(8,128)} %param.25), channel_id=1, source_target_pairs={{0,32},{32,0},{1,33},{33,1},{2,34},{34,2},{3,35},{35,3},{4,36},{36... | collective-permute-start | bytes 393224 | tf_op jit(solution)/shard_map/ppermute | solution.py:43
  49.9 6.0 %collective-permute-start.10 = (f32[1,256,128]{2,1,0:T(8,128)S(1)}, f32[1,256,128]{2,1,0:T(8,128)S(1)}, u32[]{:S(2)}, u32[]{:S(2)}) collective-permute-start(f32[1,256,128]{2,1,0:T(8,128)S(1)} %get-tuple-element.155), channel_id=1, source_target_pairs={{0,16},{16,0},{1,17},{17,1},{2,18},{18,2},{3,19},{19,3},{4,20},{20... | collective-permute-start | bytes 393224 | tf_op jit(solution)/shard_map/ppermute | solution.py:43
  52.8 19.4 %collective-permute-start.17 = (f32[2,256,128]{2,1,0:T(8,128)S(1)}, f32[2,256,128]{2,1,0:T(8,128)S(1)}, u32[]{:S(2)}, u32[]{:S(2)}) collective-permute-start(f32[2,256,128]{2,1,0:T(8,128)S(1)} %maximum_select_fusion.2), channel_id=1, source_target_pairs={{0,64},{64,0},{1,65},{65,1},{2,66},{66,2},{3,67},{67,3},{4,68},{68... | collective-permute-start | bytes 786440 | tf_op jit(solution)/shard_map/ppermute | solution.py:43
  55.9 11.6 %collective-permute-start.11 = (f32[2,256,128]{2,1,0:T(8,128)S(1)}, f32[2,256,128]{2,1,0:T(8,128)S(1)}, u32[]{:S(2)}, u32[]{:S(2)}) collective-permute-start(f32[2,256,128]{2,1,0:T(8,128)S(1)} %maximum_select_fusion), channel_id=1, source_target_pairs={{0,32},{32,0},{1,33},{33,1},{2,34},{34,2},{3,35},{35,3},{4,36},{36... | collective-permute-start | bytes 786440 | tf_op jit(solution)/shard_map/ppermute | solution.py:43
  68.8 7.4 %collective-permute-start.12 = (f32[256,128]{1,0:T(8,128)S(1)}, f32[256,128]{1,0:T(8,128)S(1)}, u32[]{:S(2)}, u32[]{:S(2)}) collective-permute-start(f32[256,128]{1,0:T(8,128)S(1)} %get-tuple-element.152), channel_id=1, source_target_pairs={{0,4},{4,8},{8,12},{12,0},{1,5},{5,9},{9,13},{13,1},{2,6},{6,10},{... | collective-permute-start | bytes 393224 | tf_op jit(solution)/shard_map/ppermute | solution.py:39
  68.8 9.7 %collective-permute-start.13 = (f32[256,128]{1,0:T(8,128)S(1)}, f32[256,128]{1,0:T(8,128)S(1)}, u32[]{:S(2)}, u32[]{:S(2)}) collective-permute-start(f32[256,128]{1,0:T(8,128)S(1)} %get-tuple-element.151), channel_id=1, source_target_pairs={{0,8},{4,12},{8,0},{12,4},{1,9},{5,13},{9,1},{13,5},{2,10},{6,14},... | collective-permute-start | bytes 393224 | tf_op jit(solution)/shard_map/ppermute | solution.py:39
  72.2 6.7 %collective-permute-start.14 = (f32[256,128]{1,0:T(8,128)S(1)}, f32[256,128]{1,0:T(8,128)S(1)}, u32[]{:S(2)}, u32[]{:S(2)}) collective-permute-start(f32[256,128]{1,0:T(8,128)S(1)} %get-tuple-element.150), channel_id=1, source_target_pairs={{0,12},{4,0},{8,4},{12,8},{1,13},{5,1},{9,5},{13,9},{2,14},{6,2},{... | collective-permute-start | bytes 393224 | tf_op jit(solution)/shard_map/ppermute | solution.py:39
  80.9 92.7 %all-gather.11.cloned.1.call-start = ((), (), s32[]{:S(2)}) async-start(), calls=%async_computation.3 | async-start | bytes 2621440 | tf_op jit(solution)/shard_map/all_gather | solution.py:436
  81.0 15.1 %collective-permute-start.19 = (f32[2,512,128]{2,1,0:T(8,128)S(1)}, f32[2,512,128]{2,1,0:T(8,128)}, u32[]{:S(2)}, u32[]{:S(2)}) collective-permute-start(f32[2,512,128]{2,1,0:T(8,128)S(1)} %slice.47), channel_id=1, source_target_pairs={{0,4},{4,8},{8,12},{12,0},{1,5},{5,9},{9,13},{13,1},{2,6},{6,10},{... | collective-permute-start | bytes 1572872 | tf_op jit(solution)/shard_map/ppermute | solution.py:39
  82.9 13.6 %collective-permute-start.20 = (f32[2,512,128]{2,1,0:T(8,128)S(1)}, f32[2,512,128]{2,1,0:T(8,128)}, u32[]{:S(2)}, u32[]{:S(2)}) collective-permute-start(f32[2,512,128]{2,1,0:T(8,128)S(1)} %slice.48), channel_id=1, source_target_pairs={{0,12},{4,0},{8,4},{12,8},{1,13},{5,1},{9,5},{13,9},{2,14},{6,2},{... | collective-permute-start | bytes 1572872 | tf_op jit(solution)/shard_map/ppermute | solution.py:39
  85.6 7.0 %collective-permute-start.21 = (f32[16,2048]{1,0:T(8,128)S(1)}, f32[16,2048]{1,0:T(8,128)S(1)}, u32[]{:S(2)}, u32[]{:S(2)}) collective-permute-start(f32[16,2048]{1,0:T(8,128)S(1)} %copy-done), channel_id=1, source_target_pairs={{0,1},{1,2},{2,3},{3,0},{4,5},{5,6},{6,7},{7,4},{8,9},{9,10},{10,1... | collective-permute-start | bytes 393224 | tf_op jit(solution)/shard_map/ppermute | solution.py:39
  87.3 8.4 %collective-permute-start.22 = (f32[16,2048]{1,0:T(8,128)S(1)}, f32[16,2048]{1,0:T(8,128)S(1)}, u32[]{:S(2)}, u32[]{:S(2)}) collective-permute-start(f32[16,2048]{1,0:T(8,128)S(1)} %copy-done), channel_id=1, source_target_pairs={{0,2},{1,3},{2,0},{3,1},{4,6},{5,7},{6,4},{7,5},{8,10},{9,11},{10,... | collective-permute-start | bytes 393224 | tf_op jit(solution)/shard_map/ppermute | solution.py:39
  90.2 5.5 %collective-permute-start.23 = (f32[16,2048]{1,0:T(8,128)S(1)}, f32[16,2048]{1,0:T(8,128)S(1)}, u32[]{:S(2)}, u32[]{:S(2)}) collective-permute-start(f32[16,2048]{1,0:T(8,128)S(1)} %copy-done), channel_id=1, source_target_pairs={{0,3},{1,0},{2,1},{3,2},{4,7},{5,4},{6,5},{7,6},{8,11},{9,8},{10,9... | collective-permute-start | bytes 393224 | tf_op jit(solution)/shard_map/ppermute | solution.py:39
  102.5 6.7 %collective-permute-start.24 = (f32[16,1024]{1,0:T(8,128)S(1)}, f32[16,1024]{1,0:T(8,128)S(1)}, u32[]{:S(2)}, u32[]{:S(2)}) collective-permute-start(f32[16,1024]{1,0:T(8,128)S(1)} %get-tuple-element.94), channel_id=1, source_target_pairs={{0,3},{1,0},{2,1},{3,2},{4,7},{5,4},{6,5},{7,6},{8,11},{9,8},{10,9... | collective-permute-start | bytes 196616 | tf_op jit(solution)/shard_map/ppermute | solution.py:39
  105.6 7.7 %collective-permute-start.25 = (f32[16,1024]{1,0:T(8,128)S(1)}, f32[16,1024]{1,0:T(8,128)S(1)}, u32[]{:S(2)}, u32[]{:S(2)}) collective-permute-start(f32[16,1024]{1,0:T(8,128)S(1)} %get-tuple-element.95), channel_id=1, source_target_pairs={{0,2},{1,3},{2,0},{3,1},{4,6},{5,7},{6,4},{7,5},{8,10},{9,11},{10,... | collective-permute-start | bytes 196616 | tf_op jit(solution)/shard_map/ppermute | solution.py:39
  106.3 7.5 %collective-permute-start.26 = (f32[16,1024]{1,0:T(8,128)S(1)}, f32[16,1024]{1,0:T(8,128)S(1)}, u32[]{:S(2)}, u32[]{:S(2)}) collective-permute-start(f32[16,1024]{1,0:T(8,128)S(1)} %get-tuple-element.96), channel_id=1, source_target_pairs={{0,1},{1,2},{2,3},{3,0},{4,5},{5,6},{6,7},{7,4},{8,9},{9,10},{10,1... | collective-permute-start | bytes 196616 | tf_op jit(solution)/shard_map/ppermute | solution.py:39
  113.8 17.5 %collective-permute-start.31 = (f32[4,6,256,128]{3,2,1,0:T(8,128)}, f32[4,6,256,128]{3,2,1,0:T(8,128)S(1)}, u32[]{:S(2)}, u32[]{:S(2)}) collective-permute-start(f32[4,6,256,128]{3,2,1,0:T(8,128)} %bitcast.84), channel_id=1, source_target_pairs={{0,16},{16,0},{1,17},{17,1},{2,18},{18,2},{3,19},{19,3},{4,20},{20... | collective-permute-start | bytes 9437192 | tf_op jit(solution)/shard_map/ppermute | solution.py:43
  114.1 5.3 %collective-permute-start.27 = (f32[8,1024]{1,0:T(8,128)S(1)}, f32[8,1024]{1,0:T(8,128)S(1)}, u32[]{:S(2)}, u32[]{:S(2)}) collective-permute-start(f32[8,1024]{1,0:T(8,128)S(1)} %get-tuple-element.167), channel_id=1, source_target_pairs={{0,16},{16,0},{1,17},{17,1},{2,18},{18,2},{3,19},{19,3},{4,20},{20... | collective-permute-start | bytes 98312 | tf_op jit(solution)/shard_map/ppermute | solution.py:43
  120.1 7.1 %collective-permute-start.28 = (f32[8,2048]{1,0:T(8,128)S(1)}, f32[8,2048]{1,0:T(8,128)S(1)}, u32[]{:S(2)}, u32[]{:S(2)}) collective-permute-start(f32[8,2048]{1,0:T(8,128)S(1)} %get-tuple-element.99.refs_0_), channel_id=1, source_target_pairs={{0,4},{4,8},{8,12},{12,0},{1,5},{5,9},{9,13},{13,1},{2,6},{6,10},{... | collective-permute-start | bytes 196616 | tf_op jit(solution)/shard_map/ppermute | solution.py:39
  122.0 7.4 %collective-permute-start.29 = (f32[8,2048]{1,0:T(8,128)S(1)}, f32[8,2048]{1,0:T(8,128)S(1)}, u32[]{:S(2)}, u32[]{:S(2)}) collective-permute-start(f32[8,2048]{1,0:T(8,128)S(1)} %get-tuple-element.99.refs_0_), channel_id=1, source_target_pairs={{0,8},{4,12},{8,0},{12,4},{1,9},{5,13},{9,1},{13,5},{2,10},{6,14},... | collective-permute-start | bytes 196616 | tf_op jit(solution)/shard_map/ppermute | solution.py:39
  126.4 12.3 %collective-permute-start.43 = (f32[256,128]{1,0:T(8,128)S(1)}, f32[256,128]{1,0:T(8,128)S(1)}, u32[]{:S(2)}, u32[]{:S(2)}) collective-permute-start(f32[256,128]{1,0:T(8,128)S(1)} %get-tuple-element.148), channel_id=1, source_target_pairs={{0,4},{4,8},{8,12},{12,0},{1,5},{5,9},{9,13},{13,1},{2,6},{6,10},{... | collective-permute-start | bytes 393224 | tf_op jit(solution)/shard_map/ppermute | solution.py:39
  127.2 11.5 %collective-permute-start.44 = (f32[256,128]{1,0:T(8,128)S(1)}, f32[256,128]{1,0:T(8,128)S(1)}, u32[]{:S(2)}, u32[]{:S(2)}) collective-permute-start(f32[256,128]{1,0:T(8,128)S(1)} %get-tuple-element.147), channel_id=1, source_target_pairs={{0,8},{4,12},{8,0},{12,4},{1,9},{5,13},{9,1},{13,5},{2,10},{6,14},... | collective-permute-start | bytes 393224 | tf_op jit(solution)/shard_map/ppermute | solution.py:39
  129.4 9.2 %collective-permute-start.45 = (f32[256,128]{1,0:T(8,128)S(1)}, f32[256,128]{1,0:T(8,128)S(1)}, u32[]{:S(2)}, u32[]{:S(2)}) collective-permute-start(f32[256,128]{1,0:T(8,128)S(1)} %get-tuple-element.146), channel_id=1, source_target_pairs={{0,12},{4,0},{8,4},{12,8},{1,13},{5,1},{9,5},{13,9},{2,14},{6,2},{... | collective-permute-start | bytes 393224 | tf_op jit(solution)/shard_map/ppermute | solution.py:39
  129.9 8.8 %collective-permute-start.33 = (f32[2,4,2048]{2,1,0:T(4,128)S(1)}, f32[2,4,2048]{2,1,0:T(4,128)S(1)}, u32[]{:S(2)}, u32[]{:S(2)}) collective-permute-start(f32[2,4,2048]{2,1,0:T(4,128)S(1)} %get-tuple-element.108), channel_id=1, source_target_pairs={{0,32},{32,0},{1,33},{33,1},{2,34},{34,2},{3,35},{35,3},{4,36},{36... | collective-permute-start | bytes 196616 | tf_op jit(solution)/shard_map/ppermute | solution.py:43
  143.1 11.5 %collective-permute-start.37 = (f32[4,6,256,128]{3,2,1,0:T(8,128)}, f32[4,6,256,128]{3,2,1,0:T(8,128)}, u32[]{:S(2)}, u32[]{:S(2)}) collective-permute-start(f32[4,6,256,128]{3,2,1,0:T(8,128)} %bitcast.87), channel_id=1, source_target_pairs={{0,16},{16,0},{1,17},{17,1},{2,18},{18,2},{3,19},{19,3},{4,20},{20... | collective-permute-start | bytes 9437192 | tf_op jit(solution)/shard_map/ppermute | solution.py:43
  144.1 7.4 %collective-permute-start.34 = (f32[16,2048]{1,0:T(8,128)S(1)}, f32[16,2048]{1,0:T(8,128)S(1)}, u32[]{:S(2)}, u32[]{:S(2)}) collective-permute-start(f32[16,2048]{1,0:T(8,128)S(1)} %get-tuple-element.109.refs_0_), channel_id=1, source_target_pairs={{0,4},{4,8},{8,12},{12,0},{1,5},{5,9},{9,13},{13,1},{2,6},{6,10},{... | collective-permute-start | bytes 393224 | tf_op jit(solution)/shard_map/ppermute | solution.py:39
  145.7 8.5 %collective-permute-start.35 = (f32[16,2048]{1,0:T(8,128)S(1)}, f32[16,2048]{1,0:T(8,128)S(1)}, u32[]{:S(2)}, u32[]{:S(2)}) collective-permute-start(f32[16,2048]{1,0:T(8,128)S(1)} %get-tuple-element.109.refs_0_), channel_id=1, source_target_pairs={{0,8},{4,12},{8,0},{12,4},{1,9},{5,13},{9,1},{13,5},{2,10},{6,14},... | collective-permute-start | bytes 393224 | tf_op jit(solution)/shard_map/ppermute | solution.py:39
  147.6 7.1 %collective-permute-start.36 = (f32[16,2048]{1,0:T(8,128)S(1)}, f32[16,2048]{1,0:T(8,128)S(1)}, u32[]{:S(2)}, u32[]{:S(2)}) collective-permute-start(f32[16,2048]{1,0:T(8,128)S(1)} %get-tuple-element.109.refs_0_), channel_id=1, source_target_pairs={{0,12},{4,0},{8,4},{12,8},{1,13},{5,1},{9,5},{13,9},{2,14},{6,2},{... | collective-permute-start | bytes 393224 | tf_op jit(solution)/shard_map/ppermute | solution.py:39
  149.4 10.9 %collective-permute-start.39 = (f32[8,2048]{1,0:T(8,128)S(1)}, f32[8,2048]{1,0:T(8,128)S(1)}, u32[]{:S(2)}, u32[]{:S(2)}) collective-permute-start(f32[8,2048]{1,0:T(8,128)S(1)} %get-tuple-element.119), channel_id=1, source_target_pairs={{0,64},{64,0},{1,65},{65,1},{2,66},{66,2},{3,67},{67,3},{4,68},{68... | collective-permute-start | bytes 196616 | tf_op jit(solution)/shard_map/ppermute | solution.py:43
  159.4 5.5 %collective-permute-start.38 = (f32[8,1024]{1,0:T(8,128)S(1)}, f32[8,1024]{1,0:T(8,128)S(1)}, u32[]{:S(2)}, u32[]{:S(2)}) collective-permute-start(f32[8,1024]{1,0:T(8,128)S(1)} %get-tuple-element.117), channel_id=1, source_target_pairs={{0,64},{64,0},{1,65},{65,1},{2,66},{66,2},{3,67},{67,3},{4,68},{68... | collective-permute-start | bytes 98312 | tf_op jit(solution)/shard_map/ppermute | solution.py:43
  173.5 8.7 %collective-permute-start.46 = (f32[4,4,256,128]{3,2,1,0:T(8,128)}, f32[4,4,256,128]{3,2,1,0:T(8,128)S(1)}, u32[]{:S(2)}, u32[]{:S(2)}) collective-permute-start(f32[4,4,256,128]{3,2,1,0:T(8,128)} %bitcast.90), channel_id=1, source_target_pairs={{0,16},{16,0},{1,17},{17,1},{2,18},{18,2},{3,19},{19,3},{4,20},{20... | collective-permute-start | bytes 6291464 | tf_op jit(solution)/shard_map/ppermute | solution.py:43
  173.5 5.8 %collective-permute-start.40 = (f32[8,2048]{1,0:T(8,128)S(1)}, f32[8,2048]{1,0:T(8,128)S(1)}, u32[]{:S(2)}, u32[]{:S(2)}) collective-permute-start(f32[8,2048]{1,0:T(8,128)S(1)} %s23.1.c0), channel_id=1, source_target_pairs={{0,4},{4,8},{8,12},{12,0},{1,5},{5,9},{9,13},{13,1},{2,6},{6,10},{... | collective-permute-start | bytes 196616 | tf_op jit(solution)/shard_map/ppermute | solution.py:39
  175.1 6.7 %collective-permute-start.41 = (f32[8,2048]{1,0:T(8,128)S(1)}, f32[8,2048]{1,0:T(8,128)S(1)}, u32[]{:S(2)}, u32[]{:S(2)}) collective-permute-start(f32[8,2048]{1,0:T(8,128)S(1)} %s23.1.c0), channel_id=1, source_target_pairs={{0,8},{4,12},{8,0},{12,4},{1,9},{5,13},{9,1},{13,5},{2,10},{6,14},... | collective-permute-start | bytes 196616 | tf_op jit(solution)/shard_map/ppermute | solution.py:39
  188.2 5.6 %collective-permute-start.47 = (f32[8,2048]{1,0:T(8,128)S(1)}, f32[8,2048]{1,0:T(8,128)S(1)}, u32[]{:S(2)}, u32[]{:S(2)}) collective-permute-start(f32[8,2048]{1,0:T(8,128)S(1)} %top.1.c0), channel_id=1, source_target_pairs={{0,4},{4,8},{8,12},{12,0},{1,5},{5,9},{9,13},{13,1},{2,6},{6,10},{... | collective-permute-start | bytes 196616 | tf_op jit(solution)/shard_map/ppermute | solution.py:39
  189.1 6.1 %collective-permute-start.48 = (f32[8,2048]{1,0:T(8,128)S(1)}, f32[8,2048]{1,0:T(8,128)S(1)}, u32[]{:S(2)}, u32[]{:S(2)}) collective-permute-start(f32[8,2048]{1,0:T(8,128)S(1)} %top.1.c0), channel_id=1, source_target_pairs={{0,8},{4,12},{8,0},{12,4},{1,9},{5,13},{9,1},{13,5},{2,10},{6,14},... | collective-permute-start | bytes 196616 | tf_op jit(solution)/shard_map/ppermute | solution.py:39
  197.2 5.8 %collective-permute-start.50 = (f32[8,2048]{1,0:T(8,128)S(1)}, f32[8,2048]{1,0:T(8,128)S(1)}, u32[]{:S(2)}, u32[]{:S(2)}) collective-permute-start(f32[8,2048]{1,0:T(8,128)S(1)} %x3.1), channel_id=1, source_target_pairs={{0,64},{64,0},{1,65},{65,1},{2,66},{66,2},{3,67},{67,3},{4,68},{68... | collective-permute-start | bytes 196616 | tf_op jit(solution)/shard_map/ppermute | solution.py:43
  207.8 6.2 %collective-permute-start.51 = (f32[16,2048]{1,0:T(8,128)S(1)}, f32[16,2048]{1,0:T(8,128)S(1)}, u32[]{:S(2)}, u32[]{:S(2)}) collective-permute-start(f32[16,2048]{1,0:T(8,128)S(1)} %b2.1.c0), channel_id=1, source_target_pairs={{0,4},{4,8},{8,12},{12,0},{1,5},{5,9},{9,13},{13,1},{2,6},{6,10},{... | collective-permute-start | bytes 393224 | tf_op jit(solution)/shard_map/ppermute | solution.py:39
  208.1 7.5 %collective-permute-start.52 = (f32[16,2048]{1,0:T(8,128)S(1)}, f32[16,2048]{1,0:T(8,128)S(1)}, u32[]{:S(2)}, u32[]{:S(2)}) collective-permute-start(f32[16,2048]{1,0:T(8,128)S(1)} %b2.1.c0), channel_id=1, source_target_pairs={{0,8},{4,12},{8,0},{12,4},{1,9},{5,13},{9,1},{13,5},{2,10},{6,14},... | collective-permute-start | bytes 393224 | tf_op jit(solution)/shard_map/ppermute | solution.py:39
  211.3 5.0 %collective-permute-start.53 = (f32[16,2048]{1,0:T(8,128)S(1)}, f32[16,2048]{1,0:T(8,128)S(1)}, u32[]{:S(2)}, u32[]{:S(2)}) collective-permute-start(f32[16,2048]{1,0:T(8,128)S(1)} %b2.1.c0), channel_id=1, source_target_pairs={{0,12},{4,0},{8,4},{12,8},{1,13},{5,1},{9,5},{13,9},{2,14},{6,2},{... | collective-permute-start | bytes 393224 | tf_op jit(solution)/shard_map/ppermute | solution.py:39
  218.5 11.3 %collective-permute-start.58 = (f32[2,4,2048]{2,1,0:T(4,128)S(1)}, f32[2,4,2048]{2,1,0:T(4,128)S(1)}, u32[]{:S(2)}, u32[]{:S(2)}) collective-permute-start(f32[2,4,2048]{2,1,0:T(4,128)S(1)} %slice.51.a_mine), channel_id=1, source_target_pairs={{0,32},{32,0},{1,33},{33,1},{2,34},{34,2},{3,35},{35,3},{4,36},{36... | collective-permute-start | bytes 196616 | tf_op jit(solution)/shard_map/ppermute | solution.py:43
  226.1 5.3 %collective-permute-start.55 = (f32[8,2048]{1,0:T(8,128)S(1)}, f32[8,2048]{1,0:T(8,128)S(1)}, u32[]{:S(2)}, u32[]{:S(2)}) collective-permute-start(f32[8,2048]{1,0:T(8,128)S(1)} %get-tuple-element.132), channel_id=1, source_target_pairs={{0,12},{4,0},{8,4},{12,8},{1,13},{5,1},{9,5},{13,9},{2,14},{6,2},{... | collective-permute-start | bytes 196616 | tf_op jit(solution)/shard_map/ppermute | solution.py:39
  228.9 5.8 %collective-permute-start.56 = (f32[8,2048]{1,0:T(8,128)S(1)}, f32[8,2048]{1,0:T(8,128)S(1)}, u32[]{:S(2)}, u32[]{:S(2)}) collective-permute-start(f32[8,2048]{1,0:T(8,128)S(1)} %get-tuple-element.133), channel_id=1, source_target_pairs={{0,8},{4,12},{8,0},{12,4},{1,9},{5,13},{9,1},{13,5},{2,10},{6,14},... | collective-permute-start | bytes 196616 | tf_op jit(solution)/shard_map/ppermute | solution.py:39
  229.2 6.2 %collective-permute-start.57 = (f32[8,2048]{1,0:T(8,128)S(1)}, f32[8,2048]{1,0:T(8,128)S(1)}, u32[]{:S(2)}, u32[]{:S(2)}) collective-permute-start(f32[8,2048]{1,0:T(8,128)S(1)} %get-tuple-element.134), channel_id=1, source_target_pairs={{0,4},{4,8},{8,12},{12,0},{1,5},{5,9},{9,13},{13,1},{2,6},{6,10},{... | collective-permute-start | bytes 196616 | tf_op jit(solution)/shard_map/ppermute | solution.py:39
  236.1 17.7 %collective-permute-start.67 = (f32[8,512]{1,0:T(8,128)S(1)}, f32[8,512]{1,0:T(8,128)S(1)}, u32[]{:S(2)}, u32[]{:S(2)}) collective-permute-start(f32[8,512]{1,0:T(8,128)S(1)} %get-tuple-element.164), channel_id=1, source_target_pairs={{0,16},{16,0},{1,17},{17,1},{2,18},{18,2},{3,19},{19,3},{4,20},{20... | collective-permute-start | bytes 49160 | tf_op jit(solution)/shard_map/ppermute | solution.py:43
  236.7 17.7 %collective-permute-start.66 = (f32[8,1024]{1,0:T(8,128)S(1)}, f32[8,1024]{1,0:T(8,128)S(1)}, u32[]{:S(2)}, u32[]{:S(2)}) collective-permute-start(f32[8,1024]{1,0:T(8,128)S(1)} %get-tuple-element.166), channel_id=1, source_target_pairs={{0,16},{16,0},{1,17},{17,1},{2,18},{18,2},{3,19},{19,3},{4,20},{20... | collective-permute-start | bytes 98312 | tf_op jit(solution)/shard_map/ppermute | solution.py:43
  237.8 6.8 %collective-permute-start.60 = (f32[16,1024]{1,0:T(8,128)S(1)}, f32[16,1024]{1,0:T(8,128)S(1)}, u32[]{:S(2)}, u32[]{:S(2)}) collective-permute-start(f32[16,1024]{1,0:T(8,128)S(1)} %maximum_select_fusion.3.refs_0_), channel_id=1, source_target_pairs={{0,1},{1,2},{2,3},{3,0},{4,5},{5,6},{6,7},{7,4},{8,9},{9,10},{10,1... | collective-permute-start | bytes 196616 | tf_op jit(solution)/shard_map/ppermute | solution.py:39
  238.4 6.2 %collective-permute-start.61 = (f32[16,1024]{1,0:T(8,128)S(1)}, f32[16,1024]{1,0:T(8,128)S(1)}, u32[]{:S(2)}, u32[]{:S(2)}) collective-permute-start(f32[16,1024]{1,0:T(8,128)S(1)} %maximum_select_fusion.3.refs_0_), channel_id=1, source_target_pairs={{0,2},{1,3},{2,0},{3,1},{4,6},{5,7},{6,4},{7,5},{8,10},{9,11},{10,... | collective-permute-start | bytes 196616 | tf_op jit(solution)/shard_map/ppermute | solution.py:39
  240.2 5.0 %collective-permute-start.62 = (f32[16,1024]{1,0:T(8,128)S(1)}, f32[16,1024]{1,0:T(8,128)S(1)}, u32[]{:S(2)}, u32[]{:S(2)}) collective-permute-start(f32[16,1024]{1,0:T(8,128)S(1)} %maximum_select_fusion.3.refs_0_), channel_id=1, source_target_pairs={{0,3},{1,0},{2,1},{3,2},{4,7},{5,4},{6,5},{7,6},{8,11},{9,8},{10,9... | collective-permute-start | bytes 196616 | tf_op jit(solution)/shard_map/ppermute | solution.py:39
  250.1 7.5 %collective-permute-start.63 = (f32[16,2048]{1,0:T(8,128)S(1)}, f32[16,2048]{1,0:T(8,128)S(1)}, u32[]{:S(2)}, u32[]{:S(2)}) collective-permute-start(f32[16,2048]{1,0:T(8,128)S(1)} %get-tuple-element.138), channel_id=1, source_target_pairs={{0,3},{1,0},{2,1},{3,2},{4,7},{5,4},{6,5},{7,6},{8,11},{9,8},{10,9... | collective-permute-start | bytes 393224 | tf_op jit(solution)/shard_map/ppermute | solution.py:39
  252.9 7.1 %collective-permute-start.64 = (f32[16,2048]{1,0:T(8,128)S(1)}, f32[16,2048]{1,0:T(8,128)S(1)}, u32[]{:S(2)}, u32[]{:S(2)}) collective-permute-start(f32[16,2048]{1,0:T(8,128)S(1)} %get-tuple-element.139), channel_id=1, source_target_pairs={{0,2},{1,3},{2,0},{3,1},{4,6},{5,7},{6,4},{7,5},{8,10},{9,11},{10,... | collective-permute-start | bytes 393224 | tf_op jit(solution)/shard_map/ppermute | solution.py:39
  253.4 7.9 %collective-permute-start.65 = (f32[16,2048]{1,0:T(8,128)S(1)}, f32[16,2048]{1,0:T(8,128)S(1)}, u32[]{:S(2)}, u32[]{:S(2)}) collective-permute-start(f32[16,2048]{1,0:T(8,128)S(1)} %get-tuple-element.140), channel_id=1, source_target_pairs={{0,1},{1,2},{2,3},{3,0},{4,5},{5,6},{6,7},{7,4},{8,9},{9,10},{10,1... | collective-permute-start | bytes 393224 | tf_op jit(solution)/shard_map/ppermute | solution.py:39
  (27 other events, 270.9 us)
Sparse Core Ops, SparseCore 0:
  44.0 41.5 all-gather.6
  87.3 42.5 all-gather.8
  144.2 29.3 all-gather.10

commit v10 on v9

--- a/solution.py
+++ b/solution.py
@@ -443,30 +443,28 @@
     e0 = lax.all_to_all(e0, "y", 0, 0, tiled=True)
     e1 = dinv1.reshape(2, 2, 256, B)
     e1 = over_z(for_z(pick(e1, ci, 1), flip(pick(e1, 1 - ci, 1), "core"), ci))
-    e0, e1, fa, fb, fc, fd, dinv2, off2, dinv3, rhs0, rhs1 = gate(
-        (e0, e1, fa, fb, fc, fd, dinv2, off2, dinv3, rhs0, rhs1)
-    )
-    m1 = gathered(e1, off1)
-
-    ea, eb = shift(e0, "z", 1), shift(e0, "z", -1)
     e2 = dinv2.reshape(2, 256, B)
     e2 = ordered(pick(e2, ci)[None], flip(pick(e2, 1 - ci)[None], "core"), ci, 0)
     e2_other = flip(e2, "x0")
-    f2 = joined(off2, 1)
     e3 = joined(dinv3[None], 1)
     e3_other = flip(e3, "x1")
-    e2 = over_z(for_z(e2, e2_other, x0))
+    e0, e1, e2, e2_other, e3, e3_other, fa, fb, fc, fd, off2, rhs0, rhs1 = gate(
+        (e0, e1, e2, e2_other, e3, e3_other, fa, fb, fc, fd, off2, rhs0, rhs1)
+    )
+    m1 = gathered(e1, off1)
+
+    ea, eb = shift(e0, "z", 1), shift(e0, "z", -1)
+    f2 = joined(off2, 1)
+    e23 = zip(for_z(e2, e2_other, x0), for_z(e3, e3_other, x1))
+    e23 = over_z([jnp.stack(pair) for pair in e23])
     b_mine, b_other = halves(jnp.concatenate([rhs1, rhs2, rhs3], 1), ci)
     b_other = flip(b_other, "core")
-    ea, eb, e2, f2, e3, e3_other, b_mine, b_other = gate(
-        (ea, eb, e2, f2, e3, e3_other, b_mine, b_other)
-    )
+    ea, eb, e23, f2, b_mine, b_other = gate((ea, eb, e23, f2, b_mine, b_other))
 
     ec, ed = shift(ea[:2], "z", 1), shift(eb[2:], "z", -1)
-    m2 = gathered(e2, f2)
-    e3 = over_z(for_z(e3, e3_other, x1))
+    m2 = gathered([v[0] for v in e23], f2)
     c0 = gather4(rhs0, "y")
-    e3[0], ec, ed, c0 = gate((e3[0], ec, ed, c0))
+    ec, ed, c0 = gate((ec, ed, c0))
     w0 = [e0, ea, eb, ec, ed, off0, fa, fb, fc, fd]
 
     dma = pltpu.SemaphoreType.DMA
@@ -483,16 +481,16 @@
         [ev, fv, *work(64), dma((10,))], meta, c0, w0, flops(64),
     )
     parts = scatter4(u, "y")
-    e3, _ = gate((e3, y0))
-    m3 = gathered(e3, None)
     u = (parts[0] + parts[1]) + (parts[2] + parts[3])
-    m1, _ = gate((m1, u))
-    w1 = m1, flip(m1, "core")
+    e23, _ = gate((e23, u))
+    m3 = gathered([v[1] for v in e23], None)
     keep, give = halves(u, ci)
     c1, pk, pg = call(
         s01_kernel, "s01", [(8, ORDER), (2, 4, ORDER), (2, 4, ORDER)],
         [pltpu.VMEM((3, 8, ORDER), f32)], meta, [keep, flip(give, "core"), b_mine, b_other],
     )
+    m1, _ = gate((m1, c1))
+    w1 = m1, flip(m1, "core")
     pr = flip(pg, "x0")
     y1, keep, give = call(
         functools.partial(forward_kernel, 1, 32, "ar"), "f1", [(32, 512), (16, 1024), (16, 1024)],

time: 269 us -> 264 us (0.981)
  starting transfers between devices: 94.8 us -> 86.8 us
  waiting for transfers between devices: 99.2 us -> 103 us
    ppermute x47 -> x44, waiting for transfers between devices: 59.2 us -> 75.9 us  [shift(): return lax.ppermute(v, axis, [(i, (i + s) % 4) for i in range(4)])]
    ppermute x22, waiting for transfers between devices: 31.9 us -> 19.6 us  [flip(): return lax.ppermute(v, axis, [(0, 1), (1, 0)])]
    ppermute x47 -> x44, starting transfers between devices: 73.2 us -> 65.3 us  [shift(): return lax.ppermute(v, axis, [(i, (i + s) % 4) for i in range(4)])]
    unnamed x47 -> x57, local copies, waits for them, and re-layouts: 10.4 us -> 9.59 us
  transfers between devices with their start and end apart: 73 -> 70, of which waited for: 43 -> 38; matrix products, arithmetic and copies ran while one was open for 4% -> 4% of each run, Pallas kernels for 10% -> 10%
where the time goes in v10:
time: 264 us; the launch traced here: 263 us
  waiting for transfers between devices  103 us (39%)
  starting transfers between devices  86.8 us (33%)
  Pallas kernels  38.6 us (15%)
  local copies, waits for them, and re-layouts  17 us (6%)
  between operations  14.5 us (5%)
  other arithmetic  3.82 us (1%)
    ppermute x44, waiting for transfers between devices, shift(): return lax.ppermute(v, axis, [(i, (i + s) % 4) for i in range(4)])  75.9 us
    ppermute x44, starting transfers between devices, shift(): return lax.ppermute(v, axis, [(i, (i + s) % 4) for i in range(4)])  65.3 us
    pallas_call x13, Pallas kernels, call(): pl.pallas_call(kernel, out_shape=[jax.ShapeDtypeStruct(s, f32) for s in s...  38.6 us
    ppermute x22, waiting for transfers between devices, flip(): return lax.ppermute(v, axis, [(0, 1), (1, 0)])  19.6 us
    ppermute x22, starting transfers between devices, flip(): return lax.ppermute(v, axis, [(0, 1), (1, 0)])  17 us
    unnamed x57, local copies, waits for them, and re-layouts  9.59 us
    all_gather x3, waiting for transfers between devices, gathered(): return lax.all_gather(jnp.concatenate(parts, 0), 'y', axis=0, tiled=False)  7.03 us
  transfers between devices with their start and end apart: 70, of which 38 were waited for; matrix products, arithmetic and copies ran while one was open for 4% of the time, Pallas kernels for 10%

profile of v10, /device:TPU:0, one launch (start us, length us, event | category | flops | bytes accessed | tf_op | source)
XLA Modules:
  0.0 263.2 jit_solution(4004910618991225356)
XLA Ops:
  8.3 2.1 collective-permute-start.8
  10.4 2.2 collective-permute-start.9
  12.6 2.3 copy.22
  14.9 4.5 %all-to-all-start = ((f32[4,512,128]{2,1,0:T(8,128)}), f32[4,512,128]{2,1,0:T(8,128)S(1)}, u32[]{:S(2)}, u32[]{:S(2)}) async-start(f32[4,512,128]{2,1,0:T(8,128)} %bitcast.3), calls=%async_computation | async-start | bytes 2097152 | tf_op jit(solution)/shard_map/all_to_all | solution.py:443
  19.5 1.6 collective-permute-start.6
  22.5 3.5 %collective-permute-done.6 = f32[1,256,128]{2,1,0:T(8,128)S(1)} collective-permute-done((f32[1,256,128]{2,1,0:T(8,128)S(1)}, f32[1,256,128]{2,1,0:T(8,128)S(1)}, u32[]{:S(2)}, u32[]{:S(2)}) %collective-permute-start.6) | collective-permute-done | bytes 131104 | tf_op jit(solution)/shard_map/ppermute | solution.py:43
  25.9 3.1 %collective-permute-start.7 = (f32[2,256,128]{2,1,0:T(8,128)S(1)}, f32[2,256,128]{2,1,0:T(8,128)S(1)}, u32[]{:S(2)}, u32[]{:S(2)}) collective-permute-start(f32[2,256,128]{2,1,0:T(8,128)S(1)} %maximum_select_fusion.1), channel_id=1, source_target_pairs={{0,64},{64,0},{1,65},{65,1},{2,66},{66,2},{3,67},{67,3},{4,68},{68... | collective-permute-start | bytes 786440 | tf_op jit(solution)/shard_map/ppermute | solution.py:43
  29.1 1.5 collective-permute-start.2
  31.6 1.3 collective-permute-start.10
  33.9 2.1 collective-permute-start.11
  37.5 6.0 %collective-permute-done.3 = f32[256,128]{1,0:T(8,128)S(1)} collective-permute-done((f32[256,128]{1,0:T(8,128)S(1)}, f32[256,128]{1,0:T(8,128)S(1)}, u32[]{:S(2)}, u32[]{:S(2)}) %collective-permute-start.3) | collective-permute-done | bytes 131104 | tf_op jit(solution)/shard_map/ppermute | solution.py:39
  48.1 2.8 %collective-permute-start.13 = (f32[4,512,128]{2,1,0:T(8,128)S(1)}, f32[4,512,128]{2,1,0:T(8,128)S(1)}, u32[]{:S(2)}, u32[]{:S(2)}) collective-permute-start(f32[4,512,128]{2,1,0:T(8,128)S(1)} %all-to-all-done.refs_4_.refs_5_), channel_id=1, source_target_pairs={{0,12},{4,0},{8,4},{12,8},{1,13},{5,1},{9,5},{13,9},{2,14},{6,2},{... | collective-permute-start | bytes 3145736 | tf_op jit(solution)/shard_map/ppermute | solution.py:39
  51.6 2.0 collective-permute-start.16
  57.5 25.1 %collective-permute-done.16 = f32[2,256,128]{2,1,0:T(8,128)S(1)} collective-permute-done((f32[2,256,128]{2,1,0:T(8,128)S(1)}, f32[2,256,128]{2,1,0:T(8,128)S(1)}, u32[]{:S(2)}, u32[]{:S(2)}) %collective-permute-start.16) | collective-permute-done | bytes 262176 | tf_op jit(solution)/shard_map/ppermute | solution.py:39
  85.3 2.4 collective-permute-start.19
  89.7 2.0 collective-permute-start.21
  91.8 2.7 %collective-permute-start.22 = (f32[16,2048]{1,0:T(8,128)S(1)}, f32[16,2048]{1,0:T(8,128)S(1)}, u32[]{:S(2)}, u32[]{:S(2)}) collective-permute-start(f32[16,2048]{1,0:T(8,128)S(1)} %copy-done), channel_id=1, source_target_pairs={{0,2},{1,3},{2,0},{3,1},{4,6},{5,7},{6,4},{7,5},{8,10},{9,11},{10,... | collective-permute-start | bytes 393224 | tf_op jit(solution)/shard_map/ppermute | solution.py:39
  94.4 1.5 collective-permute-start.23
  96.2 2.6 collective-permute-done.22.refs_2_
  99.4 5.9 %f0.1 = (f32[64,512]{1,0:T(8,128)S(1)}, f32[16,1024]{1,0:T(8,128)S(1)}, f32[16,1024]{1,0:T(8,128)S(1)}, f32[16,1024]{1,0:T(8,128)S(1)}, f32[16,1024]{1,0:T(8,128)S(1)}) custom-call(s32[128]{0:T(128)S(1)} %pad_add_fusion.meta, f32[16,2048]{1,0:T(8,128)S(1)} %copy-done, f32[16,2048]{1,0:T(8,128)S(1)} %collective-permute-done.21.refs_1_, ...), custom_call_target="tpu_custom_call" | custom-call | flops 2415919104 | bytes 6815744 | tf_op jit(solution)/shard_map/f0/pallas_call | solution.py:395
  105.3 3.1 %collective-permute-start.24 = (f32[16,1024]{1,0:T(8,128)S(1)}, f32[16,1024]{1,0:T(8,128)S(1)}, u32[]{:S(2)}, u32[]{:S(2)}) collective-permute-start(f32[16,1024]{1,0:T(8,128)S(1)} %get-tuple-element.93), channel_id=1, source_target_pairs={{0,3},{1,0},{2,1},{3,2},{4,7},{5,4},{6,5},{7,6},{8,11},{9,8},{10,9... | collective-permute-start | bytes 196616 | tf_op jit(solution)/shard_map/ppermute | solution.py:39
  109.9 1.7 collective-permute-done.24
  111.6 4.0 %collective-permute-done.25 = f32[16,1024]{1,0:T(8,128)S(1)} collective-permute-done((f32[16,1024]{1,0:T(8,128)S(1)}, f32[16,1024]{1,0:T(8,128)S(1)}, u32[]{:S(2)}, u32[]{:S(2)}) %collective-permute-start.25) | collective-permute-done | bytes 65568 | tf_op jit(solution)/shard_map/ppermute | solution.py:39
  119.6 2.5 collective-permute-start.29
  123.4 2.4 collective-permute-done.28.refs_1_
  126.5 1.8 copy-done.1
  128.3 4.9 %f1.1 = (f32[32,512]{1,0:T(8,128)S(1)}, f32[16,1024]{1,0:T(8,128)S(1)}, f32[16,1024]{1,0:T(8,128)S(1)}) custom-call(s32[128]{0:T(128)S(1)} %pad_add_fusion.meta, f32[8,2048]{1,0:T(8,128)S(1)} %get-tuple-element.98.refs_0_, f32[8,2048]{1,0:T(8,128)S(1)} %collective-permute-done.28.refs_1_, f32[8,2048]{1,0:T(8,128)S(1)} %collective-permute-done.29.refs_2_, ...), custom_call_target="tpu_custom_call" | custom-call | flops 1207959552 | bytes 6553600 | tf_op jit(solution)/shard_map/f1/pallas_call | solution.py:395
  133.7 3.8 %collective-permute-done.32.recv = f32[16,1024]{1,0:T(8,128)S(1)} collective-permute-done((f32[16,1024]{1,0:T(8,128)S(1)}, f32[16,1024]{1,0:T(8,128)S(1)}, u32[]{:S(2)}, u32[]{:S(2)}) %collective-permute-start.32) | collective-permute-done | bytes 65568 | tf_op jit(solution)/shard_map/ppermute | solution.py:43
  140.3 3.1 %collective-permute-start.35 = (f32[16,2048]{1,0:T(8,128)S(1)}, f32[16,2048]{1,0:T(8,128)S(1)}, u32[]{:S(2)}, u32[]{:S(2)}) collective-permute-start(f32[16,2048]{1,0:T(8,128)S(1)} %get-tuple-element.108.refs_0_), channel_id=1, source_target_pairs={{0,8},{4,12},{8,0},{12,4},{1,9},{5,13},{9,1},{13,5},{2,10},{6,14},... | collective-permute-start | bytes 393224 | tf_op jit(solution)/shard_map/ppermute | solution.py:39
  144.6 1.9 collective-permute-done.34.refs_1_
  146.5 3.7 %collective-permute-done.35.refs_2_ = f32[16,2048]{1,0:T(8,128)S(1)} collective-permute-done((f32[16,2048]{1,0:T(8,128)S(1)}, f32[16,2048]{1,0:T(8,128)S(1)}, u32[]{:S(2)}, u32[]{:S(2)}) %collective-permute-start.35) | collective-permute-done | bytes 131104 | tf_op jit(solution)/shard_map/ppermute | solution.py:39
  150.1 4.7 %f2.1 = (f32[16,512]{1,0:T(8,128)S(1)}, f32[8,1024]{1,0:T(8,128)S(1)}, f32[8,1024]{1,0:T(8,128)S(1)}) custom-call(s32[128]{0:T(128)S(1)} %pad_add_fusion.meta, f32[16,2048]{1,0:T(8,128)S(1)} %get-tuple-element.108.refs_0_, f32[16,2048]{1,0:T(8,128)S(1)} %collective-permute-done.34.refs_1_, f32[16,2048]{1,0:T(8,128)S(1)} %collective-permute-done.35.refs_2_, ...), custom_call_target="tpu_custom_call" | custom-call | flops 603979776 | bytes 6815744 | tf_op jit(solution)/shard_map/f2/pallas_call | solution.py:395
  154.9 1.2 collective-permute-start.38
  156.1 4.3 %collective-permute-done.38.recv = f32[8,1024]{1,0:T(8,128)S(1)} collective-permute-done((f32[8,1024]{1,0:T(8,128)S(1)}, f32[8,1024]{1,0:T(8,128)S(1)}, u32[]{:S(2)}, u32[]{:S(2)}) %collective-permute-start.38) | collective-permute-done | bytes 32800 | tf_op jit(solution)/shard_map/ppermute | solution.py:43
  161.0 7.0 %all-gather.11.cloned.1.call-done = f32[16,256,128]{2,1,0:T(8,128)} async-done(((f32[4,256,128]{2,1,0:T(8,128)}), f32[16,256,128]{2,1,0:T(8,128)}) %all-gather.11.cloned.1.call-update) | async-done | bytes 2097168 | tf_op jit(solution)/shard_map/all_gather | solution.py:436
  168.0 1.6 collective-permute-start.40
  169.5 2.9 %collective-permute-start.41 = (f32[8,2048]{1,0:T(8,128)S(1)}, f32[8,2048]{1,0:T(8,128)S(1)}, u32[]{:S(2)}, u32[]{:S(2)}) collective-permute-start(f32[8,2048]{1,0:T(8,128)S(1)} %s23.1.c0), channel_id=1, source_target_pairs={{0,8},{4,12},{8,0},{12,4},{1,9},{5,13},{9,1},{13,5},{2,10},{6,14},... | collective-permute-start | bytes 196616 | tf_op jit(solution)/shard_map/ppermute | solution.py:39
  172.4 1.4 collective-permute-start.42
  173.8 2.5 collective-permute-done.41.c2
  176.7 1.3 copy-done.2
  178.0 4.6 %top.1.c0 = f32[8,2048]{1,0:T(8,128)S(1)} custom-call(s32[128]{0:T(128)S(1)} %pad_add_fusion.meta, f32[8,2048]{1,0:T(8,128)S(1)} %s23.1.c0, f32[8,2048]{1,0:T(8,128)S(1)} %collective-permute-done.40.c1, f32[8,2048]{1,0:T(8,128)S(1)} %collective-permute-done.41.c2, f32[8,2048]{1,0:T(8,128)S(1)} %collective-permute-done.42.c3, f32[4,4,256,128]{3,2,1,0:T(8,128)} %bitcast.63, ...), custom_call_target="tpu_custom_call" | custom-call | flops 301989888 | bytes 4456448 | tf_op jit(solution)/shard_map/top/pallas_call | solution.py:395
  183.6 3.2 %collective-permute-start.45 = (f32[8,2048]{1,0:T(8,128)S(1)}, f32[8,2048]{1,0:T(8,128)S(1)}, u32[]{:S(2)}, u32[]{:S(2)}) collective-permute-start(f32[8,2048]{1,0:T(8,128)S(1)} %top.1.c0), channel_id=1, source_target_pairs={{0,8},{4,12},{8,0},{12,4},{1,9},{5,13},{9,1},{13,5},{2,10},{6,14},... | collective-permute-start | bytes 196616 | tf_op jit(solution)/shard_map/ppermute | solution.py:39
  188.2 1.5 collective-permute-done.45.c2
  189.7 1.3 collective-permute-done.46.c3
  191.6 3.1 %collective-permute-start.47 = (f32[8,2048]{1,0:T(8,128)S(1)}, f32[8,2048]{1,0:T(8,128)S(1)}, u32[]{:S(2)}, u32[]{:S(2)}) collective-permute-start(f32[8,2048]{1,0:T(8,128)S(1)} %x3.1), channel_id=1, source_target_pairs={{0,64},{64,0},{1,65},{65,1},{2,66},{66,2},{3,67},{67,3},{4,68},{68... | collective-permute-start | bytes 196616 | tf_op jit(solution)/shard_map/ppermute | solution.py:43
  194.7 2.8 %collective-permute-done.47.x3r = f32[8,2048]{1,0:T(8,128)S(1)} collective-permute-done((f32[8,2048]{1,0:T(8,128)S(1)}, f32[8,2048]{1,0:T(8,128)S(1)}, u32[]{:S(2)}, u32[]{:S(2)}) %collective-permute-start.47) | collective-permute-done | bytes 65568 | tf_op jit(solution)/shard_map/ppermute | solution.py:43
  197.5 4.7 %b2.1.c0 = f32[16,2048]{1,0:T(8,128)S(1)} custom-call(s32[128]{0:T(128)S(1)} %pad_add_fusion.meta, f32[1,8,2048]{2,1,0:T(8,128)S(1)} %bitcast.54, f32[1,8,2048]{2,1,0:T(8,128)S(1)} %bitcast.55, f32[16,512]{1,0:T(8,128)S(1)} %get-tuple-element.124.refs_2_, f32[4,6,256,128]{3,2,1,0:T(8,128)} %bitcast.61, f32[4,6,256,128]{3,2,1,0:T(8,128)} %collective-permute-done.37.refs_5_.refs_4_), custom_call_target="tpu_custom_call" | custom-call | flops 603979776 | bytes 6455296 | tf_op jit(solution)/shard_map/b2/pallas_call | solution.py:395
  202.6 3.1 %collective-permute-start.49 = (f32[16,2048]{1,0:T(8,128)S(1)}, f32[16,2048]{1,0:T(8,128)S(1)}, u32[]{:S(2)}, u32[]{:S(2)}) collective-permute-start(f32[16,2048]{1,0:T(8,128)S(1)} %b2.1.c0), channel_id=1, source_target_pairs={{0,8},{4,12},{8,0},{12,4},{1,9},{5,13},{9,1},{13,5},{2,10},{6,14},... | collective-permute-start | bytes 393224 | tf_op jit(solution)/shard_map/ppermute | solution.py:39
  206.4 2.0 collective-permute-done.48.c1
  208.5 1.6 collective-permute-done.49.c2
  211.4 1.8 collective-permute-start.51
  213.8 2.1 collective-permute-done.51.refs_1_
  216.0 4.9 %b1.1 = (f32[8,2048]{1,0:T(8,128)S(1)}, f32[8,2048]{1,0:T(8,128)S(1)}, f32[8,2048]{1,0:T(8,128)S(1)}, f32[8,2048]{1,0:T(8,128)S(1)}) custom-call(s32[128]{0:T(128)S(1)} %pad_add_fusion.meta, f32[2,16,2048]{2,1,0:T(8,128)S(1)} %get-tuple-element.125.refs_0_, f32[16,1024]{1,0:T(8,128)S(1)} %collective-permute-done.51.refs_1_, ...), custom_call_target="tpu_custom_call" | custom-call | flops 1207959552 | bytes 6684672 | tf_op jit(solution)/shard_map/b1/pallas_call | solution.py:395
  220.8 2.7 %collective-permute-start.52 = (f32[8,2048]{1,0:T(8,128)S(1)}, f32[8,2048]{1,0:T(8,128)S(1)}, u32[]{:S(2)}, u32[]{:S(2)}) collective-permute-start(f32[8,2048]{1,0:T(8,128)S(1)} %get-tuple-element.129), channel_id=1, source_target_pairs={{0,12},{4,0},{8,4},{12,8},{1,13},{5,1},{9,5},{13,9},{2,14},{6,2},{... | collective-permute-start | bytes 196616 | tf_op jit(solution)/shard_map/ppermute | solution.py:39
  224.5 1.6 collective-permute-done.52.c1
  226.1 3.3 %collective-permute-done.53.c2 = f32[8,2048]{1,0:T(8,128)S(1)} collective-permute-done((f32[8,2048]{1,0:T(8,128)S(1)}, f32[8,2048]{1,0:T(8,128)S(1)}, u32[]{:S(2)}, u32[]{:S(2)}) %collective-permute-start.53) | collective-permute-done | bytes 65568 | tf_op jit(solution)/shard_map/ppermute | solution.py:39
  233.1 1.8 collective-permute-start.58
  234.9 2.1 collective-permute-start.59
  237.6 1.8 collective-permute-done.57.refs_1_
  239.9 4.9 %b0.1 = (f32[16,2048]{1,0:T(8,128)S(1)}, f32[16,2048]{1,0:T(8,128)S(1)}, f32[16,2048]{1,0:T(8,128)S(1)}, f32[16,2048]{1,0:T(8,128)S(1)}) custom-call(s32[128]{0:T(128)S(1)} %pad_add_fusion.meta, f32[16,1024]{1,0:T(8,128)S(1)} %maximum_select_fusion.3.refs_0_, f32[16,1024]{1,0:T(8,128)S(1)} %collective-permute-done.57.refs_1_, ...), custom_call_target="tpu_custom_call" | custom-call | flops 2415919104 | bytes 6684672 | tf_op jit(solution)/shard_map/b0/pallas_call | solution.py:395
  244.8 2.7 %collective-permute-start.60 = (f32[16,2048]{1,0:T(8,128)S(1)}, f32[16,2048]{1,0:T(8,128)S(1)}, u32[]{:S(2)}, u32[]{:S(2)}) collective-permute-start(f32[16,2048]{1,0:T(8,128)S(1)} %get-tuple-element.136), channel_id=1, source_target_pairs={{0,3},{1,0},{2,1},{3,2},{4,7},{5,4},{6,5},{7,6},{8,11},{9,8},{10,9... | collective-permute-start | bytes 393224 | tf_op jit(solution)/shard_map/ppermute | solution.py:39
  249.8 2.5 collective-permute-done.60
  252.3 2.4 collective-permute-done.61
  254.7 1.3 collective-permute-done.62
  (188 shorter events, 48.1 us)
Async XLA Ops:
  8.3 12.9 %collective-permute-start = (f32[2,256,128]{2,1,0:T(8,128)S(1)}, f32[2,256,128]{2,1,0:T(8,128)S(1)}, u32[]{:S(2)}, u32[]{:S(2)}) collective-permute-start(f32[2,256,128]{2,1,0:T(8,128)S(1)} %dynamic-slice_bitcast_fusion), channel_id=1, source_target_pairs={{0,16},{16,0},{1,17},{17,1},{2,18},{18,2},{3,19},{19,3},{4,20},{20... | collective-permute-start | bytes 786440 | tf_op jit(solution)/shard_map/ppermute | solution.py:43
  8.3 20.7 %collective-permute-start.8 = (f32[4,256,128]{2,1,0:T(8,128)}, f32[4,256,128]{2,1,0:T(8,128)}, u32[]{:S(2)}, u32[]{:S(2)}) collective-permute-start(f32[4,256,128]{2,1,0:T(8,128)} %bitcast.72), channel_id=1, source_target_pairs={{0,4},{4,8},{8,12},{12,0},{1,5},{5,9},{9,13},{13,1},{2,6},{6,10},{... | collective-permute-start | bytes 1572872 | tf_op jit(solution)/shard_map/ppermute | solution.py:39
  10.4 21.2 %collective-permute-start.9 = (f32[4,256,128]{2,1,0:T(8,128)}, f32[4,256,128]{2,1,0:T(8,128)}, u32[]{:S(2)}, u32[]{:S(2)}) collective-permute-start(f32[4,256,128]{2,1,0:T(8,128)} %bitcast.73), channel_id=1, source_target_pairs={{0,12},{4,0},{8,4},{12,8},{1,13},{5,1},{9,5},{13,9},{2,14},{6,2},{... | collective-permute-start | bytes 1572872 | tf_op jit(solution)/shard_map/ppermute | solution.py:39
  14.9 29.3 %all-to-all-start = ((f32[4,512,128]{2,1,0:T(8,128)}), f32[4,512,128]{2,1,0:T(8,128)S(1)}, u32[]{:S(2)}, u32[]{:S(2)}) async-start(f32[4,512,128]{2,1,0:T(8,128)} %bitcast.3), calls=%async_computation | async-start | bytes 2097152 | tf_op jit(solution)/shard_map/all_to_all | solution.py:443
  19.4 99.3 %all-gather.7.cloned.1.call-start = ((), (), s32[]{:S(2)}) async-start(), calls=%async_computation.1 | async-start | bytes 3932160 | tf_op jit(solution)/shard_map/all_gather | solution.py:436
  19.5 6.4 %collective-permute-start.6 = (f32[1,256,128]{2,1,0:T(8,128)S(1)}, f32[1,256,128]{2,1,0:T(8,128)S(1)}, u32[]{:S(2)}, u32[]{:S(2)}) collective-permute-start(f32[1,256,128]{2,1,0:T(8,128)S(1)} %bitcast.70), channel_id=1, source_target_pairs={{0,32},{32,0},{1,33},{33,1},{2,34},{34,2},{3,35},{35,3},{4,36},{36... | collective-permute-start | bytes 393224 | tf_op jit(solution)/shard_map/ppermute | solution.py:43
  21.2 12.7 %collective-permute-start.1 = (f32[256,128]{1,0:T(8,128)S(1)}, f32[256,128]{1,0:T(8,128)S(1)}, u32[]{:S(2)}, u32[]{:S(2)}) collective-permute-start(f32[256,128]{1,0:T(8,128)S(1)} %get-tuple-element.142), channel_id=1, source_target_pairs={{0,4},{4,8},{8,12},{12,0},{1,5},{5,9},{9,13},{13,1},{2,6},{6,10},{... | collective-permute-start | bytes 393224 | tf_op jit(solution)/shard_map/ppermute | solution.py:39
  21.3 22.1 %collective-permute-start.5 = (f32[2,256,128]{2,1,0:T(8,128)S(1)}, f32[2,256,128]{2,1,0:T(8,128)S(1)}, u32[]{:S(2)}, u32[]{:S(2)}) collective-permute-start(f32[2,256,128]{2,1,0:T(8,128)S(1)} %maximum_select_fusion), channel_id=1, source_target_pairs={{0,32},{32,0},{1,33},{33,1},{2,34},{34,2},{3,35},{35,3},{4,36},{36... | collective-permute-start | bytes 786440 | tf_op jit(solution)/shard_map/ppermute | solution.py:43
  25.9 17.5 %collective-permute-start.7 = (f32[2,256,128]{2,1,0:T(8,128)S(1)}, f32[2,256,128]{2,1,0:T(8,128)S(1)}, u32[]{:S(2)}, u32[]{:S(2)}) collective-permute-start(f32[2,256,128]{2,1,0:T(8,128)S(1)} %maximum_select_fusion.1), channel_id=1, source_target_pairs={{0,64},{64,0},{1,65},{65,1},{2,66},{66,2},{3,67},{67,3},{4,68},{68... | collective-permute-start | bytes 786440 | tf_op jit(solution)/shard_map/ppermute | solution.py:43
  29.1 7.9 %collective-permute-start.2 = (f32[256,128]{1,0:T(8,128)S(1)}, f32[256,128]{1,0:T(8,128)S(1)}, u32[]{:S(2)}, u32[]{:S(2)}) collective-permute-start(f32[256,128]{1,0:T(8,128)S(1)} %get-tuple-element.141), channel_id=1, source_target_pairs={{0,8},{4,12},{8,0},{12,4},{1,9},{5,13},{9,1},{13,5},{2,10},{6,14},... | collective-permute-start | bytes 393224 | tf_op jit(solution)/shard_map/ppermute | solution.py:39
  31.6 11.9 %collective-permute-start.10 = (f32[2,256,128]{2,1,0:T(8,128)S(1)}, f32[2,256,128]{2,1,0:T(8,128)S(1)}, u32[]{:S(2)}, u32[]{:S(2)}) collective-permute-start(f32[2,256,128]{2,1,0:T(8,128)S(1)} %slice.87), channel_id=1, source_target_pairs={{0,4},{4,8},{8,12},{12,0},{1,5},{5,9},{9,13},{13,1},{2,6},{6,10},{... | collective-permute-start | bytes 786440 | tf_op jit(solution)/shard_map/ppermute | solution.py:39
  33.9 10.3 %collective-permute-start.11 = (f32[2,256,128]{2,1,0:T(8,128)S(1)}, f32[2,256,128]{2,1,0:T(8,128)}, u32[]{:S(2)}, u32[]{:S(2)}) collective-permute-start(f32[2,256,128]{2,1,0:T(8,128)S(1)} %slice.88), channel_id=1, source_target_pairs={{0,12},{4,0},{8,4},{12,8},{1,13},{5,1},{9,5},{13,9},{2,14},{6,2},{... | collective-permute-start | bytes 786440 | tf_op jit(solution)/shard_map/ppermute | solution.py:39
  37.0 6.4 %collective-permute-start.3 = (f32[256,128]{1,0:T(8,128)S(1)}, f32[256,128]{1,0:T(8,128)S(1)}, u32[]{:S(2)}, u32[]{:S(2)}) collective-permute-start(f32[256,128]{1,0:T(8,128)S(1)} %get-tuple-element.140), channel_id=1, source_target_pairs={{0,12},{4,0},{8,4},{12,8},{1,13},{5,1},{9,5},{13,9},{2,14},{6,2},{... | collective-permute-start | bytes 393224 | tf_op jit(solution)/shard_map/ppermute | solution.py:39
  47.2 91.1 %all-gather.9.cloned.1.call-start = ((), (), s32[]{:S(2)}) async-start(), calls=%async_computation.2 | async-start | bytes 3932160 | tf_op jit(solution)/shard_map/all_gather | solution.py:436
  47.3 35.9 %collective-permute-start.12 = (f32[4,512,128]{2,1,0:T(8,128)S(1)}, f32[4,512,128]{2,1,0:T(8,128)S(1)}, u32[]{:S(2)}, u32[]{:S(2)}) collective-permute-start(f32[4,512,128]{2,1,0:T(8,128)S(1)} %all-to-all-done.refs_4_.refs_5_), channel_id=1, source_target_pairs={{0,4},{4,8},{8,12},{12,0},{1,5},{5,9},{9,13},{13,1},{2,6},{6,10},{... | collective-permute-start | bytes 3145736 | tf_op jit(solution)/shard_map/ppermute | solution.py:39
  48.1 35.2 %collective-permute-start.13 = (f32[4,512,128]{2,1,0:T(8,128)S(1)}, f32[4,512,128]{2,1,0:T(8,128)S(1)}, u32[]{:S(2)}, u32[]{:S(2)}) collective-permute-start(f32[4,512,128]{2,1,0:T(8,128)S(1)} %all-to-all-done.refs_4_.refs_5_), channel_id=1, source_target_pairs={{0,12},{4,0},{8,4},{12,8},{1,13},{5,1},{9,5},{13,9},{2,14},{6,2},{... | collective-permute-start | bytes 3145736 | tf_op jit(solution)/shard_map/ppermute | solution.py:39
  50.9 5.7 %collective-permute-start.17 = (f32[256,128]{1,0:T(8,128)}, f32[256,128]{1,0:T(8,128)S(1)}, u32[]{:S(2)}, u32[]{:S(2)}) collective-permute-start(f32[256,128]{1,0:T(8,128)} %param.25), channel_id=1, source_target_pairs={{0,32},{32,0},{1,33},{33,1},{2,34},{34,2},{3,35},{35,3},{4,36},{36... | collective-permute-start | bytes 393224 | tf_op jit(solution)/shard_map/ppermute | solution.py:43
  51.6 30.9 %collective-permute-start.16 = (f32[2,256,128]{2,1,0:T(8,128)S(1)}, f32[2,256,128]{2,1,0:T(8,128)S(1)}, u32[]{:S(2)}, u32[]{:S(2)}) collective-permute-start(f32[2,256,128]{2,1,0:T(8,128)S(1)} %pad_maximum_fusion.4), channel_id=1, source_target_pairs={{0,12},{4,0},{8,4},{12,8},{1,13},{5,1},{9,5},{13,9},{2,14},{6,2},{... | collective-permute-start | bytes 786440 | tf_op jit(solution)/shard_map/ppermute | solution.py:39
  56.6 26.0 %collective-permute-start.15 = (f32[2,256,128]{2,1,0:T(8,128)S(1)}, f32[2,256,128]{2,1,0:T(8,128)S(1)}, u32[]{:S(2)}, u32[]{:S(2)}) collective-permute-start(f32[2,256,128]{2,1,0:T(8,128)S(1)} %pad_maximum_fusion.3), channel_id=1, source_target_pairs={{0,8},{4,12},{8,0},{12,4},{1,9},{5,13},{9,1},{13,5},{2,10},{6,14},... | collective-permute-start | bytes 786440 | tf_op jit(solution)/shard_map/ppermute | solution.py:39
  56.6 26.7 %collective-permute-start.14 = (f32[2,256,128]{2,1,0:T(8,128)S(1)}, f32[2,256,128]{2,1,0:T(8,128)S(1)}, u32[]{:S(2)}, u32[]{:S(2)}) collective-permute-start(f32[2,256,128]{2,1,0:T(8,128)S(1)} %pad_maximum_fusion.2), channel_id=1, source_target_pairs={{0,4},{4,8},{8,12},{12,0},{1,5},{5,9},{9,13},{13,1},{2,6},{6,10},{... | collective-permute-start | bytes 786440 | tf_op jit(solution)/shard_map/ppermute | solution.py:39
  85.2 82.8 %all-gather.11.cloned.1.call-start = ((), (), s32[]{:S(2)}) async-start(), calls=%async_computation.3 | async-start | bytes 2621440 | tf_op jit(solution)/shard_map/all_gather | solution.py:436
  85.3 14.1 %collective-permute-start.19 = (f32[2,512,128]{2,1,0:T(8,128)S(1)}, f32[2,512,128]{2,1,0:T(8,128)}, u32[]{:S(2)}, u32[]{:S(2)}) collective-permute-start(f32[2,512,128]{2,1,0:T(8,128)S(1)} %slice.71), channel_id=1, source_target_pairs={{0,4},{4,8},{8,12},{12,0},{1,5},{5,9},{9,13},{13,1},{2,6},{6,10},{... | collective-permute-start | bytes 1572872 | tf_op jit(solution)/shard_map/ppermute | solution.py:39
  88.8 10.6 %collective-permute-start.20 = (f32[2,512,128]{2,1,0:T(8,128)S(1)}, f32[2,512,128]{2,1,0:T(8,128)}, u32[]{:S(2)}, u32[]{:S(2)}) collective-permute-start(f32[2,512,128]{2,1,0:T(8,128)S(1)} %slice.72), channel_id=1, source_target_pairs={{0,12},{4,0},{8,4},{12,8},{1,13},{5,1},{9,5},{13,9},{2,14},{6,2},{... | collective-permute-start | bytes 1572872 | tf_op jit(solution)/shard_map/ppermute | solution.py:39
  89.7 6.4 %collective-permute-start.21 = (f32[16,2048]{1,0:T(8,128)S(1)}, f32[16,2048]{1,0:T(8,128)S(1)}, u32[]{:S(2)}, u32[]{:S(2)}) collective-permute-start(f32[16,2048]{1,0:T(8,128)S(1)} %copy-done), channel_id=1, source_target_pairs={{0,1},{1,2},{2,3},{3,0},{4,5},{5,6},{6,7},{7,4},{8,9},{9,10},{10,1... | collective-permute-start | bytes 393224 | tf_op jit(solution)/shard_map/ppermute | solution.py:39
  91.8 7.0 %collective-permute-start.22 = (f32[16,2048]{1,0:T(8,128)S(1)}, f32[16,2048]{1,0:T(8,128)S(1)}, u32[]{:S(2)}, u32[]{:S(2)}) collective-permute-start(f32[16,2048]{1,0:T(8,128)S(1)} %copy-done), channel_id=1, source_target_pairs={{0,2},{1,3},{2,0},{3,1},{4,6},{5,7},{6,4},{7,5},{8,10},{9,11},{10,... | collective-permute-start | bytes 393224 | tf_op jit(solution)/shard_map/ppermute | solution.py:39
  94.4 5.0 %collective-permute-start.23 = (f32[16,2048]{1,0:T(8,128)S(1)}, f32[16,2048]{1,0:T(8,128)S(1)}, u32[]{:S(2)}, u32[]{:S(2)}) collective-permute-start(f32[16,2048]{1,0:T(8,128)S(1)} %copy-done), channel_id=1, source_target_pairs={{0,3},{1,0},{2,1},{3,2},{4,7},{5,4},{6,5},{7,6},{8,11},{9,8},{10,9... | collective-permute-start | bytes 393224 | tf_op jit(solution)/shard_map/ppermute | solution.py:39
  105.3 6.3 %collective-permute-start.24 = (f32[16,1024]{1,0:T(8,128)S(1)}, f32[16,1024]{1,0:T(8,128)S(1)}, u32[]{:S(2)}, u32[]{:S(2)}) collective-permute-start(f32[16,1024]{1,0:T(8,128)S(1)} %get-tuple-element.93), channel_id=1, source_target_pairs={{0,3},{1,0},{2,1},{3,2},{4,7},{5,4},{6,5},{7,6},{8,11},{9,8},{10,9... | collective-permute-start | bytes 196616 | tf_op jit(solution)/shard_map/ppermute | solution.py:39
  108.4 7.1 %collective-permute-start.25 = (f32[16,1024]{1,0:T(8,128)S(1)}, f32[16,1024]{1,0:T(8,128)S(1)}, u32[]{:S(2)}, u32[]{:S(2)}) collective-permute-start(f32[16,1024]{1,0:T(8,128)S(1)} %get-tuple-element.94), channel_id=1, source_target_pairs={{0,2},{1,3},{2,0},{3,1},{4,6},{5,7},{6,4},{7,5},{8,10},{9,11},{10,... | collective-permute-start | bytes 196616 | tf_op jit(solution)/shard_map/ppermute | solution.py:39
  109.0 7.4 %collective-permute-start.26 = (f32[16,1024]{1,0:T(8,128)S(1)}, f32[16,1024]{1,0:T(8,128)S(1)}, u32[]{:S(2)}, u32[]{:S(2)}) collective-permute-start(f32[16,1024]{1,0:T(8,128)S(1)} %get-tuple-element.95), channel_id=1, source_target_pairs={{0,1},{1,2},{2,3},{3,0},{4,5},{5,6},{6,7},{7,4},{8,9},{9,10},{10,1... | collective-permute-start | bytes 196616 | tf_op jit(solution)/shard_map/ppermute | solution.py:39
  118.7 7.8 %collective-permute-start.31 = (f32[4,6,256,128]{3,2,1,0:T(8,128)}, f32[4,6,256,128]{3,2,1,0:T(8,128)S(1)}, u32[]{:S(2)}, u32[]{:S(2)}) collective-permute-start(f32[4,6,256,128]{3,2,1,0:T(8,128)} %bitcast.56), channel_id=1, source_target_pairs={{0,16},{16,0},{1,17},{17,1},{2,18},{18,2},{3,19},{19,3},{4,20},{20... | collective-permute-start | bytes 9437192 | tf_op jit(solution)/shard_map/ppermute | solution.py:43
  118.9 7.0 %collective-permute-start.28 = (f32[8,2048]{1,0:T(8,128)S(1)}, f32[8,2048]{1,0:T(8,128)S(1)}, u32[]{:S(2)}, u32[]{:S(2)}) collective-permute-start(f32[8,2048]{1,0:T(8,128)S(1)} %get-tuple-element.98.refs_0_), channel_id=1, source_target_pairs={{0,4},{4,8},{8,12},{12,0},{1,5},{5,9},{9,13},{13,1},{2,6},{6,10},{... | collective-permute-start | bytes 196616 | tf_op jit(solution)/shard_map/ppermute | solution.py:39
  119.6 6.3 %collective-permute-start.29 = (f32[8,2048]{1,0:T(8,128)S(1)}, f32[8,2048]{1,0:T(8,128)S(1)}, u32[]{:S(2)}, u32[]{:S(2)}) collective-permute-start(f32[8,2048]{1,0:T(8,128)S(1)} %get-tuple-element.98.refs_0_), channel_id=1, source_target_pairs={{0,8},{4,12},{8,0},{12,4},{1,9},{5,13},{9,1},{13,5},{2,10},{6,14},... | collective-permute-start | bytes 196616 | tf_op jit(solution)/shard_map/ppermute | solution.py:39
  122.0 4.5 %collective-permute-start.30 = (f32[8,2048]{1,0:T(8,128)S(1)}, f32[8,2048]{1,0:T(8,128)S(1)}, u32[]{:S(2)}, u32[]{:S(2)}) collective-permute-start(f32[8,2048]{1,0:T(8,128)S(1)} %get-tuple-element.98.refs_0_), channel_id=1, source_target_pairs={{0,12},{4,0},{8,4},{12,8},{1,13},{5,1},{9,5},{13,9},{2,14},{6,2},{... | collective-permute-start | bytes 196616 | tf_op jit(solution)/shard_map/ppermute | solution.py:39
  123.0 10.7 %collective-permute-start.33 = (f32[2,4,2048]{2,1,0:T(4,128)S(1)}, f32[2,4,2048]{2,1,0:T(4,128)S(1)}, u32[]{:S(2)}, u32[]{:S(2)}) collective-permute-start(f32[2,4,2048]{2,1,0:T(4,128)S(1)} %get-tuple-element.107), channel_id=1, source_target_pairs={{0,32},{32,0},{1,33},{33,1},{2,34},{34,2},{3,35},{35,3},{4,36},{36... | collective-permute-start | bytes 196616 | tf_op jit(solution)/shard_map/ppermute | solution.py:43
  133.2 4.3 %collective-permute-start.32 = (f32[16,1024]{1,0:T(8,128)S(1)}, f32[16,1024]{1,0:T(8,128)S(1)}, u32[]{:S(2)}, u32[]{:S(2)}) collective-permute-start(f32[16,1024]{1,0:T(8,128)S(1)} %get-tuple-element.105), channel_id=1, source_target_pairs={{0,32},{32,0},{1,33},{33,1},{2,34},{34,2},{3,35},{35,3},{4,36},{36... | collective-permute-start | bytes 196616 | tf_op jit(solution)/shard_map/ppermute | solution.py:43
  138.3 11.8 %collective-permute-start.37 = (f32[4,6,256,128]{3,2,1,0:T(8,128)}, f32[4,6,256,128]{3,2,1,0:T(8,128)}, u32[]{:S(2)}, u32[]{:S(2)}) collective-permute-start(f32[4,6,256,128]{3,2,1,0:T(8,128)} %bitcast.59), channel_id=1, source_target_pairs={{0,16},{16,0},{1,17},{17,1},{2,18},{18,2},{3,19},{19,3},{4,20},{20... | collective-permute-start | bytes 9437192 | tf_op jit(solution)/shard_map/ppermute | solution.py:43
  139.3 7.2 %collective-permute-start.34 = (f32[16,2048]{1,0:T(8,128)S(1)}, f32[16,2048]{1,0:T(8,128)S(1)}, u32[]{:S(2)}, u32[]{:S(2)}) collective-permute-start(f32[16,2048]{1,0:T(8,128)S(1)} %get-tuple-element.108.refs_0_), channel_id=1, source_target_pairs={{0,4},{4,8},{8,12},{12,0},{1,5},{5,9},{9,13},{13,1},{2,6},{6,10},{... | collective-permute-start | bytes 393224 | tf_op jit(solution)/shard_map/ppermute | solution.py:39
  140.3 9.8 %collective-permute-start.35 = (f32[16,2048]{1,0:T(8,128)S(1)}, f32[16,2048]{1,0:T(8,128)S(1)}, u32[]{:S(2)}, u32[]{:S(2)}) collective-permute-start(f32[16,2048]{1,0:T(8,128)S(1)} %get-tuple-element.108.refs_0_), channel_id=1, source_target_pairs={{0,8},{4,12},{8,0},{12,4},{1,9},{5,13},{9,1},{13,5},{2,10},{6,14},... | collective-permute-start | bytes 393224 | tf_op jit(solution)/shard_map/ppermute | solution.py:39
  143.4 6.7 %collective-permute-start.36 = (f32[16,2048]{1,0:T(8,128)S(1)}, f32[16,2048]{1,0:T(8,128)S(1)}, u32[]{:S(2)}, u32[]{:S(2)}) collective-permute-start(f32[16,2048]{1,0:T(8,128)S(1)} %get-tuple-element.108.refs_0_), channel_id=1, source_target_pairs={{0,12},{4,0},{8,4},{12,8},{1,13},{5,1},{9,5},{13,9},{2,14},{6,2},{... | collective-permute-start | bytes 393224 | tf_op jit(solution)/shard_map/ppermute | solution.py:39
  143.4 12.6 %collective-permute-start.39 = (f32[8,2048]{1,0:T(8,128)S(1)}, f32[8,2048]{1,0:T(8,128)S(1)}, u32[]{:S(2)}, u32[]{:S(2)}) collective-permute-start(f32[8,2048]{1,0:T(8,128)S(1)} %get-tuple-element.118), channel_id=1, source_target_pairs={{0,64},{64,0},{1,65},{65,1},{2,66},{66,2},{3,67},{67,3},{4,68},{68... | collective-permute-start | bytes 196616 | tf_op jit(solution)/shard_map/ppermute | solution.py:43
  154.9 5.5 %collective-permute-start.38 = (f32[8,1024]{1,0:T(8,128)S(1)}, f32[8,1024]{1,0:T(8,128)S(1)}, u32[]{:S(2)}, u32[]{:S(2)}) collective-permute-start(f32[8,1024]{1,0:T(8,128)S(1)} %get-tuple-element.116), channel_id=1, source_target_pairs={{0,64},{64,0},{1,65},{65,1},{2,66},{66,2},{3,67},{67,3},{4,68},{68... | collective-permute-start | bytes 98312 | tf_op jit(solution)/shard_map/ppermute | solution.py:43
  168.0 8.7 %collective-permute-start.43 = (f32[4,4,256,128]{3,2,1,0:T(8,128)}, f32[4,4,256,128]{3,2,1,0:T(8,128)S(1)}, u32[]{:S(2)}, u32[]{:S(2)}) collective-permute-start(f32[4,4,256,128]{3,2,1,0:T(8,128)} %bitcast.62), channel_id=1, source_target_pairs={{0,16},{16,0},{1,17},{17,1},{2,18},{18,2},{3,19},{19,3},{4,20},{20... | collective-permute-start | bytes 6291464 | tf_op jit(solution)/shard_map/ppermute | solution.py:43
  168.0 5.8 %collective-permute-start.40 = (f32[8,2048]{1,0:T(8,128)S(1)}, f32[8,2048]{1,0:T(8,128)S(1)}, u32[]{:S(2)}, u32[]{:S(2)}) collective-permute-start(f32[8,2048]{1,0:T(8,128)S(1)} %s23.1.c0), channel_id=1, source_target_pairs={{0,4},{4,8},{8,12},{12,0},{1,5},{5,9},{9,13},{13,1},{2,6},{6,10},{... | collective-permute-start | bytes 196616 | tf_op jit(solution)/shard_map/ppermute | solution.py:39
  169.5 6.7 %collective-permute-start.41 = (f32[8,2048]{1,0:T(8,128)S(1)}, f32[8,2048]{1,0:T(8,128)S(1)}, u32[]{:S(2)}, u32[]{:S(2)}) collective-permute-start(f32[8,2048]{1,0:T(8,128)S(1)} %s23.1.c0), channel_id=1, source_target_pairs={{0,8},{4,12},{8,0},{12,4},{1,9},{5,13},{9,1},{13,5},{2,10},{6,14},... | collective-permute-start | bytes 196616 | tf_op jit(solution)/shard_map/ppermute | solution.py:39
  182.6 5.6 %collective-permute-start.44 = (f32[8,2048]{1,0:T(8,128)S(1)}, f32[8,2048]{1,0:T(8,128)S(1)}, u32[]{:S(2)}, u32[]{:S(2)}) collective-permute-start(f32[8,2048]{1,0:T(8,128)S(1)} %top.1.c0), channel_id=1, source_target_pairs={{0,4},{4,8},{8,12},{12,0},{1,5},{5,9},{9,13},{13,1},{2,6},{6,10},{... | collective-permute-start | bytes 196616 | tf_op jit(solution)/shard_map/ppermute | solution.py:39
  183.6 6.1 %collective-permute-start.45 = (f32[8,2048]{1,0:T(8,128)S(1)}, f32[8,2048]{1,0:T(8,128)S(1)}, u32[]{:S(2)}, u32[]{:S(2)}) collective-permute-start(f32[8,2048]{1,0:T(8,128)S(1)} %top.1.c0), channel_id=1, source_target_pairs={{0,8},{4,12},{8,0},{12,4},{1,9},{5,13},{9,1},{13,5},{2,10},{6,14},... | collective-permute-start | bytes 196616 | tf_op jit(solution)/shard_map/ppermute | solution.py:39
  186.8 4.3 %collective-permute-start.46 = (f32[8,2048]{1,0:T(8,128)S(1)}, f32[8,2048]{1,0:T(8,128)S(1)}, u32[]{:S(2)}, u32[]{:S(2)}) collective-permute-start(f32[8,2048]{1,0:T(8,128)S(1)} %top.1.c0), channel_id=1, source_target_pairs={{0,12},{4,0},{8,4},{12,8},{1,13},{5,1},{9,5},{13,9},{2,14},{6,2},{... | collective-permute-start | bytes 196616 | tf_op jit(solution)/shard_map/ppermute | solution.py:39
  191.6 5.8 %collective-permute-start.47 = (f32[8,2048]{1,0:T(8,128)S(1)}, f32[8,2048]{1,0:T(8,128)S(1)}, u32[]{:S(2)}, u32[]{:S(2)}) collective-permute-start(f32[8,2048]{1,0:T(8,128)S(1)} %x3.1), channel_id=1, source_target_pairs={{0,64},{64,0},{1,65},{65,1},{2,66},{66,2},{3,67},{67,3},{4,68},{68... | collective-permute-start | bytes 196616 | tf_op jit(solution)/shard_map/ppermute | solution.py:43
  202.2 6.2 %collective-permute-start.48 = (f32[16,2048]{1,0:T(8,128)S(1)}, f32[16,2048]{1,0:T(8,128)S(1)}, u32[]{:S(2)}, u32[]{:S(2)}) collective-permute-start(f32[16,2048]{1,0:T(8,128)S(1)} %b2.1.c0), channel_id=1, source_target_pairs={{0,4},{4,8},{8,12},{12,0},{1,5},{5,9},{9,13},{13,1},{2,6},{6,10},{... | collective-permute-start | bytes 393224 | tf_op jit(solution)/shard_map/ppermute | solution.py:39
  202.6 7.5 %collective-permute-start.49 = (f32[16,2048]{1,0:T(8,128)S(1)}, f32[16,2048]{1,0:T(8,128)S(1)}, u32[]{:S(2)}, u32[]{:S(2)}) collective-permute-start(f32[16,2048]{1,0:T(8,128)S(1)} %b2.1.c0), channel_id=1, source_target_pairs={{0,8},{4,12},{8,0},{12,4},{1,9},{5,13},{9,1},{13,5},{2,10},{6,14},... | collective-permute-start | bytes 393224 | tf_op jit(solution)/shard_map/ppermute | solution.py:39
  205.7 5.0 %collective-permute-start.50 = (f32[16,2048]{1,0:T(8,128)S(1)}, f32[16,2048]{1,0:T(8,128)S(1)}, u32[]{:S(2)}, u32[]{:S(2)}) collective-permute-start(f32[16,2048]{1,0:T(8,128)S(1)} %b2.1.c0), channel_id=1, source_target_pairs={{0,12},{4,0},{8,4},{12,8},{1,13},{5,1},{9,5},{13,9},{2,14},{6,2},{... | collective-permute-start | bytes 393224 | tf_op jit(solution)/shard_map/ppermute | solution.py:39
  211.4 4.6 %collective-permute-start.51 = (f32[16,1024]{1,0:T(8,128)S(1)}, f32[16,1024]{1,0:T(8,128)S(1)}, u32[]{:S(2)}, u32[]{:S(2)}) collective-permute-start(f32[16,1024]{1,0:T(8,128)S(1)} %get-tuple-element.126), channel_id=1, source_target_pairs={{0,32},{32,0},{1,33},{33,1},{2,34},{34,2},{3,35},{35,3},{4,36},{36... | collective-permute-start | bytes 196616 | tf_op jit(solution)/shard_map/ppermute | solution.py:43
  213.2 11.3 %collective-permute-start.55 = (f32[2,4,2048]{2,1,0:T(4,128)S(1)}, f32[2,4,2048]{2,1,0:T(4,128)S(1)}, u32[]{:S(2)}, u32[]{:S(2)}) collective-permute-start(f32[2,4,2048]{2,1,0:T(4,128)S(1)} %slice.83.a_mine), channel_id=1, source_target_pairs={{0,32},{32,0},{1,33},{33,1},{2,34},{34,2},{3,35},{35,3},{4,36},{36... | collective-permute-start | bytes 196616 | tf_op jit(solution)/shard_map/ppermute | solution.py:43
  220.8 5.3 %collective-permute-start.52 = (f32[8,2048]{1,0:T(8,128)S(1)}, f32[8,2048]{1,0:T(8,128)S(1)}, u32[]{:S(2)}, u32[]{:S(2)}) collective-permute-start(f32[8,2048]{1,0:T(8,128)S(1)} %get-tuple-element.129), channel_id=1, source_target_pairs={{0,12},{4,0},{8,4},{12,8},{1,13},{5,1},{9,5},{13,9},{2,14},{6,2},{... | collective-permute-start | bytes 196616 | tf_op jit(solution)/shard_map/ppermute | solution.py:39
  223.6 5.8 %collective-permute-start.53 = (f32[8,2048]{1,0:T(8,128)S(1)}, f32[8,2048]{1,0:T(8,128)S(1)}, u32[]{:S(2)}, u32[]{:S(2)}) collective-permute-start(f32[8,2048]{1,0:T(8,128)S(1)} %get-tuple-element.130), channel_id=1, source_target_pairs={{0,8},{4,12},{8,0},{12,4},{1,9},{5,13},{9,1},{13,5},{2,10},{6,14},... | collective-permute-start | bytes 196616 | tf_op jit(solution)/shard_map/ppermute | solution.py:39
  223.9 6.2 %collective-permute-start.54 = (f32[8,2048]{1,0:T(8,128)S(1)}, f32[8,2048]{1,0:T(8,128)S(1)}, u32[]{:S(2)}, u32[]{:S(2)}) collective-permute-start(f32[8,2048]{1,0:T(8,128)S(1)} %get-tuple-element.131), channel_id=1, source_target_pairs={{0,4},{4,8},{8,12},{12,0},{1,5},{5,9},{9,13},{13,1},{2,6},{6,10},{... | collective-permute-start | bytes 196616 | tf_op jit(solution)/shard_map/ppermute | solution.py:39
  230.8 17.7 %collective-permute-start.64 = (f32[8,512]{1,0:T(8,128)S(1)}, f32[8,512]{1,0:T(8,128)S(1)}, u32[]{:S(2)}, u32[]{:S(2)}) collective-permute-start(f32[8,512]{1,0:T(8,128)S(1)} %get-tuple-element.162), channel_id=1, source_target_pairs={{0,16},{16,0},{1,17},{17,1},{2,18},{18,2},{3,19},{19,3},{4,20},{20... | collective-permute-start | bytes 49160 | tf_op jit(solution)/shard_map/ppermute | solution.py:43
  231.4 17.7 %collective-permute-start.63 = (f32[8,1024]{1,0:T(8,128)S(1)}, f32[8,1024]{1,0:T(8,128)S(1)}, u32[]{:S(2)}, u32[]{:S(2)}) collective-permute-start(f32[8,1024]{1,0:T(8,128)S(1)} %get-tuple-element.164), channel_id=1, source_target_pairs={{0,16},{16,0},{1,17},{17,1},{2,18},{18,2},{3,19},{19,3},{4,20},{20... | collective-permute-start | bytes 98312 | tf_op jit(solution)/shard_map/ppermute | solution.py:43
  232.5 6.8 %collective-permute-start.57 = (f32[16,1024]{1,0:T(8,128)S(1)}, f32[16,1024]{1,0:T(8,128)S(1)}, u32[]{:S(2)}, u32[]{:S(2)}) collective-permute-start(f32[16,1024]{1,0:T(8,128)S(1)} %maximum_select_fusion.3.refs_0_), channel_id=1, source_target_pairs={{0,1},{1,2},{2,3},{3,0},{4,5},{5,6},{6,7},{7,4},{8,9},{9,10},{10,1... | collective-permute-start | bytes 196616 | tf_op jit(solution)/shard_map/ppermute | solution.py:39
  233.1 6.2 %collective-permute-start.58 = (f32[16,1024]{1,0:T(8,128)S(1)}, f32[16,1024]{1,0:T(8,128)S(1)}, u32[]{:S(2)}, u32[]{:S(2)}) collective-permute-start(f32[16,1024]{1,0:T(8,128)S(1)} %maximum_select_fusion.3.refs_0_), channel_id=1, source_target_pairs={{0,2},{1,3},{2,0},{3,1},{4,6},{5,7},{6,4},{7,5},{8,10},{9,11},{10,... | collective-permute-start | bytes 196616 | tf_op jit(solution)/shard_map/ppermute | solution.py:39
  234.9 5.0 %collective-permute-start.59 = (f32[16,1024]{1,0:T(8,128)S(1)}, f32[16,1024]{1,0:T(8,128)S(1)}, u32[]{:S(2)}, u32[]{:S(2)}) collective-permute-start(f32[16,1024]{1,0:T(8,128)S(1)} %maximum_select_fusion.3.refs_0_), channel_id=1, source_target_pairs={{0,3},{1,0},{2,1},{3,2},{4,7},{5,4},{6,5},{7,6},{8,11},{9,8},{10,9... | collective-permute-start | bytes 196616 | tf_op jit(solution)/shard_map/ppermute | solution.py:39
  244.8 7.5 %collective-permute-start.60 = (f32[16,2048]{1,0:T(8,128)S(1)}, f32[16,2048]{1,0:T(8,128)S(1)}, u32[]{:S(2)}, u32[]{:S(2)}) collective-permute-start(f32[16,2048]{1,0:T(8,128)S(1)} %get-tuple-element.136), channel_id=1, source_target_pairs={{0,3},{1,0},{2,1},{3,2},{4,7},{5,4},{6,5},{7,6},{8,11},{9,8},{10,9... | collective-permute-start | bytes 393224 | tf_op jit(solution)/shard_map/ppermute | solution.py:39
  247.6 7.1 %collective-permute-start.61 = (f32[16,2048]{1,0:T(8,128)S(1)}, f32[16,2048]{1,0:T(8,128)S(1)}, u32[]{:S(2)}, u32[]{:S(2)}) collective-permute-start(f32[16,2048]{1,0:T(8,128)S(1)} %get-tuple-element.137), channel_id=1, source_target_pairs={{0,2},{1,3},{2,0},{3,1},{4,6},{5,7},{6,4},{7,5},{8,10},{9,11},{10,... | collective-permute-start | bytes 393224 | tf_op jit(solution)/shard_map/ppermute | solution.py:39
  248.1 7.9 %collective-permute-start.62 = (f32[16,2048]{1,0:T(8,128)S(1)}, f32[16,2048]{1,0:T(8,128)S(1)}, u32[]{:S(2)}, u32[]{:S(2)}) collective-permute-start(f32[16,2048]{1,0:T(8,128)S(1)} %get-tuple-element.138), channel_id=1, source_target_pairs={{0,1},{1,2},{2,3},{3,0},{4,5},{5,6},{6,7},{7,4},{8,9},{9,10},{10,1... | collective-permute-start | bytes 393224 | tf_op jit(solution)/shard_map/ppermute | solution.py:39
  (29 other events, 297.1 us)
Sparse Core Ops, SparseCore 0:
  47.4 39.7 all-gather.6
  88.9 42.5 all-gather.8
  139.4 28.5 all-gather.10

commit v11 on v10

--- a/solution.py
+++ b/solution.py
@@ -431,9 +431,12 @@
     def over_z(blocks):
         return [blocks[0]] + [shift(blocks[s], "z", s) for s in (1, 2, 3)]
 
-    def gathered(blocks, f):
+    def packed(blocks, f=None):
         parts = [v[None] for v in blocks] + ([] if f is None else [f.reshape(2, 256, B)])
-        return lax.all_gather(jnp.concatenate(parts, 0), "y", axis=0, tiled=False)
+        return jnp.concatenate(parts, 0)
+
+    def gathered(block):
+        return lax.all_gather(block, "y", axis=0, tiled=False)
 
     gate = lax.optimization_barrier
     off0 = off0.reshape(4, 256, B)
@@ -446,15 +449,15 @@
     e2 = dinv2.reshape(2, 256, B)
     e2 = ordered(pick(e2, ci)[None], flip(pick(e2, 1 - ci)[None], "core"), ci, 0)
     e2_other = flip(e2, "x0")
+    e0, e1, e2, e2_other, fa, fb, fc, fd, off2, dinv3, rhs0, rhs1 = gate(
+        (e0, e1, e2, e2_other, fa, fb, fc, fd, off2, dinv3, rhs0, rhs1)
+    )
+    m1 = gathered(packed(e1, off1))
+
+    ea, eb = shift(e0, "z", 1), shift(e0, "z", -1)
+    f2 = joined(off2, 1)
     e3 = joined(dinv3[None], 1)
     e3_other = flip(e3, "x1")
-    e0, e1, e2, e2_other, e3, e3_other, fa, fb, fc, fd, off2, rhs0, rhs1 = gate(
-        (e0, e1, e2, e2_other, e3, e3_other, fa, fb, fc, fd, off2, rhs0, rhs1)
-    )
-    m1 = gathered(e1, off1)
-
-    ea, eb = shift(e0, "z", 1), shift(e0, "z", -1)
-    f2 = joined(off2, 1)
     e23 = zip(for_z(e2, e2_other, x0), for_z(e3, e3_other, x1))
     e23 = over_z([jnp.stack(pair) for pair in e23])
     b_mine, b_other = halves(jnp.concatenate([rhs1, rhs2, rhs3], 1), ci)
@@ -462,7 +465,7 @@
     ea, eb, e23, f2, b_mine, b_other = gate((ea, eb, e23, f2, b_mine, b_other))
 
     ec, ed = shift(ea[:2], "z", 1), shift(eb[2:], "z", -1)
-    m2 = gathered([v[0] for v in e23], f2)
+    m2 = gathered(packed([v[0] for v in e23], f2))
     c0 = gather4(rhs0, "y")
     ec, ed, c0 = gate((ec, ed, c0))
     w0 = [e0, ea, eb, ec, ed, off0, fa, fb, fc, fd]
@@ -482,8 +485,8 @@
     )
     parts = scatter4(u, "y")
     u = (parts[0] + parts[1]) + (parts[2] + parts[3])
-    e23, _ = gate((e23, u))
-    m3 = gathered([v[1] for v in e23], None)
+    e3, u = gate((packed([v[1] for v in e23]), u))
+    m3 = gathered(e3)
     keep, give = halves(u, ci)
     c1, pk, pg = call(
         s01_kernel, "s01", [(8, ORDER), (2, 4, ORDER), (2, 4, ORDER)],

time: 264 us -> 262 us (level)
  waiting for transfers between devices: 103 us -> 95.1 us
  starting transfers between devices: 86.8 us -> 92.3 us
    ppermute x44, waiting for transfers between devices: 75.9 us -> 65.5 us  [shift(): return lax.ppermute(v, axis, [(i, (i + s) % 4) for i in range(4)])]
    ppermute x22, starting transfers between devices: 17 us -> 23.6 us  [flip(): return lax.ppermute(v, axis, [(0, 1), (1, 0)])]
    unnamed x57 -> x51, local copies, waits for them, and re-layouts: 9.59 us -> 11.1 us
  transfers between devices with their start and end apart: 70 -> 70, of which waited for: 38 -> 42; matrix products, arithmetic and copies ran while one was open for 4% -> 4% of each run, Pallas kernels for 10% -> 10%
where the time goes in v11:
time: 262 us
  waiting for transfers between devices  95.1 us (36%)
  starting transfers between devices  92.3 us (35%)
  Pallas kernels  38.5 us (15%)
  local copies, waits for them, and re-layouts  17.7 us (7%)
  between operations  14.4 us (5%)
  other arithmetic  3.86 us (1%)
    ppermute x44, waiting for transfers between devices, shift(): return lax.ppermute(v, axis, [(i, (i + s) % 4) for i in range(4)])  65.5 us
    ppermute x44, starting transfers between devices, shift(): return lax.ppermute(v, axis, [(i, (i + s) % 4) for i in range(4)])  64.1 us
    pallas_call x13, Pallas kernels, call(): pl.pallas_call(kernel, out_shape=[jax.ShapeDtypeStruct(s, f32) for s in s...  38.5 us
    ppermute x22, starting transfers between devices, flip(): return lax.ppermute(v, axis, [(0, 1), (1, 0)])  23.6 us
    ppermute x22, waiting for transfers between devices, flip(): return lax.ppermute(v, axis, [(0, 1), (1, 0)])  20.5 us
    unnamed x51, local copies, waits for them, and re-layouts  11.1 us
    all_gather x3, waiting for transfers between devices, gathered(): return lax.all_gather(block, 'y', axis=0, tiled=False)  9.06 us
  transfers between devices with their start and end apart: 70, of which 42 were waited for; matrix products, arithmetic and copies ran while one was open for 4% of the time, Pallas kernels for 10%

profile of v11, /device:TPU:0, one launch (start us, length us, event | category | flops | bytes accessed | tf_op | source)
XLA Modules:
  0.0 261.8 jit_solution(415174403351951050)
XLA Ops:
  7.2 2.1 collective-permute-start.6
  9.3 2.2 collective-permute-start.7
  11.5 2.3 copy.22
  13.8 4.5 %all-to-all-start = ((f32[4,512,128]{2,1,0:T(8,128)}), f32[4,512,128]{2,1,0:T(8,128)S(1)}, u32[]{:S(2)}, u32[]{:S(2)}) async-start(f32[4,512,128]{2,1,0:T(8,128)} %bitcast.3), calls=%async_computation | async-start | bytes 2097152 | tf_op jit(solution)/shard_map/all_to_all | solution.py:446
  20.1 1.6 collective-permute-start.5
  21.8 1.8 collective-permute-done.6.refs_10_.refs_11_
  25.7 3.3 %collective-permute-start.9 = (f32[2,256,128]{2,1,0:T(8,128)S(1)}, f32[2,256,128]{2,1,0:T(8,128)}, u32[]{:S(2)}, u32[]{:S(2)}) collective-permute-start(f32[2,256,128]{2,1,0:T(8,128)S(1)} %slice.88), channel_id=1, source_target_pairs={{0,12},{4,0},{8,4},{12,8},{1,13},{5,1},{9,5},{13,9},{2,14},{6,2},{... | collective-permute-start | bytes 786440 | tf_op jit(solution)/shard_map/ppermute | solution.py:39
  30.4 6.5 %collective-permute-done.2 = f32[256,128]{1,0:T(8,128)S(1)} collective-permute-done((f32[256,128]{1,0:T(8,128)S(1)}, f32[256,128]{1,0:T(8,128)S(1)}, u32[]{:S(2)}, u32[]{:S(2)}) %collective-permute-start.2) | collective-permute-done | bytes 131104 | tf_op jit(solution)/shard_map/ppermute | solution.py:39
  37.0 2.3 collective-permute-done.3
  43.5 2.6 collective-permute-start.11
  46.1 1.5 collective-permute-start.17
  49.8 2.8 %collective-permute-done.12 = f32[1,256,128]{2,1,0:T(8,128)S(1)} collective-permute-done((f32[1,256,128]{2,1,0:T(8,128)S(1)}, f32[1,256,128]{2,1,0:T(8,128)S(1)}, u32[]{:S(2)}, u32[]{:S(2)}) %collective-permute-start.12) | collective-permute-done | bytes 131104 | tf_op jit(solution)/shard_map/ppermute | solution.py:43
  52.6 3.0 %collective-permute-start.13 = (f32[2,256,128]{2,1,0:T(8,128)S(1)}, f32[2,256,128]{2,1,0:T(8,128)S(1)}, u32[]{:S(2)}, u32[]{:S(2)}) collective-permute-start(f32[2,256,128]{2,1,0:T(8,128)S(1)} %maximum_select_fusion.1), channel_id=1, source_target_pairs={{0,64},{64,0},{1,65},{65,1},{2,66},{66,2},{3,67},{67,3},{4,68},{68... | collective-permute-start | bytes 786440 | tf_op jit(solution)/shard_map/ppermute | solution.py:43
  55.8 4.8 %collective-permute-done.13 = f32[2,256,128]{2,1,0:T(8,128)S(1)} collective-permute-done((f32[2,256,128]{2,1,0:T(8,128)S(1)}, f32[2,256,128]{2,1,0:T(8,128)S(1)}, u32[]{:S(2)}, u32[]{:S(2)}) %collective-permute-start.13) | collective-permute-done | bytes 262176 | tf_op jit(solution)/shard_map/ppermute | solution.py:43
  60.7 2.0 collective-permute-start.16
  63.8 14.3 %collective-permute-done.16 = f32[2,256,128]{2,1,0:T(8,128)S(1)} collective-permute-done((f32[2,256,128]{2,1,0:T(8,128)S(1)}, f32[2,256,128]{2,1,0:T(8,128)S(1)}, u32[]{:S(2)}, u32[]{:S(2)}) %collective-permute-start.16) | collective-permute-done | bytes 262176 | tf_op jit(solution)/shard_map/ppermute | solution.py:39
  82.2 2.4 collective-permute-start.19
  86.6 1.6 collective-permute-start.21
  88.2 2.9 %collective-permute-start.22 = (f32[16,2048]{1,0:T(8,128)S(1)}, f32[16,2048]{1,0:T(8,128)S(1)}, u32[]{:S(2)}, u32[]{:S(2)}) collective-permute-start(f32[16,2048]{1,0:T(8,128)S(1)} %copy-done), channel_id=1, source_target_pairs={{0,2},{1,3},{2,0},{3,1},{4,6},{5,7},{6,4},{7,5},{8,10},{9,11},{10,... | collective-permute-start | bytes 393224 | tf_op jit(solution)/shard_map/ppermute | solution.py:39
  91.1 1.3 collective-permute-start.23
  92.8 2.6 %collective-permute-done.22.refs_2_ = f32[16,2048]{1,0:T(8,128)S(1)} collective-permute-done((f32[16,2048]{1,0:T(8,128)S(1)}, f32[16,2048]{1,0:T(8,128)S(1)}, u32[]{:S(2)}, u32[]{:S(2)}) %collective-permute-start.22) | collective-permute-done | bytes 131104 | tf_op jit(solution)/shard_map/ppermute | solution.py:39
  97.7 5.7 %f0.1 = (f32[64,512]{1,0:T(8,128)S(1)}, f32[16,1024]{1,0:T(8,128)S(1)}, f32[16,1024]{1,0:T(8,128)S(1)}, f32[16,1024]{1,0:T(8,128)S(1)}, f32[16,1024]{1,0:T(8,128)S(1)}) custom-call(s32[128]{0:T(128)S(1)} %pad_add_fusion.meta, f32[16,2048]{1,0:T(8,128)S(1)} %copy-done, f32[16,2048]{1,0:T(8,128)S(1)} %collective-permute-done.21.refs_1_, ...), custom_call_target="tpu_custom_call" | custom-call | flops 2415919104 | bytes 6815744 | tf_op jit(solution)/shard_map/f0/pallas_call | solution.py:395
  103.4 2.6 %collective-permute-start.24 = (f32[16,1024]{1,0:T(8,128)S(1)}, f32[16,1024]{1,0:T(8,128)S(1)}, u32[]{:S(2)}, u32[]{:S(2)}) collective-permute-start(f32[16,1024]{1,0:T(8,128)S(1)} %get-tuple-element.93), channel_id=1, source_target_pairs={{0,3},{1,0},{2,1},{3,2},{4,7},{5,4},{6,5},{7,6},{8,11},{9,8},{10,9... | collective-permute-start | bytes 196616 | tf_op jit(solution)/shard_map/ppermute | solution.py:39
  109.3 3.9 %collective-permute-done.25 = f32[16,1024]{1,0:T(8,128)S(1)} collective-permute-done((f32[16,1024]{1,0:T(8,128)S(1)}, f32[16,1024]{1,0:T(8,128)S(1)}, u32[]{:S(2)}, u32[]{:S(2)}) %collective-permute-start.25) | collective-permute-done | bytes 65568 | tf_op jit(solution)/shard_map/ppermute | solution.py:39
  117.7 2.3 collective-permute-start.29
  120.8 1.5 collective-permute-start.33
  122.4 1.4 collective-permute-done.29.refs_2_
  124.3 1.8 copy-done.1
  126.0 4.9 %f1.1 = (f32[32,512]{1,0:T(8,128)S(1)}, f32[16,1024]{1,0:T(8,128)S(1)}, f32[16,1024]{1,0:T(8,128)S(1)}) custom-call(s32[128]{0:T(128)S(1)} %pad_add_fusion.meta, f32[8,2048]{1,0:T(8,128)S(1)} %get-tuple-element.99.refs_0_, f32[8,2048]{1,0:T(8,128)S(1)} %collective-permute-done.28.refs_1_, f32[8,2048]{1,0:T(8,128)S(1)} %collective-permute-done.29.refs_2_, ...), custom_call_target="tpu_custom_call" | custom-call | flops 1207959552 | bytes 6553600 | tf_op jit(solution)/shard_map/f1/pallas_call | solution.py:395
  131.0 1.6 collective-permute-start.32
  132.5 2.8 %collective-permute-done.32.recv = f32[16,1024]{1,0:T(8,128)S(1)} collective-permute-done((f32[16,1024]{1,0:T(8,128)S(1)}, f32[16,1024]{1,0:T(8,128)S(1)}, u32[]{:S(2)}, u32[]{:S(2)}) %collective-permute-start.32) | collective-permute-done | bytes 65568 | tf_op jit(solution)/shard_map/ppermute | solution.py:43
  137.1 3.1 %collective-permute-start.35 = (f32[16,2048]{1,0:T(8,128)S(1)}, f32[16,2048]{1,0:T(8,128)S(1)}, u32[]{:S(2)}, u32[]{:S(2)}) collective-permute-start(f32[16,2048]{1,0:T(8,128)S(1)} %get-tuple-element.109.refs_0_), channel_id=1, source_target_pairs={{0,8},{4,12},{8,0},{12,4},{1,9},{5,13},{9,1},{13,5},{2,10},{6,14},... | collective-permute-start | bytes 393224 | tf_op jit(solution)/shard_map/ppermute | solution.py:39
  140.4 3.0 %collective-permute-start.39 = (f32[8,2048]{1,0:T(8,128)S(1)}, f32[8,2048]{1,0:T(8,128)S(1)}, u32[]{:S(2)}, u32[]{:S(2)}) collective-permute-start(f32[8,2048]{1,0:T(8,128)S(1)} %get-tuple-element.115), channel_id=1, source_target_pairs={{0,64},{64,0},{1,65},{65,1},{2,66},{66,2},{3,67},{67,3},{4,68},{68... | collective-permute-start | bytes 196616 | tf_op jit(solution)/shard_map/ppermute | solution.py:43
  143.4 3.5 %collective-permute-done.35.refs_2_ = f32[16,2048]{1,0:T(8,128)S(1)} collective-permute-done((f32[16,2048]{1,0:T(8,128)S(1)}, f32[16,2048]{1,0:T(8,128)S(1)}, u32[]{:S(2)}, u32[]{:S(2)}) %collective-permute-start.35) | collective-permute-done | bytes 131104 | tf_op jit(solution)/shard_map/ppermute | solution.py:39
  146.9 4.7 %f2.1 = (f32[16,512]{1,0:T(8,128)S(1)}, f32[8,1024]{1,0:T(8,128)S(1)}, f32[8,1024]{1,0:T(8,128)S(1)}) custom-call(s32[128]{0:T(128)S(1)} %pad_add_fusion.meta, f32[16,2048]{1,0:T(8,128)S(1)} %get-tuple-element.109.refs_0_, f32[16,2048]{1,0:T(8,128)S(1)} %collective-permute-done.34.refs_1_, f32[16,2048]{1,0:T(8,128)S(1)} %collective-permute-done.35.refs_2_, ...), custom_call_target="tpu_custom_call" | custom-call | flops 603979776 | bytes 6815744 | tf_op jit(solution)/shard_map/f2/pallas_call | solution.py:395
  151.6 3.1 %collective-permute-start.38 = (f32[8,1024]{1,0:T(8,128)S(1)}, f32[8,1024]{1,0:T(8,128)S(1)}, u32[]{:S(2)}, u32[]{:S(2)}) collective-permute-start(f32[8,1024]{1,0:T(8,128)S(1)} %get-tuple-element.113), channel_id=1, source_target_pairs={{0,64},{64,0},{1,65},{65,1},{2,66},{66,2},{3,67},{67,3},{4,68},{68... | collective-permute-start | bytes 98312 | tf_op jit(solution)/shard_map/ppermute | solution.py:43
  154.7 2.4 collective-permute-done.38.recv
  157.8 9.0 %all-gather.11.cloned.1.call-done = f32[16,256,128]{2,1,0:T(8,128)} async-done(((f32[4,256,128]{2,1,0:T(8,128)}), f32[16,256,128]{2,1,0:T(8,128)}) %all-gather.11.cloned.1.call-update) | async-done | bytes 2097168 | tf_op jit(solution)/shard_map/all_gather | solution.py:439
  166.8 1.6 collective-permute-start.40
  168.4 2.9 %collective-permute-start.41 = (f32[8,2048]{1,0:T(8,128)S(1)}, f32[8,2048]{1,0:T(8,128)S(1)}, u32[]{:S(2)}, u32[]{:S(2)}) collective-permute-start(f32[8,2048]{1,0:T(8,128)S(1)} %s23.1.c0), channel_id=1, source_target_pairs={{0,8},{4,12},{8,0},{12,4},{1,9},{5,13},{9,1},{13,5},{2,10},{6,14},... | collective-permute-start | bytes 196616 | tf_op jit(solution)/shard_map/ppermute | solution.py:39
  171.2 1.4 collective-permute-start.42
  172.6 2.5 collective-permute-done.41.c2
  176.8 4.6 %top.1.c0 = f32[8,2048]{1,0:T(8,128)S(1)} custom-call(s32[128]{0:T(128)S(1)} %pad_add_fusion.meta, f32[8,2048]{1,0:T(8,128)S(1)} %s23.1.c0, f32[8,2048]{1,0:T(8,128)S(1)} %collective-permute-done.40.c1, f32[8,2048]{1,0:T(8,128)S(1)} %collective-permute-done.41.c2, f32[8,2048]{1,0:T(8,128)S(1)} %collective-permute-done.42.c3, f32[4,4,256,128]{3,2,1,0:T(8,128)} %bitcast.63, ...), custom_call_target="tpu_custom_call" | custom-call | flops 301989888 | bytes 4456448 | tf_op jit(solution)/shard_map/top/pallas_call | solution.py:395
  182.4 3.2 %collective-permute-start.45 = (f32[8,2048]{1,0:T(8,128)S(1)}, f32[8,2048]{1,0:T(8,128)S(1)}, u32[]{:S(2)}, u32[]{:S(2)}) collective-permute-start(f32[8,2048]{1,0:T(8,128)S(1)} %top.1.c0), channel_id=1, source_target_pairs={{0,8},{4,12},{8,0},{12,4},{1,9},{5,13},{9,1},{13,5},{2,10},{6,14},... | collective-permute-start | bytes 196616 | tf_op jit(solution)/shard_map/ppermute | solution.py:39
  187.0 1.5 collective-permute-done.45.c2
  190.5 3.1 %collective-permute-start.47 = (f32[8,2048]{1,0:T(8,128)S(1)}, f32[8,2048]{1,0:T(8,128)S(1)}, u32[]{:S(2)}, u32[]{:S(2)}) collective-permute-start(f32[8,2048]{1,0:T(8,128)S(1)} %x3.1), channel_id=1, source_target_pairs={{0,64},{64,0},{1,65},{65,1},{2,66},{66,2},{3,67},{67,3},{4,68},{68... | collective-permute-start | bytes 196616 | tf_op jit(solution)/shard_map/ppermute | solution.py:43
  193.5 2.8 %collective-permute-done.47.x3r = f32[8,2048]{1,0:T(8,128)S(1)} collective-permute-done((f32[8,2048]{1,0:T(8,128)S(1)}, f32[8,2048]{1,0:T(8,128)S(1)}, u32[]{:S(2)}, u32[]{:S(2)}) %collective-permute-start.47) | collective-permute-done | bytes 65568 | tf_op jit(solution)/shard_map/ppermute | solution.py:43
  196.3 4.7 %b2.1.c0 = f32[16,2048]{1,0:T(8,128)S(1)} custom-call(s32[128]{0:T(128)S(1)} %pad_add_fusion.meta, f32[1,8,2048]{2,1,0:T(8,128)S(1)} %bitcast.54, f32[1,8,2048]{2,1,0:T(8,128)S(1)} %bitcast.55, f32[16,512]{1,0:T(8,128)S(1)} %get-tuple-element.118.refs_2_, f32[4,6,256,128]{3,2,1,0:T(8,128)} %bitcast.61, f32[4,6,256,128]{3,2,1,0:T(8,128)} %collective-permute-done.37.refs_5_.refs_4_), custom_call_target="tpu_custom_call" | custom-call | flops 603979776 | bytes 6455296 | tf_op jit(solution)/shard_map/b2/pallas_call | solution.py:395
  201.4 3.1 %collective-permute-start.49 = (f32[16,2048]{1,0:T(8,128)S(1)}, f32[16,2048]{1,0:T(8,128)S(1)}, u32[]{:S(2)}, u32[]{:S(2)}) collective-permute-start(f32[16,2048]{1,0:T(8,128)S(1)} %b2.1.c0), channel_id=1, source_target_pairs={{0,8},{4,12},{8,0},{12,4},{1,9},{5,13},{9,1},{13,5},{2,10},{6,14},... | collective-permute-start | bytes 393224 | tf_op jit(solution)/shard_map/ppermute | solution.py:39
  205.2 2.0 collective-permute-done.48.c1
  207.3 1.6 collective-permute-done.49.c2
  210.2 1.5 collective-permute-start.51
  212.6 1.9 collective-permute-done.51.refs_1_
  214.6 4.9 %b1.1 = (f32[8,2048]{1,0:T(8,128)S(1)}, f32[8,2048]{1,0:T(8,128)S(1)}, f32[8,2048]{1,0:T(8,128)S(1)}, f32[8,2048]{1,0:T(8,128)S(1)}) custom-call(s32[128]{0:T(128)S(1)} %pad_add_fusion.meta, f32[2,16,2048]{2,1,0:T(8,128)S(1)} %get-tuple-element.119.refs_0_, f32[16,1024]{1,0:T(8,128)S(1)} %collective-permute-done.51.refs_1_, ...), custom_call_target="tpu_custom_call" | custom-call | flops 1207959552 | bytes 6684672 | tf_op jit(solution)/shard_map/b1/pallas_call | solution.py:395
  219.4 2.7 %collective-permute-start.52 = (f32[8,2048]{1,0:T(8,128)S(1)}, f32[8,2048]{1,0:T(8,128)S(1)}, u32[]{:S(2)}, u32[]{:S(2)}) collective-permute-start(f32[8,2048]{1,0:T(8,128)S(1)} %get-tuple-element.123), channel_id=1, source_target_pairs={{0,12},{4,0},{8,4},{12,8},{1,13},{5,1},{9,5},{13,9},{2,14},{6,2},{... | collective-permute-start | bytes 196616 | tf_op jit(solution)/shard_map/ppermute | solution.py:39
  223.1 1.6 collective-permute-done.52.c1
  224.7 3.3 %collective-permute-done.53.c2 = f32[8,2048]{1,0:T(8,128)S(1)} collective-permute-done((f32[8,2048]{1,0:T(8,128)S(1)}, f32[8,2048]{1,0:T(8,128)S(1)}, u32[]{:S(2)}, u32[]{:S(2)}) %collective-permute-start.53) | collective-permute-done | bytes 65568 | tf_op jit(solution)/shard_map/ppermute | solution.py:39
  231.7 1.8 collective-permute-start.58
  233.5 2.1 collective-permute-start.59
  236.2 1.8 collective-permute-done.57.refs_1_
  238.5 4.9 %b0.1 = (f32[16,2048]{1,0:T(8,128)S(1)}, f32[16,2048]{1,0:T(8,128)S(1)}, f32[16,2048]{1,0:T(8,128)S(1)}, f32[16,2048]{1,0:T(8,128)S(1)}) custom-call(s32[128]{0:T(128)S(1)} %pad_add_fusion.meta, f32[16,1024]{1,0:T(8,128)S(1)} %maximum_select_fusion.3.refs_0_, f32[16,1024]{1,0:T(8,128)S(1)} %collective-permute-done.57.refs_1_, ...), custom_call_target="tpu_custom_call" | custom-call | flops 2415919104 | bytes 6684672 | tf_op jit(solution)/shard_map/b0/pallas_call | solution.py:395
  243.5 2.7 %collective-permute-start.60 = (f32[16,2048]{1,0:T(8,128)S(1)}, f32[16,2048]{1,0:T(8,128)S(1)}, u32[]{:S(2)}, u32[]{:S(2)}) collective-permute-start(f32[16,2048]{1,0:T(8,128)S(1)} %get-tuple-element.130), channel_id=1, source_target_pairs={{0,3},{1,0},{2,1},{3,2},{4,7},{5,4},{6,5},{7,6},{8,11},{9,8},{10,9... | collective-permute-start | bytes 393224 | tf_op jit(solution)/shard_map/ppermute | solution.py:39
  248.4 2.5 collective-permute-done.60
  251.0 2.4 collective-permute-done.61
  (179 shorter events, 52.7 us)
Async XLA Ops:
  7.2 16.4 %collective-permute-start.6 = (f32[4,256,128]{2,1,0:T(8,128)}, f32[4,256,128]{2,1,0:T(8,128)}, u32[]{:S(2)}, u32[]{:S(2)}) collective-permute-start(f32[4,256,128]{2,1,0:T(8,128)} %bitcast.72), channel_id=1, source_target_pairs={{0,4},{4,8},{8,12},{12,0},{1,5},{5,9},{9,13},{13,1},{2,6},{6,10},{... | collective-permute-start | bytes 1572872 | tf_op jit(solution)/shard_map/ppermute | solution.py:39
  9.3 15.4 %collective-permute-start.7 = (f32[4,256,128]{2,1,0:T(8,128)}, f32[4,256,128]{2,1,0:T(8,128)}, u32[]{:S(2)}, u32[]{:S(2)}) collective-permute-start(f32[4,256,128]{2,1,0:T(8,128)} %bitcast.73), channel_id=1, source_target_pairs={{0,12},{4,0},{8,4},{12,8},{1,13},{5,1},{9,5},{13,9},{2,14},{6,2},{... | collective-permute-start | bytes 1572872 | tf_op jit(solution)/shard_map/ppermute | solution.py:39
  13.8 25.6 %all-to-all-start = ((f32[4,512,128]{2,1,0:T(8,128)}), f32[4,512,128]{2,1,0:T(8,128)S(1)}, u32[]{:S(2)}, u32[]{:S(2)}) async-start(f32[4,512,128]{2,1,0:T(8,128)} %bitcast.3), calls=%async_computation | async-start | bytes 2097152 | tf_op jit(solution)/shard_map/all_to_all | solution.py:446
  18.2 98.1 %all-gather.7.cloned.1.call-start = ((), (), s32[]{:S(2)}) async-start(), calls=%async_computation.1 | async-start | bytes 3932160 | tf_op jit(solution)/shard_map/all_gather | solution.py:439
  20.1 19.2 %collective-permute-start.5 = (f32[2,256,128]{2,1,0:T(8,128)S(1)}, f32[2,256,128]{2,1,0:T(8,128)S(1)}, u32[]{:S(2)}, u32[]{:S(2)}) collective-permute-start(f32[2,256,128]{2,1,0:T(8,128)S(1)} %maximum_select_fusion), channel_id=1, source_target_pairs={{0,32},{32,0},{1,33},{33,1},{2,34},{34,2},{3,35},{35,3},{4,36},{36... | collective-permute-start | bytes 786440 | tf_op jit(solution)/shard_map/ppermute | solution.py:43
  21.7 7.6 %collective-permute-start.1 = (f32[256,128]{1,0:T(8,128)S(1)}, f32[256,128]{1,0:T(8,128)S(1)}, u32[]{:S(2)}, u32[]{:S(2)}) collective-permute-start(f32[256,128]{1,0:T(8,128)S(1)} %get-tuple-element.136), channel_id=1, source_target_pairs={{0,4},{4,8},{8,12},{12,0},{1,5},{5,9},{9,13},{13,1},{2,6},{6,10},{... | collective-permute-start | bytes 393224 | tf_op jit(solution)/shard_map/ppermute | solution.py:39
  24.6 14.7 %collective-permute-start.8 = (f32[2,256,128]{2,1,0:T(8,128)S(1)}, f32[2,256,128]{2,1,0:T(8,128)S(1)}, u32[]{:S(2)}, u32[]{:S(2)}) collective-permute-start(f32[2,256,128]{2,1,0:T(8,128)S(1)} %slice.87), channel_id=1, source_target_pairs={{0,4},{4,8},{8,12},{12,0},{1,5},{5,9},{9,13},{13,1},{2,6},{6,10},{... | collective-permute-start | bytes 786440 | tf_op jit(solution)/shard_map/ppermute | solution.py:39
  25.7 13.6 %collective-permute-start.9 = (f32[2,256,128]{2,1,0:T(8,128)S(1)}, f32[2,256,128]{2,1,0:T(8,128)}, u32[]{:S(2)}, u32[]{:S(2)}) collective-permute-start(f32[2,256,128]{2,1,0:T(8,128)S(1)} %slice.88), channel_id=1, source_target_pairs={{0,12},{4,0},{8,4},{12,8},{1,13},{5,1},{9,5},{13,9},{2,14},{6,2},{... | collective-permute-start | bytes 786440 | tf_op jit(solution)/shard_map/ppermute | solution.py:39
  28.9 8.0 %collective-permute-start.2 = (f32[256,128]{1,0:T(8,128)S(1)}, f32[256,128]{1,0:T(8,128)S(1)}, u32[]{:S(2)}, u32[]{:S(2)}) collective-permute-start(f32[256,128]{1,0:T(8,128)S(1)} %get-tuple-element.135), channel_id=1, source_target_pairs={{0,8},{4,12},{8,0},{12,4},{1,9},{5,13},{9,1},{13,5},{2,10},{6,14},... | collective-permute-start | bytes 393224 | tf_op jit(solution)/shard_map/ppermute | solution.py:39
  29.3 10.0 %collective-permute-start.3 = (f32[256,128]{1,0:T(8,128)S(1)}, f32[256,128]{1,0:T(8,128)S(1)}, u32[]{:S(2)}, u32[]{:S(2)}) collective-permute-start(f32[256,128]{1,0:T(8,128)S(1)} %get-tuple-element.134), channel_id=1, source_target_pairs={{0,12},{4,0},{8,4},{12,8},{1,13},{5,1},{9,5},{13,9},{2,14},{6,2},{... | collective-permute-start | bytes 393224 | tf_op jit(solution)/shard_map/ppermute | solution.py:39
  42.2 93.9 %all-gather.9.cloned.1.call-start = ((), (), s32[]{:S(2)}) async-start(), calls=%async_computation.2 | async-start | bytes 3932160 | tf_op jit(solution)/shard_map/all_gather | solution.py:439
  42.3 36.5 %collective-permute-start.10 = (f32[4,512,128]{2,1,0:T(8,128)S(1)}, f32[4,512,128]{2,1,0:T(8,128)S(1)}, u32[]{:S(2)}, u32[]{:S(2)}) collective-permute-start(f32[4,512,128]{2,1,0:T(8,128)S(1)} %all-to-all-done.refs_4_.refs_5_), channel_id=1, source_target_pairs={{0,4},{4,8},{8,12},{12,0},{1,5},{5,9},{9,13},{13,1},{2,6},{6,10},{... | collective-permute-start | bytes 3145736 | tf_op jit(solution)/shard_map/ppermute | solution.py:39
  43.5 35.2 %collective-permute-start.11 = (f32[4,512,128]{2,1,0:T(8,128)S(1)}, f32[4,512,128]{2,1,0:T(8,128)S(1)}, u32[]{:S(2)}, u32[]{:S(2)}) collective-permute-start(f32[4,512,128]{2,1,0:T(8,128)S(1)} %all-to-all-done.refs_4_.refs_5_), channel_id=1, source_target_pairs={{0,12},{4,0},{8,4},{12,8},{1,13},{5,1},{9,5},{13,9},{2,14},{6,2},{... | collective-permute-start | bytes 3145736 | tf_op jit(solution)/shard_map/ppermute | solution.py:39
  46.1 16.7 %collective-permute-start.17 = (f32[256,128]{1,0:T(8,128)S(1)}, f32[256,128]{1,0:T(8,128)S(1)}, u32[]{:S(2)}, u32[]{:S(2)}) collective-permute-start(f32[256,128]{1,0:T(8,128)S(1)} %copy-done.12), channel_id=1, source_target_pairs={{0,32},{32,0},{1,33},{33,1},{2,34},{34,2},{3,35},{35,3},{4,36},{36... | collective-permute-start | bytes 393224 | tf_op jit(solution)/shard_map/ppermute | solution.py:43
  47.6 5.0 %collective-permute-start.12 = (f32[1,256,128]{2,1,0:T(8,128)S(1)}, f32[1,256,128]{2,1,0:T(8,128)S(1)}, u32[]{:S(2)}, u32[]{:S(2)}) collective-permute-start(f32[1,256,128]{2,1,0:T(8,128)S(1)} %bitcast.70), channel_id=1, source_target_pairs={{0,32},{32,0},{1,33},{33,1},{2,34},{34,2},{3,35},{35,3},{4,36},{36... | collective-permute-start | bytes 393224 | tf_op jit(solution)/shard_map/ppermute | solution.py:43
  52.6 8.0 %collective-permute-start.13 = (f32[2,256,128]{2,1,0:T(8,128)S(1)}, f32[2,256,128]{2,1,0:T(8,128)S(1)}, u32[]{:S(2)}, u32[]{:S(2)}) collective-permute-start(f32[2,256,128]{2,1,0:T(8,128)S(1)} %maximum_select_fusion.1), channel_id=1, source_target_pairs={{0,64},{64,0},{1,65},{65,1},{2,66},{66,2},{3,67},{67,3},{4,68},{68... | collective-permute-start | bytes 786440 | tf_op jit(solution)/shard_map/ppermute | solution.py:43
  55.6 7.1 %collective-permute-start.18 = (f32[8,1792]{1,0:T(8,128)S(1)}, f32[8,1792]{1,0:T(8,128)S(1)}, u32[]{:S(2)}, u32[]{:S(2)}) collective-permute-start(f32[8,1792]{1,0:T(8,128)S(1)} %get-tuple-element.159), channel_id=1, source_target_pairs={{0,16},{16,0},{1,17},{17,1},{2,18},{18,2},{3,19},{19,3},{4,20},{20... | collective-permute-start | bytes 172040 | tf_op jit(solution)/shard_map/ppermute | solution.py:43
  60.7 17.5 %collective-permute-start.16 = (f32[2,256,128]{2,1,0:T(8,128)S(1)}, f32[2,256,128]{2,1,0:T(8,128)S(1)}, u32[]{:S(2)}, u32[]{:S(2)}) collective-permute-start(f32[2,256,128]{2,1,0:T(8,128)S(1)} %pad_maximum_fusion.4), channel_id=1, source_target_pairs={{0,12},{4,0},{8,4},{12,8},{1,13},{5,1},{9,5},{13,9},{2,14},{6,2},{... | collective-permute-start | bytes 786440 | tf_op jit(solution)/shard_map/ppermute | solution.py:39
  62.7 15.4 %collective-permute-start.15 = (f32[2,256,128]{2,1,0:T(8,128)S(1)}, f32[2,256,128]{2,1,0:T(8,128)S(1)}, u32[]{:S(2)}, u32[]{:S(2)}) collective-permute-start(f32[2,256,128]{2,1,0:T(8,128)S(1)} %pad_maximum_fusion.3), channel_id=1, source_target_pairs={{0,8},{4,12},{8,0},{12,4},{1,9},{5,13},{9,1},{13,5},{2,10},{6,14},... | collective-permute-start | bytes 786440 | tf_op jit(solution)/shard_map/ppermute | solution.py:39
  62.8 15.9 %collective-permute-start.14 = (f32[2,256,128]{2,1,0:T(8,128)S(1)}, f32[2,256,128]{2,1,0:T(8,128)S(1)}, u32[]{:S(2)}, u32[]{:S(2)}) collective-permute-start(f32[2,256,128]{2,1,0:T(8,128)S(1)} %pad_maximum_fusion.2), channel_id=1, source_target_pairs={{0,4},{4,8},{8,12},{12,0},{1,5},{5,9},{9,13},{13,1},{2,6},{6,10},{... | collective-permute-start | bytes 786440 | tf_op jit(solution)/shard_map/ppermute | solution.py:39
  81.1 85.8 %all-gather.11.cloned.1.call-start = ((), (), s32[]{:S(2)}) async-start(), calls=%async_computation.3 | async-start | bytes 2621440 | tf_op jit(solution)/shard_map/all_gather | solution.py:439
  82.2 13.9 %collective-permute-start.19 = (f32[2,512,128]{2,1,0:T(8,128)S(1)}, f32[2,512,128]{2,1,0:T(8,128)S(1)}, u32[]{:S(2)}, u32[]{:S(2)}) collective-permute-start(f32[2,512,128]{2,1,0:T(8,128)S(1)} %slice.75), channel_id=1, source_target_pairs={{0,4},{4,8},{8,12},{12,0},{1,5},{5,9},{9,13},{13,1},{2,6},{6,10},{... | collective-permute-start | bytes 1572872 | tf_op jit(solution)/shard_map/ppermute | solution.py:39
  85.7 10.7 %collective-permute-start.20 = (f32[2,512,128]{2,1,0:T(8,128)S(1)}, f32[2,512,128]{2,1,0:T(8,128)S(1)}, u32[]{:S(2)}, u32[]{:S(2)}) collective-permute-start(f32[2,512,128]{2,1,0:T(8,128)S(1)} %slice.76), channel_id=1, source_target_pairs={{0,12},{4,0},{8,4},{12,8},{1,13},{5,1},{9,5},{13,9},{2,14},{6,2},{... | collective-permute-start | bytes 1572872 | tf_op jit(solution)/shard_map/ppermute | solution.py:39
  86.6 6.2 %collective-permute-start.21 = (f32[16,2048]{1,0:T(8,128)S(1)}, f32[16,2048]{1,0:T(8,128)S(1)}, u32[]{:S(2)}, u32[]{:S(2)}) collective-permute-start(f32[16,2048]{1,0:T(8,128)S(1)} %copy-done), channel_id=1, source_target_pairs={{0,1},{1,2},{2,3},{3,0},{4,5},{5,6},{6,7},{7,4},{8,9},{9,10},{10,1... | collective-permute-start | bytes 393224 | tf_op jit(solution)/shard_map/ppermute | solution.py:39
  88.2 7.2 %collective-permute-start.22 = (f32[16,2048]{1,0:T(8,128)S(1)}, f32[16,2048]{1,0:T(8,128)S(1)}, u32[]{:S(2)}, u32[]{:S(2)}) collective-permute-start(f32[16,2048]{1,0:T(8,128)S(1)} %copy-done), channel_id=1, source_target_pairs={{0,2},{1,3},{2,0},{3,1},{4,6},{5,7},{6,4},{7,5},{8,10},{9,11},{10,... | collective-permute-start | bytes 393224 | tf_op jit(solution)/shard_map/ppermute | solution.py:39
  91.1 5.0 %collective-permute-start.23 = (f32[16,2048]{1,0:T(8,128)S(1)}, f32[16,2048]{1,0:T(8,128)S(1)}, u32[]{:S(2)}, u32[]{:S(2)}) collective-permute-start(f32[16,2048]{1,0:T(8,128)S(1)} %copy-done), channel_id=1, source_target_pairs={{0,3},{1,0},{2,1},{3,2},{4,7},{5,4},{6,5},{7,6},{8,11},{9,8},{10,9... | collective-permute-start | bytes 393224 | tf_op jit(solution)/shard_map/ppermute | solution.py:39
  103.4 5.9 %collective-permute-start.24 = (f32[16,1024]{1,0:T(8,128)S(1)}, f32[16,1024]{1,0:T(8,128)S(1)}, u32[]{:S(2)}, u32[]{:S(2)}) collective-permute-start(f32[16,1024]{1,0:T(8,128)S(1)} %get-tuple-element.93), channel_id=1, source_target_pairs={{0,3},{1,0},{2,1},{3,2},{4,7},{5,4},{6,5},{7,6},{8,11},{9,8},{10,9... | collective-permute-start | bytes 196616 | tf_op jit(solution)/shard_map/ppermute | solution.py:39
  106.1 7.2 %collective-permute-start.25 = (f32[16,1024]{1,0:T(8,128)S(1)}, f32[16,1024]{1,0:T(8,128)S(1)}, u32[]{:S(2)}, u32[]{:S(2)}) collective-permute-start(f32[16,1024]{1,0:T(8,128)S(1)} %get-tuple-element.94), channel_id=1, source_target_pairs={{0,2},{1,3},{2,0},{3,1},{4,6},{5,7},{6,4},{7,5},{8,10},{9,11},{10,... | collective-permute-start | bytes 196616 | tf_op jit(solution)/shard_map/ppermute | solution.py:39
  106.6 7.5 %collective-permute-start.26 = (f32[16,1024]{1,0:T(8,128)S(1)}, f32[16,1024]{1,0:T(8,128)S(1)}, u32[]{:S(2)}, u32[]{:S(2)}) collective-permute-start(f32[16,1024]{1,0:T(8,128)S(1)} %get-tuple-element.95), channel_id=1, source_target_pairs={{0,1},{1,2},{2,3},{3,0},{4,5},{5,6},{6,7},{7,4},{8,9},{9,10},{10,1... | collective-permute-start | bytes 196616 | tf_op jit(solution)/shard_map/ppermute | solution.py:39
  116.3 8.0 %collective-permute-start.31 = (f32[4,6,256,128]{3,2,1,0:T(8,128)}, f32[4,6,256,128]{3,2,1,0:T(8,128)S(1)}, u32[]{:S(2)}, u32[]{:S(2)}) collective-permute-start(f32[4,6,256,128]{3,2,1,0:T(8,128)} %bitcast.56), channel_id=1, source_target_pairs={{0,16},{16,0},{1,17},{17,1},{2,18},{18,2},{3,19},{19,3},{4,20},{20... | collective-permute-start | bytes 9437192 | tf_op jit(solution)/shard_map/ppermute | solution.py:43
  116.5 5.8 %collective-permute-start.28 = (f32[8,2048]{1,0:T(8,128)S(1)}, f32[8,2048]{1,0:T(8,128)S(1)}, u32[]{:S(2)}, u32[]{:S(2)}) collective-permute-start(f32[8,2048]{1,0:T(8,128)S(1)} %get-tuple-element.99.refs_0_), channel_id=1, source_target_pairs={{0,4},{4,8},{8,12},{12,0},{1,5},{5,9},{9,13},{13,1},{2,6},{6,10},{... | collective-permute-start | bytes 196616 | tf_op jit(solution)/shard_map/ppermute | solution.py:39
  117.7 6.0 %collective-permute-start.29 = (f32[8,2048]{1,0:T(8,128)S(1)}, f32[8,2048]{1,0:T(8,128)S(1)}, u32[]{:S(2)}, u32[]{:S(2)}) collective-permute-start(f32[8,2048]{1,0:T(8,128)S(1)} %get-tuple-element.99.refs_0_), channel_id=1, source_target_pairs={{0,8},{4,12},{8,0},{12,4},{1,9},{5,13},{9,1},{13,5},{2,10},{6,14},... | collective-permute-start | bytes 196616 | tf_op jit(solution)/shard_map/ppermute | solution.py:39
  120.0 4.3 %collective-permute-start.30 = (f32[8,2048]{1,0:T(8,128)S(1)}, f32[8,2048]{1,0:T(8,128)S(1)}, u32[]{:S(2)}, u32[]{:S(2)}) collective-permute-start(f32[8,2048]{1,0:T(8,128)S(1)} %get-tuple-element.99.refs_0_), channel_id=1, source_target_pairs={{0,12},{4,0},{8,4},{12,8},{1,13},{5,1},{9,5},{13,9},{2,14},{6,2},{... | collective-permute-start | bytes 196616 | tf_op jit(solution)/shard_map/ppermute | solution.py:39
  120.8 11.7 %collective-permute-start.33 = (f32[2,4,2048]{2,1,0:T(4,128)S(1)}, f32[2,4,2048]{2,1,0:T(4,128)S(1)}, u32[]{:S(2)}, u32[]{:S(2)}) collective-permute-start(f32[2,4,2048]{2,1,0:T(4,128)S(1)} %get-tuple-element.108), channel_id=1, source_target_pairs={{0,32},{32,0},{1,33},{33,1},{2,34},{34,2},{3,35},{35,3},{4,36},{36... | collective-permute-start | bytes 196616 | tf_op jit(solution)/shard_map/ppermute | solution.py:43
  131.0 4.3 %collective-permute-start.32 = (f32[16,1024]{1,0:T(8,128)S(1)}, f32[16,1024]{1,0:T(8,128)S(1)}, u32[]{:S(2)}, u32[]{:S(2)}) collective-permute-start(f32[16,1024]{1,0:T(8,128)S(1)} %get-tuple-element.106), channel_id=1, source_target_pairs={{0,32},{32,0},{1,33},{33,1},{2,34},{34,2},{3,35},{35,3},{4,36},{36... | collective-permute-start | bytes 196616 | tf_op jit(solution)/shard_map/ppermute | solution.py:43
  136.1 10.8 %collective-permute-start.37 = (f32[4,6,256,128]{3,2,1,0:T(8,128)}, f32[4,6,256,128]{3,2,1,0:T(8,128)}, u32[]{:S(2)}, u32[]{:S(2)}) collective-permute-start(f32[4,6,256,128]{3,2,1,0:T(8,128)} %bitcast.59), channel_id=1, source_target_pairs={{0,16},{16,0},{1,17},{17,1},{2,18},{18,2},{3,19},{19,3},{4,20},{20... | collective-permute-start | bytes 9437192 | tf_op jit(solution)/shard_map/ppermute | solution.py:43
  136.2 7.2 %collective-permute-start.34 = (f32[16,2048]{1,0:T(8,128)S(1)}, f32[16,2048]{1,0:T(8,128)S(1)}, u32[]{:S(2)}, u32[]{:S(2)}) collective-permute-start(f32[16,2048]{1,0:T(8,128)S(1)} %get-tuple-element.109.refs_0_), channel_id=1, source_target_pairs={{0,4},{4,8},{8,12},{12,0},{1,5},{5,9},{9,13},{13,1},{2,6},{6,10},{... | collective-permute-start | bytes 393224 | tf_op jit(solution)/shard_map/ppermute | solution.py:39
  137.1 9.8 %collective-permute-start.35 = (f32[16,2048]{1,0:T(8,128)S(1)}, f32[16,2048]{1,0:T(8,128)S(1)}, u32[]{:S(2)}, u32[]{:S(2)}) collective-permute-start(f32[16,2048]{1,0:T(8,128)S(1)} %get-tuple-element.109.refs_0_), channel_id=1, source_target_pairs={{0,8},{4,12},{8,0},{12,4},{1,9},{5,13},{9,1},{13,5},{2,10},{6,14},... | collective-permute-start | bytes 393224 | tf_op jit(solution)/shard_map/ppermute | solution.py:39
  140.2 6.7 %collective-permute-start.36 = (f32[16,2048]{1,0:T(8,128)S(1)}, f32[16,2048]{1,0:T(8,128)S(1)}, u32[]{:S(2)}, u32[]{:S(2)}) collective-permute-start(f32[16,2048]{1,0:T(8,128)S(1)} %get-tuple-element.109.refs_0_), channel_id=1, source_target_pairs={{0,12},{4,0},{8,4},{12,8},{1,13},{5,1},{9,5},{13,9},{2,14},{6,2},{... | collective-permute-start | bytes 393224 | tf_op jit(solution)/shard_map/ppermute | solution.py:39
  140.4 14.3 %collective-permute-start.39 = (f32[8,2048]{1,0:T(8,128)S(1)}, f32[8,2048]{1,0:T(8,128)S(1)}, u32[]{:S(2)}, u32[]{:S(2)}) collective-permute-start(f32[8,2048]{1,0:T(8,128)S(1)} %get-tuple-element.115), channel_id=1, source_target_pairs={{0,64},{64,0},{1,65},{65,1},{2,66},{66,2},{3,67},{67,3},{4,68},{68... | collective-permute-start | bytes 196616 | tf_op jit(solution)/shard_map/ppermute | solution.py:43
  151.6 5.5 %collective-permute-start.38 = (f32[8,1024]{1,0:T(8,128)S(1)}, f32[8,1024]{1,0:T(8,128)S(1)}, u32[]{:S(2)}, u32[]{:S(2)}) collective-permute-start(f32[8,1024]{1,0:T(8,128)S(1)} %get-tuple-element.113), channel_id=1, source_target_pairs={{0,64},{64,0},{1,65},{65,1},{2,66},{66,2},{3,67},{67,3},{4,68},{68... | collective-permute-start | bytes 98312 | tf_op jit(solution)/shard_map/ppermute | solution.py:43
  166.8 8.7 %collective-permute-start.43 = (f32[4,4,256,128]{3,2,1,0:T(8,128)}, f32[4,4,256,128]{3,2,1,0:T(8,128)S(1)}, u32[]{:S(2)}, u32[]{:S(2)}) collective-permute-start(f32[4,4,256,128]{3,2,1,0:T(8,128)} %bitcast.62), channel_id=1, source_target_pairs={{0,16},{16,0},{1,17},{17,1},{2,18},{18,2},{3,19},{19,3},{4,20},{20... | collective-permute-start | bytes 6291464 | tf_op jit(solution)/shard_map/ppermute | solution.py:43
  166.8 5.8 %collective-permute-start.40 = (f32[8,2048]{1,0:T(8,128)S(1)}, f32[8,2048]{1,0:T(8,128)S(1)}, u32[]{:S(2)}, u32[]{:S(2)}) collective-permute-start(f32[8,2048]{1,0:T(8,128)S(1)} %s23.1.c0), channel_id=1, source_target_pairs={{0,4},{4,8},{8,12},{12,0},{1,5},{5,9},{9,13},{13,1},{2,6},{6,10},{... | collective-permute-start | bytes 196616 | tf_op jit(solution)/shard_map/ppermute | solution.py:39
  168.4 6.7 %collective-permute-start.41 = (f32[8,2048]{1,0:T(8,128)S(1)}, f32[8,2048]{1,0:T(8,128)S(1)}, u32[]{:S(2)}, u32[]{:S(2)}) collective-permute-start(f32[8,2048]{1,0:T(8,128)S(1)} %s23.1.c0), channel_id=1, source_target_pairs={{0,8},{4,12},{8,0},{12,4},{1,9},{5,13},{9,1},{13,5},{2,10},{6,14},... | collective-permute-start | bytes 196616 | tf_op jit(solution)/shard_map/ppermute | solution.py:39
  171.2 4.3 %collective-permute-start.42 = (f32[8,2048]{1,0:T(8,128)S(1)}, f32[8,2048]{1,0:T(8,128)S(1)}, u32[]{:S(2)}, u32[]{:S(2)}) collective-permute-start(f32[8,2048]{1,0:T(8,128)S(1)} %s23.1.c0), channel_id=1, source_target_pairs={{0,12},{4,0},{8,4},{12,8},{1,13},{5,1},{9,5},{13,9},{2,14},{6,2},{... | collective-permute-start | bytes 196616 | tf_op jit(solution)/shard_map/ppermute | solution.py:39
  181.5 5.6 %collective-permute-start.44 = (f32[8,2048]{1,0:T(8,128)S(1)}, f32[8,2048]{1,0:T(8,128)S(1)}, u32[]{:S(2)}, u32[]{:S(2)}) collective-permute-start(f32[8,2048]{1,0:T(8,128)S(1)} %top.1.c0), channel_id=1, source_target_pairs={{0,4},{4,8},{8,12},{12,0},{1,5},{5,9},{9,13},{13,1},{2,6},{6,10},{... | collective-permute-start | bytes 196616 | tf_op jit(solution)/shard_map/ppermute | solution.py:39
  182.4 6.1 %collective-permute-start.45 = (f32[8,2048]{1,0:T(8,128)S(1)}, f32[8,2048]{1,0:T(8,128)S(1)}, u32[]{:S(2)}, u32[]{:S(2)}) collective-permute-start(f32[8,2048]{1,0:T(8,128)S(1)} %top.1.c0), channel_id=1, source_target_pairs={{0,8},{4,12},{8,0},{12,4},{1,9},{5,13},{9,1},{13,5},{2,10},{6,14},... | collective-permute-start | bytes 196616 | tf_op jit(solution)/shard_map/ppermute | solution.py:39
  190.5 5.8 %collective-permute-start.47 = (f32[8,2048]{1,0:T(8,128)S(1)}, f32[8,2048]{1,0:T(8,128)S(1)}, u32[]{:S(2)}, u32[]{:S(2)}) collective-permute-start(f32[8,2048]{1,0:T(8,128)S(1)} %x3.1), channel_id=1, source_target_pairs={{0,64},{64,0},{1,65},{65,1},{2,66},{66,2},{3,67},{67,3},{4,68},{68... | collective-permute-start | bytes 196616 | tf_op jit(solution)/shard_map/ppermute | solution.py:43
  201.0 6.2 %collective-permute-start.48 = (f32[16,2048]{1,0:T(8,128)S(1)}, f32[16,2048]{1,0:T(8,128)S(1)}, u32[]{:S(2)}, u32[]{:S(2)}) collective-permute-start(f32[16,2048]{1,0:T(8,128)S(1)} %b2.1.c0), channel_id=1, source_target_pairs={{0,4},{4,8},{8,12},{12,0},{1,5},{5,9},{9,13},{13,1},{2,6},{6,10},{... | collective-permute-start | bytes 393224 | tf_op jit(solution)/shard_map/ppermute | solution.py:39
  201.4 7.5 %collective-permute-start.49 = (f32[16,2048]{1,0:T(8,128)S(1)}, f32[16,2048]{1,0:T(8,128)S(1)}, u32[]{:S(2)}, u32[]{:S(2)}) collective-permute-start(f32[16,2048]{1,0:T(8,128)S(1)} %b2.1.c0), channel_id=1, source_target_pairs={{0,8},{4,12},{8,0},{12,4},{1,9},{5,13},{9,1},{13,5},{2,10},{6,14},... | collective-permute-start | bytes 393224 | tf_op jit(solution)/shard_map/ppermute | solution.py:39
  204.5 5.0 %collective-permute-start.50 = (f32[16,2048]{1,0:T(8,128)S(1)}, f32[16,2048]{1,0:T(8,128)S(1)}, u32[]{:S(2)}, u32[]{:S(2)}) collective-permute-start(f32[16,2048]{1,0:T(8,128)S(1)} %b2.1.c0), channel_id=1, source_target_pairs={{0,12},{4,0},{8,4},{12,8},{1,13},{5,1},{9,5},{13,9},{2,14},{6,2},{... | collective-permute-start | bytes 393224 | tf_op jit(solution)/shard_map/ppermute | solution.py:39
  210.2 4.3 %collective-permute-start.51 = (f32[16,1024]{1,0:T(8,128)S(1)}, f32[16,1024]{1,0:T(8,128)S(1)}, u32[]{:S(2)}, u32[]{:S(2)}) collective-permute-start(f32[16,1024]{1,0:T(8,128)S(1)} %get-tuple-element.120), channel_id=1, source_target_pairs={{0,32},{32,0},{1,33},{33,1},{2,34},{34,2},{3,35},{35,3},{4,36},{36... | collective-permute-start | bytes 196616 | tf_op jit(solution)/shard_map/ppermute | solution.py:43
  211.8 11.4 %collective-permute-start.55 = (f32[2,4,2048]{2,1,0:T(4,128)S(1)}, f32[2,4,2048]{2,1,0:T(4,128)S(1)}, u32[]{:S(2)}, u32[]{:S(2)}) collective-permute-start(f32[2,4,2048]{2,1,0:T(4,128)S(1)} %slice.83.a_mine), channel_id=1, source_target_pairs={{0,32},{32,0},{1,33},{33,1},{2,34},{34,2},{3,35},{35,3},{4,36},{36... | collective-permute-start | bytes 196616 | tf_op jit(solution)/shard_map/ppermute | solution.py:43
  219.4 5.3 %collective-permute-start.52 = (f32[8,2048]{1,0:T(8,128)S(1)}, f32[8,2048]{1,0:T(8,128)S(1)}, u32[]{:S(2)}, u32[]{:S(2)}) collective-permute-start(f32[8,2048]{1,0:T(8,128)S(1)} %get-tuple-element.123), channel_id=1, source_target_pairs={{0,12},{4,0},{8,4},{12,8},{1,13},{5,1},{9,5},{13,9},{2,14},{6,2},{... | collective-permute-start | bytes 196616 | tf_op jit(solution)/shard_map/ppermute | solution.py:39
  222.2 5.8 %collective-permute-start.53 = (f32[8,2048]{1,0:T(8,128)S(1)}, f32[8,2048]{1,0:T(8,128)S(1)}, u32[]{:S(2)}, u32[]{:S(2)}) collective-permute-start(f32[8,2048]{1,0:T(8,128)S(1)} %get-tuple-element.124), channel_id=1, source_target_pairs={{0,8},{4,12},{8,0},{12,4},{1,9},{5,13},{9,1},{13,5},{2,10},{6,14},... | collective-permute-start | bytes 196616 | tf_op jit(solution)/shard_map/ppermute | solution.py:39
  222.5 6.2 %collective-permute-start.54 = (f32[8,2048]{1,0:T(8,128)S(1)}, f32[8,2048]{1,0:T(8,128)S(1)}, u32[]{:S(2)}, u32[]{:S(2)}) collective-permute-start(f32[8,2048]{1,0:T(8,128)S(1)} %get-tuple-element.125), channel_id=1, source_target_pairs={{0,4},{4,8},{8,12},{12,0},{1,5},{5,9},{9,13},{13,1},{2,6},{6,10},{... | collective-permute-start | bytes 196616 | tf_op jit(solution)/shard_map/ppermute | solution.py:39
  229.4 17.7 %collective-permute-start.64 = (f32[8,512]{1,0:T(8,128)S(1)}, f32[8,512]{1,0:T(8,128)S(1)}, u32[]{:S(2)}, u32[]{:S(2)}) collective-permute-start(f32[8,512]{1,0:T(8,128)S(1)} %get-tuple-element.164), channel_id=1, source_target_pairs={{0,16},{16,0},{1,17},{17,1},{2,18},{18,2},{3,19},{19,3},{4,20},{20... | collective-permute-start | bytes 49160 | tf_op jit(solution)/shard_map/ppermute | solution.py:43
  230.0 17.7 %collective-permute-start.63 = (f32[8,1024]{1,0:T(8,128)S(1)}, f32[8,1024]{1,0:T(8,128)S(1)}, u32[]{:S(2)}, u32[]{:S(2)}) collective-permute-start(f32[8,1024]{1,0:T(8,128)S(1)} %get-tuple-element.166), channel_id=1, source_target_pairs={{0,16},{16,0},{1,17},{17,1},{2,18},{18,2},{3,19},{19,3},{4,20},{20... | collective-permute-start | bytes 98312 | tf_op jit(solution)/shard_map/ppermute | solution.py:43
  231.1 6.8 %collective-permute-start.57 = (f32[16,1024]{1,0:T(8,128)S(1)}, f32[16,1024]{1,0:T(8,128)S(1)}, u32[]{:S(2)}, u32[]{:S(2)}) collective-permute-start(f32[16,1024]{1,0:T(8,128)S(1)} %maximum_select_fusion.3.refs_0_), channel_id=1, source_target_pairs={{0,1},{1,2},{2,3},{3,0},{4,5},{5,6},{6,7},{7,4},{8,9},{9,10},{10,1... | collective-permute-start | bytes 196616 | tf_op jit(solution)/shard_map/ppermute | solution.py:39
  231.7 6.2 %collective-permute-start.58 = (f32[16,1024]{1,0:T(8,128)S(1)}, f32[16,1024]{1,0:T(8,128)S(1)}, u32[]{:S(2)}, u32[]{:S(2)}) collective-permute-start(f32[16,1024]{1,0:T(8,128)S(1)} %maximum_select_fusion.3.refs_0_), channel_id=1, source_target_pairs={{0,2},{1,3},{2,0},{3,1},{4,6},{5,7},{6,4},{7,5},{8,10},{9,11},{10,... | collective-permute-start | bytes 196616 | tf_op jit(solution)/shard_map/ppermute | solution.py:39
  233.5 5.0 %collective-permute-start.59 = (f32[16,1024]{1,0:T(8,128)S(1)}, f32[16,1024]{1,0:T(8,128)S(1)}, u32[]{:S(2)}, u32[]{:S(2)}) collective-permute-start(f32[16,1024]{1,0:T(8,128)S(1)} %maximum_select_fusion.3.refs_0_), channel_id=1, source_target_pairs={{0,3},{1,0},{2,1},{3,2},{4,7},{5,4},{6,5},{7,6},{8,11},{9,8},{10,9... | collective-permute-start | bytes 196616 | tf_op jit(solution)/shard_map/ppermute | solution.py:39
  243.5 7.5 %collective-permute-start.60 = (f32[16,2048]{1,0:T(8,128)S(1)}, f32[16,2048]{1,0:T(8,128)S(1)}, u32[]{:S(2)}, u32[]{:S(2)}) collective-permute-start(f32[16,2048]{1,0:T(8,128)S(1)} %get-tuple-element.130), channel_id=1, source_target_pairs={{0,3},{1,0},{2,1},{3,2},{4,7},{5,4},{6,5},{7,6},{8,11},{9,8},{10,9... | collective-permute-start | bytes 393224 | tf_op jit(solution)/shard_map/ppermute | solution.py:39
  246.2 7.1 %collective-permute-start.61 = (f32[16,2048]{1,0:T(8,128)S(1)}, f32[16,2048]{1,0:T(8,128)S(1)}, u32[]{:S(2)}, u32[]{:S(2)}) collective-permute-start(f32[16,2048]{1,0:T(8,128)S(1)} %get-tuple-element.131), channel_id=1, source_target_pairs={{0,2},{1,3},{2,0},{3,1},{4,6},{5,7},{6,4},{7,5},{8,10},{9,11},{10,... | collective-permute-start | bytes 393224 | tf_op jit(solution)/shard_map/ppermute | solution.py:39
  246.7 7.9 %collective-permute-start.62 = (f32[16,2048]{1,0:T(8,128)S(1)}, f32[16,2048]{1,0:T(8,128)S(1)}, u32[]{:S(2)}, u32[]{:S(2)}) collective-permute-start(f32[16,2048]{1,0:T(8,128)S(1)} %get-tuple-element.132), channel_id=1, source_target_pairs={{0,1},{1,2},{2,3},{3,0},{4,5},{5,6},{6,7},{7,4},{8,9},{9,10},{10,1... | collective-permute-start | bytes 393224 | tf_op jit(solution)/shard_map/ppermute | solution.py:39
  (26 other events, 261.0 us)
Sparse Core Ops, SparseCore 0:
  42.3 41.5 all-gather.6
  85.6 42.5 all-gather.8
  136.3 30.4 all-gather.10

commit v12 on v11

--- a/solution.py
+++ b/solution.py
@@ -462,10 +462,11 @@
     e23 = over_z([jnp.stack(pair) for pair in e23])
     b_mine, b_other = halves(jnp.concatenate([rhs1, rhs2, rhs3], 1), ci)
     b_other = flip(b_other, "core")
-    ea, eb, e23, f2, b_mine, b_other = gate((ea, eb, e23, f2, b_mine, b_other))
+    ea, eb, e23[0], f2, b_mine, b_other = gate((ea, eb, e23[0], f2, b_mine, b_other))
 
     ec, ed = shift(ea[:2], "z", 1), shift(eb[2:], "z", -1)
-    m2 = gathered(packed([v[0] for v in e23], f2))
+    e2, rhs0 = gate((packed([v[0] for v in e23], f2), rhs0))
+    m2 = gathered(e2)
     c0 = gather4(rhs0, "y")
     ec, ed, c0 = gate((ec, ed, c0))
     w0 = [e0, ea, eb, ec, ed, off0, fa, fb, fc, fd]
@@ -499,11 +500,12 @@
         functools.partial(forward_kernel, 1, 32, "ar"), "f1", [(32, 512), (16, 1024), (16, 1024)],
         [ev, fv, *work(32), dma((12,))], meta, gather4(c1, "z"), w1, flops(32),
     )
+    recv = flip(give, "x0")
     part, keep3, give3 = call(
         s12_kernel, "s12", [(16, ORDER), (8, ORDER), (8, ORDER)],
-        [pltpu.VMEM((2, 16, ORDER), f32)], meta, [keep, flip(give, "x0"), pk, pr],
-    )
-    m2, _ = gate((m2, part))
+        [pltpu.VMEM((2, 16, ORDER), f32)], meta, [keep, recv, pk, pr],
+    )
+    m2, _ = gate((m2, recv))
     w2 = m2, flip(m2, "core")
     recv3 = flip(give3, "x1")
     y2, keep, give = call(

time: 262 us -> 261 us (level)
    all_gather x3, waiting for transfers between devices: 9.06 us -> 4.41 us  [gathered(): return lax.all_gather(block, 'y', axis=0, tiled=False)]
    ppermute x22, waiting for transfers between devices: 20.5 us -> 23.2 us  [flip(): return lax.ppermute(v, axis, [(0, 1), (1, 0)])]
  transfers between devices with their start and end apart: 70 -> 70, of which waited for: 42 -> 45; matrix products, arithmetic and copies ran while one was open for 4% -> 4% of each run, Pallas kernels for 10% -> 10%
where the time goes in v12:
time: 261 us
  waiting for transfers between devices  95.1 us (36%)
  starting transfers between devices  92.3 us (35%)
  Pallas kernels  38.5 us (15%)
  local copies, waits for them, and re-layouts  16.8 us (6%)
  between operations  14.4 us (6%)
  other arithmetic  3.88 us (1%)
    ppermute x44, waiting for transfers between devices, shift(): return lax.ppermute(v, axis, [(i, (i + s) % 4) for i in range(4)])  67.5 us
    ppermute x44, starting transfers between devices, shift(): return lax.ppermute(v, axis, [(i, (i + s) % 4) for i in range(4)])  64.1 us
    pallas_call x13, Pallas kernels, call(): pl.pallas_call(kernel, out_shape=[jax.ShapeDtypeStruct(s, f32) for s in s...  38.5 us
    ppermute x22, starting transfers between devices, flip(): return lax.ppermute(v, axis, [(0, 1), (1, 0)])  23.6 us
    ppermute x22, waiting for transfers between devices, flip(): return lax.ppermute(v, axis, [(0, 1), (1, 0)])  23.2 us
    unnamed x51, local copies, waits for them, and re-layouts  10.1 us
  transfers between devices with their start and end apart: 70, of which 45 were waited for; matrix products, arithmetic and copies ran while one was open for 4% of the time, Pallas kernels for 10%

profile of v12, /device:TPU:0, one launch (start us, length us, event | category | flops | bytes accessed | tf_op | source)
XLA Modules:
  0.0 260.8 jit_solution(4418283520239654536)
XLA Ops:
  7.2 2.1 collective-permute-start.6
  9.3 2.2 collective-permute-start.7
  11.5 2.3 copy.22
  13.8 4.5 %all-to-all-start = ((f32[4,512,128]{2,1,0:T(8,128)}), f32[4,512,128]{2,1,0:T(8,128)S(1)}, u32[]{:S(2)}, u32[]{:S(2)}) async-start(f32[4,512,128]{2,1,0:T(8,128)} %bitcast.3), calls=%async_computation | async-start | bytes 2097152 | tf_op jit(solution)/shard_map/all_to_all | solution.py:446
  20.1 1.6 collective-permute-start.5
  21.8 1.8 collective-permute-done.6.refs_10_.refs_11_
  25.7 3.3 %collective-permute-start.9 = (f32[2,256,128]{2,1,0:T(8,128)S(1)}, f32[2,256,128]{2,1,0:T(8,128)}, u32[]{:S(2)}, u32[]{:S(2)}) collective-permute-start(f32[2,256,128]{2,1,0:T(8,128)S(1)} %slice.88), channel_id=1, source_target_pairs={{0,12},{4,0},{8,4},{12,8},{1,13},{5,1},{9,5},{13,9},{2,14},{6,2},{... | collective-permute-start | bytes 786440 | tf_op jit(solution)/shard_map/ppermute | solution.py:39
  30.4 6.5 %collective-permute-done.2 = f32[256,128]{1,0:T(8,128)S(1)} collective-permute-done((f32[256,128]{1,0:T(8,128)S(1)}, f32[256,128]{1,0:T(8,128)S(1)}, u32[]{:S(2)}, u32[]{:S(2)}) %collective-permute-start.2) | collective-permute-done | bytes 131104 | tf_op jit(solution)/shard_map/ppermute | solution.py:39
  37.0 2.3 collective-permute-done.3
  43.5 2.6 collective-permute-start.11
  51.1 3.1 %collective-permute-start.13 = (f32[2,256,128]{2,1,0:T(8,128)S(1)}, f32[2,256,128]{2,1,0:T(8,128)S(1)}, u32[]{:S(2)}, u32[]{:S(2)}) collective-permute-start(f32[2,256,128]{2,1,0:T(8,128)S(1)} %maximum_select_fusion.1), channel_id=1, source_target_pairs={{0,64},{64,0},{1,65},{65,1},{2,66},{66,2},{3,67},{67,3},{4,68},{68... | collective-permute-start | bytes 786440 | tf_op jit(solution)/shard_map/ppermute | solution.py:43
  54.4 5.9 %collective-permute-done.13 = f32[2,256,128]{2,1,0:T(8,128)S(1)} collective-permute-done((f32[2,256,128]{2,1,0:T(8,128)S(1)}, f32[2,256,128]{2,1,0:T(8,128)S(1)}, u32[]{:S(2)}, u32[]{:S(2)}) %collective-permute-start.13) | collective-permute-done | bytes 262176 | tf_op jit(solution)/shard_map/ppermute | solution.py:43
  60.4 2.0 collective-permute-start.18
  64.2 5.9 %collective-permute-done.10.refs_5_.refs_6_ = f32[4,512,128]{2,1,0:T(8,128)S(1)} collective-permute-done((f32[4,512,128]{2,1,0:T(8,128)S(1)}, f32[4,512,128]{2,1,0:T(8,128)S(1)}, u32[]{:S(2)}, u32[]{:S(2)}) %collective-permute-start.10) | collective-permute-done | bytes 1048608 | tf_op jit(solution)/shard_map/ppermute | solution.py:39
  70.1 2.3 collective-permute-done.11.refs_6_.refs_7_
  72.4 2.4 collective-permute-done.16
  74.8 5.1 %collective-permute-done.17 = f32[2,256,128]{2,1,0:T(8,128)S(1)} collective-permute-done((f32[2,256,128]{2,1,0:T(8,128)S(1)}, f32[2,256,128]{2,1,0:T(8,128)S(1)}, u32[]{:S(2)}, u32[]{:S(2)}) %collective-permute-start.17) | collective-permute-done | bytes 262176 | tf_op jit(solution)/shard_map/ppermute | solution.py:39
  84.4 2.2 collective-permute-start.20
  86.5 1.6 collective-permute-start.21
  88.1 2.9 %collective-permute-start.22 = (f32[16,2048]{1,0:T(8,128)S(1)}, f32[16,2048]{1,0:T(8,128)S(1)}, u32[]{:S(2)}, u32[]{:S(2)}) collective-permute-start(f32[16,2048]{1,0:T(8,128)S(1)} %copy-done), channel_id=1, source_target_pairs={{0,2},{1,3},{2,0},{3,1},{4,6},{5,7},{6,4},{7,5},{8,10},{9,11},{10,... | collective-permute-start | bytes 393224 | tf_op jit(solution)/shard_map/ppermute | solution.py:39
  92.7 2.6 %collective-permute-done.22.refs_2_ = f32[16,2048]{1,0:T(8,128)S(1)} collective-permute-done((f32[16,2048]{1,0:T(8,128)S(1)}, f32[16,2048]{1,0:T(8,128)S(1)}, u32[]{:S(2)}, u32[]{:S(2)}) %collective-permute-start.22) | collective-permute-done | bytes 131104 | tf_op jit(solution)/shard_map/ppermute | solution.py:39
  97.6 5.7 %f0.1 = (f32[64,512]{1,0:T(8,128)S(1)}, f32[16,1024]{1,0:T(8,128)S(1)}, f32[16,1024]{1,0:T(8,128)S(1)}, f32[16,1024]{1,0:T(8,128)S(1)}, f32[16,1024]{1,0:T(8,128)S(1)}) custom-call(s32[128]{0:T(128)S(1)} %pad_add_fusion.meta, f32[16,2048]{1,0:T(8,128)S(1)} %copy-done, f32[16,2048]{1,0:T(8,128)S(1)} %collective-permute-done.21.refs_1_, ...), custom_call_target="tpu_custom_call" | custom-call | flops 2415919104 | bytes 6815744 | tf_op jit(solution)/shard_map/f0/pallas_call | solution.py:395
  103.4 2.6 %collective-permute-start.24 = (f32[16,1024]{1,0:T(8,128)S(1)}, f32[16,1024]{1,0:T(8,128)S(1)}, u32[]{:S(2)}, u32[]{:S(2)}) collective-permute-start(f32[16,1024]{1,0:T(8,128)S(1)} %get-tuple-element.91), channel_id=1, source_target_pairs={{0,3},{1,0},{2,1},{3,2},{4,7},{5,4},{6,5},{7,6},{8,11},{9,8},{10,9... | collective-permute-start | bytes 196616 | tf_op jit(solution)/shard_map/ppermute | solution.py:39
  109.4 3.7 %collective-permute-done.25 = f32[16,1024]{1,0:T(8,128)S(1)} collective-permute-done((f32[16,1024]{1,0:T(8,128)S(1)}, f32[16,1024]{1,0:T(8,128)S(1)}, u32[]{:S(2)}, u32[]{:S(2)}) %collective-permute-start.25) | collective-permute-done | bytes 65568 | tf_op jit(solution)/shard_map/ppermute | solution.py:39
  116.6 3.4 %collective-permute-start.29 = (f32[8,2048]{1,0:T(8,128)S(1)}, f32[8,2048]{1,0:T(8,128)S(1)}, u32[]{:S(2)}, u32[]{:S(2)}) collective-permute-start(f32[8,2048]{1,0:T(8,128)S(1)} %get-tuple-element.97.refs_0_), channel_id=1, source_target_pairs={{0,8},{4,12},{8,0},{12,4},{1,9},{5,13},{9,1},{13,5},{2,10},{6,14},... | collective-permute-start | bytes 196616 | tf_op jit(solution)/shard_map/ppermute | solution.py:39
  120.0 2.2 collective-permute-done.28.refs_1_
  122.2 1.6 collective-permute-done.29.refs_2_
  124.3 1.8 copy-done.1
  126.1 4.9 %f1.1 = (f32[32,512]{1,0:T(8,128)S(1)}, f32[16,1024]{1,0:T(8,128)S(1)}, f32[16,1024]{1,0:T(8,128)S(1)}) custom-call(s32[128]{0:T(128)S(1)} %pad_add_fusion.meta, f32[8,2048]{1,0:T(8,128)S(1)} %get-tuple-element.97.refs_0_, f32[8,2048]{1,0:T(8,128)S(1)} %collective-permute-done.28.refs_1_, f32[8,2048]{1,0:T(8,128)S(1)} %collective-permute-done.29.refs_2_, ...), custom_call_target="tpu_custom_call" | custom-call | flops 1207959552 | bytes 6553600 | tf_op jit(solution)/shard_map/f1/pallas_call | solution.py:395
  131.0 1.6 collective-permute-start.32
  132.6 2.8 %collective-permute-done.32.recv = f32[16,1024]{1,0:T(8,128)S(1)} collective-permute-done((f32[16,1024]{1,0:T(8,128)S(1)}, f32[16,1024]{1,0:T(8,128)S(1)}, u32[]{:S(2)}, u32[]{:S(2)}) %collective-permute-start.32) | collective-permute-done | bytes 65568 | tf_op jit(solution)/shard_map/ppermute | solution.py:43
  135.4 1.6 collective-permute-start.33
  136.9 3.0 %collective-permute-done.33.pr = f32[2,4,2048]{2,1,0:T(4,128)S(1)} collective-permute-done((f32[2,4,2048]{2,1,0:T(4,128)S(1)}, f32[2,4,2048]{2,1,0:T(4,128)S(1)}, u32[]{:S(2)}, u32[]{:S(2)}) %collective-permute-start.33) | collective-permute-done | bytes 65568 | tf_op jit(solution)/shard_map/ppermute | solution.py:43
  141.3 3.3 %collective-permute-start.35 = (f32[16,2048]{1,0:T(8,128)S(1)}, f32[16,2048]{1,0:T(8,128)S(1)}, u32[]{:S(2)}, u32[]{:S(2)}) collective-permute-start(f32[16,2048]{1,0:T(8,128)S(1)} %get-tuple-element.107.refs_0_), channel_id=1, source_target_pairs={{0,8},{4,12},{8,0},{12,4},{1,9},{5,13},{9,1},{13,5},{2,10},{6,14},... | collective-permute-start | bytes 393224 | tf_op jit(solution)/shard_map/ppermute | solution.py:39
  144.9 3.0 %collective-permute-start.39 = (f32[8,2048]{1,0:T(8,128)S(1)}, f32[8,2048]{1,0:T(8,128)S(1)}, u32[]{:S(2)}, u32[]{:S(2)}) collective-permute-start(f32[8,2048]{1,0:T(8,128)S(1)} %get-tuple-element.113), channel_id=1, source_target_pairs={{0,64},{64,0},{1,65},{65,1},{2,66},{66,2},{3,67},{67,3},{4,68},{68... | collective-permute-start | bytes 196616 | tf_op jit(solution)/shard_map/ppermute | solution.py:43
  147.9 2.6 collective-permute-done.35.refs_2_
  150.6 4.7 %f2.1 = (f32[16,512]{1,0:T(8,128)S(1)}, f32[8,1024]{1,0:T(8,128)S(1)}, f32[8,1024]{1,0:T(8,128)S(1)}) custom-call(s32[128]{0:T(128)S(1)} %pad_add_fusion.meta, f32[16,2048]{1,0:T(8,128)S(1)} %get-tuple-element.107.refs_0_, f32[16,2048]{1,0:T(8,128)S(1)} %collective-permute-done.34.refs_1_, f32[16,2048]{1,0:T(8,128)S(1)} %collective-permute-done.35.refs_2_, ...), custom_call_target="tpu_custom_call" | custom-call | flops 603979776 | bytes 6815744 | tf_op jit(solution)/shard_map/f2/pallas_call | solution.py:395
  155.3 3.1 %collective-permute-start.38 = (f32[8,1024]{1,0:T(8,128)S(1)}, f32[8,1024]{1,0:T(8,128)S(1)}, u32[]{:S(2)}, u32[]{:S(2)}) collective-permute-start(f32[8,1024]{1,0:T(8,128)S(1)} %get-tuple-element.111), channel_id=1, source_target_pairs={{0,64},{64,0},{1,65},{65,1},{2,66},{66,2},{3,67},{67,3},{4,68},{68... | collective-permute-start | bytes 98312 | tf_op jit(solution)/shard_map/ppermute | solution.py:43
  158.4 2.4 collective-permute-done.38.recv
  161.4 4.4 %all-gather.11.cloned.1.call-done = f32[16,256,128]{2,1,0:T(8,128)} async-done(((f32[4,256,128]{2,1,0:T(8,128)}), f32[16,256,128]{2,1,0:T(8,128)}) %all-gather.11.cloned.1.call-update) | async-done | bytes 2097168 | tf_op jit(solution)/shard_map/all_gather | solution.py:439
  165.8 1.6 collective-permute-start.40
  167.4 2.9 %collective-permute-start.41 = (f32[8,2048]{1,0:T(8,128)S(1)}, f32[8,2048]{1,0:T(8,128)S(1)}, u32[]{:S(2)}, u32[]{:S(2)}) collective-permute-start(f32[8,2048]{1,0:T(8,128)S(1)} %s23.1.c0), channel_id=1, source_target_pairs={{0,8},{4,12},{8,0},{12,4},{1,9},{5,13},{9,1},{13,5},{2,10},{6,14},... | collective-permute-start | bytes 196616 | tf_op jit(solution)/shard_map/ppermute | solution.py:39
  171.6 2.5 collective-permute-done.41.c2
  175.9 4.6 %top.1.c0 = f32[8,2048]{1,0:T(8,128)S(1)} custom-call(s32[128]{0:T(128)S(1)} %pad_add_fusion.meta, f32[8,2048]{1,0:T(8,128)S(1)} %s23.1.c0, f32[8,2048]{1,0:T(8,128)S(1)} %collective-permute-done.40.c1, f32[8,2048]{1,0:T(8,128)S(1)} %collective-permute-done.41.c2, f32[8,2048]{1,0:T(8,128)S(1)} %collective-permute-done.42.c3, f32[4,4,256,128]{3,2,1,0:T(8,128)} %bitcast.63, ...), custom_call_target="tpu_custom_call" | custom-call | flops 301989888 | bytes 4456448 | tf_op jit(solution)/shard_map/top/pallas_call | solution.py:395
  181.4 3.2 %collective-permute-start.45 = (f32[8,2048]{1,0:T(8,128)S(1)}, f32[8,2048]{1,0:T(8,128)S(1)}, u32[]{:S(2)}, u32[]{:S(2)}) collective-permute-start(f32[8,2048]{1,0:T(8,128)S(1)} %top.1.c0), channel_id=1, source_target_pairs={{0,8},{4,12},{8,0},{12,4},{1,9},{5,13},{9,1},{13,5},{2,10},{6,14},... | collective-permute-start | bytes 196616 | tf_op jit(solution)/shard_map/ppermute | solution.py:39
  189.5 3.1 %collective-permute-start.47 = (f32[8,2048]{1,0:T(8,128)S(1)}, f32[8,2048]{1,0:T(8,128)S(1)}, u32[]{:S(2)}, u32[]{:S(2)}) collective-permute-start(f32[8,2048]{1,0:T(8,128)S(1)} %x3.1), channel_id=1, source_target_pairs={{0,64},{64,0},{1,65},{65,1},{2,66},{66,2},{3,67},{67,3},{4,68},{68... | collective-permute-start | bytes 196616 | tf_op jit(solution)/shard_map/ppermute | solution.py:43
  192.6 2.8 %collective-permute-done.47.x3r = f32[8,2048]{1,0:T(8,128)S(1)} collective-permute-done((f32[8,2048]{1,0:T(8,128)S(1)}, f32[8,2048]{1,0:T(8,128)S(1)}, u32[]{:S(2)}, u32[]{:S(2)}) %collective-permute-start.47) | collective-permute-done | bytes 65568 | tf_op jit(solution)/shard_map/ppermute | solution.py:43
  195.3 4.7 %b2.1.c0 = f32[16,2048]{1,0:T(8,128)S(1)} custom-call(s32[128]{0:T(128)S(1)} %pad_add_fusion.meta, f32[1,8,2048]{2,1,0:T(8,128)S(1)} %bitcast.54, f32[1,8,2048]{2,1,0:T(8,128)S(1)} %bitcast.55, f32[16,512]{1,0:T(8,128)S(1)} %get-tuple-element.116.refs_2_, f32[4,6,256,128]{3,2,1,0:T(8,128)} %bitcast.61, f32[4,6,256,128]{3,2,1,0:T(8,128)} %collective-permute-done.37.refs_5_.refs_4_), custom_call_target="tpu_custom_call" | custom-call | flops 603979776 | bytes 6455296 | tf_op jit(solution)/shard_map/b2/pallas_call | solution.py:395
  200.4 3.1 %collective-permute-start.49 = (f32[16,2048]{1,0:T(8,128)S(1)}, f32[16,2048]{1,0:T(8,128)S(1)}, u32[]{:S(2)}, u32[]{:S(2)}) collective-permute-start(f32[16,2048]{1,0:T(8,128)S(1)} %b2.1.c0), channel_id=1, source_target_pairs={{0,8},{4,12},{8,0},{12,4},{1,9},{5,13},{9,1},{13,5},{2,10},{6,14},... | collective-permute-start | bytes 393224 | tf_op jit(solution)/shard_map/ppermute | solution.py:39
  204.3 2.0 collective-permute-done.48.c1
  206.3 1.6 collective-permute-done.49.c2
  209.2 1.5 collective-permute-start.51
  211.7 1.9 collective-permute-done.51.refs_1_
  213.6 4.9 %b1.1 = (f32[8,2048]{1,0:T(8,128)S(1)}, f32[8,2048]{1,0:T(8,128)S(1)}, f32[8,2048]{1,0:T(8,128)S(1)}, f32[8,2048]{1,0:T(8,128)S(1)}) custom-call(s32[128]{0:T(128)S(1)} %pad_add_fusion.meta, f32[2,16,2048]{2,1,0:T(8,128)S(1)} %get-tuple-element.117.refs_0_, f32[16,1024]{1,0:T(8,128)S(1)} %collective-permute-done.51.refs_1_, ...), custom_call_target="tpu_custom_call" | custom-call | flops 1207959552 | bytes 6684672 | tf_op jit(solution)/shard_map/b1/pallas_call | solution.py:395
  218.5 2.7 %collective-permute-start.52 = (f32[8,2048]{1,0:T(8,128)S(1)}, f32[8,2048]{1,0:T(8,128)S(1)}, u32[]{:S(2)}, u32[]{:S(2)}) collective-permute-start(f32[8,2048]{1,0:T(8,128)S(1)} %get-tuple-element.121), channel_id=1, source_target_pairs={{0,12},{4,0},{8,4},{12,8},{1,13},{5,1},{9,5},{13,9},{2,14},{6,2},{... | collective-permute-start | bytes 196616 | tf_op jit(solution)/shard_map/ppermute | solution.py:39
  222.2 1.6 collective-permute-done.52.c1
  223.7 3.3 %collective-permute-done.53.c2 = f32[8,2048]{1,0:T(8,128)S(1)} collective-permute-done((f32[8,2048]{1,0:T(8,128)S(1)}, f32[8,2048]{1,0:T(8,128)S(1)}, u32[]{:S(2)}, u32[]{:S(2)}) %collective-permute-start.53) | collective-permute-done | bytes 65568 | tf_op jit(solution)/shard_map/ppermute | solution.py:39
  230.8 1.8 collective-permute-start.58
  232.5 2.1 collective-permute-start.59
  235.2 1.8 collective-permute-done.57.refs_1_
  237.6 4.9 %b0.1 = (f32[16,2048]{1,0:T(8,128)S(1)}, f32[16,2048]{1,0:T(8,128)S(1)}, f32[16,2048]{1,0:T(8,128)S(1)}, f32[16,2048]{1,0:T(8,128)S(1)}) custom-call(s32[128]{0:T(128)S(1)} %pad_add_fusion.meta, f32[16,1024]{1,0:T(8,128)S(1)} %maximum_select_fusion.3.refs_0_, f32[16,1024]{1,0:T(8,128)S(1)} %collective-permute-done.57.refs_1_, ...), custom_call_target="tpu_custom_call" | custom-call | flops 2415919104 | bytes 6684672 | tf_op jit(solution)/shard_map/b0/pallas_call | solution.py:395
  242.5 2.7 %collective-permute-start.60 = (f32[16,2048]{1,0:T(8,128)S(1)}, f32[16,2048]{1,0:T(8,128)S(1)}, u32[]{:S(2)}, u32[]{:S(2)}) collective-permute-start(f32[16,2048]{1,0:T(8,128)S(1)} %get-tuple-element.128), channel_id=1, source_target_pairs={{0,3},{1,0},{2,1},{3,2},{4,7},{5,4},{6,5},{7,6},{8,11},{9,8},{10,9... | collective-permute-start | bytes 393224 | tf_op jit(solution)/shard_map/ppermute | solution.py:39
  247.4 2.5 collective-permute-done.60
  250.0 2.4 collective-permute-done.61
  (179 shorter events, 56.8 us)
Async XLA Ops:
  7.2 16.4 %collective-permute-start.6 = (f32[4,256,128]{2,1,0:T(8,128)}, f32[4,256,128]{2,1,0:T(8,128)}, u32[]{:S(2)}, u32[]{:S(2)}) collective-permute-start(f32[4,256,128]{2,1,0:T(8,128)} %bitcast.72), channel_id=1, source_target_pairs={{0,4},{4,8},{8,12},{12,0},{1,5},{5,9},{9,13},{13,1},{2,6},{6,10},{... | collective-permute-start | bytes 1572872 | tf_op jit(solution)/shard_map/ppermute | solution.py:39
  9.3 15.4 %collective-permute-start.7 = (f32[4,256,128]{2,1,0:T(8,128)}, f32[4,256,128]{2,1,0:T(8,128)}, u32[]{:S(2)}, u32[]{:S(2)}) collective-permute-start(f32[4,256,128]{2,1,0:T(8,128)} %bitcast.73), channel_id=1, source_target_pairs={{0,12},{4,0},{8,4},{12,8},{1,13},{5,1},{9,5},{13,9},{2,14},{6,2},{... | collective-permute-start | bytes 1572872 | tf_op jit(solution)/shard_map/ppermute | solution.py:39
  13.8 25.6 %all-to-all-start = ((f32[4,512,128]{2,1,0:T(8,128)}), f32[4,512,128]{2,1,0:T(8,128)S(1)}, u32[]{:S(2)}, u32[]{:S(2)}) async-start(f32[4,512,128]{2,1,0:T(8,128)} %bitcast.3), calls=%async_computation | async-start | bytes 2097152 | tf_op jit(solution)/shard_map/all_to_all | solution.py:446
  18.2 98.0 %all-gather.7.cloned.1.call-start = ((), (), s32[]{:S(2)}) async-start(), calls=%async_computation.1 | async-start | bytes 3932160 | tf_op jit(solution)/shard_map/all_gather | solution.py:439
  20.1 19.2 %collective-permute-start.5 = (f32[2,256,128]{2,1,0:T(8,128)S(1)}, f32[2,256,128]{2,1,0:T(8,128)S(1)}, u32[]{:S(2)}, u32[]{:S(2)}) collective-permute-start(f32[2,256,128]{2,1,0:T(8,128)S(1)} %maximum_select_fusion), channel_id=1, source_target_pairs={{0,32},{32,0},{1,33},{33,1},{2,34},{34,2},{3,35},{35,3},{4,36},{36... | collective-permute-start | bytes 786440 | tf_op jit(solution)/shard_map/ppermute | solution.py:43
  21.7 7.6 %collective-permute-start.1 = (f32[256,128]{1,0:T(8,128)S(1)}, f32[256,128]{1,0:T(8,128)S(1)}, u32[]{:S(2)}, u32[]{:S(2)}) collective-permute-start(f32[256,128]{1,0:T(8,128)S(1)} %get-tuple-element.134), channel_id=1, source_target_pairs={{0,4},{4,8},{8,12},{12,0},{1,5},{5,9},{9,13},{13,1},{2,6},{6,10},{... | collective-permute-start | bytes 393224 | tf_op jit(solution)/shard_map/ppermute | solution.py:39
  24.6 14.7 %collective-permute-start.8 = (f32[2,256,128]{2,1,0:T(8,128)S(1)}, f32[2,256,128]{2,1,0:T(8,128)S(1)}, u32[]{:S(2)}, u32[]{:S(2)}) collective-permute-start(f32[2,256,128]{2,1,0:T(8,128)S(1)} %slice.87), channel_id=1, source_target_pairs={{0,4},{4,8},{8,12},{12,0},{1,5},{5,9},{9,13},{13,1},{2,6},{6,10},{... | collective-permute-start | bytes 786440 | tf_op jit(solution)/shard_map/ppermute | solution.py:39
  25.7 13.6 %collective-permute-start.9 = (f32[2,256,128]{2,1,0:T(8,128)S(1)}, f32[2,256,128]{2,1,0:T(8,128)}, u32[]{:S(2)}, u32[]{:S(2)}) collective-permute-start(f32[2,256,128]{2,1,0:T(8,128)S(1)} %slice.88), channel_id=1, source_target_pairs={{0,12},{4,0},{8,4},{12,8},{1,13},{5,1},{9,5},{13,9},{2,14},{6,2},{... | collective-permute-start | bytes 786440 | tf_op jit(solution)/shard_map/ppermute | solution.py:39
  28.9 8.0 %collective-permute-start.2 = (f32[256,128]{1,0:T(8,128)S(1)}, f32[256,128]{1,0:T(8,128)S(1)}, u32[]{:S(2)}, u32[]{:S(2)}) collective-permute-start(f32[256,128]{1,0:T(8,128)S(1)} %get-tuple-element.133), channel_id=1, source_target_pairs={{0,8},{4,12},{8,0},{12,4},{1,9},{5,13},{9,1},{13,5},{2,10},{6,14},... | collective-permute-start | bytes 393224 | tf_op jit(solution)/shard_map/ppermute | solution.py:39
  29.3 10.0 %collective-permute-start.3 = (f32[256,128]{1,0:T(8,128)S(1)}, f32[256,128]{1,0:T(8,128)S(1)}, u32[]{:S(2)}, u32[]{:S(2)}) collective-permute-start(f32[256,128]{1,0:T(8,128)S(1)} %get-tuple-element.132), channel_id=1, source_target_pairs={{0,12},{4,0},{8,4},{12,8},{1,13},{5,1},{9,5},{13,9},{2,14},{6,2},{... | collective-permute-start | bytes 393224 | tf_op jit(solution)/shard_map/ppermute | solution.py:39
  42.2 90.4 %all-gather.9.cloned.1.call-start = ((), (), s32[]{:S(2)}) async-start(), calls=%async_computation.2 | async-start | bytes 3932160 | tf_op jit(solution)/shard_map/all_gather | solution.py:439
  42.3 27.8 %collective-permute-start.10 = (f32[4,512,128]{2,1,0:T(8,128)S(1)}, f32[4,512,128]{2,1,0:T(8,128)S(1)}, u32[]{:S(2)}, u32[]{:S(2)}) collective-permute-start(f32[4,512,128]{2,1,0:T(8,128)S(1)} %all-to-all-done.refs_4_.refs_5_), channel_id=1, source_target_pairs={{0,4},{4,8},{8,12},{12,0},{1,5},{5,9},{9,13},{13,1},{2,6},{6,10},{... | collective-permute-start | bytes 3145736 | tf_op jit(solution)/shard_map/ppermute | solution.py:39
  43.5 28.9 %collective-permute-start.11 = (f32[4,512,128]{2,1,0:T(8,128)S(1)}, f32[4,512,128]{2,1,0:T(8,128)S(1)}, u32[]{:S(2)}, u32[]{:S(2)}) collective-permute-start(f32[4,512,128]{2,1,0:T(8,128)S(1)} %all-to-all-done.refs_4_.refs_5_), channel_id=1, source_target_pairs={{0,12},{4,0},{8,4},{12,8},{1,13},{5,1},{9,5},{13,9},{2,14},{6,2},{... | collective-permute-start | bytes 3145736 | tf_op jit(solution)/shard_map/ppermute | solution.py:39
  46.1 5.0 %collective-permute-start.12 = (f32[1,256,128]{2,1,0:T(8,128)S(1)}, f32[1,256,128]{2,1,0:T(8,128)S(1)}, u32[]{:S(2)}, u32[]{:S(2)}) collective-permute-start(f32[1,256,128]{2,1,0:T(8,128)S(1)} %bitcast.70), channel_id=1, source_target_pairs={{0,32},{32,0},{1,33},{33,1},{2,34},{34,2},{3,35},{35,3},{4,36},{36... | collective-permute-start | bytes 393224 | tf_op jit(solution)/shard_map/ppermute | solution.py:43
  47.6 6.8 %collective-permute-start.14 = (f32[256,128]{1,0:T(8,128)S(1)}, f32[256,128]{1,0:T(8,128)S(1)}, u32[]{:S(2)}, u32[]{:S(2)}) collective-permute-start(f32[256,128]{1,0:T(8,128)S(1)} %copy-done.12), channel_id=1, source_target_pairs={{0,32},{32,0},{1,33},{33,1},{2,34},{34,2},{3,35},{35,3},{4,36},{36... | collective-permute-start | bytes 393224 | tf_op jit(solution)/shard_map/ppermute | solution.py:43
  51.1 9.2 %collective-permute-start.13 = (f32[2,256,128]{2,1,0:T(8,128)S(1)}, f32[2,256,128]{2,1,0:T(8,128)S(1)}, u32[]{:S(2)}, u32[]{:S(2)}) collective-permute-start(f32[2,256,128]{2,1,0:T(8,128)S(1)} %maximum_select_fusion.1), channel_id=1, source_target_pairs={{0,64},{64,0},{1,65},{65,1},{2,66},{66,2},{3,67},{67,3},{4,68},{68... | collective-permute-start | bytes 786440 | tf_op jit(solution)/shard_map/ppermute | solution.py:43
  54.2 8.5 %collective-permute-start.15 = (f32[8,1792]{1,0:T(8,128)S(1)}, f32[8,1792]{1,0:T(8,128)S(1)}, u32[]{:S(2)}, u32[]{:S(2)}) collective-permute-start(f32[8,1792]{1,0:T(8,128)S(1)} %get-tuple-element.157), channel_id=1, source_target_pairs={{0,16},{16,0},{1,17},{17,1},{2,18},{18,2},{3,19},{19,3},{4,20},{20... | collective-permute-start | bytes 172040 | tf_op jit(solution)/shard_map/ppermute | solution.py:43
  60.4 19.6 %collective-permute-start.18 = (f32[2,256,128]{2,1,0:T(8,128)S(1)}, f32[2,256,128]{2,1,0:T(8,128)S(1)}, u32[]{:S(2)}, u32[]{:S(2)}) collective-permute-start(f32[2,256,128]{2,1,0:T(8,128)S(1)} %pad_maximum_fusion.4), channel_id=1, source_target_pairs={{0,12},{4,0},{8,4},{12,8},{1,13},{5,1},{9,5},{13,9},{2,14},{6,2},{... | collective-permute-start | bytes 786440 | tf_op jit(solution)/shard_map/ppermute | solution.py:39
  62.5 12.4 %collective-permute-start.16 = (f32[2,256,128]{2,1,0:T(8,128)S(1)}, f32[2,256,128]{2,1,0:T(8,128)S(1)}, u32[]{:S(2)}, u32[]{:S(2)}) collective-permute-start(f32[2,256,128]{2,1,0:T(8,128)S(1)} %pad_maximum_fusion.2), channel_id=1, source_target_pairs={{0,4},{4,8},{8,12},{12,0},{1,5},{5,9},{9,13},{13,1},{2,6},{6,10},{... | collective-permute-start | bytes 786440 | tf_op jit(solution)/shard_map/ppermute | solution.py:39
  62.7 17.3 %collective-permute-start.17 = (f32[2,256,128]{2,1,0:T(8,128)S(1)}, f32[2,256,128]{2,1,0:T(8,128)S(1)}, u32[]{:S(2)}, u32[]{:S(2)}) collective-permute-start(f32[2,256,128]{2,1,0:T(8,128)S(1)} %pad_maximum_fusion.3), channel_id=1, source_target_pairs={{0,8},{4,12},{8,0},{12,4},{1,9},{5,13},{9,1},{13,5},{2,10},{6,14},... | collective-permute-start | bytes 786440 | tf_op jit(solution)/shard_map/ppermute | solution.py:39
  81.0 84.9 %all-gather.11.cloned.1.call-start = ((), (), s32[]{:S(2)}) async-start(), calls=%async_computation.3 | async-start | bytes 2621440 | tf_op jit(solution)/shard_map/all_gather | solution.py:439
  82.1 13.9 %collective-permute-start.19 = (f32[2,512,128]{2,1,0:T(8,128)S(1)}, f32[2,512,128]{2,1,0:T(8,128)S(1)}, u32[]{:S(2)}, u32[]{:S(2)}) collective-permute-start(f32[2,512,128]{2,1,0:T(8,128)S(1)} %slice.75), channel_id=1, source_target_pairs={{0,4},{4,8},{8,12},{12,0},{1,5},{5,9},{9,13},{13,1},{2,6},{6,10},{... | collective-permute-start | bytes 1572872 | tf_op jit(solution)/shard_map/ppermute | solution.py:39
  84.4 11.6 %collective-permute-start.20 = (f32[2,512,128]{2,1,0:T(8,128)S(1)}, f32[2,512,128]{2,1,0:T(8,128)S(1)}, u32[]{:S(2)}, u32[]{:S(2)}) collective-permute-start(f32[2,512,128]{2,1,0:T(8,128)S(1)} %slice.76), channel_id=1, source_target_pairs={{0,12},{4,0},{8,4},{12,8},{1,13},{5,1},{9,5},{13,9},{2,14},{6,2},{... | collective-permute-start | bytes 1572872 | tf_op jit(solution)/shard_map/ppermute | solution.py:39
  86.5 6.2 %collective-permute-start.21 = (f32[16,2048]{1,0:T(8,128)S(1)}, f32[16,2048]{1,0:T(8,128)S(1)}, u32[]{:S(2)}, u32[]{:S(2)}) collective-permute-start(f32[16,2048]{1,0:T(8,128)S(1)} %copy-done), channel_id=1, source_target_pairs={{0,1},{1,2},{2,3},{3,0},{4,5},{5,6},{6,7},{7,4},{8,9},{9,10},{10,1... | collective-permute-start | bytes 393224 | tf_op jit(solution)/shard_map/ppermute | solution.py:39
  88.1 7.2 %collective-permute-start.22 = (f32[16,2048]{1,0:T(8,128)S(1)}, f32[16,2048]{1,0:T(8,128)S(1)}, u32[]{:S(2)}, u32[]{:S(2)}) collective-permute-start(f32[16,2048]{1,0:T(8,128)S(1)} %copy-done), channel_id=1, source_target_pairs={{0,2},{1,3},{2,0},{3,1},{4,6},{5,7},{6,4},{7,5},{8,10},{9,11},{10,... | collective-permute-start | bytes 393224 | tf_op jit(solution)/shard_map/ppermute | solution.py:39
  91.0 5.0 %collective-permute-start.23 = (f32[16,2048]{1,0:T(8,128)S(1)}, f32[16,2048]{1,0:T(8,128)S(1)}, u32[]{:S(2)}, u32[]{:S(2)}) collective-permute-start(f32[16,2048]{1,0:T(8,128)S(1)} %copy-done), channel_id=1, source_target_pairs={{0,3},{1,0},{2,1},{3,2},{4,7},{5,4},{6,5},{7,6},{8,11},{9,8},{10,9... | collective-permute-start | bytes 393224 | tf_op jit(solution)/shard_map/ppermute | solution.py:39
  103.4 6.1 %collective-permute-start.24 = (f32[16,1024]{1,0:T(8,128)S(1)}, f32[16,1024]{1,0:T(8,128)S(1)}, u32[]{:S(2)}, u32[]{:S(2)}) collective-permute-start(f32[16,1024]{1,0:T(8,128)S(1)} %get-tuple-element.91), channel_id=1, source_target_pairs={{0,3},{1,0},{2,1},{3,2},{4,7},{5,4},{6,5},{7,6},{8,11},{9,8},{10,9... | collective-permute-start | bytes 196616 | tf_op jit(solution)/shard_map/ppermute | solution.py:39
  106.0 7.1 %collective-permute-start.25 = (f32[16,1024]{1,0:T(8,128)S(1)}, f32[16,1024]{1,0:T(8,128)S(1)}, u32[]{:S(2)}, u32[]{:S(2)}) collective-permute-start(f32[16,1024]{1,0:T(8,128)S(1)} %get-tuple-element.92), channel_id=1, source_target_pairs={{0,2},{1,3},{2,0},{3,1},{4,6},{5,7},{6,4},{7,5},{8,10},{9,11},{10,... | collective-permute-start | bytes 196616 | tf_op jit(solution)/shard_map/ppermute | solution.py:39
  106.5 7.5 %collective-permute-start.26 = (f32[16,1024]{1,0:T(8,128)S(1)}, f32[16,1024]{1,0:T(8,128)S(1)}, u32[]{:S(2)}, u32[]{:S(2)}) collective-permute-start(f32[16,1024]{1,0:T(8,128)S(1)} %get-tuple-element.93), channel_id=1, source_target_pairs={{0,1},{1,2},{2,3},{3,0},{4,5},{5,6},{6,7},{7,4},{8,9},{9,10},{10,1... | collective-permute-start | bytes 196616 | tf_op jit(solution)/shard_map/ppermute | solution.py:39
  116.2 8.1 %collective-permute-start.31 = (f32[4,6,256,128]{3,2,1,0:T(8,128)}, f32[4,6,256,128]{3,2,1,0:T(8,128)S(1)}, u32[]{:S(2)}, u32[]{:S(2)}) collective-permute-start(f32[4,6,256,128]{3,2,1,0:T(8,128)} %bitcast.56), channel_id=1, source_target_pairs={{0,16},{16,0},{1,17},{17,1},{2,18},{18,2},{3,19},{19,3},{4,20},{20... | collective-permute-start | bytes 9437192 | tf_op jit(solution)/shard_map/ppermute | solution.py:43
  116.4 5.8 %collective-permute-start.28 = (f32[8,2048]{1,0:T(8,128)S(1)}, f32[8,2048]{1,0:T(8,128)S(1)}, u32[]{:S(2)}, u32[]{:S(2)}) collective-permute-start(f32[8,2048]{1,0:T(8,128)S(1)} %get-tuple-element.97.refs_0_), channel_id=1, source_target_pairs={{0,4},{4,8},{8,12},{12,0},{1,5},{5,9},{9,13},{13,1},{2,6},{6,10},{... | collective-permute-start | bytes 196616 | tf_op jit(solution)/shard_map/ppermute | solution.py:39
  116.6 7.1 %collective-permute-start.29 = (f32[8,2048]{1,0:T(8,128)S(1)}, f32[8,2048]{1,0:T(8,128)S(1)}, u32[]{:S(2)}, u32[]{:S(2)}) collective-permute-start(f32[8,2048]{1,0:T(8,128)S(1)} %get-tuple-element.97.refs_0_), channel_id=1, source_target_pairs={{0,8},{4,12},{8,0},{12,4},{1,9},{5,13},{9,1},{13,5},{2,10},{6,14},... | collective-permute-start | bytes 196616 | tf_op jit(solution)/shard_map/ppermute | solution.py:39
  120.0 4.3 %collective-permute-start.30 = (f32[8,2048]{1,0:T(8,128)S(1)}, f32[8,2048]{1,0:T(8,128)S(1)}, u32[]{:S(2)}, u32[]{:S(2)}) collective-permute-start(f32[8,2048]{1,0:T(8,128)S(1)} %get-tuple-element.97.refs_0_), channel_id=1, source_target_pairs={{0,12},{4,0},{8,4},{12,8},{1,13},{5,1},{9,5},{13,9},{2,14},{6,2},{... | collective-permute-start | bytes 196616 | tf_op jit(solution)/shard_map/ppermute | solution.py:39
  131.0 4.3 %collective-permute-start.32 = (f32[16,1024]{1,0:T(8,128)S(1)}, f32[16,1024]{1,0:T(8,128)S(1)}, u32[]{:S(2)}, u32[]{:S(2)}) collective-permute-start(f32[16,1024]{1,0:T(8,128)S(1)} %get-tuple-element.104), channel_id=1, source_target_pairs={{0,32},{32,0},{1,33},{33,1},{2,34},{34,2},{3,35},{35,3},{4,36},{36... | collective-permute-start | bytes 196616 | tf_op jit(solution)/shard_map/ppermute | solution.py:43
  135.4 15.2 %collective-permute-start.37 = (f32[4,6,256,128]{3,2,1,0:T(8,128)}, f32[4,6,256,128]{3,2,1,0:T(8,128)}, u32[]{:S(2)}, u32[]{:S(2)}) collective-permute-start(f32[4,6,256,128]{3,2,1,0:T(8,128)} %bitcast.59), channel_id=1, source_target_pairs={{0,16},{16,0},{1,17},{17,1},{2,18},{18,2},{3,19},{19,3},{4,20},{20... | collective-permute-start | bytes 9437192 | tf_op jit(solution)/shard_map/ppermute | solution.py:43
  135.4 4.6 %collective-permute-start.33 = (f32[2,4,2048]{2,1,0:T(4,128)S(1)}, f32[2,4,2048]{2,1,0:T(4,128)S(1)}, u32[]{:S(2)}, u32[]{:S(2)}) collective-permute-start(f32[2,4,2048]{2,1,0:T(4,128)S(1)} %get-tuple-element.106), channel_id=1, source_target_pairs={{0,32},{32,0},{1,33},{33,1},{2,34},{34,2},{3,35},{35,3},{4,36},{36... | collective-permute-start | bytes 196616 | tf_op jit(solution)/shard_map/ppermute | solution.py:43
  140.7 7.2 %collective-permute-start.34 = (f32[16,2048]{1,0:T(8,128)S(1)}, f32[16,2048]{1,0:T(8,128)S(1)}, u32[]{:S(2)}, u32[]{:S(2)}) collective-permute-start(f32[16,2048]{1,0:T(8,128)S(1)} %get-tuple-element.107.refs_0_), channel_id=1, source_target_pairs={{0,4},{4,8},{8,12},{12,0},{1,5},{5,9},{9,13},{13,1},{2,6},{6,10},{... | collective-permute-start | bytes 393224 | tf_op jit(solution)/shard_map/ppermute | solution.py:39
  141.3 9.2 %collective-permute-start.35 = (f32[16,2048]{1,0:T(8,128)S(1)}, f32[16,2048]{1,0:T(8,128)S(1)}, u32[]{:S(2)}, u32[]{:S(2)}) collective-permute-start(f32[16,2048]{1,0:T(8,128)S(1)} %get-tuple-element.107.refs_0_), channel_id=1, source_target_pairs={{0,8},{4,12},{8,0},{12,4},{1,9},{5,13},{9,1},{13,5},{2,10},{6,14},... | collective-permute-start | bytes 393224 | tf_op jit(solution)/shard_map/ppermute | solution.py:39
  144.6 6.0 %collective-permute-start.36 = (f32[16,2048]{1,0:T(8,128)S(1)}, f32[16,2048]{1,0:T(8,128)S(1)}, u32[]{:S(2)}, u32[]{:S(2)}) collective-permute-start(f32[16,2048]{1,0:T(8,128)S(1)} %get-tuple-element.107.refs_0_), channel_id=1, source_target_pairs={{0,12},{4,0},{8,4},{12,8},{1,13},{5,1},{9,5},{13,9},{2,14},{6,2},{... | collective-permute-start | bytes 393224 | tf_op jit(solution)/shard_map/ppermute | solution.py:39
  144.9 13.5 %collective-permute-start.39 = (f32[8,2048]{1,0:T(8,128)S(1)}, f32[8,2048]{1,0:T(8,128)S(1)}, u32[]{:S(2)}, u32[]{:S(2)}) collective-permute-start(f32[8,2048]{1,0:T(8,128)S(1)} %get-tuple-element.113), channel_id=1, source_target_pairs={{0,64},{64,0},{1,65},{65,1},{2,66},{66,2},{3,67},{67,3},{4,68},{68... | collective-permute-start | bytes 196616 | tf_op jit(solution)/shard_map/ppermute | solution.py:43
  155.3 5.5 %collective-permute-start.38 = (f32[8,1024]{1,0:T(8,128)S(1)}, f32[8,1024]{1,0:T(8,128)S(1)}, u32[]{:S(2)}, u32[]{:S(2)}) collective-permute-start(f32[8,1024]{1,0:T(8,128)S(1)} %get-tuple-element.111), channel_id=1, source_target_pairs={{0,64},{64,0},{1,65},{65,1},{2,66},{66,2},{3,67},{67,3},{4,68},{68... | collective-permute-start | bytes 98312 | tf_op jit(solution)/shard_map/ppermute | solution.py:43
  165.8 8.7 %collective-permute-start.43 = (f32[4,4,256,128]{3,2,1,0:T(8,128)}, f32[4,4,256,128]{3,2,1,0:T(8,128)S(1)}, u32[]{:S(2)}, u32[]{:S(2)}) collective-permute-start(f32[4,4,256,128]{3,2,1,0:T(8,128)} %bitcast.62), channel_id=1, source_target_pairs={{0,16},{16,0},{1,17},{17,1},{2,18},{18,2},{3,19},{19,3},{4,20},{20... | collective-permute-start | bytes 6291464 | tf_op jit(solution)/shard_map/ppermute | solution.py:43
  165.8 5.8 %collective-permute-start.40 = (f32[8,2048]{1,0:T(8,128)S(1)}, f32[8,2048]{1,0:T(8,128)S(1)}, u32[]{:S(2)}, u32[]{:S(2)}) collective-permute-start(f32[8,2048]{1,0:T(8,128)S(1)} %s23.1.c0), channel_id=1, source_target_pairs={{0,4},{4,8},{8,12},{12,0},{1,5},{5,9},{9,13},{13,1},{2,6},{6,10},{... | collective-permute-start | bytes 196616 | tf_op jit(solution)/shard_map/ppermute | solution.py:39
  167.4 6.7 %collective-permute-start.41 = (f32[8,2048]{1,0:T(8,128)S(1)}, f32[8,2048]{1,0:T(8,128)S(1)}, u32[]{:S(2)}, u32[]{:S(2)}) collective-permute-start(f32[8,2048]{1,0:T(8,128)S(1)} %s23.1.c0), channel_id=1, source_target_pairs={{0,8},{4,12},{8,0},{12,4},{1,9},{5,13},{9,1},{13,5},{2,10},{6,14},... | collective-permute-start | bytes 196616 | tf_op jit(solution)/shard_map/ppermute | solution.py:39
  170.3 4.3 %collective-permute-start.42 = (f32[8,2048]{1,0:T(8,128)S(1)}, f32[8,2048]{1,0:T(8,128)S(1)}, u32[]{:S(2)}, u32[]{:S(2)}) collective-permute-start(f32[8,2048]{1,0:T(8,128)S(1)} %s23.1.c0), channel_id=1, source_target_pairs={{0,12},{4,0},{8,4},{12,8},{1,13},{5,1},{9,5},{13,9},{2,14},{6,2},{... | collective-permute-start | bytes 196616 | tf_op jit(solution)/shard_map/ppermute | solution.py:39
  180.5 5.6 %collective-permute-start.44 = (f32[8,2048]{1,0:T(8,128)S(1)}, f32[8,2048]{1,0:T(8,128)S(1)}, u32[]{:S(2)}, u32[]{:S(2)}) collective-permute-start(f32[8,2048]{1,0:T(8,128)S(1)} %top.1.c0), channel_id=1, source_target_pairs={{0,4},{4,8},{8,12},{12,0},{1,5},{5,9},{9,13},{13,1},{2,6},{6,10},{... | collective-permute-start | bytes 196616 | tf_op jit(solution)/shard_map/ppermute | solution.py:39
  181.4 6.1 %collective-permute-start.45 = (f32[8,2048]{1,0:T(8,128)S(1)}, f32[8,2048]{1,0:T(8,128)S(1)}, u32[]{:S(2)}, u32[]{:S(2)}) collective-permute-start(f32[8,2048]{1,0:T(8,128)S(1)} %top.1.c0), channel_id=1, source_target_pairs={{0,8},{4,12},{8,0},{12,4},{1,9},{5,13},{9,1},{13,5},{2,10},{6,14},... | collective-permute-start | bytes 196616 | tf_op jit(solution)/shard_map/ppermute | solution.py:39
  189.5 5.8 %collective-permute-start.47 = (f32[8,2048]{1,0:T(8,128)S(1)}, f32[8,2048]{1,0:T(8,128)S(1)}, u32[]{:S(2)}, u32[]{:S(2)}) collective-permute-start(f32[8,2048]{1,0:T(8,128)S(1)} %x3.1), channel_id=1, source_target_pairs={{0,64},{64,0},{1,65},{65,1},{2,66},{66,2},{3,67},{67,3},{4,68},{68... | collective-permute-start | bytes 196616 | tf_op jit(solution)/shard_map/ppermute | solution.py:43
  200.1 6.2 %collective-permute-start.48 = (f32[16,2048]{1,0:T(8,128)S(1)}, f32[16,2048]{1,0:T(8,128)S(1)}, u32[]{:S(2)}, u32[]{:S(2)}) collective-permute-start(f32[16,2048]{1,0:T(8,128)S(1)} %b2.1.c0), channel_id=1, source_target_pairs={{0,4},{4,8},{8,12},{12,0},{1,5},{5,9},{9,13},{13,1},{2,6},{6,10},{... | collective-permute-start | bytes 393224 | tf_op jit(solution)/shard_map/ppermute | solution.py:39
  200.4 7.5 %collective-permute-start.49 = (f32[16,2048]{1,0:T(8,128)S(1)}, f32[16,2048]{1,0:T(8,128)S(1)}, u32[]{:S(2)}, u32[]{:S(2)}) collective-permute-start(f32[16,2048]{1,0:T(8,128)S(1)} %b2.1.c0), channel_id=1, source_target_pairs={{0,8},{4,12},{8,0},{12,4},{1,9},{5,13},{9,1},{13,5},{2,10},{6,14},... | collective-permute-start | bytes 393224 | tf_op jit(solution)/shard_map/ppermute | solution.py:39
  203.6 5.0 %collective-permute-start.50 = (f32[16,2048]{1,0:T(8,128)S(1)}, f32[16,2048]{1,0:T(8,128)S(1)}, u32[]{:S(2)}, u32[]{:S(2)}) collective-permute-start(f32[16,2048]{1,0:T(8,128)S(1)} %b2.1.c0), channel_id=1, source_target_pairs={{0,12},{4,0},{8,4},{12,8},{1,13},{5,1},{9,5},{13,9},{2,14},{6,2},{... | collective-permute-start | bytes 393224 | tf_op jit(solution)/shard_map/ppermute | solution.py:39
  209.2 4.3 %collective-permute-start.51 = (f32[16,1024]{1,0:T(8,128)S(1)}, f32[16,1024]{1,0:T(8,128)S(1)}, u32[]{:S(2)}, u32[]{:S(2)}) collective-permute-start(f32[16,1024]{1,0:T(8,128)S(1)} %get-tuple-element.118), channel_id=1, source_target_pairs={{0,32},{32,0},{1,33},{33,1},{2,34},{34,2},{3,35},{35,3},{4,36},{36... | collective-permute-start | bytes 196616 | tf_op jit(solution)/shard_map/ppermute | solution.py:43
  210.8 11.4 %collective-permute-start.55 = (f32[2,4,2048]{2,1,0:T(4,128)S(1)}, f32[2,4,2048]{2,1,0:T(4,128)S(1)}, u32[]{:S(2)}, u32[]{:S(2)}) collective-permute-start(f32[2,4,2048]{2,1,0:T(4,128)S(1)} %slice.83.a_mine), channel_id=1, source_target_pairs={{0,32},{32,0},{1,33},{33,1},{2,34},{34,2},{3,35},{35,3},{4,36},{36... | collective-permute-start | bytes 196616 | tf_op jit(solution)/shard_map/ppermute | solution.py:43
  218.5 5.3 %collective-permute-start.52 = (f32[8,2048]{1,0:T(8,128)S(1)}, f32[8,2048]{1,0:T(8,128)S(1)}, u32[]{:S(2)}, u32[]{:S(2)}) collective-permute-start(f32[8,2048]{1,0:T(8,128)S(1)} %get-tuple-element.121), channel_id=1, source_target_pairs={{0,12},{4,0},{8,4},{12,8},{1,13},{5,1},{9,5},{13,9},{2,14},{6,2},{... | collective-permute-start | bytes 196616 | tf_op jit(solution)/shard_map/ppermute | solution.py:39
  221.2 5.8 %collective-permute-start.53 = (f32[8,2048]{1,0:T(8,128)S(1)}, f32[8,2048]{1,0:T(8,128)S(1)}, u32[]{:S(2)}, u32[]{:S(2)}) collective-permute-start(f32[8,2048]{1,0:T(8,128)S(1)} %get-tuple-element.122), channel_id=1, source_target_pairs={{0,8},{4,12},{8,0},{12,4},{1,9},{5,13},{9,1},{13,5},{2,10},{6,14},... | collective-permute-start | bytes 196616 | tf_op jit(solution)/shard_map/ppermute | solution.py:39
  221.5 6.2 %collective-permute-start.54 = (f32[8,2048]{1,0:T(8,128)S(1)}, f32[8,2048]{1,0:T(8,128)S(1)}, u32[]{:S(2)}, u32[]{:S(2)}) collective-permute-start(f32[8,2048]{1,0:T(8,128)S(1)} %get-tuple-element.123), channel_id=1, source_target_pairs={{0,4},{4,8},{8,12},{12,0},{1,5},{5,9},{9,13},{13,1},{2,6},{6,10},{... | collective-permute-start | bytes 196616 | tf_op jit(solution)/shard_map/ppermute | solution.py:39
  228.5 17.7 %collective-permute-start.64 = (f32[8,512]{1,0:T(8,128)S(1)}, f32[8,512]{1,0:T(8,128)S(1)}, u32[]{:S(2)}, u32[]{:S(2)}) collective-permute-start(f32[8,512]{1,0:T(8,128)S(1)} %get-tuple-element.162), channel_id=1, source_target_pairs={{0,16},{16,0},{1,17},{17,1},{2,18},{18,2},{3,19},{19,3},{4,20},{20... | collective-permute-start | bytes 49160 | tf_op jit(solution)/shard_map/ppermute | solution.py:43
  229.1 17.7 %collective-permute-start.63 = (f32[8,1024]{1,0:T(8,128)S(1)}, f32[8,1024]{1,0:T(8,128)S(1)}, u32[]{:S(2)}, u32[]{:S(2)}) collective-permute-start(f32[8,1024]{1,0:T(8,128)S(1)} %get-tuple-element.164), channel_id=1, source_target_pairs={{0,16},{16,0},{1,17},{17,1},{2,18},{18,2},{3,19},{19,3},{4,20},{20... | collective-permute-start | bytes 98312 | tf_op jit(solution)/shard_map/ppermute | solution.py:43
  230.2 6.8 %collective-permute-start.57 = (f32[16,1024]{1,0:T(8,128)S(1)}, f32[16,1024]{1,0:T(8,128)S(1)}, u32[]{:S(2)}, u32[]{:S(2)}) collective-permute-start(f32[16,1024]{1,0:T(8,128)S(1)} %maximum_select_fusion.3.refs_0_), channel_id=1, source_target_pairs={{0,1},{1,2},{2,3},{3,0},{4,5},{5,6},{6,7},{7,4},{8,9},{9,10},{10,1... | collective-permute-start | bytes 196616 | tf_op jit(solution)/shard_map/ppermute | solution.py:39
  230.8 6.2 %collective-permute-start.58 = (f32[16,1024]{1,0:T(8,128)S(1)}, f32[16,1024]{1,0:T(8,128)S(1)}, u32[]{:S(2)}, u32[]{:S(2)}) collective-permute-start(f32[16,1024]{1,0:T(8,128)S(1)} %maximum_select_fusion.3.refs_0_), channel_id=1, source_target_pairs={{0,2},{1,3},{2,0},{3,1},{4,6},{5,7},{6,4},{7,5},{8,10},{9,11},{10,... | collective-permute-start | bytes 196616 | tf_op jit(solution)/shard_map/ppermute | solution.py:39
  232.5 5.0 %collective-permute-start.59 = (f32[16,1024]{1,0:T(8,128)S(1)}, f32[16,1024]{1,0:T(8,128)S(1)}, u32[]{:S(2)}, u32[]{:S(2)}) collective-permute-start(f32[16,1024]{1,0:T(8,128)S(1)} %maximum_select_fusion.3.refs_0_), channel_id=1, source_target_pairs={{0,3},{1,0},{2,1},{3,2},{4,7},{5,4},{6,5},{7,6},{8,11},{9,8},{10,9... | collective-permute-start | bytes 196616 | tf_op jit(solution)/shard_map/ppermute | solution.py:39
  242.5 7.5 %collective-permute-start.60 = (f32[16,2048]{1,0:T(8,128)S(1)}, f32[16,2048]{1,0:T(8,128)S(1)}, u32[]{:S(2)}, u32[]{:S(2)}) collective-permute-start(f32[16,2048]{1,0:T(8,128)S(1)} %get-tuple-element.128), channel_id=1, source_target_pairs={{0,3},{1,0},{2,1},{3,2},{4,7},{5,4},{6,5},{7,6},{8,11},{9,8},{10,9... | collective-permute-start | bytes 393224 | tf_op jit(solution)/shard_map/ppermute | solution.py:39
  245.2 7.1 %collective-permute-start.61 = (f32[16,2048]{1,0:T(8,128)S(1)}, f32[16,2048]{1,0:T(8,128)S(1)}, u32[]{:S(2)}, u32[]{:S(2)}) collective-permute-start(f32[16,2048]{1,0:T(8,128)S(1)} %get-tuple-element.129), channel_id=1, source_target_pairs={{0,2},{1,3},{2,0},{3,1},{4,6},{5,7},{6,4},{7,5},{8,10},{9,11},{10,... | collective-permute-start | bytes 393224 | tf_op jit(solution)/shard_map/ppermute | solution.py:39
  245.8 7.9 %collective-permute-start.62 = (f32[16,2048]{1,0:T(8,128)S(1)}, f32[16,2048]{1,0:T(8,128)S(1)}, u32[]{:S(2)}, u32[]{:S(2)}) collective-permute-start(f32[16,2048]{1,0:T(8,128)S(1)} %get-tuple-element.130), channel_id=1, source_target_pairs={{0,1},{1,2},{2,3},{3,0},{4,5},{5,6},{6,7},{7,4},{8,9},{9,10},{10,1... | collective-permute-start | bytes 393224 | tf_op jit(solution)/shard_map/ppermute | solution.py:39
  (26 other events, 279.0 us)
Sparse Core Ops, SparseCore 0:
  42.3 41.5 all-gather.6
  85.6 42.5 all-gather.8
  135.5 30.2 all-gather.10

commit v13 on v12

--- a/solution.py
+++ b/solution.py
@@ -496,17 +496,17 @@
     m1, _ = gate((m1, c1))
     w1 = m1, flip(m1, "core")
     pr = flip(pg, "x0")
+    m2, pr, c1 = gate((m2, pr, gather4(c1, "z")))
+    w2 = m2, flip(m2, "core")
     y1, keep, give = call(
         functools.partial(forward_kernel, 1, 32, "ar"), "f1", [(32, 512), (16, 1024), (16, 1024)],
-        [ev, fv, *work(32), dma((12,))], meta, gather4(c1, "z"), w1, flops(32),
+        [ev, fv, *work(32), dma((12,))], meta, c1, w1, flops(32),
     )
     recv = flip(give, "x0")
     part, keep3, give3 = call(
         s12_kernel, "s12", [(16, ORDER), (8, ORDER), (8, ORDER)],
         [pltpu.VMEM((2, 16, ORDER), f32)], meta, [keep, recv, pk, pr],
     )
-    m2, _ = gate((m2, recv))
-    w2 = m2, flip(m2, "core")
     recv3 = flip(give3, "x1")
     y2, keep, give = call(
         functools.partial(forward_kernel, 2, 16, "ar"), "f2", [(16, 512), (8, 1024), (8, 1024)],

time: 261 us -> 256 us (0.981)
  waiting for transfers between devices: 95.1 us -> 89.4 us
    ppermute x44, starting transfers between devices: 64.1 us -> 66.8 us  [shift(): return lax.ppermute(v, axis, [(i, (i + s) % 4) for i in range(4)])]
    unnamed x51 -> x45, local copies, waits for them, and re-layouts: 10.1 us -> 8.31 us
  transfers between devices with their start and end apart: 70 -> 70, of which waited for: 45 -> 43; matrix products, arithmetic and copies ran while one was open for 4% -> 5% of each run, Pallas kernels for 10% -> 11%
where the time goes in v13:
time: 256 us
  starting transfers between devices  94.8 us (37%)
  waiting for transfers between devices  89.4 us (35%)
  Pallas kernels  38.5 us (15%)
  local copies, waits for them, and re-layouts  15 us (6%)
  between operations  14.4 us (6%)
  other arithmetic  3.89 us (2%)
    ppermute x44, starting transfers between devices, shift(): return lax.ppermute(v, axis, [(i, (i + s) % 4) for i in range(4)])  66.8 us
    ppermute x44, waiting for transfers between devices, shift(): return lax.ppermute(v, axis, [(i, (i + s) % 4) for i in range(4)])  65 us
    pallas_call x13, Pallas kernels, call(): pl.pallas_call(kernel, out_shape=[jax.ShapeDtypeStruct(s, f32) for s in s...  38.5 us
    ppermute x22, starting transfers between devices, flip(): return lax.ppermute(v, axis, [(0, 1), (1, 0)])  23.5 us
    ppermute x22, waiting for transfers between devices, flip(): return lax.ppermute(v, axis, [(0, 1), (1, 0)])  20.7 us
    unnamed x45, local copies, waits for them, and re-layouts  8.31 us
  transfers between devices with their start and end apart: 70, of which 43 were waited for; matrix products, arithmetic and copies ran while one was open for 5% of the time, Pallas kernels for 11%

profile of v13, /device:TPU:0, one launch (start us, length us, event | category | flops | bytes accessed | tf_op | source)
XLA Modules:
  0.0 255.9 jit_solution(18015922309012582978)
XLA Ops:
  7.2 2.1 collective-permute-start.6
  9.3 2.2 collective-permute-start.7
  11.5 2.3 copy.22
  13.8 4.5 %all-to-all-start = ((f32[4,512,128]{2,1,0:T(8,128)}), f32[4,512,128]{2,1,0:T(8,128)S(1)}, u32[]{:S(2)}, u32[]{:S(2)}) async-start(f32[4,512,128]{2,1,0:T(8,128)} %bitcast.3), calls=%async_computation | async-start | bytes 2097152 | tf_op jit(solution)/shard_map/all_to_all | solution.py:446
  20.1 1.6 collective-permute-start.5
  21.8 1.8 collective-permute-done.6.refs_10_.refs_11_
  25.7 3.3 %collective-permute-start.9 = (f32[2,256,128]{2,1,0:T(8,128)S(1)}, f32[2,256,128]{2,1,0:T(8,128)}, u32[]{:S(2)}, u32[]{:S(2)}) collective-permute-start(f32[2,256,128]{2,1,0:T(8,128)S(1)} %slice.88), channel_id=1, source_target_pairs={{0,12},{4,0},{8,4},{12,8},{1,13},{5,1},{9,5},{13,9},{2,14},{6,2},{... | collective-permute-start | bytes 786440 | tf_op jit(solution)/shard_map/ppermute | solution.py:39
  30.4 6.6 %collective-permute-done.2 = f32[256,128]{1,0:T(8,128)S(1)} collective-permute-done((f32[256,128]{1,0:T(8,128)S(1)}, f32[256,128]{1,0:T(8,128)S(1)}, u32[]{:S(2)}, u32[]{:S(2)}) %collective-permute-start.2) | collective-permute-done | bytes 131104 | tf_op jit(solution)/shard_map/ppermute | solution.py:39
  37.0 2.3 collective-permute-done.3
  43.5 2.6 %collective-permute-start.11 = (f32[4,512,128]{2,1,0:T(8,128)S(1)}, f32[4,512,128]{2,1,0:T(8,128)S(1)}, u32[]{:S(2)}, u32[]{:S(2)}) collective-permute-start(f32[4,512,128]{2,1,0:T(8,128)S(1)} %all-to-all-done.refs_4_.refs_5_), channel_id=1, source_target_pairs={{0,12},{4,0},{8,4},{12,8},{1,13},{5,1},{9,5},{13,9},{2,14},{6,2},{... | collective-permute-start | bytes 3145736 | tf_op jit(solution)/shard_map/ppermute | solution.py:39
  46.1 1.5 collective-permute-start.14
  49.8 2.8 %collective-permute-done.12 = f32[1,256,128]{2,1,0:T(8,128)S(1)} collective-permute-done((f32[1,256,128]{2,1,0:T(8,128)S(1)}, f32[1,256,128]{2,1,0:T(8,128)S(1)}, u32[]{:S(2)}, u32[]{:S(2)}) %collective-permute-start.12) | collective-permute-done | bytes 131104 | tf_op jit(solution)/shard_map/ppermute | solution.py:43
  52.6 3.0 %collective-permute-start.13 = (f32[2,256,128]{2,1,0:T(8,128)S(1)}, f32[2,256,128]{2,1,0:T(8,128)S(1)}, u32[]{:S(2)}, u32[]{:S(2)}) collective-permute-start(f32[2,256,128]{2,1,0:T(8,128)S(1)} %maximum_select_fusion.1), channel_id=1, source_target_pairs={{0,64},{64,0},{1,65},{65,1},{2,66},{66,2},{3,67},{67,3},{4,68},{68... | collective-permute-start | bytes 786440 | tf_op jit(solution)/shard_map/ppermute | solution.py:43
  55.8 4.7 %collective-permute-done.13 = f32[2,256,128]{2,1,0:T(8,128)S(1)} collective-permute-done((f32[2,256,128]{2,1,0:T(8,128)S(1)}, f32[2,256,128]{2,1,0:T(8,128)S(1)}, u32[]{:S(2)}, u32[]{:S(2)}) %collective-permute-start.13) | collective-permute-done | bytes 262176 | tf_op jit(solution)/shard_map/ppermute | solution.py:43
  60.8 3.5 %collective-permute-start.17 = (f32[2,256,128]{2,1,0:T(8,128)S(1)}, f32[2,256,128]{2,1,0:T(8,128)S(1)}, u32[]{:S(2)}, u32[]{:S(2)}) collective-permute-start(f32[2,256,128]{2,1,0:T(8,128)S(1)} %pad_maximum_fusion.3), channel_id=1, source_target_pairs={{0,8},{4,12},{8,0},{12,4},{1,9},{5,13},{9,1},{13,5},{2,10},{6,14},... | collective-permute-start | bytes 786440 | tf_op jit(solution)/shard_map/ppermute | solution.py:39
  65.0 5.1 %collective-permute-done.10.refs_5_.refs_6_ = f32[4,512,128]{2,1,0:T(8,128)S(1)} collective-permute-done((f32[4,512,128]{2,1,0:T(8,128)S(1)}, f32[4,512,128]{2,1,0:T(8,128)S(1)}, u32[]{:S(2)}, u32[]{:S(2)}) %collective-permute-start.10) | collective-permute-done | bytes 1048608 | tf_op jit(solution)/shard_map/ppermute | solution.py:39
  70.1 5.2 %collective-permute-done.11.refs_6_.refs_7_ = f32[4,512,128]{2,1,0:T(8,128)S(1)} collective-permute-done((f32[4,512,128]{2,1,0:T(8,128)S(1)}, f32[4,512,128]{2,1,0:T(8,128)S(1)}, u32[]{:S(2)}, u32[]{:S(2)}) %collective-permute-start.11) | collective-permute-done | bytes 1048608 | tf_op jit(solution)/shard_map/ppermute | solution.py:39
  75.4 4.6 %collective-permute-done.17 = f32[2,256,128]{2,1,0:T(8,128)S(1)} collective-permute-done((f32[2,256,128]{2,1,0:T(8,128)S(1)}, f32[2,256,128]{2,1,0:T(8,128)S(1)}, u32[]{:S(2)}, u32[]{:S(2)}) %collective-permute-start.17) | collective-permute-done | bytes 262176 | tf_op jit(solution)/shard_map/ppermute | solution.py:39
  83.2 3.3 %collective-permute-start.20 = (f32[2,512,128]{2,1,0:T(8,128)S(1)}, f32[2,512,128]{2,1,0:T(8,128)S(1)}, u32[]{:S(2)}, u32[]{:S(2)}) collective-permute-start(f32[2,512,128]{2,1,0:T(8,128)S(1)} %slice.80), channel_id=1, source_target_pairs={{0,12},{4,0},{8,4},{12,8},{1,13},{5,1},{9,5},{13,9},{2,14},{6,2},{... | collective-permute-start | bytes 1572872 | tf_op jit(solution)/shard_map/ppermute | solution.py:39
  86.5 1.6 collective-permute-start.21
  88.1 2.9 %collective-permute-start.22 = (f32[16,2048]{1,0:T(8,128)S(1)}, f32[16,2048]{1,0:T(8,128)S(1)}, u32[]{:S(2)}, u32[]{:S(2)}) collective-permute-start(f32[16,2048]{1,0:T(8,128)S(1)} %copy-done), channel_id=1, source_target_pairs={{0,2},{1,3},{2,0},{3,1},{4,6},{5,7},{6,4},{7,5},{8,10},{9,11},{10,... | collective-permute-start | bytes 393224 | tf_op jit(solution)/shard_map/ppermute | solution.py:39
  92.7 2.6 %collective-permute-done.22.refs_2_ = f32[16,2048]{1,0:T(8,128)S(1)} collective-permute-done((f32[16,2048]{1,0:T(8,128)S(1)}, f32[16,2048]{1,0:T(8,128)S(1)}, u32[]{:S(2)}, u32[]{:S(2)}) %collective-permute-start.22) | collective-permute-done | bytes 131104 | tf_op jit(solution)/shard_map/ppermute | solution.py:39
  97.6 5.7 %f0.1 = (f32[64,512]{1,0:T(8,128)S(1)}, f32[16,1024]{1,0:T(8,128)S(1)}, f32[16,1024]{1,0:T(8,128)S(1)}, f32[16,1024]{1,0:T(8,128)S(1)}, f32[16,1024]{1,0:T(8,128)S(1)}) custom-call(s32[128]{0:T(128)S(1)} %pad_add_fusion.meta, f32[16,2048]{1,0:T(8,128)S(1)} %copy-done, f32[16,2048]{1,0:T(8,128)S(1)} %collective-permute-done.21.refs_1_, ...), custom_call_target="tpu_custom_call" | custom-call | flops 2415919104 | bytes 6815744 | tf_op jit(solution)/shard_map/f0/pallas_call | solution.py:395
  103.3 2.6 %collective-permute-start.24 = (f32[16,1024]{1,0:T(8,128)S(1)}, f32[16,1024]{1,0:T(8,128)S(1)}, u32[]{:S(2)}, u32[]{:S(2)}) collective-permute-start(f32[16,1024]{1,0:T(8,128)S(1)} %get-tuple-element.97), channel_id=1, source_target_pairs={{0,3},{1,0},{2,1},{3,2},{4,7},{5,4},{6,5},{7,6},{8,11},{9,8},{10,9... | collective-permute-start | bytes 196616 | tf_op jit(solution)/shard_map/ppermute | solution.py:39
  107.9 1.5 collective-permute-done.24
  109.4 3.7 %collective-permute-done.25 = f32[16,1024]{1,0:T(8,128)S(1)} collective-permute-done((f32[16,1024]{1,0:T(8,128)S(1)}, f32[16,1024]{1,0:T(8,128)S(1)}, u32[]{:S(2)}, u32[]{:S(2)}) %collective-permute-start.25) | collective-permute-done | bytes 65568 | tf_op jit(solution)/shard_map/ppermute | solution.py:39
  116.4 1.5 collective-permute-start.28
  117.9 3.6 %collective-permute-start.30 = (f32[8,2048]{1,0:T(8,128)S(1)}, f32[8,2048]{1,0:T(8,128)S(1)}, u32[]{:S(2)}, u32[]{:S(2)}) collective-permute-start(f32[8,2048]{1,0:T(8,128)S(1)} %get-tuple-element.105.refs_0_), channel_id=1, source_target_pairs={{0,8},{4,12},{8,0},{12,4},{1,9},{5,13},{9,1},{13,5},{2,10},{6,14},... | collective-permute-start | bytes 196616 | tf_op jit(solution)/shard_map/ppermute | solution.py:39
  122.0 2.1 collective-permute-done.29.refs_1_
  125.8 2.4 all-gather.7.cloned.1.call-done
  128.2 4.9 %f1.1 = (f32[32,512]{1,0:T(8,128)S(1)}, f32[16,1024]{1,0:T(8,128)S(1)}, f32[16,1024]{1,0:T(8,128)S(1)}) custom-call(s32[128]{0:T(128)S(1)} %pad_add_fusion.meta, f32[8,2048]{1,0:T(8,128)S(1)} %get-tuple-element.105.refs_0_, f32[8,2048]{1,0:T(8,128)S(1)} %collective-permute-done.29.refs_1_, f32[8,2048]{1,0:T(8,128)S(1)} %collective-permute-done.30.refs_2_, ...), custom_call_target="tpu_custom_call" | custom-call | flops 1207959552 | bytes 6553600 | tf_op jit(solution)/shard_map/f1/pallas_call | solution.py:395
  133.2 1.6 collective-permute-start.33
  134.7 3.0 %collective-permute-done.33.recv = f32[16,1024]{1,0:T(8,128)S(1)} collective-permute-done((f32[16,1024]{1,0:T(8,128)S(1)}, f32[16,1024]{1,0:T(8,128)S(1)}, u32[]{:S(2)}, u32[]{:S(2)}) %collective-permute-start.33) | collective-permute-done | bytes 65568 | tf_op jit(solution)/shard_map/ppermute | solution.py:43
  138.5 1.7 collective-permute-start.34
  140.2 2.8 %collective-permute-start.35 = (f32[16,2048]{1,0:T(8,128)S(1)}, f32[16,2048]{1,0:T(8,128)S(1)}, u32[]{:S(2)}, u32[]{:S(2)}) collective-permute-start(f32[16,2048]{1,0:T(8,128)S(1)} %get-tuple-element.118.refs_0_), channel_id=1, source_target_pairs={{0,8},{4,12},{8,0},{12,4},{1,9},{5,13},{9,1},{13,5},{2,10},{6,14},... | collective-permute-start | bytes 393224 | tf_op jit(solution)/shard_map/ppermute | solution.py:39
  144.3 3.0 %collective-permute-start.39 = (f32[8,2048]{1,0:T(8,128)S(1)}, f32[8,2048]{1,0:T(8,128)S(1)}, u32[]{:S(2)}, u32[]{:S(2)}) collective-permute-start(f32[8,2048]{1,0:T(8,128)S(1)} %get-tuple-element.123), channel_id=1, source_target_pairs={{0,64},{64,0},{1,65},{65,1},{2,66},{66,2},{3,67},{67,3},{4,68},{68... | collective-permute-start | bytes 196616 | tf_op jit(solution)/shard_map/ppermute | solution.py:43
  147.3 1.5 collective-permute-done.35.refs_2_
  148.9 4.7 %f2.1 = (f32[16,512]{1,0:T(8,128)S(1)}, f32[8,1024]{1,0:T(8,128)S(1)}, f32[8,1024]{1,0:T(8,128)S(1)}) custom-call(s32[128]{0:T(128)S(1)} %pad_add_fusion.meta, f32[16,2048]{1,0:T(8,128)S(1)} %get-tuple-element.118.refs_0_, f32[16,2048]{1,0:T(8,128)S(1)} %collective-permute-done.34.refs_1_, f32[16,2048]{1,0:T(8,128)S(1)} %collective-permute-done.35.refs_2_, ...), custom_call_target="tpu_custom_call" | custom-call | flops 603979776 | bytes 6815744 | tf_op jit(solution)/shard_map/f2/pallas_call | solution.py:395
  153.6 3.1 %collective-permute-start.38 = (f32[8,1024]{1,0:T(8,128)S(1)}, f32[8,1024]{1,0:T(8,128)S(1)}, u32[]{:S(2)}, u32[]{:S(2)}) collective-permute-start(f32[8,1024]{1,0:T(8,128)S(1)} %get-tuple-element.121), channel_id=1, source_target_pairs={{0,64},{64,0},{1,65},{65,1},{2,66},{66,2},{3,67},{67,3},{4,68},{68... | collective-permute-start | bytes 98312 | tf_op jit(solution)/shard_map/ppermute | solution.py:43
  156.7 2.4 collective-permute-done.38.recv
  160.9 1.6 collective-permute-start.40
  162.5 2.9 %collective-permute-start.41 = (f32[8,2048]{1,0:T(8,128)S(1)}, f32[8,2048]{1,0:T(8,128)S(1)}, u32[]{:S(2)}, u32[]{:S(2)}) collective-permute-start(f32[8,2048]{1,0:T(8,128)S(1)} %s23.1.c0), channel_id=1, source_target_pairs={{0,8},{4,12},{8,0},{12,4},{1,9},{5,13},{9,1},{13,5},{2,10},{6,14},... | collective-permute-start | bytes 196616 | tf_op jit(solution)/shard_map/ppermute | solution.py:39
  166.7 2.5 collective-permute-done.41.c2
  170.9 4.6 %top.1.c0 = f32[8,2048]{1,0:T(8,128)S(1)} custom-call(s32[128]{0:T(128)S(1)} %pad_add_fusion.meta, f32[8,2048]{1,0:T(8,128)S(1)} %s23.1.c0, f32[8,2048]{1,0:T(8,128)S(1)} %collective-permute-done.40.c1, f32[8,2048]{1,0:T(8,128)S(1)} %collective-permute-done.41.c2, f32[8,2048]{1,0:T(8,128)S(1)} %collective-permute-done.42.c3, f32[4,4,256,128]{3,2,1,0:T(8,128)} %bitcast.63, ...), custom_call_target="tpu_custom_call" | custom-call | flops 301989888 | bytes 4456448 | tf_op jit(solution)/shard_map/top/pallas_call | solution.py:395
  176.5 3.2 %collective-permute-start.45 = (f32[8,2048]{1,0:T(8,128)S(1)}, f32[8,2048]{1,0:T(8,128)S(1)}, u32[]{:S(2)}, u32[]{:S(2)}) collective-permute-start(f32[8,2048]{1,0:T(8,128)S(1)} %top.1.c0), channel_id=1, source_target_pairs={{0,8},{4,12},{8,0},{12,4},{1,9},{5,13},{9,1},{13,5},{2,10},{6,14},... | collective-permute-start | bytes 196616 | tf_op jit(solution)/shard_map/ppermute | solution.py:39
  184.6 3.1 %collective-permute-start.47 = (f32[8,2048]{1,0:T(8,128)S(1)}, f32[8,2048]{1,0:T(8,128)S(1)}, u32[]{:S(2)}, u32[]{:S(2)}) collective-permute-start(f32[8,2048]{1,0:T(8,128)S(1)} %x3.1), channel_id=1, source_target_pairs={{0,64},{64,0},{1,65},{65,1},{2,66},{66,2},{3,67},{67,3},{4,68},{68... | collective-permute-start | bytes 196616 | tf_op jit(solution)/shard_map/ppermute | solution.py:43
  187.6 2.8 %collective-permute-done.47.x3r = f32[8,2048]{1,0:T(8,128)S(1)} collective-permute-done((f32[8,2048]{1,0:T(8,128)S(1)}, f32[8,2048]{1,0:T(8,128)S(1)}, u32[]{:S(2)}, u32[]{:S(2)}) %collective-permute-start.47) | collective-permute-done | bytes 65568 | tf_op jit(solution)/shard_map/ppermute | solution.py:43
  190.4 4.7 %b2.1.c0 = f32[16,2048]{1,0:T(8,128)S(1)} custom-call(s32[128]{0:T(128)S(1)} %pad_add_fusion.meta, f32[1,8,2048]{2,1,0:T(8,128)S(1)} %bitcast.54, f32[1,8,2048]{2,1,0:T(8,128)S(1)} %bitcast.55, f32[16,512]{1,0:T(8,128)S(1)} %get-tuple-element.126.refs_2_, f32[4,6,256,128]{3,2,1,0:T(8,128)} %bitcast.61, f32[4,6,256,128]{3,2,1,0:T(8,128)} %collective-permute-done.37.refs_5_.refs_4_), custom_call_target="tpu_custom_call" | custom-call | flops 603979776 | bytes 6455296 | tf_op jit(solution)/shard_map/b2/pallas_call | solution.py:395
  195.5 3.1 %collective-permute-start.49 = (f32[16,2048]{1,0:T(8,128)S(1)}, f32[16,2048]{1,0:T(8,128)S(1)}, u32[]{:S(2)}, u32[]{:S(2)}) collective-permute-start(f32[16,2048]{1,0:T(8,128)S(1)} %b2.1.c0), channel_id=1, source_target_pairs={{0,8},{4,12},{8,0},{12,4},{1,9},{5,13},{9,1},{13,5},{2,10},{6,14},... | collective-permute-start | bytes 393224 | tf_op jit(solution)/shard_map/ppermute | solution.py:39
  199.4 2.0 collective-permute-done.48.c1
  201.4 1.6 collective-permute-done.49.c2
  204.3 1.5 collective-permute-start.51
  206.7 1.9 collective-permute-done.51.refs_1_
  208.7 4.9 %b1.1 = (f32[8,2048]{1,0:T(8,128)S(1)}, f32[8,2048]{1,0:T(8,128)S(1)}, f32[8,2048]{1,0:T(8,128)S(1)}, f32[8,2048]{1,0:T(8,128)S(1)}) custom-call(s32[128]{0:T(128)S(1)} %pad_add_fusion.meta, f32[2,16,2048]{2,1,0:T(8,128)S(1)} %get-tuple-element.127.refs_0_, f32[16,1024]{1,0:T(8,128)S(1)} %collective-permute-done.51.refs_1_, ...), custom_call_target="tpu_custom_call" | custom-call | flops 1207959552 | bytes 6684672 | tf_op jit(solution)/shard_map/b1/pallas_call | solution.py:395
  213.5 2.7 %collective-permute-start.52 = (f32[8,2048]{1,0:T(8,128)S(1)}, f32[8,2048]{1,0:T(8,128)S(1)}, u32[]{:S(2)}, u32[]{:S(2)}) collective-permute-start(f32[8,2048]{1,0:T(8,128)S(1)} %get-tuple-element.131), channel_id=1, source_target_pairs={{0,12},{4,0},{8,4},{12,8},{1,13},{5,1},{9,5},{13,9},{2,14},{6,2},{... | collective-permute-start | bytes 196616 | tf_op jit(solution)/shard_map/ppermute | solution.py:39
  217.2 1.6 collective-permute-done.52.c1
  218.8 3.3 %collective-permute-done.53.c2 = f32[8,2048]{1,0:T(8,128)S(1)} collective-permute-done((f32[8,2048]{1,0:T(8,128)S(1)}, f32[8,2048]{1,0:T(8,128)S(1)}, u32[]{:S(2)}, u32[]{:S(2)}) %collective-permute-start.53) | collective-permute-done | bytes 65568 | tf_op jit(solution)/shard_map/ppermute | solution.py:39
  225.8 1.8 collective-permute-start.58
  227.6 2.1 collective-permute-start.59
  230.3 1.8 collective-permute-done.57.refs_1_
  232.7 4.9 %b0.1 = (f32[16,2048]{1,0:T(8,128)S(1)}, f32[16,2048]{1,0:T(8,128)S(1)}, f32[16,2048]{1,0:T(8,128)S(1)}, f32[16,2048]{1,0:T(8,128)S(1)}) custom-call(s32[128]{0:T(128)S(1)} %pad_add_fusion.meta, f32[16,1024]{1,0:T(8,128)S(1)} %maximum_select_fusion.3.refs_0_, f32[16,1024]{1,0:T(8,128)S(1)} %collective-permute-done.57.refs_1_, ...), custom_call_target="tpu_custom_call" | custom-call | flops 2415919104 | bytes 6684672 | tf_op jit(solution)/shard_map/b0/pallas_call | solution.py:395
  237.6 2.7 %collective-permute-start.60 = (f32[16,2048]{1,0:T(8,128)S(1)}, f32[16,2048]{1,0:T(8,128)S(1)}, u32[]{:S(2)}, u32[]{:S(2)}) collective-permute-start(f32[16,2048]{1,0:T(8,128)S(1)} %get-tuple-element.138), channel_id=1, source_target_pairs={{0,3},{1,0},{2,1},{3,2},{4,7},{5,4},{6,5},{7,6},{8,11},{9,8},{10,9... | collective-permute-start | bytes 393224 | tf_op jit(solution)/shard_map/ppermute | solution.py:39
  242.5 2.5 collective-permute-done.60
  245.1 2.4 collective-permute-done.61
  (177 shorter events, 53.5 us)
Async XLA Ops:
  7.2 16.4 %collective-permute-start.6 = (f32[4,256,128]{2,1,0:T(8,128)}, f32[4,256,128]{2,1,0:T(8,128)}, u32[]{:S(2)}, u32[]{:S(2)}) collective-permute-start(f32[4,256,128]{2,1,0:T(8,128)} %bitcast.72), channel_id=1, source_target_pairs={{0,4},{4,8},{8,12},{12,0},{1,5},{5,9},{9,13},{13,1},{2,6},{6,10},{... | collective-permute-start | bytes 1572872 | tf_op jit(solution)/shard_map/ppermute | solution.py:39
  9.3 15.4 %collective-permute-start.7 = (f32[4,256,128]{2,1,0:T(8,128)}, f32[4,256,128]{2,1,0:T(8,128)}, u32[]{:S(2)}, u32[]{:S(2)}) collective-permute-start(f32[4,256,128]{2,1,0:T(8,128)} %bitcast.73), channel_id=1, source_target_pairs={{0,12},{4,0},{8,4},{12,8},{1,13},{5,1},{9,5},{13,9},{2,14},{6,2},{... | collective-permute-start | bytes 1572872 | tf_op jit(solution)/shard_map/ppermute | solution.py:39
  13.8 25.6 %all-to-all-start = ((f32[4,512,128]{2,1,0:T(8,128)}), f32[4,512,128]{2,1,0:T(8,128)S(1)}, u32[]{:S(2)}, u32[]{:S(2)}) async-start(f32[4,512,128]{2,1,0:T(8,128)} %bitcast.3), calls=%async_computation | async-start | bytes 2097152 | tf_op jit(solution)/shard_map/all_to_all | solution.py:446
  18.2 98.0 %all-gather.9.cloned.1.call-start = ((), (), s32[]{:S(2)}) async-start(), calls=%async_computation.2 | async-start | bytes 3932160 | tf_op jit(solution)/shard_map/all_gather | solution.py:439
  20.1 19.2 %collective-permute-start.5 = (f32[2,256,128]{2,1,0:T(8,128)S(1)}, f32[2,256,128]{2,1,0:T(8,128)S(1)}, u32[]{:S(2)}, u32[]{:S(2)}) collective-permute-start(f32[2,256,128]{2,1,0:T(8,128)S(1)} %maximum_select_fusion), channel_id=1, source_target_pairs={{0,32},{32,0},{1,33},{33,1},{2,34},{34,2},{3,35},{35,3},{4,36},{36... | collective-permute-start | bytes 786440 | tf_op jit(solution)/shard_map/ppermute | solution.py:43
  21.7 7.6 %collective-permute-start.1 = (f32[256,128]{1,0:T(8,128)S(1)}, f32[256,128]{1,0:T(8,128)S(1)}, u32[]{:S(2)}, u32[]{:S(2)}) collective-permute-start(f32[256,128]{1,0:T(8,128)S(1)} %get-tuple-element.144), channel_id=1, source_target_pairs={{0,4},{4,8},{8,12},{12,0},{1,5},{5,9},{9,13},{13,1},{2,6},{6,10},{... | collective-permute-start | bytes 393224 | tf_op jit(solution)/shard_map/ppermute | solution.py:39
  24.6 14.7 %collective-permute-start.8 = (f32[2,256,128]{2,1,0:T(8,128)S(1)}, f32[2,256,128]{2,1,0:T(8,128)S(1)}, u32[]{:S(2)}, u32[]{:S(2)}) collective-permute-start(f32[2,256,128]{2,1,0:T(8,128)S(1)} %slice.87), channel_id=1, source_target_pairs={{0,4},{4,8},{8,12},{12,0},{1,5},{5,9},{9,13},{13,1},{2,6},{6,10},{... | collective-permute-start | bytes 786440 | tf_op jit(solution)/shard_map/ppermute | solution.py:39
  25.7 13.6 %collective-permute-start.9 = (f32[2,256,128]{2,1,0:T(8,128)S(1)}, f32[2,256,128]{2,1,0:T(8,128)}, u32[]{:S(2)}, u32[]{:S(2)}) collective-permute-start(f32[2,256,128]{2,1,0:T(8,128)S(1)} %slice.88), channel_id=1, source_target_pairs={{0,12},{4,0},{8,4},{12,8},{1,13},{5,1},{9,5},{13,9},{2,14},{6,2},{... | collective-permute-start | bytes 786440 | tf_op jit(solution)/shard_map/ppermute | solution.py:39
  28.9 8.0 %collective-permute-start.2 = (f32[256,128]{1,0:T(8,128)S(1)}, f32[256,128]{1,0:T(8,128)S(1)}, u32[]{:S(2)}, u32[]{:S(2)}) collective-permute-start(f32[256,128]{1,0:T(8,128)S(1)} %get-tuple-element.143), channel_id=1, source_target_pairs={{0,8},{4,12},{8,0},{12,4},{1,9},{5,13},{9,1},{13,5},{2,10},{6,14},... | collective-permute-start | bytes 393224 | tf_op jit(solution)/shard_map/ppermute | solution.py:39
  29.3 10.0 %collective-permute-start.3 = (f32[256,128]{1,0:T(8,128)S(1)}, f32[256,128]{1,0:T(8,128)S(1)}, u32[]{:S(2)}, u32[]{:S(2)}) collective-permute-start(f32[256,128]{1,0:T(8,128)S(1)} %get-tuple-element.142), channel_id=1, source_target_pairs={{0,12},{4,0},{8,4},{12,8},{1,13},{5,1},{9,5},{13,9},{2,14},{6,2},{... | collective-permute-start | bytes 393224 | tf_op jit(solution)/shard_map/ppermute | solution.py:39
  42.2 86.0 %all-gather.7.cloned.1.call-start = ((), (), s32[]{:S(2)}) async-start(), calls=%async_computation.1 | async-start | bytes 3932160 | tf_op jit(solution)/shard_map/all_gather | solution.py:439
  42.3 27.8 %collective-permute-start.10 = (f32[4,512,128]{2,1,0:T(8,128)S(1)}, f32[4,512,128]{2,1,0:T(8,128)S(1)}, u32[]{:S(2)}, u32[]{:S(2)}) collective-permute-start(f32[4,512,128]{2,1,0:T(8,128)S(1)} %all-to-all-done.refs_4_.refs_5_), channel_id=1, source_target_pairs={{0,4},{4,8},{8,12},{12,0},{1,5},{5,9},{9,13},{13,1},{2,6},{6,10},{... | collective-permute-start | bytes 3145736 | tf_op jit(solution)/shard_map/ppermute | solution.py:39
  43.5 31.8 %collective-permute-start.11 = (f32[4,512,128]{2,1,0:T(8,128)S(1)}, f32[4,512,128]{2,1,0:T(8,128)S(1)}, u32[]{:S(2)}, u32[]{:S(2)}) collective-permute-start(f32[4,512,128]{2,1,0:T(8,128)S(1)} %all-to-all-done.refs_4_.refs_5_), channel_id=1, source_target_pairs={{0,12},{4,0},{8,4},{12,8},{1,13},{5,1},{9,5},{13,9},{2,14},{6,2},{... | collective-permute-start | bytes 3145736 | tf_op jit(solution)/shard_map/ppermute | solution.py:39
  46.1 9.7 %collective-permute-start.14 = (f32[256,128]{1,0:T(8,128)S(1)}, f32[256,128]{1,0:T(8,128)S(1)}, u32[]{:S(2)}, u32[]{:S(2)}) collective-permute-start(f32[256,128]{1,0:T(8,128)S(1)} %copy-done.11), channel_id=1, source_target_pairs={{0,32},{32,0},{1,33},{33,1},{2,34},{34,2},{3,35},{35,3},{4,36},{36... | collective-permute-start | bytes 393224 | tf_op jit(solution)/shard_map/ppermute | solution.py:43
  47.6 5.0 %collective-permute-start.12 = (f32[1,256,128]{2,1,0:T(8,128)S(1)}, f32[1,256,128]{2,1,0:T(8,128)S(1)}, u32[]{:S(2)}, u32[]{:S(2)}) collective-permute-start(f32[1,256,128]{2,1,0:T(8,128)S(1)} %bitcast.70), channel_id=1, source_target_pairs={{0,32},{32,0},{1,33},{33,1},{2,34},{34,2},{3,35},{35,3},{4,36},{36... | collective-permute-start | bytes 393224 | tf_op jit(solution)/shard_map/ppermute | solution.py:43
  52.6 8.0 %collective-permute-start.13 = (f32[2,256,128]{2,1,0:T(8,128)S(1)}, f32[2,256,128]{2,1,0:T(8,128)S(1)}, u32[]{:S(2)}, u32[]{:S(2)}) collective-permute-start(f32[2,256,128]{2,1,0:T(8,128)S(1)} %maximum_select_fusion.1), channel_id=1, source_target_pairs={{0,64},{64,0},{1,65},{65,1},{2,66},{66,2},{3,67},{67,3},{4,68},{68... | collective-permute-start | bytes 786440 | tf_op jit(solution)/shard_map/ppermute | solution.py:43
  55.6 8.7 %collective-permute-start.15 = (f32[8,1792]{1,0:T(8,128)S(1)}, f32[8,1792]{1,0:T(8,128)S(1)}, u32[]{:S(2)}, u32[]{:S(2)}) collective-permute-start(f32[8,1792]{1,0:T(8,128)S(1)} %get-tuple-element.167), channel_id=1, source_target_pairs={{0,16},{16,0},{1,17},{17,1},{2,18},{18,2},{3,19},{19,3},{4,20},{20... | collective-permute-start | bytes 172040 | tf_op jit(solution)/shard_map/ppermute | solution.py:43
  60.7 14.7 %collective-permute-start.16 = (f32[2,256,128]{2,1,0:T(8,128)S(1)}, f32[2,256,128]{2,1,0:T(8,128)S(1)}, u32[]{:S(2)}, u32[]{:S(2)}) collective-permute-start(f32[2,256,128]{2,1,0:T(8,128)S(1)} %pad_maximum_fusion.2), channel_id=1, source_target_pairs={{0,4},{4,8},{8,12},{12,0},{1,5},{5,9},{9,13},{13,1},{2,6},{6,10},{... | collective-permute-start | bytes 786440 | tf_op jit(solution)/shard_map/ppermute | solution.py:39
  60.8 19.2 %collective-permute-start.17 = (f32[2,256,128]{2,1,0:T(8,128)S(1)}, f32[2,256,128]{2,1,0:T(8,128)S(1)}, u32[]{:S(2)}, u32[]{:S(2)}) collective-permute-start(f32[2,256,128]{2,1,0:T(8,128)S(1)} %pad_maximum_fusion.3), channel_id=1, source_target_pairs={{0,8},{4,12},{8,0},{12,4},{1,9},{5,13},{9,1},{13,5},{2,10},{6,14},... | collective-permute-start | bytes 786440 | tf_op jit(solution)/shard_map/ppermute | solution.py:39
  64.4 15.6 %collective-permute-start.18 = (f32[2,256,128]{2,1,0:T(8,128)S(1)}, f32[2,256,128]{2,1,0:T(8,128)S(1)}, u32[]{:S(2)}, u32[]{:S(2)}) collective-permute-start(f32[2,256,128]{2,1,0:T(8,128)S(1)} %pad_maximum_fusion.4), channel_id=1, source_target_pairs={{0,12},{4,0},{8,4},{12,8},{1,13},{5,1},{9,5},{13,9},{2,14},{6,2},{... | collective-permute-start | bytes 786440 | tf_op jit(solution)/shard_map/ppermute | solution.py:39
  81.0 80.0 %all-gather.11.cloned.1.call-start = ((), (), s32[]{:S(2)}) async-start(), calls=%async_computation.3 | async-start | bytes 2621440 | tf_op jit(solution)/shard_map/all_gather | solution.py:439
  82.1 13.9 %collective-permute-start.19 = (f32[2,512,128]{2,1,0:T(8,128)S(1)}, f32[2,512,128]{2,1,0:T(8,128)S(1)}, u32[]{:S(2)}, u32[]{:S(2)}) collective-permute-start(f32[2,512,128]{2,1,0:T(8,128)S(1)} %slice.79), channel_id=1, source_target_pairs={{0,4},{4,8},{8,12},{12,0},{1,5},{5,9},{9,13},{13,1},{2,6},{6,10},{... | collective-permute-start | bytes 1572872 | tf_op jit(solution)/shard_map/ppermute | solution.py:39
  83.2 12.7 %collective-permute-start.20 = (f32[2,512,128]{2,1,0:T(8,128)S(1)}, f32[2,512,128]{2,1,0:T(8,128)S(1)}, u32[]{:S(2)}, u32[]{:S(2)}) collective-permute-start(f32[2,512,128]{2,1,0:T(8,128)S(1)} %slice.80), channel_id=1, source_target_pairs={{0,12},{4,0},{8,4},{12,8},{1,13},{5,1},{9,5},{13,9},{2,14},{6,2},{... | collective-permute-start | bytes 1572872 | tf_op jit(solution)/shard_map/ppermute | solution.py:39
  86.5 6.2 %collective-permute-start.21 = (f32[16,2048]{1,0:T(8,128)S(1)}, f32[16,2048]{1,0:T(8,128)S(1)}, u32[]{:S(2)}, u32[]{:S(2)}) collective-permute-start(f32[16,2048]{1,0:T(8,128)S(1)} %copy-done), channel_id=1, source_target_pairs={{0,1},{1,2},{2,3},{3,0},{4,5},{5,6},{6,7},{7,4},{8,9},{9,10},{10,1... | collective-permute-start | bytes 393224 | tf_op jit(solution)/shard_map/ppermute | solution.py:39
  88.1 7.2 %collective-permute-start.22 = (f32[16,2048]{1,0:T(8,128)S(1)}, f32[16,2048]{1,0:T(8,128)S(1)}, u32[]{:S(2)}, u32[]{:S(2)}) collective-permute-start(f32[16,2048]{1,0:T(8,128)S(1)} %copy-done), channel_id=1, source_target_pairs={{0,2},{1,3},{2,0},{3,1},{4,6},{5,7},{6,4},{7,5},{8,10},{9,11},{10,... | collective-permute-start | bytes 393224 | tf_op jit(solution)/shard_map/ppermute | solution.py:39
  91.0 5.0 %collective-permute-start.23 = (f32[16,2048]{1,0:T(8,128)S(1)}, f32[16,2048]{1,0:T(8,128)S(1)}, u32[]{:S(2)}, u32[]{:S(2)}) collective-permute-start(f32[16,2048]{1,0:T(8,128)S(1)} %copy-done), channel_id=1, source_target_pairs={{0,3},{1,0},{2,1},{3,2},{4,7},{5,4},{6,5},{7,6},{8,11},{9,8},{10,9... | collective-permute-start | bytes 393224 | tf_op jit(solution)/shard_map/ppermute | solution.py:39
  103.3 6.1 %collective-permute-start.24 = (f32[16,1024]{1,0:T(8,128)S(1)}, f32[16,1024]{1,0:T(8,128)S(1)}, u32[]{:S(2)}, u32[]{:S(2)}) collective-permute-start(f32[16,1024]{1,0:T(8,128)S(1)} %get-tuple-element.97), channel_id=1, source_target_pairs={{0,3},{1,0},{2,1},{3,2},{4,7},{5,4},{6,5},{7,6},{8,11},{9,8},{10,9... | collective-permute-start | bytes 196616 | tf_op jit(solution)/shard_map/ppermute | solution.py:39
  106.0 7.1 %collective-permute-start.25 = (f32[16,1024]{1,0:T(8,128)S(1)}, f32[16,1024]{1,0:T(8,128)S(1)}, u32[]{:S(2)}, u32[]{:S(2)}) collective-permute-start(f32[16,1024]{1,0:T(8,128)S(1)} %get-tuple-element.98), channel_id=1, source_target_pairs={{0,2},{1,3},{2,0},{3,1},{4,6},{5,7},{6,4},{7,5},{8,10},{9,11},{10,... | collective-permute-start | bytes 196616 | tf_op jit(solution)/shard_map/ppermute | solution.py:39
  106.5 7.5 %collective-permute-start.26 = (f32[16,1024]{1,0:T(8,128)S(1)}, f32[16,1024]{1,0:T(8,128)S(1)}, u32[]{:S(2)}, u32[]{:S(2)}) collective-permute-start(f32[16,1024]{1,0:T(8,128)S(1)} %get-tuple-element.99), channel_id=1, source_target_pairs={{0,1},{1,2},{2,3},{3,0},{4,5},{5,6},{6,7},{7,4},{8,9},{9,10},{10,1... | collective-permute-start | bytes 196616 | tf_op jit(solution)/shard_map/ppermute | solution.py:39
  116.2 12.0 %collective-permute-start.32 = (f32[4,6,256,128]{3,2,1,0:T(8,128)}, f32[4,6,256,128]{3,2,1,0:T(8,128)}, u32[]{:S(2)}, u32[]{:S(2)}) collective-permute-start(f32[4,6,256,128]{3,2,1,0:T(8,128)} %bitcast.56), channel_id=1, source_target_pairs={{0,16},{16,0},{1,17},{17,1},{2,18},{18,2},{3,19},{19,3},{4,20},{20... | collective-permute-start | bytes 9437192 | tf_op jit(solution)/shard_map/ppermute | solution.py:43
  116.4 5.5 %collective-permute-start.28 = (f32[2,4,2048]{2,1,0:T(4,128)S(1)}, f32[2,4,2048]{2,1,0:T(4,128)S(1)}, u32[]{:S(2)}, u32[]{:S(2)}) collective-permute-start(f32[2,4,2048]{2,1,0:T(4,128)S(1)} %get-tuple-element.103), channel_id=1, source_target_pairs={{0,32},{32,0},{1,33},{33,1},{2,34},{34,2},{3,35},{35,3},{4,36},{36... | collective-permute-start | bytes 196616 | tf_op jit(solution)/shard_map/ppermute | solution.py:43
  117.9 6.2 %collective-permute-start.29 = (f32[8,2048]{1,0:T(8,128)S(1)}, f32[8,2048]{1,0:T(8,128)S(1)}, u32[]{:S(2)}, u32[]{:S(2)}) collective-permute-start(f32[8,2048]{1,0:T(8,128)S(1)} %get-tuple-element.105.refs_0_), channel_id=1, source_target_pairs={{0,4},{4,8},{8,12},{12,0},{1,5},{5,9},{9,13},{13,1},{2,6},{6,10},{... | collective-permute-start | bytes 196616 | tf_op jit(solution)/shard_map/ppermute | solution.py:39
  117.9 7.0 %collective-permute-start.30 = (f32[8,2048]{1,0:T(8,128)S(1)}, f32[8,2048]{1,0:T(8,128)S(1)}, u32[]{:S(2)}, u32[]{:S(2)}) collective-permute-start(f32[8,2048]{1,0:T(8,128)S(1)} %get-tuple-element.105.refs_0_), channel_id=1, source_target_pairs={{0,8},{4,12},{8,0},{12,4},{1,9},{5,13},{9,1},{13,5},{2,10},{6,14},... | collective-permute-start | bytes 196616 | tf_op jit(solution)/shard_map/ppermute | solution.py:39
  121.5 4.3 %collective-permute-start.31 = (f32[8,2048]{1,0:T(8,128)S(1)}, f32[8,2048]{1,0:T(8,128)S(1)}, u32[]{:S(2)}, u32[]{:S(2)}) collective-permute-start(f32[8,2048]{1,0:T(8,128)S(1)} %get-tuple-element.105.refs_0_), channel_id=1, source_target_pairs={{0,12},{4,0},{8,4},{12,8},{1,13},{5,1},{9,5},{13,9},{2,14},{6,2},{... | collective-permute-start | bytes 196616 | tf_op jit(solution)/shard_map/ppermute | solution.py:39
  128.2 20.7 %collective-permute-start.37 = (f32[4,6,256,128]{3,2,1,0:T(8,128)}, f32[4,6,256,128]{3,2,1,0:T(8,128)}, u32[]{:S(2)}, u32[]{:S(2)}) collective-permute-start(f32[4,6,256,128]{3,2,1,0:T(8,128)} %bitcast.59), channel_id=1, source_target_pairs={{0,16},{16,0},{1,17},{17,1},{2,18},{18,2},{3,19},{19,3},{4,20},{20... | collective-permute-start | bytes 9437192 | tf_op jit(solution)/shard_map/ppermute | solution.py:43
  133.2 4.6 %collective-permute-start.33 = (f32[16,1024]{1,0:T(8,128)S(1)}, f32[16,1024]{1,0:T(8,128)S(1)}, u32[]{:S(2)}, u32[]{:S(2)}) collective-permute-start(f32[16,1024]{1,0:T(8,128)S(1)} %get-tuple-element.115), channel_id=1, source_target_pairs={{0,32},{32,0},{1,33},{33,1},{2,34},{34,2},{3,35},{35,3},{4,36},{36... | collective-permute-start | bytes 196616 | tf_op jit(solution)/shard_map/ppermute | solution.py:43
  138.5 8.8 %collective-permute-start.34 = (f32[16,2048]{1,0:T(8,128)S(1)}, f32[16,2048]{1,0:T(8,128)S(1)}, u32[]{:S(2)}, u32[]{:S(2)}) collective-permute-start(f32[16,2048]{1,0:T(8,128)S(1)} %get-tuple-element.118.refs_0_), channel_id=1, source_target_pairs={{0,4},{4,8},{8,12},{12,0},{1,5},{5,9},{9,13},{13,1},{2,6},{6,10},{... | collective-permute-start | bytes 393224 | tf_op jit(solution)/shard_map/ppermute | solution.py:39
  140.2 8.7 %collective-permute-start.35 = (f32[16,2048]{1,0:T(8,128)S(1)}, f32[16,2048]{1,0:T(8,128)S(1)}, u32[]{:S(2)}, u32[]{:S(2)}) collective-permute-start(f32[16,2048]{1,0:T(8,128)S(1)} %get-tuple-element.118.refs_0_), channel_id=1, source_target_pairs={{0,8},{4,12},{8,0},{12,4},{1,9},{5,13},{9,1},{13,5},{2,10},{6,14},... | collective-permute-start | bytes 393224 | tf_op jit(solution)/shard_map/ppermute | solution.py:39
  143.0 5.9 %collective-permute-start.36 = (f32[16,2048]{1,0:T(8,128)S(1)}, f32[16,2048]{1,0:T(8,128)S(1)}, u32[]{:S(2)}, u32[]{:S(2)}) collective-permute-start(f32[16,2048]{1,0:T(8,128)S(1)} %get-tuple-element.118.refs_0_), channel_id=1, source_target_pairs={{0,12},{4,0},{8,4},{12,8},{1,13},{5,1},{9,5},{13,9},{2,14},{6,2},{... | collective-permute-start | bytes 393224 | tf_op jit(solution)/shard_map/ppermute | solution.py:39
  144.3 12.4 %collective-permute-start.39 = (f32[8,2048]{1,0:T(8,128)S(1)}, f32[8,2048]{1,0:T(8,128)S(1)}, u32[]{:S(2)}, u32[]{:S(2)}) collective-permute-start(f32[8,2048]{1,0:T(8,128)S(1)} %get-tuple-element.123), channel_id=1, source_target_pairs={{0,64},{64,0},{1,65},{65,1},{2,66},{66,2},{3,67},{67,3},{4,68},{68... | collective-permute-start | bytes 196616 | tf_op jit(solution)/shard_map/ppermute | solution.py:43
  153.6 5.5 %collective-permute-start.38 = (f32[8,1024]{1,0:T(8,128)S(1)}, f32[8,1024]{1,0:T(8,128)S(1)}, u32[]{:S(2)}, u32[]{:S(2)}) collective-permute-start(f32[8,1024]{1,0:T(8,128)S(1)} %get-tuple-element.121), channel_id=1, source_target_pairs={{0,64},{64,0},{1,65},{65,1},{2,66},{66,2},{3,67},{67,3},{4,68},{68... | collective-permute-start | bytes 98312 | tf_op jit(solution)/shard_map/ppermute | solution.py:43
  160.9 8.7 %collective-permute-start.43 = (f32[4,4,256,128]{3,2,1,0:T(8,128)}, f32[4,4,256,128]{3,2,1,0:T(8,128)S(1)}, u32[]{:S(2)}, u32[]{:S(2)}) collective-permute-start(f32[4,4,256,128]{3,2,1,0:T(8,128)} %bitcast.62), channel_id=1, source_target_pairs={{0,16},{16,0},{1,17},{17,1},{2,18},{18,2},{3,19},{19,3},{4,20},{20... | collective-permute-start | bytes 6291464 | tf_op jit(solution)/shard_map/ppermute | solution.py:43
  160.9 5.8 %collective-permute-start.40 = (f32[8,2048]{1,0:T(8,128)S(1)}, f32[8,2048]{1,0:T(8,128)S(1)}, u32[]{:S(2)}, u32[]{:S(2)}) collective-permute-start(f32[8,2048]{1,0:T(8,128)S(1)} %s23.1.c0), channel_id=1, source_target_pairs={{0,4},{4,8},{8,12},{12,0},{1,5},{5,9},{9,13},{13,1},{2,6},{6,10},{... | collective-permute-start | bytes 196616 | tf_op jit(solution)/shard_map/ppermute | solution.py:39
  162.5 6.7 %collective-permute-start.41 = (f32[8,2048]{1,0:T(8,128)S(1)}, f32[8,2048]{1,0:T(8,128)S(1)}, u32[]{:S(2)}, u32[]{:S(2)}) collective-permute-start(f32[8,2048]{1,0:T(8,128)S(1)} %s23.1.c0), channel_id=1, source_target_pairs={{0,8},{4,12},{8,0},{12,4},{1,9},{5,13},{9,1},{13,5},{2,10},{6,14},... | collective-permute-start | bytes 196616 | tf_op jit(solution)/shard_map/ppermute | solution.py:39
  165.3 4.3 %collective-permute-start.42 = (f32[8,2048]{1,0:T(8,128)S(1)}, f32[8,2048]{1,0:T(8,128)S(1)}, u32[]{:S(2)}, u32[]{:S(2)}) collective-permute-start(f32[8,2048]{1,0:T(8,128)S(1)} %s23.1.c0), channel_id=1, source_target_pairs={{0,12},{4,0},{8,4},{12,8},{1,13},{5,1},{9,5},{13,9},{2,14},{6,2},{... | collective-permute-start | bytes 196616 | tf_op jit(solution)/shard_map/ppermute | solution.py:39
  175.6 5.6 %collective-permute-start.44 = (f32[8,2048]{1,0:T(8,128)S(1)}, f32[8,2048]{1,0:T(8,128)S(1)}, u32[]{:S(2)}, u32[]{:S(2)}) collective-permute-start(f32[8,2048]{1,0:T(8,128)S(1)} %top.1.c0), channel_id=1, source_target_pairs={{0,4},{4,8},{8,12},{12,0},{1,5},{5,9},{9,13},{13,1},{2,6},{6,10},{... | collective-permute-start | bytes 196616 | tf_op jit(solution)/shard_map/ppermute | solution.py:39
  176.5 6.1 %collective-permute-start.45 = (f32[8,2048]{1,0:T(8,128)S(1)}, f32[8,2048]{1,0:T(8,128)S(1)}, u32[]{:S(2)}, u32[]{:S(2)}) collective-permute-start(f32[8,2048]{1,0:T(8,128)S(1)} %top.1.c0), channel_id=1, source_target_pairs={{0,8},{4,12},{8,0},{12,4},{1,9},{5,13},{9,1},{13,5},{2,10},{6,14},... | collective-permute-start | bytes 196616 | tf_op jit(solution)/shard_map/ppermute | solution.py:39
  184.6 5.8 %collective-permute-start.47 = (f32[8,2048]{1,0:T(8,128)S(1)}, f32[8,2048]{1,0:T(8,128)S(1)}, u32[]{:S(2)}, u32[]{:S(2)}) collective-permute-start(f32[8,2048]{1,0:T(8,128)S(1)} %x3.1), channel_id=1, source_target_pairs={{0,64},{64,0},{1,65},{65,1},{2,66},{66,2},{3,67},{67,3},{4,68},{68... | collective-permute-start | bytes 196616 | tf_op jit(solution)/shard_map/ppermute | solution.py:43
  195.2 6.2 %collective-permute-start.48 = (f32[16,2048]{1,0:T(8,128)S(1)}, f32[16,2048]{1,0:T(8,128)S(1)}, u32[]{:S(2)}, u32[]{:S(2)}) collective-permute-start(f32[16,2048]{1,0:T(8,128)S(1)} %b2.1.c0), channel_id=1, source_target_pairs={{0,4},{4,8},{8,12},{12,0},{1,5},{5,9},{9,13},{13,1},{2,6},{6,10},{... | collective-permute-start | bytes 393224 | tf_op jit(solution)/shard_map/ppermute | solution.py:39
  195.5 7.5 %collective-permute-start.49 = (f32[16,2048]{1,0:T(8,128)S(1)}, f32[16,2048]{1,0:T(8,128)S(1)}, u32[]{:S(2)}, u32[]{:S(2)}) collective-permute-start(f32[16,2048]{1,0:T(8,128)S(1)} %b2.1.c0), channel_id=1, source_target_pairs={{0,8},{4,12},{8,0},{12,4},{1,9},{5,13},{9,1},{13,5},{2,10},{6,14},... | collective-permute-start | bytes 393224 | tf_op jit(solution)/shard_map/ppermute | solution.py:39
  198.7 5.0 %collective-permute-start.50 = (f32[16,2048]{1,0:T(8,128)S(1)}, f32[16,2048]{1,0:T(8,128)S(1)}, u32[]{:S(2)}, u32[]{:S(2)}) collective-permute-start(f32[16,2048]{1,0:T(8,128)S(1)} %b2.1.c0), channel_id=1, source_target_pairs={{0,12},{4,0},{8,4},{12,8},{1,13},{5,1},{9,5},{13,9},{2,14},{6,2},{... | collective-permute-start | bytes 393224 | tf_op jit(solution)/shard_map/ppermute | solution.py:39
  204.3 4.3 %collective-permute-start.51 = (f32[16,1024]{1,0:T(8,128)S(1)}, f32[16,1024]{1,0:T(8,128)S(1)}, u32[]{:S(2)}, u32[]{:S(2)}) collective-permute-start(f32[16,1024]{1,0:T(8,128)S(1)} %get-tuple-element.128), channel_id=1, source_target_pairs={{0,32},{32,0},{1,33},{33,1},{2,34},{34,2},{3,35},{35,3},{4,36},{36... | collective-permute-start | bytes 196616 | tf_op jit(solution)/shard_map/ppermute | solution.py:43
  205.9 11.4 %collective-permute-start.55 = (f32[2,4,2048]{2,1,0:T(4,128)S(1)}, f32[2,4,2048]{2,1,0:T(4,128)S(1)}, u32[]{:S(2)}, u32[]{:S(2)}) collective-permute-start(f32[2,4,2048]{2,1,0:T(4,128)S(1)} %slice.83.a_mine), channel_id=1, source_target_pairs={{0,32},{32,0},{1,33},{33,1},{2,34},{34,2},{3,35},{35,3},{4,36},{36... | collective-permute-start | bytes 196616 | tf_op jit(solution)/shard_map/ppermute | solution.py:43
  213.5 5.3 %collective-permute-start.52 = (f32[8,2048]{1,0:T(8,128)S(1)}, f32[8,2048]{1,0:T(8,128)S(1)}, u32[]{:S(2)}, u32[]{:S(2)}) collective-permute-start(f32[8,2048]{1,0:T(8,128)S(1)} %get-tuple-element.131), channel_id=1, source_target_pairs={{0,12},{4,0},{8,4},{12,8},{1,13},{5,1},{9,5},{13,9},{2,14},{6,2},{... | collective-permute-start | bytes 196616 | tf_op jit(solution)/shard_map/ppermute | solution.py:39
  216.3 5.8 %collective-permute-start.53 = (f32[8,2048]{1,0:T(8,128)S(1)}, f32[8,2048]{1,0:T(8,128)S(1)}, u32[]{:S(2)}, u32[]{:S(2)}) collective-permute-start(f32[8,2048]{1,0:T(8,128)S(1)} %get-tuple-element.132), channel_id=1, source_target_pairs={{0,8},{4,12},{8,0},{12,4},{1,9},{5,13},{9,1},{13,5},{2,10},{6,14},... | collective-permute-start | bytes 196616 | tf_op jit(solution)/shard_map/ppermute | solution.py:39
  216.6 6.2 %collective-permute-start.54 = (f32[8,2048]{1,0:T(8,128)S(1)}, f32[8,2048]{1,0:T(8,128)S(1)}, u32[]{:S(2)}, u32[]{:S(2)}) collective-permute-start(f32[8,2048]{1,0:T(8,128)S(1)} %get-tuple-element.133), channel_id=1, source_target_pairs={{0,4},{4,8},{8,12},{12,0},{1,5},{5,9},{9,13},{13,1},{2,6},{6,10},{... | collective-permute-start | bytes 196616 | tf_op jit(solution)/shard_map/ppermute | solution.py:39
  223.6 17.7 %collective-permute-start.64 = (f32[8,512]{1,0:T(8,128)S(1)}, f32[8,512]{1,0:T(8,128)S(1)}, u32[]{:S(2)}, u32[]{:S(2)}) collective-permute-start(f32[8,512]{1,0:T(8,128)S(1)} %get-tuple-element.172), channel_id=1, source_target_pairs={{0,16},{16,0},{1,17},{17,1},{2,18},{18,2},{3,19},{19,3},{4,20},{20... | collective-permute-start | bytes 49160 | tf_op jit(solution)/shard_map/ppermute | solution.py:43
  224.1 17.7 %collective-permute-start.63 = (f32[8,1024]{1,0:T(8,128)S(1)}, f32[8,1024]{1,0:T(8,128)S(1)}, u32[]{:S(2)}, u32[]{:S(2)}) collective-permute-start(f32[8,1024]{1,0:T(8,128)S(1)} %get-tuple-element.174), channel_id=1, source_target_pairs={{0,16},{16,0},{1,17},{17,1},{2,18},{18,2},{3,19},{19,3},{4,20},{20... | collective-permute-start | bytes 98312 | tf_op jit(solution)/shard_map/ppermute | solution.py:43
  225.3 6.8 %collective-permute-start.57 = (f32[16,1024]{1,0:T(8,128)S(1)}, f32[16,1024]{1,0:T(8,128)S(1)}, u32[]{:S(2)}, u32[]{:S(2)}) collective-permute-start(f32[16,1024]{1,0:T(8,128)S(1)} %maximum_select_fusion.3.refs_0_), channel_id=1, source_target_pairs={{0,1},{1,2},{2,3},{3,0},{4,5},{5,6},{6,7},{7,4},{8,9},{9,10},{10,1... | collective-permute-start | bytes 196616 | tf_op jit(solution)/shard_map/ppermute | solution.py:39
  225.8 6.2 %collective-permute-start.58 = (f32[16,1024]{1,0:T(8,128)S(1)}, f32[16,1024]{1,0:T(8,128)S(1)}, u32[]{:S(2)}, u32[]{:S(2)}) collective-permute-start(f32[16,1024]{1,0:T(8,128)S(1)} %maximum_select_fusion.3.refs_0_), channel_id=1, source_target_pairs={{0,2},{1,3},{2,0},{3,1},{4,6},{5,7},{6,4},{7,5},{8,10},{9,11},{10,... | collective-permute-start | bytes 196616 | tf_op jit(solution)/shard_map/ppermute | solution.py:39
  227.6 5.0 %collective-permute-start.59 = (f32[16,1024]{1,0:T(8,128)S(1)}, f32[16,1024]{1,0:T(8,128)S(1)}, u32[]{:S(2)}, u32[]{:S(2)}) collective-permute-start(f32[16,1024]{1,0:T(8,128)S(1)} %maximum_select_fusion.3.refs_0_), channel_id=1, source_target_pairs={{0,3},{1,0},{2,1},{3,2},{4,7},{5,4},{6,5},{7,6},{8,11},{9,8},{10,9... | collective-permute-start | bytes 196616 | tf_op jit(solution)/shard_map/ppermute | solution.py:39
  237.6 7.5 %collective-permute-start.60 = (f32[16,2048]{1,0:T(8,128)S(1)}, f32[16,2048]{1,0:T(8,128)S(1)}, u32[]{:S(2)}, u32[]{:S(2)}) collective-permute-start(f32[16,2048]{1,0:T(8,128)S(1)} %get-tuple-element.138), channel_id=1, source_target_pairs={{0,3},{1,0},{2,1},{3,2},{4,7},{5,4},{6,5},{7,6},{8,11},{9,8},{10,9... | collective-permute-start | bytes 393224 | tf_op jit(solution)/shard_map/ppermute | solution.py:39
  240.3 7.1 %collective-permute-start.61 = (f32[16,2048]{1,0:T(8,128)S(1)}, f32[16,2048]{1,0:T(8,128)S(1)}, u32[]{:S(2)}, u32[]{:S(2)}) collective-permute-start(f32[16,2048]{1,0:T(8,128)S(1)} %get-tuple-element.139), channel_id=1, source_target_pairs={{0,2},{1,3},{2,0},{3,1},{4,6},{5,7},{6,4},{7,5},{8,10},{9,11},{10,... | collective-permute-start | bytes 393224 | tf_op jit(solution)/shard_map/ppermute | solution.py:39
  240.8 7.9 %collective-permute-start.62 = (f32[16,2048]{1,0:T(8,128)S(1)}, f32[16,2048]{1,0:T(8,128)S(1)}, u32[]{:S(2)}, u32[]{:S(2)}) collective-permute-start(f32[16,2048]{1,0:T(8,128)S(1)} %get-tuple-element.140), channel_id=1, source_target_pairs={{0,1},{1,2},{2,3},{3,0},{4,5},{5,6},{6,7},{7,4},{8,9},{9,10},{10,1... | collective-permute-start | bytes 393224 | tf_op jit(solution)/shard_map/ppermute | solution.py:39
  (25 other events, 269.6 us)
Sparse Core Ops, SparseCore 0:
  42.3 41.5 all-gather.8
  85.6 42.5 all-gather.6
  129.8 31.0 all-gather.10
